TPU v7x, 128 devices: a whole 4x4x4 slice. The times are simulated.
128 devices in a mesh: freq: 8 (over y, core), sky: 16 (over z, x).
Axes of the slice: x: 4, y: 4, z: 4, core: 2. Of those that a mesh axis runs over, the one named last changes fastest.
Arguments:
- sky_cube: bfloat16 [256, 512, 1024], P(None, 'sky', 'freq'), may hold values from -6 to 6
- weight_first: bfloat16 [3, 3, 1024, 256], P(None, None, 'freq'), may hold values from -0.0625 to 0.0625
- weight_second: bfloat16 [3, 3, 256, 256], replicated, may hold values from -0.125 to 0.125
- cotangent: bfloat16 [256, 512, 256], P('freq', 'sky'), may hold values from -0.016479492 to 0.016479492
Outputs:
- features: bfloat16 [256, 512, 256], P('freq', 'sky')
- grad_first: float32 [3, 3, 1024, 256], P(None, None, 'freq')
- grad_second: float32 [3, 3, 256, 256], replicated
All inputs are finite; a program needn't handle non-finite values.
Results may differ from a plain program's by a relative error of at most 0.024.
Values may be sent and summed in bfloat16 or wider, within the bound.
No kernel may reach another device: no remote copies, remote signals or barrier semaphores. Data moves between devices by JAX's collectives and lax.ppermute only.
A program may use at most 128 MiB of HBM per device.

v0:
```python
import jax
import jax.numpy as jnp
from jax import lax
from jax.sharding import PartitionSpec as P


def with_halo(x, sides, width):
    for axis, dim in sides:
        count, length = (lax.axis_size(axis), x.shape[dim])
        up = [(i, (i + 1) % count) for i in range(count - 1)]
        down = [(j, i) for i, j in up]
        last = lax.slice_in_dim(x, length - width, length, axis=dim)
        first = lax.slice_in_dim(x, 0, width, axis=dim)
        before = lax.ppermute(last, axis, up)
        after = lax.ppermute(first, axis, down)
        x = jnp.concatenate([before, x, after], axis=dim)
    return x


def conv_taps(padded, kernel, col_count, row_count):
    total = jnp.zeros((col_count * row_count, kernel.shape[3]), jnp.float32)
    for tap_col in range(3):
        for tap_row in range(3):
            piece = padded[tap_col : tap_col + col_count, tap_row : tap_row + row_count].reshape(
                col_count * row_count, -1
            )
            total = total + jnp.dot(
                piece, kernel[tap_col, tap_row], preferred_element_type=jnp.float32
            )
    return total.reshape(col_count, row_count, kernel.shape[3])


def conv_back(padded, kernel, col_count, row_count):
    total = jnp.zeros((col_count * row_count, kernel.shape[2]), jnp.float32)
    for tap_col in range(3):
        for tap_row in range(3):
            piece = padded[
                2 - tap_col : 2 - tap_col + col_count, 2 - tap_row : 2 - tap_row + row_count
            ].reshape(col_count * row_count, -1)
            total = total + lax.dot_general(
                piece,
                kernel[tap_col, tap_row],
                (((1,), (1,)), ((), ())),
                preferred_element_type=jnp.float32,
            )
    return total.reshape(col_count, row_count, kernel.shape[2])


def kernel_grad(padded, grads, col_count, row_count):
    flat = grads.reshape(col_count * row_count, -1)
    rows_out = []
    for tap_col in range(3):
        line = []
        for tap_row in range(3):
            piece = padded[tap_col : tap_col + col_count, tap_row : tap_row + row_count].reshape(
                col_count * row_count, -1
            )
            line.append(
                lax.dot_general(
                    piece, flat, (((0,), (0,)), ((), ())), preferred_element_type=jnp.float32
                )
            )
        rows_out.append(jnp.stack(line))
    return jnp.stack(rows_out)


def pad_columns(field):
    return jnp.pad(field, ((1, 1), (0, 0), (0, 0)))


def silu_slope(pre):
    sigma = jax.nn.sigmoid(pre)
    return sigma * (1.0 + pre * (1.0 - sigma))


def body(sky_cube, weight_first, weight_second, cotangent):
    row_count = sky_cube.shape[1]
    strip = cotangent.shape[0]
    cube_rows = with_halo(sky_cube, (("sky", 1),), 1)
    cube_pad = pad_columns(cube_rows)
    slab = cube_pad
    pre = lax.psum_scatter(
        conv_taps(slab, weight_first, strip * lax.axis_size("freq"), row_count).astype(
            jnp.bfloat16
        ),
        "freq",
        scatter_dimension=0,
        tiled=True,
    ).astype(jnp.float32)
    hidden = jax.nn.silu(pre).astype(jnp.bfloat16)
    hidden_pad = with_halo(hidden, (("freq", 0), ("sky", 1)), 1)
    features = conv_taps(hidden_pad, weight_second, strip, row_count).astype(jnp.bfloat16)
    cotan_pad = with_halo(cotangent, (("freq", 0), ("sky", 1)), 1)
    back = conv_back(cotan_pad, weight_second, strip, row_count)
    delta = (back * silu_slope(pre)).astype(jnp.bfloat16)
    second_part = kernel_grad(hidden_pad, cotangent, strip, row_count)
    piece = lax.all_gather(delta, "freq", axis=0, tiled=True)
    count = piece.shape[0]
    slab = cube_pad
    first_part = kernel_grad(slab, piece, count, row_count)
    grad_first = lax.psum(first_part.astype(jnp.bfloat16), "sky").astype(jnp.float32)
    grad_second = lax.psum(second_part, ("freq", "sky"))
    return (features, grad_first, grad_second)


def solution(mesh):
    return jax.shard_map(
        body,
        mesh=mesh,
        in_specs=(P(None, "sky", "freq"), P(None, None, "freq", None), P(), P("freq", "sky", None)),
        out_specs=(P("freq", "sky", None), P(None, None, "freq", None), P()),
        check_vma=False,
    )
```

profile of v0, /device:TPU:1, one launch (start us, length us, event | category | flops | bytes accessed | tf_op | source)
XLA Modules:
  0.0 431.5 jit_solution(9368772974615477978)
XLA Ops:
  7.2 3.0 copy.25
  10.2 3.9 collective-permute-start
  15.5 3.7 collective-permute-done.1
  19.2 3.6 fusion.6
  22.8 6.3 %fusion.144 = (bf16[256,32,128]{0,2,1:T(8,128)(2,1)}, bf16[256,32,128]{0,2,1:T(8,128)(2,1)}, bf16[256,32,128]{0,2,1:T(8,128)(2,1)}, bf16[256,32,128]{0,2,1:T(8,1...) fusion(bf16[258,34,128]{0,2,1:T(8,128)(2,1)S(1)} %fusion.6), kind=kLoop, calls=%fused_computation.207 | loop fusion | bytes 25165824 | tf_op jit(solution)/shard_map/slice | solution.py:24
  29.1 4.5 %copy.28 = bf16[256,32,128]{2,1,0:T(8,128)(2,1)} copy(bf16[256,32,128]{0,2,1:T(8,128)(2,1)} %get-tuple-element.8) | data formatting | bytes 4194304 | tf_op jit(solution)/shard_map/slice | solution.py:24
  33.6 4.6 %copy.29 = bf16[256,32,128]{2,1,0:T(8,128)(2,1)} copy(bf16[256,32,128]{0,2,1:T(8,128)(2,1)} %get-tuple-element.7) | data formatting | bytes 4194304 | tf_op jit(solution)/shard_map/slice | solution.py:24
  38.1 4.6 %copy.30 = bf16[256,32,128]{2,1,0:T(8,128)(2,1)} copy(bf16[256,32,128]{0,2,1:T(8,128)(2,1)} %get-tuple-element.6) | data formatting | bytes 4194304 | tf_op jit(solution)/shard_map/slice | solution.py:24
  42.8 4.5 %pad_maximum_fusion.1 = (bf16[256,32,128]{0,2,1:T(8,128)(2,1)}, bf16[256,32,128]{0,2,1:T(8,128)(2,1)}) fusion(bf16[256,1,128]{0,2,1:T(8,128)(2,1)S(1)} %collective-permute-done.1, bf16[256,32,128]{0,2,1:T(8,128)(2,1)} %copy-done, bf16[256,1,128]{0,2,1:T(8,128)(2,1)S(1)} %collective-permute-done), kind=kLoop, calls=%fused_computation.26 | loop fusion | flops 2097152 | bytes 6422528 | tf_op jit(solution)/shard_map/slice | solution.py:24
  47.3 4.5 %copy.32 = bf16[256,32,128]{2,1,0:T(8,128)(2,1)} copy(bf16[256,32,128]{0,2,1:T(8,128)(2,1)} %get-tuple-element.10) | data formatting | bytes 4194304 | tf_op jit(solution)/shard_map/slice | solution.py:24
  51.8 4.6 %copy.34 = bf16[256,32,128]{2,1,0:T(8,128)(2,1)} copy(bf16[256,32,128]{0,2,1:T(8,128)(2,1)} %get-tuple-element.9) | data formatting | bytes 4194304 | tf_op jit(solution)/shard_map/slice | solution.py:24
  56.4 4.5 %copy.35 = bf16[256,32,128]{2,1,0:T(8,128)(2,1)} copy(bf16[256,32,128]{0,2,1:T(8,128)(2,1)} %get-tuple-element.5) | data formatting | bytes 4194304 | tf_op jit(solution)/shard_map/slice | solution.py:24
  60.9 4.6 %copy.36 = bf16[256,32,128]{2,1,0:T(8,128)(2,1)} copy(bf16[256,32,128]{0,2,1:T(8,128)(2,1)} %get-tuple-element.4) | data formatting | bytes 4194304 | tf_op jit(solution)/shard_map/slice | solution.py:24
  65.5 4.7 %copy.37 = bf16[256,32,128]{2,1,0:T(8,128)(2,1)} copy(bf16[256,32,128]{0,2,1:T(8,128)(2,1)} %get-tuple-element.3) | data formatting | bytes 4194304 | tf_op jit(solution)/shard_map/slice | solution.py:24
  70.2 3.0 fusion.110
  85.6 4.6 %copy.38 = bf16[256,32,256]{2,0,1:T(8,128)(2,1)} copy(bf16[256,32,256]{2,1,0:T(8,128)(2,1)S(1)} %bitcast.262) | data formatting | bytes 8388608 | tf_op jit(solution)/shard_map/convert_element_type | solution.py:83
  91.1 5.2 %collective-permute-start.6 = (bf16[1,32,256]{2,1,0:T(8,128)(2,1)S(1)}, bf16[1,32,256]{2,1,0:T(8,128)(2,1)S(1)}, u32[]{:S(2)}, u32[]{:S(2)}) collective-permute-start(bf16[1,32,256]{2,1,0:T(8,128)(2,1)S(1)} %get-tuple-element.40), channel_id=1, source_target_pairs={{0,16},{16,32},{32,48},{48,64},{64,80},{80,96},{96,112},{1,17},{17... | collective-permute-start | bytes 49160 | tf_op jit(solution)/shard_map/ppermute | solution.py:14
  96.3 1.9 collective-permute-start.7
  98.2 3.1 collective-permute-done.7
  104.6 4.0 collective-permute-start.9
  114.3 16.5 %reduce-scatter.2.cloned.1.call-done = bf16[32,32,256]{2,0,1:T(8,128)(2,1)} async-done(((bf16[256,32,256]{2,0,1:T(8,128)(2,1)}), bf16[32,32,256]{2,0,1:T(8,128)(2,1)}) %reduce-scatter.2.cloned.1.call-update) | async-done | bytes 524304 | tf_op jit(solution)/shard_map/reduce_scatter | solution.py:82
  130.8 3.1 fusion.57
  135.1 3.1 collective-permute-start.2
  138.1 3.8 collective-permute-start.3
  141.9 2.4 convolution_bitcast_fusion.4
  145.5 3.1 collective-permute-start.4
  154.8 1.9 fusion.146
  168.5 3.3 fusion.44
  191.6 72.7 %all-reduce.4.cloned.1.call-done = bf16[3,3,128,256]{3,2,1,0:T(8,128)(2,1)} async-done(((bf16[3,3,128,256]{3,2,1,0:T(8,128)(2,1)}), bf16[3,3,128,256]{3,2,1,0:T(8,128)(2,1)}) %all-reduce.4.cloned.1.call-update) | async-done | bytes 589840 | tf_op jit(solution)/shard_map/psum | solution.py:101
  264.4 2.2 convert_element_type.34
  266.6 154.7 %all-reduce.6.cloned.1.call-done = f32[3,3,256,256]{3,2,1,0:T(8,128)} async-done(((f32[3,3,256,256]{3,2,1,0:T(8,128)}), f32[3,3,256,256]{3,2,1,0:T(8,128)}) %all-reduce.6.cloned.1.call-update) | async-done | bytes 2359312 | tf_op jit(solution)/shard_map/psum | solution.py:102
  421.3 3.2 copy.95
  (148 shorter events, 63.2 us)
Async XLA Ops:
  7.2 123.6 %reduce-scatter.2.cloned.1.call-start = ((), (), s32[]{:S(2)}) async-start(), calls=%async_computation.1 | async-start | bytes 4718592 | tf_op jit(solution)/shard_map/reduce_scatter | solution.py:82
  10.2 5.3 %copy-start = (bf16[256,32,128]{0,2,1:T(8,128)(2,1)}, bf16[256,32,128]{0,2,1:T(8,128)(2,1)S(1)}, u32[]{:S(2)}) copy-start(bf16[256,32,128]{0,2,1:T(8,128)(2,1)S(1)} %copy.25) | copy-start | bytes 6291460
  10.2 5.3 %collective-permute-start = (bf16[256,1,128]{0,2,1:T(8,128)(2,1)S(1)}, bf16[256,1,128]{0,2,1:T(8,128)(2,1)S(1)}, u32[]{:S(2)}, u32[]{:S(2)}) collective-permute-start(bf16[256,1,128]{0,2,1:T(8,128)(2,1)S(1)} %get-tuple-element.11), channel_id=1, source_target_pairs={{0,1},{1,2},{2,3},{3,4},{4,5},{5,6},{6,7},{7,8},{8,9},{9,10},{10,1... | collective-permute-start | bytes 196616 | tf_op jit(solution)/shard_map/ppermute | solution.py:14
  14.2 5.0 %collective-permute-start.1 = (bf16[256,1,128]{0,2,1:T(8,128)(2,1)S(1)}, bf16[256,1,128]{0,2,1:T(8,128)(2,1)S(1)}, u32[]{:S(2)}, u32[]{:S(2)}) collective-permute-start(bf16[256,1,128]{0,2,1:T(8,128)(2,1)S(1)} %get-tuple-element.12), channel_id=1, source_target_pairs={{1,0},{2,1},{3,2},{4,3},{5,4},{6,5},{7,6},{8,7},{9,8},{10,9},{11,1... | collective-permute-start | bytes 196616 | tf_op jit(solution)/shard_map/ppermute | solution.py:15
  70.2 3.0 copy-start.7
  70.2 3.0 copy-start.24
  73.2 1.6 copy-start.5
  74.8 1.6 copy-start.8
  76.4 1.6 copy-start.2
  78.0 1.6 copy-start.6
  79.6 1.6 copy-start.4
  81.2 1.6 copy-start.3
  82.7 1.6 copy-start.10
  90.2 78.3 %all-gather.2.cloned.1.call-start = ((), (), s32[]{:S(2)}) async-start(), calls=%async_computation.2 | async-start | bytes 4718592 | tf_op jit(solution)/shard_map/all_gather | solution.py:97
  90.3 18.3 %copy-start.11 = (bf16[3,3,256,256]{3,2,1,0:T(8,128)(2,1)S(1)}, bf16[3,3,256,256]{3,2,1,0:T(8,128)(2,1)}, u32[]{:S(2)}) copy-start(bf16[3,3,256,256]{3,2,1,0:T(8,128)(2,1)} %param.6) | copy-start | bytes 3538948
  91.1 7.1 %collective-permute-start.6 = (bf16[1,32,256]{2,1,0:T(8,128)(2,1)S(1)}, bf16[1,32,256]{2,1,0:T(8,128)(2,1)S(1)}, u32[]{:S(2)}, u32[]{:S(2)}) collective-permute-start(bf16[1,32,256]{2,1,0:T(8,128)(2,1)S(1)} %get-tuple-element.40), channel_id=1, source_target_pairs={{0,16},{16,32},{32,48},{48,64},{64,80},{80,96},{96,112},{1,17},{17... | collective-permute-start | bytes 49160 | tf_op jit(solution)/shard_map/ppermute | solution.py:14
  96.3 5.1 %collective-permute-start.7 = (bf16[1,32,256]{2,1,0:T(8,128)(2,1)S(1)}, bf16[1,32,256]{2,1,0:T(8,128)(2,1)S(1)}, u32[]{:S(2)}, u32[]{:S(2)}) collective-permute-start(bf16[1,32,256]{2,1,0:T(8,128)(2,1)S(1)} %get-tuple-element.39), channel_id=1, source_target_pairs={{16,0},{32,16},{48,32},{64,48},{80,64},{96,80},{112,96},{17,1},{33... | collective-permute-start | bytes 49160 | tf_op jit(solution)/shard_map/ppermute | solution.py:15
  103.3 6.0 %collective-permute-start.8 = (bf16[34,1,256]{2,1,0:T(2,128)(2,1)S(1)}, bf16[34,1,256]{2,1,0:T(2,128)(2,1)S(1)}, u32[]{:S(2)}, u32[]{:S(2)}) collective-permute-start(bf16[34,1,256]{2,1,0:T(2,128)(2,1)S(1)} %get-tuple-element.32), channel_id=1, source_target_pairs={{1,0},{2,1},{3,2},{4,3},{5,4},{6,5},{7,6},{8,7},{9,8},{10,9},{11,1... | collective-permute-start | bytes 52232 | tf_op jit(solution)/shard_map/ppermute | solution.py:15
  104.6 5.0 %collective-permute-start.9 = (bf16[34,1,256]{2,1,0:T(2,128)(2,1)S(1)}, bf16[34,1,256]{2,1,0:T(2,128)(2,1)S(1)}, u32[]{:S(2)}, u32[]{:S(2)}) collective-permute-start(bf16[34,1,256]{2,1,0:T(2,128)(2,1)S(1)} %get-tuple-element.33), channel_id=1, source_target_pairs={{0,1},{1,2},{2,3},{3,4},{4,5},{5,6},{6,7},{7,8},{8,9},{9,10},{10,1... | collective-permute-start | bytes 52232 | tf_op jit(solution)/shard_map/ppermute | solution.py:14
  133.9 130.4 %all-reduce.4.cloned.1.call-start = ((), (), s32[]{:S(2)}) async-start(), calls=%async_computation.3 | async-start | bytes 1179648 | tf_op jit(solution)/shard_map/psum | solution.py:101
  134.0 10.4 %copy-start.9 = (bf16[32,32,256]{2,0,1:T(8,128)(2,1)S(1)}, bf16[32,32,256]{2,0,1:T(8,128)(2,1)}, u32[]{:S(2)}) copy-start(bf16[32,32,256]{2,0,1:T(8,128)(2,1)} %get-tuple-element.35) | copy-start | bytes 1572868
  135.1 10.4 %collective-permute-start.2 = (bf16[1,32,256]{2,0,1:T(2,128)(2,1)S(1)}, bf16[1,32,256]{2,0,1:T(2,128)(2,1)S(1)}, u32[]{:S(2)}, u32[]{:S(2)}) collective-permute-start(bf16[1,32,256]{2,0,1:T(2,128)(2,1)S(1)} %get-tuple-element.43), channel_id=1, source_target_pairs={{0,16},{16,32},{32,48},{48,64},{64,80},{80,96},{96,112},{1,17},{17... | collective-permute-start | bytes 49160 | tf_op jit(solution)/shard_map/ppermute | solution.py:14
  138.1 7.3 %collective-permute-start.3 = (bf16[1,32,256]{2,0,1:T(2,128)(2,1)S(1)}, bf16[1,32,256]{2,0,1:T(2,128)(2,1)S(1)}, u32[]{:S(2)}, u32[]{:S(2)}) collective-permute-start(bf16[1,32,256]{2,0,1:T(2,128)(2,1)S(1)} %get-tuple-element.44), channel_id=1, source_target_pairs={{16,0},{32,16},{48,32},{64,48},{80,64},{96,80},{112,96},{17,1},{33... | collective-permute-start | bytes 49160 | tf_op jit(solution)/shard_map/ppermute | solution.py:15
  144.3 6.0 %copy-start.16 = (bf16[32,32,256]{2,1,0:T(8,128)(2,1)S(1)}, bf16[32,32,256]{2,1,0:T(8,128)(2,1)}, u32[]{:S(2)}) copy-start(bf16[32,32,256]{2,1,0:T(8,128)(2,1)} %param.7) | copy-start | bytes 1572868
  145.5 8.8 %collective-permute-start.4 = (bf16[34,1,256]{2,0,1:T(8,128)(2,1)S(1)}, bf16[34,1,256]{2,0,1:T(8,128)(2,1)S(1)}, u32[]{:S(2)}, u32[]{:S(2)}) collective-permute-start(bf16[34,1,256]{2,0,1:T(8,128)(2,1)S(1)} %get-tuple-element.28), channel_id=1, source_target_pairs={{0,1},{1,2},{2,3},{3,4},{4,5},{5,6},{6,7},{7,8},{8,9},{9,10},{10,1... | collective-permute-start | bytes 52232 | tf_op jit(solution)/shard_map/ppermute | solution.py:14
  148.6 5.7 %collective-permute-start.5 = (bf16[34,1,256]{2,0,1:T(8,128)(2,1)S(1)}, bf16[34,1,256]{2,0,1:T(8,128)(2,1)S(1)}, u32[]{:S(2)}, u32[]{:S(2)}) collective-permute-start(bf16[34,1,256]{2,0,1:T(8,128)(2,1)S(1)} %get-tuple-element.27), channel_id=1, source_target_pairs={{1,0},{2,1},{3,2},{4,3},{5,4},{6,5},{7,6},{8,7},{9,8},{10,9},{11,1... | collective-permute-start | bytes 52232 | tf_op jit(solution)/shard_map/ppermute | solution.py:15
  168.5 3.4 copy-start.13
  175.6 1.6 copy-start.1
  180.6 1.6 copy-start.14
  180.7 240.6 %all-reduce.6.cloned.1.call-start = ((), (), s32[]{:S(2)}) async-start(), calls=%async_computation.4 | async-start | bytes 4718592 | tf_op jit(solution)/shard_map/psum | solution.py:102
  182.2 1.7 copy-start.12
  185.3 1.8 copy-start.22
  (12 other events, 14.1 us)
Sparse Core Ops, SparseCore 0:
  90.3 40.3 reduce-scatter.1
  134.0 34.3 all-gather.1
  180.8 83.5 all-reduce.3
  269.6 151.6 all-reduce.5
where the time goes:
time: 439 us; the launch traced here: 432 us
  waiting for transfers between devices  253 us (58%)
  local copies, waits for them, and re-layouts  70.6 us (16%)
  matrix products  42.9 us (10%)
  starting transfers between devices  29 us (7%)
  other arithmetic  21.6 us (5%)
  between operations  14.9 us (3%)
    psum x1, waiting for transfers between devices, body(): grad_second = lax.psum(second_part, ('freq', 'sky'))  155 us
    psum x1, waiting for transfers between devices, body(): lax.psum(first_part.astype(jnp.bfloat16), 'sky').astype(jnp.float32)  72.7 us
    slice x18, local copies, waits for them, and re-layouts, conv_taps(): padded[tap_col:tap_col + col_count, tap_row:tap_row + row_count]  51.2 us
    dot_general x18, matrix products, kernel_grad(): lax.dot_general(piece, flat, (((0,), (0,)), ((), ())), preferred_element_...  20.4 us
    ppermute x5, starting transfers between devices, with_halo(): before = lax.ppermute(last, axis, up)  19.3 us
    dot_general x18, matrix products, conv_taps(): jnp.dot(piece, kernel[tap_col, tap_row], preferred_element_type=jnp.float32)  18.5 us
    reduce_scatter x1, waiting for transfers between devices, body(): lax.psum_scatter(conv_taps(slab, weight_first, strip * lax.axis_size('fre...  16.5 us
    unnamed x63, local copies, waits for them, and re-layouts  11.6 us
  transfers between devices with their start and end apart: 14, of which 7 were waited for; matrix products, arithmetic and copies ran while one was open for 9% of the time, Pallas kernels for 0%

commit v1 on v0

v1 whole, which is shorter than its diff:
```python
import jax
import jax.numpy as jnp
from jax import lax
from jax.experimental import pallas as pl
from jax.experimental.pallas import tpu as pltpu
from jax.sharding import Mesh, PartitionSpec as P

FREQ = ("y", "c")
SKY = ("z", "x")
F32 = jnp.float32
BF16 = jnp.bfloat16
VMEM_LIMIT = 48 * 2**20


def shift(x, axis, step):
    count = lax.axis_size(axis)
    return lax.ppermute(x, axis, [(i, (i + step) % count) for i in range(count)])


def halo(x, axes, dim):
    count, length = lax.axis_size(axes), x.shape[dim]
    up = [(i, i + 1) for i in range(count - 1)]
    down = [(j, i) for i, j in up]
    last = lax.slice_in_dim(x, length - 1, length, axis=dim)
    first = lax.slice_in_dim(x, 0, 1, axis=dim)
    return lax.ppermute(last, axes, up), lax.ppermute(first, axes, down)


def with_halo(x):
    for axes, dim in ((FREQ, 0), (SKY, 1)):
        before, after = halo(x, axes, dim)
        x = jnp.concatenate([before, x, after], axis=dim)
    return x


def spread_kernel(cube_ref, before_ref, after_ref, out_ref):
    cols, rows, chans = cube_ref.shape
    zero = jnp.zeros((1, rows, 3 * chans), BF16)
    out_ref[0:1] = zero
    for tail in range(cols + 1, out_ref.shape[0]):
        out_ref[tail : tail + 1] = zero
    step = 8

    def block(i, _):
        at = pl.multiple_of(i * step, step)
        mid = cube_ref[pl.ds(at, step)]
        wide = mid.astype(F32).reshape(step * rows, chans)
        row = lax.broadcasted_iota(jnp.int32, (step, rows, chans), 1)
        ahead = pltpu.roll(wide, 1, 0).reshape(step, rows, chans)
        behind = pltpu.roll(wide, step * rows - 1, 0).reshape(step, rows, chans)
        before = before_ref[pl.ds(at, step), :].astype(F32)[:, None, :]
        after = after_ref[pl.ds(at, step), :].astype(F32)[:, None, :]
        ahead = jnp.where(row == 0, before, ahead)
        behind = jnp.where(row == rows - 1, after, behind)
        out_ref[pl.ds(at + 1, step), :, 0:chans] = ahead.astype(BF16)
        out_ref[pl.ds(at + 1, step), :, chans : 2 * chans] = mid
        out_ref[pl.ds(at + 1, step), :, 2 * chans : 3 * chans] = behind.astype(BF16)
        return 0

    lax.fori_loop(0, cols // step, block, 0)


def spread(cube, before, after):
    cols, rows, chans = cube.shape
    return pl.pallas_call(
        spread_kernel,
        out_shape=jax.ShapeDtypeStruct((cols + 8, rows, 3 * chans), BF16),
        in_specs=[pl.BlockSpec(memory_space=pltpu.VMEM)] * 3,
        out_specs=pl.BlockSpec(memory_space=pltpu.VMEM),
        compiler_params=pltpu.CompilerParams(vmem_limit_bytes=VMEM_LIMIT),
        name="spread",
    )(cube, before, after)


def conv_kernel(group_ref, wide_ref, kernel_ref, near_ref, far_ref):
    del group_ref
    strip, rows, outs = near_ref.shape
    step = 8
    core = lax.axis_index("c")

    def block(i, ref, base):
        at = base + i * step
        pieces = [wide_ref[pl.ds(at + tap, step)] for tap in range(3)]
        lhs = jnp.concatenate(pieces, axis=-1).reshape(step * rows, -1)
        total = jnp.dot(lhs, kernel_ref[...], preferred_element_type=F32)
        ref[pl.ds(i * step, step)] = total.reshape(step, rows, outs).astype(ref.dtype)
        return 0

    count = strip // step
    lax.fori_loop(0, count, lambda i, _: block(i, far_ref, (1 - core) * strip), 0)
    lax.fori_loop(0, count, lambda i, _: block(i, near_ref, core * strip), 0)


def conv_group(group, wide, kernel, strip):
    rows, depth, outs = wide.shape[1], wide.shape[2], kernel.shape[1]
    window = (pl.Element(2 * strip + 2), pl.Element(rows), pl.Element(depth))
    shape = (strip, rows, outs)
    return pl.pallas_call(
        conv_kernel,
        out_shape=(jax.ShapeDtypeStruct(shape, F32), jax.ShapeDtypeStruct(shape, BF16)),
        grid_spec=pltpu.PrefetchScalarGridSpec(
            num_scalar_prefetch=1,
            grid=(1,),
            in_specs=[
                pl.BlockSpec(window, lambda i, g: (g[0] * 2 * strip, 0, 0)),
                pl.BlockSpec(kernel.shape, lambda i, g: (0, 0)),
            ],
            out_specs=[pl.BlockSpec(shape, lambda i, g: (0, 0, 0))] * 2,
        ),
        compiler_params=pltpu.CompilerParams(vmem_limit_bytes=VMEM_LIMIT),
        cost_estimate=pl.CostEstimate(
            flops=4 * strip * rows * 3 * depth * outs, bytes_accessed=4 * 2**20, transcendentals=0
        ),
        name="conv_first",
    )(group.reshape(1), wide, kernel)


def grad_kernel(strips_ref, wide_a, wide_b, delta_a, delta_b, old_ref, new_ref, pad_ref):
    del strips_ref
    strip, rows, outs = delta_a.shape
    zero = jnp.zeros((2, rows, outs), BF16)
    total = old_ref[...]
    for wide_ref, delta_ref in ((wide_a, delta_a), (wide_b, delta_b)):
        cols = wide_ref.shape[0]
        pad_ref[0:2] = zero
        pad_ref[2 : 2 + strip] = delta_ref[...]
        pad_ref[2 + strip :] = jnp.zeros((pad_ref.shape[0] - 2 - strip, rows, outs), BF16)
        lhs = wide_ref[...].reshape(cols * rows, -1)
        rhs = jnp.concatenate(
            [pad_ref[2 - tap : 2 - tap + cols].reshape(cols * rows, outs) for tap in range(3)],
            axis=-1,
        )
        total = total + lax.dot_general(
            lhs, rhs, (((0,), (0,)), ((), ())), preferred_element_type=F32
        )
    new_ref[...] = total


def grad_strips(wide, deltas, strips, old):
    strip, rows, outs = deltas[0].shape
    depth = wide.shape[2]
    cols = strip + 8
    window = (pl.Element(cols), pl.Element(rows), pl.Element(depth))
    dspec = pl.BlockSpec((strip, rows, outs), lambda i, s: (0, 0, 0))
    tspec = pl.BlockSpec(old.shape, lambda i, s: (0, 0))
    return pl.pallas_call(
        grad_kernel,
        out_shape=jax.ShapeDtypeStruct(old.shape, F32),
        grid_spec=pltpu.PrefetchScalarGridSpec(
            num_scalar_prefetch=1,
            grid=(1,),
            in_specs=[
                pl.BlockSpec(window, lambda i, s: (s[0] * strip, 0, 0)),
                pl.BlockSpec(window, lambda i, s: (s[1] * strip, 0, 0)),
                dspec,
                dspec,
                tspec,
            ],
            out_specs=tspec,
            scratch_shapes=[pltpu.VMEM((cols + 2, rows, outs), BF16)],
        ),
        compiler_params=pltpu.CompilerParams(vmem_limit_bytes=VMEM_LIMIT),
        cost_estimate=pl.CostEstimate(
            flops=4 * cols * rows * depth * 3 * outs, bytes_accessed=6 * 2**20, transcendentals=0
        ),
        input_output_aliases={5: 0},
        name="grad_first",
    )(jnp.stack(strips), wide, wide, deltas[0], deltas[1], old)


def conv_taps(padded, kernel, col_count, row_count):
    total = jnp.zeros((col_count * row_count, kernel.shape[3]), F32)
    for tap_col in range(3):
        for tap_row in range(3):
            piece = padded[tap_col : tap_col + col_count, tap_row : tap_row + row_count].reshape(
                col_count * row_count, -1
            )
            total = total + jnp.dot(piece, kernel[tap_col, tap_row], preferred_element_type=F32)
    return total.reshape(col_count, row_count, kernel.shape[3])


def conv_back(padded, kernel, col_count, row_count):
    total = jnp.zeros((col_count * row_count, kernel.shape[2]), F32)
    for tap_col in range(3):
        for tap_row in range(3):
            piece = padded[
                2 - tap_col : 2 - tap_col + col_count, 2 - tap_row : 2 - tap_row + row_count
            ].reshape(col_count * row_count, -1)
            total = total + lax.dot_general(
                piece,
                kernel[tap_col, tap_row],
                (((1,), (1,)), ((), ())),
                preferred_element_type=F32,
            )
    return total.reshape(col_count, row_count, kernel.shape[2])


def kernel_grad(padded, grads, col_count, row_count):
    flat = grads.reshape(col_count * row_count, -1)
    lines = []
    for tap_col in range(3):
        for tap_row in range(3):
            piece = padded[tap_col : tap_col + col_count, tap_row : tap_row + row_count].reshape(
                col_count * row_count, -1
            )
            lines.append(
                lax.dot_general(piece, flat, (((0,), (0,)), ((), ())), preferred_element_type=F32)
            )
    return jnp.concatenate(lines, axis=0)


def reduce_pieces(parts, axis):
    count = lax.axis_size(axis)
    me = lax.axis_index(axis)

    def pick(at):
        return lax.dynamic_index_in_dim(parts, at, 0, keepdims=False)

    total = pick(me)
    for step in (1, count - 1, 2) if count == 4 else range(1, count):
        total = total + shift(pick((me + step) % count).astype(BF16), axis, step).astype(F32)
    return total


def gather_pieces(piece, axis):
    count = lax.axis_size(axis)
    me = lax.axis_index(axis)
    got = {0: piece}
    for step in (1, count - 1, 2) if count == 4 else range(1, count):
        got[step] = shift(piece, axis, step)
    turned = jnp.stack([got[(-j) % count] for j in range(count)] * 2)
    return lax.dynamic_slice_in_dim(turned, count - me, count, 0)


def body(sky_cube, weight_first, weight_second, cotangent):
    cols, rows, chans = sky_cube.shape
    strip, _, outs = cotangent.shape
    here, core = lax.axis_index("y"), lax.axis_index("c")
    chips = lax.axis_size("y")

    before, after = halo(sky_cube, SKY, 1)
    wide = spread(sky_cube, before.reshape(cols, chans), after.reshape(cols, chans))
    kernel = weight_first.reshape(9 * chans, outs)

    pre = None
    sent = []
    for step in (2, 1, chips - 1, 0):
        near, far = conv_group((here + step) % chips, wide, kernel, strip)
        both = near + shift(far, "c", 1).astype(F32)
        sent.append(shift(both.astype(BF16), "y", step).astype(F32) if step else both)
    pre = sent[3] + sent[0] + sent[1] + sent[2]

    back = conv_back(with_halo(cotangent), weight_second, strip, rows)
    sigma = jax.nn.sigmoid(pre)
    delta = (back * (sigma * (1.0 + pre * (1.0 - sigma)))).astype(BF16)
    hidden = (pre * sigma).astype(BF16)

    total = jnp.zeros((3 * chans, 3 * outs), F32)
    for step in (0, 1, chips - 1, 2):
        mine = shift(delta, "y", step) if step else delta
        other = shift(mine, "c", 1)
        chip = (here - step) % chips
        strips = [2 * chip + core, 2 * chip + 1 - core]
        total = grad_strips(wide, [mine, other], strips, total)

    hidden_pad = with_halo(hidden)
    features = conv_taps(hidden_pad, weight_second, strip, rows).astype(BF16)
    second = kernel_grad(hidden_pad, cotangent, strip, rows)
    depth = second.shape[0]
    second = reduce_pieces(second.reshape(2, depth // 2, outs), "c")
    second = reduce_pieces(second.reshape(chips, depth // (2 * chips), outs), "y")

    sx, sz = lax.axis_size("x"), lax.axis_size("z")
    width = 3 * outs
    first_parts = total.reshape(sx, -1, width)
    second_parts = second.reshape(sx, -1, width)
    split = first_parts.shape[1] // sz
    joined = jnp.concatenate(
        [first_parts.reshape(sx, sz, -1, width), second_parts.reshape(sx, sz, -1, width)], axis=2
    )
    summed = reduce_pieces(joined, "x")
    summed = reduce_pieces(summed, "z").astype(BF16)
    summed = gather_pieces(gather_pieces(summed, "z"), "x")
    first = summed[:, :, :split].reshape(3, chans, 3, outs)
    grad_first = jnp.transpose(first, (2, 0, 1, 3)).astype(F32)
    share = summed[:, :, split:].reshape(depth // (2 * chips), outs)
    share = gather_pieces(gather_pieces(share, "y"), "c")
    grad_second = share.reshape(3, 3, outs, outs).astype(F32)
    return features, grad_first, grad_second


def solution(mesh):
    sizes = (mesh.devices.shape[0] // 2, 2, 4, mesh.devices.shape[1] // 4)
    fine = Mesh(mesh.devices.reshape(sizes), FREQ + SKY)
    return jax.shard_map(
        body,
        mesh=fine,
        in_specs=(P(None, SKY, FREQ), P(None, None, FREQ, None), P(), P(FREQ, SKY, None)),
        out_specs=(P(FREQ, SKY, None), P(None, None, FREQ, None), P()),
        check_vma=False,
    )
```

time: 439 us -> 208 us (0.47); the launches traced: 432 us -> 207 us
  waiting for transfers between devices: 253 us -> 49.6 us
  local copies, waits for them, and re-layouts: 70.6 us -> 13.7 us
  starting transfers between devices: 29 us -> 83.6 us
  Pallas kernels: 0 us -> 36.8 us
  matrix products: 42.9 us -> 13.4 us
  between operations: 14.9 us -> 1.73 us
  other arithmetic: 21.6 us -> 8.66 us
    psum x2 -> x0, waiting for transfers between devices: 227 us -> none  [the longest x1 155 us: body(): grad_second = lax.psum(second_part, ('freq', 'sky'))]
    ppermute x10 -> x44, starting transfers between devices: 28.9 us -> 83.6 us  [the longest x34 55.6 us: shift(): lax.ppermute(x, axis, [(i, (i + step) % count) for i in range(count)])]
    slice x18 -> x1, local copies, waits for them, and re-layouts: 51.2 us -> 1.64 us  [conv_taps(): padded[tap_col:tap_col + col_count, tap_row:tap_row + row_count]]
    ppermute x10 -> x44, waiting for transfers between devices: 7.16 us -> 49.6 us  [the longest x34 47.8 us: shift(): lax.ppermute(x, axis, [(i, (i + step) % count) for i in range(count)])]
    pallas_call x0 -> x9, Pallas kernels: none -> 36.8 us  [the longest x4 16.5 us: conv_group(): pl.pallas_call(conv_kernel, out_shape=(jax.ShapeDtypeStruct(shape, F32),...]
    dot_general x18 -> x9, matrix products: 20.4 us -> 3.13 us  [kernel_grad(): lax.dot_general(piece, flat, (((0,), (0,)), ((), ())), preferred_element_...]
    reduce_scatter x1 -> x0, waiting for transfers between devices: 16.5 us -> none  [body(): lax.psum_scatter(conv_taps(slab, weight_first, strip * lax.axis_size('fre...]
    dot_general x18 -> x9, matrix products: 18.5 us -> 7.28 us  [conv_taps(): jnp.dot(piece, kernel[tap_col, tap_row], preferred_element_type=F32)]
  transfers between devices with their start and end apart: 14 -> 44, of which waited for: 7 -> 15; matrix products, arithmetic and copies ran while one was open for 9% -> 13% of each run, Pallas kernels for 0% -> 12%
where the time goes in v1:
time: 208 us; the launch traced here: 207 us
  starting transfers between devices  83.6 us (40%)
  waiting for transfers between devices  49.6 us (24%)
  Pallas kernels  36.8 us (18%)
  local copies, waits for them, and re-layouts  13.7 us (7%)
  matrix products  13.4 us (6%)
  other arithmetic  8.66 us (4%)
    ppermute x34, starting transfers between devices, shift(): lax.ppermute(x, axis, [(i, (i + step) % count) for i in range(count)])  55.6 us
    ppermute x34, waiting for transfers between devices, shift(): lax.ppermute(x, axis, [(i, (i + step) % count) for i in range(count)])  47.8 us
    ppermute x10, starting transfers between devices, halo(): return (lax.ppermute(last, axes, up), lax.ppermute(first, axes, down))  28 us
    pallas_call x4, Pallas kernels, conv_group(): pl.pallas_call(conv_kernel, out_shape=(jax.ShapeDtypeStruct(shape, F32),...  16.5 us
    pallas_call x4, Pallas kernels, grad_strips(): pl.pallas_call(grad_kernel, out_shape=jax.ShapeDtypeStruct(old.shape, F32...  15.9 us
    dot_general x9, matrix products, conv_taps(): jnp.dot(piece, kernel[tap_col, tap_row], preferred_element_type=F32)  7.28 us
    pallas_call x1, Pallas kernels, spread(): pl.pallas_call(spread_kernel, out_shape=jax.ShapeDtypeStruct((cols + 8, r...  4.3 us
    unnamed x62, local copies, waits for them, and re-layouts  4.26 us
  transfers between devices with their start and end apart: 44, of which 15 were waited for; matrix products, arithmetic and copies ran while one was open for 13% of the time, Pallas kernels for 12%

profile of v1, /device:TPU:1, one launch (start us, length us, event | category | flops | bytes accessed | tf_op | source)
XLA Modules:
  0.0 207.4 jit_solution(14074851489341822927)
XLA Ops:
  1.4 3.3 %collective-permute-start.14 = (bf16[1,32,256]{2,1,0:T(8,128)(2,1)S(1)}, bf16[1,32,256]{2,1,0:T(8,128)(2,1)S(1)}, u32[]{:S(2)}, u32[]{:S(2)}) collective-permute-start(bf16[1,32,256]{2,1,0:T(8,128)(2,1)S(1)} %get-tuple-element.60), channel_id=1, source_target_pairs={{16,0},{32,16},{48,32},{64,48},{80,64},{96,80},{112,96},{17,1},{33... | collective-permute-start | bytes 49160 | tf_op jit(solution)/shard_map/ppermute | solution.py:26
  4.8 3.2 %collective-permute-start.13 = (bf16[1,32,256]{2,1,0:T(8,128)(2,1)S(1)}, bf16[1,32,256]{2,1,0:T(8,128)(2,1)S(1)}, u32[]{:S(2)}, u32[]{:S(2)}) collective-permute-start(bf16[1,32,256]{2,1,0:T(8,128)(2,1)S(1)} %get-tuple-element.61), channel_id=1, source_target_pairs={{0,16},{16,32},{32,48},{48,64},{64,80},{80,96},{96,112},{1,17},{17... | collective-permute-start | bytes 49160 | tf_op jit(solution)/shard_map/ppermute | solution.py:26
  9.4 3.1 %collective-permute-start = (bf16[256,1,128]{2,0,1:T(8,128)(2,1)S(1)}, bf16[256,1,128]{2,0,1:T(8,128)(2,1)S(1)}, u32[]{:S(2)}, u32[]{:S(2)}) collective-permute-start(bf16[256,1,128]{2,0,1:T(8,128)(2,1)S(1)} %copy.16), channel_id=1, source_target_pairs={{0,1},{1,2},{2,3},{3,4},{4,5},{5,6},{6,7},{7,8},{8,9},{9,10},{10,1... | collective-permute-start | bytes 196616 | tf_op jit(solution)/shard_map/ppermute | solution.py:26
  15.8 4.6 %collective-permute-start.16 = (bf16[34,1,256]{2,1,0:T(2,128)(2,1)S(1)}, bf16[34,1,256]{2,1,0:T(2,128)(2,1)S(1)}, u32[]{:S(2)}, u32[]{:S(2)}) collective-permute-start(bf16[34,1,256]{2,1,0:T(2,128)(2,1)S(1)} %get-tuple-element.52), channel_id=1, source_target_pairs={{0,1},{1,2},{2,3},{3,4},{4,5},{5,6},{6,7},{7,8},{8,9},{9,10},{10,1... | collective-permute-start | bytes 52232 | tf_op jit(solution)/shard_map/ppermute | solution.py:26
  25.0 4.3 %spread.1.wide_ref.wide_a.wide_b = bf16[264,32,384]{2,1,0:T(8,128)(2,1)} custom-call(bf16[256,32,128]{2,1,0:T(8,128)(2,1)S(1)} %copy-done.1, bf16[256,128]{1,0:T(8,128)(2,1)S(1)} %bitcast.239, bf16[256,128]{1,0:T(8,128)(2,1)S(1)} %bitcast.240), custom_call_target="tpu_custom_call" | custom-call | tf_op jit(solution)/shard_map/spread/pallas_call | solution.py:65
  29.3 4.1 %conv_first.7 = (f32[32,32,256]{2,1,0:T(8,128)S(1)}, bf16[32,32,256]{2,1,0:T(8,128)(2,1)S(1)}) custom-call(s32[1]{0:T(128)} %bitcast.6.group_ref, bf16[264,32,384]{2,1,0:T(8,128)(2,1)} %spread.1.wide_ref.wide_a.wide_b, bf16[1152,256]{1,0:T(8,128)(2,1)S(1)} %bitcast.235), custom_call_target="tpu_custom_call" | custom-call | flops 1207959552 | bytes 4194304 | tf_op jit(solution)/shard_map/conv_first/pallas_call | solution.py:98
  34.2 4.1 %conv_first.6 = (f32[32,32,256]{2,1,0:T(8,128)S(1)}, bf16[32,32,256]{2,1,0:T(8,128)(2,1)S(1)}) custom-call(s32[1]{0:T(128)} %bitcast.5.group_ref, bf16[264,32,384]{2,1,0:T(8,128)(2,1)} %spread.1.wide_ref.wide_a.wide_b, bf16[1152,256]{1,0:T(8,128)(2,1)S(1)} %bitcast.236), custom_call_target="tpu_custom_call" | custom-call | flops 1207959552 | bytes 4194304 | tf_op jit(solution)/shard_map/conv_first/pallas_call | solution.py:98
  38.8 4.1 %conv_first.5 = (f32[32,32,256]{2,1,0:T(8,128)S(1)}, bf16[32,32,256]{2,1,0:T(8,128)(2,1)S(1)}) custom-call(s32[1]{0:T(128)} %bitcast.4.group_ref, bf16[264,32,384]{2,1,0:T(8,128)(2,1)} %spread.1.wide_ref.wide_a.wide_b, bf16[1152,256]{1,0:T(8,128)(2,1)S(1)} %bitcast.237), custom_call_target="tpu_custom_call" | custom-call | flops 1207959552 | bytes 4194304 | tf_op jit(solution)/shard_map/conv_first/pallas_call | solution.py:98
  43.5 4.1 %conv_first.4 = (f32[32,32,256]{2,1,0:T(8,128)S(1)}, bf16[32,32,256]{2,1,0:T(8,128)(2,1)S(1)}) custom-call(s32[1]{0:T(128)} %bitcast.group_ref, bf16[264,32,384]{2,1,0:T(8,128)(2,1)} %spread.1.wide_ref.wide_a.wide_b, bf16[1152,256]{1,0:T(8,128)(2,1)S(1)} %bitcast.238), custom_call_target="tpu_custom_call" | custom-call | flops 1207959552 | bytes 4194304 | tf_op jit(solution)/shard_map/conv_first/pallas_call | solution.py:98
  47.9 2.8 %collective-permute-start.8 = (bf16[32,32,256]{2,1,0:T(8,128)(2,1)S(1)}, bf16[32,32,256]{2,1,0:T(8,128)(2,1)S(1)}, u32[]{:S(2)}, u32[]{:S(2)}) collective-permute-start(bf16[32,32,256]{2,1,0:T(8,128)(2,1)S(1)} %add_convert_fusion), channel_id=1, source_target_pairs={{0,96},{32,0},{64,32},{96,64},{1,97},{33,1},{65,33},{97,65},{2,98}... | collective-permute-start | bytes 1572872 | tf_op jit(solution)/shard_map/ppermute | solution.py:17
  53.6 19.1 %collective-permute-done.8 = bf16[32,32,256]{2,1,0:T(8,128)(2,1)S(1)} collective-permute-done((bf16[32,32,256]{2,1,0:T(8,128)(2,1)S(1)}, bf16[32,32,256]{2,1,0:T(8,128)(2,1)S(1)}, u32[]{:S(2)}, u32[]{:S(2)}) %collective-permute-start.8) | collective-permute-done | bytes 524320 | tf_op jit(solution)/shard_map/ppermute | solution.py:17
  72.6 2.5 %collective-permute-done.4 = bf16[32,32,256]{2,1,0:T(8,128)(2,1)S(1)} collective-permute-done((bf16[32,32,256]{2,1,0:T(8,128)(2,1)S(1)}, bf16[32,32,256]{2,1,0:T(8,128)(2,1)S(1)}, u32[]{:S(2)}, u32[]{:S(2)}) %collective-permute-start.4) | collective-permute-done | bytes 524320 | tf_op jit(solution)/shard_map/ppermute | solution.py:17
  75.9 2.5 %collective-permute-start.9 = (bf16[1,32,256]{2,1,0:T(8,128)(2,1)S(1)}, bf16[1,32,256]{2,1,0:T(8,128)(2,1)S(1)}, u32[]{:S(2)}, u32[]{:S(2)}) collective-permute-start(bf16[1,32,256]{2,1,0:T(8,128)(2,1)S(1)} %get-tuple-element.64), channel_id=1, source_target_pairs={{0,16},{16,32},{32,48},{48,64},{64,80},{80,96},{96,112},{1,17},{17... | collective-permute-start | bytes 49160 | tf_op jit(solution)/shard_map/ppermute | solution.py:26
  78.4 3.3 %collective-permute-start.10 = (bf16[1,32,256]{2,1,0:T(8,128)(2,1)S(1)}, bf16[1,32,256]{2,1,0:T(8,128)(2,1)S(1)}, u32[]{:S(2)}, u32[]{:S(2)}) collective-permute-start(bf16[1,32,256]{2,1,0:T(8,128)(2,1)S(1)} %get-tuple-element.65), channel_id=1, source_target_pairs={{16,0},{32,16},{48,32},{64,48},{80,64},{96,80},{112,96},{17,1},{33... | collective-permute-start | bytes 49160 | tf_op jit(solution)/shard_map/ppermute | solution.py:26
  82.5 2.2 %collective-permute-start.19 = (bf16[32,32,256]{2,1,0:T(8,128)(2,1)S(1)}, bf16[32,32,256]{2,1,0:T(8,128)(2,1)S(1)}, u32[]{:S(2)}, u32[]{:S(2)}) collective-permute-start(bf16[32,32,256]{2,1,0:T(8,128)(2,1)S(1)} %get-tuple-element.26.delta_a), channel_id=1, source_target_pairs={{0,96},{32,0},{64,32},{96,64},{1,97},{33,1},{65,33},{97,65},{2,98}... | collective-permute-start | bytes 1572872 | tf_op jit(solution)/shard_map/ppermute | solution.py:17
  84.8 3.9 %collective-permute-start.11 = (bf16[34,1,256]{2,1,0:T(2,128)(2,1)S(1)}, bf16[34,1,256]{2,1,0:T(2,128)(2,1)S(1)}, u32[]{:S(2)}, u32[]{:S(2)}) collective-permute-start(bf16[34,1,256]{2,1,0:T(2,128)(2,1)S(1)} %get-tuple-element.55), channel_id=1, source_target_pairs={{0,1},{1,2},{2,3},{3,4},{4,5},{5,6},{6,7},{7,8},{8,9},{9,10},{10,1... | collective-permute-start | bytes 52232 | tf_op jit(solution)/shard_map/ppermute | solution.py:26
  102.7 5.3 %collective-permute-start.25 = (bf16[288,256]{1,0:T(8,128)(2,1)S(1)}, bf16[288,256]{1,0:T(8,128)(2,1)S(1)}, u32[]{:S(2)}, u32[]{:S(2)}) collective-permute-start(bf16[288,256]{1,0:T(8,128)(2,1)S(1)} %get-tuple-element.33), channel_id=1, source_target_pairs={{0,32},{32,64},{64,96},{96,0},{1,33},{33,65},{65,97},{97,1},{2,34}... | collective-permute-start | bytes 442376 | tf_op jit(solution)/shard_map/ppermute | solution.py:17
  108.0 2.6 %collective-permute-start.27 = (bf16[288,256]{1,0:T(8,128)(2,1)S(1)}, bf16[288,256]{1,0:T(8,128)(2,1)S(1)}, u32[]{:S(2)}, u32[]{:S(2)}) collective-permute-start(bf16[288,256]{1,0:T(8,128)(2,1)S(1)} %get-tuple-element.34), channel_id=1, source_target_pairs={{0,64},{32,96},{64,0},{96,32},{1,65},{33,97},{65,1},{97,33},{2,66}... | collective-permute-start | bytes 442376 | tf_op jit(solution)/shard_map/ppermute | solution.py:17
  115.6 3.9 %grad_first.4.old_ref = f32[384,768]{1,0:T(8,128)S(1)} custom-call(s32[2]{0:T(128)S(1)} %pad_add_fusion.3.strips_ref, bf16[264,32,384]{2,1,0:T(8,128)(2,1)} %spread.1.wide_ref.wide_a.wide_b, bf16[264,32,384]{2,1,0:T(8,128)(2,1)} %spread.1.wide_ref.wide_a.wide_b, bf16[32,32,256]{2,1,0:T(8,128)(2,1)S(1)} %get-tuple-element.26.delta_a, ...), custom_call_target="tpu_custom_call", output_to_operand_aliasing={{}: (5, {})} | custom-call | flops 1509949440 | bytes 6291456 | tf_op jit(solution)/shard_map/grad_first/pallas_call | solution.py:146
  122.3 4.0 %grad_first.5.old_ref = f32[384,768]{1,0:T(8,128)S(1)} custom-call(s32[2]{0:T(128)S(1)} %pad_add_fusion.2.strips_ref, bf16[264,32,384]{2,1,0:T(8,128)(2,1)} %spread.1.wide_ref.wide_a.wide_b, bf16[264,32,384]{2,1,0:T(8,128)(2,1)} %spread.1.wide_ref.wide_a.wide_b, ...), custom_call_target="tpu_custom_call", output_to_operand_aliasing={{}: (5, {})} | custom-call | flops 1509949440 | bytes 6291456 | tf_op jit(solution)/shard_map/grad_first/pallas_call | solution.py:146
  126.4 4.0 %grad_first.6.old_ref = f32[384,768]{1,0:T(8,128)S(1)} custom-call(s32[2]{0:T(128)S(1)} %pad_add_fusion.1.strips_ref, bf16[264,32,384]{2,1,0:T(8,128)(2,1)} %spread.1.wide_ref.wide_a.wide_b, bf16[264,32,384]{2,1,0:T(8,128)(2,1)} %spread.1.wide_ref.wide_a.wide_b, ...), custom_call_target="tpu_custom_call", output_to_operand_aliasing={{}: (5, {})} | custom-call | flops 1509949440 | bytes 6291456 | tf_op jit(solution)/shard_map/grad_first/pallas_call | solution.py:146
  130.5 3.9 %grad_first.7 = f32[384,768]{1,0:T(8,128)S(1)} custom-call(s32[2]{0:T(128)S(1)} %pad_add_fusion.strips_ref, bf16[264,32,384]{2,1,0:T(8,128)(2,1)} %spread.1.wide_ref.wide_a.wide_b, bf16[264,32,384]{2,1,0:T(8,128)(2,1)} %spread.1.wide_ref.wide_a.wide_b, bf16[32,32,256]{2,1,0:T(8,128)(2,1)S(1)} %collective-permute-done.17.delta_a, ...), custom_call_target="tpu_custom_call", output_to_operand_aliasing={{}: (5, {})} | custom-call | flops 1509949440 | bytes 6291456 | tf_op jit(solution)/shard_map/grad_first/pallas_call | solution.py:146
  134.5 2.3 %collective-permute-start.28 = (bf16[4,30,768]{2,1,0:T(8,128)(2,1)S(1)}, bf16[4,30,768]{2,1,0:T(8,128)(2,1)S(1)}, u32[]{:S(2)}, u32[]{:S(2)}) collective-permute-start(bf16[4,30,768]{2,1,0:T(8,128)(2,1)S(1)} %get-tuple-element.30), channel_id=1, source_target_pairs={{0,1},{1,2},{2,3},{3,0},{4,5},{5,6},{6,7},{7,4},{8,9},{9,10},{10,1... | collective-permute-start | bytes 552968 | tf_op jit(solution)/shard_map/ppermute | solution.py:17
  140.7 2.5 %collective-permute-done.28 = bf16[4,30,768]{2,1,0:T(8,128)(2,1)S(1)} collective-permute-done((bf16[4,30,768]{2,1,0:T(8,128)(2,1)S(1)}, bf16[4,30,768]{2,1,0:T(8,128)(2,1)S(1)}, u32[]{:S(2)}, u32[]{:S(2)}) %collective-permute-start.28) | collective-permute-done | bytes 184352 | tf_op jit(solution)/shard_map/ppermute | solution.py:17
  143.2 5.1 %collective-permute-done.30 = bf16[4,30,768]{2,1,0:T(8,128)(2,1)S(1)} collective-permute-done((bf16[4,30,768]{2,1,0:T(8,128)(2,1)S(1)}, bf16[4,30,768]{2,1,0:T(8,128)(2,1)S(1)}, u32[]{:S(2)}, u32[]{:S(2)}) %collective-permute-start.30) | collective-permute-done | bytes 184352 | tf_op jit(solution)/shard_map/ppermute | solution.py:17
  148.3 7.0 %collective-permute-start.31 = (bf16[30,768]{1,0:T(8,128)(2,1)S(1)}, bf16[30,768]{1,0:T(8,128)(2,1)S(1)}, u32[]{:S(2)}, u32[]{:S(2)}) collective-permute-start(bf16[30,768]{1,0:T(8,128)(2,1)S(1)} %get-tuple-element.66), channel_id=1, source_target_pairs={{0,4},{4,8},{8,12},{12,0},{1,5},{5,9},{9,13},{13,1},{2,6},{6,10},{... | collective-permute-start | bytes 138248 | tf_op jit(solution)/shard_map/ppermute | solution.py:17
  155.4 3.6 %collective-permute-start.33 = (bf16[30,768]{1,0:T(8,128)(2,1)S(1)}, bf16[30,768]{1,0:T(8,128)(2,1)S(1)}, u32[]{:S(2)}, u32[]{:S(2)}) collective-permute-start(bf16[30,768]{1,0:T(8,128)(2,1)S(1)} %get-tuple-element.67), channel_id=1, source_target_pairs={{0,8},{4,12},{8,0},{12,4},{1,9},{5,13},{9,1},{13,5},{2,10},{6,14},... | collective-permute-start | bytes 138248 | tf_op jit(solution)/shard_map/ppermute | solution.py:17
  165.6 3.3 %collective-permute-done.35 = bf16[30,768]{1,0:T(8,128)(2,1)S(1)} collective-permute-done((bf16[30,768]{1,0:T(8,128)(2,1)S(1)}, bf16[30,768]{1,0:T(8,128)(2,1)S(1)}, u32[]{:S(2)}, u32[]{:S(2)}) %collective-permute-start.35) | collective-permute-done | bytes 46112 | tf_op jit(solution)/shard_map/ppermute | solution.py:17
  169.0 2.5 %collective-permute-start.37 = (bf16[4,30,768]{2,1,0:T(8,128)(2,1)S(1)}, bf16[4,30,768]{2,1,0:T(8,128)(2,1)S(1)}, u32[]{:S(2)}, u32[]{:S(2)}) collective-permute-start(bf16[4,30,768]{2,1,0:T(8,128)(2,1)S(1)} %get-tuple-element.23), channel_id=1, source_target_pairs={{0,3},{1,0},{2,1},{3,2},{4,7},{5,4},{6,5},{7,6},{8,11},{9,8},{10,9... | collective-permute-start | bytes 552968 | tf_op jit(solution)/shard_map/ppermute | solution.py:17
  174.2 4.2 %collective-permute-done.38 = bf16[4,30,768]{2,1,0:T(8,128)(2,1)S(1)} collective-permute-done((bf16[4,30,768]{2,1,0:T(8,128)(2,1)S(1)}, bf16[4,30,768]{2,1,0:T(8,128)(2,1)S(1)}, u32[]{:S(2)}, u32[]{:S(2)}) %collective-permute-start.38) | collective-permute-done | bytes 184352 | tf_op jit(solution)/shard_map/ppermute | solution.py:17
  186.0 5.4 %collective-permute-done.41 = bf16[288,256]{1,0:T(8,128)(2,1)S(1)} collective-permute-done((bf16[288,256]{1,0:T(8,128)(2,1)}, bf16[288,256]{1,0:T(8,128)(2,1)S(1)}, u32[]{:S(2)}, u32[]{:S(2)}) %collective-permute-start.41) | collective-permute-done | bytes 147488 | tf_op jit(solution)/shard_map/ppermute | solution.py:17
  192.5 7.6 %collective-permute-start.43 = (bf16[4,288,256]{2,1,0:T(8,128)(2,1)}, bf16[4,288,256]{2,1,0:T(8,128)(2,1)S(1)}, u32[]{:S(2)}, u32[]{:S(2)}) collective-permute-start(bf16[4,288,256]{2,1,0:T(8,128)(2,1)} %constant_dynamic-slice_fusion), channel_id=1, source_target_pairs={{0,16},{16,0},{1,17},{17,1},{2,18},{18,2},{3,19},{19,3},{4,20},{20... | collective-permute-start | bytes 1769480 | tf_op jit(solution)/shard_map/ppermute | solution.py:17
  (195 shorter events, 66.9 us)
Async XLA Ops:
  1.4 12.7 %collective-permute-start.14 = (bf16[1,32,256]{2,1,0:T(8,128)(2,1)S(1)}, bf16[1,32,256]{2,1,0:T(8,128)(2,1)S(1)}, u32[]{:S(2)}, u32[]{:S(2)}) collective-permute-start(bf16[1,32,256]{2,1,0:T(8,128)(2,1)S(1)} %get-tuple-element.60), channel_id=1, source_target_pairs={{16,0},{32,16},{48,32},{64,48},{80,64},{96,80},{112,96},{17,1},{33... | collective-permute-start | bytes 49160 | tf_op jit(solution)/shard_map/ppermute | solution.py:26
  4.8 9.4 %collective-permute-start.13 = (bf16[1,32,256]{2,1,0:T(8,128)(2,1)S(1)}, bf16[1,32,256]{2,1,0:T(8,128)(2,1)S(1)}, u32[]{:S(2)}, u32[]{:S(2)}) collective-permute-start(bf16[1,32,256]{2,1,0:T(8,128)(2,1)S(1)} %get-tuple-element.61), channel_id=1, source_target_pairs={{0,16},{16,32},{32,48},{48,64},{64,80},{80,96},{96,112},{1,17},{17... | collective-permute-start | bytes 49160 | tf_op jit(solution)/shard_map/ppermute | solution.py:26
  9.4 14.3 %collective-permute-start = (bf16[256,1,128]{2,0,1:T(8,128)(2,1)S(1)}, bf16[256,1,128]{2,0,1:T(8,128)(2,1)S(1)}, u32[]{:S(2)}, u32[]{:S(2)}) collective-permute-start(bf16[256,1,128]{2,0,1:T(8,128)(2,1)S(1)} %copy.16), channel_id=1, source_target_pairs={{0,1},{1,2},{2,3},{3,4},{4,5},{5,6},{6,7},{7,8},{8,9},{9,10},{10,1... | collective-permute-start | bytes 196616 | tf_op jit(solution)/shard_map/ppermute | solution.py:26
  12.5 11.2 %collective-permute-start.1 = (bf16[256,1,128]{2,0,1:T(8,128)(2,1)S(1)}, bf16[256,1,128]{2,0,1:T(8,128)(2,1)S(1)}, u32[]{:S(2)}, u32[]{:S(2)}) collective-permute-start(bf16[256,1,128]{2,0,1:T(8,128)(2,1)S(1)} %copy.17), channel_id=1, source_target_pairs={{1,0},{2,1},{3,2},{4,3},{5,4},{6,5},{7,6},{8,7},{9,8},{10,9},{11,1... | collective-permute-start | bytes 196616 | tf_op jit(solution)/shard_map/ppermute | solution.py:26
  14.4 6.7 %collective-permute-start.15 = (bf16[34,1,256]{2,1,0:T(2,128)(2,1)S(1)}, bf16[34,1,256]{2,1,0:T(2,128)(2,1)S(1)}, u32[]{:S(2)}, u32[]{:S(2)}) collective-permute-start(bf16[34,1,256]{2,1,0:T(2,128)(2,1)S(1)} %get-tuple-element.51), channel_id=1, source_target_pairs={{1,0},{2,1},{3,2},{4,3},{5,4},{6,5},{7,6},{8,7},{9,8},{10,9},{11,1... | collective-permute-start | bytes 52232 | tf_op jit(solution)/shard_map/ppermute | solution.py:26
  33.4 14.3 %collective-permute-start.7 = (bf16[32,32,256]{2,1,0:T(8,128)(2,1)S(1)}, bf16[32,32,256]{2,1,0:T(8,128)(2,1)S(1)}, u32[]{:S(2)}, u32[]{:S(2)}) collective-permute-start(bf16[32,32,256]{2,1,0:T(8,128)(2,1)S(1)} %get-tuple-element.18), channel_id=1, source_target_pairs={{0,16},{16,0},{1,17},{17,1},{2,18},{18,2},{3,19},{19,3},{4,20},{20... | collective-permute-start | bytes 1572872 | tf_op jit(solution)/shard_map/ppermute | solution.py:17
  38.3 12.4 %collective-permute-start.5 = (bf16[32,32,256]{2,1,0:T(8,128)(2,1)S(1)}, bf16[32,32,256]{2,1,0:T(8,128)(2,1)S(1)}, u32[]{:S(2)}, u32[]{:S(2)}) collective-permute-start(bf16[32,32,256]{2,1,0:T(8,128)(2,1)S(1)} %get-tuple-element.16), channel_id=1, source_target_pairs={{0,16},{16,0},{1,17},{17,1},{2,18},{18,2},{3,19},{19,3},{4,20},{20... | collective-permute-start | bytes 1572872 | tf_op jit(solution)/shard_map/ppermute | solution.py:17
  42.9 8.1 %collective-permute-start.3 = (bf16[32,32,256]{2,1,0:T(8,128)(2,1)S(1)}, bf16[32,32,256]{2,1,0:T(8,128)(2,1)S(1)}, u32[]{:S(2)}, u32[]{:S(2)}) collective-permute-start(bf16[32,32,256]{2,1,0:T(8,128)(2,1)S(1)} %get-tuple-element.14), channel_id=1, source_target_pairs={{0,16},{16,0},{1,17},{17,1},{2,18},{18,2},{3,19},{19,3},{4,20},{20... | collective-permute-start | bytes 1572872 | tf_op jit(solution)/shard_map/ppermute | solution.py:17
  47.9 24.7 %collective-permute-start.8 = (bf16[32,32,256]{2,1,0:T(8,128)(2,1)S(1)}, bf16[32,32,256]{2,1,0:T(8,128)(2,1)S(1)}, u32[]{:S(2)}, u32[]{:S(2)}) collective-permute-start(bf16[32,32,256]{2,1,0:T(8,128)(2,1)S(1)} %add_convert_fusion), channel_id=1, source_target_pairs={{0,96},{32,0},{64,32},{96,64},{1,97},{33,1},{65,33},{97,65},{2,98}... | collective-permute-start | bytes 1572872 | tf_op jit(solution)/shard_map/ppermute | solution.py:17
  50.9 21.7 %collective-permute-start.6 = (bf16[32,32,256]{2,1,0:T(8,128)(2,1)S(1)}, bf16[32,32,256]{2,1,0:T(8,128)(2,1)S(1)}, u32[]{:S(2)}, u32[]{:S(2)}) collective-permute-start(bf16[32,32,256]{2,1,0:T(8,128)(2,1)S(1)} %add_convert_fusion.1), channel_id=1, source_target_pairs={{0,32},{32,64},{64,96},{96,0},{1,33},{33,65},{65,97},{97,1},{2,34}... | collective-permute-start | bytes 1572872 | tf_op jit(solution)/shard_map/ppermute | solution.py:17
  51.2 23.9 %collective-permute-start.4 = (bf16[32,32,256]{2,1,0:T(8,128)(2,1)S(1)}, bf16[32,32,256]{2,1,0:T(8,128)(2,1)S(1)}, u32[]{:S(2)}, u32[]{:S(2)}) collective-permute-start(bf16[32,32,256]{2,1,0:T(8,128)(2,1)S(1)} %add_convert_fusion.2), channel_id=1, source_target_pairs={{0,64},{32,96},{64,0},{96,32},{1,65},{33,97},{65,1},{97,33},{2,66}... | collective-permute-start | bytes 1572872 | tf_op jit(solution)/shard_map/ppermute | solution.py:17
  75.9 8.8 %collective-permute-start.9 = (bf16[1,32,256]{2,1,0:T(8,128)(2,1)S(1)}, bf16[1,32,256]{2,1,0:T(8,128)(2,1)S(1)}, u32[]{:S(2)}, u32[]{:S(2)}) collective-permute-start(bf16[1,32,256]{2,1,0:T(8,128)(2,1)S(1)} %get-tuple-element.64), channel_id=1, source_target_pairs={{0,16},{16,32},{32,48},{48,64},{64,80},{80,96},{96,112},{1,17},{17... | collective-permute-start | bytes 49160 | tf_op jit(solution)/shard_map/ppermute | solution.py:26
  78.4 6.3 %collective-permute-start.10 = (bf16[1,32,256]{2,1,0:T(8,128)(2,1)S(1)}, bf16[1,32,256]{2,1,0:T(8,128)(2,1)S(1)}, u32[]{:S(2)}, u32[]{:S(2)}) collective-permute-start(bf16[1,32,256]{2,1,0:T(8,128)(2,1)S(1)} %get-tuple-element.65), channel_id=1, source_target_pairs={{16,0},{32,16},{48,32},{64,48},{80,64},{96,80},{112,96},{17,1},{33... | collective-permute-start | bytes 49160 | tf_op jit(solution)/shard_map/ppermute | solution.py:26
  81.9 26.1 %collective-permute-start.23 = (bf16[32,32,256]{2,1,0:T(8,128)(2,1)S(1)}, bf16[32,32,256]{2,1,0:T(8,128)(2,1)S(1)}, u32[]{:S(2)}, u32[]{:S(2)}) collective-permute-start(bf16[32,32,256]{2,1,0:T(8,128)(2,1)S(1)} %get-tuple-element.26.delta_a), channel_id=1, source_target_pairs={{0,16},{16,0},{1,17},{17,1},{2,18},{18,2},{3,19},{19,3},{4,20},{20... | collective-permute-start | bytes 1572872 | tf_op jit(solution)/shard_map/ppermute | solution.py:17
  82.0 20.5 %collective-permute-start.21 = (bf16[32,32,256]{2,1,0:T(8,128)(2,1)S(1)}, bf16[32,32,256]{2,1,0:T(8,128)(2,1)S(1)}, u32[]{:S(2)}, u32[]{:S(2)}) collective-permute-start(bf16[32,32,256]{2,1,0:T(8,128)(2,1)S(1)} %get-tuple-element.26.delta_a), channel_id=1, source_target_pairs={{0,32},{32,64},{64,96},{96,0},{1,33},{33,65},{65,97},{97,1},{2,34}... | collective-permute-start | bytes 1572872 | tf_op jit(solution)/shard_map/ppermute | solution.py:17
  82.5 28.0 %collective-permute-start.19 = (bf16[32,32,256]{2,1,0:T(8,128)(2,1)S(1)}, bf16[32,32,256]{2,1,0:T(8,128)(2,1)S(1)}, u32[]{:S(2)}, u32[]{:S(2)}) collective-permute-start(bf16[32,32,256]{2,1,0:T(8,128)(2,1)S(1)} %get-tuple-element.26.delta_a), channel_id=1, source_target_pairs={{0,96},{32,0},{64,32},{96,64},{1,97},{33,1},{65,33},{97,65},{2,98}... | collective-permute-start | bytes 1572872 | tf_op jit(solution)/shard_map/ppermute | solution.py:17
  84.8 6.1 %collective-permute-start.11 = (bf16[34,1,256]{2,1,0:T(2,128)(2,1)S(1)}, bf16[34,1,256]{2,1,0:T(2,128)(2,1)S(1)}, u32[]{:S(2)}, u32[]{:S(2)}) collective-permute-start(bf16[34,1,256]{2,1,0:T(2,128)(2,1)S(1)} %get-tuple-element.55), channel_id=1, source_target_pairs={{0,1},{1,2},{2,3},{3,4},{4,5},{5,6},{6,7},{7,8},{8,9},{9,10},{10,1... | collective-permute-start | bytes 52232 | tf_op jit(solution)/shard_map/ppermute | solution.py:26
  90.9 23.8 %collective-permute-start.17 = (bf16[32,32,256]{2,1,0:T(8,128)(2,1)S(1)}, bf16[32,32,256]{2,1,0:T(8,128)(2,1)S(1)}, u32[]{:S(2)}, u32[]{:S(2)}) collective-permute-start(bf16[32,32,256]{2,1,0:T(8,128)(2,1)S(1)} %get-tuple-element.26.delta_a), channel_id=1, source_target_pairs={{0,64},{32,96},{64,0},{96,32},{1,65},{33,97},{65,1},{97,33},{2,66}... | collective-permute-start | bytes 1572872 | tf_op jit(solution)/shard_map/ppermute | solution.py:17
  102.5 19.8 %collective-permute-start.22 = (bf16[32,32,256]{2,1,0:T(8,128)(2,1)S(1)}, bf16[32,32,256]{2,1,0:T(8,128)(2,1)}, u32[]{:S(2)}, u32[]{:S(2)}) collective-permute-start(bf16[32,32,256]{2,1,0:T(8,128)(2,1)S(1)} %collective-permute-done.21.delta_a), channel_id=1, source_target_pairs={{0,16},{16,0},{1,17},{17,1},{2,18},{18,2},{3,19},{19,3},{4,20},{20... | collective-permute-start | bytes 1572872 | tf_op jit(solution)/shard_map/ppermute | solution.py:17
  102.7 16.9 %collective-permute-start.25 = (bf16[288,256]{1,0:T(8,128)(2,1)S(1)}, bf16[288,256]{1,0:T(8,128)(2,1)S(1)}, u32[]{:S(2)}, u32[]{:S(2)}) collective-permute-start(bf16[288,256]{1,0:T(8,128)(2,1)S(1)} %get-tuple-element.33), channel_id=1, source_target_pairs={{0,32},{32,64},{64,96},{96,0},{1,33},{33,65},{65,97},{97,1},{2,34}... | collective-permute-start | bytes 442376 | tf_op jit(solution)/shard_map/ppermute | solution.py:17
  108.0 11.7 %collective-permute-start.27 = (bf16[288,256]{1,0:T(8,128)(2,1)S(1)}, bf16[288,256]{1,0:T(8,128)(2,1)S(1)}, u32[]{:S(2)}, u32[]{:S(2)}) collective-permute-start(bf16[288,256]{1,0:T(8,128)(2,1)S(1)} %get-tuple-element.34), channel_id=1, source_target_pairs={{0,64},{32,96},{64,0},{96,32},{1,65},{33,97},{65,1},{97,33},{2,66}... | collective-permute-start | bytes 442376 | tf_op jit(solution)/shard_map/ppermute | solution.py:17
  110.6 9.1 %collective-permute-start.26 = (bf16[288,256]{1,0:T(8,128)(2,1)S(1)}, bf16[288,256]{1,0:T(8,128)(2,1)S(1)}, u32[]{:S(2)}, u32[]{:S(2)}) collective-permute-start(bf16[288,256]{1,0:T(8,128)(2,1)S(1)} %get-tuple-element.35), channel_id=1, source_target_pairs={{0,96},{32,0},{64,32},{96,64},{1,97},{33,1},{65,33},{97,65},{2,98}... | collective-permute-start | bytes 442376 | tf_op jit(solution)/shard_map/ppermute | solution.py:17
  114.7 11.6 %collective-permute-start.20 = (bf16[32,32,256]{2,1,0:T(8,128)(2,1)S(1)}, bf16[32,32,256]{2,1,0:T(8,128)(2,1)}, u32[]{:S(2)}, u32[]{:S(2)}) collective-permute-start(bf16[32,32,256]{2,1,0:T(8,128)(2,1)S(1)} %collective-permute-done.19.delta_a), channel_id=1, source_target_pairs={{0,16},{16,0},{1,17},{17,1},{2,18},{18,2},{3,19},{19,3},{4,20},{20... | collective-permute-start | bytes 1572872 | tf_op jit(solution)/shard_map/ppermute | solution.py:17
  119.6 10.8 %collective-permute-start.18 = (bf16[32,32,256]{2,1,0:T(8,128)(2,1)S(1)}, bf16[32,32,256]{2,1,0:T(8,128)(2,1)S(1)}, u32[]{:S(2)}, u32[]{:S(2)}) collective-permute-start(bf16[32,32,256]{2,1,0:T(8,128)(2,1)S(1)} %collective-permute-done.17.delta_a), channel_id=1, source_target_pairs={{0,16},{16,0},{1,17},{17,1},{2,18},{18,2},{3,19},{19,3},{4,20},{20... | collective-permute-start | bytes 1572872 | tf_op jit(solution)/shard_map/ppermute | solution.py:17
  134.5 8.7 %collective-permute-start.28 = (bf16[4,30,768]{2,1,0:T(8,128)(2,1)S(1)}, bf16[4,30,768]{2,1,0:T(8,128)(2,1)S(1)}, u32[]{:S(2)}, u32[]{:S(2)}) collective-permute-start(bf16[4,30,768]{2,1,0:T(8,128)(2,1)S(1)} %get-tuple-element.30), channel_id=1, source_target_pairs={{0,1},{1,2},{2,3},{3,0},{4,5},{5,6},{6,7},{7,4},{8,9},{9,10},{10,1... | collective-permute-start | bytes 552968 | tf_op jit(solution)/shard_map/ppermute | solution.py:17
  136.8 6.3 %collective-permute-start.29 = (bf16[4,30,768]{2,1,0:T(8,128)(2,1)S(1)}, bf16[4,30,768]{2,1,0:T(8,128)(2,1)S(1)}, u32[]{:S(2)}, u32[]{:S(2)}) collective-permute-start(bf16[4,30,768]{2,1,0:T(8,128)(2,1)S(1)} %get-tuple-element.31), channel_id=1, source_target_pairs={{0,3},{1,0},{2,1},{3,2},{4,7},{5,4},{6,5},{7,6},{8,11},{9,8},{10,9... | collective-permute-start | bytes 552968 | tf_op jit(solution)/shard_map/ppermute | solution.py:17
  138.4 9.8 %collective-permute-start.30 = (bf16[4,30,768]{2,1,0:T(8,128)(2,1)S(1)}, bf16[4,30,768]{2,1,0:T(8,128)(2,1)S(1)}, u32[]{:S(2)}, u32[]{:S(2)}) collective-permute-start(bf16[4,30,768]{2,1,0:T(8,128)(2,1)S(1)} %get-tuple-element.32), channel_id=1, source_target_pairs={{0,2},{1,3},{2,0},{3,1},{4,6},{5,7},{6,4},{7,5},{8,10},{9,11},{10,... | collective-permute-start | bytes 552968 | tf_op jit(solution)/shard_map/ppermute | solution.py:17
  148.3 11.3 %collective-permute-start.31 = (bf16[30,768]{1,0:T(8,128)(2,1)S(1)}, bf16[30,768]{1,0:T(8,128)(2,1)S(1)}, u32[]{:S(2)}, u32[]{:S(2)}) collective-permute-start(bf16[30,768]{1,0:T(8,128)(2,1)S(1)} %get-tuple-element.66), channel_id=1, source_target_pairs={{0,4},{4,8},{8,12},{12,0},{1,5},{5,9},{9,13},{13,1},{2,6},{6,10},{... | collective-permute-start | bytes 138248 | tf_op jit(solution)/shard_map/ppermute | solution.py:17
  171.8 7.9 %collective-permute-start.39 = (bf16[4,30,768]{2,1,0:T(8,128)(2,1)S(1)}, bf16[4,30,768]{2,1,0:T(8,128)(2,1)S(1)}, u32[]{:S(2)}, u32[]{:S(2)}) collective-permute-start(bf16[4,30,768]{2,1,0:T(8,128)(2,1)S(1)} %get-tuple-element.23), channel_id=1, source_target_pairs={{0,1},{1,2},{2,3},{3,0},{4,5},{5,6},{6,7},{7,4},{8,9},{9,10},{10,1... | collective-permute-start | bytes 552968 | tf_op jit(solution)/shard_map/ppermute | solution.py:17
  171.9 6.5 %collective-permute-start.38 = (bf16[4,30,768]{2,1,0:T(8,128)(2,1)S(1)}, bf16[4,30,768]{2,1,0:T(8,128)(2,1)S(1)}, u32[]{:S(2)}, u32[]{:S(2)}) collective-permute-start(bf16[4,30,768]{2,1,0:T(8,128)(2,1)S(1)} %get-tuple-element.23), channel_id=1, source_target_pairs={{0,2},{1,3},{2,0},{3,1},{4,6},{5,7},{6,4},{7,5},{8,10},{9,11},{10,... | collective-permute-start | bytes 552968 | tf_op jit(solution)/shard_map/ppermute | solution.py:17
  184.2 7.3 %collective-permute-start.42 = (bf16[288,256]{1,0:T(8,128)(2,1)}, bf16[288,256]{1,0:T(8,128)(2,1)S(1)}, u32[]{:S(2)}, u32[]{:S(2)}) collective-permute-start(bf16[288,256]{1,0:T(8,128)(2,1)} %reshape.149), channel_id=1, source_target_pairs={{0,32},{32,64},{64,96},{96,0},{1,33},{33,65},{65,97},{97,1},{2,34}... | collective-permute-start | bytes 442376 | tf_op jit(solution)/shard_map/ppermute | solution.py:17
  192.5 12.5 %collective-permute-start.43 = (bf16[4,288,256]{2,1,0:T(8,128)(2,1)}, bf16[4,288,256]{2,1,0:T(8,128)(2,1)S(1)}, u32[]{:S(2)}, u32[]{:S(2)}) collective-permute-start(bf16[4,288,256]{2,1,0:T(8,128)(2,1)} %constant_dynamic-slice_fusion), channel_id=1, source_target_pairs={{0,16},{16,0},{1,17},{17,1},{2,18},{18,2},{3,19},{19,3},{4,20},{20... | collective-permute-start | bytes 1769480 | tf_op jit(solution)/shard_map/ppermute | solution.py:17
  (31 other events, 194.8 us)

commit v2 on v1

v2 whole, which is shorter than its diff:
```python
import functools

import jax
import jax.numpy as jnp
from jax import lax
from jax.experimental import pallas as pl
from jax.experimental.pallas import tpu as pltpu
from jax.sharding import Mesh, PartitionSpec as P

FREQ = ("y", "c")
SKY = ("z", "x")
F32 = jnp.float32
BF16 = jnp.bfloat16


def shift(x, axis, step):
    count = lax.axis_size(axis)
    return lax.ppermute(x, axis, [(i, (i + step) % count) for i in range(count)])


def halo(x, axes, dim):
    count, length = lax.axis_size(axes), x.shape[dim]
    up = [(i, i + 1) for i in range(count - 1)]
    down = [(j, i) for i, j in up]
    last = lax.slice_in_dim(x, length - 1, length, axis=dim)
    first = lax.slice_in_dim(x, 0, 1, axis=dim)
    return lax.ppermute(last, axes, up), lax.ppermute(first, axes, down)


def with_halo(x):
    for axes, dim in ((FREQ, 0), (SKY, 1)):
        before, after = halo(x, axes, dim)
        x = jnp.concatenate([before, x, after], axis=dim)
    return x


def spread_kernel(own_ref, far_ref, own_halo_ref, far_halo_ref, out_ref):
    chips, width, rows, depth = out_ref.shape
    cols, _, chans = own_ref.shape
    strip = cols // (2 * chips)
    core = lax.axis_index("c")
    step = 8
    row = lax.broadcasted_iota(jnp.int32, (step, rows, chans), 1)

    def block(i, base, chip):
        for side, (cube_ref, halo_ref) in enumerate(
            ((own_ref, own_halo_ref), (far_ref, far_halo_ref))
        ):
            at = pl.multiple_of(base + i * step, step)
            mid = cube_ref[pl.ds(at, step)]
            wide = mid.astype(F32).reshape(step * rows, chans)
            ahead = pltpu.roll(wide, 1, 0).reshape(step, rows, chans)
            behind = pltpu.roll(wide, step * rows - 1, 0).reshape(step, rows, chans)
            before = halo_ref[0, pl.ds(at, step), :].astype(F32)[:, None, :]
            after = halo_ref[1, pl.ds(at, step), :].astype(F32)[:, None, :]
            ahead = jnp.where(row == 0, before, ahead)
            behind = jnp.where(row == rows - 1, after, behind)
            to = pl.ds(1 + i * step, step)
            for tap, value in enumerate((ahead.astype(BF16), mid, behind.astype(BF16))):
                lane = (2 * tap + side) * chans
                out_ref[chip, to, :, lane : lane + chans] = value

    def edge(at, chip, slot):
        for side, (cube_ref, halo_ref) in enumerate(
            ((own_ref, own_halo_ref), (far_ref, far_halo_ref))
        ):
            first = pl.multiple_of((at // step) * step, step)
            mid = cube_ref[at]
            wide = mid.astype(F32)
            line = lax.broadcasted_iota(jnp.int32, (step, chans), 0) == at - first
            pick = lambda k: jnp.sum(
                jnp.where(line, halo_ref[k, pl.ds(first, step), :].astype(F32), 0.0),
                axis=0,
                keepdims=True,
            )
            place = lax.broadcasted_iota(jnp.int32, (rows, chans), 0)
            ahead = jnp.where(place == 0, pick(0), pltpu.roll(wide, 1, 0))
            behind = jnp.where(place == rows - 1, pick(1), pltpu.roll(wide, rows - 1, 0))
            for tap, value in enumerate((ahead.astype(BF16), mid, behind.astype(BF16))):
                lane = (2 * tap + side) * chans
                out_ref[chip, slot, :, lane : lane + chans] = value

    blank = jnp.zeros((rows, depth), BF16)
    for chip in range(chips):
        base = (2 * chip + core) * strip
        lax.fori_loop(0, strip // step, lambda i, _: block(i, base, chip), None)
        edge(jnp.maximum(base - 1, 0), chip, 0)
        edge(jnp.minimum(base + strip, cols - 1), chip, strip + 1)
        for slot in range(strip + 2, width):
            out_ref[chip, slot] = blank

    @pl.when(core == 0)
    def _():
        out_ref[0, 0] = blank

    @pl.when(core == 1)
    def _():
        out_ref[chips - 1, strip + 1] = blank


VMEM_SPEC = pl.BlockSpec(memory_space=pltpu.VMEM)
SMEM_SPEC = pl.BlockSpec(memory_space=pltpu.SMEM)


def spread(own, far, own_halo, far_halo, chips):
    cols, rows, chans = own.shape
    return pl.pallas_call(
        spread_kernel,
        out_shape=jax.ShapeDtypeStruct((chips, cols // (2 * chips) + 8, rows, 6 * chans), BF16),
        in_specs=[VMEM_SPEC] * 4,
        out_specs=VMEM_SPEC,
        compiler_params=pltpu.CompilerParams(vmem_limit_bytes=16 * 2**20),
        cost_estimate=pl.CostEstimate(flops=2**20, bytes_accessed=12 * 2**20, transcendentals=0),
        name="spread",
    )(own, far, own_halo, far_halo)


def conv_kernel(chip_ref, wide_ref, kernel_ref, out_ref):
    strip, rows, outs = out_ref.shape
    chip = chip_ref[0]
    pieces = [wide_ref[chip, tap : tap + strip] for tap in range(3)]
    lhs = jnp.concatenate(pieces, axis=-1).reshape(strip * rows, -1)
    total = jnp.dot(lhs, kernel_ref[...], preferred_element_type=F32)
    out_ref[...] = total.reshape(strip, rows, outs).astype(out_ref.dtype)


def conv_strip(chip, wide, kernel, strip, dtype):
    rows, depth, outs = wide.shape[2], kernel.shape[0], kernel.shape[1]
    return pl.pallas_call(
        conv_kernel,
        out_shape=jax.ShapeDtypeStruct((strip, rows, outs), dtype),
        in_specs=[SMEM_SPEC, VMEM_SPEC, VMEM_SPEC],
        out_specs=VMEM_SPEC,
        compiler_params=pltpu.CompilerParams(vmem_limit_bytes=16 * 2**20),
        cost_estimate=pl.CostEstimate(
            flops=2 * strip * rows * depth * outs, bytes_accessed=4 * 2**20, transcendentals=0
        ),
        name="conv_first",
    )(chip.reshape(1), wide, kernel)


def grad_kernel(has_old, last, chip_ref, wide_ref, delta_ref, *refs):
    old_ref = refs[0] if has_old else None
    outs_refs, pad_ref = refs[1 if has_old else 0 : -1], refs[-1]
    strip, rows, outs = delta_ref.shape
    cols, depth = wide_ref.shape[1], wide_ref.shape[3]
    pad_ref[0:2] = jnp.zeros((2, rows, outs), BF16)
    pad_ref[2 : 2 + strip] = delta_ref[...]
    pad_ref[2 + strip :] = jnp.zeros((cols - strip, rows, outs), BF16)
    lhs = wide_ref[chip_ref[0]].reshape(cols * rows, depth)
    rhs = jnp.concatenate(
        [pad_ref[2 - tap : 2 - tap + cols].reshape(cols * rows, outs) for tap in range(3)], axis=-1
    )
    total = lax.dot_general(lhs, rhs, (((0,), (0,)), ((), ())), preferred_element_type=F32)
    if has_old:
        total = total + old_ref[...]
    if not last:
        outs_refs[0][...] = total
    else:
        chans = depth // 6
        for tap in range(3):
            at = 2 * tap * chans
            outs_refs[0][tap * chans : (tap + 1) * chans] = total[at : at + chans]
            outs_refs[1][tap * chans : (tap + 1) * chans] = total[
                at + chans : at + 2 * chans
            ].astype(BF16)


def grad_strip(chip, wide, delta, old, last):
    strip, rows, outs = delta.shape
    depth, cols = wide.shape[3], wide.shape[1]
    shape = (depth, 3 * outs)
    half = (depth // 2, 3 * outs)
    if last:
        out_shape = (jax.ShapeDtypeStruct(half, F32), jax.ShapeDtypeStruct(half, BF16))
    else:
        out_shape = (jax.ShapeDtypeStruct(shape, F32),)
    args = [chip.reshape(1), wide, delta] + ([old] if old is not None else [])
    out = pl.pallas_call(
        functools.partial(grad_kernel, old is not None, last),
        out_shape=out_shape,
        in_specs=[SMEM_SPEC] + [VMEM_SPEC] * (len(args) - 1),
        out_specs=tuple([VMEM_SPEC] * len(out_shape)),
        scratch_shapes=[pltpu.VMEM((cols + 2, rows, outs), BF16)],
        compiler_params=pltpu.CompilerParams(vmem_limit_bytes=20 * 2**20),
        cost_estimate=pl.CostEstimate(
            flops=2 * cols * rows * depth * 3 * outs, bytes_accessed=6 * 2**20, transcendentals=0
        ),
        name="grad_first",
    )(*args)
    return out if last else out[0]


def conv_taps(padded, kernel, col_count, row_count):
    total = jnp.zeros((col_count * row_count, kernel.shape[3]), F32)
    for tap_col in range(3):
        for tap_row in range(3):
            piece = padded[tap_col : tap_col + col_count, tap_row : tap_row + row_count].reshape(
                col_count * row_count, -1
            )
            total = total + jnp.dot(piece, kernel[tap_col, tap_row], preferred_element_type=F32)
    return total.reshape(col_count, row_count, kernel.shape[3])


def conv_back(padded, kernel, col_count, row_count):
    total = jnp.zeros((col_count * row_count, kernel.shape[2]), F32)
    for tap_col in range(3):
        for tap_row in range(3):
            piece = padded[
                2 - tap_col : 2 - tap_col + col_count, 2 - tap_row : 2 - tap_row + row_count
            ].reshape(col_count * row_count, -1)
            total = total + lax.dot_general(
                piece,
                kernel[tap_col, tap_row],
                (((1,), (1,)), ((), ())),
                preferred_element_type=F32,
            )
    return total.reshape(col_count, row_count, kernel.shape[2])


def kernel_grad(padded, grads, col_count, row_count):
    flat = grads.reshape(col_count * row_count, -1)
    lines = []
    for tap_col in range(3):
        for tap_row in range(3):
            piece = padded[tap_col : tap_col + col_count, tap_row : tap_row + row_count].reshape(
                col_count * row_count, -1
            )
            lines.append(
                lax.dot_general(piece, flat, (((0,), (0,)), ((), ())), preferred_element_type=F32)
            )
    return jnp.concatenate(lines, axis=0)


def reduce_pieces(parts, axis):
    count = lax.axis_size(axis)
    me = lax.axis_index(axis)

    def pick(at):
        return lax.dynamic_index_in_dim(parts, at, 0, keepdims=False)

    total = pick(me)
    for step in (1, count - 1, 2) if count == 4 else range(1, count):
        total = total + shift(pick((me + step) % count).astype(BF16), axis, step).astype(F32)
    return total


def gather_pieces(piece, axis):
    count = lax.axis_size(axis)
    me = lax.axis_index(axis)
    got = {0: piece}
    for step in (1, count - 1, 2) if count == 4 else range(1, count):
        got[step] = shift(piece, axis, step)
    turned = jnp.stack([got[(-j) % count] for j in range(count)] * 2)
    return lax.dynamic_slice_in_dim(turned, count - me, count, 0)


def body(sky_cube, weight_first, weight_second, cotangent):
    cols, rows, chans = sky_cube.shape
    strip, _, outs = cotangent.shape
    here, core = lax.axis_index("y"), lax.axis_index("c")
    chips = lax.axis_size("y")

    edges = jnp.concatenate(halo(sky_cube, SKY, 1), axis=1)
    far_cube = shift(sky_cube, "c", 1)
    far_weight = shift(weight_first, "c", 1)
    edges = jnp.transpose(edges, (1, 0, 2))
    far_edges = shift(edges, "c", 1)
    wide = spread(sky_cube, far_cube, edges, far_edges, chips)
    kernel = jnp.concatenate([weight_first, far_weight], axis=2).reshape(18 * chans, outs)

    order = (2, 1, chips - 1)
    near = []
    hold = wide
    for step in order:
        part = conv_strip((here + step) % chips, hold, kernel, strip, BF16)
        near.append(part)
        hold, _ = lax.optimization_barrier((wide, part))
    own = conv_strip(here, hold, kernel, strip, F32)
    pre = own
    for step, part in zip(order, near):
        pre = pre + shift(part, "y", step).astype(F32)

    late_cotangent, _ = lax.optimization_barrier((cotangent, own))
    back = conv_back(with_halo(late_cotangent), weight_second, strip, rows)
    sigma = jax.nn.sigmoid(pre)
    delta = (back * (sigma * (1.0 + pre * (1.0 - sigma)))).astype(BF16)
    hidden = (pre * sigma).astype(BF16)

    total = grad_strip(here, wide, delta, None, False)
    for step in (1, chips - 1, 2):
        piece = shift(delta, "y", step)
        total = grad_strip((here - step) % chips, wide, piece, total, step == 2)
    first_own, first_far = total
    first = first_own + shift(first_far, "c", 1).astype(F32)

    hidden_pad = with_halo(hidden)
    features = conv_taps(hidden_pad, weight_second, strip, rows).astype(BF16)
    second = kernel_grad(hidden_pad, cotangent, strip, rows)
    depth = second.shape[0]
    second = reduce_pieces(second.reshape(2, depth // 2, outs), "c")
    second = reduce_pieces(second.reshape(chips, depth // (2 * chips), outs), "y")

    sx, sz = lax.axis_size("x"), lax.axis_size("z")
    width = 3 * outs
    first_parts = first.reshape(sx, -1, width)
    second_parts = second.reshape(sx, -1, width)
    split = first_parts.shape[1] // sz
    joined = jnp.concatenate(
        [first_parts.reshape(sx, sz, -1, width), second_parts.reshape(sx, sz, -1, width)], axis=2
    )
    summed = reduce_pieces(joined, "x")
    summed = reduce_pieces(summed, "z").astype(BF16)
    summed = gather_pieces(gather_pieces(summed, "z"), "x")
    first = summed[:, :, :split].reshape(3, chans, 3, outs)
    grad_first = jnp.transpose(first, (2, 0, 1, 3)).astype(F32)
    share = summed[:, :, split:].reshape(depth // (2 * chips), outs)
    share = gather_pieces(gather_pieces(share, "y"), "c")
    grad_second = share.reshape(3, 3, outs, outs).astype(F32)
    return features, grad_first, grad_second


def solution(mesh):
    sizes = (mesh.devices.shape[0] // 2, 2, 4, mesh.devices.shape[1] // 4)
    fine = Mesh(mesh.devices.reshape(sizes), FREQ + SKY)
    return jax.shard_map(
        body,
        mesh=fine,
        in_specs=(P(None, SKY, FREQ), P(None, None, FREQ, None), P(), P(FREQ, SKY, None)),
        out_specs=(P(FREQ, SKY, None), P(None, None, FREQ, None), P()),
        check_vma=False,
    )
```

time: 208 us -> 188 us (0.904)
  Pallas kernels: 36.8 us -> 14.4 us
  waiting for transfers between devices: 49.6 us -> 58.9 us
  starting transfers between devices: 83.6 us -> 80.6 us
  matrix products: 13.4 us -> 10.6 us
    ppermute x10, waiting for transfers between devices: 1.83 us -> 25.3 us  [halo(): return (lax.ppermute(last, axes, up), lax.ppermute(first, axes, down))]
    pallas_call x9, Pallas kernels: 36.8 us -> 14.4 us  [the longest x4 6.97 us: grad_strip(): pl.pallas_call(functools.partial(grad_kernel, old is not None, last), out...]
    ppermute x34 -> x30, waiting for transfers between devices: 47.8 us -> 33.6 us  [shift(): lax.ppermute(x, axis, [(i, (i + step) % count) for i in range(count)])]
    dot_general x9, matrix products: 7.28 us -> 4.47 us  [conv_taps(): jnp.dot(piece, kernel[tap_col, tap_row], preferred_element_type=F32)]
    ppermute x10, starting transfers between devices: 28 us -> 25.3 us  [halo(): return (lax.ppermute(last, axes, up), lax.ppermute(first, axes, down))]
    slice x3 -> x2, local copies, waits for them, and re-layouts: 2.28 us -> 0.06 us  [halo(): first = lax.slice_in_dim(x, 0, 1, axis=dim)]
    unnamed x62 -> x58, local copies, waits for them, and re-layouts: 4.26 us -> 4.89 us
    ppermute x34 -> x30, starting transfers between devices: 55.6 us -> 55.3 us  [shift(): lax.ppermute(x, axis, [(i, (i + step) % count) for i in range(count)])]
  transfers between devices with their start and end apart: 44 -> 40, of which waited for: 15 -> 20; matrix products, arithmetic and copies ran while one was open for 13% -> 12% of each run, Pallas kernels for 12% -> 4%
where the time goes in v2:
time: 188 us
  starting transfers between devices  80.6 us (43%)
  waiting for transfers between devices  58.9 us (31%)
  Pallas kernels  14.4 us (8%)
  local copies, waits for them, and re-layouts  12.4 us (7%)
  matrix products  10.6 us (6%)
  other arithmetic  9.09 us (5%)
    ppermute x30, starting transfers between devices, shift(): lax.ppermute(x, axis, [(i, (i + step) % count) for i in range(count)])  55.3 us
    ppermute x30, waiting for transfers between devices, shift(): lax.ppermute(x, axis, [(i, (i + step) % count) for i in range(count)])  33.6 us
    ppermute x10, starting transfers between devices, halo(): return (lax.ppermute(last, axes, up), lax.ppermute(first, axes, down))  25.3 us
    ppermute x10, waiting for transfers between devices, halo(): return (lax.ppermute(last, axes, up), lax.ppermute(first, axes, down))  25.3 us
    pallas_call x4, Pallas kernels, grad_strip(): pl.pallas_call(functools.partial(grad_kernel, old is not None, last), out...  6.97 us
    pallas_call x4, Pallas kernels, conv_strip(): pl.pallas_call(conv_kernel, out_shape=jax.ShapeDtypeStruct((strip, rows,...  5.57 us
    unnamed x58, local copies, waits for them, and re-layouts  4.89 us
    dot_general x9, matrix products, conv_taps(): jnp.dot(piece, kernel[tap_col, tap_row], preferred_element_type=F32)  4.47 us
  transfers between devices with their start and end apart: 40, of which 20 were waited for; matrix products, arithmetic and copies ran while one was open for 12% of the time, Pallas kernels for 4%

profile of v2, /device:TPU:1, one launch (start us, length us, event | category | flops | bytes accessed | tf_op | source)
XLA Modules:
  0.0 187.8 jit_solution(8001642951019054966)
XLA Ops:
  3.7 3.2 %collective-permute-start.1 = (bf16[256,1,128]{2,0,1:T(8,128)(2,1)S(1)}, bf16[256,1,128]{2,0,1:T(8,128)(2,1)S(1)}, u32[]{:S(2)}, u32[]{:S(2)}) collective-permute-start(bf16[256,1,128]{2,0,1:T(8,128)(2,1)S(1)} %copy.12), channel_id=1, source_target_pairs={{0,1},{1,2},{2,3},{3,4},{4,5},{5,6},{6,7},{7,8},{8,9},{9,10},{10,1... | collective-permute-start | bytes 196616 | tf_op jit(solution)/shard_map/ppermute | solution.py:27
  8.3 3.7 %collective-permute-done.2 = bf16[256,1,128]{2,0,1:T(8,128)(2,1)S(1)} collective-permute-done((bf16[256,1,128]{2,0,1:T(8,128)(2,1)S(1)}, bf16[256,1,128]{2,0,1:T(8,128)(2,1)S(1)}, u32[]{:S(2)}, u32[]{:S(2)}) %collective-permute-start.2) | collective-permute-done | bytes 65568 | tf_op jit(solution)/shard_map/ppermute | solution.py:27
  11.9 1.9 %collective-permute-start.3 = (bf16[2,256,128]{2,1,0:T(8,128)(2,1)S(1)}, bf16[2,256,128]{2,1,0:T(8,128)(2,1)S(1)}, u32[]{:S(2)}, u32[]{:S(2)}) collective-permute-start(bf16[2,256,128]{2,1,0:T(8,128)(2,1)S(1)} %maximum_bitcast_fusion.own_halo_ref), channel_id=1, source_target_pairs={{0,16},{16,0},{1,17},{17,1},{2,18},{18,2},{3,19},{19,3},{4,20},{20... | collective-permute-start | bytes 393224 | tf_op jit(solution)/shard_map/ppermute | solution.py:18
  22.3 3.6 %collective-permute-start.12 = (bf16[1,32,256]{2,1,0:T(8,128)(2,1)S(1)}, bf16[1,32,256]{2,1,0:T(8,128)(2,1)S(1)}, u32[]{:S(2)}, u32[]{:S(2)}) collective-permute-start(bf16[1,32,256]{2,1,0:T(8,128)(2,1)S(1)} %get-tuple-element.57), channel_id=1, source_target_pairs={{0,16},{16,32},{32,48},{48,64},{64,80},{80,96},{96,112},{1,17},{17... | collective-permute-start | bytes 49160 | tf_op jit(solution)/shard_map/ppermute | solution.py:27
  27.7 2.6 %collective-permute-start.5 = (bf16[32,32,256]{2,1,0:T(8,128)(2,1)S(1)}, bf16[32,32,256]{2,1,0:T(8,128)(2,1)S(1)}, u32[]{:S(2)}, u32[]{:S(2)}) collective-permute-start(bf16[32,32,256]{2,1,0:T(8,128)(2,1)S(1)} %conv_first.4), channel_id=1, source_target_pairs={{0,64},{32,96},{64,0},{96,32},{1,65},{33,97},{65,1},{97,33},{2,66}... | collective-permute-start | bytes 1572872 | tf_op jit(solution)/shard_map/ppermute | solution.py:18
  30.3 1.9 %collective-permute-start.13 = (bf16[1,32,256]{2,1,0:T(8,128)(2,1)S(1)}, bf16[1,32,256]{2,1,0:T(8,128)(2,1)S(1)}, u32[]{:S(2)}, u32[]{:S(2)}) collective-permute-start(bf16[1,32,256]{2,1,0:T(8,128)(2,1)S(1)} %get-tuple-element.56), channel_id=1, source_target_pairs={{16,0},{32,16},{48,32},{64,48},{80,64},{96,80},{112,96},{17,1},{33... | collective-permute-start | bytes 49160 | tf_op jit(solution)/shard_map/ppermute | solution.py:27
  32.2 18.1 %collective-permute-done.13 = bf16[1,32,256]{2,1,0:T(8,128)(2,1)S(1)} collective-permute-done((bf16[1,32,256]{2,1,0:T(8,128)(2,1)S(1)}, bf16[1,32,256]{2,1,0:T(8,128)(2,1)S(1)}, u32[]{:S(2)}, u32[]{:S(2)}) %collective-permute-start.13) | collective-permute-done | bytes 16416 | tf_op jit(solution)/shard_map/ppermute | solution.py:27
  51.9 4.0 %collective-permute-start.15 = (bf16[34,1,256]{2,1,0:T(2,128)(2,1)S(1)}, bf16[34,1,256]{2,1,0:T(2,128)(2,1)S(1)}, u32[]{:S(2)}, u32[]{:S(2)}) collective-permute-start(bf16[34,1,256]{2,1,0:T(2,128)(2,1)S(1)} %get-tuple-element.48), channel_id=1, source_target_pairs={{0,1},{1,2},{2,3},{3,4},{4,5},{5,6},{6,7},{7,8},{8,9},{9,10},{10,1... | collective-permute-start | bytes 52232 | tf_op jit(solution)/shard_map/ppermute | solution.py:27
  60.9 2.7 %collective-permute-start.8 = (bf16[1,32,256]{2,1,0:T(8,128)(2,1)S(1)}, bf16[1,32,256]{2,1,0:T(8,128)(2,1)S(1)}, u32[]{:S(2)}, u32[]{:S(2)}) collective-permute-start(bf16[1,32,256]{2,1,0:T(8,128)(2,1)S(1)} %get-tuple-element.60), channel_id=1, source_target_pairs={{0,16},{16,32},{32,48},{48,64},{64,80},{80,96},{96,112},{1,17},{17... | collective-permute-start | bytes 49160 | tf_op jit(solution)/shard_map/ppermute | solution.py:27
  63.6 2.1 %collective-permute-start.9 = (bf16[1,32,256]{2,1,0:T(8,128)(2,1)S(1)}, bf16[1,32,256]{2,1,0:T(8,128)(2,1)S(1)}, u32[]{:S(2)}, u32[]{:S(2)}) collective-permute-start(bf16[1,32,256]{2,1,0:T(8,128)(2,1)S(1)} %get-tuple-element.61), channel_id=1, source_target_pairs={{16,0},{32,16},{48,32},{64,48},{80,64},{96,80},{112,96},{17,1},{33... | collective-permute-start | bytes 49160 | tf_op jit(solution)/shard_map/ppermute | solution.py:27
  67.7 2.6 %collective-permute-start.17 = (bf16[32,32,256]{2,1,0:T(8,128)(2,1)S(1)}, bf16[32,32,256]{2,1,0:T(8,128)(2,1)S(1)}, u32[]{:S(2)}, u32[]{:S(2)}) collective-permute-start(bf16[32,32,256]{2,1,0:T(8,128)(2,1)S(1)} %get-tuple-element.22.delta_ref), channel_id=1, source_target_pairs={{0,96},{32,0},{64,32},{96,64},{1,97},{33,1},{65,33},{97,65},{2,98}... | collective-permute-start | bytes 1572872 | tf_op jit(solution)/shard_map/ppermute | solution.py:18
  70.3 2.1 %collective-permute-start.16 = (bf16[32,32,256]{2,1,0:T(8,128)(2,1)S(1)}, bf16[32,32,256]{2,1,0:T(8,128)(2,1)S(1)}, u32[]{:S(2)}, u32[]{:S(2)}) collective-permute-start(bf16[32,32,256]{2,1,0:T(8,128)(2,1)S(1)} %get-tuple-element.22.delta_ref), channel_id=1, source_target_pairs={{0,64},{32,96},{64,0},{96,32},{1,65},{33,97},{65,1},{97,33},{2,66}... | collective-permute-start | bytes 1572872 | tf_op jit(solution)/shard_map/ppermute | solution.py:18
  72.4 3.9 %collective-permute-start.10 = (bf16[34,1,256]{2,1,0:T(2,128)(2,1)S(1)}, bf16[34,1,256]{2,1,0:T(2,128)(2,1)S(1)}, u32[]{:S(2)}, u32[]{:S(2)}) collective-permute-start(bf16[34,1,256]{2,1,0:T(2,128)(2,1)S(1)} %get-tuple-element.51), channel_id=1, source_target_pairs={{0,1},{1,2},{2,3},{3,4},{4,5},{5,6},{6,7},{7,8},{8,9},{9,10},{10,1... | collective-permute-start | bytes 52232 | tf_op jit(solution)/shard_map/ppermute | solution.py:27
  78.8 3.2 %collective-permute-done.11 = bf16[34,1,256]{2,1,0:T(2,128)(2,1)S(1)} collective-permute-done((bf16[34,1,256]{2,1,0:T(2,128)(2,1)S(1)}, bf16[34,1,256]{2,1,0:T(2,128)(2,1)S(1)}, u32[]{:S(2)}, u32[]{:S(2)}) %collective-permute-start.11) | collective-permute-done | bytes 17440 | tf_op jit(solution)/shard_map/ppermute | solution.py:27
  94.4 2.5 %collective-permute-start.19 = (bf16[384,768]{1,0:T(8,128)(2,1)S(1)}, bf16[384,768]{1,0:T(8,128)(2,1)}, u32[]{:S(2)}, u32[]{:S(2)}) collective-permute-start(bf16[384,768]{1,0:T(8,128)(2,1)S(1)} %get-tuple-element.14), channel_id=1, source_target_pairs={{0,16},{16,0},{1,17},{17,1},{2,18},{18,2},{3,19},{19,3},{4,20},{20... | collective-permute-start | bytes 1769480 | tf_op jit(solution)/shard_map/ppermute | solution.py:18
  97.1 2.9 %collective-permute-start.21 = (bf16[288,256]{1,0:T(8,128)(2,1)S(1)}, bf16[288,256]{1,0:T(8,128)(2,1)S(1)}, u32[]{:S(2)}, u32[]{:S(2)}) collective-permute-start(bf16[288,256]{1,0:T(8,128)(2,1)S(1)} %get-tuple-element.29), channel_id=1, source_target_pairs={{0,32},{32,64},{64,96},{96,0},{1,33},{33,65},{65,97},{97,1},{2,34}... | collective-permute-start | bytes 442376 | tf_op jit(solution)/shard_map/ppermute | solution.py:18
  100.0 3.5 %collective-permute-start.23 = (bf16[288,256]{1,0:T(8,128)(2,1)S(1)}, bf16[288,256]{1,0:T(8,128)(2,1)S(1)}, u32[]{:S(2)}, u32[]{:S(2)}) collective-permute-start(bf16[288,256]{1,0:T(8,128)(2,1)S(1)} %get-tuple-element.30), channel_id=1, source_target_pairs={{0,64},{32,96},{64,0},{96,32},{1,65},{33,97},{65,1},{97,33},{2,66}... | collective-permute-start | bytes 442376 | tf_op jit(solution)/shard_map/ppermute | solution.py:18
  105.7 3.7 %collective-permute-done.23 = bf16[288,256]{1,0:T(8,128)(2,1)S(1)} collective-permute-done((bf16[288,256]{1,0:T(8,128)(2,1)S(1)}, bf16[288,256]{1,0:T(8,128)(2,1)S(1)}, u32[]{:S(2)}, u32[]{:S(2)}) %collective-permute-start.23) | collective-permute-done | bytes 147488 | tf_op jit(solution)/shard_map/ppermute | solution.py:18
  113.3 2.0 %collective-permute-start.24 = (bf16[4,30,768]{2,1,0:T(8,128)(2,1)S(1)}, bf16[4,30,768]{2,1,0:T(8,128)(2,1)S(1)}, u32[]{:S(2)}, u32[]{:S(2)}) collective-permute-start(bf16[4,30,768]{2,1,0:T(8,128)(2,1)S(1)} %get-tuple-element.26), channel_id=1, source_target_pairs={{0,1},{1,2},{2,3},{3,0},{4,5},{5,6},{6,7},{7,4},{8,9},{9,10},{10,1... | collective-permute-start | bytes 552968 | tf_op jit(solution)/shard_map/ppermute | solution.py:18
  115.3 4.7 %collective-permute-start.25 = (bf16[4,30,768]{2,1,0:T(8,128)(2,1)S(1)}, bf16[4,30,768]{2,1,0:T(8,128)(2,1)S(1)}, u32[]{:S(2)}, u32[]{:S(2)}) collective-permute-start(bf16[4,30,768]{2,1,0:T(8,128)(2,1)S(1)} %get-tuple-element.27), channel_id=1, source_target_pairs={{0,3},{1,0},{2,1},{3,2},{4,7},{5,4},{6,5},{7,6},{8,11},{9,8},{10,9... | collective-permute-start | bytes 552968 | tf_op jit(solution)/shard_map/ppermute | solution.py:18
  121.4 2.6 %collective-permute-done.24 = bf16[4,30,768]{2,1,0:T(8,128)(2,1)S(1)} collective-permute-done((bf16[4,30,768]{2,1,0:T(8,128)(2,1)S(1)}, bf16[4,30,768]{2,1,0:T(8,128)(2,1)S(1)}, u32[]{:S(2)}, u32[]{:S(2)}) %collective-permute-start.24) | collective-permute-done | bytes 184352 | tf_op jit(solution)/shard_map/ppermute | solution.py:18
  124.0 3.1 %collective-permute-done.25 = bf16[4,30,768]{2,1,0:T(8,128)(2,1)S(1)} collective-permute-done((bf16[4,30,768]{2,1,0:T(8,128)(2,1)S(1)}, bf16[4,30,768]{2,1,0:T(8,128)(2,1)S(1)}, u32[]{:S(2)}, u32[]{:S(2)}) %collective-permute-start.25) | collective-permute-done | bytes 184352 | tf_op jit(solution)/shard_map/ppermute | solution.py:18
  127.2 2.0 %collective-permute-done.26 = bf16[4,30,768]{2,1,0:T(8,128)(2,1)S(1)} collective-permute-done((bf16[4,30,768]{2,1,0:T(8,128)(2,1)S(1)}, bf16[4,30,768]{2,1,0:T(8,128)(2,1)S(1)}, u32[]{:S(2)}, u32[]{:S(2)}) %collective-permute-start.26) | collective-permute-done | bytes 184352 | tf_op jit(solution)/shard_map/ppermute | solution.py:18
  129.3 2.4 %collective-permute-start.27 = (bf16[30,768]{1,0:T(8,128)(2,1)S(1)}, bf16[30,768]{1,0:T(8,128)(2,1)S(1)}, u32[]{:S(2)}, u32[]{:S(2)}) collective-permute-start(bf16[30,768]{1,0:T(8,128)(2,1)S(1)} %get-tuple-element.62), channel_id=1, source_target_pairs={{0,4},{4,8},{8,12},{12,0},{1,5},{5,9},{9,13},{13,1},{2,6},{6,10},{... | collective-permute-start | bytes 138248 | tf_op jit(solution)/shard_map/ppermute | solution.py:18
  131.7 2.2 %collective-permute-start.28 = (bf16[30,768]{1,0:T(8,128)(2,1)S(1)}, bf16[30,768]{1,0:T(8,128)(2,1)S(1)}, u32[]{:S(2)}, u32[]{:S(2)}) collective-permute-start(bf16[30,768]{1,0:T(8,128)(2,1)S(1)} %get-tuple-element.64), channel_id=1, source_target_pairs={{0,12},{4,0},{8,4},{12,8},{1,13},{5,1},{9,5},{13,9},{2,14},{6,2},{... | collective-permute-start | bytes 138248 | tf_op jit(solution)/shard_map/ppermute | solution.py:18
  135.5 2.8 %collective-permute-done.29 = bf16[30,768]{1,0:T(8,128)(2,1)S(1)} collective-permute-done((bf16[30,768]{1,0:T(8,128)(2,1)S(1)}, bf16[30,768]{1,0:T(8,128)(2,1)S(1)}, u32[]{:S(2)}, u32[]{:S(2)}) %collective-permute-start.29) | collective-permute-done | bytes 46112 | tf_op jit(solution)/shard_map/ppermute | solution.py:18
  141.9 2.9 %collective-permute-done.31 = bf16[30,768]{1,0:T(8,128)(2,1)S(1)} collective-permute-done((bf16[30,768]{1,0:T(8,128)(2,1)S(1)}, bf16[30,768]{1,0:T(8,128)(2,1)S(1)}, u32[]{:S(2)}, u32[]{:S(2)}) %collective-permute-start.31) | collective-permute-done | bytes 46112 | tf_op jit(solution)/shard_map/ppermute | solution.py:18
  145.1 3.3 %collective-permute-start.33 = (bf16[4,30,768]{2,1,0:T(8,128)(2,1)S(1)}, bf16[4,30,768]{2,1,0:T(8,128)(2,1)S(1)}, u32[]{:S(2)}, u32[]{:S(2)}) collective-permute-start(bf16[4,30,768]{2,1,0:T(8,128)(2,1)S(1)} %get-tuple-element.19), channel_id=1, source_target_pairs={{0,3},{1,0},{2,1},{3,2},{4,7},{5,4},{6,5},{7,6},{8,11},{9,8},{10,9... | collective-permute-start | bytes 552968 | tf_op jit(solution)/shard_map/ppermute | solution.py:18
  149.9 3.2 %collective-permute-done.33 = bf16[4,30,768]{2,1,0:T(8,128)(2,1)S(1)} collective-permute-done((bf16[4,30,768]{2,1,0:T(8,128)(2,1)S(1)}, bf16[4,30,768]{2,1,0:T(8,128)(2,1)S(1)}, u32[]{:S(2)}, u32[]{:S(2)}) %collective-permute-start.33) | collective-permute-done | bytes 184352 | tf_op jit(solution)/shard_map/ppermute | solution.py:18
  154.9 2.0 %collective-permute-done.35 = bf16[4,30,768]{2,1,0:T(8,128)(2,1)S(1)} collective-permute-done((bf16[4,30,768]{2,1,0:T(8,128)(2,1)S(1)}, bf16[4,30,768]{2,1,0:T(8,128)(2,1)S(1)}, u32[]{:S(2)}, u32[]{:S(2)}) %collective-permute-start.35) | collective-permute-done | bytes 184352 | tf_op jit(solution)/shard_map/ppermute | solution.py:18
  164.3 3.5 %collective-permute-done.37 = bf16[288,256]{1,0:T(8,128)(2,1)S(1)} collective-permute-done((bf16[288,256]{1,0:T(8,128)(2,1)}, bf16[288,256]{1,0:T(8,128)(2,1)S(1)}, u32[]{:S(2)}, u32[]{:S(2)}) %collective-permute-start.37) | collective-permute-done | bytes 147488 | tf_op jit(solution)/shard_map/ppermute | solution.py:18
  171.2 9.3 %collective-permute-start.39 = (bf16[4,288,256]{2,1,0:T(8,128)(2,1)}, bf16[4,288,256]{2,1,0:T(8,128)(2,1)S(1)}, u32[]{:S(2)}, u32[]{:S(2)}) collective-permute-start(bf16[4,288,256]{2,1,0:T(8,128)(2,1)} %constant_dynamic-slice_fusion), channel_id=1, source_target_pairs={{0,16},{16,0},{1,17},{17,1},{2,18},{18,2},{3,19},{19,3},{4,20},{20... | collective-permute-start | bytes 1769480 | tf_op jit(solution)/shard_map/ppermute | solution.py:18
  (179 shorter events, 71.8 us)
Async XLA Ops:
  0.6 14.2 %collective-permute-start = (bf16[256,32,128]{2,1,0:T(8,128)(2,1)}, bf16[256,32,128]{2,1,0:T(8,128)(2,1)S(1)}, u32[]{:S(2)}, u32[]{:S(2)}) collective-permute-start(bf16[256,32,128]{2,1,0:T(8,128)(2,1)} %own_ref.1), channel_id=1, source_target_pairs={{0,16},{16,0},{1,17},{17,1},{2,18},{18,2},{3,19},{19,3},{4,20},{20... | collective-permute-start | bytes 6291464 | tf_op jit(solution)/shard_map/ppermute | solution.py:18
  2.1 11.7 %collective-permute-start.4 = (bf16[3,3,128,256]{3,2,1,0:T(8,128)(2,1)}, bf16[3,3,128,256]{3,2,1,0:T(8,128)(2,1)S(1)}, u32[]{:S(2)}, u32[]{:S(2)}) collective-permute-start(bf16[3,3,128,256]{3,2,1,0:T(8,128)(2,1)} %param.5), channel_id=1, source_target_pairs={{0,16},{16,0},{1,17},{17,1},{2,18},{18,2},{3,19},{19,3},{4,20},{20... | collective-permute-start | bytes 1769480 | tf_op jit(solution)/shard_map/ppermute | solution.py:18
  6.9 5.0 %collective-permute-start.2 = (bf16[256,1,128]{2,0,1:T(8,128)(2,1)S(1)}, bf16[256,1,128]{2,0,1:T(8,128)(2,1)S(1)}, u32[]{:S(2)}, u32[]{:S(2)}) collective-permute-start(bf16[256,1,128]{2,0,1:T(8,128)(2,1)S(1)} %copy.13), channel_id=1, source_target_pairs={{1,0},{2,1},{3,2},{4,3},{5,4},{6,5},{7,6},{8,7},{9,8},{10,9},{11,1... | collective-permute-start | bytes 196616 | tf_op jit(solution)/shard_map/ppermute | solution.py:27
  22.3 9.9 %collective-permute-start.12 = (bf16[1,32,256]{2,1,0:T(8,128)(2,1)S(1)}, bf16[1,32,256]{2,1,0:T(8,128)(2,1)S(1)}, u32[]{:S(2)}, u32[]{:S(2)}) collective-permute-start(bf16[1,32,256]{2,1,0:T(8,128)(2,1)S(1)} %get-tuple-element.57), channel_id=1, source_target_pairs={{0,16},{16,32},{32,48},{48,64},{64,80},{80,96},{96,112},{1,17},{17... | collective-permute-start | bytes 49160 | tf_op jit(solution)/shard_map/ppermute | solution.py:27
  26.1 34.1 %collective-permute-start.7 = (bf16[32,32,256]{2,1,0:T(8,128)(2,1)S(1)}, bf16[32,32,256]{2,1,0:T(8,128)(2,1)S(1)}, u32[]{:S(2)}, u32[]{:S(2)}) collective-permute-start(bf16[32,32,256]{2,1,0:T(8,128)(2,1)S(1)} %conv_first.6), channel_id=1, source_target_pairs={{0,96},{32,0},{64,32},{96,64},{1,97},{33,1},{65,33},{97,65},{2,98}... | collective-permute-start | bytes 1572872 | tf_op jit(solution)/shard_map/ppermute | solution.py:18
  26.6 33.6 %collective-permute-start.6 = (bf16[32,32,256]{2,1,0:T(8,128)(2,1)S(1)}, bf16[32,32,256]{2,1,0:T(8,128)(2,1)S(1)}, u32[]{:S(2)}, u32[]{:S(2)}) collective-permute-start(bf16[32,32,256]{2,1,0:T(8,128)(2,1)S(1)} %conv_first.5), channel_id=1, source_target_pairs={{0,32},{32,64},{64,96},{96,0},{1,33},{33,65},{65,97},{97,1},{2,34}... | collective-permute-start | bytes 1572872 | tf_op jit(solution)/shard_map/ppermute | solution.py:18
  27.7 32.5 %collective-permute-start.5 = (bf16[32,32,256]{2,1,0:T(8,128)(2,1)S(1)}, bf16[32,32,256]{2,1,0:T(8,128)(2,1)S(1)}, u32[]{:S(2)}, u32[]{:S(2)}) collective-permute-start(bf16[32,32,256]{2,1,0:T(8,128)(2,1)S(1)} %conv_first.4), channel_id=1, source_target_pairs={{0,64},{32,96},{64,0},{96,32},{1,65},{33,97},{65,1},{97,33},{2,66}... | collective-permute-start | bytes 1572872 | tf_op jit(solution)/shard_map/ppermute | solution.py:18
  30.3 20.0 %collective-permute-start.13 = (bf16[1,32,256]{2,1,0:T(8,128)(2,1)S(1)}, bf16[1,32,256]{2,1,0:T(8,128)(2,1)S(1)}, u32[]{:S(2)}, u32[]{:S(2)}) collective-permute-start(bf16[1,32,256]{2,1,0:T(8,128)(2,1)S(1)} %get-tuple-element.56), channel_id=1, source_target_pairs={{16,0},{32,16},{48,32},{64,48},{80,64},{96,80},{112,96},{17,1},{33... | collective-permute-start | bytes 49160 | tf_op jit(solution)/shard_map/ppermute | solution.py:27
  50.6 6.0 %collective-permute-start.14 = (bf16[34,1,256]{2,1,0:T(2,128)(2,1)S(1)}, bf16[34,1,256]{2,1,0:T(2,128)(2,1)S(1)}, u32[]{:S(2)}, u32[]{:S(2)}) collective-permute-start(bf16[34,1,256]{2,1,0:T(2,128)(2,1)S(1)} %get-tuple-element.47), channel_id=1, source_target_pairs={{1,0},{2,1},{3,2},{4,3},{5,4},{6,5},{7,6},{8,7},{9,8},{10,9},{11,1... | collective-permute-start | bytes 52232 | tf_op jit(solution)/shard_map/ppermute | solution.py:27
  51.9 5.0 %collective-permute-start.15 = (bf16[34,1,256]{2,1,0:T(2,128)(2,1)S(1)}, bf16[34,1,256]{2,1,0:T(2,128)(2,1)S(1)}, u32[]{:S(2)}, u32[]{:S(2)}) collective-permute-start(bf16[34,1,256]{2,1,0:T(2,128)(2,1)S(1)} %get-tuple-element.48), channel_id=1, source_target_pairs={{0,1},{1,2},{2,3},{3,4},{4,5},{5,6},{6,7},{7,8},{8,9},{9,10},{10,1... | collective-permute-start | bytes 52232 | tf_op jit(solution)/shard_map/ppermute | solution.py:27
  60.9 11.5 %collective-permute-start.8 = (bf16[1,32,256]{2,1,0:T(8,128)(2,1)S(1)}, bf16[1,32,256]{2,1,0:T(8,128)(2,1)S(1)}, u32[]{:S(2)}, u32[]{:S(2)}) collective-permute-start(bf16[1,32,256]{2,1,0:T(8,128)(2,1)S(1)} %get-tuple-element.60), channel_id=1, source_target_pairs={{0,16},{16,32},{32,48},{48,64},{64,80},{80,96},{96,112},{1,17},{17... | collective-permute-start | bytes 49160 | tf_op jit(solution)/shard_map/ppermute | solution.py:27
  63.6 8.7 %collective-permute-start.9 = (bf16[1,32,256]{2,1,0:T(8,128)(2,1)S(1)}, bf16[1,32,256]{2,1,0:T(8,128)(2,1)S(1)}, u32[]{:S(2)}, u32[]{:S(2)}) collective-permute-start(bf16[1,32,256]{2,1,0:T(8,128)(2,1)S(1)} %get-tuple-element.61), channel_id=1, source_target_pairs={{16,0},{32,16},{48,32},{64,48},{80,64},{96,80},{112,96},{17,1},{33... | collective-permute-start | bytes 49160 | tf_op jit(solution)/shard_map/ppermute | solution.py:27
  67.5 21.6 %collective-permute-start.18 = (bf16[32,32,256]{2,1,0:T(8,128)(2,1)S(1)}, bf16[32,32,256]{2,1,0:T(8,128)(2,1)S(1)}, u32[]{:S(2)}, u32[]{:S(2)}) collective-permute-start(bf16[32,32,256]{2,1,0:T(8,128)(2,1)S(1)} %get-tuple-element.22.delta_ref), channel_id=1, source_target_pairs={{0,32},{32,64},{64,96},{96,0},{1,33},{33,65},{65,97},{97,1},{2,34}... | collective-permute-start | bytes 1572872 | tf_op jit(solution)/shard_map/ppermute | solution.py:18
  67.7 23.2 %collective-permute-start.17 = (bf16[32,32,256]{2,1,0:T(8,128)(2,1)S(1)}, bf16[32,32,256]{2,1,0:T(8,128)(2,1)S(1)}, u32[]{:S(2)}, u32[]{:S(2)}) collective-permute-start(bf16[32,32,256]{2,1,0:T(8,128)(2,1)S(1)} %get-tuple-element.22.delta_ref), channel_id=1, source_target_pairs={{0,96},{32,0},{64,32},{96,64},{1,97},{33,1},{65,33},{97,65},{2,98}... | collective-permute-start | bytes 1572872 | tf_op jit(solution)/shard_map/ppermute | solution.py:18
  70.3 22.4 %collective-permute-start.16 = (bf16[32,32,256]{2,1,0:T(8,128)(2,1)S(1)}, bf16[32,32,256]{2,1,0:T(8,128)(2,1)S(1)}, u32[]{:S(2)}, u32[]{:S(2)}) collective-permute-start(bf16[32,32,256]{2,1,0:T(8,128)(2,1)S(1)} %get-tuple-element.22.delta_ref), channel_id=1, source_target_pairs={{0,64},{32,96},{64,0},{96,32},{1,65},{33,97},{65,1},{97,33},{2,66}... | collective-permute-start | bytes 1572872 | tf_op jit(solution)/shard_map/ppermute | solution.py:18
  72.4 6.4 %collective-permute-start.10 = (bf16[34,1,256]{2,1,0:T(2,128)(2,1)S(1)}, bf16[34,1,256]{2,1,0:T(2,128)(2,1)S(1)}, u32[]{:S(2)}, u32[]{:S(2)}) collective-permute-start(bf16[34,1,256]{2,1,0:T(2,128)(2,1)S(1)} %get-tuple-element.51), channel_id=1, source_target_pairs={{0,1},{1,2},{2,3},{3,4},{4,5},{5,6},{6,7},{7,8},{8,9},{9,10},{10,1... | collective-permute-start | bytes 52232 | tf_op jit(solution)/shard_map/ppermute | solution.py:27
  76.4 5.6 %collective-permute-start.11 = (bf16[34,1,256]{2,1,0:T(2,128)(2,1)S(1)}, bf16[34,1,256]{2,1,0:T(2,128)(2,1)S(1)}, u32[]{:S(2)}, u32[]{:S(2)}) collective-permute-start(bf16[34,1,256]{2,1,0:T(2,128)(2,1)S(1)} %get-tuple-element.52), channel_id=1, source_target_pairs={{1,0},{2,1},{3,2},{4,3},{5,4},{6,5},{7,6},{8,7},{9,8},{10,9},{11,1... | collective-permute-start | bytes 52232 | tf_op jit(solution)/shard_map/ppermute | solution.py:27
  85.7 11.2 %collective-permute-start.20 = (bf16[1152,256]{1,0:T(8,128)(2,1)S(1)}, bf16[1152,256]{1,0:T(8,128)(2,1)S(1)}, u32[]{:S(2)}, u32[]{:S(2)}) collective-permute-start(bf16[1152,256]{1,0:T(8,128)(2,1)S(1)} %fusion.16), channel_id=1, source_target_pairs={{0,16},{16,0},{1,17},{17,1},{2,18},{18,2},{3,19},{19,3},{4,20},{20... | collective-permute-start | bytes 1769480 | tf_op jit(solution)/shard_map/ppermute | solution.py:18
  94.4 17.6 %collective-permute-start.19 = (bf16[384,768]{1,0:T(8,128)(2,1)S(1)}, bf16[384,768]{1,0:T(8,128)(2,1)}, u32[]{:S(2)}, u32[]{:S(2)}) collective-permute-start(bf16[384,768]{1,0:T(8,128)(2,1)S(1)} %get-tuple-element.14), channel_id=1, source_target_pairs={{0,16},{16,0},{1,17},{17,1},{2,18},{18,2},{3,19},{19,3},{4,20},{20... | collective-permute-start | bytes 1769480 | tf_op jit(solution)/shard_map/ppermute | solution.py:18
  97.1 6.7 %collective-permute-start.21 = (bf16[288,256]{1,0:T(8,128)(2,1)S(1)}, bf16[288,256]{1,0:T(8,128)(2,1)S(1)}, u32[]{:S(2)}, u32[]{:S(2)}) collective-permute-start(bf16[288,256]{1,0:T(8,128)(2,1)S(1)} %get-tuple-element.29), channel_id=1, source_target_pairs={{0,32},{32,64},{64,96},{96,0},{1,33},{33,65},{65,97},{97,1},{2,34}... | collective-permute-start | bytes 442376 | tf_op jit(solution)/shard_map/ppermute | solution.py:18
  100.0 5.7 %collective-permute-start.22 = (bf16[288,256]{1,0:T(8,128)(2,1)S(1)}, bf16[288,256]{1,0:T(8,128)(2,1)S(1)}, u32[]{:S(2)}, u32[]{:S(2)}) collective-permute-start(bf16[288,256]{1,0:T(8,128)(2,1)S(1)} %get-tuple-element.31), channel_id=1, source_target_pairs={{0,96},{32,0},{64,32},{96,64},{1,97},{33,1},{65,33},{97,65},{2,98}... | collective-permute-start | bytes 442376 | tf_op jit(solution)/shard_map/ppermute | solution.py:18
  100.0 9.4 %collective-permute-start.23 = (bf16[288,256]{1,0:T(8,128)(2,1)S(1)}, bf16[288,256]{1,0:T(8,128)(2,1)S(1)}, u32[]{:S(2)}, u32[]{:S(2)}) collective-permute-start(bf16[288,256]{1,0:T(8,128)(2,1)S(1)} %get-tuple-element.30), channel_id=1, source_target_pairs={{0,64},{32,96},{64,0},{96,32},{1,65},{33,97},{65,1},{97,33},{2,66}... | collective-permute-start | bytes 442376 | tf_op jit(solution)/shard_map/ppermute | solution.py:18
  113.3 10.7 %collective-permute-start.24 = (bf16[4,30,768]{2,1,0:T(8,128)(2,1)S(1)}, bf16[4,30,768]{2,1,0:T(8,128)(2,1)S(1)}, u32[]{:S(2)}, u32[]{:S(2)}) collective-permute-start(bf16[4,30,768]{2,1,0:T(8,128)(2,1)S(1)} %get-tuple-element.26), channel_id=1, source_target_pairs={{0,1},{1,2},{2,3},{3,0},{4,5},{5,6},{6,7},{7,4},{8,9},{9,10},{10,1... | collective-permute-start | bytes 552968 | tf_op jit(solution)/shard_map/ppermute | solution.py:18
  115.3 11.9 %collective-permute-start.25 = (bf16[4,30,768]{2,1,0:T(8,128)(2,1)S(1)}, bf16[4,30,768]{2,1,0:T(8,128)(2,1)S(1)}, u32[]{:S(2)}, u32[]{:S(2)}) collective-permute-start(bf16[4,30,768]{2,1,0:T(8,128)(2,1)S(1)} %get-tuple-element.27), channel_id=1, source_target_pairs={{0,3},{1,0},{2,1},{3,2},{4,7},{5,4},{6,5},{7,6},{8,11},{9,8},{10,9... | collective-permute-start | bytes 552968 | tf_op jit(solution)/shard_map/ppermute | solution.py:18
  120.0 9.1 %collective-permute-start.26 = (bf16[4,30,768]{2,1,0:T(8,128)(2,1)S(1)}, bf16[4,30,768]{2,1,0:T(8,128)(2,1)S(1)}, u32[]{:S(2)}, u32[]{:S(2)}) collective-permute-start(bf16[4,30,768]{2,1,0:T(8,128)(2,1)S(1)} %get-tuple-element.28), channel_id=1, source_target_pairs={{0,2},{1,3},{2,0},{3,1},{4,6},{5,7},{6,4},{7,5},{8,10},{9,11},{10,... | collective-permute-start | bytes 552968 | tf_op jit(solution)/shard_map/ppermute | solution.py:18
  129.3 6.2 %collective-permute-start.27 = (bf16[30,768]{1,0:T(8,128)(2,1)S(1)}, bf16[30,768]{1,0:T(8,128)(2,1)S(1)}, u32[]{:S(2)}, u32[]{:S(2)}) collective-permute-start(bf16[30,768]{1,0:T(8,128)(2,1)S(1)} %get-tuple-element.62), channel_id=1, source_target_pairs={{0,4},{4,8},{8,12},{12,0},{1,5},{5,9},{9,13},{13,1},{2,6},{6,10},{... | collective-permute-start | bytes 138248 | tf_op jit(solution)/shard_map/ppermute | solution.py:18
  145.1 8.0 %collective-permute-start.33 = (bf16[4,30,768]{2,1,0:T(8,128)(2,1)S(1)}, bf16[4,30,768]{2,1,0:T(8,128)(2,1)S(1)}, u32[]{:S(2)}, u32[]{:S(2)}) collective-permute-start(bf16[4,30,768]{2,1,0:T(8,128)(2,1)S(1)} %get-tuple-element.19), channel_id=1, source_target_pairs={{0,3},{1,0},{2,1},{3,2},{4,7},{5,4},{6,5},{7,6},{8,11},{9,8},{10,9... | collective-permute-start | bytes 552968 | tf_op jit(solution)/shard_map/ppermute | solution.py:18
  148.7 6.2 %collective-permute-start.34 = (bf16[4,30,768]{2,1,0:T(8,128)(2,1)S(1)}, bf16[4,30,768]{2,1,0:T(8,128)(2,1)S(1)}, u32[]{:S(2)}, u32[]{:S(2)}) collective-permute-start(bf16[4,30,768]{2,1,0:T(8,128)(2,1)S(1)} %get-tuple-element.19), channel_id=1, source_target_pairs={{0,2},{1,3},{2,0},{3,1},{4,6},{5,7},{6,4},{7,5},{8,10},{9,11},{10,... | collective-permute-start | bytes 552968 | tf_op jit(solution)/shard_map/ppermute | solution.py:18
  149.9 7.0 %collective-permute-start.35 = (bf16[4,30,768]{2,1,0:T(8,128)(2,1)S(1)}, bf16[4,30,768]{2,1,0:T(8,128)(2,1)S(1)}, u32[]{:S(2)}, u32[]{:S(2)}) collective-permute-start(bf16[4,30,768]{2,1,0:T(8,128)(2,1)S(1)} %get-tuple-element.19), channel_id=1, source_target_pairs={{0,1},{1,2},{2,3},{3,0},{4,5},{5,6},{6,7},{7,4},{8,9},{9,10},{10,1... | collective-permute-start | bytes 552968 | tf_op jit(solution)/shard_map/ppermute | solution.py:18
  161.9 5.9 %collective-permute-start.37 = (bf16[288,256]{1,0:T(8,128)(2,1)}, bf16[288,256]{1,0:T(8,128)(2,1)S(1)}, u32[]{:S(2)}, u32[]{:S(2)}) collective-permute-start(bf16[288,256]{1,0:T(8,128)(2,1)} %reshape.154), channel_id=1, source_target_pairs={{0,64},{32,96},{64,0},{96,32},{1,65},{33,97},{65,1},{97,33},{2,66}... | collective-permute-start | bytes 442376 | tf_op jit(solution)/shard_map/ppermute | solution.py:18
  162.5 6.8 %collective-permute-start.38 = (bf16[288,256]{1,0:T(8,128)(2,1)}, bf16[288,256]{1,0:T(8,128)(2,1)S(1)}, u32[]{:S(2)}, u32[]{:S(2)}) collective-permute-start(bf16[288,256]{1,0:T(8,128)(2,1)} %reshape.154), channel_id=1, source_target_pairs={{0,32},{32,64},{64,96},{96,0},{1,33},{33,65},{65,97},{97,1},{2,34}... | collective-permute-start | bytes 442376 | tf_op jit(solution)/shard_map/ppermute | solution.py:18
  171.2 14.1 %collective-permute-start.39 = (bf16[4,288,256]{2,1,0:T(8,128)(2,1)}, bf16[4,288,256]{2,1,0:T(8,128)(2,1)S(1)}, u32[]{:S(2)}, u32[]{:S(2)}) collective-permute-start(bf16[4,288,256]{2,1,0:T(8,128)(2,1)} %constant_dynamic-slice_fusion), channel_id=1, source_target_pairs={{0,16},{16,0},{1,17},{17,1},{2,18},{18,2},{3,19},{19,3},{4,20},{20... | collective-permute-start | bytes 1769480 | tf_op jit(solution)/shard_map/ppermute | solution.py:18
  (25 other events, 171.3 us)

commit v3 on v2

--- a/solution.py
+++ b/solution.py
@@ -11,6 +11,7 @@
 SKY = ("z", "x")
 F32 = jnp.float32
 BF16 = jnp.bfloat16
+QUICK = pl.CostEstimate(flops=1, bytes_accessed=1, transcendentals=0)
 
 
 def shift(x, axis, step):
@@ -25,13 +26,6 @@
     last = lax.slice_in_dim(x, length - 1, length, axis=dim)
     first = lax.slice_in_dim(x, 0, 1, axis=dim)
     return lax.ppermute(last, axes, up), lax.ppermute(first, axes, down)
-
-
-def with_halo(x):
-    for axes, dim in ((FREQ, 0), (SKY, 1)):
-        before, after = halo(x, axes, dim)
-        x = jnp.concatenate([before, x, after], axis=dim)
-    return x
 
 
 def spread_kernel(own_ref, far_ref, own_halo_ref, far_halo_ref, out_ref):
@@ -110,7 +104,7 @@
         in_specs=[VMEM_SPEC] * 4,
         out_specs=VMEM_SPEC,
         compiler_params=pltpu.CompilerParams(vmem_limit_bytes=16 * 2**20),
-        cost_estimate=pl.CostEstimate(flops=2**20, bytes_accessed=12 * 2**20, transcendentals=0),
+        cost_estimate=QUICK,
         name="spread",
     )(own, far, own_halo, far_halo)
 
@@ -132,9 +126,7 @@
         in_specs=[SMEM_SPEC, VMEM_SPEC, VMEM_SPEC],
         out_specs=VMEM_SPEC,
         compiler_params=pltpu.CompilerParams(vmem_limit_bytes=16 * 2**20),
-        cost_estimate=pl.CostEstimate(
-            flops=2 * strip * rows * depth * outs, bytes_accessed=4 * 2**20, transcendentals=0
-        ),
+        cost_estimate=QUICK,
         name="conv_first",
     )(chip.reshape(1), wide, kernel)
 
@@ -183,76 +175,250 @@
         out_specs=tuple([VMEM_SPEC] * len(out_shape)),
         scratch_shapes=[pltpu.VMEM((cols + 2, rows, outs), BF16)],
         compiler_params=pltpu.CompilerParams(vmem_limit_bytes=20 * 2**20),
-        cost_estimate=pl.CostEstimate(
-            flops=2 * cols * rows * depth * 3 * outs, bytes_accessed=6 * 2**20, transcendentals=0
-        ),
+        cost_estimate=QUICK,
         name="grad_first",
     )(*args)
     return out if last else out[0]
 
 
-def conv_taps(padded, kernel, col_count, row_count):
-    total = jnp.zeros((col_count * row_count, kernel.shape[3]), F32)
+def spread_tile(ref, left_ref, right_ref, edge_ref, wide_ref):
+    cols, rows, chans = ref.shape
+    place = lax.broadcasted_iota(jnp.int32, (rows, chans), 0)
+
+    def put(mid, j):
+        wide = mid.astype(F32)
+        before = edge_ref[0, j : j + 1, :].astype(F32)
+        after = edge_ref[1, j : j + 1, :].astype(F32)
+        ahead = jnp.where(place == 0, before, pltpu.roll(wide, 1, 0))
+        behind = jnp.where(place == rows - 1, after, pltpu.roll(wide, rows - 1, 0))
+        wide_ref[j, :, 0:chans] = ahead.astype(BF16)
+        wide_ref[j, :, chans : 2 * chans] = mid
+        wide_ref[j, :, 2 * chans :] = behind.astype(BF16)
+
+    put(left_ref[0], 0)
+    for j in range(cols):
+        put(ref[j], j + 1)
+    put(right_ref[0], cols + 1)
+
+
+def back_kernel(cot_ref, left_ref, right_ref, edge_ref, kernel_ref, out_ref, wide_ref):
+    cols, rows, chans = cot_ref.shape
+    spread_tile(cot_ref, left_ref, right_ref, edge_ref, wide_ref)
+    total = None
     for tap_col in range(3):
+        lhs = wide_ref[tap_col : tap_col + cols].reshape(cols * rows, 3 * chans)
         for tap_row in range(3):
-            piece = padded[tap_col : tap_col + col_count, tap_row : tap_row + row_count].reshape(
-                col_count * row_count, -1
-            )
-            total = total + jnp.dot(piece, kernel[tap_col, tap_row], preferred_element_type=F32)
-    return total.reshape(col_count, row_count, kernel.shape[3])
-
-
-def conv_back(padded, kernel, col_count, row_count):
-    total = jnp.zeros((col_count * row_count, kernel.shape[2]), F32)
-    for tap_col in range(3):
-        for tap_row in range(3):
-            piece = padded[
-                2 - tap_col : 2 - tap_col + col_count, 2 - tap_row : 2 - tap_row + row_count
-            ].reshape(col_count * row_count, -1)
-            total = total + lax.dot_general(
-                piece,
-                kernel[tap_col, tap_row],
+            part = lax.dot_general(
+                lhs[:, tap_row * chans : (tap_row + 1) * chans],
+                kernel_ref[2 - tap_col, 2 - tap_row],
                 (((1,), (1,)), ((), ())),
                 preferred_element_type=F32,
             )
-    return total.reshape(col_count, row_count, kernel.shape[2])
-
-
-def kernel_grad(padded, grads, col_count, row_count):
-    flat = grads.reshape(col_count * row_count, -1)
-    lines = []
+            total = part if total is None else total + part
+    out_ref[...] = total.reshape(cols, rows, -1)
+
+
+def back_tile(tile, left, right, edges, kernel):
+    cols, rows, chans = tile.shape
+    return pl.pallas_call(
+        back_kernel,
+        out_shape=jax.ShapeDtypeStruct((cols, rows, kernel.shape[2]), F32),
+        in_specs=[VMEM_SPEC] * 5,
+        out_specs=VMEM_SPEC,
+        scratch_shapes=[pltpu.VMEM((cols + 2, rows, 3 * chans), BF16)],
+        compiler_params=pltpu.CompilerParams(vmem_limit_bytes=20 * 2**20),
+        cost_estimate=QUICK,
+        name="back",
+    )(tile, left, right, edges, kernel)
+
+
+def second_kernel(
+    chips, hid_ref, left_ref, right_ref, edge_ref, kernel_ref, cot_ref,
+    out_ref, near_ref, far_ref, wide_ref, pad_ref, sum_ref,
+):
+    cols, rows, chans = hid_ref.shape
+    outs = cot_ref.shape[2]
+    width = wide_ref.shape[0]
+    core = lax.axis_index("c")
+    spread_tile(hid_ref, left_ref, right_ref, edge_ref, wide_ref)
+    wide_ref[cols + 2 :] = jnp.zeros((width - cols - 2, rows, 3 * chans), BF16)
+    pieces = [wide_ref[tap : tap + cols] for tap in range(3)]
+    lhs = jnp.concatenate(pieces, axis=-1).reshape(cols * rows, 9 * chans)
+    total = jnp.dot(lhs, kernel_ref[...], preferred_element_type=F32)
+    out_ref[...] = total.reshape(cols, rows, outs).astype(BF16)
+
+    pad_ref[0:2] = jnp.zeros((2, rows, outs), BF16)
+    pad_ref[2 : 2 + cols] = cot_ref[...]
+    pad_ref[2 + cols :] = jnp.zeros((width - cols, rows, outs), BF16)
+    rhs = jnp.concatenate(
+        [pad_ref[2 - tap : 2 - tap + width].reshape(width * rows, outs) for tap in range(3)],
+        axis=-1,
+    )
+    sum_ref[...] = lax.dot_general(
+        wide_ref[...].reshape(width * rows, 3 * chans),
+        rhs,
+        (((0,), (0,)), ((), ())),
+        preferred_element_type=F32,
+    )
+    size = sum_ref.shape[0] // (2 * chips)
+    for half, ref in ((core, near_ref), (1 - core, far_ref)):
+        for chip in range(chips):
+            at = pl.multiple_of((half * chips + chip) * size, size)
+            for tap in range(3):
+                ref[chip, tap * size : (tap + 1) * size, :] = sum_ref[
+                    pl.ds(at, size), tap * outs : (tap + 1) * outs
+                ].astype(ref.dtype)
+
+
+def second_tile(tile, left, right, edges, kernel, cotangent, chips):
+    cols, rows, chans = tile.shape
+    outs = cotangent.shape[2]
+    width = cols + 8
+    cut = (chips, 9 * chans // (2 * chips), outs)
+    return pl.pallas_call(
+        functools.partial(second_kernel, chips),
+        out_shape=(
+            jax.ShapeDtypeStruct((cols, rows, outs), BF16),
+            jax.ShapeDtypeStruct(cut, F32),
+            jax.ShapeDtypeStruct(cut, BF16),
+        ),
+        in_specs=[VMEM_SPEC] * 6,
+        out_specs=(VMEM_SPEC,) * 3,
+        scratch_shapes=[
+            pltpu.VMEM((width, rows, 3 * chans), BF16),
+            pltpu.VMEM((width + 2, rows, outs), BF16),
+            pltpu.VMEM((3 * chans, 3 * outs), F32),
+        ],
+        compiler_params=pltpu.CompilerParams(vmem_limit_bytes=28 * 2**20),
+        cost_estimate=QUICK,
+        name="second",
+    )(tile, left, right, edges, kernel.reshape(9 * chans, outs), cotangent)
+
+
+def fold_kernel(near_ref, got_ref, keep_ref, *send_refs):
+    chips = near_ref.shape[0]
+    here = lax.axis_index("y")
+    keep_ref[...] = near_ref[here] + got_ref[here].astype(F32)
+    for step, ref in zip(STEPS[1:], send_refs):
+        to = lax.rem(here + step, chips)
+        ref[...] = (near_ref[to] + got_ref[to].astype(F32)).astype(BF16)
+
+
+def fold(near, got):
+    shape = near.shape[1:]
+    return pl.pallas_call(
+        fold_kernel,
+        out_shape=(jax.ShapeDtypeStruct(shape, F32),) + (jax.ShapeDtypeStruct(shape, BF16),) * 3,
+        in_specs=[VMEM_SPEC] * 2,
+        out_specs=(VMEM_SPEC,) * 4,
+        compiler_params=pltpu.CompilerParams(vmem_limit_bytes=12 * 2**20),
+        cost_estimate=QUICK,
+        name="fold",
+    )(near, got)
+
+
+def tile_halo(x):
+    left, right = halo(x, FREQ, 0)
+    last = x.shape[1] - 1
+    ends = [
+        jnp.concatenate([left[:, r], x[:, r], right[:, r]], axis=0) for r in (last, 0)
+    ]
+    count = lax.axis_size(SKY)
+    up = [(i, i + 1) for i in range(count - 1)]
+    down = [(j, i) for i, j in up]
+    edges = jnp.stack([lax.ppermute(ends[0], SKY, up), lax.ppermute(ends[1], SKY, down)])
+    return left, right, edges
+
+
+def join_kernel(own_ref, far_ref, second_ref, out_ref):
+    pieces, extra, outs = second_ref.shape
+    chans = own_ref.shape[0] // 3
+    size = chans // pieces
     for tap_col in range(3):
         for tap_row in range(3):
-            piece = padded[tap_col : tap_col + col_count, tap_row : tap_row + row_count].reshape(
-                col_count * row_count, -1
-            )
-            lines.append(
-                lax.dot_general(piece, flat, (((0,), (0,)), ((), ())), preferred_element_type=F32)
-            )
-    return jnp.concatenate(lines, axis=0)
-
-
-def reduce_pieces(parts, axis):
-    count = lax.axis_size(axis)
-    me = lax.axis_index(axis)
-
-    def pick(at):
-        return lax.dynamic_index_in_dim(parts, at, 0, keepdims=False)
-
-    total = pick(me)
-    for step in (1, count - 1, 2) if count == 4 else range(1, count):
-        total = total + shift(pick((me + step) % count).astype(BF16), axis, step).astype(F32)
-    return total
-
-
-def gather_pieces(piece, axis):
-    count = lax.axis_size(axis)
-    me = lax.axis_index(axis)
-    got = {0: piece}
-    for step in (1, count - 1, 2) if count == 4 else range(1, count):
-        got[step] = shift(piece, axis, step)
-    turned = jnp.stack([got[(-j) % count] for j in range(count)] * 2)
-    return lax.dynamic_slice_in_dim(turned, count - me, count, 0)
+            rows = slice(tap_row * chans, (tap_row + 1) * chans)
+            lanes = slice(tap_col * outs, (tap_col + 1) * outs)
+            value = own_ref[rows, lanes] + far_ref[rows, lanes].astype(F32)
+            at = (3 * tap_col + tap_row) * size
+            out_ref[:, at : at + size, :] = value.reshape(pieces, size, outs).astype(BF16)
+    out_ref[:, 9 * size :, :] = second_ref[...]
+
+
+def join(own, far, second):
+    pieces, extra, outs = second.shape
+    rows = 9 * (own.shape[0] // 3 // pieces) + extra
+    return pl.pallas_call(
+        join_kernel,
+        out_shape=jax.ShapeDtypeStruct((pieces, rows, outs), BF16),
+        in_specs=[VMEM_SPEC] * 3,
+        out_specs=VMEM_SPEC,
+        compiler_params=pltpu.CompilerParams(vmem_limit_bytes=16 * 2**20),
+        cost_estimate=QUICK,
+        name="join",
+    )(own, far, second)
+
+
+STEPS = (0, 1, 3, 2)
+
+
+def first_kernel(sz, a_ref, b_ref, c_ref, d_ref, out_ref):
+    sx = lax.axis_size("x")
+    size = out_ref.shape[2] // (sx * sz)
+    me = lax.axis_index("x")
+    for step, ref in zip(STEPS, (a_ref, b_ref, c_ref, d_ref)):
+        x = lax.rem(me + sx - step, sx)
+        value = ref[...].astype(F32)
+        for z in range(sz):
+            at = pl.multiple_of((z * sx + x) * size, size)
+            for tap in range(9):
+                rows = (z * 9 + tap) * size
+                out_ref[tap // 3, tap % 3, pl.ds(at, size), :] = value[rows : rows + size]
+
+
+def lay_first(parts, sz, chans):
+    outs = parts[0].shape[1]
+    return pl.pallas_call(
+        functools.partial(first_kernel, sz),
+        out_shape=jax.ShapeDtypeStruct((3, 3, chans, outs), F32),
+        in_specs=[VMEM_SPEC] * 4,
+        out_specs=VMEM_SPEC,
+        compiler_params=pltpu.CompilerParams(vmem_limit_bytes=16 * 2**20),
+        cost_estimate=QUICK,
+        name="lay_first",
+    )(*parts)
+
+
+def lay_second_kernel(near_ref, far_ref, out_ref):
+    sy, sx, rows, _ = near_ref.shape
+    size = rows // 3
+    third = out_ref.shape[0] // 3
+    core, y, x = lax.axis_index("c"), lax.axis_index("y"), lax.axis_index("x")
+    for half, ref in ((core, near_ref), (1 - core, far_ref)):
+        for i in range(sy):
+            for j in range(sx):
+                place = (half * sy + lax.rem(y + sy - STEPS[i], sy)) * sx
+                place = place + lax.rem(x + sx - STEPS[j], sx)
+                value = ref[i, j].astype(F32)
+                for tap in range(3):
+                    at = pl.multiple_of(tap * third + place * size, 8)
+                    out_ref[pl.ds(at, size), :] = value[tap * size : (tap + 1) * size]
+
+
+def lay_second(near, far):
+    sy, sx, rows, outs = near.shape
+    return pl.pallas_call(
+        lay_second_kernel,
+        out_shape=jax.ShapeDtypeStruct((2 * sy * sx * rows, outs), F32),
+        in_specs=[VMEM_SPEC] * 2,
+        out_specs=VMEM_SPEC,
+        compiler_params=pltpu.CompilerParams(vmem_limit_bytes=16 * 2**20),
+        cost_estimate=QUICK,
+        name="lay_second",
+    )(near, far)
+
+
+def gather_steps(piece, axis):
+    return [piece] + [shift(piece, axis, step) for step in STEPS[1:]]
 
 
 def body(sky_cube, weight_first, weight_second, cotangent):
@@ -276,47 +442,54 @@
         part = conv_strip((here + step) % chips, hold, kernel, strip, BF16)
         near.append(part)
         hold, _ = lax.optimization_barrier((wide, part))
-    own = conv_strip(here, hold, kernel, strip, F32)
+    own = conv_strip(here, wide, kernel, strip, F32)
     pre = own
     for step, part in zip(order, near):
         pre = pre + shift(part, "y", step).astype(F32)
 
-    late_cotangent, _ = lax.optimization_barrier((cotangent, own))
-    back = conv_back(with_halo(late_cotangent), weight_second, strip, rows)
+    late_cotangent, _ = lax.optimization_barrier((cotangent, near[-1]))
+    back = back_tile(late_cotangent, *tile_halo(late_cotangent), weight_second)
     sigma = jax.nn.sigmoid(pre)
     delta = (back * (sigma * (1.0 + pre * (1.0 - sigma)))).astype(BF16)
     hidden = (pre * sigma).astype(BF16)
 
+    pieces = [(step, shift(delta, "y", step)) for step in (1, chips - 1, 2)]
     total = grad_strip(here, wide, delta, None, False)
-    for step in (1, chips - 1, 2):
-        piece = shift(delta, "y", step)
-        total = grad_strip((here - step) % chips, wide, piece, total, step == 2)
+    late_hidden, _ = lax.optimization_barrier((hidden, total))
+
+    edges = tile_halo(late_hidden)
+    for step, piece in pieces[:2]:
+        total = grad_strip((here - step) % chips, wide, piece, total, False)
+    late_hidden, _ = lax.optimization_barrier((late_hidden, total))
+    features, near, far = second_tile(late_hidden, *edges, weight_second, cotangent, chips)
+    keep, *sends = fold(near, shift(far, "c", 1))
+    for step, send in zip(STEPS[1:], sends):
+        keep = keep + shift(send, "y", step).astype(F32)
+    sx, sz = lax.axis_size("x"), lax.axis_size("z")
+    second = keep.astype(BF16).reshape(3, sx, -1, outs)
+    second = jnp.transpose(second, (1, 0, 2, 3)).reshape(sx, sz, -1, outs)
+    second = jnp.transpose(second, (1, 0, 2, 3)).reshape(sx * sz, -1, outs)
+    extra = second.shape[1]
+
+    step, piece = pieces[2]
+    total = grad_strip((here - step) % chips, wide, piece, total, True)
     first_own, first_far = total
-    first = first_own + shift(first_far, "c", 1).astype(F32)
-
-    hidden_pad = with_halo(hidden)
-    features = conv_taps(hidden_pad, weight_second, strip, rows).astype(BF16)
-    second = kernel_grad(hidden_pad, cotangent, strip, rows)
-    depth = second.shape[0]
-    second = reduce_pieces(second.reshape(2, depth // 2, outs), "c")
-    second = reduce_pieces(second.reshape(chips, depth // (2 * chips), outs), "y")
-
-    sx, sz = lax.axis_size("x"), lax.axis_size("z")
-    width = 3 * outs
-    first_parts = first.reshape(sx, -1, width)
-    second_parts = second.reshape(sx, -1, width)
-    split = first_parts.shape[1] // sz
-    joined = jnp.concatenate(
-        [first_parts.reshape(sx, sz, -1, width), second_parts.reshape(sx, sz, -1, width)], axis=2
-    )
-    summed = reduce_pieces(joined, "x")
-    summed = reduce_pieces(summed, "z").astype(BF16)
-    summed = gather_pieces(gather_pieces(summed, "z"), "x")
-    first = summed[:, :, :split].reshape(3, chans, 3, outs)
-    grad_first = jnp.transpose(first, (2, 0, 1, 3)).astype(F32)
-    share = summed[:, :, split:].reshape(depth // (2 * chips), outs)
-    share = gather_pieces(gather_pieces(share, "y"), "c")
-    grad_second = share.reshape(3, 3, outs, outs).astype(F32)
+
+    joined = join(first_own, shift(first_far, "c", 1), second)
+    summed = lax.all_to_all(joined, SKY, 0, 0, tiled=True)
+    summed = jnp.sum(summed.astype(F32), axis=0).astype(BF16)
+    rows_z = jnp.stack(gather_steps(summed, "z"))
+    me_z = lax.axis_index("z")
+    back_to = jnp.stack([(me_z - k) % sz for k in range(sz)])
+    slot_of = jnp.asarray([STEPS.index(k) for k in range(sz)])[back_to]
+    rows_z = jnp.concatenate([lax.dynamic_index_in_dim(rows_z, slot_of[k], 0) for k in range(sz)])
+    main = rows_z[:, :-extra].reshape(-1, outs)
+    rest = rows_z[:, -extra:].reshape(-1, outs)
+    parts = gather_steps(jnp.concatenate([main, rest]), "x")
+    grad_first = lay_first([part[: main.shape[0]] for part in parts], sz, chans)
+    share = jnp.stack([part[main.shape[0] :] for part in parts])
+    share = jnp.stack(gather_steps(share, "y"))
+    grad_second = lay_second(share, shift(share, "c", 1)).reshape(3, 3, outs, outs)
     return features, grad_first, grad_second
 
 

time: 188 us -> 184 us (0.979)
  Pallas kernels: 14.4 us -> 29.7 us
  starting transfers between devices: 80.6 us -> 68.8 us
  matrix products: 10.6 us -> 0 us
  between operations: 1.78 us -> 8.89 us
  other arithmetic: 9.09 us -> 3.2 us
  waiting for transfers between devices: 58.9 us -> 62.2 us
    ppermute x30 -> x24, starting transfers between devices: 55.3 us -> 30.7 us  [shift(): lax.ppermute(x, axis, [(i, (i + step) % count) for i in range(count)])]
    ppermute x30 -> x24, waiting for transfers between devices: 33.6 us -> 18.9 us  [shift(): lax.ppermute(x, axis, [(i, (i + step) % count) for i in range(count)])]
    all_to_all x0 -> x1, waiting for transfers between devices: none -> 11.8 us  [body(): summed = lax.all_to_all(joined, SKY, 0, 0, tiled=True)]
    dot_general x27 -> x0, matrix products: 10.6 us -> none  [the longest x9 4.47 us: conv_taps(): jnp.dot(piece, kernel[tap_col, tap_row], preferred_element_type=F32)]
    ppermute x0 -> x4, starting transfers between devices: none -> 10.5 us  [the longest x2 7.88 us: tile_halo(): lax.ppermute(ends[0], SKY, up)]
    pallas_call x0 -> x6, Pallas kernels: none -> 9.41 us  [the longest x1 4.14 us: second_tile(): pl.pallas_call(functools.partial(second_kernel, chips), out_shape=(jax.Sh...]
    all_to_all x0 -> x1, starting transfers between devices: none -> 9.02 us  [body(): summed = lax.all_to_all(joined, SKY, 0, 0, tiled=True)]
    ppermute x10 -> x6, starting transfers between devices: 25.3 us -> 18.5 us  [halo(): return (lax.ppermute(last, axes, up), lax.ppermute(first, axes, down))]
  transfers between devices with their start and end apart: 40 -> 35, of which waited for: 20 -> 14; matrix products, arithmetic and copies ran while one was open for 12% -> 2% of each run, Pallas kernels for 4% -> 9%
where the time goes in v3:
time: 184 us
  starting transfers between devices  68.8 us (37%)
  waiting for transfers between devices  62.2 us (34%)
  Pallas kernels  29.7 us (16%)
  local copies, waits for them, and re-layouts  10.8 us (6%)
  between operations  8.89 us (5%)
  other arithmetic  3.2 us (2%)
    ppermute x24, starting transfers between devices, shift(): lax.ppermute(x, axis, [(i, (i + step) % count) for i in range(count)])  30.7 us
    ppermute x6, waiting for transfers between devices, halo(): return (lax.ppermute(last, axes, up), lax.ppermute(first, axes, down))  28.1 us
    ppermute x24, waiting for transfers between devices, shift(): lax.ppermute(x, axis, [(i, (i + step) % count) for i in range(count)])  18.9 us
    ppermute x6, starting transfers between devices, halo(): return (lax.ppermute(last, axes, up), lax.ppermute(first, axes, down))  18.5 us
    all_to_all x1, waiting for transfers between devices, body(): summed = lax.all_to_all(joined, SKY, 0, 0, tiled=True)  11.8 us
    pallas_call x4, Pallas kernels, grad_strip(): pl.pallas_call(functools.partial(grad_kernel, old is not None, last), out...  11.3 us
    all_to_all x1, starting transfers between devices, body(): summed = lax.all_to_all(joined, SKY, 0, 0, tiled=True)  9.02 us
    ppermute x2, starting transfers between devices, tile_halo(): lax.ppermute(ends[0], SKY, up)  7.88 us
  transfers between devices with their start and end apart: 35, of which 14 were waited for; matrix products, arithmetic and copies ran while one was open for 2% of the time, Pallas kernels for 9%

profile of v3, /device:TPU:1, one launch (start us, length us, event | category | flops | bytes accessed | tf_op | source)
XLA Modules:
  0.0 183.6 jit_solution(5622753840872835658)
XLA Ops:
  3.7 3.2 %collective-permute-start.1 = (bf16[256,1,128]{2,0,1:T(8,128)(2,1)S(1)}, bf16[256,1,128]{2,0,1:T(8,128)(2,1)S(1)}, u32[]{:S(2)}, u32[]{:S(2)}) collective-permute-start(bf16[256,1,128]{2,0,1:T(8,128)(2,1)S(1)} %copy.27), channel_id=1, source_target_pairs={{0,1},{1,2},{2,3},{3,4},{4,5},{5,6},{6,7},{7,8},{8,9},{9,10},{10,1... | collective-permute-start | bytes 196616 | tf_op jit(solution)/shard_map/ppermute | solution.py:28
  8.3 3.7 %collective-permute-done.2 = bf16[256,1,128]{2,0,1:T(8,128)(2,1)S(1)} collective-permute-done((bf16[256,1,128]{2,0,1:T(8,128)(2,1)S(1)}, bf16[256,1,128]{2,0,1:T(8,128)(2,1)S(1)}, u32[]{:S(2)}, u32[]{:S(2)}) %collective-permute-start.2) | collective-permute-done | bytes 65568 | tf_op jit(solution)/shard_map/ppermute | solution.py:28
  11.9 2.0 %collective-permute-start.3 = (bf16[2,256,128]{2,1,0:T(8,128)(2,1)S(1)}, bf16[2,256,128]{2,1,0:T(8,128)(2,1)S(1)}, u32[]{:S(2)}, u32[]{:S(2)}) collective-permute-start(bf16[2,256,128]{2,1,0:T(8,128)(2,1)S(1)} %maximum_bitcast_fusion.own_halo_ref), channel_id=1, source_target_pairs={{0,16},{16,0},{1,17},{17,1},{2,18},{18,2},{3,19},{19,3},{4,20},{20... | collective-permute-start | bytes 393224 | tf_op jit(solution)/shard_map/ppermute | solution.py:19
  15.1 3.4 %spread.1.wide_ref = bf16[4,40,32,768]{3,2,1,0:T(8,128)(2,1)S(1)} custom-call(bf16[256,32,128]{2,1,0:T(8,128)(2,1)S(1)} %copy-done.6, bf16[256,32,128]{2,1,0:T(8,128)(2,1)} %collective-permute-done.far_ref, bf16[2,256,128]{2,1,0:T(8,128)(2,1)S(1)} %maximum_bitcast_fusion.own_halo_ref, bf16[2,256,128]{2,1,0:T(8,128)(2,1)S(1)} %collective-permute-done.3.far_halo_ref), custom_call_target="tpu_custom_call" | custom-call | flops 1 | bytes 1 | tf_op jit(solution)/shard_map/spread/pallas_call | solution.py:101
  23.0 2.8 %collective-permute-start.7 = (bf16[32,32,256]{2,1,0:T(8,128)(2,1)S(1)}, bf16[32,32,256]{2,1,0:T(8,128)(2,1)S(1)}, u32[]{:S(2)}, u32[]{:S(2)}) collective-permute-start(bf16[32,32,256]{2,1,0:T(8,128)(2,1)S(1)} %conv_first.7), channel_id=1, source_target_pairs={{0,96},{32,0},{64,32},{96,64},{1,97},{33,1},{65,33},{97,65},{2,98}... | collective-permute-start | bytes 1572872 | tf_op jit(solution)/shard_map/ppermute | solution.py:19
  27.5 4.4 %collective-permute-start.8 = (bf16[1,32,256]{2,1,0:T(8,128)(2,1)S(1)}, bf16[1,32,256]{2,1,0:T(8,128)(2,1)S(1)}, u32[]{:S(2)}, u32[]{:S(2)}) collective-permute-start(bf16[1,32,256]{2,1,0:T(8,128)(2,1)S(1)} %get-tuple-element.42), channel_id=1, source_target_pairs={{0,16},{16,32},{32,48},{48,64},{64,80},{80,96},{96,112},{1,17},{17... | collective-permute-start | bytes 49160 | tf_op jit(solution)/shard_map/ppermute | solution.py:28
  31.9 1.9 %collective-permute-start.9 = (bf16[1,32,256]{2,1,0:T(8,128)(2,1)S(1)}, bf16[1,32,256]{2,1,0:T(8,128)(2,1)S(1)}, u32[]{:S(2)}, u32[]{:S(2)}) collective-permute-start(bf16[1,32,256]{2,1,0:T(8,128)(2,1)S(1)} %get-tuple-element.41), channel_id=1, source_target_pairs={{16,0},{32,16},{48,32},{64,48},{80,64},{96,80},{112,96},{17,1},{33... | collective-permute-start | bytes 49160 | tf_op jit(solution)/shard_map/ppermute | solution.py:28
  33.8 14.8 %collective-permute-done.8.left_ref = bf16[1,32,256]{2,1,0:T(8,128)(2,1)S(1)} collective-permute-done((bf16[1,32,256]{2,1,0:T(8,128)(2,1)S(1)}, bf16[1,32,256]{2,1,0:T(8,128)(2,1)S(1)}, u32[]{:S(2)}, u32[]{:S(2)}) %collective-permute-start.8) | collective-permute-done | bytes 16416 | tf_op jit(solution)/shard_map/ppermute | solution.py:28
  48.6 3.1 %collective-permute-start.10 = (bf16[34,256]{1,0:T(8,128)(2,1)S(1)}, bf16[34,256]{1,0:T(8,128)(2,1)S(1)}, u32[]{:S(2)}, u32[]{:S(2)}) collective-permute-start(bf16[34,256]{1,0:T(8,128)(2,1)S(1)} %pad_maximum_fusion.9), channel_id=1, source_target_pairs={{0,1},{1,2},{2,3},{3,4},{4,5},{5,6},{6,7},{7,8},{8,9},{9,10},{10,1... | collective-permute-start | bytes 52232 | tf_op jit(solution)/shard_map/ppermute | solution.py:329
  59.3 2.8 %grad_first.4.refs_0_ = f32[768,768]{1,0:T(8,128)S(1)} custom-call(s32[1]{0:T(128)} %bitcast.chip_ref, bf16[4,40,32,768]{3,2,1,0:T(8,128)(2,1)S(1)} %spread.1.wide_ref, bf16[32,32,256]{2,1,0:T(8,128)(2,1)} %get-tuple-element.31.delta_ref), custom_call_target="tpu_custom_call" | custom-call | flops 1 | bytes 1 | tf_op jit(solution)/shard_map/grad_first/pallas_call | solution.py:171
  62.1 5.8 %collective-permute-start.14 = (bf16[1,32,256]{2,1,0:T(8,128)(2,1)S(1)}, bf16[1,32,256]{2,1,0:T(8,128)(2,1)S(1)}, u32[]{:S(2)}, u32[]{:S(2)}) collective-permute-start(bf16[1,32,256]{2,1,0:T(8,128)(2,1)S(1)} %get-tuple-element.38), channel_id=1, source_target_pairs={{0,16},{16,32},{32,48},{48,64},{64,80},{80,96},{96,112},{1,17},{17... | collective-permute-start | bytes 49160 | tf_op jit(solution)/shard_map/ppermute | solution.py:28
  68.1 2.7 %collective-permute-start.12 = (bf16[32,32,256]{2,1,0:T(8,128)(2,1)}, bf16[32,32,256]{2,1,0:T(8,128)(2,1)}, u32[]{:S(2)}, u32[]{:S(2)}) collective-permute-start(bf16[32,32,256]{2,1,0:T(8,128)(2,1)} %get-tuple-element.31.delta_ref), channel_id=1, source_target_pairs={{0,96},{32,0},{64,32},{96,64},{1,97},{33,1},{65,33},{97,65},{2,98}... | collective-permute-start | bytes 1572872 | tf_op jit(solution)/shard_map/ppermute | solution.py:19
  72.7 9.7 %collective-permute-done.15.right_ref = bf16[1,32,256]{2,1,0:T(8,128)(2,1)S(1)} collective-permute-done((bf16[1,32,256]{2,1,0:T(8,128)(2,1)S(1)}, bf16[1,32,256]{2,1,0:T(8,128)(2,1)S(1)}, u32[]{:S(2)}, u32[]{:S(2)}) %collective-permute-start.15) | collective-permute-done | bytes 16416 | tf_op jit(solution)/shard_map/ppermute | solution.py:28
  82.4 4.8 %collective-permute-start.16 = (bf16[34,256]{1,0:T(8,128)(2,1)S(1)}, bf16[34,256]{1,0:T(8,128)(2,1)S(1)}, u32[]{:S(2)}, u32[]{:S(2)}) collective-permute-start(bf16[34,256]{1,0:T(8,128)(2,1)S(1)} %pad_maximum_fusion.11), channel_id=1, source_target_pairs={{0,1},{1,2},{2,3},{3,4},{4,5},{5,6},{6,7},{7,8},{8,9},{9,10},{10,1... | collective-permute-start | bytes 52232 | tf_op jit(solution)/shard_map/ppermute | solution.py:329
  88.5 2.2 %collective-permute-start.18 = (bf16[32,32,256]{2,1,0:T(8,128)(2,1)}, bf16[32,32,256]{2,1,0:T(8,128)(2,1)}, u32[]{:S(2)}, u32[]{:S(2)}) collective-permute-start(bf16[32,32,256]{2,1,0:T(8,128)(2,1)} %get-tuple-element.31.delta_ref), channel_id=1, source_target_pairs={{0,64},{32,96},{64,0},{96,32},{1,65},{33,97},{65,1},{97,33},{2,66}... | collective-permute-start | bytes 1572872 | tf_op jit(solution)/shard_map/ppermute | solution.py:19
  92.4 3.2 %copy-done.1 = bf16[4,40,32,768]{3,2,1,0:T(8,128)(2,1)S(1)} copy-done((bf16[4,40,32,768]{3,2,1,0:T(8,128)(2,1)S(1)}, bf16[4,40,32,768]{3,2,1,0:T(8,128)(2,1)}, u32[]{:S(2)}) %copy-start.1) | copy-done | bytes 7864344
  95.7 2.8 %grad_first.5.refs_0_ = f32[768,768]{1,0:T(8,128)S(1)} custom-call(s32[1]{0:T(128)} %bitcast.15.chip_ref, bf16[4,40,32,768]{3,2,1,0:T(8,128)(2,1)S(1)} %copy-done.1, bf16[32,32,256]{2,1,0:T(8,128)(2,1)} %collective-permute-done.13.delta_ref, f32[768,768]{1,0:T(8,128)S(1)} %grad_first.4.refs_0_), custom_call_target="tpu_custom_call" | custom-call | flops 1 | bytes 1 | tf_op jit(solution)/shard_map/grad_first/pallas_call | solution.py:171
  98.5 2.9 %grad_first.6.refs_0_ = f32[768,768]{1,0:T(8,128)S(1)} custom-call(s32[1]{0:T(128)} %bitcast.14.chip_ref, bf16[4,40,32,768]{3,2,1,0:T(8,128)(2,1)S(1)} %copy-done.1, bf16[32,32,256]{2,1,0:T(8,128)(2,1)} %collective-permute-done.12.delta_ref, f32[768,768]{1,0:T(8,128)S(1)} %grad_first.5.refs_0_), custom_call_target="tpu_custom_call" | custom-call | flops 1 | bytes 1 | tf_op jit(solution)/shard_map/grad_first/pallas_call | solution.py:171
  101.4 4.1 %second.1 = (bf16[32,32,256]{2,1,0:T(8,128)(2,1)}, f32[4,288,256]{2,1,0:T(8,128)S(1)}, bf16[4,288,256]{2,1,0:T(8,128)(2,1)}) custom-call(bf16[32,32,256]{2,1,0:T(8,128)(2,1)S(1)} %get-tuple-element.21.hid_ref, bf16[1,32,256]{2,1,0:T(8,128)(2,1)S(1)} %collective-permute-done.14.left_ref, bf16[1,32,256]{2,1,0:T(8,128)(2,1)S(1)} %collective-permute-done.15.right_ref, ...), custom_call_target="tpu_custom_call" | custom-call | flops 1 | bytes 1 | tf_op jit(solution)/shard_map/second/pallas_call | solution.py:278
  106.5 3.2 %copy-done.2 = bf16[4,40,32,768]{3,2,1,0:T(8,128)(2,1)S(1)} copy-done((bf16[4,40,32,768]{3,2,1,0:T(8,128)(2,1)S(1)}, bf16[4,40,32,768]{3,2,1,0:T(8,128)(2,1)}, u32[]{:S(2)}) %copy-start.2) | copy-done | bytes 7864344
  109.8 2.9 %grad_first.7 = (f32[384,768]{1,0:T(8,128)S(1)}, bf16[384,768]{1,0:T(8,128)(2,1)S(1)}) custom-call(s32[1]{0:T(128)} %bitcast.23.chip_ref, bf16[4,40,32,768]{3,2,1,0:T(8,128)(2,1)S(1)} %copy-done.2, bf16[32,32,256]{2,1,0:T(8,128)(2,1)} %collective-permute-done.18.delta_ref, f32[768,768]{1,0:T(8,128)S(1)} %grad_first.6.refs_0_), custom_call_target="tpu_custom_call" | custom-call | flops 1 | bytes 1 | tf_op jit(solution)/shard_map/grad_first/pallas_call | solution.py:171
  113.6 2.5 %collective-permute-start.22 = (bf16[288,256]{1,0:T(8,128)(2,1)S(1)}, bf16[288,256]{1,0:T(8,128)(2,1)S(1)}, u32[]{:S(2)}, u32[]{:S(2)}) collective-permute-start(bf16[288,256]{1,0:T(8,128)(2,1)S(1)} %get-tuple-element.29), channel_id=1, source_target_pairs={{0,96},{32,0},{64,32},{96,64},{1,97},{33,1},{65,33},{97,65},{2,98}... | collective-permute-start | bytes 442376 | tf_op jit(solution)/shard_map/ppermute | solution.py:19
  116.4 3.6 %collective-permute-done.21 = bf16[288,256]{1,0:T(8,128)(2,1)S(1)} collective-permute-done((bf16[288,256]{1,0:T(8,128)(2,1)S(1)}, bf16[288,256]{1,0:T(8,128)(2,1)S(1)}, u32[]{:S(2)}, u32[]{:S(2)}) %collective-permute-start.21) | collective-permute-done | bytes 147488 | tf_op jit(solution)/shard_map/ppermute | solution.py:19
  120.0 2.0 %collective-permute-done.22 = bf16[288,256]{1,0:T(8,128)(2,1)S(1)} collective-permute-done((bf16[288,256]{1,0:T(8,128)(2,1)S(1)}, bf16[288,256]{1,0:T(8,128)(2,1)S(1)}, u32[]{:S(2)}, u32[]{:S(2)}) %collective-permute-start.22) | collective-permute-done | bytes 147488 | tf_op jit(solution)/shard_map/ppermute | solution.py:19
  123.7 9.0 %all-to-all-start = ((bf16[16,90,256]{2,1,0:T(8,128)(2,1)}), bf16[16,90,256]{2,1,0:T(8,128)(2,1)S(1)}, u32[]{:S(2)}, u32[]{:S(2)}) async-start(bf16[16,90,256]{2,1,0:T(8,128)(2,1)} %join.1), calls=%async_computation | async-start | bytes 1572864 | tf_op jit(solution)/shard_map/all_to_all | solution.py:479
  133.5 11.8 %all-to-all-done = bf16[16,90,256]{2,1,0:T(8,128)(2,1)S(1)} async-done(((bf16[16,90,256]{2,1,0:T(8,128)(2,1)}), bf16[16,90,256]{2,1,0:T(8,128)(2,1)S(1)}, u32[]{:S(2)}, u32[]{:S(2)}) %all-to-all-start) | async-done | bytes 737312 | tf_op jit(solution)/shard_map/all_to_all | solution.py:479
  145.4 2.7 %collective-permute-start.25 = (bf16[90,256]{1,0:T(8,128)(2,1)S(1)}, bf16[90,256]{1,0:T(8,128)(2,1)S(1)}, u32[]{:S(2)}, u32[]{:S(2)}) collective-permute-start(bf16[90,256]{1,0:T(8,128)(2,1)S(1)} %reduce_sum.12), channel_id=1, source_target_pairs={{0,12},{4,0},{8,4},{12,8},{1,13},{5,1},{9,5},{13,9},{2,14},{6,2},{... | collective-permute-start | bytes 138248 | tf_op jit(solution)/shard_map/ppermute | solution.py:19
  159.3 3.2 %collective-permute-done.29 = bf16[360,256]{1,0:T(8,128)(2,1)S(1)} collective-permute-done((bf16[360,256]{1,0:T(8,128)(2,1)S(1)}, bf16[360,256]{1,0:T(8,128)(2,1)S(1)}, u32[]{:S(2)}, u32[]{:S(2)}) %collective-permute-start.29) | collective-permute-done | bytes 184352 | tf_op jit(solution)/shard_map/ppermute | solution.py:19
  162.5 4.3 %collective-permute-done.27 = bf16[360,256]{1,0:T(8,128)(2,1)S(1)} collective-permute-done((bf16[360,256]{1,0:T(8,128)(2,1)S(1)}, bf16[360,256]{1,0:T(8,128)(2,1)S(1)}, u32[]{:S(2)}, u32[]{:S(2)}) %collective-permute-start.27) | collective-permute-done | bytes 184352 | tf_op jit(solution)/shard_map/ppermute | solution.py:19
  168.2 2.4 %collective-permute-start.31 = (bf16[4,72,256]{2,1,0:T(8,128)(2,1)S(1)}, bf16[4,72,256]{2,1,0:T(8,128)(2,1)S(1)}, u32[]{:S(2)}, u32[]{:S(2)}) collective-permute-start(bf16[4,72,256]{2,1,0:T(8,128)(2,1)S(1)} %get-tuple-element.48), channel_id=1, source_target_pairs={{0,96},{32,0},{64,32},{96,64},{1,97},{33,1},{65,33},{97,65},{2,98}... | collective-permute-start | bytes 442376 | tf_op jit(solution)/shard_map/ppermute | solution.py:19
  173.0 3.4 %collective-permute-done.32 = bf16[4,72,256]{2,1,0:T(8,128)(2,1)S(1)} collective-permute-done((bf16[4,72,256]{2,1,0:T(8,128)(2,1)S(1)}, bf16[4,72,256]{2,1,0:T(8,128)(2,1)S(1)}, u32[]{:S(2)}, u32[]{:S(2)}) %collective-permute-start.32) | collective-permute-done | bytes 147488 | tf_op jit(solution)/shard_map/ppermute | solution.py:19
  176.5 3.8 %collective-permute-start.33 = (bf16[4,4,72,256]{3,2,1,0:T(8,128)(2,1)S(1)}, bf16[4,4,72,256]{3,2,1,0:T(8,128)(2,1)S(1)}, u32[]{:S(2)}, u32[]{:S(2)}) collective-permute-start(bf16[4,4,72,256]{3,2,1,0:T(8,128)(2,1)S(1)} %pad_maximum_fusion.1.near_ref), channel_id=1, source_target_pairs={{0,16},{16,0},{1,17},{17,1},{2,18},{18,2},{3,19},{19,3},{4,20},{20... | collective-permute-start | bytes 1769480 | tf_op jit(solution)/shard_map/ppermute | solution.py:19
  (120 shorter events, 39.7 us)
Async XLA Ops:
  0.6 14.4 %collective-permute-start = (bf16[256,32,128]{2,1,0:T(8,128)(2,1)}, bf16[256,32,128]{2,1,0:T(8,128)(2,1)}, u32[]{:S(2)}, u32[]{:S(2)}) collective-permute-start(bf16[256,32,128]{2,1,0:T(8,128)(2,1)} %own_ref.1), channel_id=1, source_target_pairs={{0,16},{16,0},{1,17},{17,1},{2,18},{18,2},{3,19},{19,3},{4,20},{20... | collective-permute-start | bytes 6291464 | tf_op jit(solution)/shard_map/ppermute | solution.py:19
  2.1 11.8 %collective-permute-start.4 = (bf16[3,3,128,256]{3,2,1,0:T(8,128)(2,1)}, bf16[3,3,128,256]{3,2,1,0:T(8,128)(2,1)S(1)}, u32[]{:S(2)}, u32[]{:S(2)}) collective-permute-start(bf16[3,3,128,256]{3,2,1,0:T(8,128)(2,1)} %param.6), channel_id=1, source_target_pairs={{0,16},{16,0},{1,17},{17,1},{2,18},{18,2},{3,19},{19,3},{4,20},{20... | collective-permute-start | bytes 1769480 | tf_op jit(solution)/shard_map/ppermute | solution.py:19
  6.9 5.0 %collective-permute-start.2 = (bf16[256,1,128]{2,0,1:T(8,128)(2,1)S(1)}, bf16[256,1,128]{2,0,1:T(8,128)(2,1)S(1)}, u32[]{:S(2)}, u32[]{:S(2)}) collective-permute-start(bf16[256,1,128]{2,0,1:T(8,128)(2,1)S(1)} %copy.28), channel_id=1, source_target_pairs={{1,0},{2,1},{3,2},{4,3},{5,4},{6,5},{7,6},{8,7},{9,8},{10,9},{11,1... | collective-permute-start | bytes 196616 | tf_op jit(solution)/shard_map/ppermute | solution.py:28
  23.0 34.7 %collective-permute-start.7 = (bf16[32,32,256]{2,1,0:T(8,128)(2,1)S(1)}, bf16[32,32,256]{2,1,0:T(8,128)(2,1)S(1)}, u32[]{:S(2)}, u32[]{:S(2)}) collective-permute-start(bf16[32,32,256]{2,1,0:T(8,128)(2,1)S(1)} %conv_first.7), channel_id=1, source_target_pairs={{0,96},{32,0},{64,32},{96,64},{1,97},{33,1},{65,33},{97,65},{2,98}... | collective-permute-start | bytes 1572872 | tf_op jit(solution)/shard_map/ppermute | solution.py:19
  25.8 31.9 %collective-permute-start.6 = (bf16[32,32,256]{2,1,0:T(8,128)(2,1)S(1)}, bf16[32,32,256]{2,1,0:T(8,128)(2,1)S(1)}, u32[]{:S(2)}, u32[]{:S(2)}) collective-permute-start(bf16[32,32,256]{2,1,0:T(8,128)(2,1)S(1)} %conv_first.6), channel_id=1, source_target_pairs={{0,32},{32,64},{64,96},{96,0},{1,33},{33,65},{65,97},{97,1},{2,34}... | collective-permute-start | bytes 1572872 | tf_op jit(solution)/shard_map/ppermute | solution.py:19
  25.8 31.9 %collective-permute-start.5 = (bf16[32,32,256]{2,1,0:T(8,128)(2,1)S(1)}, bf16[32,32,256]{2,1,0:T(8,128)(2,1)S(1)}, u32[]{:S(2)}, u32[]{:S(2)}) collective-permute-start(bf16[32,32,256]{2,1,0:T(8,128)(2,1)S(1)} %conv_first.5), channel_id=1, source_target_pairs={{0,64},{32,96},{64,0},{96,32},{1,65},{33,97},{65,1},{97,33},{2,66}... | collective-permute-start | bytes 1572872 | tf_op jit(solution)/shard_map/ppermute | solution.py:19
  27.5 21.1 %collective-permute-start.8 = (bf16[1,32,256]{2,1,0:T(8,128)(2,1)S(1)}, bf16[1,32,256]{2,1,0:T(8,128)(2,1)S(1)}, u32[]{:S(2)}, u32[]{:S(2)}) collective-permute-start(bf16[1,32,256]{2,1,0:T(8,128)(2,1)S(1)} %get-tuple-element.42), channel_id=1, source_target_pairs={{0,16},{16,32},{32,48},{48,64},{64,80},{80,96},{96,112},{1,17},{17... | collective-permute-start | bytes 49160 | tf_op jit(solution)/shard_map/ppermute | solution.py:28
  31.9 16.7 %collective-permute-start.9 = (bf16[1,32,256]{2,1,0:T(8,128)(2,1)S(1)}, bf16[1,32,256]{2,1,0:T(8,128)(2,1)S(1)}, u32[]{:S(2)}, u32[]{:S(2)}) collective-permute-start(bf16[1,32,256]{2,1,0:T(8,128)(2,1)S(1)} %get-tuple-element.41), channel_id=1, source_target_pairs={{16,0},{32,16},{48,32},{64,48},{80,64},{96,80},{112,96},{17,1},{33... | collective-permute-start | bytes 49160 | tf_op jit(solution)/shard_map/ppermute | solution.py:28
  48.6 5.9 %collective-permute-start.10 = (bf16[34,256]{1,0:T(8,128)(2,1)S(1)}, bf16[34,256]{1,0:T(8,128)(2,1)S(1)}, u32[]{:S(2)}, u32[]{:S(2)}) collective-permute-start(bf16[34,256]{1,0:T(8,128)(2,1)S(1)} %pad_maximum_fusion.9), channel_id=1, source_target_pairs={{0,1},{1,2},{2,3},{3,4},{4,5},{5,6},{6,7},{7,8},{8,9},{9,10},{10,1... | collective-permute-start | bytes 52232 | tf_op jit(solution)/shard_map/ppermute | solution.py:329
  62.1 10.6 %collective-permute-start.14 = (bf16[1,32,256]{2,1,0:T(8,128)(2,1)S(1)}, bf16[1,32,256]{2,1,0:T(8,128)(2,1)S(1)}, u32[]{:S(2)}, u32[]{:S(2)}) collective-permute-start(bf16[1,32,256]{2,1,0:T(8,128)(2,1)S(1)} %get-tuple-element.38), channel_id=1, source_target_pairs={{0,16},{16,32},{32,48},{48,64},{64,80},{80,96},{96,112},{1,17},{17... | collective-permute-start | bytes 49160 | tf_op jit(solution)/shard_map/ppermute | solution.py:28
  68.0 24.4 %collective-permute-start.13 = (bf16[32,32,256]{2,1,0:T(8,128)(2,1)}, bf16[32,32,256]{2,1,0:T(8,128)(2,1)}, u32[]{:S(2)}, u32[]{:S(2)}) collective-permute-start(bf16[32,32,256]{2,1,0:T(8,128)(2,1)} %get-tuple-element.31.delta_ref), channel_id=1, source_target_pairs={{0,32},{32,64},{64,96},{96,0},{1,33},{33,65},{65,97},{97,1},{2,34}... | collective-permute-start | bytes 1572872 | tf_op jit(solution)/shard_map/ppermute | solution.py:19
  68.1 30.4 %collective-permute-start.12 = (bf16[32,32,256]{2,1,0:T(8,128)(2,1)}, bf16[32,32,256]{2,1,0:T(8,128)(2,1)}, u32[]{:S(2)}, u32[]{:S(2)}) collective-permute-start(bf16[32,32,256]{2,1,0:T(8,128)(2,1)} %get-tuple-element.31.delta_ref), channel_id=1, source_target_pairs={{0,96},{32,0},{64,32},{96,64},{1,97},{33,1},{65,33},{97,65},{2,98}... | collective-permute-start | bytes 1572872 | tf_op jit(solution)/shard_map/ppermute | solution.py:19
  70.7 11.7 %collective-permute-start.15 = (bf16[1,32,256]{2,1,0:T(8,128)(2,1)S(1)}, bf16[1,32,256]{2,1,0:T(8,128)(2,1)S(1)}, u32[]{:S(2)}, u32[]{:S(2)}) collective-permute-start(bf16[1,32,256]{2,1,0:T(8,128)(2,1)S(1)} %get-tuple-element.37), channel_id=1, source_target_pairs={{16,0},{32,16},{48,32},{64,48},{80,64},{96,80},{112,96},{17,1},{33... | collective-permute-start | bytes 49160 | tf_op jit(solution)/shard_map/ppermute | solution.py:28
  82.4 8.3 %collective-permute-start.16 = (bf16[34,256]{1,0:T(8,128)(2,1)S(1)}, bf16[34,256]{1,0:T(8,128)(2,1)S(1)}, u32[]{:S(2)}, u32[]{:S(2)}) collective-permute-start(bf16[34,256]{1,0:T(8,128)(2,1)S(1)} %pad_maximum_fusion.11), channel_id=1, source_target_pairs={{0,1},{1,2},{2,3},{3,4},{4,5},{5,6},{6,7},{7,8},{8,9},{9,10},{10,1... | collective-permute-start | bytes 52232 | tf_op jit(solution)/shard_map/ppermute | solution.py:329
  87.2 5.2 %collective-permute-start.17 = (bf16[34,256]{1,0:T(8,128)(2,1)S(1)}, bf16[34,256]{1,0:T(8,128)(2,1)S(1)}, u32[]{:S(2)}, u32[]{:S(2)}) collective-permute-start(bf16[34,256]{1,0:T(8,128)(2,1)S(1)} %pad_maximum_fusion.12), channel_id=1, source_target_pairs={{1,0},{2,1},{3,2},{4,3},{5,4},{6,5},{7,6},{8,7},{9,8},{10,9},{11,1... | collective-permute-start | bytes 52232 | tf_op jit(solution)/shard_map/ppermute | solution.py:329
  88.5 18.0 %collective-permute-start.18 = (bf16[32,32,256]{2,1,0:T(8,128)(2,1)}, bf16[32,32,256]{2,1,0:T(8,128)(2,1)}, u32[]{:S(2)}, u32[]{:S(2)}) collective-permute-start(bf16[32,32,256]{2,1,0:T(8,128)(2,1)} %get-tuple-element.31.delta_ref), channel_id=1, source_target_pairs={{0,64},{32,96},{64,0},{96,32},{1,65},{33,97},{65,1},{97,33},{2,66}... | collective-permute-start | bytes 1572872 | tf_op jit(solution)/shard_map/ppermute | solution.py:19
  106.5 6.7 %collective-permute-start.20 = (bf16[4,288,256]{2,1,0:T(8,128)(2,1)}, bf16[4,288,256]{2,1,0:T(8,128)(2,1)S(1)}, u32[]{:S(2)}, u32[]{:S(2)}) collective-permute-start(bf16[4,288,256]{2,1,0:T(8,128)(2,1)} %get-tuple-element.26), channel_id=1, source_target_pairs={{0,16},{16,0},{1,17},{17,1},{2,18},{18,2},{3,19},{19,3},{4,20},{20... | collective-permute-start | bytes 1769480 | tf_op jit(solution)/shard_map/ppermute | solution.py:19
  112.6 10.0 %collective-permute-start.19 = (bf16[384,768]{1,0:T(8,128)(2,1)S(1)}, bf16[384,768]{1,0:T(8,128)(2,1)S(1)}, u32[]{:S(2)}, u32[]{:S(2)}) collective-permute-start(bf16[384,768]{1,0:T(8,128)(2,1)S(1)} %get-tuple-element.24), channel_id=1, source_target_pairs={{0,16},{16,0},{1,17},{17,1},{2,18},{18,2},{3,19},{19,3},{4,20},{20... | collective-permute-start | bytes 1769480 | tf_op jit(solution)/shard_map/ppermute | solution.py:19
  113.3 6.7 %collective-permute-start.21 = (bf16[288,256]{1,0:T(8,128)(2,1)S(1)}, bf16[288,256]{1,0:T(8,128)(2,1)S(1)}, u32[]{:S(2)}, u32[]{:S(2)}) collective-permute-start(bf16[288,256]{1,0:T(8,128)(2,1)S(1)} %get-tuple-element.28), channel_id=1, source_target_pairs={{0,32},{32,64},{64,96},{96,0},{1,33},{33,65},{65,97},{97,1},{2,34}... | collective-permute-start | bytes 442376 | tf_op jit(solution)/shard_map/ppermute | solution.py:19
  113.6 8.4 %collective-permute-start.22 = (bf16[288,256]{1,0:T(8,128)(2,1)S(1)}, bf16[288,256]{1,0:T(8,128)(2,1)S(1)}, u32[]{:S(2)}, u32[]{:S(2)}) collective-permute-start(bf16[288,256]{1,0:T(8,128)(2,1)S(1)} %get-tuple-element.29), channel_id=1, source_target_pairs={{0,96},{32,0},{64,32},{96,64},{1,97},{33,1},{65,33},{97,65},{2,98}... | collective-permute-start | bytes 442376 | tf_op jit(solution)/shard_map/ppermute | solution.py:19
  116.1 6.4 %collective-permute-start.23 = (bf16[288,256]{1,0:T(8,128)(2,1)S(1)}, bf16[288,256]{1,0:T(8,128)(2,1)S(1)}, u32[]{:S(2)}, u32[]{:S(2)}) collective-permute-start(bf16[288,256]{1,0:T(8,128)(2,1)S(1)} %get-tuple-element.30), channel_id=1, source_target_pairs={{0,64},{32,96},{64,0},{96,32},{1,65},{33,97},{65,1},{97,33},{2,66}... | collective-permute-start | bytes 442376 | tf_op jit(solution)/shard_map/ppermute | solution.py:19
  123.7 21.6 %all-to-all-start = ((bf16[16,90,256]{2,1,0:T(8,128)(2,1)}), bf16[16,90,256]{2,1,0:T(8,128)(2,1)S(1)}, u32[]{:S(2)}, u32[]{:S(2)}) async-start(bf16[16,90,256]{2,1,0:T(8,128)(2,1)} %join.1), calls=%async_computation | async-start | bytes 1572864 | tf_op jit(solution)/shard_map/all_to_all | solution.py:479
  145.4 11.0 %collective-permute-start.24 = (bf16[90,256]{1,0:T(8,128)(2,1)S(1)}, bf16[90,256]{1,0:T(8,128)(2,1)S(1)}, u32[]{:S(2)}, u32[]{:S(2)}) collective-permute-start(bf16[90,256]{1,0:T(8,128)(2,1)S(1)} %reduce_sum.12), channel_id=1, source_target_pairs={{0,4},{4,8},{8,12},{12,0},{1,5},{5,9},{9,13},{13,1},{2,6},{6,10},{... | collective-permute-start | bytes 138248 | tf_op jit(solution)/shard_map/ppermute | solution.py:19
  145.4 10.9 %collective-permute-start.25 = (bf16[90,256]{1,0:T(8,128)(2,1)S(1)}, bf16[90,256]{1,0:T(8,128)(2,1)S(1)}, u32[]{:S(2)}, u32[]{:S(2)}) collective-permute-start(bf16[90,256]{1,0:T(8,128)(2,1)S(1)} %reduce_sum.12), channel_id=1, source_target_pairs={{0,12},{4,0},{8,4},{12,8},{1,13},{5,1},{9,5},{13,9},{2,14},{6,2},{... | collective-permute-start | bytes 138248 | tf_op jit(solution)/shard_map/ppermute | solution.py:19
  148.1 8.2 %collective-permute-start.26 = (bf16[90,256]{1,0:T(8,128)(2,1)S(1)}, bf16[90,256]{1,0:T(8,128)(2,1)S(1)}, u32[]{:S(2)}, u32[]{:S(2)}) collective-permute-start(bf16[90,256]{1,0:T(8,128)(2,1)S(1)} %reduce_sum.12), channel_id=1, source_target_pairs={{0,8},{4,12},{8,0},{12,4},{1,9},{5,13},{9,1},{13,5},{2,10},{6,14},... | collective-permute-start | bytes 138248 | tf_op jit(solution)/shard_map/ppermute | solution.py:19
  156.6 6.0 %collective-permute-start.29 = (bf16[360,256]{1,0:T(8,128)(2,1)S(1)}, bf16[360,256]{1,0:T(8,128)(2,1)S(1)}, u32[]{:S(2)}, u32[]{:S(2)}) collective-permute-start(bf16[360,256]{1,0:T(8,128)(2,1)S(1)} %pad_maximum_fusion.4), channel_id=1, source_target_pairs={{0,2},{1,3},{2,0},{3,1},{4,6},{5,7},{6,4},{7,5},{8,10},{9,11},{10,... | collective-permute-start | bytes 552968 | tf_op jit(solution)/shard_map/ppermute | solution.py:19
  157.8 4.7 %collective-permute-start.28 = (bf16[360,256]{1,0:T(8,128)(2,1)S(1)}, bf16[360,256]{1,0:T(8,128)(2,1)S(1)}, u32[]{:S(2)}, u32[]{:S(2)}) collective-permute-start(bf16[360,256]{1,0:T(8,128)(2,1)S(1)} %pad_maximum_fusion.4), channel_id=1, source_target_pairs={{0,3},{1,0},{2,1},{3,2},{4,7},{5,4},{6,5},{7,6},{8,11},{9,8},{10,9... | collective-permute-start | bytes 552968 | tf_op jit(solution)/shard_map/ppermute | solution.py:19
  159.3 7.6 %collective-permute-start.27 = (bf16[360,256]{1,0:T(8,128)(2,1)S(1)}, bf16[360,256]{1,0:T(8,128)(2,1)S(1)}, u32[]{:S(2)}, u32[]{:S(2)}) collective-permute-start(bf16[360,256]{1,0:T(8,128)(2,1)S(1)} %pad_maximum_fusion.4), channel_id=1, source_target_pairs={{0,1},{1,2},{2,3},{3,0},{4,5},{5,6},{6,7},{7,4},{8,9},{9,10},{10,1... | collective-permute-start | bytes 552968 | tf_op jit(solution)/shard_map/ppermute | solution.py:19
  166.9 6.1 %collective-permute-start.30 = (bf16[4,72,256]{2,1,0:T(8,128)(2,1)S(1)}, bf16[4,72,256]{2,1,0:T(8,128)(2,1)S(1)}, u32[]{:S(2)}, u32[]{:S(2)}) collective-permute-start(bf16[4,72,256]{2,1,0:T(8,128)(2,1)S(1)} %get-tuple-element.48), channel_id=1, source_target_pairs={{0,32},{32,64},{64,96},{96,0},{1,33},{33,65},{65,97},{97,1},{2,34}... | collective-permute-start | bytes 442376 | tf_op jit(solution)/shard_map/ppermute | solution.py:19
  168.2 4.9 %collective-permute-start.31 = (bf16[4,72,256]{2,1,0:T(8,128)(2,1)S(1)}, bf16[4,72,256]{2,1,0:T(8,128)(2,1)S(1)}, u32[]{:S(2)}, u32[]{:S(2)}) collective-permute-start(bf16[4,72,256]{2,1,0:T(8,128)(2,1)S(1)} %get-tuple-element.48), channel_id=1, source_target_pairs={{0,96},{32,0},{64,32},{96,64},{1,97},{33,1},{65,33},{97,65},{2,98}... | collective-permute-start | bytes 442376 | tf_op jit(solution)/shard_map/ppermute | solution.py:19
  170.6 5.9 %collective-permute-start.32 = (bf16[4,72,256]{2,1,0:T(8,128)(2,1)S(1)}, bf16[4,72,256]{2,1,0:T(8,128)(2,1)S(1)}, u32[]{:S(2)}, u32[]{:S(2)}) collective-permute-start(bf16[4,72,256]{2,1,0:T(8,128)(2,1)S(1)} %get-tuple-element.48), channel_id=1, source_target_pairs={{0,64},{32,96},{64,0},{96,32},{1,65},{33,97},{65,1},{97,33},{2,66}... | collective-permute-start | bytes 442376 | tf_op jit(solution)/shard_map/ppermute | solution.py:19
  176.5 5.4 %collective-permute-start.33 = (bf16[4,4,72,256]{3,2,1,0:T(8,128)(2,1)S(1)}, bf16[4,4,72,256]{3,2,1,0:T(8,128)(2,1)S(1)}, u32[]{:S(2)}, u32[]{:S(2)}) collective-permute-start(bf16[4,4,72,256]{3,2,1,0:T(8,128)(2,1)S(1)} %pad_maximum_fusion.1.near_ref), channel_id=1, source_target_pairs={{0,16},{16,0},{1,17},{17,1},{2,18},{18,2},{3,19},{19,3},{4,20},{20... | collective-permute-start | bytes 1769480 | tf_op jit(solution)/shard_map/ppermute | solution.py:19
  (13 other events, 96.1 us)

commit v4 on v3

--- a/solution.py
+++ b/solution.py
@@ -11,7 +11,7 @@
 SKY = ("z", "x")
 F32 = jnp.float32
 BF16 = jnp.bfloat16
-QUICK = pl.CostEstimate(flops=1, bytes_accessed=1, transcendentals=0)
+QUICK = pl.CostEstimate(flops=1, bytes_accessed=8 * 2**20, transcendentals=0)
 
 
 def shift(x, axis, step):
@@ -49,7 +49,7 @@
             after = halo_ref[1, pl.ds(at, step), :].astype(F32)[:, None, :]
             ahead = jnp.where(row == 0, before, ahead)
             behind = jnp.where(row == rows - 1, after, behind)
-            to = pl.ds(1 + i * step, step)
+            to = pl.ds(2 + i * step, step)
             for tap, value in enumerate((ahead.astype(BF16), mid, behind.astype(BF16))):
                 lane = (2 * tap + side) * chans
                 out_ref[chip, to, :, lane : lane + chans] = value
@@ -78,22 +78,24 @@
     for chip in range(chips):
         base = (2 * chip + core) * strip
         lax.fori_loop(0, strip // step, lambda i, _: block(i, base, chip), None)
-        edge(jnp.maximum(base - 1, 0), chip, 0)
-        edge(jnp.minimum(base + strip, cols - 1), chip, strip + 1)
-        for slot in range(strip + 2, width):
+        for slot in (0, 1):
+            edge(jnp.maximum(base - 2 + slot, 0), chip, slot)
+            edge(jnp.minimum(base + strip + slot, cols - 1), chip, strip + 2 + slot)
+        for slot in range(strip + 4, width):
             out_ref[chip, slot] = blank
 
     @pl.when(core == 0)
     def _():
         out_ref[0, 0] = blank
+        out_ref[0, 1] = blank
 
     @pl.when(core == 1)
     def _():
-        out_ref[chips - 1, strip + 1] = blank
+        out_ref[chips - 1, strip + 2] = blank
+        out_ref[chips - 1, strip + 3] = blank
 
 
 VMEM_SPEC = pl.BlockSpec(memory_space=pltpu.VMEM)
-SMEM_SPEC = pl.BlockSpec(memory_space=pltpu.SMEM)
 
 
 def spread(own, far, own_halo, far_halo, chips):
@@ -103,43 +105,47 @@
         out_shape=jax.ShapeDtypeStruct((chips, cols // (2 * chips) + 8, rows, 6 * chans), BF16),
         in_specs=[VMEM_SPEC] * 4,
         out_specs=VMEM_SPEC,
-        compiler_params=pltpu.CompilerParams(vmem_limit_bytes=16 * 2**20),
+        compiler_params=pltpu.CompilerParams(vmem_limit_bytes=2 * 2**20),
         cost_estimate=QUICK,
         name="spread",
     )(own, far, own_halo, far_halo)
 
 
-def conv_kernel(chip_ref, wide_ref, kernel_ref, out_ref):
+def chip_at(step):
+    return lax.rem(lax.axis_index("y") + step, lax.axis_size("y"))
+
+
+def conv_kernel(step, wide_ref, kernel_ref, out_ref):
     strip, rows, outs = out_ref.shape
-    chip = chip_ref[0]
+    chip = chip_at(step)
     pieces = [wide_ref[chip, tap : tap + strip] for tap in range(3)]
     lhs = jnp.concatenate(pieces, axis=-1).reshape(strip * rows, -1)
     total = jnp.dot(lhs, kernel_ref[...], preferred_element_type=F32)
     out_ref[...] = total.reshape(strip, rows, outs).astype(out_ref.dtype)
 
 
-def conv_strip(chip, wide, kernel, strip, dtype):
+def conv_strip(step, wide, kernel, strip, dtype):
     rows, depth, outs = wide.shape[2], kernel.shape[0], kernel.shape[1]
     return pl.pallas_call(
-        conv_kernel,
+        functools.partial(conv_kernel, step),
         out_shape=jax.ShapeDtypeStruct((strip, rows, outs), dtype),
-        in_specs=[SMEM_SPEC, VMEM_SPEC, VMEM_SPEC],
-        out_specs=VMEM_SPEC,
-        compiler_params=pltpu.CompilerParams(vmem_limit_bytes=16 * 2**20),
+        in_specs=[VMEM_SPEC, VMEM_SPEC],
+        out_specs=VMEM_SPEC,
+        compiler_params=pltpu.CompilerParams(vmem_limit_bytes=3 * 2**20),
         cost_estimate=QUICK,
         name="conv_first",
-    )(chip.reshape(1), wide, kernel)
-
-
-def grad_kernel(has_old, last, chip_ref, wide_ref, delta_ref, *refs):
+    )(wide, kernel)
+
+
+def grad_kernel(step, has_old, last, wide_ref, delta_ref, *refs):
     old_ref = refs[0] if has_old else None
     outs_refs, pad_ref = refs[1 if has_old else 0 : -1], refs[-1]
     strip, rows, outs = delta_ref.shape
     cols, depth = wide_ref.shape[1], wide_ref.shape[3]
-    pad_ref[0:2] = jnp.zeros((2, rows, outs), BF16)
-    pad_ref[2 : 2 + strip] = delta_ref[...]
-    pad_ref[2 + strip :] = jnp.zeros((cols - strip, rows, outs), BF16)
-    lhs = wide_ref[chip_ref[0]].reshape(cols * rows, depth)
+    pad_ref[0:3] = jnp.zeros((3, rows, outs), BF16)
+    pad_ref[3 : 3 + strip] = delta_ref[...]
+    pad_ref[3 + strip :] = jnp.zeros((cols - strip - 1, rows, outs), BF16)
+    lhs = wide_ref[chip_at(step)].reshape(cols * rows, depth)
     rhs = jnp.concatenate(
         [pad_ref[2 - tap : 2 - tap + cols].reshape(cols * rows, outs) for tap in range(3)], axis=-1
     )
@@ -158,7 +164,7 @@
             ].astype(BF16)
 
 
-def grad_strip(chip, wide, delta, old, last):
+def grad_strip(step, wide, delta, old, last):
     strip, rows, outs = delta.shape
     depth, cols = wide.shape[3], wide.shape[1]
     shape = (depth, 3 * outs)
@@ -167,22 +173,22 @@
         out_shape = (jax.ShapeDtypeStruct(half, F32), jax.ShapeDtypeStruct(half, BF16))
     else:
         out_shape = (jax.ShapeDtypeStruct(shape, F32),)
-    args = [chip.reshape(1), wide, delta] + ([old] if old is not None else [])
+    args = [wide, delta] + ([old] if old is not None else [])
     out = pl.pallas_call(
-        functools.partial(grad_kernel, old is not None, last),
+        functools.partial(grad_kernel, step, old is not None, last),
         out_shape=out_shape,
-        in_specs=[SMEM_SPEC] + [VMEM_SPEC] * (len(args) - 1),
+        in_specs=[VMEM_SPEC] * len(args),
         out_specs=tuple([VMEM_SPEC] * len(out_shape)),
         scratch_shapes=[pltpu.VMEM((cols + 2, rows, outs), BF16)],
-        compiler_params=pltpu.CompilerParams(vmem_limit_bytes=20 * 2**20),
+        compiler_params=pltpu.CompilerParams(vmem_limit_bytes=5 * 2**20),
         cost_estimate=QUICK,
         name="grad_first",
     )(*args)
     return out if last else out[0]
 
 
-def spread_tile(ref, left_ref, right_ref, edge_ref, wide_ref):
-    cols, rows, chans = ref.shape
+def spread_tile(columns, edge_ref, wide_ref):
+    rows, chans = wide_ref.shape[1], wide_ref.shape[2] // 3
     place = lax.broadcasted_iota(jnp.int32, (rows, chans), 0)
 
     def put(mid, j):
@@ -195,15 +201,14 @@
         wide_ref[j, :, chans : 2 * chans] = mid
         wide_ref[j, :, 2 * chans :] = behind.astype(BF16)
 
-    put(left_ref[0], 0)
-    for j in range(cols):
-        put(ref[j], j + 1)
-    put(right_ref[0], cols + 1)
+    for j, (ref, at) in enumerate(columns):
+        put(ref[at], j)
 
 
 def back_kernel(cot_ref, left_ref, right_ref, edge_ref, kernel_ref, out_ref, wide_ref):
     cols, rows, chans = cot_ref.shape
-    spread_tile(cot_ref, left_ref, right_ref, edge_ref, wide_ref)
+    columns = [(left_ref, 0)] + [(cot_ref, j) for j in range(cols)] + [(right_ref, 0)]
+    spread_tile(columns, edge_ref, wide_ref)
     total = None
     for tap_col in range(3):
         lhs = wide_ref[tap_col : tap_col + cols].reshape(cols * rows, 3 * chans)
@@ -226,21 +231,21 @@
         in_specs=[VMEM_SPEC] * 5,
         out_specs=VMEM_SPEC,
         scratch_shapes=[pltpu.VMEM((cols + 2, rows, 3 * chans), BF16)],
-        compiler_params=pltpu.CompilerParams(vmem_limit_bytes=20 * 2**20),
+        compiler_params=pltpu.CompilerParams(vmem_limit_bytes=4 * 2**20),
         cost_estimate=QUICK,
         name="back",
     )(tile, left, right, edges, kernel)
 
 
 def second_kernel(
-    chips, hid_ref, left_ref, right_ref, edge_ref, kernel_ref, cot_ref,
+    chips, hid_ref, edge_ref, kernel_ref, cot_ref,
     out_ref, near_ref, far_ref, wide_ref, pad_ref, sum_ref,
 ):
-    cols, rows, chans = hid_ref.shape
-    outs = cot_ref.shape[2]
+    chans = hid_ref.shape[2]
+    cols, rows, outs = cot_ref.shape
     width = wide_ref.shape[0]
     core = lax.axis_index("c")
-    spread_tile(hid_ref, left_ref, right_ref, edge_ref, wide_ref)
+    spread_tile([(hid_ref, j) for j in range(cols + 2)], edge_ref, wide_ref)
     wide_ref[cols + 2 :] = jnp.zeros((width - cols - 2, rows, 3 * chans), BF16)
     pieces = [wide_ref[tap : tap + cols] for tap in range(3)]
     lhs = jnp.concatenate(pieces, axis=-1).reshape(cols * rows, 9 * chans)
@@ -270,9 +275,9 @@
                 ].astype(ref.dtype)
 
 
-def second_tile(tile, left, right, edges, kernel, cotangent, chips):
-    cols, rows, chans = tile.shape
-    outs = cotangent.shape[2]
+def second_tile(tile, edges, kernel, cotangent, chips):
+    chans = tile.shape[2]
+    cols, rows, outs = cotangent.shape
     width = cols + 8
     cut = (chips, 9 * chans // (2 * chips), outs)
     return pl.pallas_call(
@@ -282,17 +287,57 @@
             jax.ShapeDtypeStruct(cut, F32),
             jax.ShapeDtypeStruct(cut, BF16),
         ),
-        in_specs=[VMEM_SPEC] * 6,
+        in_specs=[VMEM_SPEC] * 4,
         out_specs=(VMEM_SPEC,) * 3,
         scratch_shapes=[
             pltpu.VMEM((width, rows, 3 * chans), BF16),
             pltpu.VMEM((width + 2, rows, outs), BF16),
             pltpu.VMEM((3 * chans, 3 * outs), F32),
         ],
-        compiler_params=pltpu.CompilerParams(vmem_limit_bytes=28 * 2**20),
+        compiler_params=pltpu.CompilerParams(vmem_limit_bytes=9 * 2**20),
         cost_estimate=QUICK,
         name="second",
-    )(tile, left, right, edges, kernel.reshape(9 * chans, outs), cotangent)
+    )(tile, edges, kernel.reshape(9 * chans, outs), cotangent)
+
+
+def point_kernel(own_ref, a_ref, b_ref, c_ref, back_ref, delta_ref, hidden_ref):
+    cols = own_ref.shape[0]
+    strip = 2 * lax.axis_index("y") + lax.axis_index("c")
+    strips = 2 * lax.axis_size("y")
+
+    def column(j, sees_delta, keep):
+        pre = own_ref[j] + a_ref[j].astype(F32) + b_ref[j].astype(F32) + c_ref[j].astype(F32)
+        sigma = jax.nn.sigmoid(pre)
+        hidden = pre * sigma
+        if keep is not None:
+            hidden = jnp.where(keep, hidden, 0.0)
+        hidden_ref[j] = hidden.astype(BF16)
+        if sees_delta:
+            slope = sigma * (1.0 + pre * (1.0 - sigma))
+            delta_ref[j - 1] = (back_ref[j - 1] * slope).astype(BF16)
+
+    column(0, False, strip > 0)
+    column(cols - 1, False, strip < strips - 1)
+
+    def each(j, _):
+        column(j, True, None)
+
+    lax.fori_loop(1, cols - 1, each, None)
+
+
+def point(own, parts, back):
+    return pl.pallas_call(
+        point_kernel,
+        out_shape=(
+            jax.ShapeDtypeStruct(back.shape, BF16),
+            jax.ShapeDtypeStruct(own.shape, BF16),
+        ),
+        in_specs=[VMEM_SPEC] * 5,
+        out_specs=(VMEM_SPEC,) * 2,
+        compiler_params=pltpu.CompilerParams(vmem_limit_bytes=2 * 2**20),
+        cost_estimate=QUICK,
+        name="point",
+    )(own, *parts, back)
 
 
 def fold_kernel(near_ref, got_ref, keep_ref, *send_refs):
@@ -311,23 +356,19 @@
         out_shape=(jax.ShapeDtypeStruct(shape, F32),) + (jax.ShapeDtypeStruct(shape, BF16),) * 3,
         in_specs=[VMEM_SPEC] * 2,
         out_specs=(VMEM_SPEC,) * 4,
-        compiler_params=pltpu.CompilerParams(vmem_limit_bytes=12 * 2**20),
+        compiler_params=pltpu.CompilerParams(vmem_limit_bytes=2 * 2**20),
         cost_estimate=QUICK,
         name="fold",
     )(near, got)
 
 
-def tile_halo(x):
-    left, right = halo(x, FREQ, 0)
-    last = x.shape[1] - 1
-    ends = [
-        jnp.concatenate([left[:, r], x[:, r], right[:, r]], axis=0) for r in (last, 0)
-    ]
+def row_halo(pieces):
+    last = pieces[0].shape[1] - 1
+    ends = [jnp.concatenate([piece[:, r] for piece in pieces], axis=0) for r in (last, 0)]
     count = lax.axis_size(SKY)
     up = [(i, i + 1) for i in range(count - 1)]
     down = [(j, i) for i, j in up]
-    edges = jnp.stack([lax.ppermute(ends[0], SKY, up), lax.ppermute(ends[1], SKY, down)])
-    return left, right, edges
+    return jnp.stack([lax.ppermute(ends[0], SKY, up), lax.ppermute(ends[1], SKY, down)])
 
 
 def join_kernel(own_ref, far_ref, second_ref, out_ref):
@@ -352,13 +393,41 @@
         out_shape=jax.ShapeDtypeStruct((pieces, rows, outs), BF16),
         in_specs=[VMEM_SPEC] * 3,
         out_specs=VMEM_SPEC,
-        compiler_params=pltpu.CompilerParams(vmem_limit_bytes=16 * 2**20),
+        compiler_params=pltpu.CompilerParams(vmem_limit_bytes=2 * 2**20),
         cost_estimate=QUICK,
         name="join",
     )(own, far, second)
 
 
 STEPS = (0, 1, 3, 2)
+
+
+def order_kernel(extra, a_ref, b_ref, c_ref, d_ref, out_ref):
+    rows = a_ref.shape[0] - extra
+    sz = lax.axis_size("z")
+    me = lax.axis_index("z")
+    values = [ref[...].astype(F32) for ref in (a_ref, b_ref, c_ref, d_ref)]
+    rest = []
+    for z in range(len(STEPS)):
+        value = values[0]
+        for step, other in zip(STEPS[1:], values[1:]):
+            value = jnp.where(lax.rem(me + sz - step, sz) == z, other, value)
+        out_ref[z * rows : (z + 1) * rows, :] = value[:rows].astype(BF16)
+        rest.append(value[rows:])
+    out_ref[len(STEPS) * rows :, :] = jnp.concatenate(rest, axis=0).astype(BF16)
+
+
+def order_pieces(parts, extra):
+    rows, outs = parts[0].shape
+    return pl.pallas_call(
+        functools.partial(order_kernel, extra),
+        out_shape=jax.ShapeDtypeStruct((4 * rows, outs), BF16),
+        in_specs=[VMEM_SPEC] * 4,
+        out_specs=VMEM_SPEC,
+        compiler_params=pltpu.CompilerParams(vmem_limit_bytes=4 * 2**20),
+        cost_estimate=QUICK,
+        name="order_pieces",
+    )(*parts)
 
 
 def first_kernel(sz, a_ref, b_ref, c_ref, d_ref, out_ref):
@@ -382,7 +451,7 @@
         out_shape=jax.ShapeDtypeStruct((3, 3, chans, outs), F32),
         in_specs=[VMEM_SPEC] * 4,
         out_specs=VMEM_SPEC,
-        compiler_params=pltpu.CompilerParams(vmem_limit_bytes=16 * 2**20),
+        compiler_params=pltpu.CompilerParams(vmem_limit_bytes=4 * 2**20),
         cost_estimate=QUICK,
         name="lay_first",
     )(*parts)
@@ -411,7 +480,7 @@
         out_shape=jax.ShapeDtypeStruct((2 * sy * sx * rows, outs), F32),
         in_specs=[VMEM_SPEC] * 2,
         out_specs=VMEM_SPEC,
-        compiler_params=pltpu.CompilerParams(vmem_limit_bytes=16 * 2**20),
+        compiler_params=pltpu.CompilerParams(vmem_limit_bytes=4 * 2**20),
         cost_estimate=QUICK,
         name="lay_second",
     )(near, far)
@@ -424,7 +493,6 @@
 def body(sky_cube, weight_first, weight_second, cotangent):
     cols, rows, chans = sky_cube.shape
     strip, _, outs = cotangent.shape
-    here, core = lax.axis_index("y"), lax.axis_index("c")
     chips = lax.axis_size("y")
 
     edges = jnp.concatenate(halo(sky_cube, SKY, 1), axis=1)
@@ -432,36 +500,34 @@
     far_weight = shift(weight_first, "c", 1)
     edges = jnp.transpose(edges, (1, 0, 2))
     far_edges = shift(edges, "c", 1)
-    wide = spread(sky_cube, far_cube, edges, far_edges, chips)
+    left, right = halo(cotangent, FREQ, 0)
+    own_cube, left, right = lax.optimization_barrier((sky_cube, left, right))
+    wide = spread(own_cube, far_cube, edges, far_edges, chips)
     kernel = jnp.concatenate([weight_first, far_weight], axis=2).reshape(18 * chans, outs)
 
     order = (2, 1, chips - 1)
     near = []
     hold = wide
     for step in order:
-        part = conv_strip((here + step) % chips, hold, kernel, strip, BF16)
+        part = conv_strip(step, hold, kernel, strip + 2, BF16)
         near.append(part)
         hold, _ = lax.optimization_barrier((wide, part))
-    own = conv_strip(here, wide, kernel, strip, F32)
-    pre = own
-    for step, part in zip(order, near):
-        pre = pre + shift(part, "y", step).astype(F32)
-
-    late_cotangent, _ = lax.optimization_barrier((cotangent, near[-1]))
-    back = back_tile(late_cotangent, *tile_halo(late_cotangent), weight_second)
-    sigma = jax.nn.sigmoid(pre)
-    delta = (back * (sigma * (1.0 + pre * (1.0 - sigma)))).astype(BF16)
-    hidden = (pre * sigma).astype(BF16)
+    own = conv_strip(0, wide, kernel, strip + 2, F32)
+    got = [shift(part, "y", step) for step, part in zip(order, near)]
+
+    late, left, right, _ = lax.optimization_barrier((cotangent, left, right, near[-1]))
+    back = back_tile(late, left, right, row_halo([left, late, right]), weight_second)
+    delta, hidden = point(own, got, back)
 
     pieces = [(step, shift(delta, "y", step)) for step in (1, chips - 1, 2)]
-    total = grad_strip(here, wide, delta, None, False)
+    total = grad_strip(0, wide, delta, None, False)
     late_hidden, _ = lax.optimization_barrier((hidden, total))
 
-    edges = tile_halo(late_hidden)
+    edges = row_halo([late_hidden])
     for step, piece in pieces[:2]:
-        total = grad_strip((here - step) % chips, wide, piece, total, False)
+        total = grad_strip(chips - step, wide, piece, total, False)
     late_hidden, _ = lax.optimization_barrier((late_hidden, total))
-    features, near, far = second_tile(late_hidden, *edges, weight_second, cotangent, chips)
+    features, near, far = second_tile(late_hidden, edges, weight_second, cotangent, chips)
     keep, *sends = fold(near, shift(far, "c", 1))
     for step, send in zip(STEPS[1:], sends):
         keep = keep + shift(send, "y", step).astype(F32)
@@ -472,22 +538,16 @@
     extra = second.shape[1]
 
     step, piece = pieces[2]
-    total = grad_strip((here - step) % chips, wide, piece, total, True)
+    total = grad_strip(chips - step, wide, piece, total, True)
     first_own, first_far = total
 
     joined = join(first_own, shift(first_far, "c", 1), second)
     summed = lax.all_to_all(joined, SKY, 0, 0, tiled=True)
     summed = jnp.sum(summed.astype(F32), axis=0).astype(BF16)
-    rows_z = jnp.stack(gather_steps(summed, "z"))
-    me_z = lax.axis_index("z")
-    back_to = jnp.stack([(me_z - k) % sz for k in range(sz)])
-    slot_of = jnp.asarray([STEPS.index(k) for k in range(sz)])[back_to]
-    rows_z = jnp.concatenate([lax.dynamic_index_in_dim(rows_z, slot_of[k], 0) for k in range(sz)])
-    main = rows_z[:, :-extra].reshape(-1, outs)
-    rest = rows_z[:, -extra:].reshape(-1, outs)
-    parts = gather_steps(jnp.concatenate([main, rest]), "x")
-    grad_first = lay_first([part[: main.shape[0]] for part in parts], sz, chans)
-    share = jnp.stack([part[main.shape[0] :] for part in parts])
+    parts = gather_steps(order_pieces(gather_steps(summed, "z"), extra), "x")
+    main = parts[0].shape[0] - sz * extra
+    grad_first = lay_first(parts, sz, chans)
+    share = jnp.stack([part[main:] for part in parts])
     share = jnp.stack(gather_steps(share, "y"))
     grad_second = lay_second(share, shift(share, "c", 1)).reshape(3, 3, outs, outs)
     return features, grad_first, grad_second

time: 184 us -> 152 us (0.83)
  blocking collectives: 0 us -> 22 us
  starting transfers between devices: 68.8 us -> 52.5 us
  waiting for transfers between devices: 62.2 us -> 48.4 us
  between operations: 8.89 us -> 1 us
  local copies, waits for them, and re-layouts: 10.8 us -> 2.92 us
  Pallas kernels: 29.7 us -> 23.6 us
    ppermute x6 -> x4, waiting for transfers between devices: 28.1 us -> 4.54 us  [halo(): return (lax.ppermute(last, axes, up), lax.ppermute(first, axes, down))]
    all_to_all x0 -> x1, blocking collectives: none -> 22 us  [body(): summed = lax.all_to_all(joined, SKY, 0, 0, tiled=True)]
    ppermute x24, waiting for transfers between devices: 18.9 us -> 40 us  [shift(): lax.ppermute(x, axis, [(i, (i + step) % count) for i in range(count)])]
    all_to_all x1 -> x0, waiting for transfers between devices: 11.8 us -> none  [body(): summed = lax.all_to_all(joined, SKY, 0, 0, tiled=True)]
    all_to_all x1 -> x0, starting transfers between devices: 9.02 us -> none  [body(): summed = lax.all_to_all(joined, SKY, 0, 0, tiled=True)]
    ppermute x6 -> x4, starting transfers between devices: 18.5 us -> 10.2 us  [halo(): return (lax.ppermute(last, axes, up), lax.ppermute(first, axes, down))]
    unnamed x24 -> x8, local copies, waits for them, and re-layouts: 7.54 us -> 0.04 us
    pallas_call x8 -> x10, Pallas kernels: 16.9 us -> 13.8 us  [the longest x4 7 us: grad_strip(): pl.pallas_call(functools.partial(grad_kernel, step, old is not None, last...]
  transfers between devices with their start and end apart: 35 -> 32, of which waited for: 14 -> 17; matrix products, arithmetic and copies ran while one was open for 2% -> 3% of each run, Pallas kernels for 9% -> 11%
where the time goes in v4:
time: 152 us
  starting transfers between devices  52.5 us (35%)
  waiting for transfers between devices  48.4 us (32%)
  Pallas kernels  23.6 us (16%)
  blocking collectives  22 us (14%)
  local copies, waits for them, and re-layouts  2.92 us (2%)
    ppermute x24, waiting for transfers between devices, shift(): lax.ppermute(x, axis, [(i, (i + step) % count) for i in range(count)])  40 us
    ppermute x24, starting transfers between devices, shift(): lax.ppermute(x, axis, [(i, (i + step) % count) for i in range(count)])  31 us
    all_to_all x1, blocking collectives, body(): summed = lax.all_to_all(joined, SKY, 0, 0, tiled=True)  22 us
    ppermute x4, starting transfers between devices, halo(): return (lax.ppermute(last, axes, up), lax.ppermute(first, axes, down))  10.2 us
    ppermute x2, starting transfers between devices, row_halo(): lax.ppermute(ends[0], SKY, up)  8.53 us
    pallas_call x4, Pallas kernels, grad_strip(): pl.pallas_call(functools.partial(grad_kernel, step, old is not None, last...  7 us
    pallas_call x4, Pallas kernels, conv_strip(): pl.pallas_call(functools.partial(conv_kernel, step), out_shape=jax.ShapeD...  5.88 us
    ppermute x4, waiting for transfers between devices, halo(): return (lax.ppermute(last, axes, up), lax.ppermute(first, axes, down))  4.54 us
  transfers between devices with their start and end apart: 32, of which 17 were waited for; matrix products, arithmetic and copies ran while one was open for 3% of the time, Pallas kernels for 11%

profile of v4, /device:TPU:1, one launch (start us, length us, event | category | flops | bytes accessed | tf_op | source)
XLA Modules:
  0.0 151.9 jit_solution(13197552101785143757)
XLA Ops:
  3.7 3.2 %collective-permute-start.3 = (bf16[256,1,128]{2,0,1:T(8,128)(2,1)S(1)}, bf16[256,1,128]{2,0,1:T(8,128)(2,1)S(1)}, u32[]{:S(2)}, u32[]{:S(2)}) collective-permute-start(bf16[256,1,128]{2,0,1:T(8,128)(2,1)S(1)} %copy.21), channel_id=1, source_target_pairs={{0,1},{1,2},{2,3},{3,4},{4,5},{5,6},{6,7},{7,8},{8,9},{9,10},{10,1... | collective-permute-start | bytes 196616 | tf_op jit(solution)/shard_map/ppermute | solution.py:28
  8.9 3.8 %collective-permute-start = (bf16[1,32,256]{2,1,0:T(8,128)(2,1)S(1)}, bf16[1,32,256]{2,1,0:T(8,128)(2,1)S(1)}, u32[]{:S(2)}, u32[]{:S(2)}) collective-permute-start(bf16[1,32,256]{2,1,0:T(8,128)(2,1)S(1)} %get-tuple-element.52), channel_id=1, source_target_pairs={{0,16},{16,32},{32,48},{48,64},{64,80},{80,96},{96,112},{1,17},{17... | collective-permute-start | bytes 49160 | tf_op jit(solution)/shard_map/ppermute | solution.py:28
  13.6 1.9 %collective-permute-start.1 = (bf16[1,32,256]{2,1,0:T(8,128)(2,1)S(1)}, bf16[1,32,256]{2,1,0:T(8,128)(2,1)S(1)}, u32[]{:S(2)}, u32[]{:S(2)}) collective-permute-start(bf16[1,32,256]{2,1,0:T(8,128)(2,1)S(1)} %get-tuple-element.51), channel_id=1, source_target_pairs={{16,0},{32,16},{48,32},{64,48},{80,64},{96,80},{112,96},{17,1},{33... | collective-permute-start | bytes 49160 | tf_op jit(solution)/shard_map/ppermute | solution.py:28
  15.5 3.7 %collective-permute-done.1.right_ref = bf16[1,32,256]{2,1,0:T(8,128)(2,1)S(1)} collective-permute-done((bf16[1,32,256]{2,1,0:T(8,128)(2,1)S(1)}, bf16[1,32,256]{2,1,0:T(8,128)(2,1)S(1)}, u32[]{:S(2)}, u32[]{:S(2)}) %collective-permute-start.1) | collective-permute-done | bytes 16416 | tf_op jit(solution)/shard_map/ppermute | solution.py:28
  20.7 1.9 %spread.1.wide_ref = bf16[4,40,32,768]{3,2,1,0:T(8,128)(2,1)S(1)} custom-call(bf16[256,32,128]{2,1,0:T(8,128)(2,1)S(1)} %copy-done.2, bf16[256,32,128]{2,1,0:T(8,128)(2,1)S(1)} %collective-permute-done.2.far_ref, bf16[2,256,128]{2,1,0:T(8,128)(2,1)S(1)} %maximum_bitcast_fusion.own_halo_ref, bf16[2,256,128]{2,1,0:T(8,128)(2,1)S(1)} %collective-permute-done.5.far_halo_ref), custom_call_target="tpu_custom_call" | custom-call | flops 1 | bytes 8388608 | tf_op jit(solution)/shard_map/spread/pallas_call | solution.py:103
  29.8 2.0 %collective-permute-start.9 = (bf16[34,32,256]{2,1,0:T(8,128)(2,1)S(1)}, bf16[34,32,256]{2,1,0:T(8,128)(2,1)S(1)}, u32[]{:S(2)}, u32[]{:S(2)}) collective-permute-start(bf16[34,32,256]{2,1,0:T(8,128)(2,1)S(1)} %conv_first.7), channel_id=1, source_target_pairs={{0,96},{32,0},{64,32},{96,64},{1,97},{33,1},{65,33},{97,65},{2,98}... | collective-permute-start | bytes 1671176 | tf_op jit(solution)/shard_map/ppermute | solution.py:19
  32.2 4.3 %collective-permute-start.10 = (bf16[34,256]{1,0:T(8,128)(2,1)S(1)}, bf16[34,256]{1,0:T(8,128)(2,1)S(1)}, u32[]{:S(2)}, u32[]{:S(2)}) collective-permute-start(bf16[34,256]{1,0:T(8,128)(2,1)S(1)} %pad_maximum_fusion.5), channel_id=1, source_target_pairs={{0,1},{1,2},{2,3},{3,4},{4,5},{5,6},{6,7},{7,8},{8,9},{9,10},{10,1... | collective-permute-start | bytes 52232 | tf_op jit(solution)/shard_map/ppermute | solution.py:371
  39.4 2.0 %collective-permute-done.11 = bf16[34,256]{1,0:T(8,128)(2,1)S(1)} collective-permute-done((bf16[34,256]{1,0:T(8,128)(2,1)S(1)}, bf16[34,256]{1,0:T(8,128)(2,1)S(1)}, u32[]{:S(2)}, u32[]{:S(2)}) %collective-permute-start.11) | collective-permute-done | bytes 17440 | tf_op jit(solution)/shard_map/ppermute | solution.py:371
  42.9 10.0 %collective-permute-done.9.c_ref = bf16[34,32,256]{2,1,0:T(8,128)(2,1)S(1)} collective-permute-done((bf16[34,32,256]{2,1,0:T(8,128)(2,1)S(1)}, bf16[34,32,256]{2,1,0:T(8,128)(2,1)S(1)}, u32[]{:S(2)}, u32[]{:S(2)}) %collective-permute-start.9) | collective-permute-done | bytes 557088 | tf_op jit(solution)/shard_map/ppermute | solution.py:19
  53.8 3.0 %collective-permute-start.13 = (bf16[32,32,256]{2,1,0:T(8,128)(2,1)S(1)}, bf16[32,32,256]{2,1,0:T(8,128)(2,1)S(1)}, u32[]{:S(2)}, u32[]{:S(2)}) collective-permute-start(bf16[32,32,256]{2,1,0:T(8,128)(2,1)S(1)} %get-tuple-element.33.delta_ref), channel_id=1, source_target_pairs={{0,32},{32,64},{64,96},{96,0},{1,33},{33,65},{65,97},{97,1},{2,34}... | collective-permute-start | bytes 1572872 | tf_op jit(solution)/shard_map/ppermute | solution.py:19
  57.3 1.7 %grad_first.4.refs_0_ = f32[768,768]{1,0:T(8,128)S(1)} custom-call(bf16[4,40,32,768]{3,2,1,0:T(8,128)(2,1)S(1)} %spread.1.wide_ref, bf16[32,32,256]{2,1,0:T(8,128)(2,1)S(1)} %get-tuple-element.33.delta_ref), custom_call_target="tpu_custom_call" | custom-call | flops 1 | bytes 8388608 | tf_op jit(solution)/shard_map/grad_first/pallas_call | solution.py:177
  59.4 4.3 %collective-permute-start.14 = (bf16[34,256]{1,0:T(8,128)(2,1)S(1)}, bf16[34,256]{1,0:T(8,128)(2,1)S(1)}, u32[]{:S(2)}, u32[]{:S(2)}) collective-permute-start(bf16[34,256]{1,0:T(8,128)(2,1)S(1)} %get-tuple-element.47), channel_id=1, source_target_pairs={{0,1},{1,2},{2,3},{3,4},{4,5},{5,6},{6,7},{7,8},{8,9},{9,10},{10,1... | collective-permute-start | bytes 52232 | tf_op jit(solution)/shard_map/ppermute | solution.py:371
  66.6 1.8 %collective-permute-done.15 = bf16[34,256]{1,0:T(8,128)(2,1)S(1)} collective-permute-done((bf16[34,256]{1,0:T(8,128)(2,1)S(1)}, bf16[34,256]{1,0:T(8,128)(2,1)S(1)}, u32[]{:S(2)}, u32[]{:S(2)}) %collective-permute-start.15) | collective-permute-done | bytes 17440 | tf_op jit(solution)/shard_map/ppermute | solution.py:371
  68.5 1.7 %grad_first.5.refs_0_ = f32[768,768]{1,0:T(8,128)S(1)} custom-call(bf16[4,40,32,768]{3,2,1,0:T(8,128)(2,1)S(1)} %spread.1.wide_ref, bf16[32,32,256]{2,1,0:T(8,128)(2,1)S(1)} %collective-permute-done.13.delta_ref, f32[768,768]{1,0:T(8,128)S(1)} %grad_first.4.refs_0_), custom_call_target="tpu_custom_call" | custom-call | flops 1 | bytes 8388608 | tf_op jit(solution)/shard_map/grad_first/pallas_call | solution.py:177
  70.2 1.7 %grad_first.6.refs_0_ = f32[768,768]{1,0:T(8,128)S(1)} custom-call(bf16[4,40,32,768]{3,2,1,0:T(8,128)(2,1)S(1)} %spread.1.wide_ref, bf16[32,32,256]{2,1,0:T(8,128)(2,1)S(1)} %collective-permute-done.12.delta_ref, f32[768,768]{1,0:T(8,128)S(1)} %grad_first.5.refs_0_), custom_call_target="tpu_custom_call" | custom-call | flops 1 | bytes 8388608 | tf_op jit(solution)/shard_map/grad_first/pallas_call | solution.py:177
  72.0 3.5 %second.1 = (bf16[32,32,256]{2,1,0:T(8,128)(2,1)}, f32[4,288,256]{2,1,0:T(8,128)S(1)}, bf16[4,288,256]{2,1,0:T(8,128)(2,1)S(1)}) custom-call(bf16[34,32,256]{2,1,0:T(8,128)(2,1)S(1)} %get-tuple-element.35.hid_ref, bf16[2,34,256]{2,1,0:T(8,128)(2,1)S(1)} %pad_maximum_fusion.4.edge_ref, bf16[2304,256]{1,0:T(8,128)(2,1)S(1)} %bitcast.49, ...), custom_call_target="tpu_custom_call" | custom-call | flops 1 | bytes 8388608 | tf_op jit(solution)/shard_map/second/pallas_call | solution.py:283
  75.5 2.4 %collective-permute-start.18 = (bf16[4,288,256]{2,1,0:T(8,128)(2,1)S(1)}, bf16[4,288,256]{2,1,0:T(8,128)(2,1)S(1)}, u32[]{:S(2)}, u32[]{:S(2)}) collective-permute-start(bf16[4,288,256]{2,1,0:T(8,128)(2,1)S(1)} %get-tuple-element.40), channel_id=1, source_target_pairs={{0,16},{16,0},{1,17},{17,1},{2,18},{18,2},{3,19},{19,3},{4,20},{20... | collective-permute-start | bytes 1769480 | tf_op jit(solution)/shard_map/ppermute | solution.py:19
  78.0 3.2 %collective-permute-done.16.delta_ref = bf16[32,32,256]{2,1,0:T(8,128)(2,1)S(1)} collective-permute-done((bf16[32,32,256]{2,1,0:T(8,128)(2,1)S(1)}, bf16[32,32,256]{2,1,0:T(8,128)(2,1)S(1)}, u32[]{:S(2)}, u32[]{:S(2)}) %collective-permute-start.16) | collective-permute-done | bytes 524320 | tf_op jit(solution)/shard_map/ppermute | solution.py:19
  81.2 1.8 %grad_first.7 = (f32[384,768]{1,0:T(8,128)S(1)}, bf16[384,768]{1,0:T(8,128)(2,1)S(1)}) custom-call(bf16[4,40,32,768]{3,2,1,0:T(8,128)(2,1)S(1)} %spread.1.wide_ref, bf16[32,32,256]{2,1,0:T(8,128)(2,1)S(1)} %collective-permute-done.16.delta_ref, f32[768,768]{1,0:T(8,128)S(1)} %grad_first.6.refs_0_), custom_call_target="tpu_custom_call" | custom-call | flops 1 | bytes 8388608 | tf_op jit(solution)/shard_map/grad_first/pallas_call | solution.py:177
  85.4 1.8 %collective-permute-start.20 = (bf16[288,256]{1,0:T(8,128)(2,1)S(1)}, bf16[288,256]{1,0:T(8,128)(2,1)S(1)}, u32[]{:S(2)}, u32[]{:S(2)}) collective-permute-start(bf16[288,256]{1,0:T(8,128)(2,1)S(1)} %get-tuple-element.43), channel_id=1, source_target_pairs={{0,96},{32,0},{64,32},{96,64},{1,97},{33,1},{65,33},{97,65},{2,98}... | collective-permute-start | bytes 442376 | tf_op jit(solution)/shard_map/ppermute | solution.py:19
  88.0 3.2 %collective-permute-done.19 = bf16[288,256]{1,0:T(8,128)(2,1)S(1)} collective-permute-done((bf16[288,256]{1,0:T(8,128)(2,1)S(1)}, bf16[288,256]{1,0:T(8,128)(2,1)S(1)}, u32[]{:S(2)}, u32[]{:S(2)}) %collective-permute-start.19) | collective-permute-done | bytes 147488 | tf_op jit(solution)/shard_map/ppermute | solution.py:19
  91.2 4.0 %collective-permute-done.21 = bf16[288,256]{1,0:T(8,128)(2,1)S(1)} collective-permute-done((bf16[288,256]{1,0:T(8,128)(2,1)S(1)}, bf16[288,256]{1,0:T(8,128)(2,1)S(1)}, u32[]{:S(2)}, u32[]{:S(2)}) %collective-permute-start.21) | collective-permute-done | bytes 147488 | tf_op jit(solution)/shard_map/ppermute | solution.py:19
  95.5 22.0 %all_to_all.5 = bf16[16,90,256]{2,1,0:T(8,128)(2,1)S(1)} all-to-all(bf16[16,90,256]{2,1,0:T(8,128)(2,1)S(1)} %join.1), channel_id=1, replica_groups=mesh['y'=4,'c'=2,'z'=4,'x'=4] {'z','x'}, dimensions={0} | all-to-all | bytes 1474560 | tf_op jit(solution)/shard_map/all_to_all | solution.py:545
  117.7 2.7 %collective-permute-start.23 = (bf16[90,256]{1,0:T(8,128)(2,1)S(1)}, bf16[90,256]{1,0:T(8,128)(2,1)S(1)}, u32[]{:S(2)}, u32[]{:S(2)}) collective-permute-start(bf16[90,256]{1,0:T(8,128)(2,1)S(1)} %reduce_sum.12.a_ref), channel_id=1, source_target_pairs={{0,12},{4,0},{8,4},{12,8},{1,13},{5,1},{9,5},{13,9},{2,14},{6,2},{... | collective-permute-start | bytes 138248 | tf_op jit(solution)/shard_map/ppermute | solution.py:19
  121.8 3.0 %collective-permute-done.24.d_ref = bf16[90,256]{1,0:T(8,128)(2,1)S(1)} collective-permute-done((bf16[90,256]{1,0:T(8,128)(2,1)S(1)}, bf16[90,256]{1,0:T(8,128)(2,1)S(1)}, u32[]{:S(2)}, u32[]{:S(2)}) %collective-permute-start.24) | collective-permute-done | bytes 46112 | tf_op jit(solution)/shard_map/ppermute | solution.py:19
  125.1 2.4 %collective-permute-start.26 = (bf16[360,256]{1,0:T(8,128)(2,1)S(1)}, bf16[360,256]{1,0:T(8,128)(2,1)S(1)}, u32[]{:S(2)}, u32[]{:S(2)}) collective-permute-start(bf16[360,256]{1,0:T(8,128)(2,1)S(1)} %order_pieces.1.a_ref), channel_id=1, source_target_pairs={{0,3},{1,0},{2,1},{3,2},{4,7},{5,4},{6,5},{7,6},{8,11},{9,8},{10,9... | collective-permute-start | bytes 552968 | tf_op jit(solution)/shard_map/ppermute | solution.py:19
  127.5 3.3 %collective-permute-done.27.d_ref = bf16[360,256]{1,0:T(8,128)(2,1)S(1)} collective-permute-done((bf16[360,256]{1,0:T(8,128)(2,1)S(1)}, bf16[360,256]{1,0:T(8,128)(2,1)S(1)}, u32[]{:S(2)}, u32[]{:S(2)}) %collective-permute-start.27) | collective-permute-done | bytes 184352 | tf_op jit(solution)/shard_map/ppermute | solution.py:19
  130.9 4.3 %collective-permute-done.25.b_ref = bf16[360,256]{1,0:T(8,128)(2,1)S(1)} collective-permute-done((bf16[360,256]{1,0:T(8,128)(2,1)S(1)}, bf16[360,256]{1,0:T(8,128)(2,1)S(1)}, u32[]{:S(2)}, u32[]{:S(2)}) %collective-permute-start.25) | collective-permute-done | bytes 184352 | tf_op jit(solution)/shard_map/ppermute | solution.py:19
  135.4 2.7 %collective-permute-start.29 = (bf16[4,72,256]{2,1,0:T(8,128)(2,1)S(1)}, bf16[4,72,256]{2,1,0:T(8,128)(2,1)S(1)}, u32[]{:S(2)}, u32[]{:S(2)}) collective-permute-start(bf16[4,72,256]{2,1,0:T(8,128)(2,1)S(1)} %get-tuple-element.54), channel_id=1, source_target_pairs={{0,96},{32,0},{64,32},{96,64},{1,97},{33,1},{65,33},{97,65},{2,98}... | collective-permute-start | bytes 442376 | tf_op jit(solution)/shard_map/ppermute | solution.py:19
  138.0 2.5 %collective-permute-done.28 = bf16[4,72,256]{2,1,0:T(8,128)(2,1)S(1)} collective-permute-done((bf16[4,72,256]{2,1,0:T(8,128)(2,1)S(1)}, bf16[4,72,256]{2,1,0:T(8,128)(2,1)S(1)}, u32[]{:S(2)}, u32[]{:S(2)}) %collective-permute-start.28) | collective-permute-done | bytes 147488 | tf_op jit(solution)/shard_map/ppermute | solution.py:19
  141.7 3.1 %collective-permute-done.30 = bf16[4,72,256]{2,1,0:T(8,128)(2,1)S(1)} collective-permute-done((bf16[4,72,256]{2,1,0:T(8,128)(2,1)S(1)}, bf16[4,72,256]{2,1,0:T(8,128)(2,1)S(1)}, u32[]{:S(2)}, u32[]{:S(2)}) %collective-permute-start.30) | collective-permute-done | bytes 147488 | tf_op jit(solution)/shard_map/ppermute | solution.py:19
  144.8 3.8 %collective-permute-start.31 = (bf16[4,4,72,256]{3,2,1,0:T(8,128)(2,1)S(1)}, bf16[4,4,72,256]{3,2,1,0:T(8,128)(2,1)S(1)}, u32[]{:S(2)}, u32[]{:S(2)}) collective-permute-start(bf16[4,4,72,256]{3,2,1,0:T(8,128)(2,1)S(1)} %pad_maximum_fusion.1.near_ref), channel_id=1, source_target_pairs={{0,16},{16,0},{1,17},{17,1},{2,18},{18,2},{3,19},{19,3},{4,20},{20... | collective-permute-start | bytes 1769480 | tf_op jit(solution)/shard_map/ppermute | solution.py:19
  (81 shorter events, 34.0 us)
Async XLA Ops:
  0.6 20.0 %collective-permute-start.2 = (bf16[256,32,128]{2,1,0:T(8,128)(2,1)}, bf16[256,32,128]{2,1,0:T(8,128)(2,1)S(1)}, u32[]{:S(2)}, u32[]{:S(2)}) collective-permute-start(bf16[256,32,128]{2,1,0:T(8,128)(2,1)} %own_ref), channel_id=1, source_target_pairs={{0,16},{16,0},{1,17},{17,1},{2,18},{18,2},{3,19},{19,3},{4,20},{20... | collective-permute-start | bytes 6291464 | tf_op jit(solution)/shard_map/ppermute | solution.py:19
  2.1 17.2 %collective-permute-start.6 = (bf16[3,3,128,256]{3,2,1,0:T(8,128)(2,1)}, bf16[3,3,128,256]{3,2,1,0:T(8,128)(2,1)S(1)}, u32[]{:S(2)}, u32[]{:S(2)}) collective-permute-start(bf16[3,3,128,256]{3,2,1,0:T(8,128)(2,1)} %param.5), channel_id=1, source_target_pairs={{0,16},{16,0},{1,17},{17,1},{2,18},{18,2},{3,19},{19,3},{4,20},{20... | collective-permute-start | bytes 1769480 | tf_op jit(solution)/shard_map/ppermute | solution.py:19
  3.7 15.5 %collective-permute-start.3 = (bf16[256,1,128]{2,0,1:T(8,128)(2,1)S(1)}, bf16[256,1,128]{2,0,1:T(8,128)(2,1)S(1)}, u32[]{:S(2)}, u32[]{:S(2)}) collective-permute-start(bf16[256,1,128]{2,0,1:T(8,128)(2,1)S(1)} %copy.21), channel_id=1, source_target_pairs={{0,1},{1,2},{2,3},{3,4},{4,5},{5,6},{6,7},{7,8},{8,9},{9,10},{10,1... | collective-permute-start | bytes 196616 | tf_op jit(solution)/shard_map/ppermute | solution.py:28
  6.9 12.3 %collective-permute-start.4 = (bf16[256,1,128]{2,0,1:T(8,128)(2,1)S(1)}, bf16[256,1,128]{2,0,1:T(8,128)(2,1)S(1)}, u32[]{:S(2)}, u32[]{:S(2)}) collective-permute-start(bf16[256,1,128]{2,0,1:T(8,128)(2,1)S(1)} %copy.22), channel_id=1, source_target_pairs={{1,0},{2,1},{3,2},{4,3},{5,4},{6,5},{7,6},{8,7},{9,8},{10,9},{11,1... | collective-permute-start | bytes 196616 | tf_op jit(solution)/shard_map/ppermute | solution.py:28
  8.9 4.7 %collective-permute-start = (bf16[1,32,256]{2,1,0:T(8,128)(2,1)S(1)}, bf16[1,32,256]{2,1,0:T(8,128)(2,1)S(1)}, u32[]{:S(2)}, u32[]{:S(2)}) collective-permute-start(bf16[1,32,256]{2,1,0:T(8,128)(2,1)S(1)} %get-tuple-element.52), channel_id=1, source_target_pairs={{0,16},{16,32},{32,48},{48,64},{64,80},{80,96},{96,112},{1,17},{17... | collective-permute-start | bytes 49160 | tf_op jit(solution)/shard_map/ppermute | solution.py:28
  13.6 5.6 %collective-permute-start.1 = (bf16[1,32,256]{2,1,0:T(8,128)(2,1)S(1)}, bf16[1,32,256]{2,1,0:T(8,128)(2,1)S(1)}, u32[]{:S(2)}, u32[]{:S(2)}) collective-permute-start(bf16[1,32,256]{2,1,0:T(8,128)(2,1)S(1)} %get-tuple-element.51), channel_id=1, source_target_pairs={{16,0},{32,16},{48,32},{64,48},{80,64},{96,80},{112,96},{17,1},{33... | collective-permute-start | bytes 49160 | tf_op jit(solution)/shard_map/ppermute | solution.py:28
  19.2 1.4 collective-permute-start.5
  25.5 27.4 %collective-permute-start.8 = (bf16[34,32,256]{2,1,0:T(8,128)(2,1)S(1)}, bf16[34,32,256]{2,1,0:T(8,128)(2,1)S(1)}, u32[]{:S(2)}, u32[]{:S(2)}) collective-permute-start(bf16[34,32,256]{2,1,0:T(8,128)(2,1)S(1)} %conv_first.6), channel_id=1, source_target_pairs={{0,32},{32,64},{64,96},{96,0},{1,33},{33,65},{65,97},{97,1},{2,34}... | collective-permute-start | bytes 1671176 | tf_op jit(solution)/shard_map/ppermute | solution.py:19
  26.9 26.0 %collective-permute-start.7 = (bf16[34,32,256]{2,1,0:T(8,128)(2,1)S(1)}, bf16[34,32,256]{2,1,0:T(8,128)(2,1)S(1)}, u32[]{:S(2)}, u32[]{:S(2)}) collective-permute-start(bf16[34,32,256]{2,1,0:T(8,128)(2,1)S(1)} %conv_first.5), channel_id=1, source_target_pairs={{0,64},{32,96},{64,0},{96,32},{1,65},{33,97},{65,1},{97,33},{2,66}... | collective-permute-start | bytes 1671176 | tf_op jit(solution)/shard_map/ppermute | solution.py:19
  29.8 23.1 %collective-permute-start.9 = (bf16[34,32,256]{2,1,0:T(8,128)(2,1)S(1)}, bf16[34,32,256]{2,1,0:T(8,128)(2,1)S(1)}, u32[]{:S(2)}, u32[]{:S(2)}) collective-permute-start(bf16[34,32,256]{2,1,0:T(8,128)(2,1)S(1)} %conv_first.7), channel_id=1, source_target_pairs={{0,96},{32,0},{64,32},{96,64},{1,97},{33,1},{65,33},{97,65},{2,98}... | collective-permute-start | bytes 1671176 | tf_op jit(solution)/shard_map/ppermute | solution.py:19
  32.2 7.2 %collective-permute-start.10 = (bf16[34,256]{1,0:T(8,128)(2,1)S(1)}, bf16[34,256]{1,0:T(8,128)(2,1)S(1)}, u32[]{:S(2)}, u32[]{:S(2)}) collective-permute-start(bf16[34,256]{1,0:T(8,128)(2,1)S(1)} %pad_maximum_fusion.5), channel_id=1, source_target_pairs={{0,1},{1,2},{2,3},{3,4},{4,5},{5,6},{6,7},{7,8},{8,9},{9,10},{10,1... | collective-permute-start | bytes 52232 | tf_op jit(solution)/shard_map/ppermute | solution.py:371
  36.5 5.0 %collective-permute-start.11 = (bf16[34,256]{1,0:T(8,128)(2,1)S(1)}, bf16[34,256]{1,0:T(8,128)(2,1)S(1)}, u32[]{:S(2)}, u32[]{:S(2)}) collective-permute-start(bf16[34,256]{1,0:T(8,128)(2,1)S(1)} %pad_maximum_fusion.6), channel_id=1, source_target_pairs={{1,0},{2,1},{3,2},{4,3},{5,4},{6,5},{7,6},{8,7},{9,8},{10,9},{11,1... | collective-permute-start | bytes 52232 | tf_op jit(solution)/shard_map/ppermute | solution.py:371
  53.8 14.7 %collective-permute-start.13 = (bf16[32,32,256]{2,1,0:T(8,128)(2,1)S(1)}, bf16[32,32,256]{2,1,0:T(8,128)(2,1)S(1)}, u32[]{:S(2)}, u32[]{:S(2)}) collective-permute-start(bf16[32,32,256]{2,1,0:T(8,128)(2,1)S(1)} %get-tuple-element.33.delta_ref), channel_id=1, source_target_pairs={{0,32},{32,64},{64,96},{96,0},{1,33},{33,65},{65,97},{97,1},{2,34}... | collective-permute-start | bytes 1572872 | tf_op jit(solution)/shard_map/ppermute | solution.py:19
  56.8 13.4 %collective-permute-start.12 = (bf16[32,32,256]{2,1,0:T(8,128)(2,1)S(1)}, bf16[32,32,256]{2,1,0:T(8,128)(2,1)S(1)}, u32[]{:S(2)}, u32[]{:S(2)}) collective-permute-start(bf16[32,32,256]{2,1,0:T(8,128)(2,1)S(1)} %get-tuple-element.33.delta_ref), channel_id=1, source_target_pairs={{0,96},{32,0},{64,32},{96,64},{1,97},{33,1},{65,33},{97,65},{2,98}... | collective-permute-start | bytes 1572872 | tf_op jit(solution)/shard_map/ppermute | solution.py:19
  59.4 7.2 %collective-permute-start.14 = (bf16[34,256]{1,0:T(8,128)(2,1)S(1)}, bf16[34,256]{1,0:T(8,128)(2,1)S(1)}, u32[]{:S(2)}, u32[]{:S(2)}) collective-permute-start(bf16[34,256]{1,0:T(8,128)(2,1)S(1)} %get-tuple-element.47), channel_id=1, source_target_pairs={{0,1},{1,2},{2,3},{3,4},{4,5},{5,6},{6,7},{7,8},{8,9},{9,10},{10,1... | collective-permute-start | bytes 52232 | tf_op jit(solution)/shard_map/ppermute | solution.py:371
  63.6 4.8 %collective-permute-start.15 = (bf16[34,256]{1,0:T(8,128)(2,1)S(1)}, bf16[34,256]{1,0:T(8,128)(2,1)S(1)}, u32[]{:S(2)}, u32[]{:S(2)}) collective-permute-start(bf16[34,256]{1,0:T(8,128)(2,1)S(1)} %get-tuple-element.48), channel_id=1, source_target_pairs={{1,0},{2,1},{3,2},{4,3},{5,4},{6,5},{7,6},{8,7},{9,8},{10,9},{11,1... | collective-permute-start | bytes 52232 | tf_op jit(solution)/shard_map/ppermute | solution.py:371
  64.9 16.2 %collective-permute-start.16 = (bf16[32,32,256]{2,1,0:T(8,128)(2,1)S(1)}, bf16[32,32,256]{2,1,0:T(8,128)(2,1)S(1)}, u32[]{:S(2)}, u32[]{:S(2)}) collective-permute-start(bf16[32,32,256]{2,1,0:T(8,128)(2,1)S(1)} %get-tuple-element.33.delta_ref), channel_id=1, source_target_pairs={{0,64},{32,96},{64,0},{96,32},{1,65},{33,97},{65,1},{97,33},{2,66}... | collective-permute-start | bytes 1572872 | tf_op jit(solution)/shard_map/ppermute | solution.py:19
  75.5 8.8 %collective-permute-start.18 = (bf16[4,288,256]{2,1,0:T(8,128)(2,1)S(1)}, bf16[4,288,256]{2,1,0:T(8,128)(2,1)S(1)}, u32[]{:S(2)}, u32[]{:S(2)}) collective-permute-start(bf16[4,288,256]{2,1,0:T(8,128)(2,1)S(1)} %get-tuple-element.40), channel_id=1, source_target_pairs={{0,16},{16,0},{1,17},{17,1},{2,18},{18,2},{3,19},{19,3},{4,20},{20... | collective-permute-start | bytes 1769480 | tf_op jit(solution)/shard_map/ppermute | solution.py:19
  82.9 12.4 %collective-permute-start.17 = (bf16[384,768]{1,0:T(8,128)(2,1)S(1)}, bf16[384,768]{1,0:T(8,128)(2,1)S(1)}, u32[]{:S(2)}, u32[]{:S(2)}) collective-permute-start(bf16[384,768]{1,0:T(8,128)(2,1)S(1)} %get-tuple-element.38), channel_id=1, source_target_pairs={{0,16},{16,0},{1,17},{17,1},{2,18},{18,2},{3,19},{19,3},{4,20},{20... | collective-permute-start | bytes 1769480 | tf_op jit(solution)/shard_map/ppermute | solution.py:19
  84.5 6.7 %collective-permute-start.19 = (bf16[288,256]{1,0:T(8,128)(2,1)S(1)}, bf16[288,256]{1,0:T(8,128)(2,1)S(1)}, u32[]{:S(2)}, u32[]{:S(2)}) collective-permute-start(bf16[288,256]{1,0:T(8,128)(2,1)S(1)} %get-tuple-element.42), channel_id=1, source_target_pairs={{0,32},{32,64},{64,96},{96,0},{1,33},{33,65},{65,97},{97,1},{2,34}... | collective-permute-start | bytes 442376 | tf_op jit(solution)/shard_map/ppermute | solution.py:19
  85.4 5.8 %collective-permute-start.20 = (bf16[288,256]{1,0:T(8,128)(2,1)S(1)}, bf16[288,256]{1,0:T(8,128)(2,1)S(1)}, u32[]{:S(2)}, u32[]{:S(2)}) collective-permute-start(bf16[288,256]{1,0:T(8,128)(2,1)S(1)} %get-tuple-element.43), channel_id=1, source_target_pairs={{0,96},{32,0},{64,32},{96,64},{1,97},{33,1},{65,33},{97,65},{2,98}... | collective-permute-start | bytes 442376 | tf_op jit(solution)/shard_map/ppermute | solution.py:19
  87.2 7.9 %collective-permute-start.21 = (bf16[288,256]{1,0:T(8,128)(2,1)S(1)}, bf16[288,256]{1,0:T(8,128)(2,1)S(1)}, u32[]{:S(2)}, u32[]{:S(2)}) collective-permute-start(bf16[288,256]{1,0:T(8,128)(2,1)S(1)} %get-tuple-element.44), channel_id=1, source_target_pairs={{0,64},{32,96},{64,0},{96,32},{1,65},{33,97},{65,1},{97,33},{2,66}... | collective-permute-start | bytes 442376 | tf_op jit(solution)/shard_map/ppermute | solution.py:19
  117.6 4.2 %collective-permute-start.22 = (bf16[90,256]{1,0:T(8,128)(2,1)S(1)}, bf16[90,256]{1,0:T(8,128)(2,1)S(1)}, u32[]{:S(2)}, u32[]{:S(2)}) collective-permute-start(bf16[90,256]{1,0:T(8,128)(2,1)S(1)} %reduce_sum.12.a_ref), channel_id=1, source_target_pairs={{0,4},{4,8},{8,12},{12,0},{1,5},{5,9},{9,13},{13,1},{2,6},{6,10},{... | collective-permute-start | bytes 138248 | tf_op jit(solution)/shard_map/ppermute | solution.py:19
  117.7 4.1 %collective-permute-start.23 = (bf16[90,256]{1,0:T(8,128)(2,1)S(1)}, bf16[90,256]{1,0:T(8,128)(2,1)S(1)}, u32[]{:S(2)}, u32[]{:S(2)}) collective-permute-start(bf16[90,256]{1,0:T(8,128)(2,1)S(1)} %reduce_sum.12.a_ref), channel_id=1, source_target_pairs={{0,12},{4,0},{8,4},{12,8},{1,13},{5,1},{9,5},{13,9},{2,14},{6,2},{... | collective-permute-start | bytes 138248 | tf_op jit(solution)/shard_map/ppermute | solution.py:19
  120.3 4.4 %collective-permute-start.24 = (bf16[90,256]{1,0:T(8,128)(2,1)S(1)}, bf16[90,256]{1,0:T(8,128)(2,1)S(1)}, u32[]{:S(2)}, u32[]{:S(2)}) collective-permute-start(bf16[90,256]{1,0:T(8,128)(2,1)S(1)} %reduce_sum.12.a_ref), channel_id=1, source_target_pairs={{0,8},{4,12},{8,0},{12,4},{1,9},{5,13},{9,1},{13,5},{2,10},{6,14},... | collective-permute-start | bytes 138248 | tf_op jit(solution)/shard_map/ppermute | solution.py:19
  124.9 6.0 %collective-permute-start.27 = (bf16[360,256]{1,0:T(8,128)(2,1)S(1)}, bf16[360,256]{1,0:T(8,128)(2,1)S(1)}, u32[]{:S(2)}, u32[]{:S(2)}) collective-permute-start(bf16[360,256]{1,0:T(8,128)(2,1)S(1)} %order_pieces.1.a_ref), channel_id=1, source_target_pairs={{0,2},{1,3},{2,0},{3,1},{4,6},{5,7},{6,4},{7,5},{8,10},{9,11},{10,... | collective-permute-start | bytes 552968 | tf_op jit(solution)/shard_map/ppermute | solution.py:19
  125.1 5.8 %collective-permute-start.26 = (bf16[360,256]{1,0:T(8,128)(2,1)S(1)}, bf16[360,256]{1,0:T(8,128)(2,1)S(1)}, u32[]{:S(2)}, u32[]{:S(2)}) collective-permute-start(bf16[360,256]{1,0:T(8,128)(2,1)S(1)} %order_pieces.1.a_ref), channel_id=1, source_target_pairs={{0,3},{1,0},{2,1},{3,2},{4,7},{5,4},{6,5},{7,6},{8,11},{9,8},{10,9... | collective-permute-start | bytes 552968 | tf_op jit(solution)/shard_map/ppermute | solution.py:19
  127.5 7.7 %collective-permute-start.25 = (bf16[360,256]{1,0:T(8,128)(2,1)S(1)}, bf16[360,256]{1,0:T(8,128)(2,1)S(1)}, u32[]{:S(2)}, u32[]{:S(2)}) collective-permute-start(bf16[360,256]{1,0:T(8,128)(2,1)S(1)} %order_pieces.1.a_ref), channel_id=1, source_target_pairs={{0,1},{1,2},{2,3},{3,0},{4,5},{5,6},{6,7},{7,4},{8,9},{9,10},{10,1... | collective-permute-start | bytes 552968 | tf_op jit(solution)/shard_map/ppermute | solution.py:19
  135.3 5.3 %collective-permute-start.28 = (bf16[4,72,256]{2,1,0:T(8,128)(2,1)S(1)}, bf16[4,72,256]{2,1,0:T(8,128)(2,1)S(1)}, u32[]{:S(2)}, u32[]{:S(2)}) collective-permute-start(bf16[4,72,256]{2,1,0:T(8,128)(2,1)S(1)} %get-tuple-element.54), channel_id=1, source_target_pairs={{0,32},{32,64},{64,96},{96,0},{1,33},{33,65},{65,97},{97,1},{2,34}... | collective-permute-start | bytes 442376 | tf_op jit(solution)/shard_map/ppermute | solution.py:19
  135.4 6.3 %collective-permute-start.29 = (bf16[4,72,256]{2,1,0:T(8,128)(2,1)S(1)}, bf16[4,72,256]{2,1,0:T(8,128)(2,1)S(1)}, u32[]{:S(2)}, u32[]{:S(2)}) collective-permute-start(bf16[4,72,256]{2,1,0:T(8,128)(2,1)S(1)} %get-tuple-element.54), channel_id=1, source_target_pairs={{0,96},{32,0},{64,32},{96,64},{1,97},{33,1},{65,33},{97,65},{2,98}... | collective-permute-start | bytes 442376 | tf_op jit(solution)/shard_map/ppermute | solution.py:19
  138.0 6.7 %collective-permute-start.30 = (bf16[4,72,256]{2,1,0:T(8,128)(2,1)S(1)}, bf16[4,72,256]{2,1,0:T(8,128)(2,1)S(1)}, u32[]{:S(2)}, u32[]{:S(2)}) collective-permute-start(bf16[4,72,256]{2,1,0:T(8,128)(2,1)S(1)} %get-tuple-element.54), channel_id=1, source_target_pairs={{0,64},{32,96},{64,0},{96,32},{1,65},{33,97},{65,1},{97,33},{2,66}... | collective-permute-start | bytes 442376 | tf_op jit(solution)/shard_map/ppermute | solution.py:19
  144.8 5.4 %collective-permute-start.31 = (bf16[4,4,72,256]{3,2,1,0:T(8,128)(2,1)S(1)}, bf16[4,4,72,256]{3,2,1,0:T(8,128)(2,1)S(1)}, u32[]{:S(2)}, u32[]{:S(2)}) collective-permute-start(bf16[4,4,72,256]{3,2,1,0:T(8,128)(2,1)S(1)} %pad_maximum_fusion.1.near_ref), channel_id=1, source_target_pairs={{0,16},{16,0},{1,17},{17,1},{2,18},{18,2},{3,19},{19,3},{4,20},{20... | collective-permute-start | bytes 1769480 | tf_op jit(solution)/shard_map/ppermute | solution.py:19
  (3 other events, 31.3 us)

commit v5 on v4

--- a/solution.py
+++ b/solution.py
@@ -11,7 +11,7 @@
 SKY = ("z", "x")
 F32 = jnp.float32
 BF16 = jnp.bfloat16
-QUICK = pl.CostEstimate(flops=1, bytes_accessed=8 * 2**20, transcendentals=0)
+QUICK = pl.CostEstimate(flops=1, bytes_accessed=1, transcendentals=0)
 
 
 def shift(x, axis, step):
@@ -115,35 +115,42 @@
     return lax.rem(lax.axis_index("y") + step, lax.axis_size("y"))
 
 
-def conv_kernel(step, wide_ref, kernel_ref, out_ref):
-    strip, rows, outs = out_ref.shape
-    chip = chip_at(step)
-    pieces = [wide_ref[chip, tap : tap + strip] for tap in range(3)]
-    lhs = jnp.concatenate(pieces, axis=-1).reshape(strip * rows, -1)
-    total = jnp.dot(lhs, kernel_ref[...], preferred_element_type=F32)
-    out_ref[...] = total.reshape(strip, rows, outs).astype(out_ref.dtype)
-
-
-def conv_strip(step, wide, kernel, strip, dtype):
-    rows, depth, outs = wide.shape[2], kernel.shape[0], kernel.shape[1]
-    return pl.pallas_call(
-        functools.partial(conv_kernel, step),
-        out_shape=jax.ShapeDtypeStruct((strip, rows, outs), dtype),
-        in_specs=[VMEM_SPEC, VMEM_SPEC],
-        out_specs=VMEM_SPEC,
-        compiler_params=pltpu.CompilerParams(vmem_limit_bytes=3 * 2**20),
+def conv_kernel(parts, adds, wide_ref, kernel_ref, *refs):
+    rows = wide_ref.shape[2]
+    for (step, first), add_ref, out_ref in zip(parts, refs[:adds] or [None] * len(parts), refs[adds:]):
+        count, _, outs = out_ref.shape
+        chip = chip_at(step)
+        pieces = [wide_ref[chip, first + tap : first + tap + count] for tap in range(3)]
+        lhs = jnp.concatenate(pieces, axis=-1).reshape(count * rows, -1)
+        total = jnp.dot(lhs, kernel_ref[...], preferred_element_type=F32)
+        total = total.reshape(count, rows, outs)
+        if add_ref is not None:
+            total = total + add_ref[...].astype(F32)
+        out_ref[...] = total.astype(out_ref.dtype)
+
+
+def conv_parts(parts, wide, kernel, count, dtype, adds=()):
+    rows, outs = wide.shape[2], kernel.shape[1]
+    return pl.pallas_call(
+        functools.partial(conv_kernel, parts, len(adds)),
+        out_shape=(jax.ShapeDtypeStruct((count, rows, outs), dtype),) * len(parts),
+        in_specs=[VMEM_SPEC] * (2 + len(adds)),
+        out_specs=(VMEM_SPEC,) * len(parts),
+        compiler_params=pltpu.CompilerParams(vmem_limit_bytes=4 * 2**20),
         cost_estimate=QUICK,
         name="conv_first",
-    )(wide, kernel)
-
-
-def grad_kernel(step, has_old, last, wide_ref, delta_ref, *refs):
+    )(wide, kernel, *adds)
+
+
+def grad_kernel(step, has_old, last, wide_ref, a_ref, b_ref, *refs):
     old_ref = refs[0] if has_old else None
     outs_refs, pad_ref = refs[1 if has_old else 0 : -1], refs[-1]
-    strip, rows, outs = delta_ref.shape
+    half, rows, outs = a_ref.shape
+    strip = 2 * half
     cols, depth = wide_ref.shape[1], wide_ref.shape[3]
     pad_ref[0:3] = jnp.zeros((3, rows, outs), BF16)
-    pad_ref[3 : 3 + strip] = delta_ref[...]
+    pad_ref[3 : 3 + half] = a_ref[...]
+    pad_ref[3 + half : 3 + strip] = b_ref[...]
     pad_ref[3 + strip :] = jnp.zeros((cols - strip - 1, rows, outs), BF16)
     lhs = wide_ref[chip_at(step)].reshape(cols * rows, depth)
     rhs = jnp.concatenate(
@@ -164,8 +171,8 @@
             ].astype(BF16)
 
 
-def grad_strip(step, wide, delta, old, last):
-    strip, rows, outs = delta.shape
+def grad_strip(step, wide, halves, old, last):
+    _, rows, outs = halves[0].shape
     depth, cols = wide.shape[3], wide.shape[1]
     shape = (depth, 3 * outs)
     half = (depth // 2, 3 * outs)
@@ -173,7 +180,7 @@
         out_shape = (jax.ShapeDtypeStruct(half, F32), jax.ShapeDtypeStruct(half, BF16))
     else:
         out_shape = (jax.ShapeDtypeStruct(shape, F32),)
-    args = [wide, delta] + ([old] if old is not None else [])
+    args = [wide, *halves] + ([old] if old is not None else [])
     out = pl.pallas_call(
         functools.partial(grad_kernel, step, old is not None, last),
         out_shape=out_shape,
@@ -300,44 +307,47 @@
     )(tile, edges, kernel.reshape(9 * chans, outs), cotangent)
 
 
-def point_kernel(own_ref, a_ref, b_ref, c_ref, back_ref, delta_ref, hidden_ref):
+def point_kernel(own_ref, a0_ref, a1_ref, b0_ref, b1_ref, back_ref, da_ref, db_ref, hidden_ref):
     cols = own_ref.shape[0]
+    half = da_ref.shape[0]
     strip = 2 * lax.axis_index("y") + lax.axis_index("c")
     strips = 2 * lax.axis_size("y")
 
-    def column(j, sees_delta, keep):
-        pre = own_ref[j] + a_ref[j].astype(F32) + b_ref[j].astype(F32) + c_ref[j].astype(F32)
+    def column(j, i, refs, delta_ref, keep):
+        pre = own_ref[j] + refs[0][i].astype(F32) + refs[1][i].astype(F32)
         sigma = jax.nn.sigmoid(pre)
         hidden = pre * sigma
         if keep is not None:
             hidden = jnp.where(keep, hidden, 0.0)
         hidden_ref[j] = hidden.astype(BF16)
-        if sees_delta:
+        if keep is None:
             slope = sigma * (1.0 + pre * (1.0 - sigma))
-            delta_ref[j - 1] = (back_ref[j - 1] * slope).astype(BF16)
-
-    column(0, False, strip > 0)
-    column(cols - 1, False, strip < strips - 1)
-
-    def each(j, _):
-        column(j, True, None)
-
-    lax.fori_loop(1, cols - 1, each, None)
-
-
-def point(own, parts, back):
+            at = j - 1 if delta_ref is da_ref else j - 1 - half
+            delta_ref[at] = (back_ref[j - 1] * slope).astype(BF16)
+
+    left, right = (a0_ref, a1_ref), (b0_ref, b1_ref)
+    column(0, 0, left, None, strip > 0)
+    column(cols - 1, half, right, None, strip < strips - 1)
+
+    def each(i, _):
+        column(i, i, left, da_ref, None)
+        column(half + i, i - 1, right, db_ref, None)
+
+    lax.fori_loop(1, half + 1, each, None)
+
+
+def point(own, left, right, back):
+    strip, rows, outs = back.shape
+    cut = jax.ShapeDtypeStruct((strip // 2, rows, outs), BF16)
     return pl.pallas_call(
         point_kernel,
-        out_shape=(
-            jax.ShapeDtypeStruct(back.shape, BF16),
-            jax.ShapeDtypeStruct(own.shape, BF16),
-        ),
-        in_specs=[VMEM_SPEC] * 5,
-        out_specs=(VMEM_SPEC,) * 2,
+        out_shape=(cut, cut, jax.ShapeDtypeStruct(own.shape, BF16)),
+        in_specs=[VMEM_SPEC] * 6,
+        out_specs=(VMEM_SPEC,) * 3,
         compiler_params=pltpu.CompilerParams(vmem_limit_bytes=2 * 2**20),
         cost_estimate=QUICK,
         name="point",
-    )(own, *parts, back)
+    )(own, *left, *right, back)
 
 
 def fold_kernel(near_ref, got_ref, keep_ref, *send_refs):
@@ -501,33 +511,35 @@
     edges = jnp.transpose(edges, (1, 0, 2))
     far_edges = shift(edges, "c", 1)
     left, right = halo(cotangent, FREQ, 0)
-    own_cube, left, right = lax.optimization_barrier((sky_cube, left, right))
-    wide = spread(own_cube, far_cube, edges, far_edges, chips)
+    wide = spread(sky_cube, far_cube, edges, far_edges, chips)
     kernel = jnp.concatenate([weight_first, far_weight], axis=2).reshape(18 * chans, outs)
 
-    order = (2, 1, chips - 1)
-    near = []
-    hold = wide
-    for step in order:
-        part = conv_strip(step, hold, kernel, strip + 2, BF16)
-        near.append(part)
-        hold, _ = lax.optimization_barrier((wide, part))
-    own = conv_strip(0, wide, kernel, strip + 2, F32)
-    got = [shift(part, "y", step) for step, part in zip(order, near)]
-
-    late, left, right, _ = lax.optimization_barrier((cotangent, left, right, near[-1]))
-    back = back_tile(late, left, right, row_halo([left, late, right]), weight_second)
-    delta, hidden = point(own, got, back)
-
-    pieces = [(step, shift(delta, "y", step)) for step in (1, chips - 1, 2)]
-    total = grad_strip(0, wide, delta, None, False)
-    late_hidden, _ = lax.optimization_barrier((hidden, total))
-
-    edges = row_halo([late_hidden])
-    for step, piece in pieces[:2]:
-        total = grad_strip(chips - step, wide, piece, total, False)
-    late_hidden, _ = lax.optimization_barrier((late_hidden, total))
-    features, near, far = second_tile(late_hidden, edges, weight_second, cotangent, chips)
+    on, off = 1, chips - 1
+    cut = strip // 2 + 1
+    far_a, far_b = conv_parts(((2, 0), (2, cut)), wide, kernel, cut, BF16)
+    hold, left, right, _ = lax.optimization_barrier((wide, left, right, far_a))
+    near_b, near_a = conv_parts(((on, cut), (off, 0)), hold, kernel, cut, BF16)
+    got_a, got_b = shift(far_a, "y", on), shift(far_b, "y", off)
+    late, left, right, _ = lax.optimization_barrier((cotangent, left, right, near_b))
+    edges = row_halo([left, late, right])
+    got_a, edges = lax.optimization_barrier((got_a, edges))
+    both_a, both_b = conv_parts(((on, 0), (off, cut)), wide, kernel, cut, BF16, (got_a, got_b))
+    own = conv_parts(((0, 0),), wide, kernel, strip + 2, F32)[0]
+    from_a = shift(both_a, "y", on), shift(near_a, "y", off)
+    from_b = shift(near_b, "y", on), shift(both_b, "y", off)
+
+    back = back_tile(late, left, right, edges, weight_second)
+    delta_a, delta_b, hidden = point(own, from_a, from_b, back)
+
+    on_a, off_b = shift(delta_a, "y", on), shift(delta_b, "y", off)
+    on_b, off_a = shift(delta_b, "y", on), shift(delta_a, "y", off)
+    on_a, off_b, edges = lax.optimization_barrier((on_a, off_b, row_halo([hidden])))
+    fwd_a, fwd_b = shift(on_a, "y", on), shift(off_b, "y", off)
+    total = grad_strip(0, wide, (delta_a, delta_b), None, False)
+    total = grad_strip(off, wide, (on_a, on_b), total, False)
+    total = grad_strip(on, wide, (off_a, off_b), total, False)
+    features, near, far = second_tile(hidden, edges, weight_second, cotangent, chips)
+    far, fwd_a, fwd_b, total = lax.optimization_barrier((far, fwd_a, fwd_b, total))
     keep, *sends = fold(near, shift(far, "c", 1))
     for step, send in zip(STEPS[1:], sends):
         keep = keep + shift(send, "y", step).astype(F32)
@@ -536,10 +548,7 @@
     second = jnp.transpose(second, (1, 0, 2, 3)).reshape(sx, sz, -1, outs)
     second = jnp.transpose(second, (1, 0, 2, 3)).reshape(sx * sz, -1, outs)
     extra = second.shape[1]
-
-    step, piece = pieces[2]
-    total = grad_strip(chips - step, wide, piece, total, True)
-    first_own, first_far = total
+    first_own, first_far = grad_strip(2, wide, (fwd_a, fwd_b), total, True)
 
     joined = join(first_own, shift(first_far, "c", 1), second)
     summed = lax.all_to_all(joined, SKY, 0, 0, tiled=True)

time: 152 us -> 146 us (0.961)
  waiting for transfers between devices: 48.4 us -> 26.7 us
  starting transfers between devices: 52.5 us -> 64.8 us
  blocking collectives: 22 us -> 25.5 us
    ppermute x24 -> x30, waiting for transfers between devices: 40 us -> 25.7 us  [shift(): lax.ppermute(x, axis, [(i, (i + step) % count) for i in range(count)])]
    ppermute x24 -> x30, starting transfers between devices: 31 us -> 44.1 us  [shift(): lax.ppermute(x, axis, [(i, (i + step) % count) for i in range(count)])]
    ppermute x4, waiting for transfers between devices: 4.54 us -> 0.01 us  [halo(): return (lax.ppermute(last, axes, up), lax.ppermute(first, axes, down))]
    all_to_all x1, blocking collectives: 22 us -> 25.5 us  [body(): summed = lax.all_to_all(joined, SKY, 0, 0, tiled=True)]
    ppermute x2, waiting for transfers between devices: 3.88 us -> 0.95 us  [row_halo(): lax.ppermute(ends[1], SKY, down)]
  transfers between devices with their start and end apart: 32 -> 38, of which waited for: 17 -> 13; matrix products, arithmetic and copies ran while one was open for 3% -> 3% of each run, Pallas kernels for 11% -> 14%
where the time goes in v5:
time: 146 us
  starting transfers between devices  64.8 us (44%)
  waiting for transfers between devices  26.7 us (18%)
  blocking collectives  25.5 us (17%)
  Pallas kernels  23.4 us (16%)
  local copies, waits for them, and re-layouts  2.92 us (2%)
  other arithmetic  1.49 us (1%)
    ppermute x30, starting transfers between devices, shift(): lax.ppermute(x, axis, [(i, (i + step) % count) for i in range(count)])  44.1 us
    ppermute x30, waiting for transfers between devices, shift(): lax.ppermute(x, axis, [(i, (i + step) % count) for i in range(count)])  25.7 us
    all_to_all x1, blocking collectives, body(): summed = lax.all_to_all(joined, SKY, 0, 0, tiled=True)  25.5 us
    ppermute x4, starting transfers between devices, halo(): return (lax.ppermute(last, axes, up), lax.ppermute(first, axes, down))  10.2 us
    ppermute x2, starting transfers between devices, row_halo(): lax.ppermute(ends[0], SKY, up)  7.92 us
    pallas_call x4, Pallas kernels, grad_strip(): pl.pallas_call(functools.partial(grad_kernel, step, old is not None, last...  7 us
    pallas_call x4, Pallas kernels, conv_parts(): pl.pallas_call(functools.partial(conv_kernel, parts, len(adds)), out_shap...  5.84 us
    pallas_call x1, Pallas kernels, second_tile(): pl.pallas_call(functools.partial(second_kernel, chips), out_shape=(jax.Sh...  3.53 us
  transfers between devices with their start and end apart: 38, of which 13 were waited for; matrix products, arithmetic and copies ran while one was open for 3% of the time, Pallas kernels for 14%

profile of v5, /device:TPU:1, one launch (start us, length us, event | category | flops | bytes accessed | tf_op | source)
XLA Modules:
  0.0 145.9 jit_solution(7209683354834647637)
XLA Ops:
  3.7 3.2 %collective-permute-start.1 = (bf16[256,1,128]{2,0,1:T(8,128)(2,1)S(1)}, bf16[256,1,128]{2,0,1:T(8,128)(2,1)S(1)}, u32[]{:S(2)}, u32[]{:S(2)}) collective-permute-start(bf16[256,1,128]{2,0,1:T(8,128)(2,1)S(1)} %copy.21), channel_id=1, source_target_pairs={{0,1},{1,2},{2,3},{3,4},{4,5},{5,6},{6,7},{7,8},{8,9},{9,10},{10,1... | collective-permute-start | bytes 196616 | tf_op jit(solution)/shard_map/ppermute | solution.py:28
  8.9 3.8 %collective-permute-start.6 = (bf16[1,32,256]{2,1,0:T(8,128)(2,1)S(1)}, bf16[1,32,256]{2,1,0:T(8,128)(2,1)S(1)}, u32[]{:S(2)}, u32[]{:S(2)}) collective-permute-start(bf16[1,32,256]{2,1,0:T(8,128)(2,1)S(1)} %get-tuple-element.76), channel_id=1, source_target_pairs={{0,16},{16,32},{32,48},{48,64},{64,80},{80,96},{96,112},{1,17},{17... | collective-permute-start | bytes 49160 | tf_op jit(solution)/shard_map/ppermute | solution.py:28
  12.8 1.9 %collective-permute-start.7 = (bf16[1,32,256]{2,1,0:T(8,128)(2,1)S(1)}, bf16[1,32,256]{2,1,0:T(8,128)(2,1)S(1)}, u32[]{:S(2)}, u32[]{:S(2)}) collective-permute-start(bf16[1,32,256]{2,1,0:T(8,128)(2,1)S(1)} %get-tuple-element.75), channel_id=1, source_target_pairs={{16,0},{32,16},{48,32},{64,48},{80,64},{96,80},{112,96},{17,1},{33... | collective-permute-start | bytes 49160 | tf_op jit(solution)/shard_map/ppermute | solution.py:28
  16.2 1.9 %spread.1.wide_ref = bf16[4,40,32,768]{3,2,1,0:T(8,128)(2,1)S(1)} custom-call(bf16[256,32,128]{2,1,0:T(8,128)(2,1)S(1)} %copy-done.2, bf16[256,32,128]{2,1,0:T(8,128)(2,1)S(1)} %collective-permute-done.far_ref, bf16[2,256,128]{2,1,0:T(8,128)(2,1)S(1)} %maximum_bitcast_fusion.own_halo_ref, bf16[2,256,128]{2,1,0:T(8,128)(2,1)S(1)} %collective-permute-done.3.far_halo_ref), custom_call_target="tpu_custom_call" | custom-call | flops 1 | bytes 1 | tf_op jit(solution)/shard_map/spread/pallas_call | solution.py:103
  19.5 1.8 %collective-permute-start.5 = (bf16[17,32,256]{2,1,0:T(8,128)(2,1)S(1)}, bf16[17,32,256]{2,1,0:T(8,128)(2,1)S(1)}, u32[]{:S(2)}, u32[]{:S(2)}) collective-permute-start(bf16[17,32,256]{2,1,0:T(8,128)(2,1)S(1)} %get-tuple-element.36), channel_id=1, source_target_pairs={{0,32},{32,64},{64,96},{96,0},{1,33},{33,65},{65,97},{97,1},{2,34}... | collective-permute-start | bytes 835592 | tf_op jit(solution)/shard_map/ppermute | solution.py:19
  24.6 4.3 %collective-permute-start.8 = (bf16[34,256]{1,0:T(8,128)(2,1)S(1)}, bf16[34,256]{1,0:T(8,128)(2,1)S(1)}, u32[]{:S(2)}, u32[]{:S(2)}) collective-permute-start(bf16[34,256]{1,0:T(8,128)(2,1)S(1)} %pad_maximum_fusion.5), channel_id=1, source_target_pairs={{0,1},{1,2},{2,3},{3,4},{4,5},{5,6},{6,7},{7,8},{8,9},{9,10},{10,1... | collective-permute-start | bytes 52232 | tf_op jit(solution)/shard_map/ppermute | solution.py:381
  30.3 2.7 %collective-permute-start.12 = (bf16[17,32,256]{2,1,0:T(8,128)(2,1)S(1)}, bf16[17,32,256]{2,1,0:T(8,128)(2,1)S(1)}, u32[]{:S(2)}, u32[]{:S(2)}) collective-permute-start(bf16[17,32,256]{2,1,0:T(8,128)(2,1)S(1)} %get-tuple-element.47), channel_id=1, source_target_pairs={{0,96},{32,0},{64,32},{96,64},{1,97},{33,1},{65,33},{97,65},{2,98}... | collective-permute-start | bytes 835592 | tf_op jit(solution)/shard_map/ppermute | solution.py:19
  35.1 2.7 %collective-permute-start.14 = (bf16[17,32,256]{2,1,0:T(8,128)(2,1)S(1)}, bf16[17,32,256]{2,1,0:T(8,128)(2,1)S(1)}, u32[]{:S(2)}, u32[]{:S(2)}) collective-permute-start(bf16[17,32,256]{2,1,0:T(8,128)(2,1)S(1)} %get-tuple-element.48), channel_id=1, source_target_pairs={{0,96},{32,0},{64,32},{96,64},{1,97},{33,1},{65,33},{97,65},{2,98}... | collective-permute-start | bytes 835592 | tf_op jit(solution)/shard_map/ppermute | solution.py:19
  40.6 4.3 %collective-permute-done.11.a0_ref = bf16[17,32,256]{2,1,0:T(8,128)(2,1)S(1)} collective-permute-done((bf16[17,32,256]{2,1,0:T(8,128)(2,1)S(1)}, bf16[17,32,256]{2,1,0:T(8,128)(2,1)S(1)}, u32[]{:S(2)}, u32[]{:S(2)}) %collective-permute-start.11) | collective-permute-done | bytes 278560 | tf_op jit(solution)/shard_map/ppermute | solution.py:19
  46.0 2.7 %collective-permute-start.16 = (bf16[16,32,256]{2,1,0:T(8,128)(2,1)S(1)}, bf16[16,32,256]{2,1,0:T(8,128)(2,1)S(1)}, u32[]{:S(2)}, u32[]{:S(2)}) collective-permute-start(bf16[16,32,256]{2,1,0:T(8,128)(2,1)S(1)} %get-tuple-element.52.b_ref), channel_id=1, source_target_pairs={{0,96},{32,0},{64,32},{96,64},{1,97},{33,1},{65,33},{97,65},{2,98}... | collective-permute-start | bytes 786440 | tf_op jit(solution)/shard_map/ppermute | solution.py:19
  48.7 3.7 %collective-permute-start.17 = (bf16[34,256]{1,0:T(8,128)(2,1)S(1)}, bf16[34,256]{1,0:T(8,128)(2,1)S(1)}, u32[]{:S(2)}, u32[]{:S(2)}) collective-permute-start(bf16[34,256]{1,0:T(8,128)(2,1)S(1)} %get-tuple-element.71), channel_id=1, source_target_pairs={{0,1},{1,2},{2,3},{3,4},{4,5},{5,6},{6,7},{7,8},{8,9},{9,10},{10,1... | collective-permute-start | bytes 52232 | tf_op jit(solution)/shard_map/ppermute | solution.py:381
  53.7 2.7 %collective-permute-start.21 = (bf16[16,32,256]{2,1,0:T(8,128)(2,1)S(1)}, bf16[16,32,256]{2,1,0:T(8,128)(2,1)S(1)}, u32[]{:S(2)}, u32[]{:S(2)}) collective-permute-start(bf16[16,32,256]{2,1,0:T(8,128)(2,1)S(1)} %get-tuple-element.51.a_ref), channel_id=1, source_target_pairs={{0,96},{32,0},{64,32},{96,64},{1,97},{33,1},{65,33},{97,65},{2,98}... | collective-permute-start | bytes 786440 | tf_op jit(solution)/shard_map/ppermute | solution.py:19
  57.0 2.7 %collective-permute-start.20 = (bf16[16,32,256]{2,1,0:T(8,128)(2,1)S(1)}, bf16[16,32,256]{2,1,0:T(8,128)(2,1)S(1)}, u32[]{:S(2)}, u32[]{:S(2)}) collective-permute-start(bf16[16,32,256]{2,1,0:T(8,128)(2,1)S(1)} %collective-permute-done.16.b_ref), channel_id=1, source_target_pairs={{0,96},{32,0},{64,32},{96,64},{1,97},{33,1},{65,33},{97,65},{2,98}... | collective-permute-start | bytes 786440 | tf_op jit(solution)/shard_map/ppermute | solution.py:19
  59.6 1.7 %grad_first.4.refs_0_ = f32[768,768]{1,0:T(8,128)S(1)} custom-call(bf16[4,40,32,768]{3,2,1,0:T(8,128)(2,1)S(1)} %spread.1.wide_ref, bf16[16,32,256]{2,1,0:T(8,128)(2,1)S(1)} %get-tuple-element.51.a_ref, bf16[16,32,256]{2,1,0:T(8,128)(2,1)S(1)} %get-tuple-element.52.b_ref), custom_call_target="tpu_custom_call" | custom-call | flops 1 | bytes 1 | tf_op jit(solution)/shard_map/grad_first/pallas_call | solution.py:184
  61.4 3.5 %second.1 = (bf16[32,32,256]{2,1,0:T(8,128)(2,1)}, f32[4,288,256]{2,1,0:T(8,128)S(1)}, bf16[4,288,256]{2,1,0:T(8,128)(2,1)S(1)}) custom-call(bf16[34,32,256]{2,1,0:T(8,128)(2,1)S(1)} %get-tuple-element.50.hid_ref, bf16[2,34,256]{2,1,0:T(8,128)(2,1)S(1)} %pad_maximum_fusion.4.edge_ref, bf16[2304,256]{1,0:T(8,128)(2,1)S(1)} %bitcast.49, ...), custom_call_target="tpu_custom_call" | custom-call | flops 1 | bytes 1 | tf_op jit(solution)/shard_map/second/pallas_call | solution.py:290
  64.9 1.8 %grad_first.5.refs_0_ = f32[768,768]{1,0:T(8,128)S(1)} custom-call(bf16[4,40,32,768]{3,2,1,0:T(8,128)(2,1)S(1)} %spread.1.wide_ref, bf16[16,32,256]{2,1,0:T(8,128)(2,1)S(1)} %collective-permute-done.15.a_ref, bf16[16,32,256]{2,1,0:T(8,128)(2,1)S(1)} %collective-permute-done.22.b_ref, f32[768,768]{1,0:T(8,128)S(1)} %grad_first.4.refs_0_), custom_call_target="tpu_custom_call" | custom-call | flops 1 | bytes 1 | tf_op jit(solution)/shard_map/grad_first/pallas_call | solution.py:184
  66.7 1.8 %grad_first.6.refs_0_ = f32[768,768]{1,0:T(8,128)S(1)} custom-call(bf16[4,40,32,768]{3,2,1,0:T(8,128)(2,1)S(1)} %spread.1.wide_ref, bf16[16,32,256]{2,1,0:T(8,128)(2,1)S(1)} %collective-permute-done.21.a_ref, bf16[16,32,256]{2,1,0:T(8,128)(2,1)S(1)} %collective-permute-done.16.b_ref, f32[768,768]{1,0:T(8,128)S(1)} %grad_first.5.refs_0_), custom_call_target="tpu_custom_call" | custom-call | flops 1 | bytes 1 | tf_op jit(solution)/shard_map/grad_first/pallas_call | solution.py:184
  68.5 4.5 %collective-permute-start.24 = (bf16[4,288,256]{2,1,0:T(8,128)(2,1)S(1)}, bf16[4,288,256]{2,1,0:T(8,128)(2,1)S(1)}, u32[]{:S(2)}, u32[]{:S(2)}) collective-permute-start(bf16[4,288,256]{2,1,0:T(8,128)(2,1)S(1)} %get-tuple-element.64), channel_id=1, source_target_pairs={{0,16},{16,0},{1,17},{17,1},{2,18},{18,2},{3,19},{19,3},{4,20},{20... | collective-permute-start | bytes 1769480 | tf_op jit(solution)/shard_map/ppermute | solution.py:19
  73.0 1.7 %grad_first.7 = (f32[384,768]{1,0:T(8,128)S(1)}, bf16[384,768]{1,0:T(8,128)(2,1)S(1)}) custom-call(bf16[4,40,32,768]{3,2,1,0:T(8,128)(2,1)S(1)} %spread.1.wide_ref, bf16[16,32,256]{2,1,0:T(8,128)(2,1)S(1)} %collective-permute-done.19.a_ref, bf16[16,32,256]{2,1,0:T(8,128)(2,1)S(1)} %collective-permute-done.20.b_ref, f32[768,768]{1,0:T(8,128)S(1)} %grad_first.6.refs_0_), custom_call_target="tpu_custom_call" | custom-call | flops 1 | bytes 1 | tf_op jit(solution)/shard_map/grad_first/pallas_call | solution.py:184
  75.1 2.7 %collective-permute-start.26 = (bf16[288,256]{1,0:T(8,128)(2,1)S(1)}, bf16[288,256]{1,0:T(8,128)(2,1)S(1)}, u32[]{:S(2)}, u32[]{:S(2)}) collective-permute-start(bf16[288,256]{1,0:T(8,128)(2,1)S(1)} %get-tuple-element.67), channel_id=1, source_target_pairs={{0,96},{32,0},{64,32},{96,64},{1,97},{33,1},{65,33},{97,65},{2,98}... | collective-permute-start | bytes 442376 | tf_op jit(solution)/shard_map/ppermute | solution.py:19
  77.8 3.5 %collective-permute-done.25 = bf16[288,256]{1,0:T(8,128)(2,1)S(1)} collective-permute-done((bf16[288,256]{1,0:T(8,128)(2,1)S(1)}, bf16[288,256]{1,0:T(8,128)(2,1)S(1)}, u32[]{:S(2)}, u32[]{:S(2)}) %collective-permute-start.25) | collective-permute-done | bytes 147488 | tf_op jit(solution)/shard_map/ppermute | solution.py:19
  81.3 2.4 %collective-permute-done.27 = bf16[288,256]{1,0:T(8,128)(2,1)S(1)} collective-permute-done((bf16[288,256]{1,0:T(8,128)(2,1)S(1)}, bf16[288,256]{1,0:T(8,128)(2,1)S(1)}, u32[]{:S(2)}, u32[]{:S(2)}) %collective-permute-start.27) | collective-permute-done | bytes 147488 | tf_op jit(solution)/shard_map/ppermute | solution.py:19
  84.0 25.5 %all_to_all.5 = bf16[16,90,256]{2,1,0:T(8,128)(2,1)S(1)} all-to-all(bf16[16,90,256]{2,1,0:T(8,128)(2,1)S(1)} %join.1), channel_id=1, replica_groups=mesh['y'=4,'c'=2,'z'=4,'x'=4] {'z','x'}, dimensions={0} | all-to-all | bytes 1474560 | tf_op jit(solution)/shard_map/all_to_all | solution.py:554
  109.6 2.7 %collective-permute-start.29 = (bf16[90,256]{1,0:T(8,128)(2,1)S(1)}, bf16[90,256]{1,0:T(8,128)(2,1)S(1)}, u32[]{:S(2)}, u32[]{:S(2)}) collective-permute-start(bf16[90,256]{1,0:T(8,128)(2,1)S(1)} %reduce_sum.12.a_ref), channel_id=1, source_target_pairs={{0,12},{4,0},{8,4},{12,8},{1,13},{5,1},{9,5},{13,9},{2,14},{6,2},{... | collective-permute-start | bytes 138248 | tf_op jit(solution)/shard_map/ppermute | solution.py:19
  113.8 3.3 %collective-permute-done.30.d_ref = bf16[90,256]{1,0:T(8,128)(2,1)S(1)} collective-permute-done((bf16[90,256]{1,0:T(8,128)(2,1)S(1)}, bf16[90,256]{1,0:T(8,128)(2,1)S(1)}, u32[]{:S(2)}, u32[]{:S(2)}) %collective-permute-start.30) | collective-permute-done | bytes 46112 | tf_op jit(solution)/shard_map/ppermute | solution.py:19
  117.5 2.8 %collective-permute-start.32 = (bf16[360,256]{1,0:T(8,128)(2,1)S(1)}, bf16[360,256]{1,0:T(8,128)(2,1)S(1)}, u32[]{:S(2)}, u32[]{:S(2)}) collective-permute-start(bf16[360,256]{1,0:T(8,128)(2,1)S(1)} %order_pieces.1.a_ref), channel_id=1, source_target_pairs={{0,3},{1,0},{2,1},{3,2},{4,7},{5,4},{6,5},{7,6},{8,11},{9,8},{10,9... | collective-permute-start | bytes 552968 | tf_op jit(solution)/shard_map/ppermute | solution.py:19
  120.2 3.1 %collective-permute-done.33.d_ref = bf16[360,256]{1,0:T(8,128)(2,1)S(1)} collective-permute-done((bf16[360,256]{1,0:T(8,128)(2,1)S(1)}, bf16[360,256]{1,0:T(8,128)(2,1)S(1)}, u32[]{:S(2)}, u32[]{:S(2)}) %collective-permute-start.33) | collective-permute-done | bytes 184352 | tf_op jit(solution)/shard_map/ppermute | solution.py:19
  123.4 2.5 %collective-permute-done.31.b_ref = bf16[360,256]{1,0:T(8,128)(2,1)S(1)} collective-permute-done((bf16[360,256]{1,0:T(8,128)(2,1)S(1)}, bf16[360,256]{1,0:T(8,128)(2,1)S(1)}, u32[]{:S(2)}, u32[]{:S(2)}) %collective-permute-start.31) | collective-permute-done | bytes 184352 | tf_op jit(solution)/shard_map/ppermute | solution.py:19
  125.9 1.8 %collective-permute-start.34 = (bf16[4,72,256]{2,1,0:T(8,128)(2,1)S(1)}, bf16[4,72,256]{2,1,0:T(8,128)(2,1)S(1)}, u32[]{:S(2)}, u32[]{:S(2)}) collective-permute-start(bf16[4,72,256]{2,1,0:T(8,128)(2,1)S(1)} %get-tuple-element.78), channel_id=1, source_target_pairs={{0,32},{32,64},{64,96},{96,0},{1,33},{33,65},{65,97},{97,1},{2,34}... | collective-permute-start | bytes 442376 | tf_op jit(solution)/shard_map/ppermute | solution.py:19
  131.7 3.0 %collective-permute-done.36 = bf16[4,72,256]{2,1,0:T(8,128)(2,1)S(1)} collective-permute-done((bf16[4,72,256]{2,1,0:T(8,128)(2,1)S(1)}, bf16[4,72,256]{2,1,0:T(8,128)(2,1)S(1)}, u32[]{:S(2)}, u32[]{:S(2)}) %collective-permute-start.36) | collective-permute-done | bytes 147488 | tf_op jit(solution)/shard_map/ppermute | solution.py:19
  134.8 7.8 %collective-permute-start.37 = (bf16[4,4,72,256]{3,2,1,0:T(8,128)(2,1)S(1)}, bf16[4,4,72,256]{3,2,1,0:T(8,128)(2,1)S(1)}, u32[]{:S(2)}, u32[]{:S(2)}) collective-permute-start(bf16[4,4,72,256]{3,2,1,0:T(8,128)(2,1)S(1)} %pad_maximum_fusion.1.near_ref), channel_id=1, source_target_pairs={{0,16},{16,0},{1,17},{17,1},{2,18},{18,2},{3,19},{19,3},{4,20},{20... | collective-permute-start | bytes 1769480 | tf_op jit(solution)/shard_map/ppermute | solution.py:19
  144.2 1.7 %lay_second.1 = f32[2304,256]{1,0:T(8,128)} custom-call(bf16[4,4,72,256]{3,2,1,0:T(8,128)(2,1)S(1)} %pad_maximum_fusion.1.near_ref, bf16[4,4,72,256]{3,2,1,0:T(8,128)(2,1)S(1)} %collective-permute-done.37.far_ref), custom_call_target="tpu_custom_call" | custom-call | flops 1 | bytes 1 | tf_op jit(solution)/shard_map/lay_second/pallas_call | solution.py:488
  (93 shorter events, 29.0 us)
Async XLA Ops:
  0.6 15.5 %collective-permute-start = (bf16[256,32,128]{2,1,0:T(8,128)(2,1)}, bf16[256,32,128]{2,1,0:T(8,128)(2,1)S(1)}, u32[]{:S(2)}, u32[]{:S(2)}) collective-permute-start(bf16[256,32,128]{2,1,0:T(8,128)(2,1)} %own_ref.1), channel_id=1, source_target_pairs={{0,16},{16,0},{1,17},{17,1},{2,18},{18,2},{3,19},{19,3},{4,20},{20... | collective-permute-start | bytes 6291464 | tf_op jit(solution)/shard_map/ppermute | solution.py:19
  2.1 12.7 %collective-permute-start.4 = (bf16[3,3,128,256]{3,2,1,0:T(8,128)(2,1)}, bf16[3,3,128,256]{3,2,1,0:T(8,128)(2,1)S(1)}, u32[]{:S(2)}, u32[]{:S(2)}) collective-permute-start(bf16[3,3,128,256]{3,2,1,0:T(8,128)(2,1)} %param.5), channel_id=1, source_target_pairs={{0,16},{16,0},{1,17},{17,1},{2,18},{18,2},{3,19},{19,3},{4,20},{20... | collective-permute-start | bytes 1769480 | tf_op jit(solution)/shard_map/ppermute | solution.py:19
  3.7 9.1 %collective-permute-start.1 = (bf16[256,1,128]{2,0,1:T(8,128)(2,1)S(1)}, bf16[256,1,128]{2,0,1:T(8,128)(2,1)S(1)}, u32[]{:S(2)}, u32[]{:S(2)}) collective-permute-start(bf16[256,1,128]{2,0,1:T(8,128)(2,1)S(1)} %copy.21), channel_id=1, source_target_pairs={{0,1},{1,2},{2,3},{3,4},{4,5},{5,6},{6,7},{7,8},{8,9},{9,10},{10,1... | collective-permute-start | bytes 196616 | tf_op jit(solution)/shard_map/ppermute | solution.py:28
  6.9 7.8 %collective-permute-start.2 = (bf16[256,1,128]{2,0,1:T(8,128)(2,1)S(1)}, bf16[256,1,128]{2,0,1:T(8,128)(2,1)S(1)}, u32[]{:S(2)}, u32[]{:S(2)}) collective-permute-start(bf16[256,1,128]{2,0,1:T(8,128)(2,1)S(1)} %copy.22), channel_id=1, source_target_pairs={{1,0},{2,1},{3,2},{4,3},{5,4},{6,5},{7,6},{8,7},{9,8},{10,9},{11,1... | collective-permute-start | bytes 196616 | tf_op jit(solution)/shard_map/ppermute | solution.py:28
  8.9 12.4 %collective-permute-start.6 = (bf16[1,32,256]{2,1,0:T(8,128)(2,1)S(1)}, bf16[1,32,256]{2,1,0:T(8,128)(2,1)S(1)}, u32[]{:S(2)}, u32[]{:S(2)}) collective-permute-start(bf16[1,32,256]{2,1,0:T(8,128)(2,1)S(1)} %get-tuple-element.76), channel_id=1, source_target_pairs={{0,16},{16,32},{32,48},{48,64},{64,80},{80,96},{96,112},{1,17},{17... | collective-permute-start | bytes 49160 | tf_op jit(solution)/shard_map/ppermute | solution.py:28
  12.8 8.5 %collective-permute-start.7 = (bf16[1,32,256]{2,1,0:T(8,128)(2,1)S(1)}, bf16[1,32,256]{2,1,0:T(8,128)(2,1)S(1)}, u32[]{:S(2)}, u32[]{:S(2)}) collective-permute-start(bf16[1,32,256]{2,1,0:T(8,128)(2,1)S(1)} %get-tuple-element.75), channel_id=1, source_target_pairs={{16,0},{32,16},{48,32},{64,48},{80,64},{96,80},{112,96},{17,1},{33... | collective-permute-start | bytes 49160 | tf_op jit(solution)/shard_map/ppermute | solution.py:28
  19.5 13.9 %collective-permute-start.5 = (bf16[17,32,256]{2,1,0:T(8,128)(2,1)S(1)}, bf16[17,32,256]{2,1,0:T(8,128)(2,1)S(1)}, u32[]{:S(2)}, u32[]{:S(2)}) collective-permute-start(bf16[17,32,256]{2,1,0:T(8,128)(2,1)S(1)} %get-tuple-element.36), channel_id=1, source_target_pairs={{0,32},{32,64},{64,96},{96,0},{1,33},{33,65},{65,97},{97,1},{2,34}... | collective-permute-start | bytes 835592 | tf_op jit(solution)/shard_map/ppermute | solution.py:19
  23.1 10.4 %collective-permute-start.10 = (bf16[17,32,256]{2,1,0:T(8,128)(2,1)S(1)}, bf16[17,32,256]{2,1,0:T(8,128)(2,1)S(1)}, u32[]{:S(2)}, u32[]{:S(2)}) collective-permute-start(bf16[17,32,256]{2,1,0:T(8,128)(2,1)S(1)} %get-tuple-element.45), channel_id=1, source_target_pairs={{0,96},{32,0},{64,32},{96,64},{1,97},{33,1},{65,33},{97,65},{2,98}... | collective-permute-start | bytes 835592 | tf_op jit(solution)/shard_map/ppermute | solution.py:19
  24.6 5.7 %collective-permute-start.8 = (bf16[34,256]{1,0:T(8,128)(2,1)S(1)}, bf16[34,256]{1,0:T(8,128)(2,1)S(1)}, u32[]{:S(2)}, u32[]{:S(2)}) collective-permute-start(bf16[34,256]{1,0:T(8,128)(2,1)S(1)} %pad_maximum_fusion.5), channel_id=1, source_target_pairs={{0,1},{1,2},{2,3},{3,4},{4,5},{5,6},{6,7},{7,8},{8,9},{9,10},{10,1... | collective-permute-start | bytes 52232 | tf_op jit(solution)/shard_map/ppermute | solution.py:381
  30.2 10.4 %collective-permute-start.13 = (bf16[17,32,256]{2,1,0:T(8,128)(2,1)S(1)}, bf16[17,32,256]{2,1,0:T(8,128)(2,1)S(1)}, u32[]{:S(2)}, u32[]{:S(2)}) collective-permute-start(bf16[17,32,256]{2,1,0:T(8,128)(2,1)S(1)} %get-tuple-element.40), channel_id=1, source_target_pairs={{0,32},{32,64},{64,96},{96,0},{1,33},{33,65},{65,97},{97,1},{2,34}... | collective-permute-start | bytes 835592 | tf_op jit(solution)/shard_map/ppermute | solution.py:19
  30.3 10.3 %collective-permute-start.12 = (bf16[17,32,256]{2,1,0:T(8,128)(2,1)S(1)}, bf16[17,32,256]{2,1,0:T(8,128)(2,1)S(1)}, u32[]{:S(2)}, u32[]{:S(2)}) collective-permute-start(bf16[17,32,256]{2,1,0:T(8,128)(2,1)S(1)} %get-tuple-element.47), channel_id=1, source_target_pairs={{0,96},{32,0},{64,32},{96,64},{1,97},{33,1},{65,33},{97,65},{2,98}... | collective-permute-start | bytes 835592 | tf_op jit(solution)/shard_map/ppermute | solution.py:19
  35.0 10.0 %collective-permute-start.11 = (bf16[17,32,256]{2,1,0:T(8,128)(2,1)S(1)}, bf16[17,32,256]{2,1,0:T(8,128)(2,1)S(1)}, u32[]{:S(2)}, u32[]{:S(2)}) collective-permute-start(bf16[17,32,256]{2,1,0:T(8,128)(2,1)S(1)} %get-tuple-element.46), channel_id=1, source_target_pairs={{0,32},{32,64},{64,96},{96,0},{1,33},{33,65},{65,97},{97,1},{2,34}... | collective-permute-start | bytes 835592 | tf_op jit(solution)/shard_map/ppermute | solution.py:19
  35.1 9.9 %collective-permute-start.14 = (bf16[17,32,256]{2,1,0:T(8,128)(2,1)S(1)}, bf16[17,32,256]{2,1,0:T(8,128)(2,1)S(1)}, u32[]{:S(2)}, u32[]{:S(2)}) collective-permute-start(bf16[17,32,256]{2,1,0:T(8,128)(2,1)S(1)} %get-tuple-element.48), channel_id=1, source_target_pairs={{0,96},{32,0},{64,32},{96,64},{1,97},{33,1},{65,33},{97,65},{2,98}... | collective-permute-start | bytes 835592 | tf_op jit(solution)/shard_map/ppermute | solution.py:19
  45.9 11.0 %collective-permute-start.15 = (bf16[16,32,256]{2,1,0:T(8,128)(2,1)S(1)}, bf16[16,32,256]{2,1,0:T(8,128)(2,1)S(1)}, u32[]{:S(2)}, u32[]{:S(2)}) collective-permute-start(bf16[16,32,256]{2,1,0:T(8,128)(2,1)S(1)} %get-tuple-element.51.a_ref), channel_id=1, source_target_pairs={{0,32},{32,64},{64,96},{96,0},{1,33},{33,65},{65,97},{97,1},{2,34}... | collective-permute-start | bytes 786440 | tf_op jit(solution)/shard_map/ppermute | solution.py:19
  46.0 10.9 %collective-permute-start.16 = (bf16[16,32,256]{2,1,0:T(8,128)(2,1)S(1)}, bf16[16,32,256]{2,1,0:T(8,128)(2,1)S(1)}, u32[]{:S(2)}, u32[]{:S(2)}) collective-permute-start(bf16[16,32,256]{2,1,0:T(8,128)(2,1)S(1)} %get-tuple-element.52.b_ref), channel_id=1, source_target_pairs={{0,96},{32,0},{64,32},{96,64},{1,97},{33,1},{65,33},{97,65},{2,98}... | collective-permute-start | bytes 786440 | tf_op jit(solution)/shard_map/ppermute | solution.py:19
  48.7 5.0 %collective-permute-start.17 = (bf16[34,256]{1,0:T(8,128)(2,1)S(1)}, bf16[34,256]{1,0:T(8,128)(2,1)S(1)}, u32[]{:S(2)}, u32[]{:S(2)}) collective-permute-start(bf16[34,256]{1,0:T(8,128)(2,1)S(1)} %get-tuple-element.71), channel_id=1, source_target_pairs={{0,1},{1,2},{2,3},{3,4},{4,5},{5,6},{6,7},{7,8},{8,9},{9,10},{10,1... | collective-permute-start | bytes 52232 | tf_op jit(solution)/shard_map/ppermute | solution.py:381
  53.6 11.3 %collective-permute-start.22 = (bf16[16,32,256]{2,1,0:T(8,128)(2,1)S(1)}, bf16[16,32,256]{2,1,0:T(8,128)(2,1)S(1)}, u32[]{:S(2)}, u32[]{:S(2)}) collective-permute-start(bf16[16,32,256]{2,1,0:T(8,128)(2,1)S(1)} %get-tuple-element.52.b_ref), channel_id=1, source_target_pairs={{0,32},{32,64},{64,96},{96,0},{1,33},{33,65},{65,97},{97,1},{2,34}... | collective-permute-start | bytes 786440 | tf_op jit(solution)/shard_map/ppermute | solution.py:19
  53.7 12.9 %collective-permute-start.21 = (bf16[16,32,256]{2,1,0:T(8,128)(2,1)S(1)}, bf16[16,32,256]{2,1,0:T(8,128)(2,1)S(1)}, u32[]{:S(2)}, u32[]{:S(2)}) collective-permute-start(bf16[16,32,256]{2,1,0:T(8,128)(2,1)S(1)} %get-tuple-element.51.a_ref), channel_id=1, source_target_pairs={{0,96},{32,0},{64,32},{96,64},{1,97},{33,1},{65,33},{97,65},{2,98}... | collective-permute-start | bytes 786440 | tf_op jit(solution)/shard_map/ppermute | solution.py:19
  56.9 11.6 %collective-permute-start.19 = (bf16[16,32,256]{2,1,0:T(8,128)(2,1)S(1)}, bf16[16,32,256]{2,1,0:T(8,128)(2,1)S(1)}, u32[]{:S(2)}, u32[]{:S(2)}) collective-permute-start(bf16[16,32,256]{2,1,0:T(8,128)(2,1)S(1)} %collective-permute-done.15.a_ref), channel_id=1, source_target_pairs={{0,32},{32,64},{64,96},{96,0},{1,33},{33,65},{65,97},{97,1},{2,34}... | collective-permute-start | bytes 786440 | tf_op jit(solution)/shard_map/ppermute | solution.py:19
  57.0 11.5 %collective-permute-start.20 = (bf16[16,32,256]{2,1,0:T(8,128)(2,1)S(1)}, bf16[16,32,256]{2,1,0:T(8,128)(2,1)S(1)}, u32[]{:S(2)}, u32[]{:S(2)}) collective-permute-start(bf16[16,32,256]{2,1,0:T(8,128)(2,1)S(1)} %collective-permute-done.16.b_ref), channel_id=1, source_target_pairs={{0,96},{32,0},{64,32},{96,64},{1,97},{33,1},{65,33},{97,65},{2,98}... | collective-permute-start | bytes 786440 | tf_op jit(solution)/shard_map/ppermute | solution.py:19
  68.5 6.4 %collective-permute-start.24 = (bf16[4,288,256]{2,1,0:T(8,128)(2,1)S(1)}, bf16[4,288,256]{2,1,0:T(8,128)(2,1)S(1)}, u32[]{:S(2)}, u32[]{:S(2)}) collective-permute-start(bf16[4,288,256]{2,1,0:T(8,128)(2,1)S(1)} %get-tuple-element.64), channel_id=1, source_target_pairs={{0,16},{16,0},{1,17},{17,1},{2,18},{18,2},{3,19},{19,3},{4,20},{20... | collective-permute-start | bytes 1769480 | tf_op jit(solution)/shard_map/ppermute | solution.py:19
  74.8 9.1 %collective-permute-start.23 = (bf16[384,768]{1,0:T(8,128)(2,1)S(1)}, bf16[384,768]{1,0:T(8,128)(2,1)S(1)}, u32[]{:S(2)}, u32[]{:S(2)}) collective-permute-start(bf16[384,768]{1,0:T(8,128)(2,1)S(1)} %get-tuple-element.62), channel_id=1, source_target_pairs={{0,16},{16,0},{1,17},{17,1},{2,18},{18,2},{3,19},{19,3},{4,20},{20... | collective-permute-start | bytes 1769480 | tf_op jit(solution)/shard_map/ppermute | solution.py:19
  75.0 6.2 %collective-permute-start.25 = (bf16[288,256]{1,0:T(8,128)(2,1)S(1)}, bf16[288,256]{1,0:T(8,128)(2,1)S(1)}, u32[]{:S(2)}, u32[]{:S(2)}) collective-permute-start(bf16[288,256]{1,0:T(8,128)(2,1)S(1)} %get-tuple-element.66), channel_id=1, source_target_pairs={{0,32},{32,64},{64,96},{96,0},{1,33},{33,65},{65,97},{97,1},{2,34}... | collective-permute-start | bytes 442376 | tf_op jit(solution)/shard_map/ppermute | solution.py:19
  75.1 6.1 %collective-permute-start.26 = (bf16[288,256]{1,0:T(8,128)(2,1)S(1)}, bf16[288,256]{1,0:T(8,128)(2,1)S(1)}, u32[]{:S(2)}, u32[]{:S(2)}) collective-permute-start(bf16[288,256]{1,0:T(8,128)(2,1)S(1)} %get-tuple-element.67), channel_id=1, source_target_pairs={{0,96},{32,0},{64,32},{96,64},{1,97},{33,1},{65,33},{97,65},{2,98}... | collective-permute-start | bytes 442376 | tf_op jit(solution)/shard_map/ppermute | solution.py:19
  77.8 5.9 %collective-permute-start.27 = (bf16[288,256]{1,0:T(8,128)(2,1)S(1)}, bf16[288,256]{1,0:T(8,128)(2,1)S(1)}, u32[]{:S(2)}, u32[]{:S(2)}) collective-permute-start(bf16[288,256]{1,0:T(8,128)(2,1)S(1)} %get-tuple-element.68), channel_id=1, source_target_pairs={{0,64},{32,96},{64,0},{96,32},{1,65},{33,97},{65,1},{97,33},{2,66}... | collective-permute-start | bytes 442376 | tf_op jit(solution)/shard_map/ppermute | solution.py:19
  112.3 4.8 %collective-permute-start.30 = (bf16[90,256]{1,0:T(8,128)(2,1)S(1)}, bf16[90,256]{1,0:T(8,128)(2,1)S(1)}, u32[]{:S(2)}, u32[]{:S(2)}) collective-permute-start(bf16[90,256]{1,0:T(8,128)(2,1)S(1)} %reduce_sum.12.a_ref), channel_id=1, source_target_pairs={{0,8},{4,12},{8,0},{12,4},{1,9},{5,13},{9,1},{13,5},{2,10},{6,14},... | collective-permute-start | bytes 138248 | tf_op jit(solution)/shard_map/ppermute | solution.py:19
  117.2 6.2 %collective-permute-start.33 = (bf16[360,256]{1,0:T(8,128)(2,1)S(1)}, bf16[360,256]{1,0:T(8,128)(2,1)S(1)}, u32[]{:S(2)}, u32[]{:S(2)}) collective-permute-start(bf16[360,256]{1,0:T(8,128)(2,1)S(1)} %order_pieces.1.a_ref), channel_id=1, source_target_pairs={{0,2},{1,3},{2,0},{3,1},{4,6},{5,7},{6,4},{7,5},{8,10},{9,11},{10,... | collective-permute-start | bytes 552968 | tf_op jit(solution)/shard_map/ppermute | solution.py:19
  117.5 5.9 %collective-permute-start.32 = (bf16[360,256]{1,0:T(8,128)(2,1)S(1)}, bf16[360,256]{1,0:T(8,128)(2,1)S(1)}, u32[]{:S(2)}, u32[]{:S(2)}) collective-permute-start(bf16[360,256]{1,0:T(8,128)(2,1)S(1)} %order_pieces.1.a_ref), channel_id=1, source_target_pairs={{0,3},{1,0},{2,1},{3,2},{4,7},{5,4},{6,5},{7,6},{8,11},{9,8},{10,9... | collective-permute-start | bytes 552968 | tf_op jit(solution)/shard_map/ppermute | solution.py:19
  120.2 5.6 %collective-permute-start.31 = (bf16[360,256]{1,0:T(8,128)(2,1)S(1)}, bf16[360,256]{1,0:T(8,128)(2,1)S(1)}, u32[]{:S(2)}, u32[]{:S(2)}) collective-permute-start(bf16[360,256]{1,0:T(8,128)(2,1)S(1)} %order_pieces.1.a_ref), channel_id=1, source_target_pairs={{0,1},{1,2},{2,3},{3,0},{4,5},{5,6},{6,7},{7,4},{8,9},{9,10},{10,1... | collective-permute-start | bytes 552968 | tf_op jit(solution)/shard_map/ppermute | solution.py:19
  125.9 5.8 %collective-permute-start.34 = (bf16[4,72,256]{2,1,0:T(8,128)(2,1)S(1)}, bf16[4,72,256]{2,1,0:T(8,128)(2,1)S(1)}, u32[]{:S(2)}, u32[]{:S(2)}) collective-permute-start(bf16[4,72,256]{2,1,0:T(8,128)(2,1)S(1)} %get-tuple-element.78), channel_id=1, source_target_pairs={{0,32},{32,64},{64,96},{96,0},{1,33},{33,65},{65,97},{97,1},{2,34}... | collective-permute-start | bytes 442376 | tf_op jit(solution)/shard_map/ppermute | solution.py:19
  129.3 5.5 %collective-permute-start.36 = (bf16[4,72,256]{2,1,0:T(8,128)(2,1)S(1)}, bf16[4,72,256]{2,1,0:T(8,128)(2,1)S(1)}, u32[]{:S(2)}, u32[]{:S(2)}) collective-permute-start(bf16[4,72,256]{2,1,0:T(8,128)(2,1)S(1)} %get-tuple-element.78), channel_id=1, source_target_pairs={{0,64},{32,96},{64,0},{96,32},{1,65},{33,97},{65,1},{97,33},{2,66}... | collective-permute-start | bytes 442376 | tf_op jit(solution)/shard_map/ppermute | solution.py:19
  134.8 9.4 %collective-permute-start.37 = (bf16[4,4,72,256]{3,2,1,0:T(8,128)(2,1)S(1)}, bf16[4,4,72,256]{3,2,1,0:T(8,128)(2,1)S(1)}, u32[]{:S(2)}, u32[]{:S(2)}) collective-permute-start(bf16[4,4,72,256]{3,2,1,0:T(8,128)(2,1)S(1)} %pad_maximum_fusion.1.near_ref), channel_id=1, source_target_pairs={{0,16},{16,0},{1,17},{17,1},{2,18},{18,2},{3,19},{19,3},{4,20},{20... | collective-permute-start | bytes 1769480 | tf_op jit(solution)/shard_map/ppermute | solution.py:19
  (9 other events, 45.8 us)

commit v6 on v5

--- a/solution.py
+++ b/solution.py
@@ -17,15 +17,6 @@
 def shift(x, axis, step):
     count = lax.axis_size(axis)
     return lax.ppermute(x, axis, [(i, (i + step) % count) for i in range(count)])
-
-
-def halo(x, axes, dim):
-    count, length = lax.axis_size(axes), x.shape[dim]
-    up = [(i, i + 1) for i in range(count - 1)]
-    down = [(j, i) for i, j in up]
-    last = lax.slice_in_dim(x, length - 1, length, axis=dim)
-    first = lax.slice_in_dim(x, 0, 1, axis=dim)
-    return lax.ppermute(last, axes, up), lax.ppermute(first, axes, down)
 
 
 def spread_kernel(own_ref, far_ref, own_halo_ref, far_halo_ref, out_ref):
@@ -194,28 +185,33 @@
     return out if last else out[0]
 
 
-def spread_tile(columns, edge_ref, wide_ref):
+def spread_tile(columns, wide_ref):
     rows, chans = wide_ref.shape[1], wide_ref.shape[2] // 3
     place = lax.broadcasted_iota(jnp.int32, (rows, chans), 0)
-
-    def put(mid, j):
+    for j, (mid, before, after) in enumerate(columns):
         wide = mid.astype(F32)
-        before = edge_ref[0, j : j + 1, :].astype(F32)
-        after = edge_ref[1, j : j + 1, :].astype(F32)
-        ahead = jnp.where(place == 0, before, pltpu.roll(wide, 1, 0))
-        behind = jnp.where(place == rows - 1, after, pltpu.roll(wide, rows - 1, 0))
+        ahead = jnp.where(place == 0, before.astype(F32), pltpu.roll(wide, 1, 0))
+        behind = jnp.where(place == rows - 1, after.astype(F32), pltpu.roll(wide, rows - 1, 0))
         wide_ref[j, :, 0:chans] = ahead.astype(BF16)
         wide_ref[j, :, chans : 2 * chans] = mid
         wide_ref[j, :, 2 * chans :] = behind.astype(BF16)
 
-    for j, (ref, at) in enumerate(columns):
-        put(ref[at], j)
-
 
 def back_kernel(cot_ref, left_ref, right_ref, edge_ref, kernel_ref, out_ref, wide_ref):
     cols, rows, chans = cot_ref.shape
-    columns = [(left_ref, 0)] + [(cot_ref, j) for j in range(cols)] + [(right_ref, 0)]
-    spread_tile(columns, edge_ref, wide_ref)
+    start = edge_ref.shape[1] - 2 * cols
+
+    def beside(k, j):
+        low, high = start + j, start + cols + j
+        return jnp.concatenate(
+            [edge_ref[k, low : low + 1, :], edge_ref[k, high : high + 1, :]], axis=-1
+        )
+
+    def whole(ref):
+        return ref[0:rows], ref[rows : rows + 1], ref[rows + 1 : rows + 2]
+
+    columns = [(cot_ref[j], beside(0, j), beside(1, j)) for j in range(cols)]
+    spread_tile([whole(left_ref)] + columns + [whole(right_ref)], wide_ref)
     total = None
     for tap_col in range(3):
         lhs = wide_ref[tap_col : tap_col + cols].reshape(cols * rows, 3 * chans)
@@ -252,7 +248,10 @@
     cols, rows, outs = cot_ref.shape
     width = wide_ref.shape[0]
     core = lax.axis_index("c")
-    spread_tile([(hid_ref, j) for j in range(cols + 2)], edge_ref, wide_ref)
+    columns = [
+        (hid_ref[j], edge_ref[0, j : j + 1, :], edge_ref[1, j : j + 1, :]) for j in range(cols + 2)
+    ]
+    spread_tile(columns, wide_ref)
     wide_ref[cols + 2 :] = jnp.zeros((width - cols - 2, rows, 3 * chans), BF16)
     pieces = [wide_ref[tap : tap + cols] for tap in range(3)]
     lhs = jnp.concatenate(pieces, axis=-1).reshape(cols * rows, 9 * chans)
@@ -372,17 +371,15 @@
     )(near, got)
 
 
-def row_halo(pieces):
-    last = pieces[0].shape[1] - 1
-    ends = [jnp.concatenate([piece[:, r] for piece in pieces], axis=0) for r in (last, 0)]
+def row_halo(ends):
     count = lax.axis_size(SKY)
     up = [(i, i + 1) for i in range(count - 1)]
     down = [(j, i) for i, j in up]
     return jnp.stack([lax.ppermute(ends[0], SKY, up), lax.ppermute(ends[1], SKY, down)])
 
 
-def join_kernel(own_ref, far_ref, second_ref, out_ref):
-    pieces, extra, outs = second_ref.shape
+def join_kernel(own_ref, far_ref, keep_ref, a_ref, b_ref, c_ref, out_ref):
+    pieces, total, outs = out_ref.shape
     chans = own_ref.shape[0] // 3
     size = chans // pieces
     for tap_col in range(3):
@@ -392,21 +389,35 @@
             value = own_ref[rows, lanes] + far_ref[rows, lanes].astype(F32)
             at = (3 * tap_col + tap_row) * size
             out_ref[:, at : at + size, :] = value.reshape(pieces, size, outs).astype(BF16)
-    out_ref[:, 9 * size :, :] = second_ref[...]
-
-
-def join(own, far, second):
-    pieces, extra, outs = second.shape
-    rows = 9 * (own.shape[0] // 3 // pieces) + extra
+    second = keep_ref[...]
+    for ref in (a_ref, b_ref, c_ref):
+        second = second + ref[...].astype(F32)
+    sx = lax.axis_size("x")
+    sz = pieces // sx
+    third = second.shape[0] // 3
+    size_x = third // sx
+    extra = total - 9 * size
+    for x in range(sx):
+        value = jnp.concatenate(
+            [second[tap * third + x * size_x : tap * third + (x + 1) * size_x] for tap in range(3)],
+            axis=0,
+        )
+        for z in range(sz):
+            out_ref[z * sx + x, 9 * size :, :] = value[z * extra : (z + 1) * extra].astype(BF16)
+
+
+def join(own, far, keep, got, pieces):
+    outs = keep.shape[1]
+    rows = 9 * (own.shape[0] // 3 // pieces) + keep.shape[0] // pieces
     return pl.pallas_call(
         join_kernel,
         out_shape=jax.ShapeDtypeStruct((pieces, rows, outs), BF16),
-        in_specs=[VMEM_SPEC] * 3,
+        in_specs=[VMEM_SPEC] * 6,
         out_specs=VMEM_SPEC,
-        compiler_params=pltpu.CompilerParams(vmem_limit_bytes=2 * 2**20),
+        compiler_params=pltpu.CompilerParams(vmem_limit_bytes=4 * 2**20),
         cost_estimate=QUICK,
         name="join",
-    )(own, far, second)
+    )(own, far, keep, *got)
 
 
 STEPS = (0, 1, 3, 2)
@@ -505,52 +516,67 @@
     strip, _, outs = cotangent.shape
     chips = lax.axis_size("y")
 
-    edges = jnp.concatenate(halo(sky_cube, SKY, 1), axis=1)
+    ends = [
+        jnp.concatenate(
+            [sky_cube[:, r], cotangent[:, r, : outs // 2], cotangent[:, r, outs // 2 :]], axis=0
+        )
+        for r in (rows - 1, 0)
+    ]
+    edges = row_halo(ends)
     far_cube = shift(sky_cube, "c", 1)
     far_weight = shift(weight_first, "c", 1)
-    edges = jnp.transpose(edges, (1, 0, 2))
     far_edges = shift(edges, "c", 1)
-    left, right = halo(cotangent, FREQ, 0)
     wide = spread(sky_cube, far_cube, edges, far_edges, chips)
     kernel = jnp.concatenate([weight_first, far_weight], axis=2).reshape(18 * chans, outs)
+
+    def side(col):
+        beside = [
+            jnp.concatenate(
+                [edges[k, at + col : at + col + 1] for at in (cols, cols + strip)], axis=1
+            )
+            for k in range(2)
+        ]
+        return jnp.concatenate([cotangent[col]] + beside, axis=0)
+
+    count = lax.axis_size(FREQ)
+    up = [(i, i + 1) for i in range(count - 1)]
+    down = [(j, i) for i, j in up]
+    left = lax.ppermute(side(strip - 1), FREQ, up)
+    right = lax.ppermute(side(0), FREQ, down)
 
     on, off = 1, chips - 1
     cut = strip // 2 + 1
     far_a, far_b = conv_parts(((2, 0), (2, cut)), wide, kernel, cut, BF16)
-    hold, left, right, _ = lax.optimization_barrier((wide, left, right, far_a))
+    hold, _ = lax.optimization_barrier((wide, far_a))
     near_b, near_a = conv_parts(((on, cut), (off, 0)), hold, kernel, cut, BF16)
     got_a, got_b = shift(far_a, "y", on), shift(far_b, "y", off)
-    late, left, right, _ = lax.optimization_barrier((cotangent, left, right, near_b))
-    edges = row_halo([left, late, right])
-    got_a, edges = lax.optimization_barrier((got_a, edges))
+    got_a, left, right = lax.optimization_barrier((got_a, left, right))
     both_a, both_b = conv_parts(((on, 0), (off, cut)), wide, kernel, cut, BF16, (got_a, got_b))
     own = conv_parts(((0, 0),), wide, kernel, strip + 2, F32)[0]
     from_a = shift(both_a, "y", on), shift(near_a, "y", off)
     from_b = shift(near_b, "y", on), shift(both_b, "y", off)
 
-    back = back_tile(late, left, right, edges, weight_second)
+    back = back_tile(cotangent, left, right, edges, weight_second)
     delta_a, delta_b, hidden = point(own, from_a, from_b, back)
 
     on_a, off_b = shift(delta_a, "y", on), shift(delta_b, "y", off)
     on_b, off_a = shift(delta_b, "y", on), shift(delta_a, "y", off)
-    on_a, off_b, edges = lax.optimization_barrier((on_a, off_b, row_halo([hidden])))
+    on_a, off_b, edges = lax.optimization_barrier(
+        (on_a, off_b, row_halo([hidden[:, rows - 1], hidden[:, 0]]))
+    )
     fwd_a, fwd_b = shift(on_a, "y", on), shift(off_b, "y", off)
     total = grad_strip(0, wide, (delta_a, delta_b), None, False)
+    features, near, far = second_tile(hidden, edges, weight_second, cotangent, chips)
+    far, on_b, off_a = lax.optimization_barrier((far, on_b, off_a))
+    keep, *sends = fold(near, shift(far, "c", 1))
+    got = [shift(send, "y", step) for step, send in zip(STEPS[1:], sends)]
     total = grad_strip(off, wide, (on_a, on_b), total, False)
     total = grad_strip(on, wide, (off_a, off_b), total, False)
-    features, near, far = second_tile(hidden, edges, weight_second, cotangent, chips)
-    far, fwd_a, fwd_b, total = lax.optimization_barrier((far, fwd_a, fwd_b, total))
-    keep, *sends = fold(near, shift(far, "c", 1))
-    for step, send in zip(STEPS[1:], sends):
-        keep = keep + shift(send, "y", step).astype(F32)
+    first_own, first_far = grad_strip(2, wide, (fwd_a, fwd_b), total, True)
+
     sx, sz = lax.axis_size("x"), lax.axis_size("z")
-    second = keep.astype(BF16).reshape(3, sx, -1, outs)
-    second = jnp.transpose(second, (1, 0, 2, 3)).reshape(sx, sz, -1, outs)
-    second = jnp.transpose(second, (1, 0, 2, 3)).reshape(sx * sz, -1, outs)
-    extra = second.shape[1]
-    first_own, first_far = grad_strip(2, wide, (fwd_a, fwd_b), total, True)
-
-    joined = join(first_own, shift(first_far, "c", 1), second)
+    joined = join(first_own, shift(first_far, "c", 1), keep, got, sx * sz)
+    extra = keep.shape[0] // (sx * sz)
     summed = lax.all_to_all(joined, SKY, 0, 0, tiled=True)
     summed = jnp.sum(summed.astype(F32), axis=0).astype(BF16)
     parts = gather_steps(order_pieces(gather_steps(summed, "z"), extra), "x")

time: 146 us -> 145 us (level)
  waiting for transfers between devices: 26.7 us -> 35.7 us
  starting transfers between devices: 64.8 us -> 57.4 us
  blocking collectives: 25.5 us -> 22.3 us
    ppermute x2, waiting for transfers between devices: 0.95 us -> 7.37 us  [row_halo(): lax.ppermute(ends[1], SKY, down)]
    ppermute x4 -> x2, starting transfers between devices: 10.2 us -> 4.41 us  [the longest x1 2.49 us: body(): left = lax.ppermute(side(strip - 1), FREQ, up)]
    all_to_all x1, blocking collectives: 25.5 us -> 22.3 us  [body(): summed = lax.all_to_all(joined, SKY, 0, 0, tiled=True)]
    ppermute x30, waiting for transfers between devices: 25.7 us -> 28.2 us  [shift(): lax.ppermute(x, axis, [(i, (i + step) % count) for i in range(count)])]
    ppermute x2, starting transfers between devices: 7.92 us -> 6.31 us  [row_halo(): lax.ppermute(ends[0], SKY, up)]
  transfers between devices with their start and end apart: 38 -> 36, of which waited for: 13 -> 15; matrix products, arithmetic and copies ran while one was open for 3% -> 3% of each run, Pallas kernels for 14% -> 12%
where the time goes in v6:
time: 145 us
  starting transfers between devices  57.4 us (40%)
  waiting for transfers between devices  35.7 us (25%)
  Pallas kernels  23.5 us (16%)
  blocking collectives  22.3 us (15%)
  local copies, waits for them, and re-layouts  3.55 us (2%)
    ppermute x30, starting transfers between devices, shift(): lax.ppermute(x, axis, [(i, (i + step) % count) for i in range(count)])  44.1 us
    ppermute x30, waiting for transfers between devices, shift(): lax.ppermute(x, axis, [(i, (i + step) % count) for i in range(count)])  28.2 us
    all_to_all x1, blocking collectives, body(): summed = lax.all_to_all(joined, SKY, 0, 0, tiled=True)  22.3 us
    ppermute x2, waiting for transfers between devices, row_halo(): lax.ppermute(ends[1], SKY, down)  7.37 us
    pallas_call x4, Pallas kernels, grad_strip(): pl.pallas_call(functools.partial(grad_kernel, step, old is not None, last...  7 us
    ppermute x2, starting transfers between devices, row_halo(): lax.ppermute(ends[0], SKY, up)  6.31 us
    pallas_call x4, Pallas kernels, conv_parts(): pl.pallas_call(functools.partial(conv_kernel, parts, len(adds)), out_shap...  5.84 us
    pallas_call x1, Pallas kernels, second_tile(): pl.pallas_call(functools.partial(second_kernel, chips), out_shape=(jax.Sh...  3.54 us
  transfers between devices with their start and end apart: 36, of which 15 were waited for; matrix products, arithmetic and copies ran while one was open for 3% of the time, Pallas kernels for 12%

profile of v6, /device:TPU:1, one launch (start us, length us, event | category | flops | bytes accessed | tf_op | source)
XLA Modules:
  0.0 144.9 jit_solution(3602093541964231394)
XLA Ops:
  4.6 3.2 %collective-permute-start.1 = (bf16[320,128]{1,0:T(8,128)(2,1)S(1)}, bf16[320,128]{1,0:T(8,128)(2,1)S(1)}, u32[]{:S(2)}, u32[]{:S(2)}) collective-permute-start(bf16[320,128]{1,0:T(8,128)(2,1)S(1)} %pad_maximum_fusion.4), channel_id=1, source_target_pairs={{0,1},{1,2},{2,3},{3,4},{4,5},{5,6},{6,7},{7,8},{8,9},{9,10},{10,1... | collective-permute-start | bytes 245768 | tf_op jit(solution)/shard_map/ppermute | solution.py:378
  10.4 3.8 %collective-permute-done.2 = bf16[320,128]{1,0:T(8,128)(2,1)S(1)} collective-permute-done((bf16[320,128]{1,0:T(8,128)(2,1)S(1)}, bf16[320,128]{1,0:T(8,128)(2,1)S(1)}, u32[]{:S(2)}, u32[]{:S(2)}) %collective-permute-start.2) | collective-permute-done | bytes 81952 | tf_op jit(solution)/shard_map/ppermute | solution.py:378
  16.4 1.9 %spread.1.wide_ref = bf16[4,40,32,768]{3,2,1,0:T(8,128)(2,1)S(1)} custom-call(bf16[256,32,128]{2,1,0:T(8,128)(2,1)S(1)} %copy-done.1, bf16[256,32,128]{2,1,0:T(8,128)(2,1)S(1)} %collective-permute-done.far_ref, bf16[2,320,128]{2,1,0:T(8,128)(2,1)S(1)} %pad_maximum_fusion.2.own_halo_ref.edge_ref, bf16[2,320,128]{2,1,0:T(8,128)(2,1)S(1)} %collective-permute-done.3.far_halo_ref), custom_call_target="tpu_custom_call" | custom-call | flops 1 | bytes 1 | tf_op jit(solution)/shard_map/spread/pallas_call | solution.py:94
  22.7 2.5 %collective-permute-start.6 = (bf16[34,256]{1,0:T(8,128)(2,1)S(1)}, bf16[34,256]{1,0:T(8,128)(2,1)S(1)}, u32[]{:S(2)}, u32[]{:S(2)}) collective-permute-start(bf16[34,256]{1,0:T(8,128)(2,1)S(1)} %maximum_maximum_fusion), channel_id=1, source_target_pairs={{0,16},{16,32},{32,48},{48,64},{64,80},{80,96},{96,112},{1,17},{17... | collective-permute-start | bytes 52232 | tf_op jit(solution)/shard_map/ppermute | solution.py:544
  25.2 1.9 %collective-permute-start.7 = (bf16[34,256]{1,0:T(8,128)(2,1)S(1)}, bf16[34,256]{1,0:T(8,128)(2,1)S(1)}, u32[]{:S(2)}, u32[]{:S(2)}) collective-permute-start(bf16[34,256]{1,0:T(8,128)(2,1)S(1)} %maximum_maximum_fusion.1), channel_id=1, source_target_pairs={{16,0},{32,16},{48,32},{64,48},{80,64},{96,80},{112,96},{17,1},{33... | collective-permute-start | bytes 52232 | tf_op jit(solution)/shard_map/ppermute | solution.py:545
  28.6 1.6 %collective-permute-start.10 = (bf16[17,32,256]{2,1,0:T(8,128)(2,1)S(1)}, bf16[17,32,256]{2,1,0:T(8,128)(2,1)S(1)}, u32[]{:S(2)}, u32[]{:S(2)}) collective-permute-start(bf16[17,32,256]{2,1,0:T(8,128)(2,1)S(1)} %get-tuple-element.36), channel_id=1, source_target_pairs={{0,96},{32,0},{64,32},{96,64},{1,97},{33,1},{65,33},{97,65},{2,98}... | collective-permute-start | bytes 835592 | tf_op jit(solution)/shard_map/ppermute | solution.py:19
  31.8 2.7 %collective-permute-start.12 = (bf16[17,32,256]{2,1,0:T(8,128)(2,1)S(1)}, bf16[17,32,256]{2,1,0:T(8,128)(2,1)S(1)}, u32[]{:S(2)}, u32[]{:S(2)}) collective-permute-start(bf16[17,32,256]{2,1,0:T(8,128)(2,1)S(1)} %get-tuple-element.38), channel_id=1, source_target_pairs={{0,96},{32,0},{64,32},{96,64},{1,97},{33,1},{65,33},{97,65},{2,98}... | collective-permute-start | bytes 835592 | tf_op jit(solution)/shard_map/ppermute | solution.py:19
  37.6 5.2 %collective-permute-done.12.b1_ref = bf16[17,32,256]{2,1,0:T(8,128)(2,1)S(1)} collective-permute-done((bf16[17,32,256]{2,1,0:T(8,128)(2,1)S(1)}, bf16[17,32,256]{2,1,0:T(8,128)(2,1)S(1)}, u32[]{:S(2)}, u32[]{:S(2)}) %collective-permute-start.12) | collective-permute-done | bytes 278560 | tf_op jit(solution)/shard_map/ppermute | solution.py:19
  45.5 2.7 %collective-permute-start.14 = (bf16[16,32,256]{2,1,0:T(8,128)(2,1)S(1)}, bf16[16,32,256]{2,1,0:T(8,128)(2,1)S(1)}, u32[]{:S(2)}, u32[]{:S(2)}) collective-permute-start(bf16[16,32,256]{2,1,0:T(8,128)(2,1)S(1)} %get-tuple-element.43.b_ref), channel_id=1, source_target_pairs={{0,96},{32,0},{64,32},{96,64},{1,97},{33,1},{65,33},{97,65},{2,98}... | collective-permute-start | bytes 786440 | tf_op jit(solution)/shard_map/ppermute | solution.py:19
  48.1 3.1 %collective-permute-start.15 = (bf16[34,256]{1,0:T(8,128)(2,1)S(1)}, bf16[34,256]{1,0:T(8,128)(2,1)S(1)}, u32[]{:S(2)}, u32[]{:S(2)}) collective-permute-start(bf16[34,256]{1,0:T(8,128)(2,1)S(1)} %get-tuple-element.61), channel_id=1, source_target_pairs={{0,1},{1,2},{2,3},{3,4},{4,5},{5,6},{6,7},{7,8},{8,9},{9,10},{10,1... | collective-permute-start | bytes 52232 | tf_op jit(solution)/shard_map/ppermute | solution.py:378
  51.3 2.7 %collective-permute-start.20 = (bf16[16,32,256]{2,1,0:T(8,128)(2,1)S(1)}, bf16[16,32,256]{2,1,0:T(8,128)(2,1)S(1)}, u32[]{:S(2)}, u32[]{:S(2)}) collective-permute-start(bf16[16,32,256]{2,1,0:T(8,128)(2,1)S(1)} %get-tuple-element.42.a_ref), channel_id=1, source_target_pairs={{0,96},{32,0},{64,32},{96,64},{1,97},{33,1},{65,33},{97,65},{2,98}... | collective-permute-start | bytes 786440 | tf_op jit(solution)/shard_map/ppermute | solution.py:19
  55.3 3.5 %collective-permute-done.16 = bf16[34,256]{1,0:T(8,128)(2,1)S(1)} collective-permute-done((bf16[34,256]{1,0:T(8,128)(2,1)S(1)}, bf16[34,256]{1,0:T(8,128)(2,1)S(1)}, u32[]{:S(2)}, u32[]{:S(2)}) %collective-permute-start.16) | collective-permute-done | bytes 17440 | tf_op jit(solution)/shard_map/ppermute | solution.py:378
  58.9 2.7 %collective-permute-start.18 = (bf16[16,32,256]{2,1,0:T(8,128)(2,1)S(1)}, bf16[16,32,256]{2,1,0:T(8,128)(2,1)S(1)}, u32[]{:S(2)}, u32[]{:S(2)}) collective-permute-start(bf16[16,32,256]{2,1,0:T(8,128)(2,1)S(1)} %collective-permute-done.14.b_ref), channel_id=1, source_target_pairs={{0,96},{32,0},{64,32},{96,64},{1,97},{33,1},{65,33},{97,65},{2,98}... | collective-permute-start | bytes 786440 | tf_op jit(solution)/shard_map/ppermute | solution.py:19
  61.6 3.5 %second.1 = (bf16[32,32,256]{2,1,0:T(8,128)(2,1)}, f32[4,288,256]{2,1,0:T(8,128)S(1)}, bf16[4,288,256]{2,1,0:T(8,128)(2,1)S(1)}) custom-call(bf16[34,32,256]{2,1,0:T(8,128)(2,1)S(1)} %get-tuple-element.41.hid_ref, bf16[2,34,256]{2,1,0:T(8,128)(2,1)S(1)} %pad_maximum_fusion.6.edge_ref, bf16[2304,256]{1,0:T(8,128)(2,1)S(1)} %bitcast.62, ...), custom_call_target="tpu_custom_call" | custom-call | flops 1 | bytes 1 | tf_op jit(solution)/shard_map/second/pallas_call | solution.py:289
  65.1 4.9 %collective-permute-start.22 = (bf16[4,288,256]{2,1,0:T(8,128)(2,1)S(1)}, bf16[4,288,256]{2,1,0:T(8,128)(2,1)S(1)}, u32[]{:S(2)}, u32[]{:S(2)}) collective-permute-start(bf16[4,288,256]{2,1,0:T(8,128)(2,1)S(1)} %get-tuple-element.54), channel_id=1, source_target_pairs={{0,16},{16,0},{1,17},{17,1},{2,18},{18,2},{3,19},{19,3},{4,20},{20... | collective-permute-start | bytes 1769480 | tf_op jit(solution)/shard_map/ppermute | solution.py:19
  70.0 1.7 %grad_first.4.refs_0_ = f32[768,768]{1,0:T(8,128)S(1)} custom-call(bf16[4,40,32,768]{3,2,1,0:T(8,128)(2,1)S(1)} %spread.1.wide_ref, bf16[16,32,256]{2,1,0:T(8,128)(2,1)S(1)} %get-tuple-element.42.a_ref, bf16[16,32,256]{2,1,0:T(8,128)(2,1)S(1)} %get-tuple-element.43.b_ref), custom_call_target="tpu_custom_call" | custom-call | flops 1 | bytes 1 | tf_op jit(solution)/shard_map/grad_first/pallas_call | solution.py:175
  71.7 1.8 %grad_first.5.refs_0_ = f32[768,768]{1,0:T(8,128)S(1)} custom-call(bf16[4,40,32,768]{3,2,1,0:T(8,128)(2,1)S(1)} %spread.1.wide_ref, bf16[16,32,256]{2,1,0:T(8,128)(2,1)S(1)} %collective-permute-done.13.a_ref, bf16[16,32,256]{2,1,0:T(8,128)(2,1)S(1)} %collective-permute-done.19.b_ref, f32[768,768]{1,0:T(8,128)S(1)} %grad_first.4.refs_0_), custom_call_target="tpu_custom_call" | custom-call | flops 1 | bytes 1 | tf_op jit(solution)/shard_map/grad_first/pallas_call | solution.py:175
  73.5 1.8 %grad_first.6.refs_0_ = f32[768,768]{1,0:T(8,128)S(1)} custom-call(bf16[4,40,32,768]{3,2,1,0:T(8,128)(2,1)S(1)} %spread.1.wide_ref, bf16[16,32,256]{2,1,0:T(8,128)(2,1)S(1)} %collective-permute-done.20.a_ref, bf16[16,32,256]{2,1,0:T(8,128)(2,1)S(1)} %collective-permute-done.14.b_ref, f32[768,768]{1,0:T(8,128)S(1)} %grad_first.5.refs_0_), custom_call_target="tpu_custom_call" | custom-call | flops 1 | bytes 1 | tf_op jit(solution)/shard_map/grad_first/pallas_call | solution.py:175
  75.3 1.8 %grad_first.7 = (f32[384,768]{1,0:T(8,128)S(1)}, bf16[384,768]{1,0:T(8,128)(2,1)S(1)}) custom-call(bf16[4,40,32,768]{3,2,1,0:T(8,128)(2,1)S(1)} %spread.1.wide_ref, bf16[16,32,256]{2,1,0:T(8,128)(2,1)S(1)} %collective-permute-done.17.a_ref, bf16[16,32,256]{2,1,0:T(8,128)(2,1)S(1)} %collective-permute-done.18.b_ref, f32[768,768]{1,0:T(8,128)S(1)} %grad_first.6.refs_0_), custom_call_target="tpu_custom_call" | custom-call | flops 1 | bytes 1 | tf_op jit(solution)/shard_map/grad_first/pallas_call | solution.py:175
  77.4 2.7 %collective-permute-start.24 = (bf16[288,256]{1,0:T(8,128)(2,1)S(1)}, bf16[288,256]{1,0:T(8,128)(2,1)S(1)}, u32[]{:S(2)}, u32[]{:S(2)}) collective-permute-start(bf16[288,256]{1,0:T(8,128)(2,1)S(1)} %get-tuple-element.57), channel_id=1, source_target_pairs={{0,96},{32,0},{64,32},{96,64},{1,97},{33,1},{65,33},{97,65},{2,98}... | collective-permute-start | bytes 442376 | tf_op jit(solution)/shard_map/ppermute | solution.py:19
  80.0 3.5 %collective-permute-done.23.a_ref = bf16[288,256]{1,0:T(8,128)(2,1)S(1)} collective-permute-done((bf16[288,256]{1,0:T(8,128)(2,1)S(1)}, bf16[288,256]{1,0:T(8,128)(2,1)S(1)}, u32[]{:S(2)}, u32[]{:S(2)}) %collective-permute-start.23) | collective-permute-done | bytes 147488 | tf_op jit(solution)/shard_map/ppermute | solution.py:19
  83.5 2.4 %collective-permute-done.25.c_ref = bf16[288,256]{1,0:T(8,128)(2,1)S(1)} collective-permute-done((bf16[288,256]{1,0:T(8,128)(2,1)S(1)}, bf16[288,256]{1,0:T(8,128)(2,1)S(1)}, u32[]{:S(2)}, u32[]{:S(2)}) %collective-permute-start.25) | collective-permute-done | bytes 147488 | tf_op jit(solution)/shard_map/ppermute | solution.py:19
  86.1 22.3 %all_to_all.5 = bf16[16,90,256]{2,1,0:T(8,128)(2,1)S(1)} all-to-all(bf16[16,90,256]{2,1,0:T(8,128)(2,1)S(1)} %join.1), channel_id=1, replica_groups=mesh['y'=4,'c'=2,'z'=4,'x'=4] {'z','x'}, dimensions={0} | all-to-all | bytes 1474560 | tf_op jit(solution)/shard_map/all_to_all | solution.py:580
  108.6 2.7 %collective-permute-start.27 = (bf16[90,256]{1,0:T(8,128)(2,1)S(1)}, bf16[90,256]{1,0:T(8,128)(2,1)S(1)}, u32[]{:S(2)}, u32[]{:S(2)}) collective-permute-start(bf16[90,256]{1,0:T(8,128)(2,1)S(1)} %reduce_sum.12.a_ref), channel_id=1, source_target_pairs={{0,12},{4,0},{8,4},{12,8},{1,13},{5,1},{9,5},{13,9},{2,14},{6,2},{... | collective-permute-start | bytes 138248 | tf_op jit(solution)/shard_map/ppermute | solution.py:19
  112.8 3.3 %collective-permute-done.28.d_ref = bf16[90,256]{1,0:T(8,128)(2,1)S(1)} collective-permute-done((bf16[90,256]{1,0:T(8,128)(2,1)S(1)}, bf16[90,256]{1,0:T(8,128)(2,1)S(1)}, u32[]{:S(2)}, u32[]{:S(2)}) %collective-permute-start.28) | collective-permute-done | bytes 46112 | tf_op jit(solution)/shard_map/ppermute | solution.py:19
  116.5 2.8 %collective-permute-start.30 = (bf16[360,256]{1,0:T(8,128)(2,1)S(1)}, bf16[360,256]{1,0:T(8,128)(2,1)S(1)}, u32[]{:S(2)}, u32[]{:S(2)}) collective-permute-start(bf16[360,256]{1,0:T(8,128)(2,1)S(1)} %order_pieces.1.a_ref), channel_id=1, source_target_pairs={{0,3},{1,0},{2,1},{3,2},{4,7},{5,4},{6,5},{7,6},{8,11},{9,8},{10,9... | collective-permute-start | bytes 552968 | tf_op jit(solution)/shard_map/ppermute | solution.py:19
  119.2 3.1 %collective-permute-done.31.d_ref = bf16[360,256]{1,0:T(8,128)(2,1)S(1)} collective-permute-done((bf16[360,256]{1,0:T(8,128)(2,1)S(1)}, bf16[360,256]{1,0:T(8,128)(2,1)S(1)}, u32[]{:S(2)}, u32[]{:S(2)}) %collective-permute-start.31) | collective-permute-done | bytes 184352 | tf_op jit(solution)/shard_map/ppermute | solution.py:19
  122.4 2.5 %collective-permute-done.29.b_ref = bf16[360,256]{1,0:T(8,128)(2,1)S(1)} collective-permute-done((bf16[360,256]{1,0:T(8,128)(2,1)S(1)}, bf16[360,256]{1,0:T(8,128)(2,1)S(1)}, u32[]{:S(2)}, u32[]{:S(2)}) %collective-permute-start.29) | collective-permute-done | bytes 184352 | tf_op jit(solution)/shard_map/ppermute | solution.py:19
  124.9 1.8 %collective-permute-start.32 = (bf16[4,72,256]{2,1,0:T(8,128)(2,1)S(1)}, bf16[4,72,256]{2,1,0:T(8,128)(2,1)S(1)}, u32[]{:S(2)}, u32[]{:S(2)}) collective-permute-start(bf16[4,72,256]{2,1,0:T(8,128)(2,1)S(1)} %get-tuple-element.70), channel_id=1, source_target_pairs={{0,32},{32,64},{64,96},{96,0},{1,33},{33,65},{65,97},{97,1},{2,34}... | collective-permute-start | bytes 442376 | tf_op jit(solution)/shard_map/ppermute | solution.py:19
  130.7 3.0 %collective-permute-done.34 = bf16[4,72,256]{2,1,0:T(8,128)(2,1)S(1)} collective-permute-done((bf16[4,72,256]{2,1,0:T(8,128)(2,1)S(1)}, bf16[4,72,256]{2,1,0:T(8,128)(2,1)S(1)}, u32[]{:S(2)}, u32[]{:S(2)}) %collective-permute-start.34) | collective-permute-done | bytes 147488 | tf_op jit(solution)/shard_map/ppermute | solution.py:19
  133.8 7.8 %collective-permute-start.35 = (bf16[4,4,72,256]{3,2,1,0:T(8,128)(2,1)S(1)}, bf16[4,4,72,256]{3,2,1,0:T(8,128)(2,1)S(1)}, u32[]{:S(2)}, u32[]{:S(2)}) collective-permute-start(bf16[4,4,72,256]{3,2,1,0:T(8,128)(2,1)S(1)} %pad_maximum_fusion.1.near_ref), channel_id=1, source_target_pairs={{0,16},{16,0},{1,17},{17,1},{2,18},{18,2},{3,19},{19,3},{4,20},{20... | collective-permute-start | bytes 1769480 | tf_op jit(solution)/shard_map/ppermute | solution.py:19
  143.3 1.7 %lay_second.1 = f32[2304,256]{1,0:T(8,128)} custom-call(bf16[4,4,72,256]{3,2,1,0:T(8,128)(2,1)S(1)} %pad_maximum_fusion.1.near_ref, bf16[4,4,72,256]{3,2,1,0:T(8,128)(2,1)S(1)} %collective-permute-done.35.far_ref), custom_call_target="tpu_custom_call" | custom-call | flops 1 | bytes 1 | tf_op jit(solution)/shard_map/lay_second/pallas_call | solution.py:499
  (89 shorter events, 31.5 us)
Async XLA Ops:
  0.6 15.8 %collective-permute-start = (bf16[256,32,128]{2,1,0:T(8,128)(2,1)}, bf16[256,32,128]{2,1,0:T(8,128)(2,1)S(1)}, u32[]{:S(2)}, u32[]{:S(2)}) collective-permute-start(bf16[256,32,128]{2,1,0:T(8,128)(2,1)} %own_ref.1), channel_id=1, source_target_pairs={{0,16},{16,0},{1,17},{17,1},{2,18},{18,2},{3,19},{19,3},{4,20},{20... | collective-permute-start | bytes 6291464 | tf_op jit(solution)/shard_map/ppermute | solution.py:19
  4.6 5.8 %collective-permute-start.1 = (bf16[320,128]{1,0:T(8,128)(2,1)S(1)}, bf16[320,128]{1,0:T(8,128)(2,1)S(1)}, u32[]{:S(2)}, u32[]{:S(2)}) collective-permute-start(bf16[320,128]{1,0:T(8,128)(2,1)S(1)} %pad_maximum_fusion.4), channel_id=1, source_target_pairs={{0,1},{1,2},{2,3},{3,4},{4,5},{5,6},{6,7},{7,8},{8,9},{9,10},{10,1... | collective-permute-start | bytes 245768 | tf_op jit(solution)/shard_map/ppermute | solution.py:378
  7.8 7.4 %collective-permute-start.4 = (bf16[3,3,128,256]{3,2,1,0:T(8,128)(2,1)}, bf16[3,3,128,256]{3,2,1,0:T(8,128)(2,1)S(1)}, u32[]{:S(2)}, u32[]{:S(2)}) collective-permute-start(bf16[3,3,128,256]{3,2,1,0:T(8,128)(2,1)} %param.5), channel_id=1, source_target_pairs={{0,16},{16,0},{1,17},{17,1},{2,18},{18,2},{3,19},{19,3},{4,20},{20... | collective-permute-start | bytes 1769480 | tf_op jit(solution)/shard_map/ppermute | solution.py:19
  8.4 5.9 %collective-permute-start.2 = (bf16[320,128]{1,0:T(8,128)(2,1)S(1)}, bf16[320,128]{1,0:T(8,128)(2,1)S(1)}, u32[]{:S(2)}, u32[]{:S(2)}) collective-permute-start(bf16[320,128]{1,0:T(8,128)(2,1)S(1)} %pad_maximum_fusion.5), channel_id=1, source_target_pairs={{1,0},{2,1},{3,2},{4,3},{5,4},{6,5},{7,6},{8,7},{9,8},{10,9},{11,1... | collective-permute-start | bytes 245768 | tf_op jit(solution)/shard_map/ppermute | solution.py:378
  19.8 10.5 %collective-permute-start.5 = (bf16[17,32,256]{2,1,0:T(8,128)(2,1)S(1)}, bf16[17,32,256]{2,1,0:T(8,128)(2,1)S(1)}, u32[]{:S(2)}, u32[]{:S(2)}) collective-permute-start(bf16[17,32,256]{2,1,0:T(8,128)(2,1)S(1)} %get-tuple-element.31), channel_id=1, source_target_pairs={{0,32},{32,64},{64,96},{96,0},{1,33},{33,65},{65,97},{97,1},{2,34}... | collective-permute-start | bytes 835592 | tf_op jit(solution)/shard_map/ppermute | solution.py:19
  21.2 9.2 %collective-permute-start.8 = (bf16[17,32,256]{2,1,0:T(8,128)(2,1)S(1)}, bf16[17,32,256]{2,1,0:T(8,128)(2,1)S(1)}, u32[]{:S(2)}, u32[]{:S(2)}) collective-permute-start(bf16[17,32,256]{2,1,0:T(8,128)(2,1)S(1)} %get-tuple-element.33), channel_id=1, source_target_pairs={{0,96},{32,0},{64,32},{96,64},{1,97},{33,1},{65,33},{97,65},{2,98}... | collective-permute-start | bytes 835592 | tf_op jit(solution)/shard_map/ppermute | solution.py:19
  22.7 7.5 %collective-permute-start.6 = (bf16[34,256]{1,0:T(8,128)(2,1)S(1)}, bf16[34,256]{1,0:T(8,128)(2,1)S(1)}, u32[]{:S(2)}, u32[]{:S(2)}) collective-permute-start(bf16[34,256]{1,0:T(8,128)(2,1)S(1)} %maximum_maximum_fusion), channel_id=1, source_target_pairs={{0,16},{16,32},{32,48},{48,64},{64,80},{80,96},{96,112},{1,17},{17... | collective-permute-start | bytes 52232 | tf_op jit(solution)/shard_map/ppermute | solution.py:544
  25.2 5.1 %collective-permute-start.7 = (bf16[34,256]{1,0:T(8,128)(2,1)S(1)}, bf16[34,256]{1,0:T(8,128)(2,1)S(1)}, u32[]{:S(2)}, u32[]{:S(2)}) collective-permute-start(bf16[34,256]{1,0:T(8,128)(2,1)S(1)} %maximum_maximum_fusion.1), channel_id=1, source_target_pairs={{16,0},{32,16},{48,32},{64,48},{80,64},{96,80},{112,96},{17,1},{33... | collective-permute-start | bytes 52232 | tf_op jit(solution)/shard_map/ppermute | solution.py:545
  28.6 8.8 %collective-permute-start.10 = (bf16[17,32,256]{2,1,0:T(8,128)(2,1)S(1)}, bf16[17,32,256]{2,1,0:T(8,128)(2,1)S(1)}, u32[]{:S(2)}, u32[]{:S(2)}) collective-permute-start(bf16[17,32,256]{2,1,0:T(8,128)(2,1)S(1)} %get-tuple-element.36), channel_id=1, source_target_pairs={{0,96},{32,0},{64,32},{96,64},{1,97},{33,1},{65,33},{97,65},{2,98}... | collective-permute-start | bytes 835592 | tf_op jit(solution)/shard_map/ppermute | solution.py:19
  30.2 7.3 %collective-permute-start.11 = (bf16[17,32,256]{2,1,0:T(8,128)(2,1)S(1)}, bf16[17,32,256]{2,1,0:T(8,128)(2,1)S(1)}, u32[]{:S(2)}, u32[]{:S(2)}) collective-permute-start(bf16[17,32,256]{2,1,0:T(8,128)(2,1)S(1)} %get-tuple-element.37), channel_id=1, source_target_pairs={{0,32},{32,64},{64,96},{96,0},{1,33},{33,65},{65,97},{97,1},{2,34}... | collective-permute-start | bytes 835592 | tf_op jit(solution)/shard_map/ppermute | solution.py:19
  31.8 11.0 %collective-permute-start.12 = (bf16[17,32,256]{2,1,0:T(8,128)(2,1)S(1)}, bf16[17,32,256]{2,1,0:T(8,128)(2,1)S(1)}, u32[]{:S(2)}, u32[]{:S(2)}) collective-permute-start(bf16[17,32,256]{2,1,0:T(8,128)(2,1)S(1)} %get-tuple-element.38), channel_id=1, source_target_pairs={{0,96},{32,0},{64,32},{96,64},{1,97},{33,1},{65,33},{97,65},{2,98}... | collective-permute-start | bytes 835592 | tf_op jit(solution)/shard_map/ppermute | solution.py:19
  34.5 9.9 %collective-permute-start.9 = (bf16[17,32,256]{2,1,0:T(8,128)(2,1)S(1)}, bf16[17,32,256]{2,1,0:T(8,128)(2,1)S(1)}, u32[]{:S(2)}, u32[]{:S(2)}) collective-permute-start(bf16[17,32,256]{2,1,0:T(8,128)(2,1)S(1)} %get-tuple-element.34), channel_id=1, source_target_pairs={{0,32},{32,64},{64,96},{96,0},{1,33},{33,65},{65,97},{97,1},{2,34}... | collective-permute-start | bytes 835592 | tf_op jit(solution)/shard_map/ppermute | solution.py:19
  45.4 13.4 %collective-permute-start.13 = (bf16[16,32,256]{2,1,0:T(8,128)(2,1)S(1)}, bf16[16,32,256]{2,1,0:T(8,128)(2,1)S(1)}, u32[]{:S(2)}, u32[]{:S(2)}) collective-permute-start(bf16[16,32,256]{2,1,0:T(8,128)(2,1)S(1)} %get-tuple-element.42.a_ref), channel_id=1, source_target_pairs={{0,32},{32,64},{64,96},{96,0},{1,33},{33,65},{65,97},{97,1},{2,34}... | collective-permute-start | bytes 786440 | tf_op jit(solution)/shard_map/ppermute | solution.py:19
  45.5 13.4 %collective-permute-start.14 = (bf16[16,32,256]{2,1,0:T(8,128)(2,1)S(1)}, bf16[16,32,256]{2,1,0:T(8,128)(2,1)S(1)}, u32[]{:S(2)}, u32[]{:S(2)}) collective-permute-start(bf16[16,32,256]{2,1,0:T(8,128)(2,1)S(1)} %get-tuple-element.43.b_ref), channel_id=1, source_target_pairs={{0,96},{32,0},{64,32},{96,64},{1,97},{33,1},{65,33},{97,65},{2,98}... | collective-permute-start | bytes 786440 | tf_op jit(solution)/shard_map/ppermute | solution.py:19
  48.1 5.9 %collective-permute-start.15 = (bf16[34,256]{1,0:T(8,128)(2,1)S(1)}, bf16[34,256]{1,0:T(8,128)(2,1)S(1)}, u32[]{:S(2)}, u32[]{:S(2)}) collective-permute-start(bf16[34,256]{1,0:T(8,128)(2,1)S(1)} %get-tuple-element.61), channel_id=1, source_target_pairs={{0,1},{1,2},{2,3},{3,4},{4,5},{5,6},{6,7},{7,8},{8,9},{9,10},{10,1... | collective-permute-start | bytes 52232 | tf_op jit(solution)/shard_map/ppermute | solution.py:378
  51.2 13.9 %collective-permute-start.19 = (bf16[16,32,256]{2,1,0:T(8,128)(2,1)S(1)}, bf16[16,32,256]{2,1,0:T(8,128)(2,1)S(1)}, u32[]{:S(2)}, u32[]{:S(2)}) collective-permute-start(bf16[16,32,256]{2,1,0:T(8,128)(2,1)S(1)} %get-tuple-element.43.b_ref), channel_id=1, source_target_pairs={{0,32},{32,64},{64,96},{96,0},{1,33},{33,65},{65,97},{97,1},{2,34}... | collective-permute-start | bytes 786440 | tf_op jit(solution)/shard_map/ppermute | solution.py:19
  51.3 13.8 %collective-permute-start.20 = (bf16[16,32,256]{2,1,0:T(8,128)(2,1)S(1)}, bf16[16,32,256]{2,1,0:T(8,128)(2,1)S(1)}, u32[]{:S(2)}, u32[]{:S(2)}) collective-permute-start(bf16[16,32,256]{2,1,0:T(8,128)(2,1)S(1)} %get-tuple-element.42.a_ref), channel_id=1, source_target_pairs={{0,96},{32,0},{64,32},{96,64},{1,97},{33,1},{65,33},{97,65},{2,98}... | collective-permute-start | bytes 786440 | tf_op jit(solution)/shard_map/ppermute | solution.py:19
  54.0 4.8 %collective-permute-start.16 = (bf16[34,256]{1,0:T(8,128)(2,1)S(1)}, bf16[34,256]{1,0:T(8,128)(2,1)S(1)}, u32[]{:S(2)}, u32[]{:S(2)}) collective-permute-start(bf16[34,256]{1,0:T(8,128)(2,1)S(1)} %get-tuple-element.62), channel_id=1, source_target_pairs={{1,0},{2,1},{3,2},{4,3},{5,4},{6,5},{7,6},{8,7},{9,8},{10,9},{11,1... | collective-permute-start | bytes 52232 | tf_op jit(solution)/shard_map/ppermute | solution.py:378
  58.8 16.4 %collective-permute-start.17 = (bf16[16,32,256]{2,1,0:T(8,128)(2,1)S(1)}, bf16[16,32,256]{2,1,0:T(8,128)(2,1)S(1)}, u32[]{:S(2)}, u32[]{:S(2)}) collective-permute-start(bf16[16,32,256]{2,1,0:T(8,128)(2,1)S(1)} %collective-permute-done.13.a_ref), channel_id=1, source_target_pairs={{0,32},{32,64},{64,96},{96,0},{1,33},{33,65},{65,97},{97,1},{2,34}... | collective-permute-start | bytes 786440 | tf_op jit(solution)/shard_map/ppermute | solution.py:19
  58.9 16.4 %collective-permute-start.18 = (bf16[16,32,256]{2,1,0:T(8,128)(2,1)S(1)}, bf16[16,32,256]{2,1,0:T(8,128)(2,1)S(1)}, u32[]{:S(2)}, u32[]{:S(2)}) collective-permute-start(bf16[16,32,256]{2,1,0:T(8,128)(2,1)S(1)} %collective-permute-done.14.b_ref), channel_id=1, source_target_pairs={{0,96},{32,0},{64,32},{96,64},{1,97},{33,1},{65,33},{97,65},{2,98}... | collective-permute-start | bytes 786440 | tf_op jit(solution)/shard_map/ppermute | solution.py:19
  65.1 12.0 %collective-permute-start.22 = (bf16[4,288,256]{2,1,0:T(8,128)(2,1)S(1)}, bf16[4,288,256]{2,1,0:T(8,128)(2,1)S(1)}, u32[]{:S(2)}, u32[]{:S(2)}) collective-permute-start(bf16[4,288,256]{2,1,0:T(8,128)(2,1)S(1)} %get-tuple-element.54), channel_id=1, source_target_pairs={{0,16},{16,0},{1,17},{17,1},{2,18},{18,2},{3,19},{19,3},{4,20},{20... | collective-permute-start | bytes 1769480 | tf_op jit(solution)/shard_map/ppermute | solution.py:19
  77.0 8.9 %collective-permute-start.21 = (bf16[384,768]{1,0:T(8,128)(2,1)S(1)}, bf16[384,768]{1,0:T(8,128)(2,1)S(1)}, u32[]{:S(2)}, u32[]{:S(2)}) collective-permute-start(bf16[384,768]{1,0:T(8,128)(2,1)S(1)} %get-tuple-element.52), channel_id=1, source_target_pairs={{0,16},{16,0},{1,17},{17,1},{2,18},{18,2},{3,19},{19,3},{4,20},{20... | collective-permute-start | bytes 1769480 | tf_op jit(solution)/shard_map/ppermute | solution.py:19
  77.3 6.2 %collective-permute-start.23 = (bf16[288,256]{1,0:T(8,128)(2,1)S(1)}, bf16[288,256]{1,0:T(8,128)(2,1)S(1)}, u32[]{:S(2)}, u32[]{:S(2)}) collective-permute-start(bf16[288,256]{1,0:T(8,128)(2,1)S(1)} %get-tuple-element.56), channel_id=1, source_target_pairs={{0,32},{32,64},{64,96},{96,0},{1,33},{33,65},{65,97},{97,1},{2,34}... | collective-permute-start | bytes 442376 | tf_op jit(solution)/shard_map/ppermute | solution.py:19
  77.4 6.1 %collective-permute-start.24 = (bf16[288,256]{1,0:T(8,128)(2,1)S(1)}, bf16[288,256]{1,0:T(8,128)(2,1)S(1)}, u32[]{:S(2)}, u32[]{:S(2)}) collective-permute-start(bf16[288,256]{1,0:T(8,128)(2,1)S(1)} %get-tuple-element.57), channel_id=1, source_target_pairs={{0,96},{32,0},{64,32},{96,64},{1,97},{33,1},{65,33},{97,65},{2,98}... | collective-permute-start | bytes 442376 | tf_op jit(solution)/shard_map/ppermute | solution.py:19
  80.0 5.9 %collective-permute-start.25 = (bf16[288,256]{1,0:T(8,128)(2,1)S(1)}, bf16[288,256]{1,0:T(8,128)(2,1)S(1)}, u32[]{:S(2)}, u32[]{:S(2)}) collective-permute-start(bf16[288,256]{1,0:T(8,128)(2,1)S(1)} %get-tuple-element.58), channel_id=1, source_target_pairs={{0,64},{32,96},{64,0},{96,32},{1,65},{33,97},{65,1},{97,33},{2,66}... | collective-permute-start | bytes 442376 | tf_op jit(solution)/shard_map/ppermute | solution.py:19
  111.3 4.8 %collective-permute-start.28 = (bf16[90,256]{1,0:T(8,128)(2,1)S(1)}, bf16[90,256]{1,0:T(8,128)(2,1)S(1)}, u32[]{:S(2)}, u32[]{:S(2)}) collective-permute-start(bf16[90,256]{1,0:T(8,128)(2,1)S(1)} %reduce_sum.12.a_ref), channel_id=1, source_target_pairs={{0,8},{4,12},{8,0},{12,4},{1,9},{5,13},{9,1},{13,5},{2,10},{6,14},... | collective-permute-start | bytes 138248 | tf_op jit(solution)/shard_map/ppermute | solution.py:19
  116.2 6.2 %collective-permute-start.31 = (bf16[360,256]{1,0:T(8,128)(2,1)S(1)}, bf16[360,256]{1,0:T(8,128)(2,1)S(1)}, u32[]{:S(2)}, u32[]{:S(2)}) collective-permute-start(bf16[360,256]{1,0:T(8,128)(2,1)S(1)} %order_pieces.1.a_ref), channel_id=1, source_target_pairs={{0,2},{1,3},{2,0},{3,1},{4,6},{5,7},{6,4},{7,5},{8,10},{9,11},{10,... | collective-permute-start | bytes 552968 | tf_op jit(solution)/shard_map/ppermute | solution.py:19
  116.5 5.9 %collective-permute-start.30 = (bf16[360,256]{1,0:T(8,128)(2,1)S(1)}, bf16[360,256]{1,0:T(8,128)(2,1)S(1)}, u32[]{:S(2)}, u32[]{:S(2)}) collective-permute-start(bf16[360,256]{1,0:T(8,128)(2,1)S(1)} %order_pieces.1.a_ref), channel_id=1, source_target_pairs={{0,3},{1,0},{2,1},{3,2},{4,7},{5,4},{6,5},{7,6},{8,11},{9,8},{10,9... | collective-permute-start | bytes 552968 | tf_op jit(solution)/shard_map/ppermute | solution.py:19
  119.2 5.6 %collective-permute-start.29 = (bf16[360,256]{1,0:T(8,128)(2,1)S(1)}, bf16[360,256]{1,0:T(8,128)(2,1)S(1)}, u32[]{:S(2)}, u32[]{:S(2)}) collective-permute-start(bf16[360,256]{1,0:T(8,128)(2,1)S(1)} %order_pieces.1.a_ref), channel_id=1, source_target_pairs={{0,1},{1,2},{2,3},{3,0},{4,5},{5,6},{6,7},{7,4},{8,9},{9,10},{10,1... | collective-permute-start | bytes 552968 | tf_op jit(solution)/shard_map/ppermute | solution.py:19
  124.9 5.8 %collective-permute-start.32 = (bf16[4,72,256]{2,1,0:T(8,128)(2,1)S(1)}, bf16[4,72,256]{2,1,0:T(8,128)(2,1)S(1)}, u32[]{:S(2)}, u32[]{:S(2)}) collective-permute-start(bf16[4,72,256]{2,1,0:T(8,128)(2,1)S(1)} %get-tuple-element.70), channel_id=1, source_target_pairs={{0,32},{32,64},{64,96},{96,0},{1,33},{33,65},{65,97},{97,1},{2,34}... | collective-permute-start | bytes 442376 | tf_op jit(solution)/shard_map/ppermute | solution.py:19
  128.3 5.5 %collective-permute-start.34 = (bf16[4,72,256]{2,1,0:T(8,128)(2,1)S(1)}, bf16[4,72,256]{2,1,0:T(8,128)(2,1)S(1)}, u32[]{:S(2)}, u32[]{:S(2)}) collective-permute-start(bf16[4,72,256]{2,1,0:T(8,128)(2,1)S(1)} %get-tuple-element.70), channel_id=1, source_target_pairs={{0,64},{32,96},{64,0},{96,32},{1,65},{33,97},{65,1},{97,33},{2,66}... | collective-permute-start | bytes 442376 | tf_op jit(solution)/shard_map/ppermute | solution.py:19
  133.8 9.4 %collective-permute-start.35 = (bf16[4,4,72,256]{3,2,1,0:T(8,128)(2,1)S(1)}, bf16[4,4,72,256]{3,2,1,0:T(8,128)(2,1)S(1)}, u32[]{:S(2)}, u32[]{:S(2)}) collective-permute-start(bf16[4,4,72,256]{3,2,1,0:T(8,128)(2,1)S(1)} %pad_maximum_fusion.1.near_ref), channel_id=1, source_target_pairs={{0,16},{16,0},{1,17},{17,1},{2,18},{18,2},{3,19},{19,3},{4,20},{20... | collective-permute-start | bytes 1769480 | tf_op jit(solution)/shard_map/ppermute | solution.py:19
  (7 other events, 33.3 us)

commit v7 on v6

--- a/solution.py
+++ b/solution.py
@@ -560,10 +560,11 @@
     delta_a, delta_b, hidden = point(own, from_a, from_b, back)
 
     on_a, off_b = shift(delta_a, "y", on), shift(delta_b, "y", off)
-    on_b, off_a = shift(delta_b, "y", on), shift(delta_a, "y", off)
-    on_a, off_b, edges = lax.optimization_barrier(
-        (on_a, off_b, row_halo([hidden[:, rows - 1], hidden[:, 0]]))
+    edges = row_halo([hidden[:, rows - 1], hidden[:, 0]])
+    on_a, off_b, edges, late_a, late_b = lax.optimization_barrier(
+        (on_a, off_b, edges, delta_a, delta_b)
     )
+    on_b, off_a = shift(late_b, "y", on), shift(late_a, "y", off)
     fwd_a, fwd_b = shift(on_a, "y", on), shift(off_b, "y", off)
     total = grad_strip(0, wide, (delta_a, delta_b), None, False)
     features, near, far = second_tile(hidden, edges, weight_second, cotangent, chips)

time: 145 us -> 145 us (level)
  transfers between devices with their start and end apart: 36 -> 36, of which waited for: 15 -> 16; matrix products, arithmetic and copies ran while one was open for 3% -> 3% of each run, Pallas kernels for 12% -> 12%
where the time goes in v7:
time: 145 us
  starting transfers between devices  57.3 us (40%)
  waiting for transfers between devices  35.3 us (24%)
  Pallas kernels  23.5 us (16%)
  blocking collectives  22.5 us (16%)
  local copies, waits for them, and re-layouts  3.55 us (2%)
    ppermute x30, starting transfers between devices, shift(): lax.ppermute(x, axis, [(i, (i + step) % count) for i in range(count)])  44 us
    ppermute x30, waiting for transfers between devices, shift(): lax.ppermute(x, axis, [(i, (i + step) % count) for i in range(count)])  28.2 us
    all_to_all x1, blocking collectives, body(): summed = lax.all_to_all(joined, SKY, 0, 0, tiled=True)  22.5 us
    ppermute x2, waiting for transfers between devices, row_halo(): lax.ppermute(ends[1], SKY, down)  7.06 us
    pallas_call x4, Pallas kernels, grad_strip(): pl.pallas_call(functools.partial(grad_kernel, step, old is not None, last...  7 us
    ppermute x2, starting transfers between devices, row_halo(): lax.ppermute(ends[0], SKY, up)  6.31 us
    pallas_call x4, Pallas kernels, conv_parts(): pl.pallas_call(functools.partial(conv_kernel, parts, len(adds)), out_shap...  5.84 us
    pallas_call x1, Pallas kernels, second_tile(): pl.pallas_call(functools.partial(second_kernel, chips), out_shape=(jax.Sh...  3.53 us
  transfers between devices with their start and end apart: 36, of which 16 were waited for; matrix products, arithmetic and copies ran while one was open for 3% of the time, Pallas kernels for 12%

profile of v7, /device:TPU:1, one launch (start us, length us, event | category | flops | bytes accessed | tf_op | source)
XLA Modules:
  0.0 144.5 jit_solution(1620199320344597867)
XLA Ops:
  4.6 3.2 %collective-permute-start.1 = (bf16[320,128]{1,0:T(8,128)(2,1)S(1)}, bf16[320,128]{1,0:T(8,128)(2,1)S(1)}, u32[]{:S(2)}, u32[]{:S(2)}) collective-permute-start(bf16[320,128]{1,0:T(8,128)(2,1)S(1)} %pad_maximum_fusion.4), channel_id=1, source_target_pairs={{0,1},{1,2},{2,3},{3,4},{4,5},{5,6},{6,7},{7,8},{8,9},{9,10},{10,1... | collective-permute-start | bytes 245768 | tf_op jit(solution)/shard_map/ppermute | solution.py:378
  10.4 3.8 %collective-permute-done.2 = bf16[320,128]{1,0:T(8,128)(2,1)S(1)} collective-permute-done((bf16[320,128]{1,0:T(8,128)(2,1)S(1)}, bf16[320,128]{1,0:T(8,128)(2,1)S(1)}, u32[]{:S(2)}, u32[]{:S(2)}) %collective-permute-start.2) | collective-permute-done | bytes 81952 | tf_op jit(solution)/shard_map/ppermute | solution.py:378
  16.4 1.9 %spread.1.wide_ref = bf16[4,40,32,768]{3,2,1,0:T(8,128)(2,1)S(1)} custom-call(bf16[256,32,128]{2,1,0:T(8,128)(2,1)S(1)} %copy-done.1, bf16[256,32,128]{2,1,0:T(8,128)(2,1)S(1)} %collective-permute-done.far_ref, bf16[2,320,128]{2,1,0:T(8,128)(2,1)S(1)} %pad_maximum_fusion.2.own_halo_ref.edge_ref, bf16[2,320,128]{2,1,0:T(8,128)(2,1)S(1)} %collective-permute-done.3.far_halo_ref), custom_call_target="tpu_custom_call" | custom-call | flops 1 | bytes 1 | tf_op jit(solution)/shard_map/spread/pallas_call | solution.py:94
  22.7 2.5 %collective-permute-start.6 = (bf16[34,256]{1,0:T(8,128)(2,1)S(1)}, bf16[34,256]{1,0:T(8,128)(2,1)S(1)}, u32[]{:S(2)}, u32[]{:S(2)}) collective-permute-start(bf16[34,256]{1,0:T(8,128)(2,1)S(1)} %maximum_maximum_fusion), channel_id=1, source_target_pairs={{0,16},{16,32},{32,48},{48,64},{64,80},{80,96},{96,112},{1,17},{17... | collective-permute-start | bytes 52232 | tf_op jit(solution)/shard_map/ppermute | solution.py:544
  25.2 1.9 %collective-permute-start.7 = (bf16[34,256]{1,0:T(8,128)(2,1)S(1)}, bf16[34,256]{1,0:T(8,128)(2,1)S(1)}, u32[]{:S(2)}, u32[]{:S(2)}) collective-permute-start(bf16[34,256]{1,0:T(8,128)(2,1)S(1)} %maximum_maximum_fusion.1), channel_id=1, source_target_pairs={{16,0},{32,16},{48,32},{64,48},{80,64},{96,80},{112,96},{17,1},{33... | collective-permute-start | bytes 52232 | tf_op jit(solution)/shard_map/ppermute | solution.py:545
  28.6 1.6 %collective-permute-start.10 = (bf16[17,32,256]{2,1,0:T(8,128)(2,1)S(1)}, bf16[17,32,256]{2,1,0:T(8,128)(2,1)S(1)}, u32[]{:S(2)}, u32[]{:S(2)}) collective-permute-start(bf16[17,32,256]{2,1,0:T(8,128)(2,1)S(1)} %get-tuple-element.38), channel_id=1, source_target_pairs={{0,96},{32,0},{64,32},{96,64},{1,97},{33,1},{65,33},{97,65},{2,98}... | collective-permute-start | bytes 835592 | tf_op jit(solution)/shard_map/ppermute | solution.py:19
  31.8 2.7 %collective-permute-start.12 = (bf16[17,32,256]{2,1,0:T(8,128)(2,1)S(1)}, bf16[17,32,256]{2,1,0:T(8,128)(2,1)S(1)}, u32[]{:S(2)}, u32[]{:S(2)}) collective-permute-start(bf16[17,32,256]{2,1,0:T(8,128)(2,1)S(1)} %get-tuple-element.40), channel_id=1, source_target_pairs={{0,96},{32,0},{64,32},{96,64},{1,97},{33,1},{65,33},{97,65},{2,98}... | collective-permute-start | bytes 835592 | tf_op jit(solution)/shard_map/ppermute | solution.py:19
  37.6 5.2 %collective-permute-done.12.b1_ref = bf16[17,32,256]{2,1,0:T(8,128)(2,1)S(1)} collective-permute-done((bf16[17,32,256]{2,1,0:T(8,128)(2,1)S(1)}, bf16[17,32,256]{2,1,0:T(8,128)(2,1)S(1)}, u32[]{:S(2)}, u32[]{:S(2)}) %collective-permute-start.12) | collective-permute-done | bytes 278560 | tf_op jit(solution)/shard_map/ppermute | solution.py:19
  45.5 2.7 %collective-permute-start.14 = (bf16[16,32,256]{2,1,0:T(8,128)(2,1)S(1)}, bf16[16,32,256]{2,1,0:T(8,128)(2,1)S(1)}, u32[]{:S(2)}, u32[]{:S(2)}) collective-permute-start(bf16[16,32,256]{2,1,0:T(8,128)(2,1)S(1)} %get-tuple-element.51.b_ref), channel_id=1, source_target_pairs={{0,96},{32,0},{64,32},{96,64},{1,97},{33,1},{65,33},{97,65},{2,98}... | collective-permute-start | bytes 786440 | tf_op jit(solution)/shard_map/ppermute | solution.py:19
  48.1 3.1 %collective-permute-start.15 = (bf16[34,256]{1,0:T(8,128)(2,1)S(1)}, bf16[34,256]{1,0:T(8,128)(2,1)S(1)}, u32[]{:S(2)}, u32[]{:S(2)}) collective-permute-start(bf16[34,256]{1,0:T(8,128)(2,1)S(1)} %get-tuple-element.65), channel_id=1, source_target_pairs={{0,1},{1,2},{2,3},{3,4},{4,5},{5,6},{6,7},{7,8},{8,9},{9,10},{10,1... | collective-permute-start | bytes 52232 | tf_op jit(solution)/shard_map/ppermute | solution.py:378
  52.5 3.2 %collective-permute-done.16 = bf16[34,256]{1,0:T(8,128)(2,1)S(1)} collective-permute-done((bf16[34,256]{1,0:T(8,128)(2,1)S(1)}, bf16[34,256]{1,0:T(8,128)(2,1)S(1)}, u32[]{:S(2)}, u32[]{:S(2)}) %collective-permute-start.16) | collective-permute-done | bytes 17440 | tf_op jit(solution)/shard_map/ppermute | solution.py:378
  55.9 2.7 %collective-permute-start.20 = (bf16[16,32,256]{2,1,0:T(8,128)(2,1)S(1)}, bf16[16,32,256]{2,1,0:T(8,128)(2,1)S(1)}, u32[]{:S(2)}, u32[]{:S(2)}) collective-permute-start(bf16[16,32,256]{2,1,0:T(8,128)(2,1)S(1)} %get-tuple-element.52.a_ref), channel_id=1, source_target_pairs={{0,96},{32,0},{64,32},{96,64},{1,97},{33,1},{65,33},{97,65},{2,98}... | collective-permute-start | bytes 786440 | tf_op jit(solution)/shard_map/ppermute | solution.py:19
  58.5 2.7 %collective-permute-start.18 = (bf16[16,32,256]{2,1,0:T(8,128)(2,1)S(1)}, bf16[16,32,256]{2,1,0:T(8,128)(2,1)S(1)}, u32[]{:S(2)}, u32[]{:S(2)}) collective-permute-start(bf16[16,32,256]{2,1,0:T(8,128)(2,1)S(1)} %collective-permute-done.14.b_ref), channel_id=1, source_target_pairs={{0,96},{32,0},{64,32},{96,64},{1,97},{33,1},{65,33},{97,65},{2,98}... | collective-permute-start | bytes 786440 | tf_op jit(solution)/shard_map/ppermute | solution.py:19
  61.2 3.5 %second.1 = (bf16[32,32,256]{2,1,0:T(8,128)(2,1)}, f32[4,288,256]{2,1,0:T(8,128)S(1)}, bf16[4,288,256]{2,1,0:T(8,128)(2,1)S(1)}) custom-call(bf16[34,32,256]{2,1,0:T(8,128)(2,1)S(1)} %get-tuple-element.43.hid_ref, bf16[2,34,256]{2,1,0:T(8,128)(2,1)S(1)} %pad_maximum_fusion.6.edge_ref, bf16[2304,256]{1,0:T(8,128)(2,1)S(1)} %bitcast.62, ...), custom_call_target="tpu_custom_call" | custom-call | flops 1 | bytes 1 | tf_op jit(solution)/shard_map/second/pallas_call | solution.py:289
  64.8 5.2 %collective-permute-start.22 = (bf16[4,288,256]{2,1,0:T(8,128)(2,1)S(1)}, bf16[4,288,256]{2,1,0:T(8,128)(2,1)S(1)}, u32[]{:S(2)}, u32[]{:S(2)}) collective-permute-start(bf16[4,288,256]{2,1,0:T(8,128)(2,1)S(1)} %get-tuple-element.58), channel_id=1, source_target_pairs={{0,16},{16,0},{1,17},{17,1},{2,18},{18,2},{3,19},{19,3},{4,20},{20... | collective-permute-start | bytes 1769480 | tf_op jit(solution)/shard_map/ppermute | solution.py:19
  69.9 1.7 %grad_first.4.refs_0_ = f32[768,768]{1,0:T(8,128)S(1)} custom-call(bf16[4,40,32,768]{3,2,1,0:T(8,128)(2,1)S(1)} %spread.1.wide_ref, bf16[16,32,256]{2,1,0:T(8,128)(2,1)S(1)} %get-tuple-element.52.a_ref, bf16[16,32,256]{2,1,0:T(8,128)(2,1)S(1)} %get-tuple-element.51.b_ref), custom_call_target="tpu_custom_call" | custom-call | flops 1 | bytes 1 | tf_op jit(solution)/shard_map/grad_first/pallas_call | solution.py:175
  71.7 1.8 %grad_first.5.refs_0_ = f32[768,768]{1,0:T(8,128)S(1)} custom-call(bf16[4,40,32,768]{3,2,1,0:T(8,128)(2,1)S(1)} %spread.1.wide_ref, bf16[16,32,256]{2,1,0:T(8,128)(2,1)S(1)} %collective-permute-done.13.a_ref, bf16[16,32,256]{2,1,0:T(8,128)(2,1)S(1)} %collective-permute-done.19.b_ref, f32[768,768]{1,0:T(8,128)S(1)} %grad_first.4.refs_0_), custom_call_target="tpu_custom_call" | custom-call | flops 1 | bytes 1 | tf_op jit(solution)/shard_map/grad_first/pallas_call | solution.py:175
  73.4 1.8 %grad_first.6.refs_0_ = f32[768,768]{1,0:T(8,128)S(1)} custom-call(bf16[4,40,32,768]{3,2,1,0:T(8,128)(2,1)S(1)} %spread.1.wide_ref, bf16[16,32,256]{2,1,0:T(8,128)(2,1)S(1)} %collective-permute-done.20.a_ref, bf16[16,32,256]{2,1,0:T(8,128)(2,1)S(1)} %collective-permute-done.14.b_ref, f32[768,768]{1,0:T(8,128)S(1)} %grad_first.5.refs_0_), custom_call_target="tpu_custom_call" | custom-call | flops 1 | bytes 1 | tf_op jit(solution)/shard_map/grad_first/pallas_call | solution.py:175
  75.2 1.8 %grad_first.7 = (f32[384,768]{1,0:T(8,128)S(1)}, bf16[384,768]{1,0:T(8,128)(2,1)S(1)}) custom-call(bf16[4,40,32,768]{3,2,1,0:T(8,128)(2,1)S(1)} %spread.1.wide_ref, bf16[16,32,256]{2,1,0:T(8,128)(2,1)S(1)} %collective-permute-done.17.a_ref, bf16[16,32,256]{2,1,0:T(8,128)(2,1)S(1)} %collective-permute-done.18.b_ref, f32[768,768]{1,0:T(8,128)S(1)} %grad_first.6.refs_0_), custom_call_target="tpu_custom_call" | custom-call | flops 1 | bytes 1 | tf_op jit(solution)/shard_map/grad_first/pallas_call | solution.py:175
  77.3 2.7 %collective-permute-start.24 = (bf16[288,256]{1,0:T(8,128)(2,1)S(1)}, bf16[288,256]{1,0:T(8,128)(2,1)S(1)}, u32[]{:S(2)}, u32[]{:S(2)}) collective-permute-start(bf16[288,256]{1,0:T(8,128)(2,1)S(1)} %get-tuple-element.61), channel_id=1, source_target_pairs={{0,96},{32,0},{64,32},{96,64},{1,97},{33,1},{65,33},{97,65},{2,98}... | collective-permute-start | bytes 442376 | tf_op jit(solution)/shard_map/ppermute | solution.py:19
  80.0 3.5 %collective-permute-done.23.a_ref = bf16[288,256]{1,0:T(8,128)(2,1)S(1)} collective-permute-done((bf16[288,256]{1,0:T(8,128)(2,1)S(1)}, bf16[288,256]{1,0:T(8,128)(2,1)S(1)}, u32[]{:S(2)}, u32[]{:S(2)}) %collective-permute-start.23) | collective-permute-done | bytes 147488 | tf_op jit(solution)/shard_map/ppermute | solution.py:19
  83.5 2.5 %collective-permute-done.25.c_ref = bf16[288,256]{1,0:T(8,128)(2,1)S(1)} collective-permute-done((bf16[288,256]{1,0:T(8,128)(2,1)S(1)}, bf16[288,256]{1,0:T(8,128)(2,1)S(1)}, u32[]{:S(2)}, u32[]{:S(2)}) %collective-permute-start.25) | collective-permute-done | bytes 147488 | tf_op jit(solution)/shard_map/ppermute | solution.py:19
  86.2 22.5 %all_to_all.5 = bf16[16,90,256]{2,1,0:T(8,128)(2,1)S(1)} all-to-all(bf16[16,90,256]{2,1,0:T(8,128)(2,1)S(1)} %join.1), channel_id=1, replica_groups=mesh['y'=4,'c'=2,'z'=4,'x'=4] {'z','x'}, dimensions={0} | all-to-all | bytes 1474560 | tf_op jit(solution)/shard_map/all_to_all | solution.py:581
  108.8 2.7 %collective-permute-start.27 = (bf16[90,256]{1,0:T(8,128)(2,1)S(1)}, bf16[90,256]{1,0:T(8,128)(2,1)S(1)}, u32[]{:S(2)}, u32[]{:S(2)}) collective-permute-start(bf16[90,256]{1,0:T(8,128)(2,1)S(1)} %reduce_sum.12.a_ref), channel_id=1, source_target_pairs={{0,12},{4,0},{8,4},{12,8},{1,13},{5,1},{9,5},{13,9},{2,14},{6,2},{... | collective-permute-start | bytes 138248 | tf_op jit(solution)/shard_map/ppermute | solution.py:19
  113.0 3.2 %collective-permute-done.28.d_ref = bf16[90,256]{1,0:T(8,128)(2,1)S(1)} collective-permute-done((bf16[90,256]{1,0:T(8,128)(2,1)S(1)}, bf16[90,256]{1,0:T(8,128)(2,1)S(1)}, u32[]{:S(2)}, u32[]{:S(2)}) %collective-permute-start.28) | collective-permute-done | bytes 46112 | tf_op jit(solution)/shard_map/ppermute | solution.py:19
  117.6 1.6 %collective-permute-start.30 = (bf16[360,256]{1,0:T(8,128)(2,1)S(1)}, bf16[360,256]{1,0:T(8,128)(2,1)S(1)}, u32[]{:S(2)}, u32[]{:S(2)}) collective-permute-start(bf16[360,256]{1,0:T(8,128)(2,1)S(1)} %order_pieces.1.a_ref), channel_id=1, source_target_pairs={{0,3},{1,0},{2,1},{3,2},{4,7},{5,4},{6,5},{7,6},{8,11},{9,8},{10,9... | collective-permute-start | bytes 552968 | tf_op jit(solution)/shard_map/ppermute | solution.py:19
  119.2 3.2 %collective-permute-done.31.d_ref = bf16[360,256]{1,0:T(8,128)(2,1)S(1)} collective-permute-done((bf16[360,256]{1,0:T(8,128)(2,1)S(1)}, bf16[360,256]{1,0:T(8,128)(2,1)S(1)}, u32[]{:S(2)}, u32[]{:S(2)}) %collective-permute-start.31) | collective-permute-done | bytes 184352 | tf_op jit(solution)/shard_map/ppermute | solution.py:19
  125.8 2.0 %collective-permute-start.33 = (bf16[4,72,256]{2,1,0:T(8,128)(2,1)S(1)}, bf16[4,72,256]{2,1,0:T(8,128)(2,1)S(1)}, u32[]{:S(2)}, u32[]{:S(2)}) collective-permute-start(bf16[4,72,256]{2,1,0:T(8,128)(2,1)S(1)} %get-tuple-element.74), channel_id=1, source_target_pairs={{0,96},{32,0},{64,32},{96,64},{1,97},{33,1},{65,33},{97,65},{2,98}... | collective-permute-start | bytes 442376 | tf_op jit(solution)/shard_map/ppermute | solution.py:19
  128.9 1.6 %collective-permute-done.32 = bf16[4,72,256]{2,1,0:T(8,128)(2,1)S(1)} collective-permute-done((bf16[4,72,256]{2,1,0:T(8,128)(2,1)S(1)}, bf16[4,72,256]{2,1,0:T(8,128)(2,1)S(1)}, u32[]{:S(2)}, u32[]{:S(2)}) %collective-permute-start.32) | collective-permute-done | bytes 147488 | tf_op jit(solution)/shard_map/ppermute | solution.py:19
  130.5 2.7 %collective-permute-done.34 = bf16[4,72,256]{2,1,0:T(8,128)(2,1)S(1)} collective-permute-done((bf16[4,72,256]{2,1,0:T(8,128)(2,1)S(1)}, bf16[4,72,256]{2,1,0:T(8,128)(2,1)S(1)}, u32[]{:S(2)}, u32[]{:S(2)}) %collective-permute-start.34) | collective-permute-done | bytes 147488 | tf_op jit(solution)/shard_map/ppermute | solution.py:19
  133.3 7.9 %collective-permute-start.35 = (bf16[4,4,72,256]{3,2,1,0:T(8,128)(2,1)S(1)}, bf16[4,4,72,256]{3,2,1,0:T(8,128)(2,1)S(1)}, u32[]{:S(2)}, u32[]{:S(2)}) collective-permute-start(bf16[4,4,72,256]{3,2,1,0:T(8,128)(2,1)S(1)} %pad_maximum_fusion.1.near_ref), channel_id=1, source_target_pairs={{0,16},{16,0},{1,17},{17,1},{2,18},{18,2},{3,19},{19,3},{4,20},{20... | collective-permute-start | bytes 1769480 | tf_op jit(solution)/shard_map/ppermute | solution.py:19
  142.9 1.7 %lay_second.1 = f32[2304,256]{1,0:T(8,128)} custom-call(bf16[4,4,72,256]{3,2,1,0:T(8,128)(2,1)S(1)} %pad_maximum_fusion.1.near_ref, bf16[4,4,72,256]{3,2,1,0:T(8,128)(2,1)S(1)} %collective-permute-done.35.far_ref), custom_call_target="tpu_custom_call" | custom-call | flops 1 | bytes 1 | tf_op jit(solution)/shard_map/lay_second/pallas_call | solution.py:499
  (89 shorter events, 32.9 us)
Async XLA Ops:
  0.6 15.8 %collective-permute-start = (bf16[256,32,128]{2,1,0:T(8,128)(2,1)}, bf16[256,32,128]{2,1,0:T(8,128)(2,1)S(1)}, u32[]{:S(2)}, u32[]{:S(2)}) collective-permute-start(bf16[256,32,128]{2,1,0:T(8,128)(2,1)} %own_ref.1), channel_id=1, source_target_pairs={{0,16},{16,0},{1,17},{17,1},{2,18},{18,2},{3,19},{19,3},{4,20},{20... | collective-permute-start | bytes 6291464 | tf_op jit(solution)/shard_map/ppermute | solution.py:19
  4.6 5.8 %collective-permute-start.1 = (bf16[320,128]{1,0:T(8,128)(2,1)S(1)}, bf16[320,128]{1,0:T(8,128)(2,1)S(1)}, u32[]{:S(2)}, u32[]{:S(2)}) collective-permute-start(bf16[320,128]{1,0:T(8,128)(2,1)S(1)} %pad_maximum_fusion.4), channel_id=1, source_target_pairs={{0,1},{1,2},{2,3},{3,4},{4,5},{5,6},{6,7},{7,8},{8,9},{9,10},{10,1... | collective-permute-start | bytes 245768 | tf_op jit(solution)/shard_map/ppermute | solution.py:378
  7.8 7.4 %collective-permute-start.4 = (bf16[3,3,128,256]{3,2,1,0:T(8,128)(2,1)}, bf16[3,3,128,256]{3,2,1,0:T(8,128)(2,1)S(1)}, u32[]{:S(2)}, u32[]{:S(2)}) collective-permute-start(bf16[3,3,128,256]{3,2,1,0:T(8,128)(2,1)} %param.5), channel_id=1, source_target_pairs={{0,16},{16,0},{1,17},{17,1},{2,18},{18,2},{3,19},{19,3},{4,20},{20... | collective-permute-start | bytes 1769480 | tf_op jit(solution)/shard_map/ppermute | solution.py:19
  8.4 5.9 %collective-permute-start.2 = (bf16[320,128]{1,0:T(8,128)(2,1)S(1)}, bf16[320,128]{1,0:T(8,128)(2,1)S(1)}, u32[]{:S(2)}, u32[]{:S(2)}) collective-permute-start(bf16[320,128]{1,0:T(8,128)(2,1)S(1)} %pad_maximum_fusion.5), channel_id=1, source_target_pairs={{1,0},{2,1},{3,2},{4,3},{5,4},{6,5},{7,6},{8,7},{9,8},{10,9},{11,1... | collective-permute-start | bytes 245768 | tf_op jit(solution)/shard_map/ppermute | solution.py:378
  19.8 10.5 %collective-permute-start.5 = (bf16[17,32,256]{2,1,0:T(8,128)(2,1)S(1)}, bf16[17,32,256]{2,1,0:T(8,128)(2,1)S(1)}, u32[]{:S(2)}, u32[]{:S(2)}) collective-permute-start(bf16[17,32,256]{2,1,0:T(8,128)(2,1)S(1)} %get-tuple-element.33), channel_id=1, source_target_pairs={{0,32},{32,64},{64,96},{96,0},{1,33},{33,65},{65,97},{97,1},{2,34}... | collective-permute-start | bytes 835592 | tf_op jit(solution)/shard_map/ppermute | solution.py:19
  21.2 9.2 %collective-permute-start.8 = (bf16[17,32,256]{2,1,0:T(8,128)(2,1)S(1)}, bf16[17,32,256]{2,1,0:T(8,128)(2,1)S(1)}, u32[]{:S(2)}, u32[]{:S(2)}) collective-permute-start(bf16[17,32,256]{2,1,0:T(8,128)(2,1)S(1)} %get-tuple-element.35), channel_id=1, source_target_pairs={{0,96},{32,0},{64,32},{96,64},{1,97},{33,1},{65,33},{97,65},{2,98}... | collective-permute-start | bytes 835592 | tf_op jit(solution)/shard_map/ppermute | solution.py:19
  22.7 7.5 %collective-permute-start.6 = (bf16[34,256]{1,0:T(8,128)(2,1)S(1)}, bf16[34,256]{1,0:T(8,128)(2,1)S(1)}, u32[]{:S(2)}, u32[]{:S(2)}) collective-permute-start(bf16[34,256]{1,0:T(8,128)(2,1)S(1)} %maximum_maximum_fusion), channel_id=1, source_target_pairs={{0,16},{16,32},{32,48},{48,64},{64,80},{80,96},{96,112},{1,17},{17... | collective-permute-start | bytes 52232 | tf_op jit(solution)/shard_map/ppermute | solution.py:544
  25.2 5.1 %collective-permute-start.7 = (bf16[34,256]{1,0:T(8,128)(2,1)S(1)}, bf16[34,256]{1,0:T(8,128)(2,1)S(1)}, u32[]{:S(2)}, u32[]{:S(2)}) collective-permute-start(bf16[34,256]{1,0:T(8,128)(2,1)S(1)} %maximum_maximum_fusion.1), channel_id=1, source_target_pairs={{16,0},{32,16},{48,32},{64,48},{80,64},{96,80},{112,96},{17,1},{33... | collective-permute-start | bytes 52232 | tf_op jit(solution)/shard_map/ppermute | solution.py:545
  28.6 8.8 %collective-permute-start.10 = (bf16[17,32,256]{2,1,0:T(8,128)(2,1)S(1)}, bf16[17,32,256]{2,1,0:T(8,128)(2,1)S(1)}, u32[]{:S(2)}, u32[]{:S(2)}) collective-permute-start(bf16[17,32,256]{2,1,0:T(8,128)(2,1)S(1)} %get-tuple-element.38), channel_id=1, source_target_pairs={{0,96},{32,0},{64,32},{96,64},{1,97},{33,1},{65,33},{97,65},{2,98}... | collective-permute-start | bytes 835592 | tf_op jit(solution)/shard_map/ppermute | solution.py:19
  30.2 7.3 %collective-permute-start.11 = (bf16[17,32,256]{2,1,0:T(8,128)(2,1)S(1)}, bf16[17,32,256]{2,1,0:T(8,128)(2,1)S(1)}, u32[]{:S(2)}, u32[]{:S(2)}) collective-permute-start(bf16[17,32,256]{2,1,0:T(8,128)(2,1)S(1)} %get-tuple-element.39), channel_id=1, source_target_pairs={{0,32},{32,64},{64,96},{96,0},{1,33},{33,65},{65,97},{97,1},{2,34}... | collective-permute-start | bytes 835592 | tf_op jit(solution)/shard_map/ppermute | solution.py:19
  31.8 11.0 %collective-permute-start.12 = (bf16[17,32,256]{2,1,0:T(8,128)(2,1)S(1)}, bf16[17,32,256]{2,1,0:T(8,128)(2,1)S(1)}, u32[]{:S(2)}, u32[]{:S(2)}) collective-permute-start(bf16[17,32,256]{2,1,0:T(8,128)(2,1)S(1)} %get-tuple-element.40), channel_id=1, source_target_pairs={{0,96},{32,0},{64,32},{96,64},{1,97},{33,1},{65,33},{97,65},{2,98}... | collective-permute-start | bytes 835592 | tf_op jit(solution)/shard_map/ppermute | solution.py:19
  34.5 9.9 %collective-permute-start.9 = (bf16[17,32,256]{2,1,0:T(8,128)(2,1)S(1)}, bf16[17,32,256]{2,1,0:T(8,128)(2,1)S(1)}, u32[]{:S(2)}, u32[]{:S(2)}) collective-permute-start(bf16[17,32,256]{2,1,0:T(8,128)(2,1)S(1)} %get-tuple-element.36), channel_id=1, source_target_pairs={{0,32},{32,64},{64,96},{96,0},{1,33},{33,65},{65,97},{97,1},{2,34}... | collective-permute-start | bytes 835592 | tf_op jit(solution)/shard_map/ppermute | solution.py:19
  45.4 10.4 %collective-permute-start.13 = (bf16[16,32,256]{2,1,0:T(8,128)(2,1)S(1)}, bf16[16,32,256]{2,1,0:T(8,128)(2,1)S(1)}, u32[]{:S(2)}, u32[]{:S(2)}) collective-permute-start(bf16[16,32,256]{2,1,0:T(8,128)(2,1)S(1)} %get-tuple-element.52.a_ref), channel_id=1, source_target_pairs={{0,32},{32,64},{64,96},{96,0},{1,33},{33,65},{65,97},{97,1},{2,34}... | collective-permute-start | bytes 786440 | tf_op jit(solution)/shard_map/ppermute | solution.py:19
  45.5 10.3 %collective-permute-start.14 = (bf16[16,32,256]{2,1,0:T(8,128)(2,1)S(1)}, bf16[16,32,256]{2,1,0:T(8,128)(2,1)S(1)}, u32[]{:S(2)}, u32[]{:S(2)}) collective-permute-start(bf16[16,32,256]{2,1,0:T(8,128)(2,1)S(1)} %get-tuple-element.51.b_ref), channel_id=1, source_target_pairs={{0,96},{32,0},{64,32},{96,64},{1,97},{33,1},{65,33},{97,65},{2,98}... | collective-permute-start | bytes 786440 | tf_op jit(solution)/shard_map/ppermute | solution.py:19
  48.1 4.4 %collective-permute-start.15 = (bf16[34,256]{1,0:T(8,128)(2,1)S(1)}, bf16[34,256]{1,0:T(8,128)(2,1)S(1)}, u32[]{:S(2)}, u32[]{:S(2)}) collective-permute-start(bf16[34,256]{1,0:T(8,128)(2,1)S(1)} %get-tuple-element.65), channel_id=1, source_target_pairs={{0,1},{1,2},{2,3},{3,4},{4,5},{5,6},{6,7},{7,8},{8,9},{9,10},{10,1... | collective-permute-start | bytes 52232 | tf_op jit(solution)/shard_map/ppermute | solution.py:378
  51.2 4.5 %collective-permute-start.16 = (bf16[34,256]{1,0:T(8,128)(2,1)S(1)}, bf16[34,256]{1,0:T(8,128)(2,1)S(1)}, u32[]{:S(2)}, u32[]{:S(2)}) collective-permute-start(bf16[34,256]{1,0:T(8,128)(2,1)S(1)} %get-tuple-element.66), channel_id=1, source_target_pairs={{1,0},{2,1},{3,2},{4,3},{5,4},{6,5},{7,6},{8,7},{9,8},{10,9},{11,1... | collective-permute-start | bytes 52232 | tf_op jit(solution)/shard_map/ppermute | solution.py:378
  55.8 9.0 %collective-permute-start.19 = (bf16[16,32,256]{2,1,0:T(8,128)(2,1)S(1)}, bf16[16,32,256]{2,1,0:T(8,128)(2,1)S(1)}, u32[]{:S(2)}, u32[]{:S(2)}) collective-permute-start(bf16[16,32,256]{2,1,0:T(8,128)(2,1)S(1)} %get-tuple-element.51.b_ref), channel_id=1, source_target_pairs={{0,32},{32,64},{64,96},{96,0},{1,33},{33,65},{65,97},{97,1},{2,34}... | collective-permute-start | bytes 786440 | tf_op jit(solution)/shard_map/ppermute | solution.py:19
  55.9 8.9 %collective-permute-start.20 = (bf16[16,32,256]{2,1,0:T(8,128)(2,1)S(1)}, bf16[16,32,256]{2,1,0:T(8,128)(2,1)S(1)}, u32[]{:S(2)}, u32[]{:S(2)}) collective-permute-start(bf16[16,32,256]{2,1,0:T(8,128)(2,1)S(1)} %get-tuple-element.52.a_ref), channel_id=1, source_target_pairs={{0,96},{32,0},{64,32},{96,64},{1,97},{33,1},{65,33},{97,65},{2,98}... | collective-permute-start | bytes 786440 | tf_op jit(solution)/shard_map/ppermute | solution.py:19
  58.5 16.7 %collective-permute-start.17 = (bf16[16,32,256]{2,1,0:T(8,128)(2,1)S(1)}, bf16[16,32,256]{2,1,0:T(8,128)(2,1)S(1)}, u32[]{:S(2)}, u32[]{:S(2)}) collective-permute-start(bf16[16,32,256]{2,1,0:T(8,128)(2,1)S(1)} %collective-permute-done.13.a_ref), channel_id=1, source_target_pairs={{0,32},{32,64},{64,96},{96,0},{1,33},{33,65},{65,97},{97,1},{2,34}... | collective-permute-start | bytes 786440 | tf_op jit(solution)/shard_map/ppermute | solution.py:19
  58.5 16.7 %collective-permute-start.18 = (bf16[16,32,256]{2,1,0:T(8,128)(2,1)S(1)}, bf16[16,32,256]{2,1,0:T(8,128)(2,1)S(1)}, u32[]{:S(2)}, u32[]{:S(2)}) collective-permute-start(bf16[16,32,256]{2,1,0:T(8,128)(2,1)S(1)} %collective-permute-done.14.b_ref), channel_id=1, source_target_pairs={{0,96},{32,0},{64,32},{96,64},{1,97},{33,1},{65,33},{97,65},{2,98}... | collective-permute-start | bytes 786440 | tf_op jit(solution)/shard_map/ppermute | solution.py:19
  64.8 12.3 %collective-permute-start.22 = (bf16[4,288,256]{2,1,0:T(8,128)(2,1)S(1)}, bf16[4,288,256]{2,1,0:T(8,128)(2,1)S(1)}, u32[]{:S(2)}, u32[]{:S(2)}) collective-permute-start(bf16[4,288,256]{2,1,0:T(8,128)(2,1)S(1)} %get-tuple-element.58), channel_id=1, source_target_pairs={{0,16},{16,0},{1,17},{17,1},{2,18},{18,2},{3,19},{19,3},{4,20},{20... | collective-permute-start | bytes 1769480 | tf_op jit(solution)/shard_map/ppermute | solution.py:19
  77.2 6.2 %collective-permute-start.23 = (bf16[288,256]{1,0:T(8,128)(2,1)S(1)}, bf16[288,256]{1,0:T(8,128)(2,1)S(1)}, u32[]{:S(2)}, u32[]{:S(2)}) collective-permute-start(bf16[288,256]{1,0:T(8,128)(2,1)S(1)} %get-tuple-element.60), channel_id=1, source_target_pairs={{0,32},{32,64},{64,96},{96,0},{1,33},{33,65},{65,97},{97,1},{2,34}... | collective-permute-start | bytes 442376 | tf_op jit(solution)/shard_map/ppermute | solution.py:19
  77.3 6.1 %collective-permute-start.24 = (bf16[288,256]{1,0:T(8,128)(2,1)S(1)}, bf16[288,256]{1,0:T(8,128)(2,1)S(1)}, u32[]{:S(2)}, u32[]{:S(2)}) collective-permute-start(bf16[288,256]{1,0:T(8,128)(2,1)S(1)} %get-tuple-element.61), channel_id=1, source_target_pairs={{0,96},{32,0},{64,32},{96,64},{1,97},{33,1},{65,33},{97,65},{2,98}... | collective-permute-start | bytes 442376 | tf_op jit(solution)/shard_map/ppermute | solution.py:19
  80.0 6.0 %collective-permute-start.25 = (bf16[288,256]{1,0:T(8,128)(2,1)S(1)}, bf16[288,256]{1,0:T(8,128)(2,1)S(1)}, u32[]{:S(2)}, u32[]{:S(2)}) collective-permute-start(bf16[288,256]{1,0:T(8,128)(2,1)S(1)} %get-tuple-element.62), channel_id=1, source_target_pairs={{0,64},{32,96},{64,0},{96,32},{1,65},{33,97},{65,1},{97,33},{2,66}... | collective-permute-start | bytes 442376 | tf_op jit(solution)/shard_map/ppermute | solution.py:19
  111.5 4.6 %collective-permute-start.28 = (bf16[90,256]{1,0:T(8,128)(2,1)S(1)}, bf16[90,256]{1,0:T(8,128)(2,1)S(1)}, u32[]{:S(2)}, u32[]{:S(2)}) collective-permute-start(bf16[90,256]{1,0:T(8,128)(2,1)S(1)} %reduce_sum.12.a_ref), channel_id=1, source_target_pairs={{0,8},{4,12},{8,0},{12,4},{1,9},{5,13},{9,1},{13,5},{2,10},{6,14},... | collective-permute-start | bytes 138248 | tf_op jit(solution)/shard_map/ppermute | solution.py:19
  116.2 6.2 %collective-permute-start.31 = (bf16[360,256]{1,0:T(8,128)(2,1)S(1)}, bf16[360,256]{1,0:T(8,128)(2,1)S(1)}, u32[]{:S(2)}, u32[]{:S(2)}) collective-permute-start(bf16[360,256]{1,0:T(8,128)(2,1)S(1)} %order_pieces.1.a_ref), channel_id=1, source_target_pairs={{0,2},{1,3},{2,0},{3,1},{4,6},{5,7},{6,4},{7,5},{8,10},{9,11},{10,... | collective-permute-start | bytes 552968 | tf_op jit(solution)/shard_map/ppermute | solution.py:19
  117.6 5.8 %collective-permute-start.30 = (bf16[360,256]{1,0:T(8,128)(2,1)S(1)}, bf16[360,256]{1,0:T(8,128)(2,1)S(1)}, u32[]{:S(2)}, u32[]{:S(2)}) collective-permute-start(bf16[360,256]{1,0:T(8,128)(2,1)S(1)} %order_pieces.1.a_ref), channel_id=1, source_target_pairs={{0,3},{1,0},{2,1},{3,2},{4,7},{5,4},{6,5},{7,6},{8,11},{9,8},{10,9... | collective-permute-start | bytes 552968 | tf_op jit(solution)/shard_map/ppermute | solution.py:19
  119.2 5.6 %collective-permute-start.29 = (bf16[360,256]{1,0:T(8,128)(2,1)S(1)}, bf16[360,256]{1,0:T(8,128)(2,1)S(1)}, u32[]{:S(2)}, u32[]{:S(2)}) collective-permute-start(bf16[360,256]{1,0:T(8,128)(2,1)S(1)} %order_pieces.1.a_ref), channel_id=1, source_target_pairs={{0,1},{1,2},{2,3},{3,0},{4,5},{5,6},{6,7},{7,4},{8,9},{9,10},{10,1... | collective-permute-start | bytes 552968 | tf_op jit(solution)/shard_map/ppermute | solution.py:19
  124.8 5.7 %collective-permute-start.32 = (bf16[4,72,256]{2,1,0:T(8,128)(2,1)S(1)}, bf16[4,72,256]{2,1,0:T(8,128)(2,1)S(1)}, u32[]{:S(2)}, u32[]{:S(2)}) collective-permute-start(bf16[4,72,256]{2,1,0:T(8,128)(2,1)S(1)} %get-tuple-element.74), channel_id=1, source_target_pairs={{0,32},{32,64},{64,96},{96,0},{1,33},{33,65},{65,97},{97,1},{2,34}... | collective-permute-start | bytes 442376 | tf_op jit(solution)/shard_map/ppermute | solution.py:19
  125.8 4.8 %collective-permute-start.33 = (bf16[4,72,256]{2,1,0:T(8,128)(2,1)S(1)}, bf16[4,72,256]{2,1,0:T(8,128)(2,1)S(1)}, u32[]{:S(2)}, u32[]{:S(2)}) collective-permute-start(bf16[4,72,256]{2,1,0:T(8,128)(2,1)S(1)} %get-tuple-element.74), channel_id=1, source_target_pairs={{0,96},{32,0},{64,32},{96,64},{1,97},{33,1},{65,33},{97,65},{2,98}... | collective-permute-start | bytes 442376 | tf_op jit(solution)/shard_map/ppermute | solution.py:19
  127.8 5.5 %collective-permute-start.34 = (bf16[4,72,256]{2,1,0:T(8,128)(2,1)S(1)}, bf16[4,72,256]{2,1,0:T(8,128)(2,1)S(1)}, u32[]{:S(2)}, u32[]{:S(2)}) collective-permute-start(bf16[4,72,256]{2,1,0:T(8,128)(2,1)S(1)} %get-tuple-element.74), channel_id=1, source_target_pairs={{0,64},{32,96},{64,0},{96,32},{1,65},{33,97},{65,1},{97,33},{2,66}... | collective-permute-start | bytes 442376 | tf_op jit(solution)/shard_map/ppermute | solution.py:19
  133.3 9.5 %collective-permute-start.35 = (bf16[4,4,72,256]{3,2,1,0:T(8,128)(2,1)S(1)}, bf16[4,4,72,256]{3,2,1,0:T(8,128)(2,1)S(1)}, u32[]{:S(2)}, u32[]{:S(2)}) collective-permute-start(bf16[4,4,72,256]{3,2,1,0:T(8,128)(2,1)S(1)} %pad_maximum_fusion.1.near_ref), channel_id=1, source_target_pairs={{0,16},{16,0},{1,17},{17,1},{2,18},{18,2},{3,19},{19,3},{4,20},{20... | collective-permute-start | bytes 1769480 | tf_op jit(solution)/shard_map/ppermute | solution.py:19
  (7 other events, 32.3 us)

commit v8 on v7

--- a/solution.py
+++ b/solution.py
@@ -240,10 +240,7 @@
     )(tile, left, right, edges, kernel)
 
 
-def second_kernel(
-    chips, hid_ref, edge_ref, kernel_ref, cot_ref,
-    out_ref, near_ref, far_ref, wide_ref, pad_ref, sum_ref,
-):
+def second_kernel(chips, hid_ref, edge_ref, cot_ref, wide_ref, near_ref, far_ref, pad_ref, sum_ref):
     chans = hid_ref.shape[2]
     cols, rows, outs = cot_ref.shape
     width = wide_ref.shape[0]
@@ -253,10 +250,6 @@
     ]
     spread_tile(columns, wide_ref)
     wide_ref[cols + 2 :] = jnp.zeros((width - cols - 2, rows, 3 * chans), BF16)
-    pieces = [wide_ref[tap : tap + cols] for tap in range(3)]
-    lhs = jnp.concatenate(pieces, axis=-1).reshape(cols * rows, 9 * chans)
-    total = jnp.dot(lhs, kernel_ref[...], preferred_element_type=F32)
-    out_ref[...] = total.reshape(cols, rows, outs).astype(BF16)
 
     pad_ref[0:2] = jnp.zeros((2, rows, outs), BF16)
     pad_ref[2 : 2 + cols] = cot_ref[...]
@@ -281,7 +274,7 @@
                 ].astype(ref.dtype)
 
 
-def second_tile(tile, edges, kernel, cotangent, chips):
+def second_tile(tile, edges, cotangent, chips):
     chans = tile.shape[2]
     cols, rows, outs = cotangent.shape
     width = cols + 8
@@ -289,25 +282,48 @@
     return pl.pallas_call(
         functools.partial(second_kernel, chips),
         out_shape=(
-            jax.ShapeDtypeStruct((cols, rows, outs), BF16),
+            jax.ShapeDtypeStruct((width, rows, 3 * chans), BF16),
             jax.ShapeDtypeStruct(cut, F32),
             jax.ShapeDtypeStruct(cut, BF16),
         ),
-        in_specs=[VMEM_SPEC] * 4,
+        in_specs=[VMEM_SPEC] * 3,
         out_specs=(VMEM_SPEC,) * 3,
         scratch_shapes=[
-            pltpu.VMEM((width, rows, 3 * chans), BF16),
             pltpu.VMEM((width + 2, rows, outs), BF16),
             pltpu.VMEM((3 * chans, 3 * outs), F32),
         ],
         compiler_params=pltpu.CompilerParams(vmem_limit_bytes=9 * 2**20),
         cost_estimate=QUICK,
         name="second",
-    )(tile, edges, kernel.reshape(9 * chans, outs), cotangent)
-
-
-def point_kernel(own_ref, a0_ref, a1_ref, b0_ref, b1_ref, back_ref, da_ref, db_ref, hidden_ref):
-    cols = own_ref.shape[0]
+    )(tile, edges, cotangent)
+
+
+def features_kernel(wide_ref, kernel_ref, out_ref):
+    cols, rows, outs = out_ref.shape
+    pieces = [wide_ref[tap : tap + cols] for tap in range(3)]
+    lhs = jnp.concatenate(pieces, axis=-1).reshape(cols * rows, -1)
+    total = jnp.dot(lhs, kernel_ref[...], preferred_element_type=F32)
+    out_ref[...] = total.reshape(cols, rows, outs).astype(BF16)
+
+
+def features_tile(wide, kernel, cols):
+    rows, outs = wide.shape[1], kernel.shape[3]
+    return pl.pallas_call(
+        features_kernel,
+        out_shape=jax.ShapeDtypeStruct((cols, rows, outs), BF16),
+        in_specs=[VMEM_SPEC] * 2,
+        out_specs=VMEM_SPEC,
+        compiler_params=pltpu.CompilerParams(vmem_limit_bytes=4 * 2**20),
+        cost_estimate=QUICK,
+        name="features",
+    )(wide, kernel.reshape(-1, outs))
+
+
+def point_kernel(
+    own_ref, a0_ref, a1_ref, b0_ref, b1_ref, back_ref,
+    da_ref, db_ref, hidden_ref, last_ref, first_ref,
+):
+    cols, rows, _ = own_ref.shape
     half = da_ref.shape[0]
     strip = 2 * lax.axis_index("y") + lax.axis_index("c")
     strips = 2 * lax.axis_size("y")
@@ -318,7 +334,10 @@
         hidden = pre * sigma
         if keep is not None:
             hidden = jnp.where(keep, hidden, 0.0)
-        hidden_ref[j] = hidden.astype(BF16)
+        hidden = hidden.astype(BF16)
+        hidden_ref[j] = hidden
+        last_ref[j : j + 1, :] = hidden[rows - 1 :]
+        first_ref[j : j + 1, :] = hidden[:1]
         if keep is None:
             slope = sigma * (1.0 + pre * (1.0 - sigma))
             at = j - 1 if delta_ref is da_ref else j - 1 - half
@@ -328,21 +347,20 @@
     column(0, 0, left, None, strip > 0)
     column(cols - 1, half, right, None, strip < strips - 1)
 
-    def each(i, _):
+    for i in range(1, half + 1):
         column(i, i, left, da_ref, None)
         column(half + i, i - 1, right, db_ref, None)
-
-    lax.fori_loop(1, half + 1, each, None)
 
 
 def point(own, left, right, back):
     strip, rows, outs = back.shape
     cut = jax.ShapeDtypeStruct((strip // 2, rows, outs), BF16)
+    edge = jax.ShapeDtypeStruct((strip + 2, outs), BF16)
     return pl.pallas_call(
         point_kernel,
-        out_shape=(cut, cut, jax.ShapeDtypeStruct(own.shape, BF16)),
+        out_shape=(cut, cut, jax.ShapeDtypeStruct(own.shape, BF16), edge, edge),
         in_specs=[VMEM_SPEC] * 6,
-        out_specs=(VMEM_SPEC,) * 3,
+        out_specs=(VMEM_SPEC,) * 5,
         compiler_params=pltpu.CompilerParams(vmem_limit_bytes=2 * 2**20),
         cost_estimate=QUICK,
         name="point",
@@ -557,17 +575,17 @@
     from_b = shift(near_b, "y", on), shift(both_b, "y", off)
 
     back = back_tile(cotangent, left, right, edges, weight_second)
-    delta_a, delta_b, hidden = point(own, from_a, from_b, back)
+    delta_a, delta_b, hidden, *ends = point(own, from_a, from_b, back)
 
     on_a, off_b = shift(delta_a, "y", on), shift(delta_b, "y", off)
-    edges = row_halo([hidden[:, rows - 1], hidden[:, 0]])
-    on_a, off_b, edges, late_a, late_b = lax.optimization_barrier(
-        (on_a, off_b, edges, delta_a, delta_b)
+    edges = row_halo(ends)
+    total = grad_strip(0, wide, (delta_a, delta_b), None, False)
+    on_a, off_b, edges, late_a, late_b, total = lax.optimization_barrier(
+        (on_a, off_b, edges, delta_a, delta_b, total)
     )
     on_b, off_a = shift(late_b, "y", on), shift(late_a, "y", off)
     fwd_a, fwd_b = shift(on_a, "y", on), shift(off_b, "y", off)
-    total = grad_strip(0, wide, (delta_a, delta_b), None, False)
-    features, near, far = second_tile(hidden, edges, weight_second, cotangent, chips)
+    wide_hidden, near, far = second_tile(hidden, edges, cotangent, chips)
     far, on_b, off_a = lax.optimization_barrier((far, on_b, off_a))
     keep, *sends = fold(near, shift(far, "c", 1))
     got = [shift(send, "y", step) for step, send in zip(STEPS[1:], sends)]
@@ -583,7 +601,9 @@
     parts = gather_steps(order_pieces(gather_steps(summed, "z"), extra), "x")
     main = parts[0].shape[0] - sz * extra
     grad_first = lay_first(parts, sz, chans)
+    features = features_tile(wide_hidden, weight_second, strip)
     share = jnp.stack([part[main:] for part in parts])
+    share, features = lax.optimization_barrier((share, features))
     share = jnp.stack(gather_steps(share, "y"))
     grad_second = lay_second(share, shift(share, "c", 1)).reshape(3, 3, outs, outs)
     return features, grad_first, grad_second

time: 145 us -> 144 us (level)
  waiting for transfers between devices: 35.3 us -> 33 us
    pallas_call x0 -> x1, Pallas kernels: none -> 2.18 us  [features_tile(): pl.pallas_call(features_kernel, out_shape=jax.ShapeDtypeStruct((cols, row...]
    ppermute x2, waiting for transfers between devices: 7.06 us -> 5.31 us  [row_halo(): lax.ppermute(ends[1], SKY, down)]
  transfers between devices with their start and end apart: 36 -> 36, of which waited for: 16 -> 16; matrix products, arithmetic and copies ran while one was open for 3% -> 3% of each run, Pallas kernels for 12% -> 13%
where the time goes in v8:
time: 144 us
  starting transfers between devices  57.1 us (40%)
  waiting for transfers between devices  33 us (23%)
  Pallas kernels  24.3 us (17%)
  blocking collectives  22.7 us (16%)
  local copies, waits for them, and re-layouts  3.23 us (2%)
  other arithmetic  2.55 us (2%)
    ppermute x30, starting transfers between devices, shift(): lax.ppermute(x, axis, [(i, (i + step) % count) for i in range(count)])  43.8 us
    ppermute x30, waiting for transfers between devices, shift(): lax.ppermute(x, axis, [(i, (i + step) % count) for i in range(count)])  27.5 us
    all_to_all x1, blocking collectives, body(): summed = lax.all_to_all(joined, SKY, 0, 0, tiled=True)  22.7 us
    pallas_call x4, Pallas kernels, grad_strip(): pl.pallas_call(functools.partial(grad_kernel, step, old is not None, last...  7.02 us
    ppermute x2, starting transfers between devices, row_halo(): lax.ppermute(ends[0], SKY, up)  6.31 us
    pallas_call x4, Pallas kernels, conv_parts(): pl.pallas_call(functools.partial(conv_kernel, parts, len(adds)), out_shap...  5.85 us
    ppermute x2, waiting for transfers between devices, row_halo(): lax.ppermute(ends[1], SKY, down)  5.31 us
  transfers between devices with their start and end apart: 36, of which 16 were waited for; matrix products, arithmetic and copies ran while one was open for 3% of the time, Pallas kernels for 13%

profile of v8, /device:TPU:1, one launch (start us, length us, event | category | flops | bytes accessed | tf_op | source)
XLA Modules:
  0.0 143.8 jit_solution(2552042899459370841)
XLA Ops:
  4.6 3.2 %collective-permute-start.1 = (bf16[320,128]{1,0:T(8,128)(2,1)S(1)}, bf16[320,128]{1,0:T(8,128)(2,1)S(1)}, u32[]{:S(2)}, u32[]{:S(2)}) collective-permute-start(bf16[320,128]{1,0:T(8,128)(2,1)S(1)} %pad_maximum_fusion.4), channel_id=1, source_target_pairs={{0,1},{1,2},{2,3},{3,4},{4,5},{5,6},{6,7},{7,8},{8,9},{9,10},{10,1... | collective-permute-start | bytes 245768 | tf_op jit(solution)/shard_map/ppermute | solution.py:396
  10.4 3.8 %collective-permute-done.2 = bf16[320,128]{1,0:T(8,128)(2,1)S(1)} collective-permute-done((bf16[320,128]{1,0:T(8,128)(2,1)S(1)}, bf16[320,128]{1,0:T(8,128)(2,1)S(1)}, u32[]{:S(2)}, u32[]{:S(2)}) %collective-permute-start.2) | collective-permute-done | bytes 81952 | tf_op jit(solution)/shard_map/ppermute | solution.py:396
  16.4 1.9 %spread.1.wide_ref = bf16[4,40,32,768]{3,2,1,0:T(8,128)(2,1)S(1)} custom-call(bf16[256,32,128]{2,1,0:T(8,128)(2,1)S(1)} %copy-done.1, bf16[256,32,128]{2,1,0:T(8,128)(2,1)S(1)} %collective-permute-done.far_ref, bf16[2,320,128]{2,1,0:T(8,128)(2,1)S(1)} %pad_maximum_fusion.2.own_halo_ref.edge_ref, bf16[2,320,128]{2,1,0:T(8,128)(2,1)S(1)} %collective-permute-done.3.far_halo_ref), custom_call_target="tpu_custom_call" | custom-call | flops 1 | bytes 1 | tf_op jit(solution)/shard_map/spread/pallas_call | solution.py:94
  22.7 2.5 %collective-permute-start.6 = (bf16[34,256]{1,0:T(8,128)(2,1)S(1)}, bf16[34,256]{1,0:T(8,128)(2,1)S(1)}, u32[]{:S(2)}, u32[]{:S(2)}) collective-permute-start(bf16[34,256]{1,0:T(8,128)(2,1)S(1)} %maximum_maximum_fusion), channel_id=1, source_target_pairs={{0,16},{16,32},{32,48},{48,64},{64,80},{80,96},{96,112},{1,17},{17... | collective-permute-start | bytes 52232 | tf_op jit(solution)/shard_map/ppermute | solution.py:562
  25.2 1.9 %collective-permute-start.7 = (bf16[34,256]{1,0:T(8,128)(2,1)S(1)}, bf16[34,256]{1,0:T(8,128)(2,1)S(1)}, u32[]{:S(2)}, u32[]{:S(2)}) collective-permute-start(bf16[34,256]{1,0:T(8,128)(2,1)S(1)} %maximum_maximum_fusion.1), channel_id=1, source_target_pairs={{16,0},{32,16},{48,32},{64,48},{80,64},{96,80},{112,96},{17,1},{33... | collective-permute-start | bytes 52232 | tf_op jit(solution)/shard_map/ppermute | solution.py:563
  31.8 2.7 %collective-permute-start.12 = (bf16[17,32,256]{2,1,0:T(8,128)(2,1)S(1)}, bf16[17,32,256]{2,1,0:T(8,128)(2,1)S(1)}, u32[]{:S(2)}, u32[]{:S(2)}) collective-permute-start(bf16[17,32,256]{2,1,0:T(8,128)(2,1)S(1)} %get-tuple-element.45), channel_id=1, source_target_pairs={{0,96},{32,0},{64,32},{96,64},{1,97},{33,1},{65,33},{97,65},{2,98}... | collective-permute-start | bytes 835592 | tf_op jit(solution)/shard_map/ppermute | solution.py:19
  37.6 5.2 %collective-permute-done.12.b1_ref = bf16[17,32,256]{2,1,0:T(8,128)(2,1)S(1)} collective-permute-done((bf16[17,32,256]{2,1,0:T(8,128)(2,1)S(1)}, bf16[17,32,256]{2,1,0:T(8,128)(2,1)S(1)}, u32[]{:S(2)}, u32[]{:S(2)}) %collective-permute-start.12) | collective-permute-done | bytes 278560 | tf_op jit(solution)/shard_map/ppermute | solution.py:19
  45.0 2.7 %collective-permute-start.14 = (bf16[16,32,256]{2,1,0:T(8,128)(2,1)S(1)}, bf16[16,32,256]{2,1,0:T(8,128)(2,1)S(1)}, u32[]{:S(2)}, u32[]{:S(2)}) collective-permute-start(bf16[16,32,256]{2,1,0:T(8,128)(2,1)S(1)} %get-tuple-element.57.b_ref), channel_id=1, source_target_pairs={{0,96},{32,0},{64,32},{96,64},{1,97},{33,1},{65,33},{97,65},{2,98}... | collective-permute-start | bytes 786440 | tf_op jit(solution)/shard_map/ppermute | solution.py:19
  47.7 3.1 %collective-permute-start.15 = (bf16[34,256]{1,0:T(8,128)(2,1)S(1)}, bf16[34,256]{1,0:T(8,128)(2,1)S(1)}, u32[]{:S(2)}, u32[]{:S(2)}) collective-permute-start(bf16[34,256]{1,0:T(8,128)(2,1)S(1)} %get-tuple-element.50), channel_id=1, source_target_pairs={{0,1},{1,2},{2,3},{3,4},{4,5},{5,6},{6,7},{7,8},{8,9},{9,10},{10,1... | collective-permute-start | bytes 52232 | tf_op jit(solution)/shard_map/ppermute | solution.py:396
  52.1 1.7 %grad_first.4.refs_0_ = f32[768,768]{1,0:T(8,128)S(1)} custom-call(bf16[4,40,32,768]{3,2,1,0:T(8,128)(2,1)S(1)} %spread.1.wide_ref, bf16[16,32,256]{2,1,0:T(8,128)(2,1)S(1)} %get-tuple-element.58.a_ref, bf16[16,32,256]{2,1,0:T(8,128)(2,1)S(1)} %get-tuple-element.57.b_ref), custom_call_target="tpu_custom_call" | custom-call | flops 1 | bytes 1 | tf_op jit(solution)/shard_map/grad_first/pallas_call | solution.py:175
  55.6 2.7 %collective-permute-start.20 = (bf16[16,32,256]{2,1,0:T(8,128)(2,1)S(1)}, bf16[16,32,256]{2,1,0:T(8,128)(2,1)S(1)}, u32[]{:S(2)}, u32[]{:S(2)}) collective-permute-start(bf16[16,32,256]{2,1,0:T(8,128)(2,1)S(1)} %get-tuple-element.58.a_ref), channel_id=1, source_target_pairs={{0,96},{32,0},{64,32},{96,64},{1,97},{33,1},{65,33},{97,65},{2,98}... | collective-permute-start | bytes 786440 | tf_op jit(solution)/shard_map/ppermute | solution.py:19
  58.2 2.7 %collective-permute-start.18 = (bf16[16,32,256]{2,1,0:T(8,128)(2,1)S(1)}, bf16[16,32,256]{2,1,0:T(8,128)(2,1)S(1)}, u32[]{:S(2)}, u32[]{:S(2)}) collective-permute-start(bf16[16,32,256]{2,1,0:T(8,128)(2,1)S(1)} %collective-permute-done.14.b_ref), channel_id=1, source_target_pairs={{0,96},{32,0},{64,32},{96,64},{1,97},{33,1},{65,33},{97,65},{2,98}... | collective-permute-start | bytes 786440 | tf_op jit(solution)/shard_map/ppermute | solution.py:19
  60.9 2.2 %second.1 = (bf16[40,32,768]{2,1,0:T(8,128)(2,1)S(1)}, f32[4,288,256]{2,1,0:T(8,128)S(1)}, bf16[4,288,256]{2,1,0:T(8,128)(2,1)S(1)}) custom-call(bf16[34,32,256]{2,1,0:T(8,128)(2,1)S(1)} %get-tuple-element.54.hid_ref, bf16[2,34,256]{2,1,0:T(8,128)(2,1)S(1)} %pad_maximum_fusion.6.edge_ref, bf16[32,32,256]{2,1,0:T(8,128)(2,1)S(1)} %copy-done.2), custom_call_target="tpu_custom_call" | custom-call | flops 1 | bytes 1 | tf_op jit(solution)/shard_map/second/pallas_call | solution.py:282
  63.2 5.3 %collective-permute-start.22 = (bf16[4,288,256]{2,1,0:T(8,128)(2,1)S(1)}, bf16[4,288,256]{2,1,0:T(8,128)(2,1)S(1)}, u32[]{:S(2)}, u32[]{:S(2)}) collective-permute-start(bf16[4,288,256]{2,1,0:T(8,128)(2,1)S(1)} %get-tuple-element.65), channel_id=1, source_target_pairs={{0,16},{16,0},{1,17},{17,1},{2,18},{18,2},{3,19},{19,3},{4,20},{20... | collective-permute-start | bytes 1769480 | tf_op jit(solution)/shard_map/ppermute | solution.py:19
  68.4 1.8 %grad_first.5.refs_0_ = f32[768,768]{1,0:T(8,128)S(1)} custom-call(bf16[4,40,32,768]{3,2,1,0:T(8,128)(2,1)S(1)} %spread.1.wide_ref, bf16[16,32,256]{2,1,0:T(8,128)(2,1)S(1)} %collective-permute-done.13.a_ref, bf16[16,32,256]{2,1,0:T(8,128)(2,1)S(1)} %collective-permute-done.19.b_ref, f32[768,768]{1,0:T(8,128)S(1)} %grad_first.4.refs_0_), custom_call_target="tpu_custom_call" | custom-call | flops 1 | bytes 1 | tf_op jit(solution)/shard_map/grad_first/pallas_call | solution.py:175
  70.2 1.8 %grad_first.6.refs_0_ = f32[768,768]{1,0:T(8,128)S(1)} custom-call(bf16[4,40,32,768]{3,2,1,0:T(8,128)(2,1)S(1)} %spread.1.wide_ref, bf16[16,32,256]{2,1,0:T(8,128)(2,1)S(1)} %collective-permute-done.20.a_ref, bf16[16,32,256]{2,1,0:T(8,128)(2,1)S(1)} %collective-permute-done.14.b_ref, f32[768,768]{1,0:T(8,128)S(1)} %grad_first.5.refs_0_), custom_call_target="tpu_custom_call" | custom-call | flops 1 | bytes 1 | tf_op jit(solution)/shard_map/grad_first/pallas_call | solution.py:175
  72.0 1.8 %grad_first.7 = (f32[384,768]{1,0:T(8,128)S(1)}, bf16[384,768]{1,0:T(8,128)(2,1)S(1)}) custom-call(bf16[4,40,32,768]{3,2,1,0:T(8,128)(2,1)S(1)} %spread.1.wide_ref, bf16[16,32,256]{2,1,0:T(8,128)(2,1)S(1)} %collective-permute-done.17.a_ref, bf16[16,32,256]{2,1,0:T(8,128)(2,1)S(1)} %collective-permute-done.18.b_ref, f32[768,768]{1,0:T(8,128)S(1)} %grad_first.6.refs_0_), custom_call_target="tpu_custom_call" | custom-call | flops 1 | bytes 1 | tf_op jit(solution)/shard_map/grad_first/pallas_call | solution.py:175
  74.1 2.7 %collective-permute-start.24 = (bf16[288,256]{1,0:T(8,128)(2,1)S(1)}, bf16[288,256]{1,0:T(8,128)(2,1)S(1)}, u32[]{:S(2)}, u32[]{:S(2)}) collective-permute-start(bf16[288,256]{1,0:T(8,128)(2,1)S(1)} %get-tuple-element.68), channel_id=1, source_target_pairs={{0,96},{32,0},{64,32},{96,64},{1,97},{33,1},{65,33},{97,65},{2,98}... | collective-permute-start | bytes 442376 | tf_op jit(solution)/shard_map/ppermute | solution.py:19
  77.8 2.4 %collective-permute-done.23.a_ref = bf16[288,256]{1,0:T(8,128)(2,1)S(1)} collective-permute-done((bf16[288,256]{1,0:T(8,128)(2,1)S(1)}, bf16[288,256]{1,0:T(8,128)(2,1)S(1)}, u32[]{:S(2)}, u32[]{:S(2)}) %collective-permute-start.23) | collective-permute-done | bytes 147488 | tf_op jit(solution)/shard_map/ppermute | solution.py:19
  80.2 4.2 %collective-permute-done.25.c_ref = bf16[288,256]{1,0:T(8,128)(2,1)S(1)} collective-permute-done((bf16[288,256]{1,0:T(8,128)(2,1)S(1)}, bf16[288,256]{1,0:T(8,128)(2,1)S(1)}, u32[]{:S(2)}, u32[]{:S(2)}) %collective-permute-start.25) | collective-permute-done | bytes 147488 | tf_op jit(solution)/shard_map/ppermute | solution.py:19
  84.6 22.7 %all_to_all.5 = bf16[16,90,256]{2,1,0:T(8,128)(2,1)} all-to-all(bf16[16,90,256]{2,1,0:T(8,128)(2,1)S(1)} %join.1), channel_id=1, replica_groups=mesh['y'=4,'c'=2,'z'=4,'x'=4] {'z','x'}, dimensions={0} | all-to-all | bytes 1474560 | tf_op jit(solution)/shard_map/all_to_all | solution.py:599
  108.7 2.7 %collective-permute-start.27 = (bf16[90,256]{1,0:T(8,128)(2,1)S(1)}, bf16[90,256]{1,0:T(8,128)(2,1)S(1)}, u32[]{:S(2)}, u32[]{:S(2)}) collective-permute-start(bf16[90,256]{1,0:T(8,128)(2,1)S(1)} %reduce_sum.12.a_ref), channel_id=1, source_target_pairs={{0,12},{4,0},{8,4},{12,8},{1,13},{5,1},{9,5},{13,9},{2,14},{6,2},{... | collective-permute-start | bytes 138248 | tf_op jit(solution)/shard_map/ppermute | solution.py:19
  111.3 2.2 %features.1 = bf16[32,32,256]{2,1,0:T(8,128)(2,1)} custom-call(bf16[40,32,768]{2,1,0:T(8,128)(2,1)S(1)} %get-tuple-element.70.wide_ref, bf16[2304,256]{1,0:T(8,128)(2,1)S(1)} %bitcast.57), custom_call_target="tpu_custom_call" | custom-call | flops 1 | bytes 1 | tf_op jit(solution)/shard_map/features/pallas_call | solution.py:311
  113.5 2.3 %collective-permute-done.28.d_ref = bf16[90,256]{1,0:T(8,128)(2,1)S(1)} collective-permute-done((bf16[90,256]{1,0:T(8,128)(2,1)S(1)}, bf16[90,256]{1,0:T(8,128)(2,1)S(1)}, u32[]{:S(2)}, u32[]{:S(2)}) %collective-permute-start.28) | collective-permute-done | bytes 46112 | tf_op jit(solution)/shard_map/ppermute | solution.py:19
  117.0 2.0 %collective-permute-start.30 = (bf16[360,256]{1,0:T(8,128)(2,1)S(1)}, bf16[360,256]{1,0:T(8,128)(2,1)S(1)}, u32[]{:S(2)}, u32[]{:S(2)}) collective-permute-start(bf16[360,256]{1,0:T(8,128)(2,1)S(1)} %order_pieces.1.a_ref), channel_id=1, source_target_pairs={{0,3},{1,0},{2,1},{3,2},{4,7},{5,4},{6,5},{7,6},{8,11},{9,8},{10,9... | collective-permute-start | bytes 552968 | tf_op jit(solution)/shard_map/ppermute | solution.py:19
  119.0 2.8 %collective-permute-done.31.d_ref = bf16[360,256]{1,0:T(8,128)(2,1)S(1)} collective-permute-done((bf16[360,256]{1,0:T(8,128)(2,1)S(1)}, bf16[360,256]{1,0:T(8,128)(2,1)S(1)}, u32[]{:S(2)}, u32[]{:S(2)}) %collective-permute-start.31) | collective-permute-done | bytes 184352 | tf_op jit(solution)/shard_map/ppermute | solution.py:19
  122.1 2.6 %collective-permute-done.29.b_ref = bf16[360,256]{1,0:T(8,128)(2,1)S(1)} collective-permute-done((bf16[360,256]{1,0:T(8,128)(2,1)S(1)}, bf16[360,256]{1,0:T(8,128)(2,1)S(1)}, u32[]{:S(2)}, u32[]{:S(2)}) %collective-permute-start.29) | collective-permute-done | bytes 184352 | tf_op jit(solution)/shard_map/ppermute | solution.py:19
  124.7 2.7 %collective-permute-start.33 = (bf16[4,72,256]{2,1,0:T(8,128)(2,1)S(1)}, bf16[4,72,256]{2,1,0:T(8,128)(2,1)S(1)}, u32[]{:S(2)}, u32[]{:S(2)}) collective-permute-start(bf16[4,72,256]{2,1,0:T(8,128)(2,1)S(1)} %pad_maximum_fusion.3), channel_id=1, source_target_pairs={{0,96},{32,0},{64,32},{96,64},{1,97},{33,1},{65,33},{97,65},{2,98}... | collective-permute-start | bytes 442376 | tf_op jit(solution)/shard_map/ppermute | solution.py:19
  127.4 2.6 %collective-permute-done.32 = bf16[4,72,256]{2,1,0:T(8,128)(2,1)S(1)} collective-permute-done((bf16[4,72,256]{2,1,0:T(8,128)(2,1)S(1)}, bf16[4,72,256]{2,1,0:T(8,128)(2,1)S(1)}, u32[]{:S(2)}, u32[]{:S(2)}) %collective-permute-start.32) | collective-permute-done | bytes 147488 | tf_op jit(solution)/shard_map/ppermute | solution.py:19
  131.1 1.8 %collective-permute-done.34 = bf16[4,72,256]{2,1,0:T(8,128)(2,1)S(1)} collective-permute-done((bf16[4,72,256]{2,1,0:T(8,128)(2,1)S(1)}, bf16[4,72,256]{2,1,0:T(8,128)(2,1)S(1)}, u32[]{:S(2)}, u32[]{:S(2)}) %collective-permute-start.34) | collective-permute-done | bytes 147488 | tf_op jit(solution)/shard_map/ppermute | solution.py:19
  133.0 7.6 %collective-permute-start.35 = (bf16[4,4,72,256]{3,2,1,0:T(8,128)(2,1)S(1)}, bf16[4,4,72,256]{3,2,1,0:T(8,128)(2,1)S(1)}, u32[]{:S(2)}, u32[]{:S(2)}) collective-permute-start(bf16[4,4,72,256]{3,2,1,0:T(8,128)(2,1)S(1)} %pad_maximum_fusion.1.near_ref), channel_id=1, source_target_pairs={{0,16},{16,0},{1,17},{17,1},{2,18},{18,2},{3,19},{19,3},{4,20},{20... | collective-permute-start | bytes 1769480 | tf_op jit(solution)/shard_map/ppermute | solution.py:19
  142.2 1.7 %lay_second.1 = f32[2304,256]{1,0:T(8,128)} custom-call(bf16[4,4,72,256]{3,2,1,0:T(8,128)(2,1)S(1)} %pad_maximum_fusion.1.near_ref, bf16[4,4,72,256]{3,2,1,0:T(8,128)(2,1)S(1)} %collective-permute-done.35.far_ref), custom_call_target="tpu_custom_call" | custom-call | flops 1 | bytes 1 | tf_op jit(solution)/shard_map/lay_second/pallas_call | solution.py:517
  (88 shorter events, 33.1 us)
Async XLA Ops:
  0.6 15.8 %collective-permute-start = (bf16[256,32,128]{2,1,0:T(8,128)(2,1)}, bf16[256,32,128]{2,1,0:T(8,128)(2,1)S(1)}, u32[]{:S(2)}, u32[]{:S(2)}) collective-permute-start(bf16[256,32,128]{2,1,0:T(8,128)(2,1)} %own_ref.1), channel_id=1, source_target_pairs={{0,16},{16,0},{1,17},{17,1},{2,18},{18,2},{3,19},{19,3},{4,20},{20... | collective-permute-start | bytes 6291464 | tf_op jit(solution)/shard_map/ppermute | solution.py:19
  4.6 5.8 %collective-permute-start.1 = (bf16[320,128]{1,0:T(8,128)(2,1)S(1)}, bf16[320,128]{1,0:T(8,128)(2,1)S(1)}, u32[]{:S(2)}, u32[]{:S(2)}) collective-permute-start(bf16[320,128]{1,0:T(8,128)(2,1)S(1)} %pad_maximum_fusion.4), channel_id=1, source_target_pairs={{0,1},{1,2},{2,3},{3,4},{4,5},{5,6},{6,7},{7,8},{8,9},{9,10},{10,1... | collective-permute-start | bytes 245768 | tf_op jit(solution)/shard_map/ppermute | solution.py:396
  7.8 7.4 %collective-permute-start.4 = (bf16[3,3,128,256]{3,2,1,0:T(8,128)(2,1)}, bf16[3,3,128,256]{3,2,1,0:T(8,128)(2,1)S(1)}, u32[]{:S(2)}, u32[]{:S(2)}) collective-permute-start(bf16[3,3,128,256]{3,2,1,0:T(8,128)(2,1)} %param.5), channel_id=1, source_target_pairs={{0,16},{16,0},{1,17},{17,1},{2,18},{18,2},{3,19},{19,3},{4,20},{20... | collective-permute-start | bytes 1769480 | tf_op jit(solution)/shard_map/ppermute | solution.py:19
  8.4 5.9 %collective-permute-start.2 = (bf16[320,128]{1,0:T(8,128)(2,1)S(1)}, bf16[320,128]{1,0:T(8,128)(2,1)S(1)}, u32[]{:S(2)}, u32[]{:S(2)}) collective-permute-start(bf16[320,128]{1,0:T(8,128)(2,1)S(1)} %pad_maximum_fusion.5), channel_id=1, source_target_pairs={{1,0},{2,1},{3,2},{4,3},{5,4},{6,5},{7,6},{8,7},{9,8},{10,9},{11,1... | collective-permute-start | bytes 245768 | tf_op jit(solution)/shard_map/ppermute | solution.py:396
  19.8 10.5 %collective-permute-start.5 = (bf16[17,32,256]{2,1,0:T(8,128)(2,1)S(1)}, bf16[17,32,256]{2,1,0:T(8,128)(2,1)S(1)}, u32[]{:S(2)}, u32[]{:S(2)}) collective-permute-start(bf16[17,32,256]{2,1,0:T(8,128)(2,1)S(1)} %get-tuple-element.38), channel_id=1, source_target_pairs={{0,32},{32,64},{64,96},{96,0},{1,33},{33,65},{65,97},{97,1},{2,34}... | collective-permute-start | bytes 835592 | tf_op jit(solution)/shard_map/ppermute | solution.py:19
  21.2 9.2 %collective-permute-start.8 = (bf16[17,32,256]{2,1,0:T(8,128)(2,1)S(1)}, bf16[17,32,256]{2,1,0:T(8,128)(2,1)S(1)}, u32[]{:S(2)}, u32[]{:S(2)}) collective-permute-start(bf16[17,32,256]{2,1,0:T(8,128)(2,1)S(1)} %get-tuple-element.40), channel_id=1, source_target_pairs={{0,96},{32,0},{64,32},{96,64},{1,97},{33,1},{65,33},{97,65},{2,98}... | collective-permute-start | bytes 835592 | tf_op jit(solution)/shard_map/ppermute | solution.py:19
  22.7 7.5 %collective-permute-start.6 = (bf16[34,256]{1,0:T(8,128)(2,1)S(1)}, bf16[34,256]{1,0:T(8,128)(2,1)S(1)}, u32[]{:S(2)}, u32[]{:S(2)}) collective-permute-start(bf16[34,256]{1,0:T(8,128)(2,1)S(1)} %maximum_maximum_fusion), channel_id=1, source_target_pairs={{0,16},{16,32},{32,48},{48,64},{64,80},{80,96},{96,112},{1,17},{17... | collective-permute-start | bytes 52232 | tf_op jit(solution)/shard_map/ppermute | solution.py:562
  25.2 5.1 %collective-permute-start.7 = (bf16[34,256]{1,0:T(8,128)(2,1)S(1)}, bf16[34,256]{1,0:T(8,128)(2,1)S(1)}, u32[]{:S(2)}, u32[]{:S(2)}) collective-permute-start(bf16[34,256]{1,0:T(8,128)(2,1)S(1)} %maximum_maximum_fusion.1), channel_id=1, source_target_pairs={{16,0},{32,16},{48,32},{64,48},{80,64},{96,80},{112,96},{17,1},{33... | collective-permute-start | bytes 52232 | tf_op jit(solution)/shard_map/ppermute | solution.py:563
  28.6 8.8 %collective-permute-start.10 = (bf16[17,32,256]{2,1,0:T(8,128)(2,1)S(1)}, bf16[17,32,256]{2,1,0:T(8,128)(2,1)S(1)}, u32[]{:S(2)}, u32[]{:S(2)}) collective-permute-start(bf16[17,32,256]{2,1,0:T(8,128)(2,1)S(1)} %get-tuple-element.43), channel_id=1, source_target_pairs={{0,96},{32,0},{64,32},{96,64},{1,97},{33,1},{65,33},{97,65},{2,98}... | collective-permute-start | bytes 835592 | tf_op jit(solution)/shard_map/ppermute | solution.py:19
  30.2 7.3 %collective-permute-start.11 = (bf16[17,32,256]{2,1,0:T(8,128)(2,1)S(1)}, bf16[17,32,256]{2,1,0:T(8,128)(2,1)S(1)}, u32[]{:S(2)}, u32[]{:S(2)}) collective-permute-start(bf16[17,32,256]{2,1,0:T(8,128)(2,1)S(1)} %get-tuple-element.44), channel_id=1, source_target_pairs={{0,32},{32,64},{64,96},{96,0},{1,33},{33,65},{65,97},{97,1},{2,34}... | collective-permute-start | bytes 835592 | tf_op jit(solution)/shard_map/ppermute | solution.py:19
  31.8 11.0 %collective-permute-start.12 = (bf16[17,32,256]{2,1,0:T(8,128)(2,1)S(1)}, bf16[17,32,256]{2,1,0:T(8,128)(2,1)S(1)}, u32[]{:S(2)}, u32[]{:S(2)}) collective-permute-start(bf16[17,32,256]{2,1,0:T(8,128)(2,1)S(1)} %get-tuple-element.45), channel_id=1, source_target_pairs={{0,96},{32,0},{64,32},{96,64},{1,97},{33,1},{65,33},{97,65},{2,98}... | collective-permute-start | bytes 835592 | tf_op jit(solution)/shard_map/ppermute | solution.py:19
  34.5 9.9 %collective-permute-start.9 = (bf16[17,32,256]{2,1,0:T(8,128)(2,1)S(1)}, bf16[17,32,256]{2,1,0:T(8,128)(2,1)S(1)}, u32[]{:S(2)}, u32[]{:S(2)}) collective-permute-start(bf16[17,32,256]{2,1,0:T(8,128)(2,1)S(1)} %get-tuple-element.41), channel_id=1, source_target_pairs={{0,32},{32,64},{64,96},{96,0},{1,33},{33,65},{65,97},{97,1},{2,34}... | collective-permute-start | bytes 835592 | tf_op jit(solution)/shard_map/ppermute | solution.py:19
  44.9 10.4 %collective-permute-start.13 = (bf16[16,32,256]{2,1,0:T(8,128)(2,1)S(1)}, bf16[16,32,256]{2,1,0:T(8,128)(2,1)S(1)}, u32[]{:S(2)}, u32[]{:S(2)}) collective-permute-start(bf16[16,32,256]{2,1,0:T(8,128)(2,1)S(1)} %get-tuple-element.58.a_ref), channel_id=1, source_target_pairs={{0,32},{32,64},{64,96},{96,0},{1,33},{33,65},{65,97},{97,1},{2,34}... | collective-permute-start | bytes 786440 | tf_op jit(solution)/shard_map/ppermute | solution.py:19
  45.0 10.3 %collective-permute-start.14 = (bf16[16,32,256]{2,1,0:T(8,128)(2,1)S(1)}, bf16[16,32,256]{2,1,0:T(8,128)(2,1)S(1)}, u32[]{:S(2)}, u32[]{:S(2)}) collective-permute-start(bf16[16,32,256]{2,1,0:T(8,128)(2,1)S(1)} %get-tuple-element.57.b_ref), channel_id=1, source_target_pairs={{0,96},{32,0},{64,32},{96,64},{1,97},{33,1},{65,33},{97,65},{2,98}... | collective-permute-start | bytes 786440 | tf_op jit(solution)/shard_map/ppermute | solution.py:19
  47.7 6.2 %collective-permute-start.15 = (bf16[34,256]{1,0:T(8,128)(2,1)S(1)}, bf16[34,256]{1,0:T(8,128)(2,1)S(1)}, u32[]{:S(2)}, u32[]{:S(2)}) collective-permute-start(bf16[34,256]{1,0:T(8,128)(2,1)S(1)} %get-tuple-element.50), channel_id=1, source_target_pairs={{0,1},{1,2},{2,3},{3,4},{4,5},{5,6},{6,7},{7,8},{8,9},{9,10},{10,1... | collective-permute-start | bytes 52232 | tf_op jit(solution)/shard_map/ppermute | solution.py:396
  55.3 7.9 %collective-permute-start.19 = (bf16[16,32,256]{2,1,0:T(8,128)(2,1)S(1)}, bf16[16,32,256]{2,1,0:T(8,128)(2,1)S(1)}, u32[]{:S(2)}, u32[]{:S(2)}) collective-permute-start(bf16[16,32,256]{2,1,0:T(8,128)(2,1)S(1)} %get-tuple-element.57.b_ref), channel_id=1, source_target_pairs={{0,32},{32,64},{64,96},{96,0},{1,33},{33,65},{65,97},{97,1},{2,34}... | collective-permute-start | bytes 786440 | tf_op jit(solution)/shard_map/ppermute | solution.py:19
  55.6 7.6 %collective-permute-start.20 = (bf16[16,32,256]{2,1,0:T(8,128)(2,1)S(1)}, bf16[16,32,256]{2,1,0:T(8,128)(2,1)S(1)}, u32[]{:S(2)}, u32[]{:S(2)}) collective-permute-start(bf16[16,32,256]{2,1,0:T(8,128)(2,1)S(1)} %get-tuple-element.58.a_ref), channel_id=1, source_target_pairs={{0,96},{32,0},{64,32},{96,64},{1,97},{33,1},{65,33},{97,65},{2,98}... | collective-permute-start | bytes 786440 | tf_op jit(solution)/shard_map/ppermute | solution.py:19
  58.2 13.7 %collective-permute-start.17 = (bf16[16,32,256]{2,1,0:T(8,128)(2,1)S(1)}, bf16[16,32,256]{2,1,0:T(8,128)(2,1)S(1)}, u32[]{:S(2)}, u32[]{:S(2)}) collective-permute-start(bf16[16,32,256]{2,1,0:T(8,128)(2,1)S(1)} %collective-permute-done.13.a_ref), channel_id=1, source_target_pairs={{0,32},{32,64},{64,96},{96,0},{1,33},{33,65},{65,97},{97,1},{2,34}... | collective-permute-start | bytes 786440 | tf_op jit(solution)/shard_map/ppermute | solution.py:19
  58.2 13.7 %collective-permute-start.18 = (bf16[16,32,256]{2,1,0:T(8,128)(2,1)S(1)}, bf16[16,32,256]{2,1,0:T(8,128)(2,1)S(1)}, u32[]{:S(2)}, u32[]{:S(2)}) collective-permute-start(bf16[16,32,256]{2,1,0:T(8,128)(2,1)S(1)} %collective-permute-done.14.b_ref), channel_id=1, source_target_pairs={{0,96},{32,0},{64,32},{96,64},{1,97},{33,1},{65,33},{97,65},{2,98}... | collective-permute-start | bytes 786440 | tf_op jit(solution)/shard_map/ppermute | solution.py:19
  63.2 10.7 %collective-permute-start.22 = (bf16[4,288,256]{2,1,0:T(8,128)(2,1)S(1)}, bf16[4,288,256]{2,1,0:T(8,128)(2,1)S(1)}, u32[]{:S(2)}, u32[]{:S(2)}) collective-permute-start(bf16[4,288,256]{2,1,0:T(8,128)(2,1)S(1)} %get-tuple-element.65), channel_id=1, source_target_pairs={{0,16},{16,0},{1,17},{17,1},{2,18},{18,2},{3,19},{19,3},{4,20},{20... | collective-permute-start | bytes 1769480 | tf_op jit(solution)/shard_map/ppermute | solution.py:19
  74.0 6.2 %collective-permute-start.23 = (bf16[288,256]{1,0:T(8,128)(2,1)S(1)}, bf16[288,256]{1,0:T(8,128)(2,1)S(1)}, u32[]{:S(2)}, u32[]{:S(2)}) collective-permute-start(bf16[288,256]{1,0:T(8,128)(2,1)S(1)} %get-tuple-element.67), channel_id=1, source_target_pairs={{0,32},{32,64},{64,96},{96,0},{1,33},{33,65},{65,97},{97,1},{2,34}... | collective-permute-start | bytes 442376 | tf_op jit(solution)/shard_map/ppermute | solution.py:19
  74.1 6.1 %collective-permute-start.24 = (bf16[288,256]{1,0:T(8,128)(2,1)S(1)}, bf16[288,256]{1,0:T(8,128)(2,1)S(1)}, u32[]{:S(2)}, u32[]{:S(2)}) collective-permute-start(bf16[288,256]{1,0:T(8,128)(2,1)S(1)} %get-tuple-element.68), channel_id=1, source_target_pairs={{0,96},{32,0},{64,32},{96,64},{1,97},{33,1},{65,33},{97,65},{2,98}... | collective-permute-start | bytes 442376 | tf_op jit(solution)/shard_map/ppermute | solution.py:19
  76.8 7.7 %collective-permute-start.25 = (bf16[288,256]{1,0:T(8,128)(2,1)S(1)}, bf16[288,256]{1,0:T(8,128)(2,1)S(1)}, u32[]{:S(2)}, u32[]{:S(2)}) collective-permute-start(bf16[288,256]{1,0:T(8,128)(2,1)S(1)} %get-tuple-element.69), channel_id=1, source_target_pairs={{0,64},{32,96},{64,0},{96,32},{1,65},{33,97},{65,1},{97,33},{2,66}... | collective-permute-start | bytes 442376 | tf_op jit(solution)/shard_map/ppermute | solution.py:19
  108.6 4.9 %collective-permute-start.26 = (bf16[90,256]{1,0:T(8,128)(2,1)S(1)}, bf16[90,256]{1,0:T(8,128)(2,1)S(1)}, u32[]{:S(2)}, u32[]{:S(2)}) collective-permute-start(bf16[90,256]{1,0:T(8,128)(2,1)S(1)} %reduce_sum.12.a_ref), channel_id=1, source_target_pairs={{0,4},{4,8},{8,12},{12,0},{1,5},{5,9},{9,13},{13,1},{2,6},{6,10},{... | collective-permute-start | bytes 138248 | tf_op jit(solution)/shard_map/ppermute | solution.py:19
  108.7 4.9 %collective-permute-start.27 = (bf16[90,256]{1,0:T(8,128)(2,1)S(1)}, bf16[90,256]{1,0:T(8,128)(2,1)S(1)}, u32[]{:S(2)}, u32[]{:S(2)}) collective-permute-start(bf16[90,256]{1,0:T(8,128)(2,1)S(1)} %reduce_sum.12.a_ref), channel_id=1, source_target_pairs={{0,12},{4,0},{8,4},{12,8},{1,13},{5,1},{9,5},{13,9},{2,14},{6,2},{... | collective-permute-start | bytes 138248 | tf_op jit(solution)/shard_map/ppermute | solution.py:19
  115.9 6.0 %collective-permute-start.31 = (bf16[360,256]{1,0:T(8,128)(2,1)S(1)}, bf16[360,256]{1,0:T(8,128)(2,1)S(1)}, u32[]{:S(2)}, u32[]{:S(2)}) collective-permute-start(bf16[360,256]{1,0:T(8,128)(2,1)S(1)} %order_pieces.1.a_ref), channel_id=1, source_target_pairs={{0,2},{1,3},{2,0},{3,1},{4,6},{5,7},{6,4},{7,5},{8,10},{9,11},{10,... | collective-permute-start | bytes 552968 | tf_op jit(solution)/shard_map/ppermute | solution.py:19
  117.0 5.1 %collective-permute-start.30 = (bf16[360,256]{1,0:T(8,128)(2,1)S(1)}, bf16[360,256]{1,0:T(8,128)(2,1)S(1)}, u32[]{:S(2)}, u32[]{:S(2)}) collective-permute-start(bf16[360,256]{1,0:T(8,128)(2,1)S(1)} %order_pieces.1.a_ref), channel_id=1, source_target_pairs={{0,3},{1,0},{2,1},{3,2},{4,7},{5,4},{6,5},{7,6},{8,11},{9,8},{10,9... | collective-permute-start | bytes 552968 | tf_op jit(solution)/shard_map/ppermute | solution.py:19
  119.0 5.6 %collective-permute-start.29 = (bf16[360,256]{1,0:T(8,128)(2,1)S(1)}, bf16[360,256]{1,0:T(8,128)(2,1)S(1)}, u32[]{:S(2)}, u32[]{:S(2)}) collective-permute-start(bf16[360,256]{1,0:T(8,128)(2,1)S(1)} %order_pieces.1.a_ref), channel_id=1, source_target_pairs={{0,1},{1,2},{2,3},{3,0},{4,5},{5,6},{6,7},{7,4},{8,9},{9,10},{10,1... | collective-permute-start | bytes 552968 | tf_op jit(solution)/shard_map/ppermute | solution.py:19
  124.6 5.4 %collective-permute-start.32 = (bf16[4,72,256]{2,1,0:T(8,128)(2,1)S(1)}, bf16[4,72,256]{2,1,0:T(8,128)(2,1)S(1)}, u32[]{:S(2)}, u32[]{:S(2)}) collective-permute-start(bf16[4,72,256]{2,1,0:T(8,128)(2,1)S(1)} %pad_maximum_fusion.3), channel_id=1, source_target_pairs={{0,32},{32,64},{64,96},{96,0},{1,33},{33,65},{65,97},{97,1},{2,34}... | collective-permute-start | bytes 442376 | tf_op jit(solution)/shard_map/ppermute | solution.py:19
  124.7 6.3 %collective-permute-start.33 = (bf16[4,72,256]{2,1,0:T(8,128)(2,1)S(1)}, bf16[4,72,256]{2,1,0:T(8,128)(2,1)S(1)}, u32[]{:S(2)}, u32[]{:S(2)}) collective-permute-start(bf16[4,72,256]{2,1,0:T(8,128)(2,1)S(1)} %pad_maximum_fusion.3), channel_id=1, source_target_pairs={{0,96},{32,0},{64,32},{96,64},{1,97},{33,1},{65,33},{97,65},{2,98}... | collective-permute-start | bytes 442376 | tf_op jit(solution)/shard_map/ppermute | solution.py:19
  127.4 5.5 %collective-permute-start.34 = (bf16[4,72,256]{2,1,0:T(8,128)(2,1)S(1)}, bf16[4,72,256]{2,1,0:T(8,128)(2,1)S(1)}, u32[]{:S(2)}, u32[]{:S(2)}) collective-permute-start(bf16[4,72,256]{2,1,0:T(8,128)(2,1)S(1)} %pad_maximum_fusion.3), channel_id=1, source_target_pairs={{0,64},{32,96},{64,0},{96,32},{1,65},{33,97},{65,1},{97,33},{2,66}... | collective-permute-start | bytes 442376 | tf_op jit(solution)/shard_map/ppermute | solution.py:19
  133.0 9.2 %collective-permute-start.35 = (bf16[4,4,72,256]{3,2,1,0:T(8,128)(2,1)S(1)}, bf16[4,4,72,256]{3,2,1,0:T(8,128)(2,1)S(1)}, u32[]{:S(2)}, u32[]{:S(2)}) collective-permute-start(bf16[4,4,72,256]{3,2,1,0:T(8,128)(2,1)S(1)} %pad_maximum_fusion.1.near_ref), channel_id=1, source_target_pairs={{0,16},{16,0},{1,17},{17,1},{2,18},{18,2},{3,19},{19,3},{4,20},{20... | collective-permute-start | bytes 1769480 | tf_op jit(solution)/shard_map/ppermute | solution.py:19
  (7 other events, 33.9 us)

commit v9 on v8

--- a/solution.py
+++ b/solution.py
@@ -240,13 +240,15 @@
     )(tile, left, right, edges, kernel)
 
 
-def second_kernel(chips, hid_ref, edge_ref, cot_ref, wide_ref, near_ref, far_ref, pad_ref, sum_ref):
+def second_kernel(
+    chips, hid_ref, before_ref, after_ref, cot_ref, wide_ref, near_ref, far_ref, pad_ref, sum_ref
+):
     chans = hid_ref.shape[2]
     cols, rows, outs = cot_ref.shape
     width = wide_ref.shape[0]
     core = lax.axis_index("c")
     columns = [
-        (hid_ref[j], edge_ref[0, j : j + 1, :], edge_ref[1, j : j + 1, :]) for j in range(cols + 2)
+        (hid_ref[j], before_ref[j : j + 1, :], after_ref[j : j + 1, :]) for j in range(cols + 2)
     ]
     spread_tile(columns, wide_ref)
     wide_ref[cols + 2 :] = jnp.zeros((width - cols - 2, rows, 3 * chans), BF16)
@@ -286,7 +288,7 @@
             jax.ShapeDtypeStruct(cut, F32),
             jax.ShapeDtypeStruct(cut, BF16),
         ),
-        in_specs=[VMEM_SPEC] * 3,
+        in_specs=[VMEM_SPEC] * 4,
         out_specs=(VMEM_SPEC,) * 3,
         scratch_shapes=[
             pltpu.VMEM((width + 2, rows, outs), BF16),
@@ -295,7 +297,7 @@
         compiler_params=pltpu.CompilerParams(vmem_limit_bytes=9 * 2**20),
         cost_estimate=QUICK,
         name="second",
-    )(tile, edges, cotangent)
+    )(tile, *edges, cotangent)
 
 
 def features_kernel(wide_ref, kernel_ref, out_ref):
@@ -393,7 +395,7 @@
     count = lax.axis_size(SKY)
     up = [(i, i + 1) for i in range(count - 1)]
     down = [(j, i) for i, j in up]
-    return jnp.stack([lax.ppermute(ends[0], SKY, up), lax.ppermute(ends[1], SKY, down)])
+    return lax.ppermute(ends[0], SKY, up), lax.ppermute(ends[1], SKY, down)
 
 
 def join_kernel(own_ref, far_ref, keep_ref, a_ref, b_ref, c_ref, out_ref):
@@ -496,33 +498,89 @@
     )(*parts)
 
 
-def lay_second_kernel(near_ref, far_ref, out_ref):
-    sy, sx, rows, _ = near_ref.shape
+def sum_kernel(in_ref, out_ref):
+    total = in_ref[0].astype(F32)
+    for i in range(1, in_ref.shape[0]):
+        total = total + in_ref[i].astype(F32)
+    out_ref[...] = total.astype(BF16)
+
+
+def sum_pieces(pieces):
+    return pl.pallas_call(
+        sum_kernel,
+        out_shape=jax.ShapeDtypeStruct(pieces.shape[1:], BF16),
+        in_specs=[VMEM_SPEC],
+        out_specs=VMEM_SPEC,
+        compiler_params=pltpu.CompilerParams(vmem_limit_bytes=4 * 2**20),
+        cost_estimate=QUICK,
+        name="sum_pieces",
+    )(pieces)
+
+
+def pick_kernel(first, a_ref, b_ref, c_ref, d_ref, out_ref):
+    for i, ref in enumerate((a_ref, b_ref, c_ref, d_ref)):
+        out_ref[i] = ref[first:, :]
+
+
+def pick_rows(parts, first):
+    rows, outs = parts[0].shape
+    return pl.pallas_call(
+        functools.partial(pick_kernel, first),
+        out_shape=jax.ShapeDtypeStruct((len(parts), rows - first, outs), BF16),
+        in_specs=[VMEM_SPEC] * 4,
+        out_specs=VMEM_SPEC,
+        compiler_params=pltpu.CompilerParams(vmem_limit_bytes=2 * 2**20),
+        cost_estimate=QUICK,
+        name="pick_rows",
+    )(*parts)
+
+
+def lay_second_kernel(other, in_ref, *refs):
+    out_ref, half_ref, sems = refs[-3:]
+    sy, sx, rows, _ = in_ref.shape
     size = rows // 3
-    third = out_ref.shape[0] // 3
+    third = half_ref.shape[0] // 3
     core, y, x = lax.axis_index("c"), lax.axis_index("y"), lax.axis_index("x")
-    for half, ref in ((core, near_ref), (1 - core, far_ref)):
-        for i in range(sy):
-            for j in range(sx):
-                place = (half * sy + lax.rem(y + sy - STEPS[i], sy)) * sx
-                place = place + lax.rem(x + sx - STEPS[j], sx)
-                value = ref[i, j].astype(F32)
-                for tap in range(3):
-                    at = pl.multiple_of(tap * third + place * size, 8)
-                    out_ref[pl.ds(at, size), :] = value[tap * size : (tap + 1) * size]
-
-
-def lay_second(near, far):
-    sy, sx, rows, outs = near.shape
-    return pl.pallas_call(
-        lay_second_kernel,
-        out_shape=jax.ShapeDtypeStruct((2 * sy * sx * rows, outs), F32),
-        in_specs=[VMEM_SPEC] * 2,
-        out_specs=VMEM_SPEC,
-        compiler_params=pltpu.CompilerParams(vmem_limit_bytes=4 * 2**20),
-        cost_estimate=QUICK,
+    half = 1 - core if other else core
+    for i in range(sy):
+        for j in range(sx):
+            place = lax.rem(y + sy - STEPS[i], sy) * sx + lax.rem(x + sx - STEPS[j], sx)
+            value = in_ref[i, j].astype(F32)
+            for tap in range(3):
+                at = pl.multiple_of(tap * third + place * size, 8)
+                half_ref[pl.ds(at, size), :] = value[tap * size : (tap + 1) * size]
+    copies = []
+    for tap in range(3):
+        to = pl.multiple_of((2 * tap + half) * third, 8)
+        copies.append(
+            pltpu.make_async_copy(
+                half_ref.at[tap * third : (tap + 1) * third],
+                out_ref.at[pl.ds(to, third)],
+                sems.at[tap],
+            )
+        )
+    for copy in copies:
+        copy.start()
+    for copy in copies:
+        copy.wait()
+
+
+def lay_second(half, whole=None):
+    sy, sx, rows, outs = half.shape
+    size = sy * sx * rows
+    anywhere = pl.BlockSpec(memory_space=pl.ANY)
+    given = [] if whole is None else [whole]
+    return pl.pallas_call(
+        functools.partial(lay_second_kernel, whole is not None),
+        out_shape=jax.ShapeDtypeStruct((2 * size, outs), F32),
+        in_specs=[VMEM_SPEC] + [anywhere] * len(given),
+        out_specs=anywhere,
+        scratch_shapes=[pltpu.VMEM((size, outs), F32), pltpu.SemaphoreType.DMA((3,))],
+        compiler_params=pltpu.CompilerParams(vmem_limit_bytes=4 * 2**20),
+        cost_estimate=QUICK,
+        input_output_aliases={1: 0} if given else {},
         name="lay_second",
-    )(near, far)
+    )(half, *given)
 
 
 def gather_steps(piece, axis):
@@ -540,7 +598,7 @@
         )
         for r in (rows - 1, 0)
     ]
-    edges = row_halo(ends)
+    edges = jnp.stack(row_halo(ends))
     far_cube = shift(sky_cube, "c", 1)
     far_weight = shift(weight_first, "c", 1)
     far_edges = shift(edges, "c", 1)
@@ -597,15 +655,16 @@
     joined = join(first_own, shift(first_far, "c", 1), keep, got, sx * sz)
     extra = keep.shape[0] // (sx * sz)
     summed = lax.all_to_all(joined, SKY, 0, 0, tiled=True)
-    summed = jnp.sum(summed.astype(F32), axis=0).astype(BF16)
+    summed = sum_pieces(summed)
     parts = gather_steps(order_pieces(gather_steps(summed, "z"), extra), "x")
     main = parts[0].shape[0] - sz * extra
     grad_first = lay_first(parts, sz, chans)
     features = features_tile(wide_hidden, weight_second, strip)
-    share = jnp.stack([part[main:] for part in parts])
+    share = pick_rows(parts, main)
     share, features = lax.optimization_barrier((share, features))
     share = jnp.stack(gather_steps(share, "y"))
-    grad_second = lay_second(share, shift(share, "c", 1)).reshape(3, 3, outs, outs)
+    grad_second = lay_second(shift(share, "c", 1), lay_second(share))
+    grad_second = grad_second.reshape(3, 3, outs, outs)
     return features, grad_first, grad_second
 
 

time: 144 us -> 143 us (level)
  transfers between devices with their start and end apart: 36 -> 36, of which waited for: 16 -> 16; matrix products, arithmetic and copies ran while one was open for 3% -> 3% of each run, Pallas kernels for 13% -> 14%
where the time goes in v9:
time: 143 us
  starting transfers between devices  55.7 us (39%)
  waiting for transfers between devices  33.8 us (24%)
  Pallas kernels  25.1 us (18%)
  blocking collectives  22.6 us (16%)
  local copies, waits for them, and re-layouts  3.22 us (2%)
    ppermute x30, starting transfers between devices, shift(): lax.ppermute(x, axis, [(i, (i + step) % count) for i in range(count)])  42.4 us
    ppermute x30, waiting for transfers between devices, shift(): lax.ppermute(x, axis, [(i, (i + step) % count) for i in range(count)])  28.4 us
    all_to_all x1, blocking collectives, body(): summed = lax.all_to_all(joined, SKY, 0, 0, tiled=True)  22.6 us
    ppermute x4, starting transfers between devices, row_halo(): return (lax.ppermute(ends[0], SKY, up), lax.ppermute(ends[1], SKY, down))  8.89 us
    pallas_call x4, Pallas kernels, grad_strip(): pl.pallas_call(functools.partial(grad_kernel, step, old is not None, last...  7.01 us
    pallas_call x4, Pallas kernels, conv_parts(): pl.pallas_call(functools.partial(conv_kernel, parts, len(adds)), out_shap...  5.84 us
    ppermute x4, waiting for transfers between devices, row_halo(): return (lax.ppermute(ends[0], SKY, up), lax.ppermute(ends[1], SKY, down))  5.32 us
  transfers between devices with their start and end apart: 36, of which 16 were waited for; matrix products, arithmetic and copies ran while one was open for 3% of the time, Pallas kernels for 14%

profile of v9, /device:TPU:1, one launch (start us, length us, event | category | flops | bytes accessed | tf_op | source)
XLA Modules:
  0.0 142.9 jit_solution(226540565989076919)
XLA Ops:
  4.6 3.2 %collective-permute-start.1 = (bf16[320,128]{1,0:T(8,128)(2,1)S(1)}, bf16[320,128]{1,0:T(8,128)(2,1)S(1)}, u32[]{:S(2)}, u32[]{:S(2)}) collective-permute-start(bf16[320,128]{1,0:T(8,128)(2,1)S(1)} %pad_maximum_fusion.3), channel_id=1, source_target_pairs={{0,1},{1,2},{2,3},{3,4},{4,5},{5,6},{6,7},{7,8},{8,9},{9,10},{10,1... | collective-permute-start | bytes 245768 | tf_op jit(solution)/shard_map/ppermute | solution.py:398
  10.4 3.8 %collective-permute-done.2 = bf16[320,128]{1,0:T(8,128)(2,1)S(1)} collective-permute-done((bf16[320,128]{1,0:T(8,128)(2,1)S(1)}, bf16[320,128]{1,0:T(8,128)(2,1)S(1)}, u32[]{:S(2)}, u32[]{:S(2)}) %collective-permute-start.2) | collective-permute-done | bytes 81952 | tf_op jit(solution)/shard_map/ppermute | solution.py:398
  16.4 1.9 %spread.1.wide_ref = bf16[4,40,32,768]{3,2,1,0:T(8,128)(2,1)S(1)} custom-call(bf16[256,32,128]{2,1,0:T(8,128)(2,1)S(1)} %copy-done.1, bf16[256,32,128]{2,1,0:T(8,128)(2,1)S(1)} %collective-permute-done.far_ref, bf16[2,320,128]{2,1,0:T(8,128)(2,1)S(1)} %pad_maximum_fusion.2.own_halo_ref.edge_ref, bf16[2,320,128]{2,1,0:T(8,128)(2,1)S(1)} %collective-permute-done.3.far_halo_ref), custom_call_target="tpu_custom_call" | custom-call | flops 1 | bytes 1 | tf_op jit(solution)/shard_map/spread/pallas_call | solution.py:94
  22.7 2.5 %collective-permute-start.6 = (bf16[34,256]{1,0:T(8,128)(2,1)S(1)}, bf16[34,256]{1,0:T(8,128)(2,1)S(1)}, u32[]{:S(2)}, u32[]{:S(2)}) collective-permute-start(bf16[34,256]{1,0:T(8,128)(2,1)S(1)} %maximum_maximum_fusion), channel_id=1, source_target_pairs={{0,16},{16,32},{32,48},{48,64},{64,80},{80,96},{96,112},{1,17},{17... | collective-permute-start | bytes 52232 | tf_op jit(solution)/shard_map/ppermute | solution.py:620
  25.2 1.9 %collective-permute-start.7 = (bf16[34,256]{1,0:T(8,128)(2,1)S(1)}, bf16[34,256]{1,0:T(8,128)(2,1)S(1)}, u32[]{:S(2)}, u32[]{:S(2)}) collective-permute-start(bf16[34,256]{1,0:T(8,128)(2,1)S(1)} %maximum_maximum_fusion.1), channel_id=1, source_target_pairs={{16,0},{32,16},{48,32},{64,48},{80,64},{96,80},{112,96},{17,1},{33... | collective-permute-start | bytes 52232 | tf_op jit(solution)/shard_map/ppermute | solution.py:621
  28.6 1.6 %collective-permute-start.10 = (bf16[17,32,256]{2,1,0:T(8,128)(2,1)S(1)}, bf16[17,32,256]{2,1,0:T(8,128)(2,1)S(1)}, u32[]{:S(2)}, u32[]{:S(2)}) collective-permute-start(bf16[17,32,256]{2,1,0:T(8,128)(2,1)S(1)} %get-tuple-element.44), channel_id=1, source_target_pairs={{0,96},{32,0},{64,32},{96,64},{1,97},{33,1},{65,33},{97,65},{2,98}... | collective-permute-start | bytes 835592 | tf_op jit(solution)/shard_map/ppermute | solution.py:19
  31.8 2.7 %collective-permute-start.12 = (bf16[17,32,256]{2,1,0:T(8,128)(2,1)S(1)}, bf16[17,32,256]{2,1,0:T(8,128)(2,1)S(1)}, u32[]{:S(2)}, u32[]{:S(2)}) collective-permute-start(bf16[17,32,256]{2,1,0:T(8,128)(2,1)S(1)} %get-tuple-element.46), channel_id=1, source_target_pairs={{0,96},{32,0},{64,32},{96,64},{1,97},{33,1},{65,33},{97,65},{2,98}... | collective-permute-start | bytes 835592 | tf_op jit(solution)/shard_map/ppermute | solution.py:19
  37.6 5.2 %collective-permute-done.12.b1_ref = bf16[17,32,256]{2,1,0:T(8,128)(2,1)S(1)} collective-permute-done((bf16[17,32,256]{2,1,0:T(8,128)(2,1)S(1)}, bf16[17,32,256]{2,1,0:T(8,128)(2,1)S(1)}, u32[]{:S(2)}, u32[]{:S(2)}) %collective-permute-start.12) | collective-permute-done | bytes 278560 | tf_op jit(solution)/shard_map/ppermute | solution.py:19
  42.8 1.6 %collective-permute-done.9.a0_ref = bf16[17,32,256]{2,1,0:T(8,128)(2,1)S(1)} collective-permute-done((bf16[17,32,256]{2,1,0:T(8,128)(2,1)S(1)}, bf16[17,32,256]{2,1,0:T(8,128)(2,1)S(1)}, u32[]{:S(2)}, u32[]{:S(2)}) %collective-permute-start.9) | collective-permute-done | bytes 278560 | tf_op jit(solution)/shard_map/ppermute | solution.py:19
  45.0 2.7 %collective-permute-start.14 = (bf16[16,32,256]{2,1,0:T(8,128)(2,1)S(1)}, bf16[16,32,256]{2,1,0:T(8,128)(2,1)S(1)}, u32[]{:S(2)}, u32[]{:S(2)}) collective-permute-start(bf16[16,32,256]{2,1,0:T(8,128)(2,1)S(1)} %get-tuple-element.59.b_ref), channel_id=1, source_target_pairs={{0,96},{32,0},{64,32},{96,64},{1,97},{33,1},{65,33},{97,65},{2,98}... | collective-permute-start | bytes 786440 | tf_op jit(solution)/shard_map/ppermute | solution.py:19
  47.7 3.1 %collective-permute-start.15 = (bf16[34,256]{1,0:T(8,128)(2,1)S(1)}, bf16[34,256]{1,0:T(8,128)(2,1)S(1)}, u32[]{:S(2)}, u32[]{:S(2)}) collective-permute-start(bf16[34,256]{1,0:T(8,128)(2,1)S(1)} %get-tuple-element.51), channel_id=1, source_target_pairs={{0,1},{1,2},{2,3},{3,4},{4,5},{5,6},{6,7},{7,8},{8,9},{9,10},{10,1... | collective-permute-start | bytes 52232 | tf_op jit(solution)/shard_map/ppermute | solution.py:398
  52.1 1.7 %grad_first.4.refs_0_ = f32[768,768]{1,0:T(8,128)S(1)} custom-call(bf16[4,40,32,768]{3,2,1,0:T(8,128)(2,1)S(1)} %spread.1.wide_ref, bf16[16,32,256]{2,1,0:T(8,128)(2,1)S(1)} %get-tuple-element.60.a_ref, bf16[16,32,256]{2,1,0:T(8,128)(2,1)S(1)} %get-tuple-element.59.b_ref), custom_call_target="tpu_custom_call" | custom-call | flops 1 | bytes 1 | tf_op jit(solution)/shard_map/grad_first/pallas_call | solution.py:175
  55.3 2.7 %collective-permute-start.20 = (bf16[16,32,256]{2,1,0:T(8,128)(2,1)S(1)}, bf16[16,32,256]{2,1,0:T(8,128)(2,1)S(1)}, u32[]{:S(2)}, u32[]{:S(2)}) collective-permute-start(bf16[16,32,256]{2,1,0:T(8,128)(2,1)S(1)} %get-tuple-element.60.a_ref), channel_id=1, source_target_pairs={{0,96},{32,0},{64,32},{96,64},{1,97},{33,1},{65,33},{97,65},{2,98}... | collective-permute-start | bytes 786440 | tf_op jit(solution)/shard_map/ppermute | solution.py:19
  58.0 2.7 %collective-permute-start.18 = (bf16[16,32,256]{2,1,0:T(8,128)(2,1)S(1)}, bf16[16,32,256]{2,1,0:T(8,128)(2,1)S(1)}, u32[]{:S(2)}, u32[]{:S(2)}) collective-permute-start(bf16[16,32,256]{2,1,0:T(8,128)(2,1)S(1)} %collective-permute-done.14.b_ref), channel_id=1, source_target_pairs={{0,96},{32,0},{64,32},{96,64},{1,97},{33,1},{65,33},{97,65},{2,98}... | collective-permute-start | bytes 786440 | tf_op jit(solution)/shard_map/ppermute | solution.py:19
  60.7 2.3 %second.1 = (bf16[40,32,768]{2,1,0:T(8,128)(2,1)S(1)}, f32[4,288,256]{2,1,0:T(8,128)S(1)}, bf16[4,288,256]{2,1,0:T(8,128)(2,1)S(1)}) custom-call(bf16[34,32,256]{2,1,0:T(8,128)(2,1)S(1)} %get-tuple-element.55.hid_ref, bf16[34,256]{1,0:T(8,128)(2,1)S(1)} %collective-permute-done.15.before_ref, bf16[34,256]{1,0:T(8,128)(2,1)S(1)} %collective-permute-done.16.after_ref, ...), custom_call_target="tpu_custom_call" | custom-call | flops 1 | bytes 1 | tf_op jit(solution)/shard_map/second/pallas_call | solution.py:284
  63.0 5.3 %collective-permute-start.22 = (bf16[4,288,256]{2,1,0:T(8,128)(2,1)S(1)}, bf16[4,288,256]{2,1,0:T(8,128)(2,1)S(1)}, u32[]{:S(2)}, u32[]{:S(2)}) collective-permute-start(bf16[4,288,256]{2,1,0:T(8,128)(2,1)S(1)} %get-tuple-element.67), channel_id=1, source_target_pairs={{0,16},{16,0},{1,17},{17,1},{2,18},{18,2},{3,19},{19,3},{4,20},{20... | collective-permute-start | bytes 1769480 | tf_op jit(solution)/shard_map/ppermute | solution.py:19
  68.2 1.8 %grad_first.5.refs_0_ = f32[768,768]{1,0:T(8,128)S(1)} custom-call(bf16[4,40,32,768]{3,2,1,0:T(8,128)(2,1)S(1)} %spread.1.wide_ref, bf16[16,32,256]{2,1,0:T(8,128)(2,1)S(1)} %collective-permute-done.13.a_ref, bf16[16,32,256]{2,1,0:T(8,128)(2,1)S(1)} %collective-permute-done.19.b_ref, f32[768,768]{1,0:T(8,128)S(1)} %grad_first.4.refs_0_), custom_call_target="tpu_custom_call" | custom-call | flops 1 | bytes 1 | tf_op jit(solution)/shard_map/grad_first/pallas_call | solution.py:175
  70.0 1.8 %grad_first.6.refs_0_ = f32[768,768]{1,0:T(8,128)S(1)} custom-call(bf16[4,40,32,768]{3,2,1,0:T(8,128)(2,1)S(1)} %spread.1.wide_ref, bf16[16,32,256]{2,1,0:T(8,128)(2,1)S(1)} %collective-permute-done.20.a_ref, bf16[16,32,256]{2,1,0:T(8,128)(2,1)S(1)} %collective-permute-done.14.b_ref, f32[768,768]{1,0:T(8,128)S(1)} %grad_first.5.refs_0_), custom_call_target="tpu_custom_call" | custom-call | flops 1 | bytes 1 | tf_op jit(solution)/shard_map/grad_first/pallas_call | solution.py:175
  71.8 1.8 %grad_first.7 = (f32[384,768]{1,0:T(8,128)S(1)}, bf16[384,768]{1,0:T(8,128)(2,1)S(1)}) custom-call(bf16[4,40,32,768]{3,2,1,0:T(8,128)(2,1)S(1)} %spread.1.wide_ref, bf16[16,32,256]{2,1,0:T(8,128)(2,1)S(1)} %collective-permute-done.17.a_ref, bf16[16,32,256]{2,1,0:T(8,128)(2,1)S(1)} %collective-permute-done.18.b_ref, f32[768,768]{1,0:T(8,128)S(1)} %grad_first.6.refs_0_), custom_call_target="tpu_custom_call" | custom-call | flops 1 | bytes 1 | tf_op jit(solution)/shard_map/grad_first/pallas_call | solution.py:175
  73.9 2.7 %collective-permute-start.24 = (bf16[288,256]{1,0:T(8,128)(2,1)S(1)}, bf16[288,256]{1,0:T(8,128)(2,1)S(1)}, u32[]{:S(2)}, u32[]{:S(2)}) collective-permute-start(bf16[288,256]{1,0:T(8,128)(2,1)S(1)} %get-tuple-element.70), channel_id=1, source_target_pairs={{0,96},{32,0},{64,32},{96,64},{1,97},{33,1},{65,33},{97,65},{2,98}... | collective-permute-start | bytes 442376 | tf_op jit(solution)/shard_map/ppermute | solution.py:19
  77.6 2.4 %collective-permute-done.23.a_ref = bf16[288,256]{1,0:T(8,128)(2,1)S(1)} collective-permute-done((bf16[288,256]{1,0:T(8,128)(2,1)S(1)}, bf16[288,256]{1,0:T(8,128)(2,1)S(1)}, u32[]{:S(2)}, u32[]{:S(2)}) %collective-permute-start.23) | collective-permute-done | bytes 147488 | tf_op jit(solution)/shard_map/ppermute | solution.py:19
  80.0 4.2 %collective-permute-done.25.c_ref = bf16[288,256]{1,0:T(8,128)(2,1)S(1)} collective-permute-done((bf16[288,256]{1,0:T(8,128)(2,1)S(1)}, bf16[288,256]{1,0:T(8,128)(2,1)S(1)}, u32[]{:S(2)}, u32[]{:S(2)}) %collective-permute-start.25) | collective-permute-done | bytes 147488 | tf_op jit(solution)/shard_map/ppermute | solution.py:19
  84.4 22.6 %all_to_all.5.in_ref = bf16[16,90,256]{2,1,0:T(8,128)(2,1)S(1)} all-to-all(bf16[16,90,256]{2,1,0:T(8,128)(2,1)S(1)} %join.1), channel_id=1, replica_groups=mesh['y'=4,'c'=2,'z'=4,'x'=4] {'z','x'}, dimensions={0} | all-to-all | bytes 1474560 | tf_op jit(solution)/shard_map/all_to_all | solution.py:657
  107.2 2.7 %collective-permute-start.27 = (bf16[90,256]{1,0:T(8,128)(2,1)S(1)}, bf16[90,256]{1,0:T(8,128)(2,1)S(1)}, u32[]{:S(2)}, u32[]{:S(2)}) collective-permute-start(bf16[90,256]{1,0:T(8,128)(2,1)S(1)} %sum_pieces.1.a_ref), channel_id=1, source_target_pairs={{0,12},{4,0},{8,4},{12,8},{1,13},{5,1},{9,5},{13,9},{2,14},{6,2},{... | collective-permute-start | bytes 138248 | tf_op jit(solution)/shard_map/ppermute | solution.py:19
  111.3 3.0 %collective-permute-done.28.d_ref = bf16[90,256]{1,0:T(8,128)(2,1)S(1)} collective-permute-done((bf16[90,256]{1,0:T(8,128)(2,1)S(1)}, bf16[90,256]{1,0:T(8,128)(2,1)S(1)}, u32[]{:S(2)}, u32[]{:S(2)}) %collective-permute-start.28) | collective-permute-done | bytes 46112 | tf_op jit(solution)/shard_map/ppermute | solution.py:19
  115.1 2.0 %collective-permute-start.30 = (bf16[360,256]{1,0:T(8,128)(2,1)S(1)}, bf16[360,256]{1,0:T(8,128)(2,1)S(1)}, u32[]{:S(2)}, u32[]{:S(2)}) collective-permute-start(bf16[360,256]{1,0:T(8,128)(2,1)S(1)} %order_pieces.1.a_ref), channel_id=1, source_target_pairs={{0,3},{1,0},{2,1},{3,2},{4,7},{5,4},{6,5},{7,6},{8,11},{9,8},{10,9... | collective-permute-start | bytes 552968 | tf_op jit(solution)/shard_map/ppermute | solution.py:19
  117.2 2.2 %features.1 = bf16[32,32,256]{2,1,0:T(8,128)(2,1)} custom-call(bf16[40,32,768]{2,1,0:T(8,128)(2,1)S(1)} %get-tuple-element.72.wide_ref, bf16[2304,256]{1,0:T(8,128)(2,1)S(1)} %bitcast.47), custom_call_target="tpu_custom_call" | custom-call | flops 1 | bytes 1 | tf_op jit(solution)/shard_map/features/pallas_call | solution.py:313
  121.6 2.5 %collective-permute-done.31.d_ref = bf16[360,256]{1,0:T(8,128)(2,1)S(1)} collective-permute-done((bf16[360,256]{1,0:T(8,128)(2,1)S(1)}, bf16[360,256]{1,0:T(8,128)(2,1)S(1)}, u32[]{:S(2)}, u32[]{:S(2)}) %collective-permute-start.31) | collective-permute-done | bytes 184352 | tf_op jit(solution)/shard_map/ppermute | solution.py:19
  124.4 2.5 %collective-permute-start.33 = (bf16[4,72,256]{2,1,0:T(8,128)(2,1)S(1)}, bf16[4,72,256]{2,1,0:T(8,128)(2,1)S(1)}, u32[]{:S(2)}, u32[]{:S(2)}) collective-permute-start(bf16[4,72,256]{2,1,0:T(8,128)(2,1)S(1)} %pick_rows.1), channel_id=1, source_target_pairs={{0,96},{32,0},{64,32},{96,64},{1,97},{33,1},{65,33},{97,65},{2,98}... | collective-permute-start | bytes 442376 | tf_op jit(solution)/shard_map/ppermute | solution.py:19
  126.9 2.5 %collective-permute-done.32 = bf16[4,72,256]{2,1,0:T(8,128)(2,1)S(1)} collective-permute-done((bf16[4,72,256]{2,1,0:T(8,128)(2,1)S(1)}, bf16[4,72,256]{2,1,0:T(8,128)(2,1)S(1)}, u32[]{:S(2)}, u32[]{:S(2)}) %collective-permute-start.32) | collective-permute-done | bytes 147488 | tf_op jit(solution)/shard_map/ppermute | solution.py:19
  130.6 1.8 %collective-permute-done.34 = bf16[4,72,256]{2,1,0:T(8,128)(2,1)S(1)} collective-permute-done((bf16[4,72,256]{2,1,0:T(8,128)(2,1)S(1)}, bf16[4,72,256]{2,1,0:T(8,128)(2,1)S(1)}, u32[]{:S(2)}, u32[]{:S(2)}) %collective-permute-start.34) | collective-permute-done | bytes 147488 | tf_op jit(solution)/shard_map/ppermute | solution.py:19
  132.5 6.8 %collective-permute-start.35 = (bf16[4,4,72,256]{3,2,1,0:T(8,128)(2,1)S(1)}, bf16[4,4,72,256]{3,2,1,0:T(8,128)(2,1)S(1)}, u32[]{:S(2)}, u32[]{:S(2)}) collective-permute-start(bf16[4,4,72,256]{3,2,1,0:T(8,128)(2,1)S(1)} %pad_maximum_fusion.1.in_ref), channel_id=1, source_target_pairs={{0,16},{16,0},{1,17},{17,1},{2,18},{18,2},{3,19},{19,3},{4,20},{20... | collective-permute-start | bytes 1769480 | tf_op jit(solution)/shard_map/ppermute | solution.py:19
  (84 shorter events, 33.7 us)
Async XLA Ops:
  0.6 15.8 %collective-permute-start = (bf16[256,32,128]{2,1,0:T(8,128)(2,1)}, bf16[256,32,128]{2,1,0:T(8,128)(2,1)S(1)}, u32[]{:S(2)}, u32[]{:S(2)}) collective-permute-start(bf16[256,32,128]{2,1,0:T(8,128)(2,1)} %own_ref.1), channel_id=1, source_target_pairs={{0,16},{16,0},{1,17},{17,1},{2,18},{18,2},{3,19},{19,3},{4,20},{20... | collective-permute-start | bytes 6291464 | tf_op jit(solution)/shard_map/ppermute | solution.py:19
  4.6 5.8 %collective-permute-start.1 = (bf16[320,128]{1,0:T(8,128)(2,1)S(1)}, bf16[320,128]{1,0:T(8,128)(2,1)S(1)}, u32[]{:S(2)}, u32[]{:S(2)}) collective-permute-start(bf16[320,128]{1,0:T(8,128)(2,1)S(1)} %pad_maximum_fusion.3), channel_id=1, source_target_pairs={{0,1},{1,2},{2,3},{3,4},{4,5},{5,6},{6,7},{7,8},{8,9},{9,10},{10,1... | collective-permute-start | bytes 245768 | tf_op jit(solution)/shard_map/ppermute | solution.py:398
  7.8 7.4 %collective-permute-start.4 = (bf16[3,3,128,256]{3,2,1,0:T(8,128)(2,1)}, bf16[3,3,128,256]{3,2,1,0:T(8,128)(2,1)S(1)}, u32[]{:S(2)}, u32[]{:S(2)}) collective-permute-start(bf16[3,3,128,256]{3,2,1,0:T(8,128)(2,1)} %param.5), channel_id=1, source_target_pairs={{0,16},{16,0},{1,17},{17,1},{2,18},{18,2},{3,19},{19,3},{4,20},{20... | collective-permute-start | bytes 1769480 | tf_op jit(solution)/shard_map/ppermute | solution.py:19
  8.4 5.9 %collective-permute-start.2 = (bf16[320,128]{1,0:T(8,128)(2,1)S(1)}, bf16[320,128]{1,0:T(8,128)(2,1)S(1)}, u32[]{:S(2)}, u32[]{:S(2)}) collective-permute-start(bf16[320,128]{1,0:T(8,128)(2,1)S(1)} %pad_maximum_fusion.4), channel_id=1, source_target_pairs={{1,0},{2,1},{3,2},{4,3},{5,4},{6,5},{7,6},{8,7},{9,8},{10,9},{11,1... | collective-permute-start | bytes 245768 | tf_op jit(solution)/shard_map/ppermute | solution.py:398
  19.8 10.5 %collective-permute-start.5 = (bf16[17,32,256]{2,1,0:T(8,128)(2,1)S(1)}, bf16[17,32,256]{2,1,0:T(8,128)(2,1)S(1)}, u32[]{:S(2)}, u32[]{:S(2)}) collective-permute-start(bf16[17,32,256]{2,1,0:T(8,128)(2,1)S(1)} %get-tuple-element.39), channel_id=1, source_target_pairs={{0,32},{32,64},{64,96},{96,0},{1,33},{33,65},{65,97},{97,1},{2,34}... | collective-permute-start | bytes 835592 | tf_op jit(solution)/shard_map/ppermute | solution.py:19
  21.2 9.2 %collective-permute-start.8 = (bf16[17,32,256]{2,1,0:T(8,128)(2,1)S(1)}, bf16[17,32,256]{2,1,0:T(8,128)(2,1)S(1)}, u32[]{:S(2)}, u32[]{:S(2)}) collective-permute-start(bf16[17,32,256]{2,1,0:T(8,128)(2,1)S(1)} %get-tuple-element.41), channel_id=1, source_target_pairs={{0,96},{32,0},{64,32},{96,64},{1,97},{33,1},{65,33},{97,65},{2,98}... | collective-permute-start | bytes 835592 | tf_op jit(solution)/shard_map/ppermute | solution.py:19
  22.7 7.5 %collective-permute-start.6 = (bf16[34,256]{1,0:T(8,128)(2,1)S(1)}, bf16[34,256]{1,0:T(8,128)(2,1)S(1)}, u32[]{:S(2)}, u32[]{:S(2)}) collective-permute-start(bf16[34,256]{1,0:T(8,128)(2,1)S(1)} %maximum_maximum_fusion), channel_id=1, source_target_pairs={{0,16},{16,32},{32,48},{48,64},{64,80},{80,96},{96,112},{1,17},{17... | collective-permute-start | bytes 52232 | tf_op jit(solution)/shard_map/ppermute | solution.py:620
  25.2 5.1 %collective-permute-start.7 = (bf16[34,256]{1,0:T(8,128)(2,1)S(1)}, bf16[34,256]{1,0:T(8,128)(2,1)S(1)}, u32[]{:S(2)}, u32[]{:S(2)}) collective-permute-start(bf16[34,256]{1,0:T(8,128)(2,1)S(1)} %maximum_maximum_fusion.1), channel_id=1, source_target_pairs={{16,0},{32,16},{48,32},{64,48},{80,64},{96,80},{112,96},{17,1},{33... | collective-permute-start | bytes 52232 | tf_op jit(solution)/shard_map/ppermute | solution.py:621
  28.6 8.8 %collective-permute-start.10 = (bf16[17,32,256]{2,1,0:T(8,128)(2,1)S(1)}, bf16[17,32,256]{2,1,0:T(8,128)(2,1)S(1)}, u32[]{:S(2)}, u32[]{:S(2)}) collective-permute-start(bf16[17,32,256]{2,1,0:T(8,128)(2,1)S(1)} %get-tuple-element.44), channel_id=1, source_target_pairs={{0,96},{32,0},{64,32},{96,64},{1,97},{33,1},{65,33},{97,65},{2,98}... | collective-permute-start | bytes 835592 | tf_op jit(solution)/shard_map/ppermute | solution.py:19
  30.2 7.3 %collective-permute-start.11 = (bf16[17,32,256]{2,1,0:T(8,128)(2,1)S(1)}, bf16[17,32,256]{2,1,0:T(8,128)(2,1)S(1)}, u32[]{:S(2)}, u32[]{:S(2)}) collective-permute-start(bf16[17,32,256]{2,1,0:T(8,128)(2,1)S(1)} %get-tuple-element.45), channel_id=1, source_target_pairs={{0,32},{32,64},{64,96},{96,0},{1,33},{33,65},{65,97},{97,1},{2,34}... | collective-permute-start | bytes 835592 | tf_op jit(solution)/shard_map/ppermute | solution.py:19
  31.8 11.0 %collective-permute-start.12 = (bf16[17,32,256]{2,1,0:T(8,128)(2,1)S(1)}, bf16[17,32,256]{2,1,0:T(8,128)(2,1)S(1)}, u32[]{:S(2)}, u32[]{:S(2)}) collective-permute-start(bf16[17,32,256]{2,1,0:T(8,128)(2,1)S(1)} %get-tuple-element.46), channel_id=1, source_target_pairs={{0,96},{32,0},{64,32},{96,64},{1,97},{33,1},{65,33},{97,65},{2,98}... | collective-permute-start | bytes 835592 | tf_op jit(solution)/shard_map/ppermute | solution.py:19
  34.5 9.9 %collective-permute-start.9 = (bf16[17,32,256]{2,1,0:T(8,128)(2,1)S(1)}, bf16[17,32,256]{2,1,0:T(8,128)(2,1)S(1)}, u32[]{:S(2)}, u32[]{:S(2)}) collective-permute-start(bf16[17,32,256]{2,1,0:T(8,128)(2,1)S(1)} %get-tuple-element.42), channel_id=1, source_target_pairs={{0,32},{32,64},{64,96},{96,0},{1,33},{33,65},{65,97},{97,1},{2,34}... | collective-permute-start | bytes 835592 | tf_op jit(solution)/shard_map/ppermute | solution.py:19
  44.9 10.4 %collective-permute-start.13 = (bf16[16,32,256]{2,1,0:T(8,128)(2,1)S(1)}, bf16[16,32,256]{2,1,0:T(8,128)(2,1)S(1)}, u32[]{:S(2)}, u32[]{:S(2)}) collective-permute-start(bf16[16,32,256]{2,1,0:T(8,128)(2,1)S(1)} %get-tuple-element.60.a_ref), channel_id=1, source_target_pairs={{0,32},{32,64},{64,96},{96,0},{1,33},{33,65},{65,97},{97,1},{2,34}... | collective-permute-start | bytes 786440 | tf_op jit(solution)/shard_map/ppermute | solution.py:19
  45.0 10.3 %collective-permute-start.14 = (bf16[16,32,256]{2,1,0:T(8,128)(2,1)S(1)}, bf16[16,32,256]{2,1,0:T(8,128)(2,1)S(1)}, u32[]{:S(2)}, u32[]{:S(2)}) collective-permute-start(bf16[16,32,256]{2,1,0:T(8,128)(2,1)S(1)} %get-tuple-element.59.b_ref), channel_id=1, source_target_pairs={{0,96},{32,0},{64,32},{96,64},{1,97},{33,1},{65,33},{97,65},{2,98}... | collective-permute-start | bytes 786440 | tf_op jit(solution)/shard_map/ppermute | solution.py:19
  47.7 6.2 %collective-permute-start.15 = (bf16[34,256]{1,0:T(8,128)(2,1)S(1)}, bf16[34,256]{1,0:T(8,128)(2,1)S(1)}, u32[]{:S(2)}, u32[]{:S(2)}) collective-permute-start(bf16[34,256]{1,0:T(8,128)(2,1)S(1)} %get-tuple-element.51), channel_id=1, source_target_pairs={{0,1},{1,2},{2,3},{3,4},{4,5},{5,6},{6,7},{7,8},{8,9},{9,10},{10,1... | collective-permute-start | bytes 52232 | tf_op jit(solution)/shard_map/ppermute | solution.py:398
  50.8 4.5 %collective-permute-start.16 = (bf16[34,256]{1,0:T(8,128)(2,1)S(1)}, bf16[34,256]{1,0:T(8,128)(2,1)S(1)}, u32[]{:S(2)}, u32[]{:S(2)}) collective-permute-start(bf16[34,256]{1,0:T(8,128)(2,1)S(1)} %get-tuple-element.52), channel_id=1, source_target_pairs={{1,0},{2,1},{3,2},{4,3},{5,4},{6,5},{7,6},{8,7},{9,8},{10,9},{11,1... | collective-permute-start | bytes 52232 | tf_op jit(solution)/shard_map/ppermute | solution.py:398
  55.3 7.6 %collective-permute-start.19 = (bf16[16,32,256]{2,1,0:T(8,128)(2,1)S(1)}, bf16[16,32,256]{2,1,0:T(8,128)(2,1)S(1)}, u32[]{:S(2)}, u32[]{:S(2)}) collective-permute-start(bf16[16,32,256]{2,1,0:T(8,128)(2,1)S(1)} %get-tuple-element.59.b_ref), channel_id=1, source_target_pairs={{0,32},{32,64},{64,96},{96,0},{1,33},{33,65},{65,97},{97,1},{2,34}... | collective-permute-start | bytes 786440 | tf_op jit(solution)/shard_map/ppermute | solution.py:19
  55.3 7.6 %collective-permute-start.20 = (bf16[16,32,256]{2,1,0:T(8,128)(2,1)S(1)}, bf16[16,32,256]{2,1,0:T(8,128)(2,1)S(1)}, u32[]{:S(2)}, u32[]{:S(2)}) collective-permute-start(bf16[16,32,256]{2,1,0:T(8,128)(2,1)S(1)} %get-tuple-element.60.a_ref), channel_id=1, source_target_pairs={{0,96},{32,0},{64,32},{96,64},{1,97},{33,1},{65,33},{97,65},{2,98}... | collective-permute-start | bytes 786440 | tf_op jit(solution)/shard_map/ppermute | solution.py:19
  58.0 13.8 %collective-permute-start.17 = (bf16[16,32,256]{2,1,0:T(8,128)(2,1)S(1)}, bf16[16,32,256]{2,1,0:T(8,128)(2,1)S(1)}, u32[]{:S(2)}, u32[]{:S(2)}) collective-permute-start(bf16[16,32,256]{2,1,0:T(8,128)(2,1)S(1)} %collective-permute-done.13.a_ref), channel_id=1, source_target_pairs={{0,32},{32,64},{64,96},{96,0},{1,33},{33,65},{65,97},{97,1},{2,34}... | collective-permute-start | bytes 786440 | tf_op jit(solution)/shard_map/ppermute | solution.py:19
  58.0 13.8 %collective-permute-start.18 = (bf16[16,32,256]{2,1,0:T(8,128)(2,1)S(1)}, bf16[16,32,256]{2,1,0:T(8,128)(2,1)S(1)}, u32[]{:S(2)}, u32[]{:S(2)}) collective-permute-start(bf16[16,32,256]{2,1,0:T(8,128)(2,1)S(1)} %collective-permute-done.14.b_ref), channel_id=1, source_target_pairs={{0,96},{32,0},{64,32},{96,64},{1,97},{33,1},{65,33},{97,65},{2,98}... | collective-permute-start | bytes 786440 | tf_op jit(solution)/shard_map/ppermute | solution.py:19
  63.0 10.7 %collective-permute-start.22 = (bf16[4,288,256]{2,1,0:T(8,128)(2,1)S(1)}, bf16[4,288,256]{2,1,0:T(8,128)(2,1)S(1)}, u32[]{:S(2)}, u32[]{:S(2)}) collective-permute-start(bf16[4,288,256]{2,1,0:T(8,128)(2,1)S(1)} %get-tuple-element.67), channel_id=1, source_target_pairs={{0,16},{16,0},{1,17},{17,1},{2,18},{18,2},{3,19},{19,3},{4,20},{20... | collective-permute-start | bytes 1769480 | tf_op jit(solution)/shard_map/ppermute | solution.py:19
  73.8 6.2 %collective-permute-start.23 = (bf16[288,256]{1,0:T(8,128)(2,1)S(1)}, bf16[288,256]{1,0:T(8,128)(2,1)S(1)}, u32[]{:S(2)}, u32[]{:S(2)}) collective-permute-start(bf16[288,256]{1,0:T(8,128)(2,1)S(1)} %get-tuple-element.69), channel_id=1, source_target_pairs={{0,32},{32,64},{64,96},{96,0},{1,33},{33,65},{65,97},{97,1},{2,34}... | collective-permute-start | bytes 442376 | tf_op jit(solution)/shard_map/ppermute | solution.py:19
  73.9 6.1 %collective-permute-start.24 = (bf16[288,256]{1,0:T(8,128)(2,1)S(1)}, bf16[288,256]{1,0:T(8,128)(2,1)S(1)}, u32[]{:S(2)}, u32[]{:S(2)}) collective-permute-start(bf16[288,256]{1,0:T(8,128)(2,1)S(1)} %get-tuple-element.70), channel_id=1, source_target_pairs={{0,96},{32,0},{64,32},{96,64},{1,97},{33,1},{65,33},{97,65},{2,98}... | collective-permute-start | bytes 442376 | tf_op jit(solution)/shard_map/ppermute | solution.py:19
  76.6 7.7 %collective-permute-start.25 = (bf16[288,256]{1,0:T(8,128)(2,1)S(1)}, bf16[288,256]{1,0:T(8,128)(2,1)S(1)}, u32[]{:S(2)}, u32[]{:S(2)}) collective-permute-start(bf16[288,256]{1,0:T(8,128)(2,1)S(1)} %get-tuple-element.71), channel_id=1, source_target_pairs={{0,64},{32,96},{64,0},{96,32},{1,65},{33,97},{65,1},{97,33},{2,66}... | collective-permute-start | bytes 442376 | tf_op jit(solution)/shard_map/ppermute | solution.py:19
  109.9 4.5 %collective-permute-start.28 = (bf16[90,256]{1,0:T(8,128)(2,1)S(1)}, bf16[90,256]{1,0:T(8,128)(2,1)S(1)}, u32[]{:S(2)}, u32[]{:S(2)}) collective-permute-start(bf16[90,256]{1,0:T(8,128)(2,1)S(1)} %sum_pieces.1.a_ref), channel_id=1, source_target_pairs={{0,8},{4,12},{8,0},{12,4},{1,9},{5,13},{9,1},{13,5},{2,10},{6,14},... | collective-permute-start | bytes 138248 | tf_op jit(solution)/shard_map/ppermute | solution.py:19
  114.4 5.7 %collective-permute-start.29 = (bf16[360,256]{1,0:T(8,128)(2,1)S(1)}, bf16[360,256]{1,0:T(8,128)(2,1)S(1)}, u32[]{:S(2)}, u32[]{:S(2)}) collective-permute-start(bf16[360,256]{1,0:T(8,128)(2,1)S(1)} %order_pieces.1.a_ref), channel_id=1, source_target_pairs={{0,1},{1,2},{2,3},{3,0},{4,5},{5,6},{6,7},{7,4},{8,9},{9,10},{10,1... | collective-permute-start | bytes 552968 | tf_op jit(solution)/shard_map/ppermute | solution.py:19
  115.1 6.5 %collective-permute-start.30 = (bf16[360,256]{1,0:T(8,128)(2,1)S(1)}, bf16[360,256]{1,0:T(8,128)(2,1)S(1)}, u32[]{:S(2)}, u32[]{:S(2)}) collective-permute-start(bf16[360,256]{1,0:T(8,128)(2,1)S(1)} %order_pieces.1.a_ref), channel_id=1, source_target_pairs={{0,3},{1,0},{2,1},{3,2},{4,7},{5,4},{6,5},{7,6},{8,11},{9,8},{10,9... | collective-permute-start | bytes 552968 | tf_op jit(solution)/shard_map/ppermute | solution.py:19
  117.2 7.0 %collective-permute-start.31 = (bf16[360,256]{1,0:T(8,128)(2,1)S(1)}, bf16[360,256]{1,0:T(8,128)(2,1)S(1)}, u32[]{:S(2)}, u32[]{:S(2)}) collective-permute-start(bf16[360,256]{1,0:T(8,128)(2,1)S(1)} %order_pieces.1.a_ref), channel_id=1, source_target_pairs={{0,2},{1,3},{2,0},{3,1},{4,6},{5,7},{6,4},{7,5},{8,10},{9,11},{10,... | collective-permute-start | bytes 552968 | tf_op jit(solution)/shard_map/ppermute | solution.py:19
  124.2 5.3 %collective-permute-start.32 = (bf16[4,72,256]{2,1,0:T(8,128)(2,1)S(1)}, bf16[4,72,256]{2,1,0:T(8,128)(2,1)S(1)}, u32[]{:S(2)}, u32[]{:S(2)}) collective-permute-start(bf16[4,72,256]{2,1,0:T(8,128)(2,1)S(1)} %pick_rows.1), channel_id=1, source_target_pairs={{0,32},{32,64},{64,96},{96,0},{1,33},{33,65},{65,97},{97,1},{2,34}... | collective-permute-start | bytes 442376 | tf_op jit(solution)/shard_map/ppermute | solution.py:19
  124.4 6.1 %collective-permute-start.33 = (bf16[4,72,256]{2,1,0:T(8,128)(2,1)S(1)}, bf16[4,72,256]{2,1,0:T(8,128)(2,1)S(1)}, u32[]{:S(2)}, u32[]{:S(2)}) collective-permute-start(bf16[4,72,256]{2,1,0:T(8,128)(2,1)S(1)} %pick_rows.1), channel_id=1, source_target_pairs={{0,96},{32,0},{64,32},{96,64},{1,97},{33,1},{65,33},{97,65},{2,98}... | collective-permute-start | bytes 442376 | tf_op jit(solution)/shard_map/ppermute | solution.py:19
  126.9 5.5 %collective-permute-start.34 = (bf16[4,72,256]{2,1,0:T(8,128)(2,1)S(1)}, bf16[4,72,256]{2,1,0:T(8,128)(2,1)S(1)}, u32[]{:S(2)}, u32[]{:S(2)}) collective-permute-start(bf16[4,72,256]{2,1,0:T(8,128)(2,1)S(1)} %pick_rows.1), channel_id=1, source_target_pairs={{0,64},{32,96},{64,0},{96,32},{1,65},{33,97},{65,1},{97,33},{2,66}... | collective-permute-start | bytes 442376 | tf_op jit(solution)/shard_map/ppermute | solution.py:19
  132.5 9.1 %collective-permute-start.35 = (bf16[4,4,72,256]{3,2,1,0:T(8,128)(2,1)S(1)}, bf16[4,4,72,256]{3,2,1,0:T(8,128)(2,1)S(1)}, u32[]{:S(2)}, u32[]{:S(2)}) collective-permute-start(bf16[4,4,72,256]{3,2,1,0:T(8,128)(2,1)S(1)} %pad_maximum_fusion.1.in_ref), channel_id=1, source_target_pairs={{0,16},{16,0},{1,17},{17,1},{2,18},{18,2},{3,19},{19,3},{4,20},{20... | collective-permute-start | bytes 1769480 | tf_op jit(solution)/shard_map/ppermute | solution.py:19
  (7 other events, 33.3 us)

commit v10 on v9

--- a/solution.py
+++ b/solution.py
@@ -133,15 +133,16 @@
     )(wide, kernel, *adds)
 
 
-def grad_kernel(step, has_old, last, wide_ref, a_ref, b_ref, *refs):
+def grad_kernel(step, pieces, has_old, last, wide_ref, *refs):
+    piece_refs, refs = refs[:pieces], refs[pieces:]
     old_ref = refs[0] if has_old else None
     outs_refs, pad_ref = refs[1 if has_old else 0 : -1], refs[-1]
-    half, rows, outs = a_ref.shape
-    strip = 2 * half
+    count, rows, outs = piece_refs[0].shape
+    strip = pieces * count
     cols, depth = wide_ref.shape[1], wide_ref.shape[3]
     pad_ref[0:3] = jnp.zeros((3, rows, outs), BF16)
-    pad_ref[3 : 3 + half] = a_ref[...]
-    pad_ref[3 + half : 3 + strip] = b_ref[...]
+    for i, ref in enumerate(piece_refs):
+        pad_ref[3 + i * count : 3 + (i + 1) * count] = ref[...]
     pad_ref[3 + strip :] = jnp.zeros((cols - strip - 1, rows, outs), BF16)
     lhs = wide_ref[chip_at(step)].reshape(cols * rows, depth)
     rhs = jnp.concatenate(
@@ -162,8 +163,8 @@
             ].astype(BF16)
 
 
-def grad_strip(step, wide, halves, old, last):
-    _, rows, outs = halves[0].shape
+def grad_strip(step, wide, pieces, old, last):
+    _, rows, outs = pieces[0].shape
     depth, cols = wide.shape[3], wide.shape[1]
     shape = (depth, 3 * outs)
     half = (depth // 2, 3 * outs)
@@ -171,9 +172,9 @@
         out_shape = (jax.ShapeDtypeStruct(half, F32), jax.ShapeDtypeStruct(half, BF16))
     else:
         out_shape = (jax.ShapeDtypeStruct(shape, F32),)
-    args = [wide, *halves] + ([old] if old is not None else [])
+    args = [wide, *pieces] + ([old] if old is not None else [])
     out = pl.pallas_call(
-        functools.partial(grad_kernel, step, old is not None, last),
+        functools.partial(grad_kernel, step, len(pieces), old is not None, last),
         out_shape=out_shape,
         in_specs=[VMEM_SPEC] * len(args),
         out_specs=tuple([VMEM_SPEC] * len(out_shape)),
@@ -323,14 +324,14 @@
 
 def point_kernel(
     own_ref, a0_ref, a1_ref, b0_ref, b1_ref, back_ref,
-    da_ref, db_ref, hidden_ref, last_ref, first_ref,
+    delta_ref, hidden_ref, last_ref, first_ref,
 ):
     cols, rows, _ = own_ref.shape
-    half = da_ref.shape[0]
+    half = delta_ref.shape[0] // 2
     strip = 2 * lax.axis_index("y") + lax.axis_index("c")
     strips = 2 * lax.axis_size("y")
 
-    def column(j, i, refs, delta_ref, keep):
+    def column(j, i, refs, keep):
         pre = own_ref[j] + refs[0][i].astype(F32) + refs[1][i].astype(F32)
         sigma = jax.nn.sigmoid(pre)
         hidden = pre * sigma
@@ -342,27 +343,26 @@
         first_ref[j : j + 1, :] = hidden[:1]
         if keep is None:
             slope = sigma * (1.0 + pre * (1.0 - sigma))
-            at = j - 1 if delta_ref is da_ref else j - 1 - half
-            delta_ref[at] = (back_ref[j - 1] * slope).astype(BF16)
+            delta_ref[j - 1] = (back_ref[j - 1] * slope).astype(BF16)
 
     left, right = (a0_ref, a1_ref), (b0_ref, b1_ref)
-    column(0, 0, left, None, strip > 0)
-    column(cols - 1, half, right, None, strip < strips - 1)
+    column(0, 0, left, strip > 0)
+    column(cols - 1, half, right, strip < strips - 1)
 
     for i in range(1, half + 1):
-        column(i, i, left, da_ref, None)
-        column(half + i, i - 1, right, db_ref, None)
+        column(i, i, left, None)
+        column(half + i, i - 1, right, None)
 
 
 def point(own, left, right, back):
     strip, rows, outs = back.shape
-    cut = jax.ShapeDtypeStruct((strip // 2, rows, outs), BF16)
+    delta = jax.ShapeDtypeStruct(back.shape, BF16)
     edge = jax.ShapeDtypeStruct((strip + 2, outs), BF16)
     return pl.pallas_call(
         point_kernel,
-        out_shape=(cut, cut, jax.ShapeDtypeStruct(own.shape, BF16), edge, edge),
+        out_shape=(delta, jax.ShapeDtypeStruct(own.shape, BF16), edge, edge),
         in_specs=[VMEM_SPEC] * 6,
-        out_specs=(VMEM_SPEC,) * 5,
+        out_specs=(VMEM_SPEC,) * 4,
         compiler_params=pltpu.CompilerParams(vmem_limit_bytes=2 * 2**20),
         cost_estimate=QUICK,
         name="point",
@@ -633,25 +633,22 @@
     from_b = shift(near_b, "y", on), shift(both_b, "y", off)
 
     back = back_tile(cotangent, left, right, edges, weight_second)
-    delta_a, delta_b, hidden, *ends = point(own, from_a, from_b, back)
-
-    on_a, off_b = shift(delta_a, "y", on), shift(delta_b, "y", off)
+    delta, hidden, *ends = point(own, from_a, from_b, back)
+
+    from_on, from_off = shift(delta, "y", on), shift(delta, "y", off)
+    half = strip // 2
+    fwd_a, fwd_b = shift(from_on[:half], "y", on), shift(from_off[half:], "y", off)
     edges = row_halo(ends)
-    total = grad_strip(0, wide, (delta_a, delta_b), None, False)
-    on_a, off_b, edges, late_a, late_b, total = lax.optimization_barrier(
-        (on_a, off_b, edges, delta_a, delta_b, total)
-    )
-    on_b, off_a = shift(late_b, "y", on), shift(late_a, "y", off)
-    fwd_a, fwd_b = shift(on_a, "y", on), shift(off_b, "y", off)
+    total = grad_strip(0, wide, (delta,), None, False)
     wide_hidden, near, far = second_tile(hidden, edges, cotangent, chips)
-    far, on_b, off_a = lax.optimization_barrier((far, on_b, off_a))
     keep, *sends = fold(near, shift(far, "c", 1))
     got = [shift(send, "y", step) for step, send in zip(STEPS[1:], sends)]
-    total = grad_strip(off, wide, (on_a, on_b), total, False)
-    total = grad_strip(on, wide, (off_a, off_b), total, False)
+    total = grad_strip(off, wide, (from_on,), total, False)
+    total = grad_strip(on, wide, (from_off,), total, False)
     first_own, first_far = grad_strip(2, wide, (fwd_a, fwd_b), total, True)
 
     sx, sz = lax.axis_size("x"), lax.axis_size("z")
+    first_far, *got = lax.optimization_barrier((first_far, *got))
     joined = join(first_own, shift(first_far, "c", 1), keep, got, sx * sz)
     extra = keep.shape[0] // (sx * sz)
     summed = lax.all_to_all(joined, SKY, 0, 0, tiled=True)
@@ -662,7 +659,9 @@
     features = features_tile(wide_hidden, weight_second, strip)
     share = pick_rows(parts, main)
     share, features = lax.optimization_barrier((share, features))
-    share = jnp.stack(gather_steps(share, "y"))
+    share, grad_first = lax.optimization_barrier(
+        (jnp.stack(gather_steps(share, "y")), grad_first)
+    )
     grad_second = lay_second(shift(share, "c", 1), lay_second(share))
     grad_second = grad_second.reshape(3, 3, outs, outs)
     return features, grad_first, grad_second

time: 143 us -> 139 us (0.972)
  waiting for transfers between devices: 33.8 us -> 26 us
  blocking collectives: 22.6 us -> 27.1 us
    ppermute x30 -> x28, waiting for transfers between devices: 28.4 us -> 21.7 us  [shift(): lax.ppermute(x, axis, [(i, (i + step) % count) for i in range(count)])]
    all_to_all x1, blocking collectives: 22.6 us -> 27.1 us  [body(): summed = lax.all_to_all(joined, SKY, 0, 0, tiled=True)]
    ppermute x30 -> x28, starting transfers between devices: 42.4 us -> 38.7 us  [shift(): lax.ppermute(x, axis, [(i, (i + step) % count) for i in range(count)])]
    ppermute x4, starting transfers between devices: 8.89 us -> 11.1 us  [row_halo(): return (lax.ppermute(ends[0], SKY, up), lax.ppermute(ends[1], SKY, down))]
  transfers between devices with their start and end apart: 36 -> 34, of which waited for: 16 -> 14; matrix products, arithmetic and copies ran while one was open for 3% -> 3% of each run, Pallas kernels for 14% -> 14%
where the time goes in v10:
time: 139 us; the launch traced here: 138 us
  starting transfers between devices  54.3 us (39%)
  blocking collectives  27.1 us (19%)
  waiting for transfers between devices  26 us (19%)
  Pallas kernels  25.1 us (18%)
  local copies, waits for them, and re-layouts  3.25 us (2%)
    ppermute x28, starting transfers between devices, shift(): lax.ppermute(x, axis, [(i, (i + step) % count) for i in range(count)])  38.7 us
    all_to_all x1, blocking collectives, body(): summed = lax.all_to_all(joined, SKY, 0, 0, tiled=True)  27.1 us
    ppermute x28, waiting for transfers between devices, shift(): lax.ppermute(x, axis, [(i, (i + step) % count) for i in range(count)])  21.7 us
    ppermute x4, starting transfers between devices, row_halo(): return (lax.ppermute(ends[0], SKY, up), lax.ppermute(ends[1], SKY, down))  11.1 us
    pallas_call x4, Pallas kernels, grad_strip(): pl.pallas_call(functools.partial(grad_kernel, step, len(pieces), old is n...  7.02 us
    pallas_call x4, Pallas kernels, conv_parts(): pl.pallas_call(functools.partial(conv_kernel, parts, len(adds)), out_shap...  5.84 us
    ppermute x4, waiting for transfers between devices, row_halo(): return (lax.ppermute(ends[0], SKY, up), lax.ppermute(ends[1], SKY, down))  4.37 us
  transfers between devices with their start and end apart: 34, of which 14 were waited for; matrix products, arithmetic and copies ran while one was open for 3% of the time, Pallas kernels for 14%

profile of v10, /device:TPU:1, one launch (start us, length us, event | category | flops | bytes accessed | tf_op | source)
XLA Modules:
  0.0 138.3 jit_solution(10398732214602164982)
XLA Ops:
  0.6 1.5 %collective-permute-start = (bf16[256,32,128]{2,1,0:T(8,128)(2,1)}, bf16[256,32,128]{2,1,0:T(8,128)(2,1)S(1)}, u32[]{:S(2)}, u32[]{:S(2)}) collective-permute-start(bf16[256,32,128]{2,1,0:T(8,128)(2,1)} %own_ref.1), channel_id=1, source_target_pairs={{0,16},{16,0},{1,17},{17,1},{2,18},{18,2},{3,19},{19,3},{4,20},{20... | collective-permute-start | bytes 6291464 | tf_op jit(solution)/shard_map/ppermute | solution.py:19
  6.2 4.3 %collective-permute-start.1 = (bf16[320,128]{1,0:T(8,128)(2,1)S(1)}, bf16[320,128]{1,0:T(8,128)(2,1)S(1)}, u32[]{:S(2)}, u32[]{:S(2)}) collective-permute-start(bf16[320,128]{1,0:T(8,128)(2,1)S(1)} %pad_maximum_fusion.3), channel_id=1, source_target_pairs={{0,1},{1,2},{2,3},{3,4},{4,5},{5,6},{6,7},{7,8},{8,9},{9,10},{10,1... | collective-permute-start | bytes 245768 | tf_op jit(solution)/shard_map/ppermute | solution.py:398
  14.4 1.9 %spread.1.wide_ref = bf16[4,40,32,768]{3,2,1,0:T(8,128)(2,1)S(1)} custom-call(bf16[256,32,128]{2,1,0:T(8,128)(2,1)S(1)} %copy-done.1, bf16[256,32,128]{2,1,0:T(8,128)(2,1)S(1)} %collective-permute-done.far_ref, bf16[2,320,128]{2,1,0:T(8,128)(2,1)S(1)} %pad_maximum_fusion.2.own_halo_ref.edge_ref, bf16[2,320,128]{2,1,0:T(8,128)(2,1)S(1)} %collective-permute-done.3.far_halo_ref), custom_call_target="tpu_custom_call" | custom-call | flops 1 | bytes 1 | tf_op jit(solution)/shard_map/spread/pallas_call | solution.py:94
  17.8 2.9 %collective-permute-start.8 = (bf16[17,32,256]{2,1,0:T(8,128)(2,1)S(1)}, bf16[17,32,256]{2,1,0:T(8,128)(2,1)S(1)}, u32[]{:S(2)}, u32[]{:S(2)}) collective-permute-start(bf16[17,32,256]{2,1,0:T(8,128)(2,1)S(1)} %get-tuple-element.36), channel_id=1, source_target_pairs={{0,96},{32,0},{64,32},{96,64},{1,97},{33,1},{65,33},{97,65},{2,98}... | collective-permute-start | bytes 835592 | tf_op jit(solution)/shard_map/ppermute | solution.py:19
  20.7 2.6 %collective-permute-start.6 = (bf16[34,256]{1,0:T(8,128)(2,1)S(1)}, bf16[34,256]{1,0:T(8,128)(2,1)S(1)}, u32[]{:S(2)}, u32[]{:S(2)}) collective-permute-start(bf16[34,256]{1,0:T(8,128)(2,1)S(1)} %maximum_maximum_fusion), channel_id=1, source_target_pairs={{0,16},{16,32},{32,48},{48,64},{64,80},{80,96},{96,112},{1,17},{17... | collective-permute-start | bytes 52232 | tf_op jit(solution)/shard_map/ppermute | solution.py:620
  23.3 1.9 %collective-permute-start.7 = (bf16[34,256]{1,0:T(8,128)(2,1)S(1)}, bf16[34,256]{1,0:T(8,128)(2,1)S(1)}, u32[]{:S(2)}, u32[]{:S(2)}) collective-permute-start(bf16[34,256]{1,0:T(8,128)(2,1)S(1)} %maximum_maximum_fusion.1), channel_id=1, source_target_pairs={{16,0},{32,16},{48,32},{64,48},{80,64},{96,80},{112,96},{17,1},{33... | collective-permute-start | bytes 52232 | tf_op jit(solution)/shard_map/ppermute | solution.py:621
  26.7 2.8 %collective-permute-start.10 = (bf16[17,32,256]{2,1,0:T(8,128)(2,1)S(1)}, bf16[17,32,256]{2,1,0:T(8,128)(2,1)S(1)}, u32[]{:S(2)}, u32[]{:S(2)}) collective-permute-start(bf16[17,32,256]{2,1,0:T(8,128)(2,1)S(1)} %get-tuple-element.39), channel_id=1, source_target_pairs={{0,96},{32,0},{64,32},{96,64},{1,97},{33,1},{65,33},{97,65},{2,98}... | collective-permute-start | bytes 835592 | tf_op jit(solution)/shard_map/ppermute | solution.py:19
  29.6 1.5 %conv_first.6 = (bf16[17,32,256]{2,1,0:T(8,128)(2,1)S(1)}, bf16[17,32,256]{2,1,0:T(8,128)(2,1)S(1)}) custom-call(bf16[4,40,32,768]{3,2,1,0:T(8,128)(2,1)S(1)} %spread.1.wide_ref, bf16[2304,256]{1,0:T(8,128)(2,1)S(1)} %bitcast.45, bf16[17,32,256]{2,1,0:T(8,128)(2,1)S(1)} %collective-permute-done.5.refs_0_, bf16[17,32,256]{2,1,0:T(8,128)(2,1)S(1)} %collective-permute-done.8.refs_1_), custom_call_target="tpu_custom_call" | custom-call | flops 1 | bytes 1 | tf_op jit(solution)/shard_map/conv_first/pallas_call | solution.py:125
  31.9 1.9 %collective-permute-start.12 = (bf16[17,32,256]{2,1,0:T(8,128)(2,1)S(1)}, bf16[17,32,256]{2,1,0:T(8,128)(2,1)S(1)}, u32[]{:S(2)}, u32[]{:S(2)}) collective-permute-start(bf16[17,32,256]{2,1,0:T(8,128)(2,1)S(1)} %get-tuple-element.41), channel_id=1, source_target_pairs={{0,96},{32,0},{64,32},{96,64},{1,97},{33,1},{65,33},{97,65},{2,98}... | collective-permute-start | bytes 835592 | tf_op jit(solution)/shard_map/ppermute | solution.py:19
  33.8 1.5 %conv_first.4.own_ref = f32[34,32,256]{2,1,0:T(8,128)S(1)} custom-call(bf16[4,40,32,768]{3,2,1,0:T(8,128)(2,1)S(1)} %spread.1.wide_ref, bf16[2304,256]{1,0:T(8,128)(2,1)S(1)} %bitcast.46), custom_call_target="tpu_custom_call" | custom-call | flops 1 | bytes 1 | tf_op jit(solution)/shard_map/conv_first/pallas_call | solution.py:125
  36.8 6.0 %collective-permute-done.9.a0_ref = bf16[17,32,256]{2,1,0:T(8,128)(2,1)S(1)} collective-permute-done((bf16[17,32,256]{2,1,0:T(8,128)(2,1)S(1)}, bf16[17,32,256]{2,1,0:T(8,128)(2,1)S(1)}, u32[]{:S(2)}, u32[]{:S(2)}) %collective-permute-start.9) | collective-permute-done | bytes 278560 | tf_op jit(solution)/shard_map/ppermute | solution.py:19
  43.3 1.8 %collective-permute-start.15 = (bf16[32,32,256]{2,1,0:T(8,128)(2,1)S(1)}, bf16[32,32,256]{2,1,0:T(8,128)(2,1)S(1)}, u32[]{:S(2)}, u32[]{:S(2)}) collective-permute-start(bf16[32,32,256]{2,1,0:T(8,128)(2,1)S(1)} %get-tuple-element.44.refs_0_), channel_id=1, source_target_pairs={{0,96},{32,0},{64,32},{96,64},{1,97},{33,1},{65,33},{97,65},{2,98}... | collective-permute-start | bytes 1572872 | tf_op jit(solution)/shard_map/ppermute | solution.py:19
  45.2 4.1 %collective-permute-start.17 = (bf16[34,256]{1,0:T(8,128)(2,1)S(1)}, bf16[34,256]{1,0:T(8,128)(2,1)S(1)}, u32[]{:S(2)}, u32[]{:S(2)}) collective-permute-start(bf16[34,256]{1,0:T(8,128)(2,1)S(1)} %get-tuple-element.48), channel_id=1, source_target_pairs={{0,1},{1,2},{2,3},{3,4},{4,5},{5,6},{6,7},{7,8},{8,9},{9,10},{10,1... | collective-permute-start | bytes 52232 | tf_op jit(solution)/shard_map/ppermute | solution.py:398
  49.3 1.5 %collective-permute-start.18 = (bf16[34,256]{1,0:T(8,128)(2,1)S(1)}, bf16[34,256]{1,0:T(8,128)(2,1)S(1)}, u32[]{:S(2)}, u32[]{:S(2)}) collective-permute-start(bf16[34,256]{1,0:T(8,128)(2,1)S(1)} %get-tuple-element.49), channel_id=1, source_target_pairs={{1,0},{2,1},{3,2},{4,3},{5,4},{6,5},{7,6},{8,7},{9,8},{10,9},{11,1... | collective-permute-start | bytes 52232 | tf_op jit(solution)/shard_map/ppermute | solution.py:398
  50.8 3.3 %collective-permute-done.18.after_ref = bf16[34,256]{1,0:T(8,128)(2,1)S(1)} collective-permute-done((bf16[34,256]{1,0:T(8,128)(2,1)S(1)}, bf16[34,256]{1,0:T(8,128)(2,1)S(1)}, u32[]{:S(2)}, u32[]{:S(2)}) %collective-permute-start.18) | collective-permute-done | bytes 17440 | tf_op jit(solution)/shard_map/ppermute | solution.py:398
  54.1 2.3 %second.1 = (bf16[40,32,768]{2,1,0:T(8,128)(2,1)S(1)}, f32[4,288,256]{2,1,0:T(8,128)S(1)}, bf16[4,288,256]{2,1,0:T(8,128)(2,1)S(1)}) custom-call(bf16[34,32,256]{2,1,0:T(8,128)(2,1)S(1)} %get-tuple-element.47.hid_ref, bf16[34,256]{1,0:T(8,128)(2,1)S(1)} %collective-permute-done.17.before_ref, bf16[34,256]{1,0:T(8,128)(2,1)S(1)} %collective-permute-done.18.after_ref, ...), custom_call_target="tpu_custom_call" | custom-call | flops 1 | bytes 1 | tf_op jit(solution)/shard_map/second/pallas_call | solution.py:285
  56.4 4.4 %collective-permute-start.19 = (bf16[4,288,256]{2,1,0:T(8,128)(2,1)S(1)}, bf16[4,288,256]{2,1,0:T(8,128)(2,1)S(1)}, u32[]{:S(2)}, u32[]{:S(2)}) collective-permute-start(bf16[4,288,256]{2,1,0:T(8,128)(2,1)S(1)} %get-tuple-element.51), channel_id=1, source_target_pairs={{0,16},{16,0},{1,17},{17,1},{2,18},{18,2},{3,19},{19,3},{4,20},{20... | collective-permute-start | bytes 1769480 | tf_op jit(solution)/shard_map/ppermute | solution.py:19
  62.7 2.6 %collective-permute-start.21 = (bf16[288,256]{1,0:T(8,128)(2,1)S(1)}, bf16[288,256]{1,0:T(8,128)(2,1)S(1)}, u32[]{:S(2)}, u32[]{:S(2)}) collective-permute-start(bf16[288,256]{1,0:T(8,128)(2,1)S(1)} %get-tuple-element.53), channel_id=1, source_target_pairs={{0,96},{32,0},{64,32},{96,64},{1,97},{33,1},{65,33},{97,65},{2,98}... | collective-permute-start | bytes 442376 | tf_op jit(solution)/shard_map/ppermute | solution.py:19
  66.4 1.8 %grad_first.4.refs_1_ = f32[768,768]{1,0:T(8,128)S(1)} custom-call(bf16[4,40,32,768]{3,2,1,0:T(8,128)(2,1)S(1)} %spread.1.wide_ref, bf16[32,32,256]{2,1,0:T(8,128)(2,1)S(1)} %get-tuple-element.44.refs_0_), custom_call_target="tpu_custom_call" | custom-call | flops 1 | bytes 1 | tf_op jit(solution)/shard_map/grad_first/pallas_call | solution.py:176
  68.2 1.7 %grad_first.5.refs_1_ = f32[768,768]{1,0:T(8,128)S(1)} custom-call(bf16[4,40,32,768]{3,2,1,0:T(8,128)(2,1)S(1)} %spread.1.wide_ref, bf16[32,32,256]{2,1,0:T(8,128)(2,1)S(1)} %collective-permute-done.13.refs_0_, f32[768,768]{1,0:T(8,128)S(1)} %grad_first.4.refs_1_), custom_call_target="tpu_custom_call" | custom-call | flops 1 | bytes 1 | tf_op jit(solution)/shard_map/grad_first/pallas_call | solution.py:176
  69.9 1.8 %grad_first.6.refs_2_ = f32[768,768]{1,0:T(8,128)S(1)} custom-call(bf16[4,40,32,768]{3,2,1,0:T(8,128)(2,1)S(1)} %spread.1.wide_ref, bf16[32,32,256]{2,1,0:T(8,128)(2,1)S(1)} %collective-permute-done.15.refs_0_, f32[768,768]{1,0:T(8,128)S(1)} %grad_first.5.refs_1_), custom_call_target="tpu_custom_call" | custom-call | flops 1 | bytes 1 | tf_op jit(solution)/shard_map/grad_first/pallas_call | solution.py:176
  71.7 1.8 %grad_first.7 = (f32[384,768]{1,0:T(8,128)S(1)}, bf16[384,768]{1,0:T(8,128)(2,1)S(1)}) custom-call(bf16[4,40,32,768]{3,2,1,0:T(8,128)(2,1)S(1)} %spread.1.wide_ref, bf16[16,32,256]{2,1,0:T(8,128)(2,1)S(1)} %collective-permute-done.14.refs_0_, bf16[16,32,256]{2,1,0:T(8,128)(2,1)S(1)} %collective-permute-done.16.refs_1_, f32[768,768]{1,0:T(8,128)S(1)} %grad_first.6.refs_2_), custom_call_target="tpu_custom_call" | custom-call | flops 1 | bytes 1 | tf_op jit(solution)/shard_map/grad_first/pallas_call | solution.py:176
  73.5 4.0 %collective-permute-done.20.a_ref = bf16[288,256]{1,0:T(8,128)(2,1)S(1)} collective-permute-done((bf16[288,256]{1,0:T(8,128)(2,1)S(1)}, bf16[288,256]{1,0:T(8,128)(2,1)S(1)}, u32[]{:S(2)}, u32[]{:S(2)}) %collective-permute-start.20) | collective-permute-done | bytes 147488 | tf_op jit(solution)/shard_map/ppermute | solution.py:19
  78.6 1.6 %collective-permute-done.23.far_ref = bf16[384,768]{1,0:T(8,128)(2,1)S(1)} collective-permute-done((bf16[384,768]{1,0:T(8,128)(2,1)S(1)}, bf16[384,768]{1,0:T(8,128)(2,1)S(1)}, u32[]{:S(2)}, u32[]{:S(2)}) %collective-permute-start.23) | collective-permute-done | bytes 589856 | tf_op jit(solution)/shard_map/ppermute | solution.py:19
  80.4 27.1 %all_to_all.5.in_ref = bf16[16,90,256]{2,1,0:T(8,128)(2,1)S(1)} all-to-all(bf16[16,90,256]{2,1,0:T(8,128)(2,1)S(1)} %join.1), channel_id=1, replica_groups=mesh['y'=4,'c'=2,'z'=4,'x'=4] {'z','x'}, dimensions={0} | all-to-all | bytes 1474560 | tf_op jit(solution)/shard_map/all_to_all | solution.py:654
  109.8 2.4 %collective-permute-done.26.d_ref = bf16[90,256]{1,0:T(8,128)(2,1)S(1)} collective-permute-done((bf16[90,256]{1,0:T(8,128)(2,1)S(1)}, bf16[90,256]{1,0:T(8,128)(2,1)S(1)}, u32[]{:S(2)}, u32[]{:S(2)}) %collective-permute-start.26) | collective-permute-done | bytes 46112 | tf_op jit(solution)/shard_map/ppermute | solution.py:19
  113.1 2.7 %collective-permute-start.29 = (bf16[360,256]{1,0:T(8,128)(2,1)S(1)}, bf16[360,256]{1,0:T(8,128)(2,1)S(1)}, u32[]{:S(2)}, u32[]{:S(2)}) collective-permute-start(bf16[360,256]{1,0:T(8,128)(2,1)S(1)} %order_pieces.1.a_ref), channel_id=1, source_target_pairs={{0,2},{1,3},{2,0},{3,1},{4,6},{5,7},{6,4},{7,5},{8,10},{9,11},{10,... | collective-permute-start | bytes 552968 | tf_op jit(solution)/shard_map/ppermute | solution.py:19
  117.3 2.2 %features.1 = bf16[32,32,256]{2,1,0:T(8,128)(2,1)} custom-call(bf16[40,32,768]{2,1,0:T(8,128)(2,1)S(1)} %get-tuple-element.60.wide_ref, bf16[2304,256]{1,0:T(8,128)(2,1)S(1)} %bitcast.47), custom_call_target="tpu_custom_call" | custom-call | flops 1 | bytes 1 | tf_op jit(solution)/shard_map/features/pallas_call | solution.py:314
  122.0 1.5 %collective-permute-start.30 = (bf16[4,72,256]{2,1,0:T(8,128)(2,1)S(1)}, bf16[4,72,256]{2,1,0:T(8,128)(2,1)S(1)}, u32[]{:S(2)}, u32[]{:S(2)}) collective-permute-start(bf16[4,72,256]{2,1,0:T(8,128)(2,1)S(1)} %pick_rows.1), channel_id=1, source_target_pairs={{0,32},{32,64},{64,96},{96,0},{1,33},{33,65},{65,97},{97,1},{2,34}... | collective-permute-start | bytes 442376 | tf_op jit(solution)/shard_map/ppermute | solution.py:19
  124.6 2.6 %collective-permute-done.32 = bf16[4,72,256]{2,1,0:T(8,128)(2,1)S(1)} collective-permute-done((bf16[4,72,256]{2,1,0:T(8,128)(2,1)S(1)}, bf16[4,72,256]{2,1,0:T(8,128)(2,1)S(1)}, u32[]{:S(2)}, u32[]{:S(2)}) %collective-permute-start.32) | collective-permute-done | bytes 147488 | tf_op jit(solution)/shard_map/ppermute | solution.py:19
  127.2 1.5 %collective-permute-done.30 = bf16[4,72,256]{2,1,0:T(8,128)(2,1)S(1)} collective-permute-done((bf16[4,72,256]{2,1,0:T(8,128)(2,1)S(1)}, bf16[4,72,256]{2,1,0:T(8,128)(2,1)S(1)}, u32[]{:S(2)}, u32[]{:S(2)}) %collective-permute-start.30) | collective-permute-done | bytes 147488 | tf_op jit(solution)/shard_map/ppermute | solution.py:19
  128.8 6.5 %collective-permute-start.33 = (bf16[4,4,72,256]{3,2,1,0:T(8,128)(2,1)S(1)}, bf16[4,4,72,256]{3,2,1,0:T(8,128)(2,1)S(1)}, u32[]{:S(2)}, u32[]{:S(2)}) collective-permute-start(bf16[4,4,72,256]{3,2,1,0:T(8,128)(2,1)S(1)} %pad_maximum_fusion.1.in_ref), channel_id=1, source_target_pairs={{0,16},{16,0},{1,17},{17,1},{2,18},{18,2},{3,19},{19,3},{4,20},{20... | collective-permute-start | bytes 1769480 | tf_op jit(solution)/shard_map/ppermute | solution.py:19
  (82 shorter events, 29.2 us)
Async XLA Ops:
  0.6 13.7 %collective-permute-start = (bf16[256,32,128]{2,1,0:T(8,128)(2,1)}, bf16[256,32,128]{2,1,0:T(8,128)(2,1)S(1)}, u32[]{:S(2)}, u32[]{:S(2)}) collective-permute-start(bf16[256,32,128]{2,1,0:T(8,128)(2,1)} %own_ref.1), channel_id=1, source_target_pairs={{0,16},{16,0},{1,17},{17,1},{2,18},{18,2},{3,19},{19,3},{4,20},{20... | collective-permute-start | bytes 6291464 | tf_op jit(solution)/shard_map/ppermute | solution.py:19
  4.6 6.6 %collective-permute-start.2 = (bf16[320,128]{1,0:T(8,128)(2,1)S(1)}, bf16[320,128]{1,0:T(8,128)(2,1)S(1)}, u32[]{:S(2)}, u32[]{:S(2)}) collective-permute-start(bf16[320,128]{1,0:T(8,128)(2,1)S(1)} %pad_maximum_fusion.4), channel_id=1, source_target_pairs={{1,0},{2,1},{3,2},{4,3},{5,4},{6,5},{7,6},{8,7},{9,8},{10,9},{11,1... | collective-permute-start | bytes 245768 | tf_op jit(solution)/shard_map/ppermute | solution.py:398
  5.9 7.3 %collective-permute-start.4 = (bf16[3,3,128,256]{3,2,1,0:T(8,128)(2,1)}, bf16[3,3,128,256]{3,2,1,0:T(8,128)(2,1)S(1)}, u32[]{:S(2)}, u32[]{:S(2)}) collective-permute-start(bf16[3,3,128,256]{3,2,1,0:T(8,128)(2,1)} %param.5), channel_id=1, source_target_pairs={{0,16},{16,0},{1,17},{17,1},{2,18},{18,2},{3,19},{19,3},{4,20},{20... | collective-permute-start | bytes 1769480 | tf_op jit(solution)/shard_map/ppermute | solution.py:19
  6.2 6.1 %collective-permute-start.1 = (bf16[320,128]{1,0:T(8,128)(2,1)S(1)}, bf16[320,128]{1,0:T(8,128)(2,1)S(1)}, u32[]{:S(2)}, u32[]{:S(2)}) collective-permute-start(bf16[320,128]{1,0:T(8,128)(2,1)S(1)} %pad_maximum_fusion.3), channel_id=1, source_target_pairs={{0,1},{1,2},{2,3},{3,4},{4,5},{5,6},{6,7},{7,8},{8,9},{9,10},{10,1... | collective-permute-start | bytes 245768 | tf_op jit(solution)/shard_map/ppermute | solution.py:398
  17.8 11.9 %collective-permute-start.8 = (bf16[17,32,256]{2,1,0:T(8,128)(2,1)S(1)}, bf16[17,32,256]{2,1,0:T(8,128)(2,1)S(1)}, u32[]{:S(2)}, u32[]{:S(2)}) collective-permute-start(bf16[17,32,256]{2,1,0:T(8,128)(2,1)S(1)} %get-tuple-element.36), channel_id=1, source_target_pairs={{0,96},{32,0},{64,32},{96,64},{1,97},{33,1},{65,33},{97,65},{2,98}... | collective-permute-start | bytes 835592 | tf_op jit(solution)/shard_map/ppermute | solution.py:19
  20.7 9.0 %collective-permute-start.5 = (bf16[17,32,256]{2,1,0:T(8,128)(2,1)S(1)}, bf16[17,32,256]{2,1,0:T(8,128)(2,1)S(1)}, u32[]{:S(2)}, u32[]{:S(2)}) collective-permute-start(bf16[17,32,256]{2,1,0:T(8,128)(2,1)S(1)} %get-tuple-element.34), channel_id=1, source_target_pairs={{0,32},{32,64},{64,96},{96,0},{1,33},{33,65},{65,97},{97,1},{2,34}... | collective-permute-start | bytes 835592 | tf_op jit(solution)/shard_map/ppermute | solution.py:19
  20.7 8.8 %collective-permute-start.6 = (bf16[34,256]{1,0:T(8,128)(2,1)S(1)}, bf16[34,256]{1,0:T(8,128)(2,1)S(1)}, u32[]{:S(2)}, u32[]{:S(2)}) collective-permute-start(bf16[34,256]{1,0:T(8,128)(2,1)S(1)} %maximum_maximum_fusion), channel_id=1, source_target_pairs={{0,16},{16,32},{32,48},{48,64},{64,80},{80,96},{96,112},{1,17},{17... | collective-permute-start | bytes 52232 | tf_op jit(solution)/shard_map/ppermute | solution.py:620
  23.3 6.2 %collective-permute-start.7 = (bf16[34,256]{1,0:T(8,128)(2,1)S(1)}, bf16[34,256]{1,0:T(8,128)(2,1)S(1)}, u32[]{:S(2)}, u32[]{:S(2)}) collective-permute-start(bf16[34,256]{1,0:T(8,128)(2,1)S(1)} %maximum_maximum_fusion.1), channel_id=1, source_target_pairs={{16,0},{32,16},{48,32},{64,48},{80,64},{96,80},{112,96},{17,1},{33... | collective-permute-start | bytes 52232 | tf_op jit(solution)/shard_map/ppermute | solution.py:621
  26.7 10.1 %collective-permute-start.10 = (bf16[17,32,256]{2,1,0:T(8,128)(2,1)S(1)}, bf16[17,32,256]{2,1,0:T(8,128)(2,1)S(1)}, u32[]{:S(2)}, u32[]{:S(2)}) collective-permute-start(bf16[17,32,256]{2,1,0:T(8,128)(2,1)S(1)} %get-tuple-element.39), channel_id=1, source_target_pairs={{0,96},{32,0},{64,32},{96,64},{1,97},{33,1},{65,33},{97,65},{2,98}... | collective-permute-start | bytes 835592 | tf_op jit(solution)/shard_map/ppermute | solution.py:19
  29.5 7.3 %collective-permute-start.11 = (bf16[17,32,256]{2,1,0:T(8,128)(2,1)S(1)}, bf16[17,32,256]{2,1,0:T(8,128)(2,1)S(1)}, u32[]{:S(2)}, u32[]{:S(2)}) collective-permute-start(bf16[17,32,256]{2,1,0:T(8,128)(2,1)S(1)} %get-tuple-element.40), channel_id=1, source_target_pairs={{0,32},{32,64},{64,96},{96,0},{1,33},{33,65},{65,97},{97,1},{2,34}... | collective-permute-start | bytes 835592 | tf_op jit(solution)/shard_map/ppermute | solution.py:19
  31.1 11.7 %collective-permute-start.9 = (bf16[17,32,256]{2,1,0:T(8,128)(2,1)S(1)}, bf16[17,32,256]{2,1,0:T(8,128)(2,1)S(1)}, u32[]{:S(2)}, u32[]{:S(2)}) collective-permute-start(bf16[17,32,256]{2,1,0:T(8,128)(2,1)S(1)} %get-tuple-element.37), channel_id=1, source_target_pairs={{0,32},{32,64},{64,96},{96,0},{1,33},{33,65},{65,97},{97,1},{2,34}... | collective-permute-start | bytes 835592 | tf_op jit(solution)/shard_map/ppermute | solution.py:19
  31.9 10.9 %collective-permute-start.12 = (bf16[17,32,256]{2,1,0:T(8,128)(2,1)S(1)}, bf16[17,32,256]{2,1,0:T(8,128)(2,1)S(1)}, u32[]{:S(2)}, u32[]{:S(2)}) collective-permute-start(bf16[17,32,256]{2,1,0:T(8,128)(2,1)S(1)} %get-tuple-element.41), channel_id=1, source_target_pairs={{0,96},{32,0},{64,32},{96,64},{1,97},{33,1},{65,33},{97,65},{2,98}... | collective-permute-start | bytes 835592 | tf_op jit(solution)/shard_map/ppermute | solution.py:19
  43.3 17.4 %collective-permute-start.15 = (bf16[32,32,256]{2,1,0:T(8,128)(2,1)S(1)}, bf16[32,32,256]{2,1,0:T(8,128)(2,1)S(1)}, u32[]{:S(2)}, u32[]{:S(2)}) collective-permute-start(bf16[32,32,256]{2,1,0:T(8,128)(2,1)S(1)} %get-tuple-element.44.refs_0_), channel_id=1, source_target_pairs={{0,96},{32,0},{64,32},{96,64},{1,97},{33,1},{65,33},{97,65},{2,98}... | collective-permute-start | bytes 1572872 | tf_op jit(solution)/shard_map/ppermute | solution.py:19
  45.2 17.1 %collective-permute-start.13 = (bf16[32,32,256]{2,1,0:T(8,128)(2,1)S(1)}, bf16[32,32,256]{2,1,0:T(8,128)(2,1)S(1)}, u32[]{:S(2)}, u32[]{:S(2)}) collective-permute-start(bf16[32,32,256]{2,1,0:T(8,128)(2,1)S(1)} %get-tuple-element.44.refs_0_), channel_id=1, source_target_pairs={{0,32},{32,64},{64,96},{96,0},{1,33},{33,65},{65,97},{97,1},{2,34}... | collective-permute-start | bytes 1572872 | tf_op jit(solution)/shard_map/ppermute | solution.py:19
  45.2 5.6 %collective-permute-start.17 = (bf16[34,256]{1,0:T(8,128)(2,1)S(1)}, bf16[34,256]{1,0:T(8,128)(2,1)S(1)}, u32[]{:S(2)}, u32[]{:S(2)}) collective-permute-start(bf16[34,256]{1,0:T(8,128)(2,1)S(1)} %get-tuple-element.48), channel_id=1, source_target_pairs={{0,1},{1,2},{2,3},{3,4},{4,5},{5,6},{6,7},{7,8},{8,9},{9,10},{10,1... | collective-permute-start | bytes 52232 | tf_op jit(solution)/shard_map/ppermute | solution.py:398
  49.3 4.8 %collective-permute-start.18 = (bf16[34,256]{1,0:T(8,128)(2,1)S(1)}, bf16[34,256]{1,0:T(8,128)(2,1)S(1)}, u32[]{:S(2)}, u32[]{:S(2)}) collective-permute-start(bf16[34,256]{1,0:T(8,128)(2,1)S(1)} %get-tuple-element.49), channel_id=1, source_target_pairs={{1,0},{2,1},{3,2},{4,3},{5,4},{6,5},{7,6},{8,7},{9,8},{10,9},{11,1... | collective-permute-start | bytes 52232 | tf_op jit(solution)/shard_map/ppermute | solution.py:398
  56.4 6.1 %collective-permute-start.19 = (bf16[4,288,256]{2,1,0:T(8,128)(2,1)S(1)}, bf16[4,288,256]{2,1,0:T(8,128)(2,1)S(1)}, u32[]{:S(2)}, u32[]{:S(2)}) collective-permute-start(bf16[4,288,256]{2,1,0:T(8,128)(2,1)S(1)} %get-tuple-element.51), channel_id=1, source_target_pairs={{0,16},{16,0},{1,17},{17,1},{2,18},{18,2},{3,19},{19,3},{4,20},{20... | collective-permute-start | bytes 1769480 | tf_op jit(solution)/shard_map/ppermute | solution.py:19
  60.8 10.9 %collective-permute-start.16 = (bf16[16,32,256]{2,1,0:T(8,128)(2,1)S(1)}, bf16[16,32,256]{2,1,0:T(8,128)(2,1)S(1)}, u32[]{:S(2)}, u32[]{:S(2)}) collective-permute-start(bf16[16,32,256]{2,1,0:T(8,128)(2,1)S(1)} %slice.81), channel_id=1, source_target_pairs={{0,96},{32,0},{64,32},{96,64},{1,97},{33,1},{65,33},{97,65},{2,98}... | collective-permute-start | bytes 786440 | tf_op jit(solution)/shard_map/ppermute | solution.py:19
  62.3 9.4 %collective-permute-start.14 = (bf16[16,32,256]{2,1,0:T(8,128)(2,1)S(1)}, bf16[16,32,256]{2,1,0:T(8,128)(2,1)S(1)}, u32[]{:S(2)}, u32[]{:S(2)}) collective-permute-start(bf16[16,32,256]{2,1,0:T(8,128)(2,1)S(1)} %slice.80), channel_id=1, source_target_pairs={{0,32},{32,64},{64,96},{96,0},{1,33},{33,65},{65,97},{97,1},{2,34}... | collective-permute-start | bytes 786440 | tf_op jit(solution)/shard_map/ppermute | solution.py:19
  62.6 14.9 %collective-permute-start.20 = (bf16[288,256]{1,0:T(8,128)(2,1)S(1)}, bf16[288,256]{1,0:T(8,128)(2,1)S(1)}, u32[]{:S(2)}, u32[]{:S(2)}) collective-permute-start(bf16[288,256]{1,0:T(8,128)(2,1)S(1)} %get-tuple-element.52), channel_id=1, source_target_pairs={{0,32},{32,64},{64,96},{96,0},{1,33},{33,65},{65,97},{97,1},{2,34}... | collective-permute-start | bytes 442376 | tf_op jit(solution)/shard_map/ppermute | solution.py:19
  62.7 14.8 %collective-permute-start.21 = (bf16[288,256]{1,0:T(8,128)(2,1)S(1)}, bf16[288,256]{1,0:T(8,128)(2,1)S(1)}, u32[]{:S(2)}, u32[]{:S(2)}) collective-permute-start(bf16[288,256]{1,0:T(8,128)(2,1)S(1)} %get-tuple-element.53), channel_id=1, source_target_pairs={{0,96},{32,0},{64,32},{96,64},{1,97},{33,1},{65,33},{97,65},{2,98}... | collective-permute-start | bytes 442376 | tf_op jit(solution)/shard_map/ppermute | solution.py:19
  65.3 12.1 %collective-permute-start.22 = (bf16[288,256]{1,0:T(8,128)(2,1)S(1)}, bf16[288,256]{1,0:T(8,128)(2,1)S(1)}, u32[]{:S(2)}, u32[]{:S(2)}) collective-permute-start(bf16[288,256]{1,0:T(8,128)(2,1)S(1)} %get-tuple-element.54), channel_id=1, source_target_pairs={{0,64},{32,96},{64,0},{96,32},{1,65},{33,97},{65,1},{97,33},{2,66}... | collective-permute-start | bytes 442376 | tf_op jit(solution)/shard_map/ppermute | solution.py:19
  107.6 4.5 %collective-permute-start.26 = (bf16[90,256]{1,0:T(8,128)(2,1)S(1)}, bf16[90,256]{1,0:T(8,128)(2,1)S(1)}, u32[]{:S(2)}, u32[]{:S(2)}) collective-permute-start(bf16[90,256]{1,0:T(8,128)(2,1)S(1)} %sum_pieces.1.a_ref), channel_id=1, source_target_pairs={{0,8},{4,12},{8,0},{12,4},{1,9},{5,13},{9,1},{13,5},{2,10},{6,14},... | collective-permute-start | bytes 138248 | tf_op jit(solution)/shard_map/ppermute | solution.py:19
  108.3 3.9 %collective-permute-start.25 = (bf16[90,256]{1,0:T(8,128)(2,1)S(1)}, bf16[90,256]{1,0:T(8,128)(2,1)S(1)}, u32[]{:S(2)}, u32[]{:S(2)}) collective-permute-start(bf16[90,256]{1,0:T(8,128)(2,1)S(1)} %sum_pieces.1.a_ref), channel_id=1, source_target_pairs={{0,12},{4,0},{8,4},{12,8},{1,13},{5,1},{9,5},{13,9},{2,14},{6,2},{... | collective-permute-start | bytes 138248 | tf_op jit(solution)/shard_map/ppermute | solution.py:19
  108.9 4.2 %collective-permute-start.24 = (bf16[90,256]{1,0:T(8,128)(2,1)S(1)}, bf16[90,256]{1,0:T(8,128)(2,1)S(1)}, u32[]{:S(2)}, u32[]{:S(2)}) collective-permute-start(bf16[90,256]{1,0:T(8,128)(2,1)S(1)} %sum_pieces.1.a_ref), channel_id=1, source_target_pairs={{0,4},{4,8},{8,12},{12,0},{1,5},{5,9},{9,13},{13,1},{2,6},{6,10},{... | collective-permute-start | bytes 138248 | tf_op jit(solution)/shard_map/ppermute | solution.py:19
  113.1 6.4 %collective-permute-start.29 = (bf16[360,256]{1,0:T(8,128)(2,1)S(1)}, bf16[360,256]{1,0:T(8,128)(2,1)S(1)}, u32[]{:S(2)}, u32[]{:S(2)}) collective-permute-start(bf16[360,256]{1,0:T(8,128)(2,1)S(1)} %order_pieces.1.a_ref), channel_id=1, source_target_pairs={{0,2},{1,3},{2,0},{3,1},{4,6},{5,7},{6,4},{7,5},{8,10},{9,11},{10,... | collective-permute-start | bytes 552968 | tf_op jit(solution)/shard_map/ppermute | solution.py:19
  115.8 5.1 %collective-permute-start.28 = (bf16[360,256]{1,0:T(8,128)(2,1)S(1)}, bf16[360,256]{1,0:T(8,128)(2,1)S(1)}, u32[]{:S(2)}, u32[]{:S(2)}) collective-permute-start(bf16[360,256]{1,0:T(8,128)(2,1)S(1)} %order_pieces.1.a_ref), channel_id=1, source_target_pairs={{0,3},{1,0},{2,1},{3,2},{4,7},{5,4},{6,5},{7,6},{8,11},{9,8},{10,9... | collective-permute-start | bytes 552968 | tf_op jit(solution)/shard_map/ppermute | solution.py:19
  115.9 5.6 %collective-permute-start.27 = (bf16[360,256]{1,0:T(8,128)(2,1)S(1)}, bf16[360,256]{1,0:T(8,128)(2,1)S(1)}, u32[]{:S(2)}, u32[]{:S(2)}) collective-permute-start(bf16[360,256]{1,0:T(8,128)(2,1)S(1)} %order_pieces.1.a_ref), channel_id=1, source_target_pairs={{0,1},{1,2},{2,3},{3,0},{4,5},{5,6},{6,7},{7,4},{8,9},{9,10},{10,1... | collective-permute-start | bytes 552968 | tf_op jit(solution)/shard_map/ppermute | solution.py:19
  121.5 5.7 %collective-permute-start.32 = (bf16[4,72,256]{2,1,0:T(8,128)(2,1)S(1)}, bf16[4,72,256]{2,1,0:T(8,128)(2,1)S(1)}, u32[]{:S(2)}, u32[]{:S(2)}) collective-permute-start(bf16[4,72,256]{2,1,0:T(8,128)(2,1)S(1)} %pick_rows.1), channel_id=1, source_target_pairs={{0,64},{32,96},{64,0},{96,32},{1,65},{33,97},{65,1},{97,33},{2,66}... | collective-permute-start | bytes 442376 | tf_op jit(solution)/shard_map/ppermute | solution.py:19
  122.0 5.2 %collective-permute-start.31 = (bf16[4,72,256]{2,1,0:T(8,128)(2,1)S(1)}, bf16[4,72,256]{2,1,0:T(8,128)(2,1)S(1)}, u32[]{:S(2)}, u32[]{:S(2)}) collective-permute-start(bf16[4,72,256]{2,1,0:T(8,128)(2,1)S(1)} %pick_rows.1), channel_id=1, source_target_pairs={{0,96},{32,0},{64,32},{96,64},{1,97},{33,1},{65,33},{97,65},{2,98}... | collective-permute-start | bytes 442376 | tf_op jit(solution)/shard_map/ppermute | solution.py:19
  122.0 6.7 %collective-permute-start.30 = (bf16[4,72,256]{2,1,0:T(8,128)(2,1)S(1)}, bf16[4,72,256]{2,1,0:T(8,128)(2,1)S(1)}, u32[]{:S(2)}, u32[]{:S(2)}) collective-permute-start(bf16[4,72,256]{2,1,0:T(8,128)(2,1)S(1)} %pick_rows.1), channel_id=1, source_target_pairs={{0,32},{32,64},{64,96},{96,0},{1,33},{33,65},{65,97},{97,1},{2,34}... | collective-permute-start | bytes 442376 | tf_op jit(solution)/shard_map/ppermute | solution.py:19
  128.8 8.2 %collective-permute-start.33 = (bf16[4,4,72,256]{3,2,1,0:T(8,128)(2,1)S(1)}, bf16[4,4,72,256]{3,2,1,0:T(8,128)(2,1)S(1)}, u32[]{:S(2)}, u32[]{:S(2)}) collective-permute-start(bf16[4,4,72,256]{3,2,1,0:T(8,128)(2,1)S(1)} %pad_maximum_fusion.1.in_ref), channel_id=1, source_target_pairs={{0,16},{16,0},{1,17},{17,1},{2,18},{18,2},{3,19},{19,3},{4,20},{20... | collective-permute-start | bytes 1769480 | tf_op jit(solution)/shard_map/ppermute | solution.py:19
  (5 other events, 25.5 us)

commit v11 on v10

--- a/solution.py
+++ b/solution.py
@@ -231,42 +231,30 @@
     cols, rows, chans = tile.shape
     return pl.pallas_call(
         back_kernel,
-        out_shape=jax.ShapeDtypeStruct((cols, rows, kernel.shape[2]), F32),
+        out_shape=(
+            jax.ShapeDtypeStruct((cols, rows, kernel.shape[2]), F32),
+            jax.ShapeDtypeStruct((cols + 2, rows, 3 * chans), BF16),
+        ),
         in_specs=[VMEM_SPEC] * 5,
-        out_specs=VMEM_SPEC,
-        scratch_shapes=[pltpu.VMEM((cols + 2, rows, 3 * chans), BF16)],
+        out_specs=(VMEM_SPEC,) * 2,
         compiler_params=pltpu.CompilerParams(vmem_limit_bytes=4 * 2**20),
         cost_estimate=QUICK,
         name="back",
     )(tile, left, right, edges, kernel)
 
 
-def second_kernel(
-    chips, hid_ref, before_ref, after_ref, cot_ref, wide_ref, near_ref, far_ref, pad_ref, sum_ref
-):
+def second_kernel(chips, hid_ref, wide_ref, near_ref, far_ref, sum_ref):
     chans = hid_ref.shape[2]
-    cols, rows, outs = cot_ref.shape
-    width = wide_ref.shape[0]
+    cols, rows, outs = hid_ref.shape[0] - 2, hid_ref.shape[1], wide_ref.shape[2] // 3
     core = lax.axis_index("c")
-    columns = [
-        (hid_ref[j], before_ref[j : j + 1, :], after_ref[j : j + 1, :]) for j in range(cols + 2)
-    ]
-    spread_tile(columns, wide_ref)
-    wide_ref[cols + 2 :] = jnp.zeros((width - cols - 2, rows, 3 * chans), BF16)
-
-    pad_ref[0:2] = jnp.zeros((2, rows, outs), BF16)
-    pad_ref[2 : 2 + cols] = cot_ref[...]
-    pad_ref[2 + cols :] = jnp.zeros((width - cols, rows, outs), BF16)
-    rhs = jnp.concatenate(
-        [pad_ref[2 - tap : 2 - tap + width].reshape(width * rows, outs) for tap in range(3)],
-        axis=-1,
-    )
-    sum_ref[...] = lax.dot_general(
-        wide_ref[...].reshape(width * rows, 3 * chans),
-        rhs,
-        (((0,), (0,)), ((), ())),
-        preferred_element_type=F32,
-    )
+    lhs = hid_ref[1 : cols + 1].reshape(cols * rows, chans)
+    for tap_col in range(3):
+        rhs = wide_ref[2 - tap_col : 2 - tap_col + cols].reshape(cols * rows, 3 * outs)
+        part = lax.dot_general(lhs, rhs, (((0,), (0,)), ((), ())), preferred_element_type=F32)
+        for tap_row in range(3):
+            sum_ref[
+                tap_row * chans : (tap_row + 1) * chans, tap_col * outs : (tap_col + 1) * outs
+            ] = part[:, (2 - tap_row) * outs : (3 - tap_row) * outs]
     size = sum_ref.shape[0] // (2 * chips)
     for half, ref in ((core, near_ref), (1 - core, far_ref)):
         for chip in range(chips):
@@ -277,49 +265,46 @@
                 ].astype(ref.dtype)
 
 
-def second_tile(tile, edges, cotangent, chips):
-    chans = tile.shape[2]
-    cols, rows, outs = cotangent.shape
-    width = cols + 8
+def second_tile(tile, wide, chips):
+    chans, outs = tile.shape[2], wide.shape[2] // 3
     cut = (chips, 9 * chans // (2 * chips), outs)
     return pl.pallas_call(
         functools.partial(second_kernel, chips),
-        out_shape=(
-            jax.ShapeDtypeStruct((width, rows, 3 * chans), BF16),
-            jax.ShapeDtypeStruct(cut, F32),
-            jax.ShapeDtypeStruct(cut, BF16),
-        ),
-        in_specs=[VMEM_SPEC] * 4,
-        out_specs=(VMEM_SPEC,) * 3,
-        scratch_shapes=[
-            pltpu.VMEM((width + 2, rows, outs), BF16),
-            pltpu.VMEM((3 * chans, 3 * outs), F32),
-        ],
+        out_shape=(jax.ShapeDtypeStruct(cut, F32), jax.ShapeDtypeStruct(cut, BF16)),
+        in_specs=[VMEM_SPEC] * 2,
+        out_specs=(VMEM_SPEC,) * 2,
+        scratch_shapes=[pltpu.VMEM((3 * chans, 3 * outs), F32)],
         compiler_params=pltpu.CompilerParams(vmem_limit_bytes=9 * 2**20),
         cost_estimate=QUICK,
         name="second",
-    )(tile, *edges, cotangent)
-
-
-def features_kernel(wide_ref, kernel_ref, out_ref):
+    )(tile, wide)
+
+
+def features_kernel(hid_ref, before_ref, after_ref, kernel_ref, out_ref, wide_ref):
     cols, rows, outs = out_ref.shape
+    columns = [
+        (hid_ref[j], before_ref[j : j + 1, :], after_ref[j : j + 1, :]) for j in range(cols + 2)
+    ]
+    spread_tile(columns, wide_ref)
     pieces = [wide_ref[tap : tap + cols] for tap in range(3)]
     lhs = jnp.concatenate(pieces, axis=-1).reshape(cols * rows, -1)
     total = jnp.dot(lhs, kernel_ref[...], preferred_element_type=F32)
     out_ref[...] = total.reshape(cols, rows, outs).astype(BF16)
 
 
-def features_tile(wide, kernel, cols):
-    rows, outs = wide.shape[1], kernel.shape[3]
+def features_tile(tile, edges, kernel):
+    cols, rows, chans = tile.shape
+    outs = kernel.shape[3]
     return pl.pallas_call(
         features_kernel,
-        out_shape=jax.ShapeDtypeStruct((cols, rows, outs), BF16),
-        in_specs=[VMEM_SPEC] * 2,
+        out_shape=jax.ShapeDtypeStruct((cols - 2, rows, outs), BF16),
+        in_specs=[VMEM_SPEC] * 4,
         out_specs=VMEM_SPEC,
-        compiler_params=pltpu.CompilerParams(vmem_limit_bytes=4 * 2**20),
+        scratch_shapes=[pltpu.VMEM((cols, rows, 3 * chans), BF16)],
+        compiler_params=pltpu.CompilerParams(vmem_limit_bytes=9 * 2**20),
         cost_estimate=QUICK,
         name="features",
-    )(wide, kernel.reshape(-1, outs))
+    )(tile, *edges, kernel.reshape(-1, outs))
 
 
 def point_kernel(
@@ -632,19 +617,23 @@
     from_a = shift(both_a, "y", on), shift(near_a, "y", off)
     from_b = shift(near_b, "y", on), shift(both_b, "y", off)
 
-    back = back_tile(cotangent, left, right, edges, weight_second)
+    back, wide_cotangent = back_tile(cotangent, left, right, edges, weight_second)
     delta, hidden, *ends = point(own, from_a, from_b, back)
 
     from_on, from_off = shift(delta, "y", on), shift(delta, "y", off)
     half = strip // 2
+    total = grad_strip(0, wide, (delta,), None, False)
+    from_on, from_off, total, *edges = lax.optimization_barrier(
+        (from_on, from_off, total, *row_halo(ends))
+    )
     fwd_a, fwd_b = shift(from_on[:half], "y", on), shift(from_off[half:], "y", off)
-    edges = row_halo(ends)
-    total = grad_strip(0, wide, (delta,), None, False)
-    wide_hidden, near, far = second_tile(hidden, edges, cotangent, chips)
+    near, far = second_tile(hidden, wide_cotangent, chips)
+    features = features_tile(hidden, edges, weight_second)
     keep, *sends = fold(near, shift(far, "c", 1))
     got = [shift(send, "y", step) for step, send in zip(STEPS[1:], sends)]
     total = grad_strip(off, wide, (from_on,), total, False)
     total = grad_strip(on, wide, (from_off,), total, False)
+    fwd_a, features = lax.optimization_barrier((fwd_a, features))
     first_own, first_far = grad_strip(2, wide, (fwd_a, fwd_b), total, True)
 
     sx, sz = lax.axis_size("x"), lax.axis_size("z")
@@ -656,9 +645,7 @@
     parts = gather_steps(order_pieces(gather_steps(summed, "z"), extra), "x")
     main = parts[0].shape[0] - sz * extra
     grad_first = lay_first(parts, sz, chans)
-    features = features_tile(wide_hidden, weight_second, strip)
     share = pick_rows(parts, main)
-    share, features = lax.optimization_barrier((share, features))
     share, grad_first = lax.optimization_barrier(
         (jnp.stack(gather_steps(share, "y")), grad_first)
     )

time: 139 us -> 137 us (0.986)
  waiting for transfers between devices: 26 us -> 29.8 us
  blocking collectives: 27.1 us -> 23.8 us
  starting transfers between devices: 54.3 us -> 52.1 us
    all_to_all x1, blocking collectives: 27.1 us -> 23.8 us  [body(): summed = lax.all_to_all(joined, SKY, 0, 0, tiled=True)]
    ppermute x28, waiting for transfers between devices: 21.7 us -> 24.4 us  [shift(): lax.ppermute(x, axis, [(i, (i + step) % count) for i in range(count)])]
    ppermute x4, starting transfers between devices: 11.1 us -> 9.08 us  [row_halo(): return (lax.ppermute(ends[0], SKY, up), lax.ppermute(ends[1], SKY, down))]
  transfers between devices with their start and end apart: 34 -> 34, of which waited for: 14 -> 15; matrix products, arithmetic and copies ran while one was open for 3% -> 3% of each run, Pallas kernels for 14% -> 14%
where the time goes in v11:
time: 137 us; the launch traced here: 136 us
  starting transfers between devices  52.1 us (38%)
  waiting for transfers between devices  29.8 us (22%)
  Pallas kernels  24.8 us (18%)
  blocking collectives  23.8 us (17%)
  local copies, waits for them, and re-layouts  3.25 us (2%)
    ppermute x28, starting transfers between devices, shift(): lax.ppermute(x, axis, [(i, (i + step) % count) for i in range(count)])  38.6 us
    ppermute x28, waiting for transfers between devices, shift(): lax.ppermute(x, axis, [(i, (i + step) % count) for i in range(count)])  24.4 us
    all_to_all x1, blocking collectives, body(): summed = lax.all_to_all(joined, SKY, 0, 0, tiled=True)  23.8 us
    ppermute x4, starting transfers between devices, row_halo(): return (lax.ppermute(ends[0], SKY, up), lax.ppermute(ends[1], SKY, down))  9.08 us
    pallas_call x4, Pallas kernels, grad_strip(): pl.pallas_call(functools.partial(grad_kernel, step, len(pieces), old is n...  7.01 us
    pallas_call x4, Pallas kernels, conv_parts(): pl.pallas_call(functools.partial(conv_kernel, parts, len(adds)), out_shap...  5.84 us
    ppermute x4, waiting for transfers between devices, row_halo(): return (lax.ppermute(ends[0], SKY, up), lax.ppermute(ends[1], SKY, down))  5.34 us
  transfers between devices with their start and end apart: 34, of which 15 were waited for; matrix products, arithmetic and copies ran while one was open for 3% of the time, Pallas kernels for 14%

profile of v11, /device:TPU:1, one launch (start us, length us, event | category | flops | bytes accessed | tf_op | source)
XLA Modules:
  0.0 136.2 jit_solution(502207083256995737)
XLA Ops:
  4.6 3.2 %collective-permute-start.1 = (bf16[320,128]{1,0:T(8,128)(2,1)S(1)}, bf16[320,128]{1,0:T(8,128)(2,1)S(1)}, u32[]{:S(2)}, u32[]{:S(2)}) collective-permute-start(bf16[320,128]{1,0:T(8,128)(2,1)S(1)} %pad_maximum_fusion.3), channel_id=1, source_target_pairs={{0,1},{1,2},{2,3},{3,4},{4,5},{5,6},{6,7},{7,8},{8,9},{9,10},{10,1... | collective-permute-start | bytes 245768 | tf_op jit(solution)/shard_map/ppermute | solution.py:383
  10.4 3.8 %collective-permute-done.2 = bf16[320,128]{1,0:T(8,128)(2,1)S(1)} collective-permute-done((bf16[320,128]{1,0:T(8,128)(2,1)S(1)}, bf16[320,128]{1,0:T(8,128)(2,1)S(1)}, u32[]{:S(2)}, u32[]{:S(2)}) %collective-permute-start.2) | collective-permute-done | bytes 81952 | tf_op jit(solution)/shard_map/ppermute | solution.py:383
  16.4 1.9 %spread.1.wide_ref = bf16[4,40,32,768]{3,2,1,0:T(8,128)(2,1)S(1)} custom-call(bf16[256,32,128]{2,1,0:T(8,128)(2,1)S(1)} %copy-done.1, bf16[256,32,128]{2,1,0:T(8,128)(2,1)S(1)} %collective-permute-done.far_ref, bf16[2,320,128]{2,1,0:T(8,128)(2,1)S(1)} %pad_maximum_fusion.2.own_halo_ref.edge_ref, bf16[2,320,128]{2,1,0:T(8,128)(2,1)S(1)} %collective-permute-done.3.far_halo_ref), custom_call_target="tpu_custom_call" | custom-call | flops 1 | bytes 1 | tf_op jit(solution)/shard_map/spread/pallas_call | solution.py:94
  22.7 2.5 %collective-permute-start.6 = (bf16[34,256]{1,0:T(8,128)(2,1)S(1)}, bf16[34,256]{1,0:T(8,128)(2,1)S(1)}, u32[]{:S(2)}, u32[]{:S(2)}) collective-permute-start(bf16[34,256]{1,0:T(8,128)(2,1)S(1)} %maximum_maximum_fusion), channel_id=1, source_target_pairs={{0,16},{16,32},{32,48},{48,64},{64,80},{80,96},{96,112},{1,17},{17... | collective-permute-start | bytes 52232 | tf_op jit(solution)/shard_map/ppermute | solution.py:605
  25.2 1.9 %collective-permute-start.7 = (bf16[34,256]{1,0:T(8,128)(2,1)S(1)}, bf16[34,256]{1,0:T(8,128)(2,1)S(1)}, u32[]{:S(2)}, u32[]{:S(2)}) collective-permute-start(bf16[34,256]{1,0:T(8,128)(2,1)S(1)} %maximum_maximum_fusion.1), channel_id=1, source_target_pairs={{16,0},{32,16},{48,32},{64,48},{80,64},{96,80},{112,96},{17,1},{33... | collective-permute-start | bytes 52232 | tf_op jit(solution)/shard_map/ppermute | solution.py:606
  28.6 1.6 %collective-permute-start.10 = (bf16[17,32,256]{2,1,0:T(8,128)(2,1)S(1)}, bf16[17,32,256]{2,1,0:T(8,128)(2,1)S(1)}, u32[]{:S(2)}, u32[]{:S(2)}) collective-permute-start(bf16[17,32,256]{2,1,0:T(8,128)(2,1)S(1)} %get-tuple-element.45), channel_id=1, source_target_pairs={{0,96},{32,0},{64,32},{96,64},{1,97},{33,1},{65,33},{97,65},{2,98}... | collective-permute-start | bytes 835592 | tf_op jit(solution)/shard_map/ppermute | solution.py:19
  31.8 2.7 %collective-permute-start.12 = (bf16[17,32,256]{2,1,0:T(8,128)(2,1)S(1)}, bf16[17,32,256]{2,1,0:T(8,128)(2,1)S(1)}, u32[]{:S(2)}, u32[]{:S(2)}) collective-permute-start(bf16[17,32,256]{2,1,0:T(8,128)(2,1)S(1)} %get-tuple-element.47), channel_id=1, source_target_pairs={{0,96},{32,0},{64,32},{96,64},{1,97},{33,1},{65,33},{97,65},{2,98}... | collective-permute-start | bytes 835592 | tf_op jit(solution)/shard_map/ppermute | solution.py:19
  37.6 5.2 %collective-permute-done.12.b1_ref = bf16[17,32,256]{2,1,0:T(8,128)(2,1)S(1)} collective-permute-done((bf16[17,32,256]{2,1,0:T(8,128)(2,1)S(1)}, bf16[17,32,256]{2,1,0:T(8,128)(2,1)S(1)}, u32[]{:S(2)}, u32[]{:S(2)}) %collective-permute-start.12) | collective-permute-done | bytes 278560 | tf_op jit(solution)/shard_map/ppermute | solution.py:19
  42.8 1.6 %collective-permute-done.9.a0_ref = bf16[17,32,256]{2,1,0:T(8,128)(2,1)S(1)} collective-permute-done((bf16[17,32,256]{2,1,0:T(8,128)(2,1)S(1)}, bf16[17,32,256]{2,1,0:T(8,128)(2,1)S(1)}, u32[]{:S(2)}, u32[]{:S(2)}) %collective-permute-start.9) | collective-permute-done | bytes 278560 | tf_op jit(solution)/shard_map/ppermute | solution.py:19
  45.0 2.7 %collective-permute-start.14 = (bf16[32,32,256]{2,1,0:T(8,128)(2,1)S(1)}, bf16[32,32,256]{2,1,0:T(8,128)(2,1)S(1)}, u32[]{:S(2)}, u32[]{:S(2)}) collective-permute-start(bf16[32,32,256]{2,1,0:T(8,128)(2,1)S(1)} %get-tuple-element.51.refs_0_), channel_id=1, source_target_pairs={{0,96},{32,0},{64,32},{96,64},{1,97},{33,1},{65,33},{97,65},{2,98}... | collective-permute-start | bytes 1572872 | tf_op jit(solution)/shard_map/ppermute | solution.py:19
  47.7 1.9 %second.1 = (f32[4,288,256]{2,1,0:T(8,128)S(1)}, bf16[4,288,256]{2,1,0:T(8,128)(2,1)S(1)}) custom-call(bf16[34,32,256]{2,1,0:T(8,128)(2,1)S(1)} %get-tuple-element.55.hid_ref, bf16[34,32,768]{2,1,0:T(8,128)(2,1)S(1)} %get-tuple-element.64.wide_ref), custom_call_target="tpu_custom_call" | custom-call | flops 1 | bytes 1 | tf_op jit(solution)/shard_map/second/pallas_call | solution.py:271
  49.6 2.7 %collective-permute-start.19 = (bf16[4,288,256]{2,1,0:T(8,128)(2,1)S(1)}, bf16[4,288,256]{2,1,0:T(8,128)(2,1)S(1)}, u32[]{:S(2)}, u32[]{:S(2)}) collective-permute-start(bf16[4,288,256]{2,1,0:T(8,128)(2,1)S(1)} %get-tuple-element.66), channel_id=1, source_target_pairs={{0,16},{16,0},{1,17},{17,1},{2,18},{18,2},{3,19},{19,3},{4,20},{20... | collective-permute-start | bytes 1769480 | tf_op jit(solution)/shard_map/ppermute | solution.py:19
  52.3 3.3 %collective-permute-start.15 = (bf16[34,256]{1,0:T(8,128)(2,1)S(1)}, bf16[34,256]{1,0:T(8,128)(2,1)S(1)}, u32[]{:S(2)}, u32[]{:S(2)}) collective-permute-start(bf16[34,256]{1,0:T(8,128)(2,1)S(1)} %get-tuple-element.52), channel_id=1, source_target_pairs={{0,1},{1,2},{2,3},{3,4},{4,5},{5,6},{6,7},{7,8},{8,9},{9,10},{10,1... | collective-permute-start | bytes 52232 | tf_op jit(solution)/shard_map/ppermute | solution.py:383
  56.9 1.7 %grad_first.4.refs_1_ = f32[768,768]{1,0:T(8,128)S(1)} custom-call(bf16[4,40,32,768]{3,2,1,0:T(8,128)(2,1)S(1)} %spread.1.wide_ref, bf16[32,32,256]{2,1,0:T(8,128)(2,1)S(1)} %get-tuple-element.51.refs_0_), custom_call_target="tpu_custom_call" | custom-call | flops 1 | bytes 1 | tf_op jit(solution)/shard_map/grad_first/pallas_call | solution.py:176
  60.3 2.7 %collective-permute-start.18 = (bf16[16,32,256]{2,1,0:T(8,128)(2,1)S(1)}, bf16[16,32,256]{2,1,0:T(8,128)(2,1)S(1)}, u32[]{:S(2)}, u32[]{:S(2)}) collective-permute-start(bf16[16,32,256]{2,1,0:T(8,128)(2,1)S(1)} %slice.71), channel_id=1, source_target_pairs={{0,96},{32,0},{64,32},{96,64},{1,97},{33,1},{65,33},{97,65},{2,98}... | collective-permute-start | bytes 786440 | tf_op jit(solution)/shard_map/ppermute | solution.py:19
  63.3 2.7 %collective-permute-start.21 = (bf16[288,256]{1,0:T(8,128)(2,1)S(1)}, bf16[288,256]{1,0:T(8,128)(2,1)S(1)}, u32[]{:S(2)}, u32[]{:S(2)}) collective-permute-start(bf16[288,256]{1,0:T(8,128)(2,1)S(1)} %get-tuple-element.68), channel_id=1, source_target_pairs={{0,96},{32,0},{64,32},{96,64},{1,97},{33,1},{65,33},{97,65},{2,98}... | collective-permute-start | bytes 442376 | tf_op jit(solution)/shard_map/ppermute | solution.py:19
  65.9 1.7 %grad_first.5.refs_1_ = f32[768,768]{1,0:T(8,128)S(1)} custom-call(bf16[4,40,32,768]{3,2,1,0:T(8,128)(2,1)S(1)} %spread.1.wide_ref, bf16[32,32,256]{2,1,0:T(8,128)(2,1)S(1)} %collective-permute-done.13.refs_0_, f32[768,768]{1,0:T(8,128)S(1)} %grad_first.4.refs_1_), custom_call_target="tpu_custom_call" | custom-call | flops 1 | bytes 1 | tf_op jit(solution)/shard_map/grad_first/pallas_call | solution.py:176
  67.7 1.7 %grad_first.6.refs_2_ = f32[768,768]{1,0:T(8,128)S(1)} custom-call(bf16[4,40,32,768]{3,2,1,0:T(8,128)(2,1)S(1)} %spread.1.wide_ref, bf16[32,32,256]{2,1,0:T(8,128)(2,1)S(1)} %collective-permute-done.14.refs_0_, f32[768,768]{1,0:T(8,128)S(1)} %grad_first.5.refs_1_), custom_call_target="tpu_custom_call" | custom-call | flops 1 | bytes 1 | tf_op jit(solution)/shard_map/grad_first/pallas_call | solution.py:176
  69.4 2.2 %features.1 = bf16[32,32,256]{2,1,0:T(8,128)(2,1)} custom-call(bf16[34,32,256]{2,1,0:T(8,128)(2,1)S(1)} %get-tuple-element.55.hid_ref, bf16[34,256]{1,0:T(8,128)(2,1)S(1)} %collective-permute-done.15.before_ref, bf16[34,256]{1,0:T(8,128)(2,1)S(1)} %collective-permute-done.16.after_ref, bf16[2304,256]{1,0:T(8,128)(2,1)S(1)} %bitcast.47), custom_call_target="tpu_custom_call" | custom-call | flops 1 | bytes 1 | tf_op jit(solution)/shard_map/features/pallas_call | solution.py:298
  71.6 1.8 %grad_first.7 = (f32[384,768]{1,0:T(8,128)S(1)}, bf16[384,768]{1,0:T(8,128)(2,1)S(1)}) custom-call(bf16[4,40,32,768]{3,2,1,0:T(8,128)(2,1)S(1)} %spread.1.wide_ref, bf16[16,32,256]{2,1,0:T(8,128)(2,1)S(1)} %collective-permute-done.17.refs_0_, bf16[16,32,256]{2,1,0:T(8,128)(2,1)S(1)} %collective-permute-done.18.refs_1_, f32[768,768]{1,0:T(8,128)S(1)} %grad_first.6.refs_2_), custom_call_target="tpu_custom_call" | custom-call | flops 1 | bytes 1 | tf_op jit(solution)/shard_map/grad_first/pallas_call | solution.py:176
  73.4 3.1 %collective-permute-start.23 = (bf16[384,768]{1,0:T(8,128)(2,1)S(1)}, bf16[384,768]{1,0:T(8,128)(2,1)S(1)}, u32[]{:S(2)}, u32[]{:S(2)}) collective-permute-start(bf16[384,768]{1,0:T(8,128)(2,1)S(1)} %get-tuple-element.70), channel_id=1, source_target_pairs={{0,16},{16,0},{1,17},{17,1},{2,18},{18,2},{3,19},{19,3},{4,20},{20... | collective-permute-start | bytes 1769480 | tf_op jit(solution)/shard_map/ppermute | solution.py:19
  76.5 1.6 %collective-permute-done.23.far_ref = bf16[384,768]{1,0:T(8,128)(2,1)S(1)} collective-permute-done((bf16[384,768]{1,0:T(8,128)(2,1)S(1)}, bf16[384,768]{1,0:T(8,128)(2,1)S(1)}, u32[]{:S(2)}, u32[]{:S(2)}) %collective-permute-start.23) | collective-permute-done | bytes 589856 | tf_op jit(solution)/shard_map/ppermute | solution.py:19
  78.3 23.8 %all_to_all.5.in_ref = bf16[16,90,256]{2,1,0:T(8,128)(2,1)S(1)} all-to-all(bf16[16,90,256]{2,1,0:T(8,128)(2,1)S(1)} %join.1), channel_id=1, replica_groups=mesh['y'=4,'c'=2,'z'=4,'x'=4] {'z','x'}, dimensions={0} | all-to-all | bytes 1474560 | tf_op jit(solution)/shard_map/all_to_all | solution.py:643
  102.4 2.7 %collective-permute-start.25 = (bf16[90,256]{1,0:T(8,128)(2,1)S(1)}, bf16[90,256]{1,0:T(8,128)(2,1)S(1)}, u32[]{:S(2)}, u32[]{:S(2)}) collective-permute-start(bf16[90,256]{1,0:T(8,128)(2,1)S(1)} %sum_pieces.1.a_ref), channel_id=1, source_target_pairs={{0,12},{4,0},{8,4},{12,8},{1,13},{5,1},{9,5},{13,9},{2,14},{6,2},{... | collective-permute-start | bytes 138248 | tf_op jit(solution)/shard_map/ppermute | solution.py:19
  106.5 3.0 %collective-permute-done.26.d_ref = bf16[90,256]{1,0:T(8,128)(2,1)S(1)} collective-permute-done((bf16[90,256]{1,0:T(8,128)(2,1)S(1)}, bf16[90,256]{1,0:T(8,128)(2,1)S(1)}, u32[]{:S(2)}, u32[]{:S(2)}) %collective-permute-start.26) | collective-permute-done | bytes 46112 | tf_op jit(solution)/shard_map/ppermute | solution.py:19
  109.9 2.4 %collective-permute-start.28 = (bf16[360,256]{1,0:T(8,128)(2,1)S(1)}, bf16[360,256]{1,0:T(8,128)(2,1)S(1)}, u32[]{:S(2)}, u32[]{:S(2)}) collective-permute-start(bf16[360,256]{1,0:T(8,128)(2,1)S(1)} %order_pieces.1.a_ref), channel_id=1, source_target_pairs={{0,3},{1,0},{2,1},{3,2},{4,7},{5,4},{6,5},{7,6},{8,11},{9,8},{10,9... | collective-permute-start | bytes 552968 | tf_op jit(solution)/shard_map/ppermute | solution.py:19
  112.3 2.9 %collective-permute-done.27.b_ref = bf16[360,256]{1,0:T(8,128)(2,1)S(1)} collective-permute-done((bf16[360,256]{1,0:T(8,128)(2,1)S(1)}, bf16[360,256]{1,0:T(8,128)(2,1)S(1)}, u32[]{:S(2)}, u32[]{:S(2)}) %collective-permute-start.27) | collective-permute-done | bytes 184352 | tf_op jit(solution)/shard_map/ppermute | solution.py:19
  115.2 1.5 %collective-permute-done.28.c_ref = bf16[360,256]{1,0:T(8,128)(2,1)S(1)} collective-permute-done((bf16[360,256]{1,0:T(8,128)(2,1)S(1)}, bf16[360,256]{1,0:T(8,128)(2,1)S(1)}, u32[]{:S(2)}, u32[]{:S(2)}) %collective-permute-start.28) | collective-permute-done | bytes 184352 | tf_op jit(solution)/shard_map/ppermute | solution.py:19
  116.7 3.1 %collective-permute-done.29.d_ref = bf16[360,256]{1,0:T(8,128)(2,1)S(1)} collective-permute-done((bf16[360,256]{1,0:T(8,128)(2,1)S(1)}, bf16[360,256]{1,0:T(8,128)(2,1)S(1)}, u32[]{:S(2)}, u32[]{:S(2)}) %collective-permute-start.29) | collective-permute-done | bytes 184352 | tf_op jit(solution)/shard_map/ppermute | solution.py:19
  120.6 2.2 %collective-permute-start.31 = (bf16[4,72,256]{2,1,0:T(8,128)(2,1)S(1)}, bf16[4,72,256]{2,1,0:T(8,128)(2,1)S(1)}, u32[]{:S(2)}, u32[]{:S(2)}) collective-permute-start(bf16[4,72,256]{2,1,0:T(8,128)(2,1)S(1)} %pick_rows.1), channel_id=1, source_target_pairs={{0,96},{32,0},{64,32},{96,64},{1,97},{33,1},{65,33},{97,65},{2,98}... | collective-permute-start | bytes 442376 | tf_op jit(solution)/shard_map/ppermute | solution.py:19
  125.2 3.1 %collective-permute-done.32 = bf16[4,72,256]{2,1,0:T(8,128)(2,1)S(1)} collective-permute-done((bf16[4,72,256]{2,1,0:T(8,128)(2,1)S(1)}, bf16[4,72,256]{2,1,0:T(8,128)(2,1)S(1)}, u32[]{:S(2)}, u32[]{:S(2)}) %collective-permute-start.32) | collective-permute-done | bytes 147488 | tf_op jit(solution)/shard_map/ppermute | solution.py:19
  128.4 4.8 %collective-permute-start.33 = (bf16[4,4,72,256]{3,2,1,0:T(8,128)(2,1)S(1)}, bf16[4,4,72,256]{3,2,1,0:T(8,128)(2,1)S(1)}, u32[]{:S(2)}, u32[]{:S(2)}) collective-permute-start(bf16[4,4,72,256]{3,2,1,0:T(8,128)(2,1)S(1)} %pad_maximum_fusion.1.in_ref), channel_id=1, source_target_pairs={{0,16},{16,0},{1,17},{17,1},{2,18},{18,2},{3,19},{19,3},{4,20},{20... | collective-permute-start | bytes 1769480 | tf_op jit(solution)/shard_map/ppermute | solution.py:19
  (82 shorter events, 31.2 us)
Async XLA Ops:
  0.6 15.8 %collective-permute-start = (bf16[256,32,128]{2,1,0:T(8,128)(2,1)}, bf16[256,32,128]{2,1,0:T(8,128)(2,1)S(1)}, u32[]{:S(2)}, u32[]{:S(2)}) collective-permute-start(bf16[256,32,128]{2,1,0:T(8,128)(2,1)} %own_ref.1), channel_id=1, source_target_pairs={{0,16},{16,0},{1,17},{17,1},{2,18},{18,2},{3,19},{19,3},{4,20},{20... | collective-permute-start | bytes 6291464 | tf_op jit(solution)/shard_map/ppermute | solution.py:19
  4.6 5.8 %collective-permute-start.1 = (bf16[320,128]{1,0:T(8,128)(2,1)S(1)}, bf16[320,128]{1,0:T(8,128)(2,1)S(1)}, u32[]{:S(2)}, u32[]{:S(2)}) collective-permute-start(bf16[320,128]{1,0:T(8,128)(2,1)S(1)} %pad_maximum_fusion.3), channel_id=1, source_target_pairs={{0,1},{1,2},{2,3},{3,4},{4,5},{5,6},{6,7},{7,8},{8,9},{9,10},{10,1... | collective-permute-start | bytes 245768 | tf_op jit(solution)/shard_map/ppermute | solution.py:383
  7.8 7.4 %collective-permute-start.4 = (bf16[3,3,128,256]{3,2,1,0:T(8,128)(2,1)}, bf16[3,3,128,256]{3,2,1,0:T(8,128)(2,1)S(1)}, u32[]{:S(2)}, u32[]{:S(2)}) collective-permute-start(bf16[3,3,128,256]{3,2,1,0:T(8,128)(2,1)} %param.5), channel_id=1, source_target_pairs={{0,16},{16,0},{1,17},{17,1},{2,18},{18,2},{3,19},{19,3},{4,20},{20... | collective-permute-start | bytes 1769480 | tf_op jit(solution)/shard_map/ppermute | solution.py:19
  8.4 5.9 %collective-permute-start.2 = (bf16[320,128]{1,0:T(8,128)(2,1)S(1)}, bf16[320,128]{1,0:T(8,128)(2,1)S(1)}, u32[]{:S(2)}, u32[]{:S(2)}) collective-permute-start(bf16[320,128]{1,0:T(8,128)(2,1)S(1)} %pad_maximum_fusion.4), channel_id=1, source_target_pairs={{1,0},{2,1},{3,2},{4,3},{5,4},{6,5},{7,6},{8,7},{9,8},{10,9},{11,1... | collective-permute-start | bytes 245768 | tf_op jit(solution)/shard_map/ppermute | solution.py:383
  19.8 10.5 %collective-permute-start.5 = (bf16[17,32,256]{2,1,0:T(8,128)(2,1)S(1)}, bf16[17,32,256]{2,1,0:T(8,128)(2,1)S(1)}, u32[]{:S(2)}, u32[]{:S(2)}) collective-permute-start(bf16[17,32,256]{2,1,0:T(8,128)(2,1)S(1)} %get-tuple-element.40), channel_id=1, source_target_pairs={{0,32},{32,64},{64,96},{96,0},{1,33},{33,65},{65,97},{97,1},{2,34}... | collective-permute-start | bytes 835592 | tf_op jit(solution)/shard_map/ppermute | solution.py:19
  21.2 9.2 %collective-permute-start.8 = (bf16[17,32,256]{2,1,0:T(8,128)(2,1)S(1)}, bf16[17,32,256]{2,1,0:T(8,128)(2,1)S(1)}, u32[]{:S(2)}, u32[]{:S(2)}) collective-permute-start(bf16[17,32,256]{2,1,0:T(8,128)(2,1)S(1)} %get-tuple-element.42), channel_id=1, source_target_pairs={{0,96},{32,0},{64,32},{96,64},{1,97},{33,1},{65,33},{97,65},{2,98}... | collective-permute-start | bytes 835592 | tf_op jit(solution)/shard_map/ppermute | solution.py:19
  22.7 7.5 %collective-permute-start.6 = (bf16[34,256]{1,0:T(8,128)(2,1)S(1)}, bf16[34,256]{1,0:T(8,128)(2,1)S(1)}, u32[]{:S(2)}, u32[]{:S(2)}) collective-permute-start(bf16[34,256]{1,0:T(8,128)(2,1)S(1)} %maximum_maximum_fusion), channel_id=1, source_target_pairs={{0,16},{16,32},{32,48},{48,64},{64,80},{80,96},{96,112},{1,17},{17... | collective-permute-start | bytes 52232 | tf_op jit(solution)/shard_map/ppermute | solution.py:605
  25.2 5.1 %collective-permute-start.7 = (bf16[34,256]{1,0:T(8,128)(2,1)S(1)}, bf16[34,256]{1,0:T(8,128)(2,1)S(1)}, u32[]{:S(2)}, u32[]{:S(2)}) collective-permute-start(bf16[34,256]{1,0:T(8,128)(2,1)S(1)} %maximum_maximum_fusion.1), channel_id=1, source_target_pairs={{16,0},{32,16},{48,32},{64,48},{80,64},{96,80},{112,96},{17,1},{33... | collective-permute-start | bytes 52232 | tf_op jit(solution)/shard_map/ppermute | solution.py:606
  28.6 8.8 %collective-permute-start.10 = (bf16[17,32,256]{2,1,0:T(8,128)(2,1)S(1)}, bf16[17,32,256]{2,1,0:T(8,128)(2,1)S(1)}, u32[]{:S(2)}, u32[]{:S(2)}) collective-permute-start(bf16[17,32,256]{2,1,0:T(8,128)(2,1)S(1)} %get-tuple-element.45), channel_id=1, source_target_pairs={{0,96},{32,0},{64,32},{96,64},{1,97},{33,1},{65,33},{97,65},{2,98}... | collective-permute-start | bytes 835592 | tf_op jit(solution)/shard_map/ppermute | solution.py:19
  30.2 7.3 %collective-permute-start.11 = (bf16[17,32,256]{2,1,0:T(8,128)(2,1)S(1)}, bf16[17,32,256]{2,1,0:T(8,128)(2,1)S(1)}, u32[]{:S(2)}, u32[]{:S(2)}) collective-permute-start(bf16[17,32,256]{2,1,0:T(8,128)(2,1)S(1)} %get-tuple-element.46), channel_id=1, source_target_pairs={{0,32},{32,64},{64,96},{96,0},{1,33},{33,65},{65,97},{97,1},{2,34}... | collective-permute-start | bytes 835592 | tf_op jit(solution)/shard_map/ppermute | solution.py:19
  31.8 11.0 %collective-permute-start.12 = (bf16[17,32,256]{2,1,0:T(8,128)(2,1)S(1)}, bf16[17,32,256]{2,1,0:T(8,128)(2,1)S(1)}, u32[]{:S(2)}, u32[]{:S(2)}) collective-permute-start(bf16[17,32,256]{2,1,0:T(8,128)(2,1)S(1)} %get-tuple-element.47), channel_id=1, source_target_pairs={{0,96},{32,0},{64,32},{96,64},{1,97},{33,1},{65,33},{97,65},{2,98}... | collective-permute-start | bytes 835592 | tf_op jit(solution)/shard_map/ppermute | solution.py:19
  34.5 9.9 %collective-permute-start.9 = (bf16[17,32,256]{2,1,0:T(8,128)(2,1)S(1)}, bf16[17,32,256]{2,1,0:T(8,128)(2,1)S(1)}, u32[]{:S(2)}, u32[]{:S(2)}) collective-permute-start(bf16[17,32,256]{2,1,0:T(8,128)(2,1)S(1)} %get-tuple-element.43), channel_id=1, source_target_pairs={{0,32},{32,64},{64,96},{96,0},{1,33},{33,65},{65,97},{97,1},{2,34}... | collective-permute-start | bytes 835592 | tf_op jit(solution)/shard_map/ppermute | solution.py:19
  44.9 15.2 %collective-permute-start.13 = (bf16[32,32,256]{2,1,0:T(8,128)(2,1)S(1)}, bf16[32,32,256]{2,1,0:T(8,128)(2,1)S(1)}, u32[]{:S(2)}, u32[]{:S(2)}) collective-permute-start(bf16[32,32,256]{2,1,0:T(8,128)(2,1)S(1)} %get-tuple-element.51.refs_0_), channel_id=1, source_target_pairs={{0,32},{32,64},{64,96},{96,0},{1,33},{33,65},{65,97},{97,1},{2,34}... | collective-permute-start | bytes 1572872 | tf_op jit(solution)/shard_map/ppermute | solution.py:19
  45.0 15.1 %collective-permute-start.14 = (bf16[32,32,256]{2,1,0:T(8,128)(2,1)S(1)}, bf16[32,32,256]{2,1,0:T(8,128)(2,1)S(1)}, u32[]{:S(2)}, u32[]{:S(2)}) collective-permute-start(bf16[32,32,256]{2,1,0:T(8,128)(2,1)S(1)} %get-tuple-element.51.refs_0_), channel_id=1, source_target_pairs={{0,96},{32,0},{64,32},{96,64},{1,97},{33,1},{65,33},{97,65},{2,98}... | collective-permute-start | bytes 1572872 | tf_op jit(solution)/shard_map/ppermute | solution.py:19
  49.6 13.4 %collective-permute-start.19 = (bf16[4,288,256]{2,1,0:T(8,128)(2,1)S(1)}, bf16[4,288,256]{2,1,0:T(8,128)(2,1)S(1)}, u32[]{:S(2)}, u32[]{:S(2)}) collective-permute-start(bf16[4,288,256]{2,1,0:T(8,128)(2,1)S(1)} %get-tuple-element.66), channel_id=1, source_target_pairs={{0,16},{16,0},{1,17},{17,1},{2,18},{18,2},{3,19},{19,3},{4,20},{20... | collective-permute-start | bytes 1769480 | tf_op jit(solution)/shard_map/ppermute | solution.py:19
  52.3 6.4 %collective-permute-start.15 = (bf16[34,256]{1,0:T(8,128)(2,1)S(1)}, bf16[34,256]{1,0:T(8,128)(2,1)S(1)}, u32[]{:S(2)}, u32[]{:S(2)}) collective-permute-start(bf16[34,256]{1,0:T(8,128)(2,1)S(1)} %get-tuple-element.52), channel_id=1, source_target_pairs={{0,1},{1,2},{2,3},{3,4},{4,5},{5,6},{6,7},{7,8},{8,9},{9,10},{10,1... | collective-permute-start | bytes 52232 | tf_op jit(solution)/shard_map/ppermute | solution.py:383
  55.6 4.6 %collective-permute-start.16 = (bf16[34,256]{1,0:T(8,128)(2,1)S(1)}, bf16[34,256]{1,0:T(8,128)(2,1)S(1)}, u32[]{:S(2)}, u32[]{:S(2)}) collective-permute-start(bf16[34,256]{1,0:T(8,128)(2,1)S(1)} %get-tuple-element.53), channel_id=1, source_target_pairs={{1,0},{2,1},{3,2},{4,3},{5,4},{6,5},{7,6},{8,7},{9,8},{10,9},{11,1... | collective-permute-start | bytes 52232 | tf_op jit(solution)/shard_map/ppermute | solution.py:383
  60.2 11.4 %collective-permute-start.17 = (bf16[16,32,256]{2,1,0:T(8,128)(2,1)S(1)}, bf16[16,32,256]{2,1,0:T(8,128)(2,1)S(1)}, u32[]{:S(2)}, u32[]{:S(2)}) collective-permute-start(bf16[16,32,256]{2,1,0:T(8,128)(2,1)S(1)} %slice.70), channel_id=1, source_target_pairs={{0,32},{32,64},{64,96},{96,0},{1,33},{33,65},{65,97},{97,1},{2,34}... | collective-permute-start | bytes 786440 | tf_op jit(solution)/shard_map/ppermute | solution.py:19
  60.3 11.3 %collective-permute-start.18 = (bf16[16,32,256]{2,1,0:T(8,128)(2,1)S(1)}, bf16[16,32,256]{2,1,0:T(8,128)(2,1)S(1)}, u32[]{:S(2)}, u32[]{:S(2)}) collective-permute-start(bf16[16,32,256]{2,1,0:T(8,128)(2,1)S(1)} %slice.71), channel_id=1, source_target_pairs={{0,96},{32,0},{64,32},{96,64},{1,97},{33,1},{65,33},{97,65},{2,98}... | collective-permute-start | bytes 786440 | tf_op jit(solution)/shard_map/ppermute | solution.py:19
  63.2 10.2 %collective-permute-start.20 = (bf16[288,256]{1,0:T(8,128)(2,1)S(1)}, bf16[288,256]{1,0:T(8,128)(2,1)S(1)}, u32[]{:S(2)}, u32[]{:S(2)}) collective-permute-start(bf16[288,256]{1,0:T(8,128)(2,1)S(1)} %get-tuple-element.67), channel_id=1, source_target_pairs={{0,32},{32,64},{64,96},{96,0},{1,33},{33,65},{65,97},{97,1},{2,34}... | collective-permute-start | bytes 442376 | tf_op jit(solution)/shard_map/ppermute | solution.py:19
  63.3 10.2 %collective-permute-start.21 = (bf16[288,256]{1,0:T(8,128)(2,1)S(1)}, bf16[288,256]{1,0:T(8,128)(2,1)S(1)}, u32[]{:S(2)}, u32[]{:S(2)}) collective-permute-start(bf16[288,256]{1,0:T(8,128)(2,1)S(1)} %get-tuple-element.68), channel_id=1, source_target_pairs={{0,96},{32,0},{64,32},{96,64},{1,97},{33,1},{65,33},{97,65},{2,98}... | collective-permute-start | bytes 442376 | tf_op jit(solution)/shard_map/ppermute | solution.py:19
  65.9 7.5 %collective-permute-start.22 = (bf16[288,256]{1,0:T(8,128)(2,1)S(1)}, bf16[288,256]{1,0:T(8,128)(2,1)S(1)}, u32[]{:S(2)}, u32[]{:S(2)}) collective-permute-start(bf16[288,256]{1,0:T(8,128)(2,1)S(1)} %get-tuple-element.69), channel_id=1, source_target_pairs={{0,64},{32,96},{64,0},{96,32},{1,65},{33,97},{65,1},{97,33},{2,66}... | collective-permute-start | bytes 442376 | tf_op jit(solution)/shard_map/ppermute | solution.py:19
  73.4 4.7 %collective-permute-start.23 = (bf16[384,768]{1,0:T(8,128)(2,1)S(1)}, bf16[384,768]{1,0:T(8,128)(2,1)S(1)}, u32[]{:S(2)}, u32[]{:S(2)}) collective-permute-start(bf16[384,768]{1,0:T(8,128)(2,1)S(1)} %get-tuple-element.70), channel_id=1, source_target_pairs={{0,16},{16,0},{1,17},{17,1},{2,18},{18,2},{3,19},{19,3},{4,20},{20... | collective-permute-start | bytes 1769480 | tf_op jit(solution)/shard_map/ppermute | solution.py:19
  102.3 4.2 %collective-permute-start.24 = (bf16[90,256]{1,0:T(8,128)(2,1)S(1)}, bf16[90,256]{1,0:T(8,128)(2,1)S(1)}, u32[]{:S(2)}, u32[]{:S(2)}) collective-permute-start(bf16[90,256]{1,0:T(8,128)(2,1)S(1)} %sum_pieces.1.a_ref), channel_id=1, source_target_pairs={{0,4},{4,8},{8,12},{12,0},{1,5},{5,9},{9,13},{13,1},{2,6},{6,10},{... | collective-permute-start | bytes 138248 | tf_op jit(solution)/shard_map/ppermute | solution.py:19
  105.0 4.4 %collective-permute-start.26 = (bf16[90,256]{1,0:T(8,128)(2,1)S(1)}, bf16[90,256]{1,0:T(8,128)(2,1)S(1)}, u32[]{:S(2)}, u32[]{:S(2)}) collective-permute-start(bf16[90,256]{1,0:T(8,128)(2,1)S(1)} %sum_pieces.1.a_ref), channel_id=1, source_target_pairs={{0,8},{4,12},{8,0},{12,4},{1,9},{5,13},{9,1},{13,5},{2,10},{6,14},... | collective-permute-start | bytes 138248 | tf_op jit(solution)/shard_map/ppermute | solution.py:19
  109.5 5.7 %collective-permute-start.27 = (bf16[360,256]{1,0:T(8,128)(2,1)S(1)}, bf16[360,256]{1,0:T(8,128)(2,1)S(1)}, u32[]{:S(2)}, u32[]{:S(2)}) collective-permute-start(bf16[360,256]{1,0:T(8,128)(2,1)S(1)} %order_pieces.1.a_ref), channel_id=1, source_target_pairs={{0,1},{1,2},{2,3},{3,0},{4,5},{5,6},{6,7},{7,4},{8,9},{9,10},{10,1... | collective-permute-start | bytes 552968 | tf_op jit(solution)/shard_map/ppermute | solution.py:19
  109.9 6.9 %collective-permute-start.28 = (bf16[360,256]{1,0:T(8,128)(2,1)S(1)}, bf16[360,256]{1,0:T(8,128)(2,1)S(1)}, u32[]{:S(2)}, u32[]{:S(2)}) collective-permute-start(bf16[360,256]{1,0:T(8,128)(2,1)S(1)} %order_pieces.1.a_ref), channel_id=1, source_target_pairs={{0,3},{1,0},{2,1},{3,2},{4,7},{5,4},{6,5},{7,6},{8,11},{9,8},{10,9... | collective-permute-start | bytes 552968 | tf_op jit(solution)/shard_map/ppermute | solution.py:19
  112.3 7.5 %collective-permute-start.29 = (bf16[360,256]{1,0:T(8,128)(2,1)S(1)}, bf16[360,256]{1,0:T(8,128)(2,1)S(1)}, u32[]{:S(2)}, u32[]{:S(2)}) collective-permute-start(bf16[360,256]{1,0:T(8,128)(2,1)S(1)} %order_pieces.1.a_ref), channel_id=1, source_target_pairs={{0,2},{1,3},{2,0},{3,1},{4,6},{5,7},{6,4},{7,5},{8,10},{9,11},{10,... | collective-permute-start | bytes 552968 | tf_op jit(solution)/shard_map/ppermute | solution.py:19
  119.8 5.4 %collective-permute-start.30 = (bf16[4,72,256]{2,1,0:T(8,128)(2,1)S(1)}, bf16[4,72,256]{2,1,0:T(8,128)(2,1)S(1)}, u32[]{:S(2)}, u32[]{:S(2)}) collective-permute-start(bf16[4,72,256]{2,1,0:T(8,128)(2,1)S(1)} %pick_rows.1), channel_id=1, source_target_pairs={{0,32},{32,64},{64,96},{96,0},{1,33},{33,65},{65,97},{97,1},{2,34}... | collective-permute-start | bytes 442376 | tf_op jit(solution)/shard_map/ppermute | solution.py:19
  120.6 4.6 %collective-permute-start.31 = (bf16[4,72,256]{2,1,0:T(8,128)(2,1)S(1)}, bf16[4,72,256]{2,1,0:T(8,128)(2,1)S(1)}, u32[]{:S(2)}, u32[]{:S(2)}) collective-permute-start(bf16[4,72,256]{2,1,0:T(8,128)(2,1)S(1)} %pick_rows.1), channel_id=1, source_target_pairs={{0,96},{32,0},{64,32},{96,64},{1,97},{33,1},{65,33},{97,65},{2,98}... | collective-permute-start | bytes 442376 | tf_op jit(solution)/shard_map/ppermute | solution.py:19
  122.7 5.6 %collective-permute-start.32 = (bf16[4,72,256]{2,1,0:T(8,128)(2,1)S(1)}, bf16[4,72,256]{2,1,0:T(8,128)(2,1)S(1)}, u32[]{:S(2)}, u32[]{:S(2)}) collective-permute-start(bf16[4,72,256]{2,1,0:T(8,128)(2,1)S(1)} %pick_rows.1), channel_id=1, source_target_pairs={{0,64},{32,96},{64,0},{96,32},{1,65},{33,97},{65,1},{97,33},{2,66}... | collective-permute-start | bytes 442376 | tf_op jit(solution)/shard_map/ppermute | solution.py:19
  128.4 6.5 %collective-permute-start.33 = (bf16[4,4,72,256]{3,2,1,0:T(8,128)(2,1)S(1)}, bf16[4,4,72,256]{3,2,1,0:T(8,128)(2,1)S(1)}, u32[]{:S(2)}, u32[]{:S(2)}) collective-permute-start(bf16[4,4,72,256]{3,2,1,0:T(8,128)(2,1)S(1)} %pad_maximum_fusion.1.in_ref), channel_id=1, source_target_pairs={{0,16},{16,0},{1,17},{17,1},{2,18},{18,2},{3,19},{19,3},{4,20},{20... | collective-permute-start | bytes 1769480 | tf_op jit(solution)/shard_map/ppermute | solution.py:19
  (5 other events, 25.0 us)

commit v12 on v11

--- a/solution.py
+++ b/solution.py
@@ -527,25 +527,22 @@
     third = half_ref.shape[0] // 3
     core, y, x = lax.axis_index("c"), lax.axis_index("y"), lax.axis_index("x")
     half = 1 - core if other else core
-    for i in range(sy):
-        for j in range(sx):
-            place = lax.rem(y + sy - STEPS[i], sy) * sx + lax.rem(x + sx - STEPS[j], sx)
-            value = in_ref[i, j].astype(F32)
-            for tap in range(3):
-                at = pl.multiple_of(tap * third + place * size, 8)
-                half_ref[pl.ds(at, size), :] = value[tap * size : (tap + 1) * size]
     copies = []
     for tap in range(3):
+        for i in range(sy):
+            for j in range(sx):
+                place = lax.rem(y + sy - STEPS[i], sy) * sx + lax.rem(x + sx - STEPS[j], sx)
+                at = pl.multiple_of(tap * third + place * size, 8)
+                value = in_ref[i, j, tap * size : (tap + 1) * size, :].astype(F32)
+                half_ref[pl.ds(at, size), :] = value
         to = pl.multiple_of((2 * tap + half) * third, 8)
-        copies.append(
-            pltpu.make_async_copy(
-                half_ref.at[tap * third : (tap + 1) * third],
-                out_ref.at[pl.ds(to, third)],
-                sems.at[tap],
-            )
+        copy = pltpu.make_async_copy(
+            half_ref.at[tap * third : (tap + 1) * third],
+            out_ref.at[pl.ds(to, third)],
+            sems.at[tap],
         )
-    for copy in copies:
         copy.start()
+        copies.append(copy)
     for copy in copies:
         copy.wait()
 
@@ -633,7 +630,6 @@
     got = [shift(send, "y", step) for step, send in zip(STEPS[1:], sends)]
     total = grad_strip(off, wide, (from_on,), total, False)
     total = grad_strip(on, wide, (from_off,), total, False)
-    fwd_a, features = lax.optimization_barrier((fwd_a, features))
     first_own, first_far = grad_strip(2, wide, (fwd_a, fwd_b), total, True)
 
     sx, sz = lax.axis_size("x"), lax.axis_size("z")
@@ -646,6 +642,7 @@
     main = parts[0].shape[0] - sz * extra
     grad_first = lay_first(parts, sz, chans)
     share = pick_rows(parts, main)
+    share, features = lax.optimization_barrier((share, features))
     share, grad_first = lax.optimization_barrier(
         (jnp.stack(gather_steps(share, "y")), grad_first)
     )

time: 137 us -> 137 us (level)
  waiting for transfers between devices: 29.8 us -> 23.3 us
  starting transfers between devices: 52.1 us -> 55.8 us
  blocking collectives: 23.8 us -> 27.1 us
    ppermute x28, waiting for transfers between devices: 24.4 us -> 20.5 us  [shift(): lax.ppermute(x, axis, [(i, (i + step) % count) for i in range(count)])]
    all_to_all x1, blocking collectives: 23.8 us -> 27.1 us  [body(): summed = lax.all_to_all(joined, SKY, 0, 0, tiled=True)]
    ppermute x4, waiting for transfers between devices: 5.34 us -> 2.79 us  [row_halo(): return (lax.ppermute(ends[0], SKY, up), lax.ppermute(ends[1], SKY, down))]
    ppermute x4, starting transfers between devices: 9.08 us -> 11.2 us  [row_halo(): return (lax.ppermute(ends[0], SKY, up), lax.ppermute(ends[1], SKY, down))]
    ppermute x28, starting transfers between devices: 38.6 us -> 40.2 us  [shift(): lax.ppermute(x, axis, [(i, (i + step) % count) for i in range(count)])]
  transfers between devices with their start and end apart: 34 -> 34, of which waited for: 15 -> 14; matrix products, arithmetic and copies ran while one was open for 3% -> 3% of each run, Pallas kernels for 14% -> 14%
where the time goes in v12:
time: 137 us
  starting transfers between devices  55.8 us (41%)
  blocking collectives  27.1 us (20%)
  Pallas kernels  24.7 us (18%)
  waiting for transfers between devices  23.3 us (17%)
  local copies, waits for them, and re-layouts  3.25 us (2%)
    ppermute x28, starting transfers between devices, shift(): lax.ppermute(x, axis, [(i, (i + step) % count) for i in range(count)])  40.2 us
    all_to_all x1, blocking collectives, body(): summed = lax.all_to_all(joined, SKY, 0, 0, tiled=True)  27.1 us
    ppermute x28, waiting for transfers between devices, shift(): lax.ppermute(x, axis, [(i, (i + step) % count) for i in range(count)])  20.5 us
    ppermute x4, starting transfers between devices, row_halo(): return (lax.ppermute(ends[0], SKY, up), lax.ppermute(ends[1], SKY, down))  11.2 us
    pallas_call x4, Pallas kernels, grad_strip(): pl.pallas_call(functools.partial(grad_kernel, step, len(pieces), old is n...  7 us
    pallas_call x4, Pallas kernels, conv_parts(): pl.pallas_call(functools.partial(conv_kernel, parts, len(adds)), out_shap...  5.84 us
    ppermute x4, waiting for transfers between devices, row_halo(): return (lax.ppermute(ends[0], SKY, up), lax.ppermute(ends[1], SKY, down))  2.79 us
  transfers between devices with their start and end apart: 34, of which 14 were waited for; matrix products, arithmetic and copies ran while one was open for 3% of the time, Pallas kernels for 14%

profile of v12, /device:TPU:1, one launch (start us, length us, event | category | flops | bytes accessed | tf_op | source)
XLA Modules:
  0.0 136.6 jit_solution(6841616313743603753)
XLA Ops:
  0.6 1.5 %collective-permute-start = (bf16[256,32,128]{2,1,0:T(8,128)(2,1)}, bf16[256,32,128]{2,1,0:T(8,128)(2,1)S(1)}, u32[]{:S(2)}, u32[]{:S(2)}) collective-permute-start(bf16[256,32,128]{2,1,0:T(8,128)(2,1)} %own_ref.1), channel_id=1, source_target_pairs={{0,16},{16,0},{1,17},{17,1},{2,18},{18,2},{3,19},{19,3},{4,20},{20... | collective-permute-start | bytes 6291464 | tf_op jit(solution)/shard_map/ppermute | solution.py:19
  6.2 4.3 %collective-permute-start.1 = (bf16[320,128]{1,0:T(8,128)(2,1)S(1)}, bf16[320,128]{1,0:T(8,128)(2,1)S(1)}, u32[]{:S(2)}, u32[]{:S(2)}) collective-permute-start(bf16[320,128]{1,0:T(8,128)(2,1)S(1)} %pad_maximum_fusion.3), channel_id=1, source_target_pairs={{0,1},{1,2},{2,3},{3,4},{4,5},{5,6},{6,7},{7,8},{8,9},{9,10},{10,1... | collective-permute-start | bytes 245768 | tf_op jit(solution)/shard_map/ppermute | solution.py:383
  14.4 1.9 %spread.1.wide_ref = bf16[4,40,32,768]{3,2,1,0:T(8,128)(2,1)S(1)} custom-call(bf16[256,32,128]{2,1,0:T(8,128)(2,1)S(1)} %copy-done.1, bf16[256,32,128]{2,1,0:T(8,128)(2,1)S(1)} %collective-permute-done.far_ref, bf16[2,320,128]{2,1,0:T(8,128)(2,1)S(1)} %pad_maximum_fusion.2.own_halo_ref.edge_ref, bf16[2,320,128]{2,1,0:T(8,128)(2,1)S(1)} %collective-permute-done.3.far_halo_ref), custom_call_target="tpu_custom_call" | custom-call | flops 1 | bytes 1 | tf_op jit(solution)/shard_map/spread/pallas_call | solution.py:94
  17.8 2.9 %collective-permute-start.8 = (bf16[17,32,256]{2,1,0:T(8,128)(2,1)S(1)}, bf16[17,32,256]{2,1,0:T(8,128)(2,1)S(1)}, u32[]{:S(2)}, u32[]{:S(2)}) collective-permute-start(bf16[17,32,256]{2,1,0:T(8,128)(2,1)S(1)} %get-tuple-element.42), channel_id=1, source_target_pairs={{0,96},{32,0},{64,32},{96,64},{1,97},{33,1},{65,33},{97,65},{2,98}... | collective-permute-start | bytes 835592 | tf_op jit(solution)/shard_map/ppermute | solution.py:19
  20.7 2.6 %collective-permute-start.6 = (bf16[34,256]{1,0:T(8,128)(2,1)S(1)}, bf16[34,256]{1,0:T(8,128)(2,1)S(1)}, u32[]{:S(2)}, u32[]{:S(2)}) collective-permute-start(bf16[34,256]{1,0:T(8,128)(2,1)S(1)} %maximum_maximum_fusion), channel_id=1, source_target_pairs={{0,16},{16,32},{32,48},{48,64},{64,80},{80,96},{96,112},{1,17},{17... | collective-permute-start | bytes 52232 | tf_op jit(solution)/shard_map/ppermute | solution.py:602
  23.3 1.9 %collective-permute-start.7 = (bf16[34,256]{1,0:T(8,128)(2,1)S(1)}, bf16[34,256]{1,0:T(8,128)(2,1)S(1)}, u32[]{:S(2)}, u32[]{:S(2)}) collective-permute-start(bf16[34,256]{1,0:T(8,128)(2,1)S(1)} %maximum_maximum_fusion.1), channel_id=1, source_target_pairs={{16,0},{32,16},{48,32},{64,48},{80,64},{96,80},{112,96},{17,1},{33... | collective-permute-start | bytes 52232 | tf_op jit(solution)/shard_map/ppermute | solution.py:603
  26.7 2.8 %collective-permute-start.10 = (bf16[17,32,256]{2,1,0:T(8,128)(2,1)S(1)}, bf16[17,32,256]{2,1,0:T(8,128)(2,1)S(1)}, u32[]{:S(2)}, u32[]{:S(2)}) collective-permute-start(bf16[17,32,256]{2,1,0:T(8,128)(2,1)S(1)} %get-tuple-element.45), channel_id=1, source_target_pairs={{0,96},{32,0},{64,32},{96,64},{1,97},{33,1},{65,33},{97,65},{2,98}... | collective-permute-start | bytes 835592 | tf_op jit(solution)/shard_map/ppermute | solution.py:19
  31.9 1.9 %collective-permute-start.12 = (bf16[17,32,256]{2,1,0:T(8,128)(2,1)S(1)}, bf16[17,32,256]{2,1,0:T(8,128)(2,1)S(1)}, u32[]{:S(2)}, u32[]{:S(2)}) collective-permute-start(bf16[17,32,256]{2,1,0:T(8,128)(2,1)S(1)} %get-tuple-element.47), channel_id=1, source_target_pairs={{0,96},{32,0},{64,32},{96,64},{1,97},{33,1},{65,33},{97,65},{2,98}... | collective-permute-start | bytes 835592 | tf_op jit(solution)/shard_map/ppermute | solution.py:19
  33.8 1.5 %conv_first.4.own_ref = f32[34,32,256]{2,1,0:T(8,128)S(1)} custom-call(bf16[4,40,32,768]{3,2,1,0:T(8,128)(2,1)S(1)} %spread.1.wide_ref, bf16[2304,256]{1,0:T(8,128)(2,1)S(1)} %bitcast.46), custom_call_target="tpu_custom_call" | custom-call | flops 1 | bytes 1 | tf_op jit(solution)/shard_map/conv_first/pallas_call | solution.py:125
  35.3 1.5 %back.1 = (f32[32,32,256]{2,1,0:T(8,128)S(1)}, bf16[34,32,768]{2,1,0:T(8,128)(2,1)S(1)}) custom-call(bf16[32,32,256]{2,1,0:T(8,128)(2,1)S(1)} %copy-done.2, bf16[34,256]{1,0:T(8,128)(2,1)S(1)} %collective-permute-done.6.left_ref, bf16[34,256]{1,0:T(8,128)(2,1)S(1)} %collective-permute-done.7.right_ref, ...), custom_call_target="tpu_custom_call" | custom-call | flops 1 | bytes 1 | tf_op jit(solution)/shard_map/back/pallas_call | solution.py:232
  36.8 6.0 %collective-permute-done.9.a0_ref = bf16[17,32,256]{2,1,0:T(8,128)(2,1)S(1)} collective-permute-done((bf16[17,32,256]{2,1,0:T(8,128)(2,1)S(1)}, bf16[17,32,256]{2,1,0:T(8,128)(2,1)S(1)}, u32[]{:S(2)}, u32[]{:S(2)}) %collective-permute-start.9) | collective-permute-done | bytes 278560 | tf_op jit(solution)/shard_map/ppermute | solution.py:19
  43.3 1.8 %collective-permute-start.14 = (bf16[32,32,256]{2,1,0:T(8,128)(2,1)S(1)}, bf16[32,32,256]{2,1,0:T(8,128)(2,1)S(1)}, u32[]{:S(2)}, u32[]{:S(2)}) collective-permute-start(bf16[32,32,256]{2,1,0:T(8,128)(2,1)S(1)} %get-tuple-element.51.refs_0_), channel_id=1, source_target_pairs={{0,96},{32,0},{64,32},{96,64},{1,97},{33,1},{65,33},{97,65},{2,98}... | collective-permute-start | bytes 1572872 | tf_op jit(solution)/shard_map/ppermute | solution.py:19
  45.2 1.9 %second.1 = (f32[4,288,256]{2,1,0:T(8,128)S(1)}, bf16[4,288,256]{2,1,0:T(8,128)(2,1)S(1)}) custom-call(bf16[34,32,256]{2,1,0:T(8,128)(2,1)S(1)} %get-tuple-element.59.hid_ref, bf16[34,32,768]{2,1,0:T(8,128)(2,1)S(1)} %get-tuple-element.60.wide_ref), custom_call_target="tpu_custom_call" | custom-call | flops 1 | bytes 1 | tf_op jit(solution)/shard_map/second/pallas_call | solution.py:271
  47.1 3.3 %collective-permute-start.19 = (bf16[4,288,256]{2,1,0:T(8,128)(2,1)S(1)}, bf16[4,288,256]{2,1,0:T(8,128)(2,1)S(1)}, u32[]{:S(2)}, u32[]{:S(2)}) collective-permute-start(bf16[4,288,256]{2,1,0:T(8,128)(2,1)S(1)} %get-tuple-element.62), channel_id=1, source_target_pairs={{0,16},{16,0},{1,17},{17,1},{2,18},{18,2},{3,19},{19,3},{4,20},{20... | collective-permute-start | bytes 1769480 | tf_op jit(solution)/shard_map/ppermute | solution.py:19
  50.4 4.3 %collective-permute-start.15 = (bf16[34,256]{1,0:T(8,128)(2,1)S(1)}, bf16[34,256]{1,0:T(8,128)(2,1)S(1)}, u32[]{:S(2)}, u32[]{:S(2)}) collective-permute-start(bf16[34,256]{1,0:T(8,128)(2,1)S(1)} %get-tuple-element.52), channel_id=1, source_target_pairs={{0,1},{1,2},{2,3},{3,4},{4,5},{5,6},{6,7},{7,8},{8,9},{9,10},{10,1... | collective-permute-start | bytes 52232 | tf_op jit(solution)/shard_map/ppermute | solution.py:383
  56.0 1.7 %grad_first.4.refs_1_ = f32[768,768]{1,0:T(8,128)S(1)} custom-call(bf16[4,40,32,768]{3,2,1,0:T(8,128)(2,1)S(1)} %spread.1.wide_ref, bf16[32,32,256]{2,1,0:T(8,128)(2,1)S(1)} %get-tuple-element.51.refs_0_), custom_call_target="tpu_custom_call" | custom-call | flops 1 | bytes 1 | tf_op jit(solution)/shard_map/grad_first/pallas_call | solution.py:176
  57.7 1.8 %collective-permute-done.16.after_ref = bf16[34,256]{1,0:T(8,128)(2,1)S(1)} collective-permute-done((bf16[34,256]{1,0:T(8,128)(2,1)S(1)}, bf16[34,256]{1,0:T(8,128)(2,1)S(1)}, u32[]{:S(2)}, u32[]{:S(2)}) %collective-permute-start.16) | collective-permute-done | bytes 17440 | tf_op jit(solution)/shard_map/ppermute | solution.py:383
  61.3 2.7 %collective-permute-start.21 = (bf16[288,256]{1,0:T(8,128)(2,1)S(1)}, bf16[288,256]{1,0:T(8,128)(2,1)S(1)}, u32[]{:S(2)}, u32[]{:S(2)}) collective-permute-start(bf16[288,256]{1,0:T(8,128)(2,1)S(1)} %get-tuple-element.64), channel_id=1, source_target_pairs={{0,96},{32,0},{64,32},{96,64},{1,97},{33,1},{65,33},{97,65},{2,98}... | collective-permute-start | bytes 442376 | tf_op jit(solution)/shard_map/ppermute | solution.py:19
  64.7 1.7 %grad_first.5.refs_1_ = f32[768,768]{1,0:T(8,128)S(1)} custom-call(bf16[4,40,32,768]{3,2,1,0:T(8,128)(2,1)S(1)} %spread.1.wide_ref, bf16[32,32,256]{2,1,0:T(8,128)(2,1)S(1)} %collective-permute-done.13.refs_0_, f32[768,768]{1,0:T(8,128)S(1)} %grad_first.4.refs_1_), custom_call_target="tpu_custom_call" | custom-call | flops 1 | bytes 1 | tf_op jit(solution)/shard_map/grad_first/pallas_call | solution.py:176
  66.5 1.7 %grad_first.6.refs_2_ = f32[768,768]{1,0:T(8,128)S(1)} custom-call(bf16[4,40,32,768]{3,2,1,0:T(8,128)(2,1)S(1)} %spread.1.wide_ref, bf16[32,32,256]{2,1,0:T(8,128)(2,1)S(1)} %collective-permute-done.14.refs_0_, f32[768,768]{1,0:T(8,128)S(1)} %grad_first.5.refs_1_), custom_call_target="tpu_custom_call" | custom-call | flops 1 | bytes 1 | tf_op jit(solution)/shard_map/grad_first/pallas_call | solution.py:176
  68.3 1.8 %grad_first.7 = (f32[384,768]{1,0:T(8,128)S(1)}, bf16[384,768]{1,0:T(8,128)(2,1)S(1)}) custom-call(bf16[4,40,32,768]{3,2,1,0:T(8,128)(2,1)S(1)} %spread.1.wide_ref, bf16[16,32,256]{2,1,0:T(8,128)(2,1)S(1)} %collective-permute-done.17.refs_0_, bf16[16,32,256]{2,1,0:T(8,128)(2,1)S(1)} %collective-permute-done.18.refs_1_, f32[768,768]{1,0:T(8,128)S(1)} %grad_first.6.refs_2_), custom_call_target="tpu_custom_call" | custom-call | flops 1 | bytes 1 | tf_op jit(solution)/shard_map/grad_first/pallas_call | solution.py:176
  70.0 2.2 %collective-permute-done.20.a_ref = bf16[288,256]{1,0:T(8,128)(2,1)S(1)} collective-permute-done((bf16[288,256]{1,0:T(8,128)(2,1)S(1)}, bf16[288,256]{1,0:T(8,128)(2,1)S(1)}, u32[]{:S(2)}, u32[]{:S(2)}) %collective-permute-start.20) | collective-permute-done | bytes 147488 | tf_op jit(solution)/shard_map/ppermute | solution.py:19
  72.8 4.1 %collective-permute-start.23 = (bf16[384,768]{1,0:T(8,128)(2,1)S(1)}, bf16[384,768]{1,0:T(8,128)(2,1)S(1)}, u32[]{:S(2)}, u32[]{:S(2)}) collective-permute-start(bf16[384,768]{1,0:T(8,128)(2,1)S(1)} %get-tuple-element.66), channel_id=1, source_target_pairs={{0,16},{16,0},{1,17},{17,1},{2,18},{18,2},{3,19},{19,3},{4,20},{20... | collective-permute-start | bytes 1769480 | tf_op jit(solution)/shard_map/ppermute | solution.py:19
  76.9 1.6 %collective-permute-done.23.far_ref = bf16[384,768]{1,0:T(8,128)(2,1)S(1)} collective-permute-done((bf16[384,768]{1,0:T(8,128)(2,1)S(1)}, bf16[384,768]{1,0:T(8,128)(2,1)S(1)}, u32[]{:S(2)}, u32[]{:S(2)}) %collective-permute-start.23) | collective-permute-done | bytes 589856 | tf_op jit(solution)/shard_map/ppermute | solution.py:19
  78.7 27.1 %all_to_all.5.in_ref = bf16[16,90,256]{2,1,0:T(8,128)(2,1)S(1)} all-to-all(bf16[16,90,256]{2,1,0:T(8,128)(2,1)S(1)} %join.1), channel_id=1, replica_groups=mesh['y'=4,'c'=2,'z'=4,'x'=4] {'z','x'}, dimensions={0} | all-to-all | bytes 1474560 | tf_op jit(solution)/shard_map/all_to_all | solution.py:639
  108.1 2.4 %collective-permute-done.26.d_ref = bf16[90,256]{1,0:T(8,128)(2,1)S(1)} collective-permute-done((bf16[90,256]{1,0:T(8,128)(2,1)S(1)}, bf16[90,256]{1,0:T(8,128)(2,1)S(1)}, u32[]{:S(2)}, u32[]{:S(2)}) %collective-permute-start.26) | collective-permute-done | bytes 46112 | tf_op jit(solution)/shard_map/ppermute | solution.py:19
  111.4 2.7 %collective-permute-start.29 = (bf16[360,256]{1,0:T(8,128)(2,1)S(1)}, bf16[360,256]{1,0:T(8,128)(2,1)S(1)}, u32[]{:S(2)}, u32[]{:S(2)}) collective-permute-start(bf16[360,256]{1,0:T(8,128)(2,1)S(1)} %order_pieces.1.a_ref), channel_id=1, source_target_pairs={{0,2},{1,3},{2,0},{3,1},{4,6},{5,7},{6,4},{7,5},{8,10},{9,11},{10,... | collective-permute-start | bytes 552968 | tf_op jit(solution)/shard_map/ppermute | solution.py:19
  115.6 2.2 %features.1 = bf16[32,32,256]{2,1,0:T(8,128)(2,1)} custom-call(bf16[34,32,256]{2,1,0:T(8,128)(2,1)S(1)} %get-tuple-element.59.hid_ref, bf16[34,256]{1,0:T(8,128)(2,1)S(1)} %collective-permute-done.15.before_ref, bf16[34,256]{1,0:T(8,128)(2,1)S(1)} %collective-permute-done.16.after_ref, bf16[2304,256]{1,0:T(8,128)(2,1)S(1)} %bitcast.47), custom_call_target="tpu_custom_call" | custom-call | flops 1 | bytes 1 | tf_op jit(solution)/shard_map/features/pallas_call | solution.py:298
  120.4 1.5 %collective-permute-start.30 = (bf16[4,72,256]{2,1,0:T(8,128)(2,1)S(1)}, bf16[4,72,256]{2,1,0:T(8,128)(2,1)S(1)}, u32[]{:S(2)}, u32[]{:S(2)}) collective-permute-start(bf16[4,72,256]{2,1,0:T(8,128)(2,1)S(1)} %pick_rows.1), channel_id=1, source_target_pairs={{0,32},{32,64},{64,96},{96,0},{1,33},{33,65},{65,97},{97,1},{2,34}... | collective-permute-start | bytes 442376 | tf_op jit(solution)/shard_map/ppermute | solution.py:19
  122.9 2.6 %collective-permute-done.32 = bf16[4,72,256]{2,1,0:T(8,128)(2,1)S(1)} collective-permute-done((bf16[4,72,256]{2,1,0:T(8,128)(2,1)S(1)}, bf16[4,72,256]{2,1,0:T(8,128)(2,1)S(1)}, u32[]{:S(2)}, u32[]{:S(2)}) %collective-permute-start.32) | collective-permute-done | bytes 147488 | tf_op jit(solution)/shard_map/ppermute | solution.py:19
  125.6 1.5 %collective-permute-done.30 = bf16[4,72,256]{2,1,0:T(8,128)(2,1)S(1)} collective-permute-done((bf16[4,72,256]{2,1,0:T(8,128)(2,1)S(1)}, bf16[4,72,256]{2,1,0:T(8,128)(2,1)S(1)}, u32[]{:S(2)}, u32[]{:S(2)}) %collective-permute-start.30) | collective-permute-done | bytes 147488 | tf_op jit(solution)/shard_map/ppermute | solution.py:19
  127.1 6.5 %collective-permute-start.33 = (bf16[4,4,72,256]{3,2,1,0:T(8,128)(2,1)S(1)}, bf16[4,4,72,256]{3,2,1,0:T(8,128)(2,1)S(1)}, u32[]{:S(2)}, u32[]{:S(2)}) collective-permute-start(bf16[4,4,72,256]{3,2,1,0:T(8,128)(2,1)S(1)} %pad_maximum_fusion.1.in_ref), channel_id=1, source_target_pairs={{0,16},{16,0},{1,17},{17,1},{2,18},{18,2},{3,19},{19,3},{4,20},{20... | collective-permute-start | bytes 1769480 | tf_op jit(solution)/shard_map/ppermute | solution.py:19
  (82 shorter events, 29.5 us)
Async XLA Ops:
  0.6 13.7 %collective-permute-start = (bf16[256,32,128]{2,1,0:T(8,128)(2,1)}, bf16[256,32,128]{2,1,0:T(8,128)(2,1)S(1)}, u32[]{:S(2)}, u32[]{:S(2)}) collective-permute-start(bf16[256,32,128]{2,1,0:T(8,128)(2,1)} %own_ref.1), channel_id=1, source_target_pairs={{0,16},{16,0},{1,17},{17,1},{2,18},{18,2},{3,19},{19,3},{4,20},{20... | collective-permute-start | bytes 6291464 | tf_op jit(solution)/shard_map/ppermute | solution.py:19
  4.6 6.6 %collective-permute-start.2 = (bf16[320,128]{1,0:T(8,128)(2,1)S(1)}, bf16[320,128]{1,0:T(8,128)(2,1)S(1)}, u32[]{:S(2)}, u32[]{:S(2)}) collective-permute-start(bf16[320,128]{1,0:T(8,128)(2,1)S(1)} %pad_maximum_fusion.4), channel_id=1, source_target_pairs={{1,0},{2,1},{3,2},{4,3},{5,4},{6,5},{7,6},{8,7},{9,8},{10,9},{11,1... | collective-permute-start | bytes 245768 | tf_op jit(solution)/shard_map/ppermute | solution.py:383
  5.9 7.3 %collective-permute-start.4 = (bf16[3,3,128,256]{3,2,1,0:T(8,128)(2,1)}, bf16[3,3,128,256]{3,2,1,0:T(8,128)(2,1)S(1)}, u32[]{:S(2)}, u32[]{:S(2)}) collective-permute-start(bf16[3,3,128,256]{3,2,1,0:T(8,128)(2,1)} %param.5), channel_id=1, source_target_pairs={{0,16},{16,0},{1,17},{17,1},{2,18},{18,2},{3,19},{19,3},{4,20},{20... | collective-permute-start | bytes 1769480 | tf_op jit(solution)/shard_map/ppermute | solution.py:19
  6.2 6.1 %collective-permute-start.1 = (bf16[320,128]{1,0:T(8,128)(2,1)S(1)}, bf16[320,128]{1,0:T(8,128)(2,1)S(1)}, u32[]{:S(2)}, u32[]{:S(2)}) collective-permute-start(bf16[320,128]{1,0:T(8,128)(2,1)S(1)} %pad_maximum_fusion.3), channel_id=1, source_target_pairs={{0,1},{1,2},{2,3},{3,4},{4,5},{5,6},{6,7},{7,8},{8,9},{9,10},{10,1... | collective-permute-start | bytes 245768 | tf_op jit(solution)/shard_map/ppermute | solution.py:383
  17.8 11.9 %collective-permute-start.8 = (bf16[17,32,256]{2,1,0:T(8,128)(2,1)S(1)}, bf16[17,32,256]{2,1,0:T(8,128)(2,1)S(1)}, u32[]{:S(2)}, u32[]{:S(2)}) collective-permute-start(bf16[17,32,256]{2,1,0:T(8,128)(2,1)S(1)} %get-tuple-element.42), channel_id=1, source_target_pairs={{0,96},{32,0},{64,32},{96,64},{1,97},{33,1},{65,33},{97,65},{2,98}... | collective-permute-start | bytes 835592 | tf_op jit(solution)/shard_map/ppermute | solution.py:19
  20.7 9.0 %collective-permute-start.5 = (bf16[17,32,256]{2,1,0:T(8,128)(2,1)S(1)}, bf16[17,32,256]{2,1,0:T(8,128)(2,1)S(1)}, u32[]{:S(2)}, u32[]{:S(2)}) collective-permute-start(bf16[17,32,256]{2,1,0:T(8,128)(2,1)S(1)} %get-tuple-element.40), channel_id=1, source_target_pairs={{0,32},{32,64},{64,96},{96,0},{1,33},{33,65},{65,97},{97,1},{2,34}... | collective-permute-start | bytes 835592 | tf_op jit(solution)/shard_map/ppermute | solution.py:19
  20.7 8.8 %collective-permute-start.6 = (bf16[34,256]{1,0:T(8,128)(2,1)S(1)}, bf16[34,256]{1,0:T(8,128)(2,1)S(1)}, u32[]{:S(2)}, u32[]{:S(2)}) collective-permute-start(bf16[34,256]{1,0:T(8,128)(2,1)S(1)} %maximum_maximum_fusion), channel_id=1, source_target_pairs={{0,16},{16,32},{32,48},{48,64},{64,80},{80,96},{96,112},{1,17},{17... | collective-permute-start | bytes 52232 | tf_op jit(solution)/shard_map/ppermute | solution.py:602
  23.3 6.2 %collective-permute-start.7 = (bf16[34,256]{1,0:T(8,128)(2,1)S(1)}, bf16[34,256]{1,0:T(8,128)(2,1)S(1)}, u32[]{:S(2)}, u32[]{:S(2)}) collective-permute-start(bf16[34,256]{1,0:T(8,128)(2,1)S(1)} %maximum_maximum_fusion.1), channel_id=1, source_target_pairs={{16,0},{32,16},{48,32},{64,48},{80,64},{96,80},{112,96},{17,1},{33... | collective-permute-start | bytes 52232 | tf_op jit(solution)/shard_map/ppermute | solution.py:603
  26.7 10.2 %collective-permute-start.10 = (bf16[17,32,256]{2,1,0:T(8,128)(2,1)S(1)}, bf16[17,32,256]{2,1,0:T(8,128)(2,1)S(1)}, u32[]{:S(2)}, u32[]{:S(2)}) collective-permute-start(bf16[17,32,256]{2,1,0:T(8,128)(2,1)S(1)} %get-tuple-element.45), channel_id=1, source_target_pairs={{0,96},{32,0},{64,32},{96,64},{1,97},{33,1},{65,33},{97,65},{2,98}... | collective-permute-start | bytes 835592 | tf_op jit(solution)/shard_map/ppermute | solution.py:19
  29.5 7.3 %collective-permute-start.11 = (bf16[17,32,256]{2,1,0:T(8,128)(2,1)S(1)}, bf16[17,32,256]{2,1,0:T(8,128)(2,1)S(1)}, u32[]{:S(2)}, u32[]{:S(2)}) collective-permute-start(bf16[17,32,256]{2,1,0:T(8,128)(2,1)S(1)} %get-tuple-element.46), channel_id=1, source_target_pairs={{0,32},{32,64},{64,96},{96,0},{1,33},{33,65},{65,97},{97,1},{2,34}... | collective-permute-start | bytes 835592 | tf_op jit(solution)/shard_map/ppermute | solution.py:19
  31.1 11.7 %collective-permute-start.9 = (bf16[17,32,256]{2,1,0:T(8,128)(2,1)S(1)}, bf16[17,32,256]{2,1,0:T(8,128)(2,1)S(1)}, u32[]{:S(2)}, u32[]{:S(2)}) collective-permute-start(bf16[17,32,256]{2,1,0:T(8,128)(2,1)S(1)} %get-tuple-element.43), channel_id=1, source_target_pairs={{0,32},{32,64},{64,96},{96,0},{1,33},{33,65},{65,97},{97,1},{2,34}... | collective-permute-start | bytes 835592 | tf_op jit(solution)/shard_map/ppermute | solution.py:19
  31.9 10.9 %collective-permute-start.12 = (bf16[17,32,256]{2,1,0:T(8,128)(2,1)S(1)}, bf16[17,32,256]{2,1,0:T(8,128)(2,1)S(1)}, u32[]{:S(2)}, u32[]{:S(2)}) collective-permute-start(bf16[17,32,256]{2,1,0:T(8,128)(2,1)S(1)} %get-tuple-element.47), channel_id=1, source_target_pairs={{0,96},{32,0},{64,32},{96,64},{1,97},{33,1},{65,33},{97,65},{2,98}... | collective-permute-start | bytes 835592 | tf_op jit(solution)/shard_map/ppermute | solution.py:19
  43.3 16.1 %collective-permute-start.14 = (bf16[32,32,256]{2,1,0:T(8,128)(2,1)S(1)}, bf16[32,32,256]{2,1,0:T(8,128)(2,1)S(1)}, u32[]{:S(2)}, u32[]{:S(2)}) collective-permute-start(bf16[32,32,256]{2,1,0:T(8,128)(2,1)S(1)} %get-tuple-element.51.refs_0_), channel_id=1, source_target_pairs={{0,96},{32,0},{64,32},{96,64},{1,97},{33,1},{65,33},{97,65},{2,98}... | collective-permute-start | bytes 1572872 | tf_op jit(solution)/shard_map/ppermute | solution.py:19
  45.2 14.3 %collective-permute-start.13 = (bf16[32,32,256]{2,1,0:T(8,128)(2,1)S(1)}, bf16[32,32,256]{2,1,0:T(8,128)(2,1)S(1)}, u32[]{:S(2)}, u32[]{:S(2)}) collective-permute-start(bf16[32,32,256]{2,1,0:T(8,128)(2,1)S(1)} %get-tuple-element.51.refs_0_), channel_id=1, source_target_pairs={{0,32},{32,64},{64,96},{96,0},{1,33},{33,65},{65,97},{97,1},{2,34}... | collective-permute-start | bytes 1572872 | tf_op jit(solution)/shard_map/ppermute | solution.py:19
  47.1 14.0 %collective-permute-start.19 = (bf16[4,288,256]{2,1,0:T(8,128)(2,1)S(1)}, bf16[4,288,256]{2,1,0:T(8,128)(2,1)S(1)}, u32[]{:S(2)}, u32[]{:S(2)}) collective-permute-start(bf16[4,288,256]{2,1,0:T(8,128)(2,1)S(1)} %get-tuple-element.62), channel_id=1, source_target_pairs={{0,16},{16,0},{1,17},{17,1},{2,18},{18,2},{3,19},{19,3},{4,20},{20... | collective-permute-start | bytes 1769480 | tf_op jit(solution)/shard_map/ppermute | solution.py:19
  50.4 7.4 %collective-permute-start.15 = (bf16[34,256]{1,0:T(8,128)(2,1)S(1)}, bf16[34,256]{1,0:T(8,128)(2,1)S(1)}, u32[]{:S(2)}, u32[]{:S(2)}) collective-permute-start(bf16[34,256]{1,0:T(8,128)(2,1)S(1)} %get-tuple-element.52), channel_id=1, source_target_pairs={{0,1},{1,2},{2,3},{3,4},{4,5},{5,6},{6,7},{7,8},{8,9},{9,10},{10,1... | collective-permute-start | bytes 52232 | tf_op jit(solution)/shard_map/ppermute | solution.py:383
  54.7 4.8 %collective-permute-start.16 = (bf16[34,256]{1,0:T(8,128)(2,1)S(1)}, bf16[34,256]{1,0:T(8,128)(2,1)S(1)}, u32[]{:S(2)}, u32[]{:S(2)}) collective-permute-start(bf16[34,256]{1,0:T(8,128)(2,1)S(1)} %get-tuple-element.53), channel_id=1, source_target_pairs={{1,0},{2,1},{3,2},{4,3},{5,4},{6,5},{7,6},{8,7},{9,8},{10,9},{11,1... | collective-permute-start | bytes 52232 | tf_op jit(solution)/shard_map/ppermute | solution.py:383
  59.5 8.7 %collective-permute-start.18 = (bf16[16,32,256]{2,1,0:T(8,128)(2,1)S(1)}, bf16[16,32,256]{2,1,0:T(8,128)(2,1)S(1)}, u32[]{:S(2)}, u32[]{:S(2)}) collective-permute-start(bf16[16,32,256]{2,1,0:T(8,128)(2,1)S(1)} %slice.71), channel_id=1, source_target_pairs={{0,96},{32,0},{64,32},{96,64},{1,97},{33,1},{65,33},{97,65},{2,98}... | collective-permute-start | bytes 786440 | tf_op jit(solution)/shard_map/ppermute | solution.py:19
  60.7 7.6 %collective-permute-start.17 = (bf16[16,32,256]{2,1,0:T(8,128)(2,1)S(1)}, bf16[16,32,256]{2,1,0:T(8,128)(2,1)S(1)}, u32[]{:S(2)}, u32[]{:S(2)}) collective-permute-start(bf16[16,32,256]{2,1,0:T(8,128)(2,1)S(1)} %slice.70), channel_id=1, source_target_pairs={{0,32},{32,64},{64,96},{96,0},{1,33},{33,65},{65,97},{97,1},{2,34}... | collective-permute-start | bytes 786440 | tf_op jit(solution)/shard_map/ppermute | solution.py:19
  61.2 11.0 %collective-permute-start.20 = (bf16[288,256]{1,0:T(8,128)(2,1)S(1)}, bf16[288,256]{1,0:T(8,128)(2,1)S(1)}, u32[]{:S(2)}, u32[]{:S(2)}) collective-permute-start(bf16[288,256]{1,0:T(8,128)(2,1)S(1)} %get-tuple-element.63), channel_id=1, source_target_pairs={{0,32},{32,64},{64,96},{96,0},{1,33},{33,65},{65,97},{97,1},{2,34}... | collective-permute-start | bytes 442376 | tf_op jit(solution)/shard_map/ppermute | solution.py:19
  61.3 10.9 %collective-permute-start.21 = (bf16[288,256]{1,0:T(8,128)(2,1)S(1)}, bf16[288,256]{1,0:T(8,128)(2,1)S(1)}, u32[]{:S(2)}, u32[]{:S(2)}) collective-permute-start(bf16[288,256]{1,0:T(8,128)(2,1)S(1)} %get-tuple-element.64), channel_id=1, source_target_pairs={{0,96},{32,0},{64,32},{96,64},{1,97},{33,1},{65,33},{97,65},{2,98}... | collective-permute-start | bytes 442376 | tf_op jit(solution)/shard_map/ppermute | solution.py:19
  64.0 8.9 %collective-permute-start.22 = (bf16[288,256]{1,0:T(8,128)(2,1)S(1)}, bf16[288,256]{1,0:T(8,128)(2,1)S(1)}, u32[]{:S(2)}, u32[]{:S(2)}) collective-permute-start(bf16[288,256]{1,0:T(8,128)(2,1)S(1)} %get-tuple-element.65), channel_id=1, source_target_pairs={{0,64},{32,96},{64,0},{96,32},{1,65},{33,97},{65,1},{97,33},{2,66}... | collective-permute-start | bytes 442376 | tf_op jit(solution)/shard_map/ppermute | solution.py:19
  72.8 5.7 %collective-permute-start.23 = (bf16[384,768]{1,0:T(8,128)(2,1)S(1)}, bf16[384,768]{1,0:T(8,128)(2,1)S(1)}, u32[]{:S(2)}, u32[]{:S(2)}) collective-permute-start(bf16[384,768]{1,0:T(8,128)(2,1)S(1)} %get-tuple-element.66), channel_id=1, source_target_pairs={{0,16},{16,0},{1,17},{17,1},{2,18},{18,2},{3,19},{19,3},{4,20},{20... | collective-permute-start | bytes 1769480 | tf_op jit(solution)/shard_map/ppermute | solution.py:19
  106.0 4.5 %collective-permute-start.26 = (bf16[90,256]{1,0:T(8,128)(2,1)S(1)}, bf16[90,256]{1,0:T(8,128)(2,1)S(1)}, u32[]{:S(2)}, u32[]{:S(2)}) collective-permute-start(bf16[90,256]{1,0:T(8,128)(2,1)S(1)} %sum_pieces.1.a_ref), channel_id=1, source_target_pairs={{0,8},{4,12},{8,0},{12,4},{1,9},{5,13},{9,1},{13,5},{2,10},{6,14},... | collective-permute-start | bytes 138248 | tf_op jit(solution)/shard_map/ppermute | solution.py:19
  107.2 4.2 %collective-permute-start.24 = (bf16[90,256]{1,0:T(8,128)(2,1)S(1)}, bf16[90,256]{1,0:T(8,128)(2,1)S(1)}, u32[]{:S(2)}, u32[]{:S(2)}) collective-permute-start(bf16[90,256]{1,0:T(8,128)(2,1)S(1)} %sum_pieces.1.a_ref), channel_id=1, source_target_pairs={{0,4},{4,8},{8,12},{12,0},{1,5},{5,9},{9,13},{13,1},{2,6},{6,10},{... | collective-permute-start | bytes 138248 | tf_op jit(solution)/shard_map/ppermute | solution.py:19
  111.4 6.4 %collective-permute-start.29 = (bf16[360,256]{1,0:T(8,128)(2,1)S(1)}, bf16[360,256]{1,0:T(8,128)(2,1)S(1)}, u32[]{:S(2)}, u32[]{:S(2)}) collective-permute-start(bf16[360,256]{1,0:T(8,128)(2,1)S(1)} %order_pieces.1.a_ref), channel_id=1, source_target_pairs={{0,2},{1,3},{2,0},{3,1},{4,6},{5,7},{6,4},{7,5},{8,10},{9,11},{10,... | collective-permute-start | bytes 552968 | tf_op jit(solution)/shard_map/ppermute | solution.py:19
  114.2 5.1 %collective-permute-start.28 = (bf16[360,256]{1,0:T(8,128)(2,1)S(1)}, bf16[360,256]{1,0:T(8,128)(2,1)S(1)}, u32[]{:S(2)}, u32[]{:S(2)}) collective-permute-start(bf16[360,256]{1,0:T(8,128)(2,1)S(1)} %order_pieces.1.a_ref), channel_id=1, source_target_pairs={{0,3},{1,0},{2,1},{3,2},{4,7},{5,4},{6,5},{7,6},{8,11},{9,8},{10,9... | collective-permute-start | bytes 552968 | tf_op jit(solution)/shard_map/ppermute | solution.py:19
  114.3 5.6 %collective-permute-start.27 = (bf16[360,256]{1,0:T(8,128)(2,1)S(1)}, bf16[360,256]{1,0:T(8,128)(2,1)S(1)}, u32[]{:S(2)}, u32[]{:S(2)}) collective-permute-start(bf16[360,256]{1,0:T(8,128)(2,1)S(1)} %order_pieces.1.a_ref), channel_id=1, source_target_pairs={{0,1},{1,2},{2,3},{3,0},{4,5},{5,6},{6,7},{7,4},{8,9},{9,10},{10,1... | collective-permute-start | bytes 552968 | tf_op jit(solution)/shard_map/ppermute | solution.py:19
  119.9 5.7 %collective-permute-start.32 = (bf16[4,72,256]{2,1,0:T(8,128)(2,1)S(1)}, bf16[4,72,256]{2,1,0:T(8,128)(2,1)S(1)}, u32[]{:S(2)}, u32[]{:S(2)}) collective-permute-start(bf16[4,72,256]{2,1,0:T(8,128)(2,1)S(1)} %pick_rows.1), channel_id=1, source_target_pairs={{0,64},{32,96},{64,0},{96,32},{1,65},{33,97},{65,1},{97,33},{2,66}... | collective-permute-start | bytes 442376 | tf_op jit(solution)/shard_map/ppermute | solution.py:19
  120.3 5.2 %collective-permute-start.31 = (bf16[4,72,256]{2,1,0:T(8,128)(2,1)S(1)}, bf16[4,72,256]{2,1,0:T(8,128)(2,1)S(1)}, u32[]{:S(2)}, u32[]{:S(2)}) collective-permute-start(bf16[4,72,256]{2,1,0:T(8,128)(2,1)S(1)} %pick_rows.1), channel_id=1, source_target_pairs={{0,96},{32,0},{64,32},{96,64},{1,97},{33,1},{65,33},{97,65},{2,98}... | collective-permute-start | bytes 442376 | tf_op jit(solution)/shard_map/ppermute | solution.py:19
  120.4 6.7 %collective-permute-start.30 = (bf16[4,72,256]{2,1,0:T(8,128)(2,1)S(1)}, bf16[4,72,256]{2,1,0:T(8,128)(2,1)S(1)}, u32[]{:S(2)}, u32[]{:S(2)}) collective-permute-start(bf16[4,72,256]{2,1,0:T(8,128)(2,1)S(1)} %pick_rows.1), channel_id=1, source_target_pairs={{0,32},{32,64},{64,96},{96,0},{1,33},{33,65},{65,97},{97,1},{2,34}... | collective-permute-start | bytes 442376 | tf_op jit(solution)/shard_map/ppermute | solution.py:19
  127.1 8.2 %collective-permute-start.33 = (bf16[4,4,72,256]{3,2,1,0:T(8,128)(2,1)S(1)}, bf16[4,4,72,256]{3,2,1,0:T(8,128)(2,1)S(1)}, u32[]{:S(2)}, u32[]{:S(2)}) collective-permute-start(bf16[4,4,72,256]{3,2,1,0:T(8,128)(2,1)S(1)} %pad_maximum_fusion.1.in_ref), channel_id=1, source_target_pairs={{0,16},{16,0},{1,17},{17,1},{2,18},{18,2},{3,19},{19,3},{4,20},{20... | collective-permute-start | bytes 1769480 | tf_op jit(solution)/shard_map/ppermute | solution.py:19
  (5 other events, 26.6 us)

commit v13 on v12

--- a/solution.py
+++ b/solution.py
@@ -620,12 +620,9 @@
     from_on, from_off = shift(delta, "y", on), shift(delta, "y", off)
     half = strip // 2
     total = grad_strip(0, wide, (delta,), None, False)
-    from_on, from_off, total, *edges = lax.optimization_barrier(
-        (from_on, from_off, total, *row_halo(ends))
-    )
+    from_on, from_off, total = lax.optimization_barrier((from_on, from_off, total))
     fwd_a, fwd_b = shift(from_on[:half], "y", on), shift(from_off[half:], "y", off)
     near, far = second_tile(hidden, wide_cotangent, chips)
-    features = features_tile(hidden, edges, weight_second)
     keep, *sends = fold(near, shift(far, "c", 1))
     got = [shift(send, "y", step) for step, send in zip(STEPS[1:], sends)]
     total = grad_strip(off, wide, (from_on,), total, False)
@@ -638,13 +635,16 @@
     extra = keep.shape[0] // (sx * sz)
     summed = lax.all_to_all(joined, SKY, 0, 0, tiled=True)
     summed = sum_pieces(summed)
+    summed, *ends = lax.optimization_barrier((summed, *ends))
+    edges = row_halo(ends)
     parts = gather_steps(order_pieces(gather_steps(summed, "z"), extra), "x")
     main = parts[0].shape[0] - sz * extra
     grad_first = lay_first(parts, sz, chans)
     share = pick_rows(parts, main)
-    share, features = lax.optimization_barrier((share, features))
-    share, grad_first = lax.optimization_barrier(
-        (jnp.stack(gather_steps(share, "y")), grad_first)
+    share, *edges = lax.optimization_barrier((share, *edges))
+    features = features_tile(hidden, edges, weight_second)
+    share, grad_first, features = lax.optimization_barrier(
+        (jnp.stack(gather_steps(share, "y")), grad_first, features)
     )
     grad_second = lay_second(shift(share, "c", 1), lay_second(share))
     grad_second = grad_second.reshape(3, 3, outs, outs)

time: 137 us -> 134 us (0.978)
  blocking collectives: 27.1 us -> 23.9 us
  waiting for transfers between devices: 23.3 us -> 25.1 us
  starting transfers between devices: 55.8 us -> 54 us
    all_to_all x1, blocking collectives: 27.1 us -> 23.9 us  [body(): summed = lax.all_to_all(joined, SKY, 0, 0, tiled=True)]
    ppermute x4, starting transfers between devices: 11.2 us -> 8.77 us  [row_halo(): return (lax.ppermute(ends[0], SKY, up), lax.ppermute(ends[1], SKY, down))]
  transfers between devices with their start and end apart: 34 -> 34, of which waited for: 14 -> 15; matrix products, arithmetic and copies ran while one was open for 3% -> 3% of each run, Pallas kernels for 14% -> 14%
where the time goes in v13:
time: 134 us; the launch traced here: 133 us
  starting transfers between devices  54 us (40%)
  waiting for transfers between devices  25.1 us (19%)
  Pallas kernels  24.7 us (18%)
  blocking collectives  23.9 us (18%)
  local copies, waits for them, and re-layouts  3.25 us (2%)
    ppermute x28, starting transfers between devices, shift(): lax.ppermute(x, axis, [(i, (i + step) % count) for i in range(count)])  40.8 us
    all_to_all x1, blocking collectives, body(): summed = lax.all_to_all(joined, SKY, 0, 0, tiled=True)  23.9 us
    ppermute x28, waiting for transfers between devices, shift(): lax.ppermute(x, axis, [(i, (i + step) % count) for i in range(count)])  21.3 us
    ppermute x4, starting transfers between devices, row_halo(): return (lax.ppermute(ends[0], SKY, up), lax.ppermute(ends[1], SKY, down))  8.77 us
    pallas_call x4, Pallas kernels, grad_strip(): pl.pallas_call(functools.partial(grad_kernel, step, len(pieces), old is n...  7 us
    pallas_call x4, Pallas kernels, conv_parts(): pl.pallas_call(functools.partial(conv_kernel, parts, len(adds)), out_shap...  5.84 us
    ppermute x4, waiting for transfers between devices, row_halo(): return (lax.ppermute(ends[0], SKY, up), lax.ppermute(ends[1], SKY, down))  3.79 us
  transfers between devices with their start and end apart: 34, of which 15 were waited for; matrix products, arithmetic and copies ran while one was open for 3% of the time, Pallas kernels for 14%

profile of v13, /device:TPU:1, one launch (start us, length us, event | category | flops | bytes accessed | tf_op | source)
XLA Modules:
  0.0 133.4 jit_solution(17881360458319443541)
XLA Ops:
  0.6 1.5 %collective-permute-start = (bf16[256,32,128]{2,1,0:T(8,128)(2,1)}, bf16[256,32,128]{2,1,0:T(8,128)(2,1)S(1)}, u32[]{:S(2)}, u32[]{:S(2)}) collective-permute-start(bf16[256,32,128]{2,1,0:T(8,128)(2,1)} %own_ref.1), channel_id=1, source_target_pairs={{0,16},{16,0},{1,17},{17,1},{2,18},{18,2},{3,19},{19,3},{4,20},{20... | collective-permute-start | bytes 6291464 | tf_op jit(solution)/shard_map/ppermute | solution.py:19
  6.2 4.3 %collective-permute-start.1 = (bf16[320,128]{1,0:T(8,128)(2,1)S(1)}, bf16[320,128]{1,0:T(8,128)(2,1)S(1)}, u32[]{:S(2)}, u32[]{:S(2)}) collective-permute-start(bf16[320,128]{1,0:T(8,128)(2,1)S(1)} %pad_maximum_fusion.3), channel_id=1, source_target_pairs={{0,1},{1,2},{2,3},{3,4},{4,5},{5,6},{6,7},{7,8},{8,9},{9,10},{10,1... | collective-permute-start | bytes 245768 | tf_op jit(solution)/shard_map/ppermute | solution.py:383
  14.4 1.9 %spread.1.wide_ref = bf16[4,40,32,768]{3,2,1,0:T(8,128)(2,1)S(1)} custom-call(bf16[256,32,128]{2,1,0:T(8,128)(2,1)S(1)} %copy-done.1, bf16[256,32,128]{2,1,0:T(8,128)(2,1)S(1)} %collective-permute-done.far_ref, bf16[2,320,128]{2,1,0:T(8,128)(2,1)S(1)} %pad_maximum_fusion.2.own_halo_ref.edge_ref, bf16[2,320,128]{2,1,0:T(8,128)(2,1)S(1)} %collective-permute-done.3.far_halo_ref), custom_call_target="tpu_custom_call" | custom-call | flops 1 | bytes 1 | tf_op jit(solution)/shard_map/spread/pallas_call | solution.py:94
  17.8 2.9 %collective-permute-start.8 = (bf16[17,32,256]{2,1,0:T(8,128)(2,1)S(1)}, bf16[17,32,256]{2,1,0:T(8,128)(2,1)S(1)}, u32[]{:S(2)}, u32[]{:S(2)}) collective-permute-start(bf16[17,32,256]{2,1,0:T(8,128)(2,1)S(1)} %get-tuple-element.45), channel_id=1, source_target_pairs={{0,96},{32,0},{64,32},{96,64},{1,97},{33,1},{65,33},{97,65},{2,98}... | collective-permute-start | bytes 835592 | tf_op jit(solution)/shard_map/ppermute | solution.py:19
  20.7 2.6 %collective-permute-start.6 = (bf16[34,256]{1,0:T(8,128)(2,1)S(1)}, bf16[34,256]{1,0:T(8,128)(2,1)S(1)}, u32[]{:S(2)}, u32[]{:S(2)}) collective-permute-start(bf16[34,256]{1,0:T(8,128)(2,1)S(1)} %maximum_maximum_fusion), channel_id=1, source_target_pairs={{0,16},{16,32},{32,48},{48,64},{64,80},{80,96},{96,112},{1,17},{17... | collective-permute-start | bytes 52232 | tf_op jit(solution)/shard_map/ppermute | solution.py:602
  23.3 1.9 %collective-permute-start.7 = (bf16[34,256]{1,0:T(8,128)(2,1)S(1)}, bf16[34,256]{1,0:T(8,128)(2,1)S(1)}, u32[]{:S(2)}, u32[]{:S(2)}) collective-permute-start(bf16[34,256]{1,0:T(8,128)(2,1)S(1)} %maximum_maximum_fusion.1), channel_id=1, source_target_pairs={{16,0},{32,16},{48,32},{64,48},{80,64},{96,80},{112,96},{17,1},{33... | collective-permute-start | bytes 52232 | tf_op jit(solution)/shard_map/ppermute | solution.py:603
  26.7 2.8 %collective-permute-start.10 = (bf16[17,32,256]{2,1,0:T(8,128)(2,1)S(1)}, bf16[17,32,256]{2,1,0:T(8,128)(2,1)S(1)}, u32[]{:S(2)}, u32[]{:S(2)}) collective-permute-start(bf16[17,32,256]{2,1,0:T(8,128)(2,1)S(1)} %get-tuple-element.48), channel_id=1, source_target_pairs={{0,96},{32,0},{64,32},{96,64},{1,97},{33,1},{65,33},{97,65},{2,98}... | collective-permute-start | bytes 835592 | tf_op jit(solution)/shard_map/ppermute | solution.py:19
  31.9 1.9 %collective-permute-start.12 = (bf16[17,32,256]{2,1,0:T(8,128)(2,1)S(1)}, bf16[17,32,256]{2,1,0:T(8,128)(2,1)S(1)}, u32[]{:S(2)}, u32[]{:S(2)}) collective-permute-start(bf16[17,32,256]{2,1,0:T(8,128)(2,1)S(1)} %get-tuple-element.50), channel_id=1, source_target_pairs={{0,96},{32,0},{64,32},{96,64},{1,97},{33,1},{65,33},{97,65},{2,98}... | collective-permute-start | bytes 835592 | tf_op jit(solution)/shard_map/ppermute | solution.py:19
  33.8 1.5 %conv_first.4.own_ref = f32[34,32,256]{2,1,0:T(8,128)S(1)} custom-call(bf16[4,40,32,768]{3,2,1,0:T(8,128)(2,1)S(1)} %spread.1.wide_ref, bf16[2304,256]{1,0:T(8,128)(2,1)S(1)} %bitcast.46), custom_call_target="tpu_custom_call" | custom-call | flops 1 | bytes 1 | tf_op jit(solution)/shard_map/conv_first/pallas_call | solution.py:125
  35.3 1.5 %back.1 = (f32[32,32,256]{2,1,0:T(8,128)S(1)}, bf16[34,32,768]{2,1,0:T(8,128)(2,1)S(1)}) custom-call(bf16[32,32,256]{2,1,0:T(8,128)(2,1)S(1)} %copy-done.2, bf16[34,256]{1,0:T(8,128)(2,1)S(1)} %collective-permute-done.6.left_ref, bf16[34,256]{1,0:T(8,128)(2,1)S(1)} %collective-permute-done.7.right_ref, ...), custom_call_target="tpu_custom_call" | custom-call | flops 1 | bytes 1 | tf_op jit(solution)/shard_map/back/pallas_call | solution.py:232
  36.8 6.0 %collective-permute-done.9.a0_ref = bf16[17,32,256]{2,1,0:T(8,128)(2,1)S(1)} collective-permute-done((bf16[17,32,256]{2,1,0:T(8,128)(2,1)S(1)}, bf16[17,32,256]{2,1,0:T(8,128)(2,1)S(1)}, u32[]{:S(2)}, u32[]{:S(2)}) %collective-permute-start.9) | collective-permute-done | bytes 278560 | tf_op jit(solution)/shard_map/ppermute | solution.py:19
  43.3 1.8 %collective-permute-start.14 = (bf16[32,32,256]{2,1,0:T(8,128)(2,1)S(1)}, bf16[32,32,256]{2,1,0:T(8,128)(2,1)S(1)}, u32[]{:S(2)}, u32[]{:S(2)}) collective-permute-start(bf16[32,32,256]{2,1,0:T(8,128)(2,1)S(1)} %get-tuple-element.54.refs_0_), channel_id=1, source_target_pairs={{0,96},{32,0},{64,32},{96,64},{1,97},{33,1},{65,33},{97,65},{2,98}... | collective-permute-start | bytes 1572872 | tf_op jit(solution)/shard_map/ppermute | solution.py:19
  45.2 1.9 %second.1 = (f32[4,288,256]{2,1,0:T(8,128)S(1)}, bf16[4,288,256]{2,1,0:T(8,128)(2,1)S(1)}) custom-call(bf16[34,32,256]{2,1,0:T(8,128)(2,1)S(1)} %get-tuple-element.60.hid_ref, bf16[34,32,768]{2,1,0:T(8,128)(2,1)S(1)} %get-tuple-element.61.wide_ref), custom_call_target="tpu_custom_call" | custom-call | flops 1 | bytes 1 | tf_op jit(solution)/shard_map/second/pallas_call | solution.py:271
  47.1 3.5 %collective-permute-start.17 = (bf16[4,288,256]{2,1,0:T(8,128)(2,1)S(1)}, bf16[4,288,256]{2,1,0:T(8,128)(2,1)S(1)}, u32[]{:S(2)}, u32[]{:S(2)}) collective-permute-start(bf16[4,288,256]{2,1,0:T(8,128)(2,1)S(1)} %get-tuple-element.63), channel_id=1, source_target_pairs={{0,16},{16,0},{1,17},{17,1},{2,18},{18,2},{3,19},{19,3},{4,20},{20... | collective-permute-start | bytes 1769480 | tf_op jit(solution)/shard_map/ppermute | solution.py:19
  50.6 1.7 %grad_first.4.refs_1_ = f32[768,768]{1,0:T(8,128)S(1)} custom-call(bf16[4,40,32,768]{3,2,1,0:T(8,128)(2,1)S(1)} %spread.1.wide_ref, bf16[32,32,256]{2,1,0:T(8,128)(2,1)S(1)} %get-tuple-element.54.refs_0_), custom_call_target="tpu_custom_call" | custom-call | flops 1 | bytes 1 | tf_op jit(solution)/shard_map/grad_first/pallas_call | solution.py:176
  52.3 2.8 %collective-permute-done.14.refs_0_ = bf16[32,32,256]{2,1,0:T(8,128)(2,1)S(1)} collective-permute-done((bf16[32,32,256]{2,1,0:T(8,128)(2,1)S(1)}, bf16[32,32,256]{2,1,0:T(8,128)(2,1)S(1)}, u32[]{:S(2)}, u32[]{:S(2)}) %collective-permute-start.14) | collective-permute-done | bytes 524320 | tf_op jit(solution)/shard_map/ppermute | solution.py:19
  55.1 3.1 %collective-permute-done.13.refs_0_ = bf16[32,32,256]{2,1,0:T(8,128)(2,1)S(1)} collective-permute-done((bf16[32,32,256]{2,1,0:T(8,128)(2,1)S(1)}, bf16[32,32,256]{2,1,0:T(8,128)(2,1)S(1)}, u32[]{:S(2)}, u32[]{:S(2)}) %collective-permute-start.13) | collective-permute-done | bytes 524320 | tf_op jit(solution)/shard_map/ppermute | solution.py:19
  60.0 2.7 %collective-permute-start.19 = (bf16[288,256]{1,0:T(8,128)(2,1)S(1)}, bf16[288,256]{1,0:T(8,128)(2,1)S(1)}, u32[]{:S(2)}, u32[]{:S(2)}) collective-permute-start(bf16[288,256]{1,0:T(8,128)(2,1)S(1)} %get-tuple-element.65), channel_id=1, source_target_pairs={{0,96},{32,0},{64,32},{96,64},{1,97},{33,1},{65,33},{97,65},{2,98}... | collective-permute-start | bytes 442376 | tf_op jit(solution)/shard_map/ppermute | solution.py:19
  62.7 1.7 %grad_first.5.refs_1_ = f32[768,768]{1,0:T(8,128)S(1)} custom-call(bf16[4,40,32,768]{3,2,1,0:T(8,128)(2,1)S(1)} %spread.1.wide_ref, bf16[32,32,256]{2,1,0:T(8,128)(2,1)S(1)} %collective-permute-done.13.refs_0_, f32[768,768]{1,0:T(8,128)S(1)} %grad_first.4.refs_1_), custom_call_target="tpu_custom_call" | custom-call | flops 1 | bytes 1 | tf_op jit(solution)/shard_map/grad_first/pallas_call | solution.py:176
  64.4 1.7 %grad_first.6.refs_2_ = f32[768,768]{1,0:T(8,128)S(1)} custom-call(bf16[4,40,32,768]{3,2,1,0:T(8,128)(2,1)S(1)} %spread.1.wide_ref, bf16[32,32,256]{2,1,0:T(8,128)(2,1)S(1)} %collective-permute-done.14.refs_0_, f32[768,768]{1,0:T(8,128)S(1)} %grad_first.5.refs_1_), custom_call_target="tpu_custom_call" | custom-call | flops 1 | bytes 1 | tf_op jit(solution)/shard_map/grad_first/pallas_call | solution.py:176
  66.2 1.8 %grad_first.7 = (f32[384,768]{1,0:T(8,128)S(1)}, bf16[384,768]{1,0:T(8,128)(2,1)S(1)}) custom-call(bf16[4,40,32,768]{3,2,1,0:T(8,128)(2,1)S(1)} %spread.1.wide_ref, bf16[16,32,256]{2,1,0:T(8,128)(2,1)S(1)} %collective-permute-done.15.refs_0_, bf16[16,32,256]{2,1,0:T(8,128)(2,1)S(1)} %collective-permute-done.16.refs_1_, f32[768,768]{1,0:T(8,128)S(1)} %grad_first.6.refs_2_), custom_call_target="tpu_custom_call" | custom-call | flops 1 | bytes 1 | tf_op jit(solution)/shard_map/grad_first/pallas_call | solution.py:176
  70.0 4.9 %collective-permute-start.21 = (bf16[384,768]{1,0:T(8,128)(2,1)S(1)}, bf16[384,768]{1,0:T(8,128)(2,1)S(1)}, u32[]{:S(2)}, u32[]{:S(2)}) collective-permute-start(bf16[384,768]{1,0:T(8,128)(2,1)S(1)} %get-tuple-element.67), channel_id=1, source_target_pairs={{0,16},{16,0},{1,17},{17,1},{2,18},{18,2},{3,19},{19,3},{4,20},{20... | collective-permute-start | bytes 1769480 | tf_op jit(solution)/shard_map/ppermute | solution.py:19
  74.9 1.6 %collective-permute-done.21.far_ref = bf16[384,768]{1,0:T(8,128)(2,1)S(1)} collective-permute-done((bf16[384,768]{1,0:T(8,128)(2,1)S(1)}, bf16[384,768]{1,0:T(8,128)(2,1)S(1)}, u32[]{:S(2)}, u32[]{:S(2)}) %collective-permute-start.21) | collective-permute-done | bytes 589856 | tf_op jit(solution)/shard_map/ppermute | solution.py:19
  76.7 23.9 %all_to_all.5.in_ref = bf16[16,90,256]{2,1,0:T(8,128)(2,1)S(1)} all-to-all(bf16[16,90,256]{2,1,0:T(8,128)(2,1)S(1)} %join.1), channel_id=1, replica_groups=mesh['y'=4,'c'=2,'z'=4,'x'=4] {'z','x'}, dimensions={0} | all-to-all | bytes 1474560 | tf_op jit(solution)/shard_map/all_to_all | solution.py:636
  102.8 2.4 %collective-permute-done.24.d_ref = bf16[90,256]{1,0:T(8,128)(2,1)S(1)} collective-permute-done((bf16[90,256]{1,0:T(8,128)(2,1)S(1)}, bf16[90,256]{1,0:T(8,128)(2,1)S(1)}, u32[]{:S(2)}, u32[]{:S(2)}) %collective-permute-start.24) | collective-permute-done | bytes 46112 | tf_op jit(solution)/shard_map/ppermute | solution.py:19
  106.2 2.7 %collective-permute-start.27 = (bf16[360,256]{1,0:T(8,128)(2,1)S(1)}, bf16[360,256]{1,0:T(8,128)(2,1)S(1)}, u32[]{:S(2)}, u32[]{:S(2)}) collective-permute-start(bf16[360,256]{1,0:T(8,128)(2,1)S(1)} %order_pieces.1.a_ref), channel_id=1, source_target_pairs={{0,2},{1,3},{2,0},{3,1},{4,6},{5,7},{6,4},{7,5},{8,10},{9,11},{10,... | collective-permute-start | bytes 552968 | tf_op jit(solution)/shard_map/ppermute | solution.py:19
  110.4 1.9 %collective-permute-start.28 = (bf16[34,256]{1,0:T(8,128)(2,1)S(1)}, bf16[34,256]{1,0:T(8,128)(2,1)S(1)}, u32[]{:S(2)}, u32[]{:S(2)}) collective-permute-start(bf16[34,256]{1,0:T(8,128)(2,1)S(1)} %get-tuple-element.75), channel_id=1, source_target_pairs={{0,1},{1,2},{2,3},{3,4},{4,5},{5,6},{6,7},{7,8},{8,9},{9,10},{10,1... | collective-permute-start | bytes 52232 | tf_op jit(solution)/shard_map/ppermute | solution.py:383
  114.6 2.8 %collective-permute-done.29.after_ref = bf16[34,256]{1,0:T(8,128)(2,1)S(1)} collective-permute-done((bf16[34,256]{1,0:T(8,128)(2,1)S(1)}, bf16[34,256]{1,0:T(8,128)(2,1)S(1)}, u32[]{:S(2)}, u32[]{:S(2)}) %collective-permute-start.29) | collective-permute-done | bytes 17440 | tf_op jit(solution)/shard_map/ppermute | solution.py:383
  117.4 1.5 %collective-permute-start.32 = (bf16[4,72,256]{2,1,0:T(8,128)(2,1)S(1)}, bf16[4,72,256]{2,1,0:T(8,128)(2,1)S(1)}, u32[]{:S(2)}, u32[]{:S(2)}) collective-permute-start(bf16[4,72,256]{2,1,0:T(8,128)(2,1)S(1)} %pick_rows.1), channel_id=1, source_target_pairs={{0,64},{32,96},{64,0},{96,32},{1,65},{33,97},{65,1},{97,33},{2,66}... | collective-permute-start | bytes 442376 | tf_op jit(solution)/shard_map/ppermute | solution.py:19
  118.8 1.5 %collective-permute-start.30 = (bf16[4,72,256]{2,1,0:T(8,128)(2,1)S(1)}, bf16[4,72,256]{2,1,0:T(8,128)(2,1)S(1)}, u32[]{:S(2)}, u32[]{:S(2)}) collective-permute-start(bf16[4,72,256]{2,1,0:T(8,128)(2,1)S(1)} %pick_rows.1), channel_id=1, source_target_pairs={{0,32},{32,64},{64,96},{96,0},{1,33},{33,65},{65,97},{97,1},{2,34}... | collective-permute-start | bytes 442376 | tf_op jit(solution)/shard_map/ppermute | solution.py:19
  120.3 2.2 %features.1 = bf16[32,32,256]{2,1,0:T(8,128)(2,1)} custom-call(bf16[34,32,256]{2,1,0:T(8,128)(2,1)S(1)} %get-tuple-element.60.hid_ref, bf16[34,256]{1,0:T(8,128)(2,1)S(1)} %collective-permute-done.28.before_ref, bf16[34,256]{1,0:T(8,128)(2,1)S(1)} %collective-permute-done.29.after_ref, bf16[2304,256]{1,0:T(8,128)(2,1)S(1)} %bitcast.47), custom_call_target="tpu_custom_call" | custom-call | flops 1 | bytes 1 | tf_op jit(solution)/shard_map/features/pallas_call | solution.py:298
  124.5 5.9 %collective-permute-start.33 = (bf16[4,4,72,256]{3,2,1,0:T(8,128)(2,1)S(1)}, bf16[4,4,72,256]{3,2,1,0:T(8,128)(2,1)S(1)}, u32[]{:S(2)}, u32[]{:S(2)}) collective-permute-start(bf16[4,4,72,256]{3,2,1,0:T(8,128)(2,1)S(1)} %pad_maximum_fusion.1.in_ref), channel_id=1, source_target_pairs={{0,16},{16,0},{1,17},{17,1},{2,18},{18,2},{3,19},{19,3},{4,20},{20... | collective-permute-start | bytes 1769480 | tf_op jit(solution)/shard_map/ppermute | solution.py:19
  (82 shorter events, 29.5 us)
Async XLA Ops:
  0.6 13.7 %collective-permute-start = (bf16[256,32,128]{2,1,0:T(8,128)(2,1)}, bf16[256,32,128]{2,1,0:T(8,128)(2,1)S(1)}, u32[]{:S(2)}, u32[]{:S(2)}) collective-permute-start(bf16[256,32,128]{2,1,0:T(8,128)(2,1)} %own_ref.1), channel_id=1, source_target_pairs={{0,16},{16,0},{1,17},{17,1},{2,18},{18,2},{3,19},{19,3},{4,20},{20... | collective-permute-start | bytes 6291464 | tf_op jit(solution)/shard_map/ppermute | solution.py:19
  4.6 6.6 %collective-permute-start.2 = (bf16[320,128]{1,0:T(8,128)(2,1)S(1)}, bf16[320,128]{1,0:T(8,128)(2,1)S(1)}, u32[]{:S(2)}, u32[]{:S(2)}) collective-permute-start(bf16[320,128]{1,0:T(8,128)(2,1)S(1)} %pad_maximum_fusion.4), channel_id=1, source_target_pairs={{1,0},{2,1},{3,2},{4,3},{5,4},{6,5},{7,6},{8,7},{9,8},{10,9},{11,1... | collective-permute-start | bytes 245768 | tf_op jit(solution)/shard_map/ppermute | solution.py:383
  5.9 7.3 %collective-permute-start.4 = (bf16[3,3,128,256]{3,2,1,0:T(8,128)(2,1)}, bf16[3,3,128,256]{3,2,1,0:T(8,128)(2,1)S(1)}, u32[]{:S(2)}, u32[]{:S(2)}) collective-permute-start(bf16[3,3,128,256]{3,2,1,0:T(8,128)(2,1)} %param.5), channel_id=1, source_target_pairs={{0,16},{16,0},{1,17},{17,1},{2,18},{18,2},{3,19},{19,3},{4,20},{20... | collective-permute-start | bytes 1769480 | tf_op jit(solution)/shard_map/ppermute | solution.py:19
  6.2 6.1 %collective-permute-start.1 = (bf16[320,128]{1,0:T(8,128)(2,1)S(1)}, bf16[320,128]{1,0:T(8,128)(2,1)S(1)}, u32[]{:S(2)}, u32[]{:S(2)}) collective-permute-start(bf16[320,128]{1,0:T(8,128)(2,1)S(1)} %pad_maximum_fusion.3), channel_id=1, source_target_pairs={{0,1},{1,2},{2,3},{3,4},{4,5},{5,6},{6,7},{7,8},{8,9},{9,10},{10,1... | collective-permute-start | bytes 245768 | tf_op jit(solution)/shard_map/ppermute | solution.py:383
  17.8 11.9 %collective-permute-start.8 = (bf16[17,32,256]{2,1,0:T(8,128)(2,1)S(1)}, bf16[17,32,256]{2,1,0:T(8,128)(2,1)S(1)}, u32[]{:S(2)}, u32[]{:S(2)}) collective-permute-start(bf16[17,32,256]{2,1,0:T(8,128)(2,1)S(1)} %get-tuple-element.45), channel_id=1, source_target_pairs={{0,96},{32,0},{64,32},{96,64},{1,97},{33,1},{65,33},{97,65},{2,98}... | collective-permute-start | bytes 835592 | tf_op jit(solution)/shard_map/ppermute | solution.py:19
  20.7 9.0 %collective-permute-start.5 = (bf16[17,32,256]{2,1,0:T(8,128)(2,1)S(1)}, bf16[17,32,256]{2,1,0:T(8,128)(2,1)S(1)}, u32[]{:S(2)}, u32[]{:S(2)}) collective-permute-start(bf16[17,32,256]{2,1,0:T(8,128)(2,1)S(1)} %get-tuple-element.43), channel_id=1, source_target_pairs={{0,32},{32,64},{64,96},{96,0},{1,33},{33,65},{65,97},{97,1},{2,34}... | collective-permute-start | bytes 835592 | tf_op jit(solution)/shard_map/ppermute | solution.py:19
  20.7 8.8 %collective-permute-start.6 = (bf16[34,256]{1,0:T(8,128)(2,1)S(1)}, bf16[34,256]{1,0:T(8,128)(2,1)S(1)}, u32[]{:S(2)}, u32[]{:S(2)}) collective-permute-start(bf16[34,256]{1,0:T(8,128)(2,1)S(1)} %maximum_maximum_fusion), channel_id=1, source_target_pairs={{0,16},{16,32},{32,48},{48,64},{64,80},{80,96},{96,112},{1,17},{17... | collective-permute-start | bytes 52232 | tf_op jit(solution)/shard_map/ppermute | solution.py:602
  23.3 6.2 %collective-permute-start.7 = (bf16[34,256]{1,0:T(8,128)(2,1)S(1)}, bf16[34,256]{1,0:T(8,128)(2,1)S(1)}, u32[]{:S(2)}, u32[]{:S(2)}) collective-permute-start(bf16[34,256]{1,0:T(8,128)(2,1)S(1)} %maximum_maximum_fusion.1), channel_id=1, source_target_pairs={{16,0},{32,16},{48,32},{64,48},{80,64},{96,80},{112,96},{17,1},{33... | collective-permute-start | bytes 52232 | tf_op jit(solution)/shard_map/ppermute | solution.py:603
  26.7 10.2 %collective-permute-start.10 = (bf16[17,32,256]{2,1,0:T(8,128)(2,1)S(1)}, bf16[17,32,256]{2,1,0:T(8,128)(2,1)S(1)}, u32[]{:S(2)}, u32[]{:S(2)}) collective-permute-start(bf16[17,32,256]{2,1,0:T(8,128)(2,1)S(1)} %get-tuple-element.48), channel_id=1, source_target_pairs={{0,96},{32,0},{64,32},{96,64},{1,97},{33,1},{65,33},{97,65},{2,98}... | collective-permute-start | bytes 835592 | tf_op jit(solution)/shard_map/ppermute | solution.py:19
  29.5 7.3 %collective-permute-start.11 = (bf16[17,32,256]{2,1,0:T(8,128)(2,1)S(1)}, bf16[17,32,256]{2,1,0:T(8,128)(2,1)S(1)}, u32[]{:S(2)}, u32[]{:S(2)}) collective-permute-start(bf16[17,32,256]{2,1,0:T(8,128)(2,1)S(1)} %get-tuple-element.49), channel_id=1, source_target_pairs={{0,32},{32,64},{64,96},{96,0},{1,33},{33,65},{65,97},{97,1},{2,34}... | collective-permute-start | bytes 835592 | tf_op jit(solution)/shard_map/ppermute | solution.py:19
  31.1 11.7 %collective-permute-start.9 = (bf16[17,32,256]{2,1,0:T(8,128)(2,1)S(1)}, bf16[17,32,256]{2,1,0:T(8,128)(2,1)S(1)}, u32[]{:S(2)}, u32[]{:S(2)}) collective-permute-start(bf16[17,32,256]{2,1,0:T(8,128)(2,1)S(1)} %get-tuple-element.46), channel_id=1, source_target_pairs={{0,32},{32,64},{64,96},{96,0},{1,33},{33,65},{65,97},{97,1},{2,34}... | collective-permute-start | bytes 835592 | tf_op jit(solution)/shard_map/ppermute | solution.py:19
  31.9 10.9 %collective-permute-start.12 = (bf16[17,32,256]{2,1,0:T(8,128)(2,1)S(1)}, bf16[17,32,256]{2,1,0:T(8,128)(2,1)S(1)}, u32[]{:S(2)}, u32[]{:S(2)}) collective-permute-start(bf16[17,32,256]{2,1,0:T(8,128)(2,1)S(1)} %get-tuple-element.50), channel_id=1, source_target_pairs={{0,96},{32,0},{64,32},{96,64},{1,97},{33,1},{65,33},{97,65},{2,98}... | collective-permute-start | bytes 835592 | tf_op jit(solution)/shard_map/ppermute | solution.py:19
  43.3 11.7 %collective-permute-start.14 = (bf16[32,32,256]{2,1,0:T(8,128)(2,1)S(1)}, bf16[32,32,256]{2,1,0:T(8,128)(2,1)S(1)}, u32[]{:S(2)}, u32[]{:S(2)}) collective-permute-start(bf16[32,32,256]{2,1,0:T(8,128)(2,1)S(1)} %get-tuple-element.54.refs_0_), channel_id=1, source_target_pairs={{0,96},{32,0},{64,32},{96,64},{1,97},{33,1},{65,33},{97,65},{2,98}... | collective-permute-start | bytes 1572872 | tf_op jit(solution)/shard_map/ppermute | solution.py:19
  45.2 13.0 %collective-permute-start.13 = (bf16[32,32,256]{2,1,0:T(8,128)(2,1)S(1)}, bf16[32,32,256]{2,1,0:T(8,128)(2,1)S(1)}, u32[]{:S(2)}, u32[]{:S(2)}) collective-permute-start(bf16[32,32,256]{2,1,0:T(8,128)(2,1)S(1)} %get-tuple-element.54.refs_0_), channel_id=1, source_target_pairs={{0,32},{32,64},{64,96},{96,0},{1,33},{33,65},{65,97},{97,1},{2,34}... | collective-permute-start | bytes 1572872 | tf_op jit(solution)/shard_map/ppermute | solution.py:19
  47.1 12.7 %collective-permute-start.17 = (bf16[4,288,256]{2,1,0:T(8,128)(2,1)S(1)}, bf16[4,288,256]{2,1,0:T(8,128)(2,1)S(1)}, u32[]{:S(2)}, u32[]{:S(2)}) collective-permute-start(bf16[4,288,256]{2,1,0:T(8,128)(2,1)S(1)} %get-tuple-element.63), channel_id=1, source_target_pairs={{0,16},{16,0},{1,17},{17,1},{2,18},{18,2},{3,19},{19,3},{4,20},{20... | collective-permute-start | bytes 1769480 | tf_op jit(solution)/shard_map/ppermute | solution.py:19
  58.3 7.9 %collective-permute-start.16 = (bf16[16,32,256]{2,1,0:T(8,128)(2,1)S(1)}, bf16[16,32,256]{2,1,0:T(8,128)(2,1)S(1)}, u32[]{:S(2)}, u32[]{:S(2)}) collective-permute-start(bf16[16,32,256]{2,1,0:T(8,128)(2,1)S(1)} %slice.71), channel_id=1, source_target_pairs={{0,96},{32,0},{64,32},{96,64},{1,97},{33,1},{65,33},{97,65},{2,98}... | collective-permute-start | bytes 786440 | tf_op jit(solution)/shard_map/ppermute | solution.py:19
  58.6 7.6 %collective-permute-start.15 = (bf16[16,32,256]{2,1,0:T(8,128)(2,1)S(1)}, bf16[16,32,256]{2,1,0:T(8,128)(2,1)S(1)}, u32[]{:S(2)}, u32[]{:S(2)}) collective-permute-start(bf16[16,32,256]{2,1,0:T(8,128)(2,1)S(1)} %slice.70), channel_id=1, source_target_pairs={{0,32},{32,64},{64,96},{96,0},{1,33},{33,65},{65,97},{97,1},{2,34}... | collective-permute-start | bytes 786440 | tf_op jit(solution)/shard_map/ppermute | solution.py:19
  59.9 9.4 %collective-permute-start.18 = (bf16[288,256]{1,0:T(8,128)(2,1)S(1)}, bf16[288,256]{1,0:T(8,128)(2,1)S(1)}, u32[]{:S(2)}, u32[]{:S(2)}) collective-permute-start(bf16[288,256]{1,0:T(8,128)(2,1)S(1)} %get-tuple-element.64), channel_id=1, source_target_pairs={{0,32},{32,64},{64,96},{96,0},{1,33},{33,65},{65,97},{97,1},{2,34}... | collective-permute-start | bytes 442376 | tf_op jit(solution)/shard_map/ppermute | solution.py:19
  60.0 9.4 %collective-permute-start.19 = (bf16[288,256]{1,0:T(8,128)(2,1)S(1)}, bf16[288,256]{1,0:T(8,128)(2,1)S(1)}, u32[]{:S(2)}, u32[]{:S(2)}) collective-permute-start(bf16[288,256]{1,0:T(8,128)(2,1)S(1)} %get-tuple-element.65), channel_id=1, source_target_pairs={{0,96},{32,0},{64,32},{96,64},{1,97},{33,1},{65,33},{97,65},{2,98}... | collective-permute-start | bytes 442376 | tf_op jit(solution)/shard_map/ppermute | solution.py:19
  62.7 7.3 %collective-permute-start.20 = (bf16[288,256]{1,0:T(8,128)(2,1)S(1)}, bf16[288,256]{1,0:T(8,128)(2,1)S(1)}, u32[]{:S(2)}, u32[]{:S(2)}) collective-permute-start(bf16[288,256]{1,0:T(8,128)(2,1)S(1)} %get-tuple-element.66), channel_id=1, source_target_pairs={{0,64},{32,96},{64,0},{96,32},{1,65},{33,97},{65,1},{97,33},{2,66}... | collective-permute-start | bytes 442376 | tf_op jit(solution)/shard_map/ppermute | solution.py:19
  70.0 6.5 %collective-permute-start.21 = (bf16[384,768]{1,0:T(8,128)(2,1)S(1)}, bf16[384,768]{1,0:T(8,128)(2,1)S(1)}, u32[]{:S(2)}, u32[]{:S(2)}) collective-permute-start(bf16[384,768]{1,0:T(8,128)(2,1)S(1)} %get-tuple-element.67), channel_id=1, source_target_pairs={{0,16},{16,0},{1,17},{17,1},{2,18},{18,2},{3,19},{19,3},{4,20},{20... | collective-permute-start | bytes 1769480 | tf_op jit(solution)/shard_map/ppermute | solution.py:19
  100.7 4.5 %collective-permute-start.24 = (bf16[90,256]{1,0:T(8,128)(2,1)S(1)}, bf16[90,256]{1,0:T(8,128)(2,1)S(1)}, u32[]{:S(2)}, u32[]{:S(2)}) collective-permute-start(bf16[90,256]{1,0:T(8,128)(2,1)S(1)} %sum_pieces.1.a_ref), channel_id=1, source_target_pairs={{0,8},{4,12},{8,0},{12,4},{1,9},{5,13},{9,1},{13,5},{2,10},{6,14},... | collective-permute-start | bytes 138248 | tf_op jit(solution)/shard_map/ppermute | solution.py:19
  101.9 4.2 %collective-permute-start.22 = (bf16[90,256]{1,0:T(8,128)(2,1)S(1)}, bf16[90,256]{1,0:T(8,128)(2,1)S(1)}, u32[]{:S(2)}, u32[]{:S(2)}) collective-permute-start(bf16[90,256]{1,0:T(8,128)(2,1)S(1)} %sum_pieces.1.a_ref), channel_id=1, source_target_pairs={{0,4},{4,8},{8,12},{12,0},{1,5},{5,9},{9,13},{13,1},{2,6},{6,10},{... | collective-permute-start | bytes 138248 | tf_op jit(solution)/shard_map/ppermute | solution.py:19
  106.2 7.4 %collective-permute-start.27 = (bf16[360,256]{1,0:T(8,128)(2,1)S(1)}, bf16[360,256]{1,0:T(8,128)(2,1)S(1)}, u32[]{:S(2)}, u32[]{:S(2)}) collective-permute-start(bf16[360,256]{1,0:T(8,128)(2,1)S(1)} %order_pieces.1.a_ref), channel_id=1, source_target_pairs={{0,2},{1,3},{2,0},{3,1},{4,6},{5,7},{6,4},{7,5},{8,10},{9,11},{10,... | collective-permute-start | bytes 552968 | tf_op jit(solution)/shard_map/ppermute | solution.py:19
  108.9 5.1 %collective-permute-start.26 = (bf16[360,256]{1,0:T(8,128)(2,1)S(1)}, bf16[360,256]{1,0:T(8,128)(2,1)S(1)}, u32[]{:S(2)}, u32[]{:S(2)}) collective-permute-start(bf16[360,256]{1,0:T(8,128)(2,1)S(1)} %order_pieces.1.a_ref), channel_id=1, source_target_pairs={{0,3},{1,0},{2,1},{3,2},{4,7},{5,4},{6,5},{7,6},{8,11},{9,8},{10,9... | collective-permute-start | bytes 552968 | tf_op jit(solution)/shard_map/ppermute | solution.py:19
  109.0 5.6 %collective-permute-start.25 = (bf16[360,256]{1,0:T(8,128)(2,1)S(1)}, bf16[360,256]{1,0:T(8,128)(2,1)S(1)}, u32[]{:S(2)}, u32[]{:S(2)}) collective-permute-start(bf16[360,256]{1,0:T(8,128)(2,1)S(1)} %order_pieces.1.a_ref), channel_id=1, source_target_pairs={{0,1},{1,2},{2,3},{3,0},{4,5},{5,6},{6,7},{7,4},{8,9},{9,10},{10,1... | collective-permute-start | bytes 552968 | tf_op jit(solution)/shard_map/ppermute | solution.py:19
  110.4 4.2 %collective-permute-start.28 = (bf16[34,256]{1,0:T(8,128)(2,1)S(1)}, bf16[34,256]{1,0:T(8,128)(2,1)S(1)}, u32[]{:S(2)}, u32[]{:S(2)}) collective-permute-start(bf16[34,256]{1,0:T(8,128)(2,1)S(1)} %get-tuple-element.75), channel_id=1, source_target_pairs={{0,1},{1,2},{2,3},{3,4},{4,5},{5,6},{6,7},{7,8},{8,9},{9,10},{10,1... | collective-permute-start | bytes 52232 | tf_op jit(solution)/shard_map/ppermute | solution.py:383
  112.3 5.1 %collective-permute-start.29 = (bf16[34,256]{1,0:T(8,128)(2,1)S(1)}, bf16[34,256]{1,0:T(8,128)(2,1)S(1)}, u32[]{:S(2)}, u32[]{:S(2)}) collective-permute-start(bf16[34,256]{1,0:T(8,128)(2,1)S(1)} %get-tuple-element.76), channel_id=1, source_target_pairs={{1,0},{2,1},{3,2},{4,3},{5,4},{6,5},{7,6},{8,7},{9,8},{10,9},{11,1... | collective-permute-start | bytes 52232 | tf_op jit(solution)/shard_map/ppermute | solution.py:383
  117.4 6.2 %collective-permute-start.32 = (bf16[4,72,256]{2,1,0:T(8,128)(2,1)S(1)}, bf16[4,72,256]{2,1,0:T(8,128)(2,1)S(1)}, u32[]{:S(2)}, u32[]{:S(2)}) collective-permute-start(bf16[4,72,256]{2,1,0:T(8,128)(2,1)S(1)} %pick_rows.1), channel_id=1, source_target_pairs={{0,64},{32,96},{64,0},{96,32},{1,65},{33,97},{65,1},{97,33},{2,66}... | collective-permute-start | bytes 442376 | tf_op jit(solution)/shard_map/ppermute | solution.py:19
  118.8 4.8 %collective-permute-start.31 = (bf16[4,72,256]{2,1,0:T(8,128)(2,1)S(1)}, bf16[4,72,256]{2,1,0:T(8,128)(2,1)S(1)}, u32[]{:S(2)}, u32[]{:S(2)}) collective-permute-start(bf16[4,72,256]{2,1,0:T(8,128)(2,1)S(1)} %pick_rows.1), channel_id=1, source_target_pairs={{0,96},{32,0},{64,32},{96,64},{1,97},{33,1},{65,33},{97,65},{2,98}... | collective-permute-start | bytes 442376 | tf_op jit(solution)/shard_map/ppermute | solution.py:19
  118.8 5.6 %collective-permute-start.30 = (bf16[4,72,256]{2,1,0:T(8,128)(2,1)S(1)}, bf16[4,72,256]{2,1,0:T(8,128)(2,1)S(1)}, u32[]{:S(2)}, u32[]{:S(2)}) collective-permute-start(bf16[4,72,256]{2,1,0:T(8,128)(2,1)S(1)} %pick_rows.1), channel_id=1, source_target_pairs={{0,32},{32,64},{64,96},{96,0},{1,33},{33,65},{65,97},{97,1},{2,34}... | collective-permute-start | bytes 442376 | tf_op jit(solution)/shard_map/ppermute | solution.py:19
  124.5 7.6 %collective-permute-start.33 = (bf16[4,4,72,256]{3,2,1,0:T(8,128)(2,1)S(1)}, bf16[4,4,72,256]{3,2,1,0:T(8,128)(2,1)S(1)}, u32[]{:S(2)}, u32[]{:S(2)}) collective-permute-start(bf16[4,4,72,256]{3,2,1,0:T(8,128)(2,1)S(1)} %pad_maximum_fusion.1.in_ref), channel_id=1, source_target_pairs={{0,16},{16,0},{1,17},{17,1},{2,18},{18,2},{3,19},{19,3},{4,20},{20... | collective-permute-start | bytes 1769480 | tf_op jit(solution)/shard_map/ppermute | solution.py:19
  (5 other events, 26.6 us)

commit v14 on v13

--- a/solution.py
+++ b/solution.py
@@ -630,13 +630,12 @@
     first_own, first_far = grad_strip(2, wide, (fwd_a, fwd_b), total, True)
 
     sx, sz = lax.axis_size("x"), lax.axis_size("z")
-    first_far, *got = lax.optimization_barrier((first_far, *got))
-    joined = join(first_own, shift(first_far, "c", 1), keep, got, sx * sz)
+    first_far, ends, *got = lax.optimization_barrier((first_far, ends, *got))
+    far, *edges = lax.optimization_barrier((shift(first_far, "c", 1), *row_halo(ends)))
+    joined = join(first_own, far, keep, got, sx * sz)
     extra = keep.shape[0] // (sx * sz)
     summed = lax.all_to_all(joined, SKY, 0, 0, tiled=True)
     summed = sum_pieces(summed)
-    summed, *ends = lax.optimization_barrier((summed, *ends))
-    edges = row_halo(ends)
     parts = gather_steps(order_pieces(gather_steps(summed, "z"), extra), "x")
     main = parts[0].shape[0] - sz * extra
     grad_first = lay_first(parts, sz, chans)

time: 134 us -> 142 us (1.060)
  waiting for transfers between devices: 25.1 us -> 29.2 us
  starting transfers between devices: 54 us -> 56.4 us
  blocking collectives: 23.9 us -> 25.8 us
    ppermute x28, waiting for transfers between devices: 21.3 us -> 24.9 us  [shift(): lax.ppermute(x, axis, [(i, (i + step) % count) for i in range(count)])]
    ppermute x4, starting transfers between devices: 8.77 us -> 11 us  [row_halo(): return (lax.ppermute(ends[0], SKY, up), lax.ppermute(ends[1], SKY, down))]
    all_to_all x1, blocking collectives: 23.9 us -> 25.8 us  [body(): summed = lax.all_to_all(joined, SKY, 0, 0, tiled=True)]
where the time goes in v14:
time: 142 us
  starting transfers between devices  56.4 us (40%)
  waiting for transfers between devices  29.2 us (21%)
  blocking collectives  25.8 us (18%)
  Pallas kernels  24.7 us (17%)
  local copies, waits for them, and re-layouts  3.25 us (2%)
    ppermute x28, starting transfers between devices, shift(): lax.ppermute(x, axis, [(i, (i + step) % count) for i in range(count)])  40.9 us
    all_to_all x1, blocking collectives, body(): summed = lax.all_to_all(joined, SKY, 0, 0, tiled=True)  25.8 us
    ppermute x28, waiting for transfers between devices, shift(): lax.ppermute(x, axis, [(i, (i + step) % count) for i in range(count)])  24.9 us
    ppermute x4, starting transfers between devices, row_halo(): return (lax.ppermute(ends[0], SKY, up), lax.ppermute(ends[1], SKY, down))  11 us
    pallas_call x4, Pallas kernels, grad_strip(): pl.pallas_call(functools.partial(grad_kernel, step, len(pieces), old is n...  6.99 us
    pallas_call x4, Pallas kernels, conv_parts(): pl.pallas_call(functools.partial(conv_kernel, parts, len(adds)), out_shap...  5.84 us
    ppermute x4, waiting for transfers between devices, row_halo(): return (lax.ppermute(ends[0], SKY, up), lax.ppermute(ends[1], SKY, down))  4.25 us
  transfers between devices with their start and end apart: 34, of which 15 were waited for; matrix products, arithmetic and copies ran while one was open for 3% of the time, Pallas kernels for 14%

profile of v14, /device:TPU:1, one launch (start us, length us, event | category | flops | bytes accessed | tf_op | source)
XLA Modules:
  0.0 141.7 jit_solution(13386225509374316810)
XLA Ops:
  0.6 1.5 %collective-permute-start = (bf16[256,32,128]{2,1,0:T(8,128)(2,1)}, bf16[256,32,128]{2,1,0:T(8,128)(2,1)S(1)}, u32[]{:S(2)}, u32[]{:S(2)}) collective-permute-start(bf16[256,32,128]{2,1,0:T(8,128)(2,1)} %own_ref.1), channel_id=1, source_target_pairs={{0,16},{16,0},{1,17},{17,1},{2,18},{18,2},{3,19},{19,3},{4,20},{20... | collective-permute-start | bytes 6291464 | tf_op jit(solution)/shard_map/ppermute | solution.py:19
  6.2 4.3 %collective-permute-start.1 = (bf16[320,128]{1,0:T(8,128)(2,1)S(1)}, bf16[320,128]{1,0:T(8,128)(2,1)S(1)}, u32[]{:S(2)}, u32[]{:S(2)}) collective-permute-start(bf16[320,128]{1,0:T(8,128)(2,1)S(1)} %pad_maximum_fusion.3), channel_id=1, source_target_pairs={{0,1},{1,2},{2,3},{3,4},{4,5},{5,6},{6,7},{7,8},{8,9},{9,10},{10,1... | collective-permute-start | bytes 245768 | tf_op jit(solution)/shard_map/ppermute | solution.py:383
  14.4 1.9 %spread.1.wide_ref = bf16[4,40,32,768]{3,2,1,0:T(8,128)(2,1)S(1)} custom-call(bf16[256,32,128]{2,1,0:T(8,128)(2,1)S(1)} %copy-done.1, bf16[256,32,128]{2,1,0:T(8,128)(2,1)S(1)} %collective-permute-done.far_ref, bf16[2,320,128]{2,1,0:T(8,128)(2,1)S(1)} %pad_maximum_fusion.2.own_halo_ref.edge_ref, bf16[2,320,128]{2,1,0:T(8,128)(2,1)S(1)} %collective-permute-done.3.far_halo_ref), custom_call_target="tpu_custom_call" | custom-call | flops 1 | bytes 1 | tf_op jit(solution)/shard_map/spread/pallas_call | solution.py:94
  17.8 2.9 %collective-permute-start.8 = (bf16[17,32,256]{2,1,0:T(8,128)(2,1)S(1)}, bf16[17,32,256]{2,1,0:T(8,128)(2,1)S(1)}, u32[]{:S(2)}, u32[]{:S(2)}) collective-permute-start(bf16[17,32,256]{2,1,0:T(8,128)(2,1)S(1)} %get-tuple-element.47), channel_id=1, source_target_pairs={{0,96},{32,0},{64,32},{96,64},{1,97},{33,1},{65,33},{97,65},{2,98}... | collective-permute-start | bytes 835592 | tf_op jit(solution)/shard_map/ppermute | solution.py:19
  20.7 2.6 %collective-permute-start.6 = (bf16[34,256]{1,0:T(8,128)(2,1)S(1)}, bf16[34,256]{1,0:T(8,128)(2,1)S(1)}, u32[]{:S(2)}, u32[]{:S(2)}) collective-permute-start(bf16[34,256]{1,0:T(8,128)(2,1)S(1)} %maximum_maximum_fusion), channel_id=1, source_target_pairs={{0,16},{16,32},{32,48},{48,64},{64,80},{80,96},{96,112},{1,17},{17... | collective-permute-start | bytes 52232 | tf_op jit(solution)/shard_map/ppermute | solution.py:602
  23.3 1.9 %collective-permute-start.7 = (bf16[34,256]{1,0:T(8,128)(2,1)S(1)}, bf16[34,256]{1,0:T(8,128)(2,1)S(1)}, u32[]{:S(2)}, u32[]{:S(2)}) collective-permute-start(bf16[34,256]{1,0:T(8,128)(2,1)S(1)} %maximum_maximum_fusion.1), channel_id=1, source_target_pairs={{16,0},{32,16},{48,32},{64,48},{80,64},{96,80},{112,96},{17,1},{33... | collective-permute-start | bytes 52232 | tf_op jit(solution)/shard_map/ppermute | solution.py:603
  26.7 2.8 %collective-permute-start.10 = (bf16[17,32,256]{2,1,0:T(8,128)(2,1)S(1)}, bf16[17,32,256]{2,1,0:T(8,128)(2,1)S(1)}, u32[]{:S(2)}, u32[]{:S(2)}) collective-permute-start(bf16[17,32,256]{2,1,0:T(8,128)(2,1)S(1)} %get-tuple-element.50), channel_id=1, source_target_pairs={{0,96},{32,0},{64,32},{96,64},{1,97},{33,1},{65,33},{97,65},{2,98}... | collective-permute-start | bytes 835592 | tf_op jit(solution)/shard_map/ppermute | solution.py:19
  31.9 1.9 %collective-permute-start.12 = (bf16[17,32,256]{2,1,0:T(8,128)(2,1)S(1)}, bf16[17,32,256]{2,1,0:T(8,128)(2,1)S(1)}, u32[]{:S(2)}, u32[]{:S(2)}) collective-permute-start(bf16[17,32,256]{2,1,0:T(8,128)(2,1)S(1)} %get-tuple-element.52), channel_id=1, source_target_pairs={{0,96},{32,0},{64,32},{96,64},{1,97},{33,1},{65,33},{97,65},{2,98}... | collective-permute-start | bytes 835592 | tf_op jit(solution)/shard_map/ppermute | solution.py:19
  35.3 1.5 %back.1 = (f32[32,32,256]{2,1,0:T(8,128)S(1)}, bf16[34,32,768]{2,1,0:T(8,128)(2,1)S(1)}) custom-call(bf16[32,32,256]{2,1,0:T(8,128)(2,1)S(1)} %copy-done.2, bf16[34,256]{1,0:T(8,128)(2,1)S(1)} %collective-permute-done.6.left_ref, bf16[34,256]{1,0:T(8,128)(2,1)S(1)} %collective-permute-done.7.right_ref, ...), custom_call_target="tpu_custom_call" | custom-call | flops 1 | bytes 1 | tf_op jit(solution)/shard_map/back/pallas_call | solution.py:232
  36.8 6.0 %collective-permute-done.9.a0_ref = bf16[17,32,256]{2,1,0:T(8,128)(2,1)S(1)} collective-permute-done((bf16[17,32,256]{2,1,0:T(8,128)(2,1)S(1)}, bf16[17,32,256]{2,1,0:T(8,128)(2,1)S(1)}, u32[]{:S(2)}, u32[]{:S(2)}) %collective-permute-start.9) | collective-permute-done | bytes 278560 | tf_op jit(solution)/shard_map/ppermute | solution.py:19
  43.3 1.8 %collective-permute-start.14 = (bf16[32,32,256]{2,1,0:T(8,128)(2,1)S(1)}, bf16[32,32,256]{2,1,0:T(8,128)(2,1)S(1)}, u32[]{:S(2)}, u32[]{:S(2)}) collective-permute-start(bf16[32,32,256]{2,1,0:T(8,128)(2,1)S(1)} %get-tuple-element.56.refs_0_), channel_id=1, source_target_pairs={{0,96},{32,0},{64,32},{96,64},{1,97},{33,1},{65,33},{97,65},{2,98}... | collective-permute-start | bytes 1572872 | tf_op jit(solution)/shard_map/ppermute | solution.py:19
  45.2 1.9 %second.1 = (f32[4,288,256]{2,1,0:T(8,128)S(1)}, bf16[4,288,256]{2,1,0:T(8,128)(2,1)S(1)}) custom-call(bf16[34,32,256]{2,1,0:T(8,128)(2,1)S(1)} %get-tuple-element.64.hid_ref, bf16[34,32,768]{2,1,0:T(8,128)(2,1)S(1)} %get-tuple-element.65.wide_ref), custom_call_target="tpu_custom_call" | custom-call | flops 1 | bytes 1 | tf_op jit(solution)/shard_map/second/pallas_call | solution.py:271
  47.1 3.5 %collective-permute-start.17 = (bf16[4,288,256]{2,1,0:T(8,128)(2,1)S(1)}, bf16[4,288,256]{2,1,0:T(8,128)(2,1)S(1)}, u32[]{:S(2)}, u32[]{:S(2)}) collective-permute-start(bf16[4,288,256]{2,1,0:T(8,128)(2,1)S(1)} %get-tuple-element.67), channel_id=1, source_target_pairs={{0,16},{16,0},{1,17},{17,1},{2,18},{18,2},{3,19},{19,3},{4,20},{20... | collective-permute-start | bytes 1769480 | tf_op jit(solution)/shard_map/ppermute | solution.py:19
  50.6 1.7 %grad_first.4.refs_1_ = f32[768,768]{1,0:T(8,128)S(1)} custom-call(bf16[4,40,32,768]{3,2,1,0:T(8,128)(2,1)S(1)} %spread.1.wide_ref, bf16[32,32,256]{2,1,0:T(8,128)(2,1)S(1)} %get-tuple-element.56.refs_0_), custom_call_target="tpu_custom_call" | custom-call | flops 1 | bytes 1 | tf_op jit(solution)/shard_map/grad_first/pallas_call | solution.py:176
  52.3 2.8 %collective-permute-done.14.refs_0_ = bf16[32,32,256]{2,1,0:T(8,128)(2,1)S(1)} collective-permute-done((bf16[32,32,256]{2,1,0:T(8,128)(2,1)S(1)}, bf16[32,32,256]{2,1,0:T(8,128)(2,1)S(1)}, u32[]{:S(2)}, u32[]{:S(2)}) %collective-permute-start.14) | collective-permute-done | bytes 524320 | tf_op jit(solution)/shard_map/ppermute | solution.py:19
  55.1 3.1 %collective-permute-done.13.refs_0_ = bf16[32,32,256]{2,1,0:T(8,128)(2,1)S(1)} collective-permute-done((bf16[32,32,256]{2,1,0:T(8,128)(2,1)S(1)}, bf16[32,32,256]{2,1,0:T(8,128)(2,1)S(1)}, u32[]{:S(2)}, u32[]{:S(2)}) %collective-permute-start.13) | collective-permute-done | bytes 524320 | tf_op jit(solution)/shard_map/ppermute | solution.py:19
  60.0 2.7 %collective-permute-start.19 = (bf16[288,256]{1,0:T(8,128)(2,1)S(1)}, bf16[288,256]{1,0:T(8,128)(2,1)S(1)}, u32[]{:S(2)}, u32[]{:S(2)}) collective-permute-start(bf16[288,256]{1,0:T(8,128)(2,1)S(1)} %get-tuple-element.69), channel_id=1, source_target_pairs={{0,96},{32,0},{64,32},{96,64},{1,97},{33,1},{65,33},{97,65},{2,98}... | collective-permute-start | bytes 442376 | tf_op jit(solution)/shard_map/ppermute | solution.py:19
  62.7 1.7 %grad_first.5.refs_1_ = f32[768,768]{1,0:T(8,128)S(1)} custom-call(bf16[4,40,32,768]{3,2,1,0:T(8,128)(2,1)S(1)} %spread.1.wide_ref, bf16[32,32,256]{2,1,0:T(8,128)(2,1)S(1)} %collective-permute-done.13.refs_0_, f32[768,768]{1,0:T(8,128)S(1)} %grad_first.4.refs_1_), custom_call_target="tpu_custom_call" | custom-call | flops 1 | bytes 1 | tf_op jit(solution)/shard_map/grad_first/pallas_call | solution.py:176
  64.4 1.7 %grad_first.6.refs_2_ = f32[768,768]{1,0:T(8,128)S(1)} custom-call(bf16[4,40,32,768]{3,2,1,0:T(8,128)(2,1)S(1)} %spread.1.wide_ref, bf16[32,32,256]{2,1,0:T(8,128)(2,1)S(1)} %collective-permute-done.14.refs_0_, f32[768,768]{1,0:T(8,128)S(1)} %grad_first.5.refs_1_), custom_call_target="tpu_custom_call" | custom-call | flops 1 | bytes 1 | tf_op jit(solution)/shard_map/grad_first/pallas_call | solution.py:176
  66.2 1.8 %grad_first.7 = (f32[384,768]{1,0:T(8,128)S(1)}, bf16[384,768]{1,0:T(8,128)(2,1)S(1)}) custom-call(bf16[4,40,32,768]{3,2,1,0:T(8,128)(2,1)S(1)} %spread.1.wide_ref, bf16[16,32,256]{2,1,0:T(8,128)(2,1)S(1)} %collective-permute-done.15.refs_0_, bf16[16,32,256]{2,1,0:T(8,128)(2,1)S(1)} %collective-permute-done.16.refs_1_, f32[768,768]{1,0:T(8,128)S(1)} %grad_first.6.refs_2_), custom_call_target="tpu_custom_call" | custom-call | flops 1 | bytes 1 | tf_op jit(solution)/shard_map/grad_first/pallas_call | solution.py:176
  70.0 4.9 %collective-permute-start.21 = (bf16[384,768]{1,0:T(8,128)(2,1)S(1)}, bf16[384,768]{1,0:T(8,128)(2,1)S(1)}, u32[]{:S(2)}, u32[]{:S(2)}) collective-permute-start(bf16[384,768]{1,0:T(8,128)(2,1)S(1)} %get-tuple-element.71), channel_id=1, source_target_pairs={{0,16},{16,0},{1,17},{17,1},{2,18},{18,2},{3,19},{19,3},{4,20},{20... | collective-permute-start | bytes 1769480 | tf_op jit(solution)/shard_map/ppermute | solution.py:19
  74.9 4.1 %collective-permute-start.22 = (bf16[34,256]{1,0:T(8,128)(2,1)S(1)}, bf16[34,256]{1,0:T(8,128)(2,1)S(1)}, u32[]{:S(2)}, u32[]{:S(2)}) collective-permute-start(bf16[34,256]{1,0:T(8,128)(2,1)S(1)} %get-tuple-element.72), channel_id=1, source_target_pairs={{0,1},{1,2},{2,3},{3,4},{4,5},{5,6},{6,7},{7,8},{8,9},{9,10},{10,1... | collective-permute-start | bytes 52232 | tf_op jit(solution)/shard_map/ppermute | solution.py:383
  80.3 3.2 %collective-permute-done.23.after_ref = bf16[34,256]{1,0:T(8,128)(2,1)S(1)} collective-permute-done((bf16[34,256]{1,0:T(8,128)(2,1)S(1)}, bf16[34,256]{1,0:T(8,128)(2,1)S(1)}, u32[]{:S(2)}, u32[]{:S(2)}) %collective-permute-start.23) | collective-permute-done | bytes 17440 | tf_op jit(solution)/shard_map/ppermute | solution.py:383
  83.7 25.8 %all_to_all.5.in_ref = bf16[16,90,256]{2,1,0:T(8,128)(2,1)S(1)} all-to-all(bf16[16,90,256]{2,1,0:T(8,128)(2,1)S(1)} %join.1), channel_id=1, replica_groups=mesh['y'=4,'c'=2,'z'=4,'x'=4] {'z','x'}, dimensions={0} | all-to-all | bytes 1474560 | tf_op jit(solution)/shard_map/all_to_all | solution.py:637
  110.3 1.6 %collective-permute-start.25 = (bf16[90,256]{1,0:T(8,128)(2,1)S(1)}, bf16[90,256]{1,0:T(8,128)(2,1)S(1)}, u32[]{:S(2)}, u32[]{:S(2)}) collective-permute-start(bf16[90,256]{1,0:T(8,128)(2,1)S(1)} %sum_pieces.1.a_ref), channel_id=1, source_target_pairs={{0,12},{4,0},{8,4},{12,8},{1,13},{5,1},{9,5},{13,9},{2,14},{6,2},{... | collective-permute-start | bytes 138248 | tf_op jit(solution)/shard_map/ppermute | solution.py:19
  111.8 2.3 %collective-permute-done.26.d_ref = bf16[90,256]{1,0:T(8,128)(2,1)S(1)} collective-permute-done((bf16[90,256]{1,0:T(8,128)(2,1)S(1)}, bf16[90,256]{1,0:T(8,128)(2,1)S(1)}, u32[]{:S(2)}, u32[]{:S(2)}) %collective-permute-start.26) | collective-permute-done | bytes 46112 | tf_op jit(solution)/shard_map/ppermute | solution.py:19
  114.1 1.8 %collective-permute-done.24.b_ref = bf16[90,256]{1,0:T(8,128)(2,1)S(1)} collective-permute-done((bf16[90,256]{1,0:T(8,128)(2,1)S(1)}, bf16[90,256]{1,0:T(8,128)(2,1)S(1)}, u32[]{:S(2)}, u32[]{:S(2)}) %collective-permute-start.24) | collective-permute-done | bytes 46112 | tf_op jit(solution)/shard_map/ppermute | solution.py:19
  118.7 3.3 %collective-permute-done.29.d_ref = bf16[360,256]{1,0:T(8,128)(2,1)S(1)} collective-permute-done((bf16[360,256]{1,0:T(8,128)(2,1)S(1)}, bf16[360,256]{1,0:T(8,128)(2,1)S(1)}, u32[]{:S(2)}, u32[]{:S(2)}) %collective-permute-start.29) | collective-permute-done | bytes 184352 | tf_op jit(solution)/shard_map/ppermute | solution.py:19
  122.4 1.7 %collective-permute-done.27.b_ref = bf16[360,256]{1,0:T(8,128)(2,1)S(1)} collective-permute-done((bf16[360,256]{1,0:T(8,128)(2,1)S(1)}, bf16[360,256]{1,0:T(8,128)(2,1)S(1)}, u32[]{:S(2)}, u32[]{:S(2)}) %collective-permute-start.27) | collective-permute-done | bytes 184352 | tf_op jit(solution)/shard_map/ppermute | solution.py:19
  124.1 1.6 %collective-permute-start.32 = (bf16[4,72,256]{2,1,0:T(8,128)(2,1)S(1)}, bf16[4,72,256]{2,1,0:T(8,128)(2,1)S(1)}, u32[]{:S(2)}, u32[]{:S(2)}) collective-permute-start(bf16[4,72,256]{2,1,0:T(8,128)(2,1)S(1)} %pick_rows.1), channel_id=1, source_target_pairs={{0,64},{32,96},{64,0},{96,32},{1,65},{33,97},{65,1},{97,33},{2,66}... | collective-permute-start | bytes 442376 | tf_op jit(solution)/shard_map/ppermute | solution.py:19
  127.2 2.2 %features.1 = bf16[32,32,256]{2,1,0:T(8,128)(2,1)} custom-call(bf16[34,32,256]{2,1,0:T(8,128)(2,1)S(1)} %get-tuple-element.64.hid_ref, bf16[34,256]{1,0:T(8,128)(2,1)S(1)} %collective-permute-done.22.before_ref, bf16[34,256]{1,0:T(8,128)(2,1)S(1)} %collective-permute-done.23.after_ref, bf16[2304,256]{1,0:T(8,128)(2,1)S(1)} %bitcast.47), custom_call_target="tpu_custom_call" | custom-call | flops 1 | bytes 1 | tf_op jit(solution)/shard_map/features/pallas_call | solution.py:298
  131.4 7.4 %collective-permute-start.33 = (bf16[4,4,72,256]{3,2,1,0:T(8,128)(2,1)S(1)}, bf16[4,4,72,256]{3,2,1,0:T(8,128)(2,1)S(1)}, u32[]{:S(2)}, u32[]{:S(2)}) collective-permute-start(bf16[4,4,72,256]{3,2,1,0:T(8,128)(2,1)S(1)} %pad_maximum_fusion.1.in_ref), channel_id=1, source_target_pairs={{0,16},{16,0},{1,17},{17,1},{2,18},{18,2},{3,19},{19,3},{4,20},{20... | collective-permute-start | bytes 1769480 | tf_op jit(solution)/shard_map/ppermute | solution.py:19
  (82 shorter events, 30.6 us)
Async XLA Ops:
  0.6 13.7 %collective-permute-start = (bf16[256,32,128]{2,1,0:T(8,128)(2,1)}, bf16[256,32,128]{2,1,0:T(8,128)(2,1)S(1)}, u32[]{:S(2)}, u32[]{:S(2)}) collective-permute-start(bf16[256,32,128]{2,1,0:T(8,128)(2,1)} %own_ref.1), channel_id=1, source_target_pairs={{0,16},{16,0},{1,17},{17,1},{2,18},{18,2},{3,19},{19,3},{4,20},{20... | collective-permute-start | bytes 6291464 | tf_op jit(solution)/shard_map/ppermute | solution.py:19
  4.6 6.6 %collective-permute-start.2 = (bf16[320,128]{1,0:T(8,128)(2,1)S(1)}, bf16[320,128]{1,0:T(8,128)(2,1)S(1)}, u32[]{:S(2)}, u32[]{:S(2)}) collective-permute-start(bf16[320,128]{1,0:T(8,128)(2,1)S(1)} %pad_maximum_fusion.4), channel_id=1, source_target_pairs={{1,0},{2,1},{3,2},{4,3},{5,4},{6,5},{7,6},{8,7},{9,8},{10,9},{11,1... | collective-permute-start | bytes 245768 | tf_op jit(solution)/shard_map/ppermute | solution.py:383
  5.9 7.3 %collective-permute-start.4 = (bf16[3,3,128,256]{3,2,1,0:T(8,128)(2,1)}, bf16[3,3,128,256]{3,2,1,0:T(8,128)(2,1)S(1)}, u32[]{:S(2)}, u32[]{:S(2)}) collective-permute-start(bf16[3,3,128,256]{3,2,1,0:T(8,128)(2,1)} %param.5), channel_id=1, source_target_pairs={{0,16},{16,0},{1,17},{17,1},{2,18},{18,2},{3,19},{19,3},{4,20},{20... | collective-permute-start | bytes 1769480 | tf_op jit(solution)/shard_map/ppermute | solution.py:19
  6.2 6.1 %collective-permute-start.1 = (bf16[320,128]{1,0:T(8,128)(2,1)S(1)}, bf16[320,128]{1,0:T(8,128)(2,1)S(1)}, u32[]{:S(2)}, u32[]{:S(2)}) collective-permute-start(bf16[320,128]{1,0:T(8,128)(2,1)S(1)} %pad_maximum_fusion.3), channel_id=1, source_target_pairs={{0,1},{1,2},{2,3},{3,4},{4,5},{5,6},{6,7},{7,8},{8,9},{9,10},{10,1... | collective-permute-start | bytes 245768 | tf_op jit(solution)/shard_map/ppermute | solution.py:383
  17.8 11.9 %collective-permute-start.8 = (bf16[17,32,256]{2,1,0:T(8,128)(2,1)S(1)}, bf16[17,32,256]{2,1,0:T(8,128)(2,1)S(1)}, u32[]{:S(2)}, u32[]{:S(2)}) collective-permute-start(bf16[17,32,256]{2,1,0:T(8,128)(2,1)S(1)} %get-tuple-element.47), channel_id=1, source_target_pairs={{0,96},{32,0},{64,32},{96,64},{1,97},{33,1},{65,33},{97,65},{2,98}... | collective-permute-start | bytes 835592 | tf_op jit(solution)/shard_map/ppermute | solution.py:19
  20.7 9.0 %collective-permute-start.5 = (bf16[17,32,256]{2,1,0:T(8,128)(2,1)S(1)}, bf16[17,32,256]{2,1,0:T(8,128)(2,1)S(1)}, u32[]{:S(2)}, u32[]{:S(2)}) collective-permute-start(bf16[17,32,256]{2,1,0:T(8,128)(2,1)S(1)} %get-tuple-element.45), channel_id=1, source_target_pairs={{0,32},{32,64},{64,96},{96,0},{1,33},{33,65},{65,97},{97,1},{2,34}... | collective-permute-start | bytes 835592 | tf_op jit(solution)/shard_map/ppermute | solution.py:19
  20.7 8.8 %collective-permute-start.6 = (bf16[34,256]{1,0:T(8,128)(2,1)S(1)}, bf16[34,256]{1,0:T(8,128)(2,1)S(1)}, u32[]{:S(2)}, u32[]{:S(2)}) collective-permute-start(bf16[34,256]{1,0:T(8,128)(2,1)S(1)} %maximum_maximum_fusion), channel_id=1, source_target_pairs={{0,16},{16,32},{32,48},{48,64},{64,80},{80,96},{96,112},{1,17},{17... | collective-permute-start | bytes 52232 | tf_op jit(solution)/shard_map/ppermute | solution.py:602
  23.3 6.2 %collective-permute-start.7 = (bf16[34,256]{1,0:T(8,128)(2,1)S(1)}, bf16[34,256]{1,0:T(8,128)(2,1)S(1)}, u32[]{:S(2)}, u32[]{:S(2)}) collective-permute-start(bf16[34,256]{1,0:T(8,128)(2,1)S(1)} %maximum_maximum_fusion.1), channel_id=1, source_target_pairs={{16,0},{32,16},{48,32},{64,48},{80,64},{96,80},{112,96},{17,1},{33... | collective-permute-start | bytes 52232 | tf_op jit(solution)/shard_map/ppermute | solution.py:603
  26.7 10.2 %collective-permute-start.10 = (bf16[17,32,256]{2,1,0:T(8,128)(2,1)S(1)}, bf16[17,32,256]{2,1,0:T(8,128)(2,1)S(1)}, u32[]{:S(2)}, u32[]{:S(2)}) collective-permute-start(bf16[17,32,256]{2,1,0:T(8,128)(2,1)S(1)} %get-tuple-element.50), channel_id=1, source_target_pairs={{0,96},{32,0},{64,32},{96,64},{1,97},{33,1},{65,33},{97,65},{2,98}... | collective-permute-start | bytes 835592 | tf_op jit(solution)/shard_map/ppermute | solution.py:19
  29.5 7.3 %collective-permute-start.11 = (bf16[17,32,256]{2,1,0:T(8,128)(2,1)S(1)}, bf16[17,32,256]{2,1,0:T(8,128)(2,1)S(1)}, u32[]{:S(2)}, u32[]{:S(2)}) collective-permute-start(bf16[17,32,256]{2,1,0:T(8,128)(2,1)S(1)} %get-tuple-element.51), channel_id=1, source_target_pairs={{0,32},{32,64},{64,96},{96,0},{1,33},{33,65},{65,97},{97,1},{2,34}... | collective-permute-start | bytes 835592 | tf_op jit(solution)/shard_map/ppermute | solution.py:19
  31.1 11.7 %collective-permute-start.9 = (bf16[17,32,256]{2,1,0:T(8,128)(2,1)S(1)}, bf16[17,32,256]{2,1,0:T(8,128)(2,1)S(1)}, u32[]{:S(2)}, u32[]{:S(2)}) collective-permute-start(bf16[17,32,256]{2,1,0:T(8,128)(2,1)S(1)} %get-tuple-element.48), channel_id=1, source_target_pairs={{0,32},{32,64},{64,96},{96,0},{1,33},{33,65},{65,97},{97,1},{2,34}... | collective-permute-start | bytes 835592 | tf_op jit(solution)/shard_map/ppermute | solution.py:19
  31.9 10.9 %collective-permute-start.12 = (bf16[17,32,256]{2,1,0:T(8,128)(2,1)S(1)}, bf16[17,32,256]{2,1,0:T(8,128)(2,1)S(1)}, u32[]{:S(2)}, u32[]{:S(2)}) collective-permute-start(bf16[17,32,256]{2,1,0:T(8,128)(2,1)S(1)} %get-tuple-element.52), channel_id=1, source_target_pairs={{0,96},{32,0},{64,32},{96,64},{1,97},{33,1},{65,33},{97,65},{2,98}... | collective-permute-start | bytes 835592 | tf_op jit(solution)/shard_map/ppermute | solution.py:19
  43.3 11.7 %collective-permute-start.14 = (bf16[32,32,256]{2,1,0:T(8,128)(2,1)S(1)}, bf16[32,32,256]{2,1,0:T(8,128)(2,1)S(1)}, u32[]{:S(2)}, u32[]{:S(2)}) collective-permute-start(bf16[32,32,256]{2,1,0:T(8,128)(2,1)S(1)} %get-tuple-element.56.refs_0_), channel_id=1, source_target_pairs={{0,96},{32,0},{64,32},{96,64},{1,97},{33,1},{65,33},{97,65},{2,98}... | collective-permute-start | bytes 1572872 | tf_op jit(solution)/shard_map/ppermute | solution.py:19
  45.2 13.0 %collective-permute-start.13 = (bf16[32,32,256]{2,1,0:T(8,128)(2,1)S(1)}, bf16[32,32,256]{2,1,0:T(8,128)(2,1)S(1)}, u32[]{:S(2)}, u32[]{:S(2)}) collective-permute-start(bf16[32,32,256]{2,1,0:T(8,128)(2,1)S(1)} %get-tuple-element.56.refs_0_), channel_id=1, source_target_pairs={{0,32},{32,64},{64,96},{96,0},{1,33},{33,65},{65,97},{97,1},{2,34}... | collective-permute-start | bytes 1572872 | tf_op jit(solution)/shard_map/ppermute | solution.py:19
  47.1 12.7 %collective-permute-start.17 = (bf16[4,288,256]{2,1,0:T(8,128)(2,1)S(1)}, bf16[4,288,256]{2,1,0:T(8,128)(2,1)S(1)}, u32[]{:S(2)}, u32[]{:S(2)}) collective-permute-start(bf16[4,288,256]{2,1,0:T(8,128)(2,1)S(1)} %get-tuple-element.67), channel_id=1, source_target_pairs={{0,16},{16,0},{1,17},{17,1},{2,18},{18,2},{3,19},{19,3},{4,20},{20... | collective-permute-start | bytes 1769480 | tf_op jit(solution)/shard_map/ppermute | solution.py:19
  58.3 7.9 %collective-permute-start.16 = (bf16[16,32,256]{2,1,0:T(8,128)(2,1)S(1)}, bf16[16,32,256]{2,1,0:T(8,128)(2,1)S(1)}, u32[]{:S(2)}, u32[]{:S(2)}) collective-permute-start(bf16[16,32,256]{2,1,0:T(8,128)(2,1)S(1)} %slice.71), channel_id=1, source_target_pairs={{0,96},{32,0},{64,32},{96,64},{1,97},{33,1},{65,33},{97,65},{2,98}... | collective-permute-start | bytes 786440 | tf_op jit(solution)/shard_map/ppermute | solution.py:19
  58.6 7.6 %collective-permute-start.15 = (bf16[16,32,256]{2,1,0:T(8,128)(2,1)S(1)}, bf16[16,32,256]{2,1,0:T(8,128)(2,1)S(1)}, u32[]{:S(2)}, u32[]{:S(2)}) collective-permute-start(bf16[16,32,256]{2,1,0:T(8,128)(2,1)S(1)} %slice.70), channel_id=1, source_target_pairs={{0,32},{32,64},{64,96},{96,0},{1,33},{33,65},{65,97},{97,1},{2,34}... | collective-permute-start | bytes 786440 | tf_op jit(solution)/shard_map/ppermute | solution.py:19
  59.9 9.4 %collective-permute-start.18 = (bf16[288,256]{1,0:T(8,128)(2,1)S(1)}, bf16[288,256]{1,0:T(8,128)(2,1)S(1)}, u32[]{:S(2)}, u32[]{:S(2)}) collective-permute-start(bf16[288,256]{1,0:T(8,128)(2,1)S(1)} %get-tuple-element.68), channel_id=1, source_target_pairs={{0,32},{32,64},{64,96},{96,0},{1,33},{33,65},{65,97},{97,1},{2,34}... | collective-permute-start | bytes 442376 | tf_op jit(solution)/shard_map/ppermute | solution.py:19
  60.0 9.4 %collective-permute-start.19 = (bf16[288,256]{1,0:T(8,128)(2,1)S(1)}, bf16[288,256]{1,0:T(8,128)(2,1)S(1)}, u32[]{:S(2)}, u32[]{:S(2)}) collective-permute-start(bf16[288,256]{1,0:T(8,128)(2,1)S(1)} %get-tuple-element.69), channel_id=1, source_target_pairs={{0,96},{32,0},{64,32},{96,64},{1,97},{33,1},{65,33},{97,65},{2,98}... | collective-permute-start | bytes 442376 | tf_op jit(solution)/shard_map/ppermute | solution.py:19
  62.7 7.3 %collective-permute-start.20 = (bf16[288,256]{1,0:T(8,128)(2,1)S(1)}, bf16[288,256]{1,0:T(8,128)(2,1)S(1)}, u32[]{:S(2)}, u32[]{:S(2)}) collective-permute-start(bf16[288,256]{1,0:T(8,128)(2,1)S(1)} %get-tuple-element.70), channel_id=1, source_target_pairs={{0,64},{32,96},{64,0},{96,32},{1,65},{33,97},{65,1},{97,33},{2,66}... | collective-permute-start | bytes 442376 | tf_op jit(solution)/shard_map/ppermute | solution.py:19
  70.0 13.5 %collective-permute-start.21 = (bf16[384,768]{1,0:T(8,128)(2,1)S(1)}, bf16[384,768]{1,0:T(8,128)(2,1)S(1)}, u32[]{:S(2)}, u32[]{:S(2)}) collective-permute-start(bf16[384,768]{1,0:T(8,128)(2,1)S(1)} %get-tuple-element.71), channel_id=1, source_target_pairs={{0,16},{16,0},{1,17},{17,1},{2,18},{18,2},{3,19},{19,3},{4,20},{20... | collective-permute-start | bytes 1769480 | tf_op jit(solution)/shard_map/ppermute | solution.py:19
  74.9 5.4 %collective-permute-start.22 = (bf16[34,256]{1,0:T(8,128)(2,1)S(1)}, bf16[34,256]{1,0:T(8,128)(2,1)S(1)}, u32[]{:S(2)}, u32[]{:S(2)}) collective-permute-start(bf16[34,256]{1,0:T(8,128)(2,1)S(1)} %get-tuple-element.72), channel_id=1, source_target_pairs={{0,1},{1,2},{2,3},{3,4},{4,5},{5,6},{6,7},{7,8},{8,9},{9,10},{10,1... | collective-permute-start | bytes 52232 | tf_op jit(solution)/shard_map/ppermute | solution.py:383
  79.0 4.5 %collective-permute-start.23 = (bf16[34,256]{1,0:T(8,128)(2,1)S(1)}, bf16[34,256]{1,0:T(8,128)(2,1)S(1)}, u32[]{:S(2)}, u32[]{:S(2)}) collective-permute-start(bf16[34,256]{1,0:T(8,128)(2,1)S(1)} %get-tuple-element.73), channel_id=1, source_target_pairs={{1,0},{2,1},{3,2},{4,3},{5,4},{6,5},{7,6},{8,7},{9,8},{10,9},{11,1... | collective-permute-start | bytes 52232 | tf_op jit(solution)/shard_map/ppermute | solution.py:383
  109.6 4.5 %collective-permute-start.26 = (bf16[90,256]{1,0:T(8,128)(2,1)S(1)}, bf16[90,256]{1,0:T(8,128)(2,1)S(1)}, u32[]{:S(2)}, u32[]{:S(2)}) collective-permute-start(bf16[90,256]{1,0:T(8,128)(2,1)S(1)} %sum_pieces.1.a_ref), channel_id=1, source_target_pairs={{0,8},{4,12},{8,0},{12,4},{1,9},{5,13},{9,1},{13,5},{2,10},{6,14},... | collective-permute-start | bytes 138248 | tf_op jit(solution)/shard_map/ppermute | solution.py:19
  111.8 4.2 %collective-permute-start.24 = (bf16[90,256]{1,0:T(8,128)(2,1)S(1)}, bf16[90,256]{1,0:T(8,128)(2,1)S(1)}, u32[]{:S(2)}, u32[]{:S(2)}) collective-permute-start(bf16[90,256]{1,0:T(8,128)(2,1)S(1)} %sum_pieces.1.a_ref), channel_id=1, source_target_pairs={{0,4},{4,8},{8,12},{12,0},{1,5},{5,9},{9,13},{13,1},{2,6},{6,10},{... | collective-permute-start | bytes 138248 | tf_op jit(solution)/shard_map/ppermute | solution.py:19
  116.0 6.0 %collective-permute-start.29 = (bf16[360,256]{1,0:T(8,128)(2,1)S(1)}, bf16[360,256]{1,0:T(8,128)(2,1)S(1)}, u32[]{:S(2)}, u32[]{:S(2)}) collective-permute-start(bf16[360,256]{1,0:T(8,128)(2,1)S(1)} %order_pieces.1.a_ref), channel_id=1, source_target_pairs={{0,2},{1,3},{2,0},{3,1},{4,6},{5,7},{6,4},{7,5},{8,10},{9,11},{10,... | collective-permute-start | bytes 552968 | tf_op jit(solution)/shard_map/ppermute | solution.py:19
  117.3 5.1 %collective-permute-start.28 = (bf16[360,256]{1,0:T(8,128)(2,1)S(1)}, bf16[360,256]{1,0:T(8,128)(2,1)S(1)}, u32[]{:S(2)}, u32[]{:S(2)}) collective-permute-start(bf16[360,256]{1,0:T(8,128)(2,1)S(1)} %order_pieces.1.a_ref), channel_id=1, source_target_pairs={{0,3},{1,0},{2,1},{3,2},{4,7},{5,4},{6,5},{7,6},{8,11},{9,8},{10,9... | collective-permute-start | bytes 552968 | tf_op jit(solution)/shard_map/ppermute | solution.py:19
  118.5 5.6 %collective-permute-start.27 = (bf16[360,256]{1,0:T(8,128)(2,1)S(1)}, bf16[360,256]{1,0:T(8,128)(2,1)S(1)}, u32[]{:S(2)}, u32[]{:S(2)}) collective-permute-start(bf16[360,256]{1,0:T(8,128)(2,1)S(1)} %order_pieces.1.a_ref), channel_id=1, source_target_pairs={{0,1},{1,2},{2,3},{3,0},{4,5},{5,6},{6,7},{7,4},{8,9},{9,10},{10,1... | collective-permute-start | bytes 552968 | tf_op jit(solution)/shard_map/ppermute | solution.py:19
  124.1 6.3 %collective-permute-start.32 = (bf16[4,72,256]{2,1,0:T(8,128)(2,1)S(1)}, bf16[4,72,256]{2,1,0:T(8,128)(2,1)S(1)}, u32[]{:S(2)}, u32[]{:S(2)}) collective-permute-start(bf16[4,72,256]{2,1,0:T(8,128)(2,1)S(1)} %pick_rows.1), channel_id=1, source_target_pairs={{0,64},{32,96},{64,0},{96,32},{1,65},{33,97},{65,1},{97,33},{2,66}... | collective-permute-start | bytes 442376 | tf_op jit(solution)/shard_map/ppermute | solution.py:19
  125.7 4.8 %collective-permute-start.31 = (bf16[4,72,256]{2,1,0:T(8,128)(2,1)S(1)}, bf16[4,72,256]{2,1,0:T(8,128)(2,1)S(1)}, u32[]{:S(2)}, u32[]{:S(2)}) collective-permute-start(bf16[4,72,256]{2,1,0:T(8,128)(2,1)S(1)} %pick_rows.1), channel_id=1, source_target_pairs={{0,96},{32,0},{64,32},{96,64},{1,97},{33,1},{65,33},{97,65},{2,98}... | collective-permute-start | bytes 442376 | tf_op jit(solution)/shard_map/ppermute | solution.py:19
  125.7 5.6 %collective-permute-start.30 = (bf16[4,72,256]{2,1,0:T(8,128)(2,1)S(1)}, bf16[4,72,256]{2,1,0:T(8,128)(2,1)S(1)}, u32[]{:S(2)}, u32[]{:S(2)}) collective-permute-start(bf16[4,72,256]{2,1,0:T(8,128)(2,1)S(1)} %pick_rows.1), channel_id=1, source_target_pairs={{0,32},{32,64},{64,96},{96,0},{1,33},{33,65},{65,97},{97,1},{2,34}... | collective-permute-start | bytes 442376 | tf_op jit(solution)/shard_map/ppermute | solution.py:19
  131.4 9.0 %collective-permute-start.33 = (bf16[4,4,72,256]{3,2,1,0:T(8,128)(2,1)S(1)}, bf16[4,4,72,256]{3,2,1,0:T(8,128)(2,1)S(1)}, u32[]{:S(2)}, u32[]{:S(2)}) collective-permute-start(bf16[4,4,72,256]{3,2,1,0:T(8,128)(2,1)S(1)} %pad_maximum_fusion.1.in_ref), channel_id=1, source_target_pairs={{0,16},{16,0},{1,17},{17,1},{2,18},{18,2},{3,19},{19,3},{4,20},{20... | collective-permute-start | bytes 1769480 | tf_op jit(solution)/shard_map/ppermute | solution.py:19
  (5 other events, 26.6 us)

commit v15 on v13

--- a/solution.py
+++ b/solution.py
@@ -637,14 +637,15 @@
     summed = sum_pieces(summed)
     summed, *ends = lax.optimization_barrier((summed, *ends))
     edges = row_halo(ends)
-    parts = gather_steps(order_pieces(gather_steps(summed, "z"), extra), "x")
+    *pieces, before, after = lax.optimization_barrier((*gather_steps(summed, "z"), *edges))
+    features = features_tile(hidden, (before, after), weight_second)
+    parts = gather_steps(order_pieces(pieces, extra), "x")
     main = parts[0].shape[0] - sz * extra
     grad_first = lay_first(parts, sz, chans)
     share = pick_rows(parts, main)
-    share, *edges = lax.optimization_barrier((share, *edges))
-    features = features_tile(hidden, edges, weight_second)
-    share, grad_first, features = lax.optimization_barrier(
-        (jnp.stack(gather_steps(share, "y")), grad_first, features)
+    share, features = lax.optimization_barrier((share, features))
+    share, grad_first = lax.optimization_barrier(
+        (jnp.stack(gather_steps(share, "y")), grad_first)
     )
     grad_second = lay_second(shift(share, "c", 1), lay_second(share))
     grad_second = grad_second.reshape(3, 3, outs, outs)

time: 134 us -> 137 us (1.022)
  waiting for transfers between devices: 25.1 us -> 28.5 us
    ppermute x28, waiting for transfers between devices: 21.3 us -> 24 us  [shift(): lax.ppermute(x, axis, [(i, (i + step) % count) for i in range(count)])]
  transfers between devices with their start and end apart: 34 -> 34, of which waited for: 15 -> 14; matrix products, arithmetic and copies ran while one was open for 3% -> 3% of each run, Pallas kernels for 14% -> 14%
where the time goes in v15:
time: 137 us
  starting transfers between devices  54 us (39%)
  waiting for transfers between devices  28.5 us (21%)
  Pallas kernels  24.7 us (18%)
  blocking collectives  23.9 us (17%)
  local copies, waits for them, and re-layouts  3.25 us (2%)
    ppermute x28, starting transfers between devices, shift(): lax.ppermute(x, axis, [(i, (i + step) % count) for i in range(count)])  40.7 us
    ppermute x28, waiting for transfers between devices, shift(): lax.ppermute(x, axis, [(i, (i + step) % count) for i in range(count)])  24 us
    all_to_all x1, blocking collectives, body(): summed = lax.all_to_all(joined, SKY, 0, 0, tiled=True)  23.9 us
    ppermute x4, starting transfers between devices, row_halo(): return (lax.ppermute(ends[0], SKY, up), lax.ppermute(ends[1], SKY, down))  8.81 us
    pallas_call x4, Pallas kernels, grad_strip(): pl.pallas_call(functools.partial(grad_kernel, step, len(pieces), old is n...  7 us
    pallas_call x4, Pallas kernels, conv_parts(): pl.pallas_call(functools.partial(conv_kernel, parts, len(adds)), out_shap...  5.84 us
    ppermute x4, waiting for transfers between devices, row_halo(): return (lax.ppermute(ends[0], SKY, up), lax.ppermute(ends[1], SKY, down))  4.55 us
  transfers between devices with their start and end apart: 34, of which 14 were waited for; matrix products, arithmetic and copies ran while one was open for 3% of the time, Pallas kernels for 14%

profile of v15, /device:TPU:1, one launch (start us, length us, event | category | flops | bytes accessed | tf_op | source)
XLA Modules:
  0.0 136.8 jit_solution(18292427852393548836)
XLA Ops:
  6.2 4.3 %collective-permute-start.1 = (bf16[320,128]{1,0:T(8,128)(2,1)S(1)}, bf16[320,128]{1,0:T(8,128)(2,1)S(1)}, u32[]{:S(2)}, u32[]{:S(2)}) collective-permute-start(bf16[320,128]{1,0:T(8,128)(2,1)S(1)} %pad_maximum_fusion.3), channel_id=1, source_target_pairs={{0,1},{1,2},{2,3},{3,4},{4,5},{5,6},{6,7},{7,8},{8,9},{9,10},{10,1... | collective-permute-start | bytes 245768 | tf_op jit(solution)/shard_map/ppermute | solution.py:383
  14.4 1.9 %spread.1.wide_ref = bf16[4,40,32,768]{3,2,1,0:T(8,128)(2,1)S(1)} custom-call(bf16[256,32,128]{2,1,0:T(8,128)(2,1)S(1)} %copy-done.1, bf16[256,32,128]{2,1,0:T(8,128)(2,1)S(1)} %collective-permute-done.far_ref, bf16[2,320,128]{2,1,0:T(8,128)(2,1)S(1)} %pad_maximum_fusion.2.own_halo_ref.edge_ref, bf16[2,320,128]{2,1,0:T(8,128)(2,1)S(1)} %collective-permute-done.3.far_halo_ref), custom_call_target="tpu_custom_call" | custom-call | flops 1 | bytes 1 | tf_op jit(solution)/shard_map/spread/pallas_call | solution.py:94
  17.8 2.9 %collective-permute-start.8 = (bf16[17,32,256]{2,1,0:T(8,128)(2,1)S(1)}, bf16[17,32,256]{2,1,0:T(8,128)(2,1)S(1)}, u32[]{:S(2)}, u32[]{:S(2)}) collective-permute-start(bf16[17,32,256]{2,1,0:T(8,128)(2,1)S(1)} %get-tuple-element.49), channel_id=1, source_target_pairs={{0,96},{32,0},{64,32},{96,64},{1,97},{33,1},{65,33},{97,65},{2,98}... | collective-permute-start | bytes 835592 | tf_op jit(solution)/shard_map/ppermute | solution.py:19
  20.7 2.6 %collective-permute-start.6 = (bf16[34,256]{1,0:T(8,128)(2,1)S(1)}, bf16[34,256]{1,0:T(8,128)(2,1)S(1)}, u32[]{:S(2)}, u32[]{:S(2)}) collective-permute-start(bf16[34,256]{1,0:T(8,128)(2,1)S(1)} %maximum_maximum_fusion), channel_id=1, source_target_pairs={{0,16},{16,32},{32,48},{48,64},{64,80},{80,96},{96,112},{1,17},{17... | collective-permute-start | bytes 52232 | tf_op jit(solution)/shard_map/ppermute | solution.py:602
  23.3 1.9 %collective-permute-start.7 = (bf16[34,256]{1,0:T(8,128)(2,1)S(1)}, bf16[34,256]{1,0:T(8,128)(2,1)S(1)}, u32[]{:S(2)}, u32[]{:S(2)}) collective-permute-start(bf16[34,256]{1,0:T(8,128)(2,1)S(1)} %maximum_maximum_fusion.1), channel_id=1, source_target_pairs={{16,0},{32,16},{48,32},{64,48},{80,64},{96,80},{112,96},{17,1},{33... | collective-permute-start | bytes 52232 | tf_op jit(solution)/shard_map/ppermute | solution.py:603
  26.7 2.8 %collective-permute-start.10 = (bf16[17,32,256]{2,1,0:T(8,128)(2,1)S(1)}, bf16[17,32,256]{2,1,0:T(8,128)(2,1)S(1)}, u32[]{:S(2)}, u32[]{:S(2)}) collective-permute-start(bf16[17,32,256]{2,1,0:T(8,128)(2,1)S(1)} %get-tuple-element.52), channel_id=1, source_target_pairs={{0,96},{32,0},{64,32},{96,64},{1,97},{33,1},{65,33},{97,65},{2,98}... | collective-permute-start | bytes 835592 | tf_op jit(solution)/shard_map/ppermute | solution.py:19
  31.9 1.9 %collective-permute-start.12 = (bf16[17,32,256]{2,1,0:T(8,128)(2,1)S(1)}, bf16[17,32,256]{2,1,0:T(8,128)(2,1)S(1)}, u32[]{:S(2)}, u32[]{:S(2)}) collective-permute-start(bf16[17,32,256]{2,1,0:T(8,128)(2,1)S(1)} %get-tuple-element.54), channel_id=1, source_target_pairs={{0,96},{32,0},{64,32},{96,64},{1,97},{33,1},{65,33},{97,65},{2,98}... | collective-permute-start | bytes 835592 | tf_op jit(solution)/shard_map/ppermute | solution.py:19
  36.8 6.0 %collective-permute-done.9.a0_ref = bf16[17,32,256]{2,1,0:T(8,128)(2,1)S(1)} collective-permute-done((bf16[17,32,256]{2,1,0:T(8,128)(2,1)S(1)}, bf16[17,32,256]{2,1,0:T(8,128)(2,1)S(1)}, u32[]{:S(2)}, u32[]{:S(2)}) %collective-permute-start.9) | collective-permute-done | bytes 278560 | tf_op jit(solution)/shard_map/ppermute | solution.py:19
  43.3 1.8 %collective-permute-start.14 = (bf16[32,32,256]{2,1,0:T(8,128)(2,1)S(1)}, bf16[32,32,256]{2,1,0:T(8,128)(2,1)S(1)}, u32[]{:S(2)}, u32[]{:S(2)}) collective-permute-start(bf16[32,32,256]{2,1,0:T(8,128)(2,1)S(1)} %get-tuple-element.58.refs_0_), channel_id=1, source_target_pairs={{0,96},{32,0},{64,32},{96,64},{1,97},{33,1},{65,33},{97,65},{2,98}... | collective-permute-start | bytes 1572872 | tf_op jit(solution)/shard_map/ppermute | solution.py:19
  45.2 1.9 %second.1 = (f32[4,288,256]{2,1,0:T(8,128)S(1)}, bf16[4,288,256]{2,1,0:T(8,128)(2,1)S(1)}) custom-call(bf16[34,32,256]{2,1,0:T(8,128)(2,1)S(1)} %get-tuple-element.64.hid_ref, bf16[34,32,768]{2,1,0:T(8,128)(2,1)S(1)} %get-tuple-element.65.wide_ref), custom_call_target="tpu_custom_call" | custom-call | flops 1 | bytes 1 | tf_op jit(solution)/shard_map/second/pallas_call | solution.py:271
  47.1 3.5 %collective-permute-start.17 = (bf16[4,288,256]{2,1,0:T(8,128)(2,1)S(1)}, bf16[4,288,256]{2,1,0:T(8,128)(2,1)S(1)}, u32[]{:S(2)}, u32[]{:S(2)}) collective-permute-start(bf16[4,288,256]{2,1,0:T(8,128)(2,1)S(1)} %get-tuple-element.67), channel_id=1, source_target_pairs={{0,16},{16,0},{1,17},{17,1},{2,18},{18,2},{3,19},{19,3},{4,20},{20... | collective-permute-start | bytes 1769480 | tf_op jit(solution)/shard_map/ppermute | solution.py:19
  50.6 1.7 %grad_first.4.refs_1_ = f32[768,768]{1,0:T(8,128)S(1)} custom-call(bf16[4,40,32,768]{3,2,1,0:T(8,128)(2,1)S(1)} %spread.1.wide_ref, bf16[32,32,256]{2,1,0:T(8,128)(2,1)S(1)} %get-tuple-element.58.refs_0_), custom_call_target="tpu_custom_call" | custom-call | flops 1 | bytes 1 | tf_op jit(solution)/shard_map/grad_first/pallas_call | solution.py:176
  52.3 2.8 %collective-permute-done.14.refs_0_ = bf16[32,32,256]{2,1,0:T(8,128)(2,1)S(1)} collective-permute-done((bf16[32,32,256]{2,1,0:T(8,128)(2,1)S(1)}, bf16[32,32,256]{2,1,0:T(8,128)(2,1)S(1)}, u32[]{:S(2)}, u32[]{:S(2)}) %collective-permute-start.14) | collective-permute-done | bytes 524320 | tf_op jit(solution)/shard_map/ppermute | solution.py:19
  55.1 3.1 %collective-permute-done.13.refs_0_ = bf16[32,32,256]{2,1,0:T(8,128)(2,1)S(1)} collective-permute-done((bf16[32,32,256]{2,1,0:T(8,128)(2,1)S(1)}, bf16[32,32,256]{2,1,0:T(8,128)(2,1)S(1)}, u32[]{:S(2)}, u32[]{:S(2)}) %collective-permute-start.13) | collective-permute-done | bytes 524320 | tf_op jit(solution)/shard_map/ppermute | solution.py:19
  60.0 2.7 %collective-permute-start.19 = (bf16[288,256]{1,0:T(8,128)(2,1)S(1)}, bf16[288,256]{1,0:T(8,128)(2,1)S(1)}, u32[]{:S(2)}, u32[]{:S(2)}) collective-permute-start(bf16[288,256]{1,0:T(8,128)(2,1)S(1)} %get-tuple-element.69), channel_id=1, source_target_pairs={{0,96},{32,0},{64,32},{96,64},{1,97},{33,1},{65,33},{97,65},{2,98}... | collective-permute-start | bytes 442376 | tf_op jit(solution)/shard_map/ppermute | solution.py:19
  62.7 1.7 %grad_first.5.refs_1_ = f32[768,768]{1,0:T(8,128)S(1)} custom-call(bf16[4,40,32,768]{3,2,1,0:T(8,128)(2,1)S(1)} %spread.1.wide_ref, bf16[32,32,256]{2,1,0:T(8,128)(2,1)S(1)} %collective-permute-done.13.refs_0_, f32[768,768]{1,0:T(8,128)S(1)} %grad_first.4.refs_1_), custom_call_target="tpu_custom_call" | custom-call | flops 1 | bytes 1 | tf_op jit(solution)/shard_map/grad_first/pallas_call | solution.py:176
  64.4 1.7 %grad_first.6.refs_2_ = f32[768,768]{1,0:T(8,128)S(1)} custom-call(bf16[4,40,32,768]{3,2,1,0:T(8,128)(2,1)S(1)} %spread.1.wide_ref, bf16[32,32,256]{2,1,0:T(8,128)(2,1)S(1)} %collective-permute-done.14.refs_0_, f32[768,768]{1,0:T(8,128)S(1)} %grad_first.5.refs_1_), custom_call_target="tpu_custom_call" | custom-call | flops 1 | bytes 1 | tf_op jit(solution)/shard_map/grad_first/pallas_call | solution.py:176
  66.2 1.8 %grad_first.7 = (f32[384,768]{1,0:T(8,128)S(1)}, bf16[384,768]{1,0:T(8,128)(2,1)S(1)}) custom-call(bf16[4,40,32,768]{3,2,1,0:T(8,128)(2,1)S(1)} %spread.1.wide_ref, bf16[16,32,256]{2,1,0:T(8,128)(2,1)S(1)} %collective-permute-done.15.refs_0_, bf16[16,32,256]{2,1,0:T(8,128)(2,1)S(1)} %collective-permute-done.16.refs_1_, f32[768,768]{1,0:T(8,128)S(1)} %grad_first.6.refs_2_), custom_call_target="tpu_custom_call" | custom-call | flops 1 | bytes 1 | tf_op jit(solution)/shard_map/grad_first/pallas_call | solution.py:176
  70.0 4.9 %collective-permute-start.21 = (bf16[384,768]{1,0:T(8,128)(2,1)S(1)}, bf16[384,768]{1,0:T(8,128)(2,1)S(1)}, u32[]{:S(2)}, u32[]{:S(2)}) collective-permute-start(bf16[384,768]{1,0:T(8,128)(2,1)S(1)} %get-tuple-element.71), channel_id=1, source_target_pairs={{0,16},{16,0},{1,17},{17,1},{2,18},{18,2},{3,19},{19,3},{4,20},{20... | collective-permute-start | bytes 1769480 | tf_op jit(solution)/shard_map/ppermute | solution.py:19
  74.9 1.6 %collective-permute-done.21.far_ref = bf16[384,768]{1,0:T(8,128)(2,1)S(1)} collective-permute-done((bf16[384,768]{1,0:T(8,128)(2,1)S(1)}, bf16[384,768]{1,0:T(8,128)(2,1)S(1)}, u32[]{:S(2)}, u32[]{:S(2)}) %collective-permute-start.21) | collective-permute-done | bytes 589856 | tf_op jit(solution)/shard_map/ppermute | solution.py:19
  76.7 23.9 %all_to_all.5.in_ref = bf16[16,90,256]{2,1,0:T(8,128)(2,1)S(1)} all-to-all(bf16[16,90,256]{2,1,0:T(8,128)(2,1)S(1)} %join.1), channel_id=1, replica_groups=mesh['y'=4,'c'=2,'z'=4,'x'=4] {'z','x'}, dimensions={0} | all-to-all | bytes 1474560 | tf_op jit(solution)/shard_map/all_to_all | solution.py:636
  102.8 1.9 %collective-permute-start.25 = (bf16[34,256]{1,0:T(8,128)(2,1)S(1)}, bf16[34,256]{1,0:T(8,128)(2,1)S(1)}, u32[]{:S(2)}, u32[]{:S(2)}) collective-permute-start(bf16[34,256]{1,0:T(8,128)(2,1)S(1)} %get-tuple-element.79), channel_id=1, source_target_pairs={{0,1},{1,2},{2,3},{3,4},{4,5},{5,6},{6,7},{7,8},{8,9},{9,10},{10,1... | collective-permute-start | bytes 52232 | tf_op jit(solution)/shard_map/ppermute | solution.py:383
  106.1 3.5 %collective-permute-done.26.after_ref = bf16[34,256]{1,0:T(8,128)(2,1)S(1)} collective-permute-done((bf16[34,256]{1,0:T(8,128)(2,1)S(1)}, bf16[34,256]{1,0:T(8,128)(2,1)S(1)}, u32[]{:S(2)}, u32[]{:S(2)}) %collective-permute-start.26) | collective-permute-done | bytes 17440 | tf_op jit(solution)/shard_map/ppermute | solution.py:383
  109.7 2.5 %collective-permute-start.29 = (bf16[360,256]{1,0:T(8,128)(2,1)S(1)}, bf16[360,256]{1,0:T(8,128)(2,1)S(1)}, u32[]{:S(2)}, u32[]{:S(2)}) collective-permute-start(bf16[360,256]{1,0:T(8,128)(2,1)S(1)} %order_pieces.1.a_ref), channel_id=1, source_target_pairs={{0,2},{1,3},{2,0},{3,1},{4,6},{5,7},{6,4},{7,5},{8,10},{9,11},{10,... | collective-permute-start | bytes 552968 | tf_op jit(solution)/shard_map/ppermute | solution.py:19
  112.2 2.5 %collective-permute-start.28 = (bf16[360,256]{1,0:T(8,128)(2,1)S(1)}, bf16[360,256]{1,0:T(8,128)(2,1)S(1)}, u32[]{:S(2)}, u32[]{:S(2)}) collective-permute-start(bf16[360,256]{1,0:T(8,128)(2,1)S(1)} %order_pieces.1.a_ref), channel_id=1, source_target_pairs={{0,3},{1,0},{2,1},{3,2},{4,7},{5,4},{6,5},{7,6},{8,11},{9,8},{10,9... | collective-permute-start | bytes 552968 | tf_op jit(solution)/shard_map/ppermute | solution.py:19
  115.1 2.2 %features.1 = bf16[32,32,256]{2,1,0:T(8,128)(2,1)} custom-call(bf16[34,32,256]{2,1,0:T(8,128)(2,1)S(1)} %get-tuple-element.64.hid_ref, bf16[34,256]{1,0:T(8,128)(2,1)S(1)} %collective-permute-done.25.before_ref, bf16[34,256]{1,0:T(8,128)(2,1)S(1)} %collective-permute-done.26.after_ref, bf16[2304,256]{1,0:T(8,128)(2,1)S(1)} %bitcast.47), custom_call_target="tpu_custom_call" | custom-call | flops 1 | bytes 1 | tf_op jit(solution)/shard_map/features/pallas_call | solution.py:298
  117.3 3.0 %collective-permute-done.28.c_ref = bf16[360,256]{1,0:T(8,128)(2,1)S(1)} collective-permute-done((bf16[360,256]{1,0:T(8,128)(2,1)S(1)}, bf16[360,256]{1,0:T(8,128)(2,1)S(1)}, u32[]{:S(2)}, u32[]{:S(2)}) %collective-permute-start.28) | collective-permute-done | bytes 184352 | tf_op jit(solution)/shard_map/ppermute | solution.py:19
  120.4 1.7 %collective-permute-done.27.b_ref = bf16[360,256]{1,0:T(8,128)(2,1)S(1)} collective-permute-done((bf16[360,256]{1,0:T(8,128)(2,1)S(1)}, bf16[360,256]{1,0:T(8,128)(2,1)S(1)}, u32[]{:S(2)}, u32[]{:S(2)}) %collective-permute-start.27) | collective-permute-done | bytes 184352 | tf_op jit(solution)/shard_map/ppermute | solution.py:19
  122.1 1.5 %collective-permute-start.32 = (bf16[4,72,256]{2,1,0:T(8,128)(2,1)S(1)}, bf16[4,72,256]{2,1,0:T(8,128)(2,1)S(1)}, u32[]{:S(2)}, u32[]{:S(2)}) collective-permute-start(bf16[4,72,256]{2,1,0:T(8,128)(2,1)S(1)} %pick_rows.1), channel_id=1, source_target_pairs={{0,64},{32,96},{64,0},{96,32},{1,65},{33,97},{65,1},{97,33},{2,66}... | collective-permute-start | bytes 442376 | tf_op jit(solution)/shard_map/ppermute | solution.py:19
  126.2 1.5 %collective-permute-done.32 = bf16[4,72,256]{2,1,0:T(8,128)(2,1)S(1)} collective-permute-done((bf16[4,72,256]{2,1,0:T(8,128)(2,1)S(1)}, bf16[4,72,256]{2,1,0:T(8,128)(2,1)S(1)}, u32[]{:S(2)}, u32[]{:S(2)}) %collective-permute-start.32) | collective-permute-done | bytes 147488 | tf_op jit(solution)/shard_map/ppermute | solution.py:19
  127.7 1.5 %collective-permute-done.30 = bf16[4,72,256]{2,1,0:T(8,128)(2,1)S(1)} collective-permute-done((bf16[4,72,256]{2,1,0:T(8,128)(2,1)S(1)}, bf16[4,72,256]{2,1,0:T(8,128)(2,1)S(1)}, u32[]{:S(2)}, u32[]{:S(2)}) %collective-permute-start.30) | collective-permute-done | bytes 147488 | tf_op jit(solution)/shard_map/ppermute | solution.py:19
  129.3 4.5 %collective-permute-start.33 = (bf16[4,4,72,256]{3,2,1,0:T(8,128)(2,1)S(1)}, bf16[4,4,72,256]{3,2,1,0:T(8,128)(2,1)S(1)}, u32[]{:S(2)}, u32[]{:S(2)}) collective-permute-start(bf16[4,4,72,256]{3,2,1,0:T(8,128)(2,1)S(1)} %pad_maximum_fusion.1.in_ref), channel_id=1, source_target_pairs={{0,16},{16,0},{1,17},{17,1},{2,18},{18,2},{3,19},{19,3},{4,20},{20... | collective-permute-start | bytes 1769480 | tf_op jit(solution)/shard_map/ppermute | solution.py:19
  (82 shorter events, 31.7 us)
Async XLA Ops:
  0.6 13.7 %collective-permute-start = (bf16[256,32,128]{2,1,0:T(8,128)(2,1)}, bf16[256,32,128]{2,1,0:T(8,128)(2,1)S(1)}, u32[]{:S(2)}, u32[]{:S(2)}) collective-permute-start(bf16[256,32,128]{2,1,0:T(8,128)(2,1)} %own_ref.1), channel_id=1, source_target_pairs={{0,16},{16,0},{1,17},{17,1},{2,18},{18,2},{3,19},{19,3},{4,20},{20... | collective-permute-start | bytes 6291464 | tf_op jit(solution)/shard_map/ppermute | solution.py:19
  4.6 6.6 %collective-permute-start.2 = (bf16[320,128]{1,0:T(8,128)(2,1)S(1)}, bf16[320,128]{1,0:T(8,128)(2,1)S(1)}, u32[]{:S(2)}, u32[]{:S(2)}) collective-permute-start(bf16[320,128]{1,0:T(8,128)(2,1)S(1)} %pad_maximum_fusion.4), channel_id=1, source_target_pairs={{1,0},{2,1},{3,2},{4,3},{5,4},{6,5},{7,6},{8,7},{9,8},{10,9},{11,1... | collective-permute-start | bytes 245768 | tf_op jit(solution)/shard_map/ppermute | solution.py:383
  5.9 7.3 %collective-permute-start.4 = (bf16[3,3,128,256]{3,2,1,0:T(8,128)(2,1)}, bf16[3,3,128,256]{3,2,1,0:T(8,128)(2,1)S(1)}, u32[]{:S(2)}, u32[]{:S(2)}) collective-permute-start(bf16[3,3,128,256]{3,2,1,0:T(8,128)(2,1)} %param.5), channel_id=1, source_target_pairs={{0,16},{16,0},{1,17},{17,1},{2,18},{18,2},{3,19},{19,3},{4,20},{20... | collective-permute-start | bytes 1769480 | tf_op jit(solution)/shard_map/ppermute | solution.py:19
  6.2 6.1 %collective-permute-start.1 = (bf16[320,128]{1,0:T(8,128)(2,1)S(1)}, bf16[320,128]{1,0:T(8,128)(2,1)S(1)}, u32[]{:S(2)}, u32[]{:S(2)}) collective-permute-start(bf16[320,128]{1,0:T(8,128)(2,1)S(1)} %pad_maximum_fusion.3), channel_id=1, source_target_pairs={{0,1},{1,2},{2,3},{3,4},{4,5},{5,6},{6,7},{7,8},{8,9},{9,10},{10,1... | collective-permute-start | bytes 245768 | tf_op jit(solution)/shard_map/ppermute | solution.py:383
  17.8 11.9 %collective-permute-start.8 = (bf16[17,32,256]{2,1,0:T(8,128)(2,1)S(1)}, bf16[17,32,256]{2,1,0:T(8,128)(2,1)S(1)}, u32[]{:S(2)}, u32[]{:S(2)}) collective-permute-start(bf16[17,32,256]{2,1,0:T(8,128)(2,1)S(1)} %get-tuple-element.49), channel_id=1, source_target_pairs={{0,96},{32,0},{64,32},{96,64},{1,97},{33,1},{65,33},{97,65},{2,98}... | collective-permute-start | bytes 835592 | tf_op jit(solution)/shard_map/ppermute | solution.py:19
  20.7 9.0 %collective-permute-start.5 = (bf16[17,32,256]{2,1,0:T(8,128)(2,1)S(1)}, bf16[17,32,256]{2,1,0:T(8,128)(2,1)S(1)}, u32[]{:S(2)}, u32[]{:S(2)}) collective-permute-start(bf16[17,32,256]{2,1,0:T(8,128)(2,1)S(1)} %get-tuple-element.47), channel_id=1, source_target_pairs={{0,32},{32,64},{64,96},{96,0},{1,33},{33,65},{65,97},{97,1},{2,34}... | collective-permute-start | bytes 835592 | tf_op jit(solution)/shard_map/ppermute | solution.py:19
  20.7 8.8 %collective-permute-start.6 = (bf16[34,256]{1,0:T(8,128)(2,1)S(1)}, bf16[34,256]{1,0:T(8,128)(2,1)S(1)}, u32[]{:S(2)}, u32[]{:S(2)}) collective-permute-start(bf16[34,256]{1,0:T(8,128)(2,1)S(1)} %maximum_maximum_fusion), channel_id=1, source_target_pairs={{0,16},{16,32},{32,48},{48,64},{64,80},{80,96},{96,112},{1,17},{17... | collective-permute-start | bytes 52232 | tf_op jit(solution)/shard_map/ppermute | solution.py:602
  23.3 6.2 %collective-permute-start.7 = (bf16[34,256]{1,0:T(8,128)(2,1)S(1)}, bf16[34,256]{1,0:T(8,128)(2,1)S(1)}, u32[]{:S(2)}, u32[]{:S(2)}) collective-permute-start(bf16[34,256]{1,0:T(8,128)(2,1)S(1)} %maximum_maximum_fusion.1), channel_id=1, source_target_pairs={{16,0},{32,16},{48,32},{64,48},{80,64},{96,80},{112,96},{17,1},{33... | collective-permute-start | bytes 52232 | tf_op jit(solution)/shard_map/ppermute | solution.py:603
  26.7 10.2 %collective-permute-start.10 = (bf16[17,32,256]{2,1,0:T(8,128)(2,1)S(1)}, bf16[17,32,256]{2,1,0:T(8,128)(2,1)S(1)}, u32[]{:S(2)}, u32[]{:S(2)}) collective-permute-start(bf16[17,32,256]{2,1,0:T(8,128)(2,1)S(1)} %get-tuple-element.52), channel_id=1, source_target_pairs={{0,96},{32,0},{64,32},{96,64},{1,97},{33,1},{65,33},{97,65},{2,98}... | collective-permute-start | bytes 835592 | tf_op jit(solution)/shard_map/ppermute | solution.py:19
  29.5 7.3 %collective-permute-start.11 = (bf16[17,32,256]{2,1,0:T(8,128)(2,1)S(1)}, bf16[17,32,256]{2,1,0:T(8,128)(2,1)S(1)}, u32[]{:S(2)}, u32[]{:S(2)}) collective-permute-start(bf16[17,32,256]{2,1,0:T(8,128)(2,1)S(1)} %get-tuple-element.53), channel_id=1, source_target_pairs={{0,32},{32,64},{64,96},{96,0},{1,33},{33,65},{65,97},{97,1},{2,34}... | collective-permute-start | bytes 835592 | tf_op jit(solution)/shard_map/ppermute | solution.py:19
  31.1 11.7 %collective-permute-start.9 = (bf16[17,32,256]{2,1,0:T(8,128)(2,1)S(1)}, bf16[17,32,256]{2,1,0:T(8,128)(2,1)S(1)}, u32[]{:S(2)}, u32[]{:S(2)}) collective-permute-start(bf16[17,32,256]{2,1,0:T(8,128)(2,1)S(1)} %get-tuple-element.50), channel_id=1, source_target_pairs={{0,32},{32,64},{64,96},{96,0},{1,33},{33,65},{65,97},{97,1},{2,34}... | collective-permute-start | bytes 835592 | tf_op jit(solution)/shard_map/ppermute | solution.py:19
  31.9 10.9 %collective-permute-start.12 = (bf16[17,32,256]{2,1,0:T(8,128)(2,1)S(1)}, bf16[17,32,256]{2,1,0:T(8,128)(2,1)S(1)}, u32[]{:S(2)}, u32[]{:S(2)}) collective-permute-start(bf16[17,32,256]{2,1,0:T(8,128)(2,1)S(1)} %get-tuple-element.54), channel_id=1, source_target_pairs={{0,96},{32,0},{64,32},{96,64},{1,97},{33,1},{65,33},{97,65},{2,98}... | collective-permute-start | bytes 835592 | tf_op jit(solution)/shard_map/ppermute | solution.py:19
  43.3 11.7 %collective-permute-start.14 = (bf16[32,32,256]{2,1,0:T(8,128)(2,1)S(1)}, bf16[32,32,256]{2,1,0:T(8,128)(2,1)S(1)}, u32[]{:S(2)}, u32[]{:S(2)}) collective-permute-start(bf16[32,32,256]{2,1,0:T(8,128)(2,1)S(1)} %get-tuple-element.58.refs_0_), channel_id=1, source_target_pairs={{0,96},{32,0},{64,32},{96,64},{1,97},{33,1},{65,33},{97,65},{2,98}... | collective-permute-start | bytes 1572872 | tf_op jit(solution)/shard_map/ppermute | solution.py:19
  45.2 13.0 %collective-permute-start.13 = (bf16[32,32,256]{2,1,0:T(8,128)(2,1)S(1)}, bf16[32,32,256]{2,1,0:T(8,128)(2,1)S(1)}, u32[]{:S(2)}, u32[]{:S(2)}) collective-permute-start(bf16[32,32,256]{2,1,0:T(8,128)(2,1)S(1)} %get-tuple-element.58.refs_0_), channel_id=1, source_target_pairs={{0,32},{32,64},{64,96},{96,0},{1,33},{33,65},{65,97},{97,1},{2,34}... | collective-permute-start | bytes 1572872 | tf_op jit(solution)/shard_map/ppermute | solution.py:19
  47.1 12.7 %collective-permute-start.17 = (bf16[4,288,256]{2,1,0:T(8,128)(2,1)S(1)}, bf16[4,288,256]{2,1,0:T(8,128)(2,1)S(1)}, u32[]{:S(2)}, u32[]{:S(2)}) collective-permute-start(bf16[4,288,256]{2,1,0:T(8,128)(2,1)S(1)} %get-tuple-element.67), channel_id=1, source_target_pairs={{0,16},{16,0},{1,17},{17,1},{2,18},{18,2},{3,19},{19,3},{4,20},{20... | collective-permute-start | bytes 1769480 | tf_op jit(solution)/shard_map/ppermute | solution.py:19
  58.3 7.9 %collective-permute-start.16 = (bf16[16,32,256]{2,1,0:T(8,128)(2,1)S(1)}, bf16[16,32,256]{2,1,0:T(8,128)(2,1)S(1)}, u32[]{:S(2)}, u32[]{:S(2)}) collective-permute-start(bf16[16,32,256]{2,1,0:T(8,128)(2,1)S(1)} %slice.71), channel_id=1, source_target_pairs={{0,96},{32,0},{64,32},{96,64},{1,97},{33,1},{65,33},{97,65},{2,98}... | collective-permute-start | bytes 786440 | tf_op jit(solution)/shard_map/ppermute | solution.py:19
  58.6 7.6 %collective-permute-start.15 = (bf16[16,32,256]{2,1,0:T(8,128)(2,1)S(1)}, bf16[16,32,256]{2,1,0:T(8,128)(2,1)S(1)}, u32[]{:S(2)}, u32[]{:S(2)}) collective-permute-start(bf16[16,32,256]{2,1,0:T(8,128)(2,1)S(1)} %slice.70), channel_id=1, source_target_pairs={{0,32},{32,64},{64,96},{96,0},{1,33},{33,65},{65,97},{97,1},{2,34}... | collective-permute-start | bytes 786440 | tf_op jit(solution)/shard_map/ppermute | solution.py:19
  59.9 9.4 %collective-permute-start.18 = (bf16[288,256]{1,0:T(8,128)(2,1)S(1)}, bf16[288,256]{1,0:T(8,128)(2,1)S(1)}, u32[]{:S(2)}, u32[]{:S(2)}) collective-permute-start(bf16[288,256]{1,0:T(8,128)(2,1)S(1)} %get-tuple-element.68), channel_id=1, source_target_pairs={{0,32},{32,64},{64,96},{96,0},{1,33},{33,65},{65,97},{97,1},{2,34}... | collective-permute-start | bytes 442376 | tf_op jit(solution)/shard_map/ppermute | solution.py:19
  60.0 9.4 %collective-permute-start.19 = (bf16[288,256]{1,0:T(8,128)(2,1)S(1)}, bf16[288,256]{1,0:T(8,128)(2,1)S(1)}, u32[]{:S(2)}, u32[]{:S(2)}) collective-permute-start(bf16[288,256]{1,0:T(8,128)(2,1)S(1)} %get-tuple-element.69), channel_id=1, source_target_pairs={{0,96},{32,0},{64,32},{96,64},{1,97},{33,1},{65,33},{97,65},{2,98}... | collective-permute-start | bytes 442376 | tf_op jit(solution)/shard_map/ppermute | solution.py:19
  62.7 7.3 %collective-permute-start.20 = (bf16[288,256]{1,0:T(8,128)(2,1)S(1)}, bf16[288,256]{1,0:T(8,128)(2,1)S(1)}, u32[]{:S(2)}, u32[]{:S(2)}) collective-permute-start(bf16[288,256]{1,0:T(8,128)(2,1)S(1)} %get-tuple-element.70), channel_id=1, source_target_pairs={{0,64},{32,96},{64,0},{96,32},{1,65},{33,97},{65,1},{97,33},{2,66}... | collective-permute-start | bytes 442376 | tf_op jit(solution)/shard_map/ppermute | solution.py:19
  70.0 6.5 %collective-permute-start.21 = (bf16[384,768]{1,0:T(8,128)(2,1)S(1)}, bf16[384,768]{1,0:T(8,128)(2,1)S(1)}, u32[]{:S(2)}, u32[]{:S(2)}) collective-permute-start(bf16[384,768]{1,0:T(8,128)(2,1)S(1)} %get-tuple-element.71), channel_id=1, source_target_pairs={{0,16},{16,0},{1,17},{17,1},{2,18},{18,2},{3,19},{19,3},{4,20},{20... | collective-permute-start | bytes 1769480 | tf_op jit(solution)/shard_map/ppermute | solution.py:19
  100.7 8.9 %collective-permute-start.24 = (bf16[90,256]{1,0:T(8,128)(2,1)S(1)}, bf16[90,256]{1,0:T(8,128)(2,1)S(1)}, u32[]{:S(2)}, u32[]{:S(2)}) collective-permute-start(bf16[90,256]{1,0:T(8,128)(2,1)S(1)} %sum_pieces.1.a_ref), channel_id=1, source_target_pairs={{0,8},{4,12},{8,0},{12,4},{1,9},{5,13},{9,1},{13,5},{2,10},{6,14},... | collective-permute-start | bytes 138248 | tf_op jit(solution)/shard_map/ppermute | solution.py:19
  101.4 8.2 %collective-permute-start.23 = (bf16[90,256]{1,0:T(8,128)(2,1)S(1)}, bf16[90,256]{1,0:T(8,128)(2,1)S(1)}, u32[]{:S(2)}, u32[]{:S(2)}) collective-permute-start(bf16[90,256]{1,0:T(8,128)(2,1)S(1)} %sum_pieces.1.a_ref), channel_id=1, source_target_pairs={{0,12},{4,0},{8,4},{12,8},{1,13},{5,1},{9,5},{13,9},{2,14},{6,2},{... | collective-permute-start | bytes 138248 | tf_op jit(solution)/shard_map/ppermute | solution.py:19
  101.9 7.7 %collective-permute-start.22 = (bf16[90,256]{1,0:T(8,128)(2,1)S(1)}, bf16[90,256]{1,0:T(8,128)(2,1)S(1)}, u32[]{:S(2)}, u32[]{:S(2)}) collective-permute-start(bf16[90,256]{1,0:T(8,128)(2,1)S(1)} %sum_pieces.1.a_ref), channel_id=1, source_target_pairs={{0,4},{4,8},{8,12},{12,0},{1,5},{5,9},{9,13},{13,1},{2,6},{6,10},{... | collective-permute-start | bytes 138248 | tf_op jit(solution)/shard_map/ppermute | solution.py:19
  104.8 4.8 %collective-permute-start.26 = (bf16[34,256]{1,0:T(8,128)(2,1)S(1)}, bf16[34,256]{1,0:T(8,128)(2,1)S(1)}, u32[]{:S(2)}, u32[]{:S(2)}) collective-permute-start(bf16[34,256]{1,0:T(8,128)(2,1)S(1)} %get-tuple-element.80), channel_id=1, source_target_pairs={{1,0},{2,1},{3,2},{4,3},{5,4},{6,5},{7,6},{8,7},{9,8},{10,9},{11,1... | collective-permute-start | bytes 52232 | tf_op jit(solution)/shard_map/ppermute | solution.py:383
  109.7 7.6 %collective-permute-start.29 = (bf16[360,256]{1,0:T(8,128)(2,1)S(1)}, bf16[360,256]{1,0:T(8,128)(2,1)S(1)}, u32[]{:S(2)}, u32[]{:S(2)}) collective-permute-start(bf16[360,256]{1,0:T(8,128)(2,1)S(1)} %order_pieces.1.a_ref), channel_id=1, source_target_pairs={{0,2},{1,3},{2,0},{3,1},{4,6},{5,7},{6,4},{7,5},{8,10},{9,11},{10,... | collective-permute-start | bytes 552968 | tf_op jit(solution)/shard_map/ppermute | solution.py:19
  112.2 8.2 %collective-permute-start.28 = (bf16[360,256]{1,0:T(8,128)(2,1)S(1)}, bf16[360,256]{1,0:T(8,128)(2,1)S(1)}, u32[]{:S(2)}, u32[]{:S(2)}) collective-permute-start(bf16[360,256]{1,0:T(8,128)(2,1)S(1)} %order_pieces.1.a_ref), channel_id=1, source_target_pairs={{0,3},{1,0},{2,1},{3,2},{4,7},{5,4},{6,5},{7,6},{8,11},{9,8},{10,9... | collective-permute-start | bytes 552968 | tf_op jit(solution)/shard_map/ppermute | solution.py:19
  114.6 7.4 %collective-permute-start.27 = (bf16[360,256]{1,0:T(8,128)(2,1)S(1)}, bf16[360,256]{1,0:T(8,128)(2,1)S(1)}, u32[]{:S(2)}, u32[]{:S(2)}) collective-permute-start(bf16[360,256]{1,0:T(8,128)(2,1)S(1)} %order_pieces.1.a_ref), channel_id=1, source_target_pairs={{0,1},{1,2},{2,3},{3,0},{4,5},{5,6},{6,7},{7,4},{8,9},{9,10},{10,1... | collective-permute-start | bytes 552968 | tf_op jit(solution)/shard_map/ppermute | solution.py:19
  122.1 5.6 %collective-permute-start.32 = (bf16[4,72,256]{2,1,0:T(8,128)(2,1)S(1)}, bf16[4,72,256]{2,1,0:T(8,128)(2,1)S(1)}, u32[]{:S(2)}, u32[]{:S(2)}) collective-permute-start(bf16[4,72,256]{2,1,0:T(8,128)(2,1)S(1)} %pick_rows.1), channel_id=1, source_target_pairs={{0,64},{32,96},{64,0},{96,32},{1,65},{33,97},{65,1},{97,33},{2,66}... | collective-permute-start | bytes 442376 | tf_op jit(solution)/shard_map/ppermute | solution.py:19
  123.6 4.1 %collective-permute-start.31 = (bf16[4,72,256]{2,1,0:T(8,128)(2,1)S(1)}, bf16[4,72,256]{2,1,0:T(8,128)(2,1)S(1)}, u32[]{:S(2)}, u32[]{:S(2)}) collective-permute-start(bf16[4,72,256]{2,1,0:T(8,128)(2,1)S(1)} %pick_rows.1), channel_id=1, source_target_pairs={{0,96},{32,0},{64,32},{96,64},{1,97},{33,1},{65,33},{97,65},{2,98}... | collective-permute-start | bytes 442376 | tf_op jit(solution)/shard_map/ppermute | solution.py:19
  123.6 5.6 %collective-permute-start.30 = (bf16[4,72,256]{2,1,0:T(8,128)(2,1)S(1)}, bf16[4,72,256]{2,1,0:T(8,128)(2,1)S(1)}, u32[]{:S(2)}, u32[]{:S(2)}) collective-permute-start(bf16[4,72,256]{2,1,0:T(8,128)(2,1)S(1)} %pick_rows.1), channel_id=1, source_target_pairs={{0,32},{32,64},{64,96},{96,0},{1,33},{33,65},{65,97},{97,1},{2,34}... | collective-permute-start | bytes 442376 | tf_op jit(solution)/shard_map/ppermute | solution.py:19
  129.3 6.2 %collective-permute-start.33 = (bf16[4,4,72,256]{3,2,1,0:T(8,128)(2,1)S(1)}, bf16[4,4,72,256]{3,2,1,0:T(8,128)(2,1)S(1)}, u32[]{:S(2)}, u32[]{:S(2)}) collective-permute-start(bf16[4,4,72,256]{3,2,1,0:T(8,128)(2,1)S(1)} %pad_maximum_fusion.1.in_ref), channel_id=1, source_target_pairs={{0,16},{16,0},{1,17},{17,1},{2,18},{18,2},{3,19},{19,3},{4,20},{20... | collective-permute-start | bytes 1769480 | tf_op jit(solution)/shard_map/ppermute | solution.py:19
  (5 other events, 26.0 us)

commit v16 on v13

--- a/solution.py
+++ b/solution.py
@@ -635,14 +635,12 @@
     extra = keep.shape[0] // (sx * sz)
     summed = lax.all_to_all(joined, SKY, 0, 0, tiled=True)
     summed = sum_pieces(summed)
-    summed, *ends = lax.optimization_barrier((summed, *ends))
-    edges = row_halo(ends)
     parts = gather_steps(order_pieces(gather_steps(summed, "z"), extra), "x")
     main = parts[0].shape[0] - sz * extra
     grad_first = lay_first(parts, sz, chans)
     share = pick_rows(parts, main)
-    share, *edges = lax.optimization_barrier((share, *edges))
-    features = features_tile(hidden, edges, weight_second)
+    share, *ends = lax.optimization_barrier((share, *ends))
+    features = features_tile(hidden, row_halo(ends), weight_second)
     share, grad_first, features = lax.optimization_barrier(
         (jnp.stack(gather_steps(share, "y")), grad_first, features)
     )

time: 134 us -> 138 us (1.030)
  waiting for transfers between devices: 25.1 us -> 27.1 us
  starting transfers between devices: 54 us -> 55.6 us
    ppermute x28, waiting for transfers between devices: 21.3 us -> 23.7 us  [shift(): lax.ppermute(x, axis, [(i, (i + step) % count) for i in range(count)])]
    ppermute x4, starting transfers between devices: 8.77 us -> 10.5 us  [row_halo(): return (lax.ppermute(ends[0], SKY, up), lax.ppermute(ends[1], SKY, down))]
where the time goes in v16:
time: 138 us; the launch traced here: 137 us
  starting transfers between devices  55.6 us (40%)
  waiting for transfers between devices  27.1 us (20%)
  Pallas kernels  24.7 us (18%)
  blocking collectives  23.9 us (17%)
  local copies, waits for them, and re-layouts  3.25 us (2%)
    ppermute x28, starting transfers between devices, shift(): lax.ppermute(x, axis, [(i, (i + step) % count) for i in range(count)])  40.6 us
    all_to_all x1, blocking collectives, body(): summed = lax.all_to_all(joined, SKY, 0, 0, tiled=True)  23.9 us
    ppermute x28, waiting for transfers between devices, shift(): lax.ppermute(x, axis, [(i, (i + step) % count) for i in range(count)])  23.7 us
    ppermute x4, starting transfers between devices, row_halo(): return (lax.ppermute(ends[0], SKY, up), lax.ppermute(ends[1], SKY, down))  10.5 us
    pallas_call x4, Pallas kernels, grad_strip(): pl.pallas_call(functools.partial(grad_kernel, step, len(pieces), old is n...  7 us
    pallas_call x4, Pallas kernels, conv_parts(): pl.pallas_call(functools.partial(conv_kernel, parts, len(adds)), out_shap...  5.84 us
    ppermute x4, waiting for transfers between devices, row_halo(): return (lax.ppermute(ends[0], SKY, up), lax.ppermute(ends[1], SKY, down))  3.45 us
  transfers between devices with their start and end apart: 34, of which 15 were waited for; matrix products, arithmetic and copies ran while one was open for 3% of the time, Pallas kernels for 14%

profile of v16, /device:TPU:1, one launch (start us, length us, event | category | flops | bytes accessed | tf_op | source)
XLA Modules:
  0.0 137.0 jit_solution(4392986316223641039)
XLA Ops:
  0.6 1.5 %collective-permute-start = (bf16[256,32,128]{2,1,0:T(8,128)(2,1)}, bf16[256,32,128]{2,1,0:T(8,128)(2,1)S(1)}, u32[]{:S(2)}, u32[]{:S(2)}) collective-permute-start(bf16[256,32,128]{2,1,0:T(8,128)(2,1)} %own_ref.1), channel_id=1, source_target_pairs={{0,16},{16,0},{1,17},{17,1},{2,18},{18,2},{3,19},{19,3},{4,20},{20... | collective-permute-start | bytes 6291464 | tf_op jit(solution)/shard_map/ppermute | solution.py:19
  6.2 4.3 %collective-permute-start.1 = (bf16[320,128]{1,0:T(8,128)(2,1)S(1)}, bf16[320,128]{1,0:T(8,128)(2,1)S(1)}, u32[]{:S(2)}, u32[]{:S(2)}) collective-permute-start(bf16[320,128]{1,0:T(8,128)(2,1)S(1)} %pad_maximum_fusion.3), channel_id=1, source_target_pairs={{0,1},{1,2},{2,3},{3,4},{4,5},{5,6},{6,7},{7,8},{8,9},{9,10},{10,1... | collective-permute-start | bytes 245768 | tf_op jit(solution)/shard_map/ppermute | solution.py:383
  14.4 1.9 %spread.1.wide_ref = bf16[4,40,32,768]{3,2,1,0:T(8,128)(2,1)S(1)} custom-call(bf16[256,32,128]{2,1,0:T(8,128)(2,1)S(1)} %copy-done.1, bf16[256,32,128]{2,1,0:T(8,128)(2,1)S(1)} %collective-permute-done.far_ref, bf16[2,320,128]{2,1,0:T(8,128)(2,1)S(1)} %pad_maximum_fusion.2.own_halo_ref.edge_ref, bf16[2,320,128]{2,1,0:T(8,128)(2,1)S(1)} %collective-permute-done.3.far_halo_ref), custom_call_target="tpu_custom_call" | custom-call | flops 1 | bytes 1 | tf_op jit(solution)/shard_map/spread/pallas_call | solution.py:94
  17.8 2.9 %collective-permute-start.8 = (bf16[17,32,256]{2,1,0:T(8,128)(2,1)S(1)}, bf16[17,32,256]{2,1,0:T(8,128)(2,1)S(1)}, u32[]{:S(2)}, u32[]{:S(2)}) collective-permute-start(bf16[17,32,256]{2,1,0:T(8,128)(2,1)S(1)} %get-tuple-element.42), channel_id=1, source_target_pairs={{0,96},{32,0},{64,32},{96,64},{1,97},{33,1},{65,33},{97,65},{2,98}... | collective-permute-start | bytes 835592 | tf_op jit(solution)/shard_map/ppermute | solution.py:19
  20.7 2.6 %collective-permute-start.6 = (bf16[34,256]{1,0:T(8,128)(2,1)S(1)}, bf16[34,256]{1,0:T(8,128)(2,1)S(1)}, u32[]{:S(2)}, u32[]{:S(2)}) collective-permute-start(bf16[34,256]{1,0:T(8,128)(2,1)S(1)} %maximum_maximum_fusion), channel_id=1, source_target_pairs={{0,16},{16,32},{32,48},{48,64},{64,80},{80,96},{96,112},{1,17},{17... | collective-permute-start | bytes 52232 | tf_op jit(solution)/shard_map/ppermute | solution.py:602
  23.3 1.9 %collective-permute-start.7 = (bf16[34,256]{1,0:T(8,128)(2,1)S(1)}, bf16[34,256]{1,0:T(8,128)(2,1)S(1)}, u32[]{:S(2)}, u32[]{:S(2)}) collective-permute-start(bf16[34,256]{1,0:T(8,128)(2,1)S(1)} %maximum_maximum_fusion.1), channel_id=1, source_target_pairs={{16,0},{32,16},{48,32},{64,48},{80,64},{96,80},{112,96},{17,1},{33... | collective-permute-start | bytes 52232 | tf_op jit(solution)/shard_map/ppermute | solution.py:603
  26.7 2.8 %collective-permute-start.10 = (bf16[17,32,256]{2,1,0:T(8,128)(2,1)S(1)}, bf16[17,32,256]{2,1,0:T(8,128)(2,1)S(1)}, u32[]{:S(2)}, u32[]{:S(2)}) collective-permute-start(bf16[17,32,256]{2,1,0:T(8,128)(2,1)S(1)} %get-tuple-element.45), channel_id=1, source_target_pairs={{0,96},{32,0},{64,32},{96,64},{1,97},{33,1},{65,33},{97,65},{2,98}... | collective-permute-start | bytes 835592 | tf_op jit(solution)/shard_map/ppermute | solution.py:19
  31.9 1.9 %collective-permute-start.12 = (bf16[17,32,256]{2,1,0:T(8,128)(2,1)S(1)}, bf16[17,32,256]{2,1,0:T(8,128)(2,1)S(1)}, u32[]{:S(2)}, u32[]{:S(2)}) collective-permute-start(bf16[17,32,256]{2,1,0:T(8,128)(2,1)S(1)} %get-tuple-element.47), channel_id=1, source_target_pairs={{0,96},{32,0},{64,32},{96,64},{1,97},{33,1},{65,33},{97,65},{2,98}... | collective-permute-start | bytes 835592 | tf_op jit(solution)/shard_map/ppermute | solution.py:19
  35.3 1.5 %back.1 = (f32[32,32,256]{2,1,0:T(8,128)S(1)}, bf16[34,32,768]{2,1,0:T(8,128)(2,1)S(1)}) custom-call(bf16[32,32,256]{2,1,0:T(8,128)(2,1)S(1)} %copy-done.2, bf16[34,256]{1,0:T(8,128)(2,1)S(1)} %collective-permute-done.6.left_ref, bf16[34,256]{1,0:T(8,128)(2,1)S(1)} %collective-permute-done.7.right_ref, ...), custom_call_target="tpu_custom_call" | custom-call | flops 1 | bytes 1 | tf_op jit(solution)/shard_map/back/pallas_call | solution.py:232
  36.8 6.0 %collective-permute-done.9.a0_ref = bf16[17,32,256]{2,1,0:T(8,128)(2,1)S(1)} collective-permute-done((bf16[17,32,256]{2,1,0:T(8,128)(2,1)S(1)}, bf16[17,32,256]{2,1,0:T(8,128)(2,1)S(1)}, u32[]{:S(2)}, u32[]{:S(2)}) %collective-permute-start.9) | collective-permute-done | bytes 278560 | tf_op jit(solution)/shard_map/ppermute | solution.py:19
  43.3 1.8 %collective-permute-start.14 = (bf16[32,32,256]{2,1,0:T(8,128)(2,1)S(1)}, bf16[32,32,256]{2,1,0:T(8,128)(2,1)S(1)}, u32[]{:S(2)}, u32[]{:S(2)}) collective-permute-start(bf16[32,32,256]{2,1,0:T(8,128)(2,1)S(1)} %get-tuple-element.51.refs_0_), channel_id=1, source_target_pairs={{0,96},{32,0},{64,32},{96,64},{1,97},{33,1},{65,33},{97,65},{2,98}... | collective-permute-start | bytes 1572872 | tf_op jit(solution)/shard_map/ppermute | solution.py:19
  45.2 1.9 %second.1 = (f32[4,288,256]{2,1,0:T(8,128)S(1)}, bf16[4,288,256]{2,1,0:T(8,128)(2,1)S(1)}) custom-call(bf16[34,32,256]{2,1,0:T(8,128)(2,1)S(1)} %get-tuple-element.57.hid_ref, bf16[34,32,768]{2,1,0:T(8,128)(2,1)S(1)} %get-tuple-element.58.wide_ref), custom_call_target="tpu_custom_call" | custom-call | flops 1 | bytes 1 | tf_op jit(solution)/shard_map/second/pallas_call | solution.py:271
  47.1 3.5 %collective-permute-start.17 = (bf16[4,288,256]{2,1,0:T(8,128)(2,1)S(1)}, bf16[4,288,256]{2,1,0:T(8,128)(2,1)S(1)}, u32[]{:S(2)}, u32[]{:S(2)}) collective-permute-start(bf16[4,288,256]{2,1,0:T(8,128)(2,1)S(1)} %get-tuple-element.60), channel_id=1, source_target_pairs={{0,16},{16,0},{1,17},{17,1},{2,18},{18,2},{3,19},{19,3},{4,20},{20... | collective-permute-start | bytes 1769480 | tf_op jit(solution)/shard_map/ppermute | solution.py:19
  50.6 1.7 %grad_first.4.refs_1_ = f32[768,768]{1,0:T(8,128)S(1)} custom-call(bf16[4,40,32,768]{3,2,1,0:T(8,128)(2,1)S(1)} %spread.1.wide_ref, bf16[32,32,256]{2,1,0:T(8,128)(2,1)S(1)} %get-tuple-element.51.refs_0_), custom_call_target="tpu_custom_call" | custom-call | flops 1 | bytes 1 | tf_op jit(solution)/shard_map/grad_first/pallas_call | solution.py:176
  52.3 2.8 %collective-permute-done.14.refs_0_ = bf16[32,32,256]{2,1,0:T(8,128)(2,1)S(1)} collective-permute-done((bf16[32,32,256]{2,1,0:T(8,128)(2,1)S(1)}, bf16[32,32,256]{2,1,0:T(8,128)(2,1)S(1)}, u32[]{:S(2)}, u32[]{:S(2)}) %collective-permute-start.14) | collective-permute-done | bytes 524320 | tf_op jit(solution)/shard_map/ppermute | solution.py:19
  55.1 3.1 %collective-permute-done.13.refs_0_ = bf16[32,32,256]{2,1,0:T(8,128)(2,1)S(1)} collective-permute-done((bf16[32,32,256]{2,1,0:T(8,128)(2,1)S(1)}, bf16[32,32,256]{2,1,0:T(8,128)(2,1)S(1)}, u32[]{:S(2)}, u32[]{:S(2)}) %collective-permute-start.13) | collective-permute-done | bytes 524320 | tf_op jit(solution)/shard_map/ppermute | solution.py:19
  60.0 2.7 %collective-permute-start.19 = (bf16[288,256]{1,0:T(8,128)(2,1)S(1)}, bf16[288,256]{1,0:T(8,128)(2,1)S(1)}, u32[]{:S(2)}, u32[]{:S(2)}) collective-permute-start(bf16[288,256]{1,0:T(8,128)(2,1)S(1)} %get-tuple-element.62), channel_id=1, source_target_pairs={{0,96},{32,0},{64,32},{96,64},{1,97},{33,1},{65,33},{97,65},{2,98}... | collective-permute-start | bytes 442376 | tf_op jit(solution)/shard_map/ppermute | solution.py:19
  62.7 1.7 %grad_first.5.refs_1_ = f32[768,768]{1,0:T(8,128)S(1)} custom-call(bf16[4,40,32,768]{3,2,1,0:T(8,128)(2,1)S(1)} %spread.1.wide_ref, bf16[32,32,256]{2,1,0:T(8,128)(2,1)S(1)} %collective-permute-done.13.refs_0_, f32[768,768]{1,0:T(8,128)S(1)} %grad_first.4.refs_1_), custom_call_target="tpu_custom_call" | custom-call | flops 1 | bytes 1 | tf_op jit(solution)/shard_map/grad_first/pallas_call | solution.py:176
  64.4 1.7 %grad_first.6.refs_2_ = f32[768,768]{1,0:T(8,128)S(1)} custom-call(bf16[4,40,32,768]{3,2,1,0:T(8,128)(2,1)S(1)} %spread.1.wide_ref, bf16[32,32,256]{2,1,0:T(8,128)(2,1)S(1)} %collective-permute-done.14.refs_0_, f32[768,768]{1,0:T(8,128)S(1)} %grad_first.5.refs_1_), custom_call_target="tpu_custom_call" | custom-call | flops 1 | bytes 1 | tf_op jit(solution)/shard_map/grad_first/pallas_call | solution.py:176
  66.2 1.8 %grad_first.7 = (f32[384,768]{1,0:T(8,128)S(1)}, bf16[384,768]{1,0:T(8,128)(2,1)S(1)}) custom-call(bf16[4,40,32,768]{3,2,1,0:T(8,128)(2,1)S(1)} %spread.1.wide_ref, bf16[16,32,256]{2,1,0:T(8,128)(2,1)S(1)} %collective-permute-done.15.refs_0_, bf16[16,32,256]{2,1,0:T(8,128)(2,1)S(1)} %collective-permute-done.16.refs_1_, f32[768,768]{1,0:T(8,128)S(1)} %grad_first.6.refs_2_), custom_call_target="tpu_custom_call" | custom-call | flops 1 | bytes 1 | tf_op jit(solution)/shard_map/grad_first/pallas_call | solution.py:176
  70.0 4.9 %collective-permute-start.21 = (bf16[384,768]{1,0:T(8,128)(2,1)S(1)}, bf16[384,768]{1,0:T(8,128)(2,1)S(1)}, u32[]{:S(2)}, u32[]{:S(2)}) collective-permute-start(bf16[384,768]{1,0:T(8,128)(2,1)S(1)} %get-tuple-element.64), channel_id=1, source_target_pairs={{0,16},{16,0},{1,17},{17,1},{2,18},{18,2},{3,19},{19,3},{4,20},{20... | collective-permute-start | bytes 1769480 | tf_op jit(solution)/shard_map/ppermute | solution.py:19
  74.9 1.6 %collective-permute-done.21.far_ref = bf16[384,768]{1,0:T(8,128)(2,1)S(1)} collective-permute-done((bf16[384,768]{1,0:T(8,128)(2,1)S(1)}, bf16[384,768]{1,0:T(8,128)(2,1)S(1)}, u32[]{:S(2)}, u32[]{:S(2)}) %collective-permute-start.21) | collective-permute-done | bytes 589856 | tf_op jit(solution)/shard_map/ppermute | solution.py:19
  76.7 23.9 %all_to_all.5.in_ref = bf16[16,90,256]{2,1,0:T(8,128)(2,1)S(1)} all-to-all(bf16[16,90,256]{2,1,0:T(8,128)(2,1)S(1)} %join.1), channel_id=1, replica_groups=mesh['y'=4,'c'=2,'z'=4,'x'=4] {'z','x'}, dimensions={0} | all-to-all | bytes 1474560 | tf_op jit(solution)/shard_map/all_to_all | solution.py:636
  102.8 2.4 %collective-permute-done.24.d_ref = bf16[90,256]{1,0:T(8,128)(2,1)S(1)} collective-permute-done((bf16[90,256]{1,0:T(8,128)(2,1)S(1)}, bf16[90,256]{1,0:T(8,128)(2,1)S(1)}, u32[]{:S(2)}, u32[]{:S(2)}) %collective-permute-start.24) | collective-permute-done | bytes 46112 | tf_op jit(solution)/shard_map/ppermute | solution.py:19
  106.2 2.7 %collective-permute-start.27 = (bf16[360,256]{1,0:T(8,128)(2,1)S(1)}, bf16[360,256]{1,0:T(8,128)(2,1)S(1)}, u32[]{:S(2)}, u32[]{:S(2)}) collective-permute-start(bf16[360,256]{1,0:T(8,128)(2,1)S(1)} %order_pieces.1.a_ref), channel_id=1, source_target_pairs={{0,2},{1,3},{2,0},{3,1},{4,6},{5,7},{6,4},{7,5},{8,10},{9,11},{10,... | collective-permute-start | bytes 552968 | tf_op jit(solution)/shard_map/ppermute | solution.py:19
  110.4 1.8 %collective-permute-done.27.d_ref = bf16[360,256]{1,0:T(8,128)(2,1)S(1)} collective-permute-done((bf16[360,256]{1,0:T(8,128)(2,1)S(1)}, bf16[360,256]{1,0:T(8,128)(2,1)S(1)}, u32[]{:S(2)}, u32[]{:S(2)}) %collective-permute-start.27) | collective-permute-done | bytes 184352 | tf_op jit(solution)/shard_map/ppermute | solution.py:19
  112.2 1.9 %collective-permute-done.26.c_ref = bf16[360,256]{1,0:T(8,128)(2,1)S(1)} collective-permute-done((bf16[360,256]{1,0:T(8,128)(2,1)S(1)}, bf16[360,256]{1,0:T(8,128)(2,1)S(1)}, u32[]{:S(2)}, u32[]{:S(2)}) %collective-permute-start.26) | collective-permute-done | bytes 184352 | tf_op jit(solution)/shard_map/ppermute | solution.py:19
  114.6 1.5 %collective-permute-start.30 = (bf16[4,72,256]{2,1,0:T(8,128)(2,1)S(1)}, bf16[4,72,256]{2,1,0:T(8,128)(2,1)S(1)}, u32[]{:S(2)}, u32[]{:S(2)}) collective-permute-start(bf16[4,72,256]{2,1,0:T(8,128)(2,1)S(1)} %pick_rows.1), channel_id=1, source_target_pairs={{0,64},{32,96},{64,0},{96,32},{1,65},{33,97},{65,1},{97,33},{2,66}... | collective-permute-start | bytes 442376 | tf_op jit(solution)/shard_map/ppermute | solution.py:19
  117.6 3.6 %collective-permute-start.31 = (bf16[34,256]{1,0:T(8,128)(2,1)S(1)}, bf16[34,256]{1,0:T(8,128)(2,1)S(1)}, u32[]{:S(2)}, u32[]{:S(2)}) collective-permute-start(bf16[34,256]{1,0:T(8,128)(2,1)S(1)} %get-tuple-element.72), channel_id=1, source_target_pairs={{0,1},{1,2},{2,3},{3,4},{4,5},{5,6},{6,7},{7,8},{8,9},{9,10},{10,1... | collective-permute-start | bytes 52232 | tf_op jit(solution)/shard_map/ppermute | solution.py:383
  123.6 2.4 %collective-permute-done.32.after_ref = bf16[34,256]{1,0:T(8,128)(2,1)S(1)} collective-permute-done((bf16[34,256]{1,0:T(8,128)(2,1)S(1)}, bf16[34,256]{1,0:T(8,128)(2,1)S(1)}, u32[]{:S(2)}, u32[]{:S(2)}) %collective-permute-start.32) | collective-permute-done | bytes 17440 | tf_op jit(solution)/shard_map/ppermute | solution.py:383
  126.1 2.2 %features.1 = bf16[32,32,256]{2,1,0:T(8,128)(2,1)} custom-call(bf16[34,32,256]{2,1,0:T(8,128)(2,1)S(1)} %get-tuple-element.57.hid_ref, bf16[34,256]{1,0:T(8,128)(2,1)S(1)} %collective-permute-done.31.before_ref, bf16[34,256]{1,0:T(8,128)(2,1)S(1)} %collective-permute-done.32.after_ref, bf16[2304,256]{1,0:T(8,128)(2,1)S(1)} %bitcast.47), custom_call_target="tpu_custom_call" | custom-call | flops 1 | bytes 1 | tf_op jit(solution)/shard_map/features/pallas_call | solution.py:298
  128.3 5.7 %collective-permute-start.33 = (bf16[4,4,72,256]{3,2,1,0:T(8,128)(2,1)S(1)}, bf16[4,4,72,256]{3,2,1,0:T(8,128)(2,1)S(1)}, u32[]{:S(2)}, u32[]{:S(2)}) collective-permute-start(bf16[4,4,72,256]{3,2,1,0:T(8,128)(2,1)S(1)} %pad_maximum_fusion.1.in_ref), channel_id=1, source_target_pairs={{0,16},{16,0},{1,17},{17,1},{2,18},{18,2},{3,19},{19,3},{4,20},{20... | collective-permute-start | bytes 1769480 | tf_op jit(solution)/shard_map/ppermute | solution.py:19
  (82 shorter events, 31.1 us)
Async XLA Ops:
  0.6 13.7 %collective-permute-start = (bf16[256,32,128]{2,1,0:T(8,128)(2,1)}, bf16[256,32,128]{2,1,0:T(8,128)(2,1)S(1)}, u32[]{:S(2)}, u32[]{:S(2)}) collective-permute-start(bf16[256,32,128]{2,1,0:T(8,128)(2,1)} %own_ref.1), channel_id=1, source_target_pairs={{0,16},{16,0},{1,17},{17,1},{2,18},{18,2},{3,19},{19,3},{4,20},{20... | collective-permute-start | bytes 6291464 | tf_op jit(solution)/shard_map/ppermute | solution.py:19
  4.6 6.6 %collective-permute-start.2 = (bf16[320,128]{1,0:T(8,128)(2,1)S(1)}, bf16[320,128]{1,0:T(8,128)(2,1)S(1)}, u32[]{:S(2)}, u32[]{:S(2)}) collective-permute-start(bf16[320,128]{1,0:T(8,128)(2,1)S(1)} %pad_maximum_fusion.4), channel_id=1, source_target_pairs={{1,0},{2,1},{3,2},{4,3},{5,4},{6,5},{7,6},{8,7},{9,8},{10,9},{11,1... | collective-permute-start | bytes 245768 | tf_op jit(solution)/shard_map/ppermute | solution.py:383
  5.9 7.3 %collective-permute-start.4 = (bf16[3,3,128,256]{3,2,1,0:T(8,128)(2,1)}, bf16[3,3,128,256]{3,2,1,0:T(8,128)(2,1)S(1)}, u32[]{:S(2)}, u32[]{:S(2)}) collective-permute-start(bf16[3,3,128,256]{3,2,1,0:T(8,128)(2,1)} %param.5), channel_id=1, source_target_pairs={{0,16},{16,0},{1,17},{17,1},{2,18},{18,2},{3,19},{19,3},{4,20},{20... | collective-permute-start | bytes 1769480 | tf_op jit(solution)/shard_map/ppermute | solution.py:19
  6.2 6.1 %collective-permute-start.1 = (bf16[320,128]{1,0:T(8,128)(2,1)S(1)}, bf16[320,128]{1,0:T(8,128)(2,1)S(1)}, u32[]{:S(2)}, u32[]{:S(2)}) collective-permute-start(bf16[320,128]{1,0:T(8,128)(2,1)S(1)} %pad_maximum_fusion.3), channel_id=1, source_target_pairs={{0,1},{1,2},{2,3},{3,4},{4,5},{5,6},{6,7},{7,8},{8,9},{9,10},{10,1... | collective-permute-start | bytes 245768 | tf_op jit(solution)/shard_map/ppermute | solution.py:383
  17.8 11.9 %collective-permute-start.8 = (bf16[17,32,256]{2,1,0:T(8,128)(2,1)S(1)}, bf16[17,32,256]{2,1,0:T(8,128)(2,1)S(1)}, u32[]{:S(2)}, u32[]{:S(2)}) collective-permute-start(bf16[17,32,256]{2,1,0:T(8,128)(2,1)S(1)} %get-tuple-element.42), channel_id=1, source_target_pairs={{0,96},{32,0},{64,32},{96,64},{1,97},{33,1},{65,33},{97,65},{2,98}... | collective-permute-start | bytes 835592 | tf_op jit(solution)/shard_map/ppermute | solution.py:19
  20.7 9.0 %collective-permute-start.5 = (bf16[17,32,256]{2,1,0:T(8,128)(2,1)S(1)}, bf16[17,32,256]{2,1,0:T(8,128)(2,1)S(1)}, u32[]{:S(2)}, u32[]{:S(2)}) collective-permute-start(bf16[17,32,256]{2,1,0:T(8,128)(2,1)S(1)} %get-tuple-element.40), channel_id=1, source_target_pairs={{0,32},{32,64},{64,96},{96,0},{1,33},{33,65},{65,97},{97,1},{2,34}... | collective-permute-start | bytes 835592 | tf_op jit(solution)/shard_map/ppermute | solution.py:19
  20.7 8.8 %collective-permute-start.6 = (bf16[34,256]{1,0:T(8,128)(2,1)S(1)}, bf16[34,256]{1,0:T(8,128)(2,1)S(1)}, u32[]{:S(2)}, u32[]{:S(2)}) collective-permute-start(bf16[34,256]{1,0:T(8,128)(2,1)S(1)} %maximum_maximum_fusion), channel_id=1, source_target_pairs={{0,16},{16,32},{32,48},{48,64},{64,80},{80,96},{96,112},{1,17},{17... | collective-permute-start | bytes 52232 | tf_op jit(solution)/shard_map/ppermute | solution.py:602
  23.3 6.2 %collective-permute-start.7 = (bf16[34,256]{1,0:T(8,128)(2,1)S(1)}, bf16[34,256]{1,0:T(8,128)(2,1)S(1)}, u32[]{:S(2)}, u32[]{:S(2)}) collective-permute-start(bf16[34,256]{1,0:T(8,128)(2,1)S(1)} %maximum_maximum_fusion.1), channel_id=1, source_target_pairs={{16,0},{32,16},{48,32},{64,48},{80,64},{96,80},{112,96},{17,1},{33... | collective-permute-start | bytes 52232 | tf_op jit(solution)/shard_map/ppermute | solution.py:603
  26.7 10.2 %collective-permute-start.10 = (bf16[17,32,256]{2,1,0:T(8,128)(2,1)S(1)}, bf16[17,32,256]{2,1,0:T(8,128)(2,1)S(1)}, u32[]{:S(2)}, u32[]{:S(2)}) collective-permute-start(bf16[17,32,256]{2,1,0:T(8,128)(2,1)S(1)} %get-tuple-element.45), channel_id=1, source_target_pairs={{0,96},{32,0},{64,32},{96,64},{1,97},{33,1},{65,33},{97,65},{2,98}... | collective-permute-start | bytes 835592 | tf_op jit(solution)/shard_map/ppermute | solution.py:19
  29.5 7.3 %collective-permute-start.11 = (bf16[17,32,256]{2,1,0:T(8,128)(2,1)S(1)}, bf16[17,32,256]{2,1,0:T(8,128)(2,1)S(1)}, u32[]{:S(2)}, u32[]{:S(2)}) collective-permute-start(bf16[17,32,256]{2,1,0:T(8,128)(2,1)S(1)} %get-tuple-element.46), channel_id=1, source_target_pairs={{0,32},{32,64},{64,96},{96,0},{1,33},{33,65},{65,97},{97,1},{2,34}... | collective-permute-start | bytes 835592 | tf_op jit(solution)/shard_map/ppermute | solution.py:19
  31.1 11.7 %collective-permute-start.9 = (bf16[17,32,256]{2,1,0:T(8,128)(2,1)S(1)}, bf16[17,32,256]{2,1,0:T(8,128)(2,1)S(1)}, u32[]{:S(2)}, u32[]{:S(2)}) collective-permute-start(bf16[17,32,256]{2,1,0:T(8,128)(2,1)S(1)} %get-tuple-element.43), channel_id=1, source_target_pairs={{0,32},{32,64},{64,96},{96,0},{1,33},{33,65},{65,97},{97,1},{2,34}... | collective-permute-start | bytes 835592 | tf_op jit(solution)/shard_map/ppermute | solution.py:19
  31.9 10.9 %collective-permute-start.12 = (bf16[17,32,256]{2,1,0:T(8,128)(2,1)S(1)}, bf16[17,32,256]{2,1,0:T(8,128)(2,1)S(1)}, u32[]{:S(2)}, u32[]{:S(2)}) collective-permute-start(bf16[17,32,256]{2,1,0:T(8,128)(2,1)S(1)} %get-tuple-element.47), channel_id=1, source_target_pairs={{0,96},{32,0},{64,32},{96,64},{1,97},{33,1},{65,33},{97,65},{2,98}... | collective-permute-start | bytes 835592 | tf_op jit(solution)/shard_map/ppermute | solution.py:19
  43.3 11.7 %collective-permute-start.14 = (bf16[32,32,256]{2,1,0:T(8,128)(2,1)S(1)}, bf16[32,32,256]{2,1,0:T(8,128)(2,1)S(1)}, u32[]{:S(2)}, u32[]{:S(2)}) collective-permute-start(bf16[32,32,256]{2,1,0:T(8,128)(2,1)S(1)} %get-tuple-element.51.refs_0_), channel_id=1, source_target_pairs={{0,96},{32,0},{64,32},{96,64},{1,97},{33,1},{65,33},{97,65},{2,98}... | collective-permute-start | bytes 1572872 | tf_op jit(solution)/shard_map/ppermute | solution.py:19
  45.2 13.0 %collective-permute-start.13 = (bf16[32,32,256]{2,1,0:T(8,128)(2,1)S(1)}, bf16[32,32,256]{2,1,0:T(8,128)(2,1)S(1)}, u32[]{:S(2)}, u32[]{:S(2)}) collective-permute-start(bf16[32,32,256]{2,1,0:T(8,128)(2,1)S(1)} %get-tuple-element.51.refs_0_), channel_id=1, source_target_pairs={{0,32},{32,64},{64,96},{96,0},{1,33},{33,65},{65,97},{97,1},{2,34}... | collective-permute-start | bytes 1572872 | tf_op jit(solution)/shard_map/ppermute | solution.py:19
  47.1 12.7 %collective-permute-start.17 = (bf16[4,288,256]{2,1,0:T(8,128)(2,1)S(1)}, bf16[4,288,256]{2,1,0:T(8,128)(2,1)S(1)}, u32[]{:S(2)}, u32[]{:S(2)}) collective-permute-start(bf16[4,288,256]{2,1,0:T(8,128)(2,1)S(1)} %get-tuple-element.60), channel_id=1, source_target_pairs={{0,16},{16,0},{1,17},{17,1},{2,18},{18,2},{3,19},{19,3},{4,20},{20... | collective-permute-start | bytes 1769480 | tf_op jit(solution)/shard_map/ppermute | solution.py:19
  58.3 7.9 %collective-permute-start.16 = (bf16[16,32,256]{2,1,0:T(8,128)(2,1)S(1)}, bf16[16,32,256]{2,1,0:T(8,128)(2,1)S(1)}, u32[]{:S(2)}, u32[]{:S(2)}) collective-permute-start(bf16[16,32,256]{2,1,0:T(8,128)(2,1)S(1)} %slice.71), channel_id=1, source_target_pairs={{0,96},{32,0},{64,32},{96,64},{1,97},{33,1},{65,33},{97,65},{2,98}... | collective-permute-start | bytes 786440 | tf_op jit(solution)/shard_map/ppermute | solution.py:19
  58.6 7.6 %collective-permute-start.15 = (bf16[16,32,256]{2,1,0:T(8,128)(2,1)S(1)}, bf16[16,32,256]{2,1,0:T(8,128)(2,1)S(1)}, u32[]{:S(2)}, u32[]{:S(2)}) collective-permute-start(bf16[16,32,256]{2,1,0:T(8,128)(2,1)S(1)} %slice.70), channel_id=1, source_target_pairs={{0,32},{32,64},{64,96},{96,0},{1,33},{33,65},{65,97},{97,1},{2,34}... | collective-permute-start | bytes 786440 | tf_op jit(solution)/shard_map/ppermute | solution.py:19
  59.9 9.4 %collective-permute-start.18 = (bf16[288,256]{1,0:T(8,128)(2,1)S(1)}, bf16[288,256]{1,0:T(8,128)(2,1)S(1)}, u32[]{:S(2)}, u32[]{:S(2)}) collective-permute-start(bf16[288,256]{1,0:T(8,128)(2,1)S(1)} %get-tuple-element.61), channel_id=1, source_target_pairs={{0,32},{32,64},{64,96},{96,0},{1,33},{33,65},{65,97},{97,1},{2,34}... | collective-permute-start | bytes 442376 | tf_op jit(solution)/shard_map/ppermute | solution.py:19
  60.0 9.4 %collective-permute-start.19 = (bf16[288,256]{1,0:T(8,128)(2,1)S(1)}, bf16[288,256]{1,0:T(8,128)(2,1)S(1)}, u32[]{:S(2)}, u32[]{:S(2)}) collective-permute-start(bf16[288,256]{1,0:T(8,128)(2,1)S(1)} %get-tuple-element.62), channel_id=1, source_target_pairs={{0,96},{32,0},{64,32},{96,64},{1,97},{33,1},{65,33},{97,65},{2,98}... | collective-permute-start | bytes 442376 | tf_op jit(solution)/shard_map/ppermute | solution.py:19
  62.7 7.3 %collective-permute-start.20 = (bf16[288,256]{1,0:T(8,128)(2,1)S(1)}, bf16[288,256]{1,0:T(8,128)(2,1)S(1)}, u32[]{:S(2)}, u32[]{:S(2)}) collective-permute-start(bf16[288,256]{1,0:T(8,128)(2,1)S(1)} %get-tuple-element.63), channel_id=1, source_target_pairs={{0,64},{32,96},{64,0},{96,32},{1,65},{33,97},{65,1},{97,33},{2,66}... | collective-permute-start | bytes 442376 | tf_op jit(solution)/shard_map/ppermute | solution.py:19
  70.0 6.5 %collective-permute-start.21 = (bf16[384,768]{1,0:T(8,128)(2,1)S(1)}, bf16[384,768]{1,0:T(8,128)(2,1)S(1)}, u32[]{:S(2)}, u32[]{:S(2)}) collective-permute-start(bf16[384,768]{1,0:T(8,128)(2,1)S(1)} %get-tuple-element.64), channel_id=1, source_target_pairs={{0,16},{16,0},{1,17},{17,1},{2,18},{18,2},{3,19},{19,3},{4,20},{20... | collective-permute-start | bytes 1769480 | tf_op jit(solution)/shard_map/ppermute | solution.py:19
  100.7 4.5 %collective-permute-start.24 = (bf16[90,256]{1,0:T(8,128)(2,1)S(1)}, bf16[90,256]{1,0:T(8,128)(2,1)S(1)}, u32[]{:S(2)}, u32[]{:S(2)}) collective-permute-start(bf16[90,256]{1,0:T(8,128)(2,1)S(1)} %sum_pieces.1.a_ref), channel_id=1, source_target_pairs={{0,8},{4,12},{8,0},{12,4},{1,9},{5,13},{9,1},{13,5},{2,10},{6,14},... | collective-permute-start | bytes 138248 | tf_op jit(solution)/shard_map/ppermute | solution.py:19
  101.9 4.2 %collective-permute-start.22 = (bf16[90,256]{1,0:T(8,128)(2,1)S(1)}, bf16[90,256]{1,0:T(8,128)(2,1)S(1)}, u32[]{:S(2)}, u32[]{:S(2)}) collective-permute-start(bf16[90,256]{1,0:T(8,128)(2,1)S(1)} %sum_pieces.1.a_ref), channel_id=1, source_target_pairs={{0,4},{4,8},{8,12},{12,0},{1,5},{5,9},{9,13},{13,1},{2,6},{6,10},{... | collective-permute-start | bytes 138248 | tf_op jit(solution)/shard_map/ppermute | solution.py:19
  106.2 6.0 %collective-permute-start.27 = (bf16[360,256]{1,0:T(8,128)(2,1)S(1)}, bf16[360,256]{1,0:T(8,128)(2,1)S(1)}, u32[]{:S(2)}, u32[]{:S(2)}) collective-permute-start(bf16[360,256]{1,0:T(8,128)(2,1)S(1)} %order_pieces.1.a_ref), channel_id=1, source_target_pairs={{0,2},{1,3},{2,0},{3,1},{4,6},{5,7},{6,4},{7,5},{8,10},{9,11},{10,... | collective-permute-start | bytes 552968 | tf_op jit(solution)/shard_map/ppermute | solution.py:19
  108.9 5.1 %collective-permute-start.26 = (bf16[360,256]{1,0:T(8,128)(2,1)S(1)}, bf16[360,256]{1,0:T(8,128)(2,1)S(1)}, u32[]{:S(2)}, u32[]{:S(2)}) collective-permute-start(bf16[360,256]{1,0:T(8,128)(2,1)S(1)} %order_pieces.1.a_ref), channel_id=1, source_target_pairs={{0,3},{1,0},{2,1},{3,2},{4,7},{5,4},{6,5},{7,6},{8,11},{9,8},{10,9... | collective-permute-start | bytes 552968 | tf_op jit(solution)/shard_map/ppermute | solution.py:19
  109.0 5.6 %collective-permute-start.25 = (bf16[360,256]{1,0:T(8,128)(2,1)S(1)}, bf16[360,256]{1,0:T(8,128)(2,1)S(1)}, u32[]{:S(2)}, u32[]{:S(2)}) collective-permute-start(bf16[360,256]{1,0:T(8,128)(2,1)S(1)} %order_pieces.1.a_ref), channel_id=1, source_target_pairs={{0,1},{1,2},{2,3},{3,0},{4,5},{5,6},{6,7},{7,4},{8,9},{9,10},{10,1... | collective-permute-start | bytes 552968 | tf_op jit(solution)/shard_map/ppermute | solution.py:19
  114.6 13.6 %collective-permute-start.30 = (bf16[4,72,256]{2,1,0:T(8,128)(2,1)S(1)}, bf16[4,72,256]{2,1,0:T(8,128)(2,1)S(1)}, u32[]{:S(2)}, u32[]{:S(2)}) collective-permute-start(bf16[4,72,256]{2,1,0:T(8,128)(2,1)S(1)} %pick_rows.1), channel_id=1, source_target_pairs={{0,64},{32,96},{64,0},{96,32},{1,65},{33,97},{65,1},{97,33},{2,66}... | collective-permute-start | bytes 442376 | tf_op jit(solution)/shard_map/ppermute | solution.py:19
  116.2 12.1 %collective-permute-start.29 = (bf16[4,72,256]{2,1,0:T(8,128)(2,1)S(1)}, bf16[4,72,256]{2,1,0:T(8,128)(2,1)S(1)}, u32[]{:S(2)}, u32[]{:S(2)}) collective-permute-start(bf16[4,72,256]{2,1,0:T(8,128)(2,1)S(1)} %pick_rows.1), channel_id=1, source_target_pairs={{0,96},{32,0},{64,32},{96,64},{1,97},{33,1},{65,33},{97,65},{2,98}... | collective-permute-start | bytes 442376 | tf_op jit(solution)/shard_map/ppermute | solution.py:19
  116.2 12.1 %collective-permute-start.28 = (bf16[4,72,256]{2,1,0:T(8,128)(2,1)S(1)}, bf16[4,72,256]{2,1,0:T(8,128)(2,1)S(1)}, u32[]{:S(2)}, u32[]{:S(2)}) collective-permute-start(bf16[4,72,256]{2,1,0:T(8,128)(2,1)S(1)} %pick_rows.1), channel_id=1, source_target_pairs={{0,32},{32,64},{64,96},{96,0},{1,33},{33,65},{65,97},{97,1},{2,34}... | collective-permute-start | bytes 442376 | tf_op jit(solution)/shard_map/ppermute | solution.py:19
  117.6 6.0 %collective-permute-start.31 = (bf16[34,256]{1,0:T(8,128)(2,1)S(1)}, bf16[34,256]{1,0:T(8,128)(2,1)S(1)}, u32[]{:S(2)}, u32[]{:S(2)}) collective-permute-start(bf16[34,256]{1,0:T(8,128)(2,1)S(1)} %get-tuple-element.72), channel_id=1, source_target_pairs={{0,1},{1,2},{2,3},{3,4},{4,5},{5,6},{6,7},{7,8},{8,9},{9,10},{10,1... | collective-permute-start | bytes 52232 | tf_op jit(solution)/shard_map/ppermute | solution.py:383
  121.2 4.8 %collective-permute-start.32 = (bf16[34,256]{1,0:T(8,128)(2,1)S(1)}, bf16[34,256]{1,0:T(8,128)(2,1)S(1)}, u32[]{:S(2)}, u32[]{:S(2)}) collective-permute-start(bf16[34,256]{1,0:T(8,128)(2,1)S(1)} %get-tuple-element.73), channel_id=1, source_target_pairs={{1,0},{2,1},{3,2},{4,3},{5,4},{6,5},{7,6},{8,7},{9,8},{10,9},{11,1... | collective-permute-start | bytes 52232 | tf_op jit(solution)/shard_map/ppermute | solution.py:383
  128.3 7.4 %collective-permute-start.33 = (bf16[4,4,72,256]{3,2,1,0:T(8,128)(2,1)S(1)}, bf16[4,4,72,256]{3,2,1,0:T(8,128)(2,1)S(1)}, u32[]{:S(2)}, u32[]{:S(2)}) collective-permute-start(bf16[4,4,72,256]{3,2,1,0:T(8,128)(2,1)S(1)} %pad_maximum_fusion.1.in_ref), channel_id=1, source_target_pairs={{0,16},{16,0},{1,17},{17,1},{2,18},{18,2},{3,19},{19,3},{4,20},{20... | collective-permute-start | bytes 1769480 | tf_op jit(solution)/shard_map/ppermute | solution.py:19
  (5 other events, 26.6 us)
